TPU v7x, 32 devices: a whole 2x2x4 slice. The times are simulated.
32 devices in a mesh: dp: 16 (over z, y, core), tensor: 2 (over x).
Axes of the slice: x: 2, y: 2, z: 4, core: 2. Of those that a mesh axis runs over, the one named last changes fastest.
Arguments:
- hidden_in: bfloat16 [2048, 2048], P('dp'), may hold values from -6 to 6
- seq_lengths: int32 [64], replicated, may hold values from 1 to 128, as said below
- seq_device: int32 [64], replicated, may hold values from 0 to 15, as said below
- positions: int32 [2048], P('dp'), may hold values from 0 to 2047, as said below
- norm_gain: bfloat16 [2, 2048], P(None, 'dp'), may hold values from 0.5 to 1.5
- norm_bias: bfloat16 [2, 2048], P(None, 'dp'), may hold values from -2 to 2
- qkv_weight: bfloat16 [2, 2048, 3, 2048], P(None, 'dp', None, 'tensor'), may hold values from -0.125 to 0.125
- qkv_bias: bfloat16 [2, 3, 2048], P(None, None, ('tensor', 'dp')), may hold values from -3 to 3
- out_weight: bfloat16 [2, 2048, 2048], P(None, 'tensor', 'dp'), may hold values from -0.375 to 0.375
- fc1_weight: bfloat16 [2, 2048, 8192], P(None, 'dp', 'tensor'), may hold values from -0.125 to 0.125
- fc1_bias: bfloat16 [2, 8192], P(None, ('tensor', 'dp')), may hold values from -3 to 3
- fc2_weight: bfloat16 [2, 8192, 2048], P(None, 'tensor', 'dp'), may hold values from -0.0625 to 0.0625
- output_bias: bfloat16 [2, 2048], P(None, 'dp'), may hold values from -2 to 2
- out_cotangent: bfloat16 [2048, 2048], P('dp'), may hold values from -6 to 6
Outputs:
- hidden_out: bfloat16 [2048, 2048], P('dp')
- grad_hidden: float32 [2048, 2048], P('dp')
- grad_norm_gain: float32 [2, 2048], P(None, 'dp')
- grad_norm_bias: float32 [2, 2048], P(None, 'dp')
- grad_qkv_weight: float32 [2, 2048, 3, 2048], P(None, 'dp', None, 'tensor')
- grad_qkv_bias: float32 [2, 3, 2048], P(None, None, ('tensor', 'dp'))
- grad_out_weight: float32 [2, 2048, 2048], P(None, 'tensor', 'dp')
- grad_fc1_weight: float32 [2, 2048, 8192], P(None, 'dp', 'tensor')
- grad_fc1_bias: float32 [2, 8192], P(None, ('tensor', 'dp'))
- grad_fc2_weight: float32 [2, 8192, 2048], P(None, 'tensor', 'dp')
- grad_output_bias: float32 [2, 2048], P(None, 'dp')
Inputs may be any that keep to these rules, and one draw needn't show every extreme that they name: `seq_lengths`: the sequences of one device hold 128 tokens or fewer together, and some device holds a single sequence of exactly 128 tokens. `seq_device`: every device of dp holds between 1 and 7 sequences; both ends occur in every draw. `positions`: the j-th row of a sequence has the sequence's starting position plus j; padding rows have position 0.
All inputs are finite; a program needn't handle non-finite values.
Results may differ from a plain program's by a relative error of at most 0.02.
Values may be sent and summed in bfloat16 or wider, within the bound.
No kernel may reach another device: no remote copies, remote signals or barrier semaphores. Data moves between devices by JAX's collectives and lax.ppermute only.
A program may use at most 384 MiB of HBM per device.

v0:
```python
from functools import partial

import jax
import jax.numpy as jnp
from jax import lax
from jax.sharding import PartitionSpec as P

HEAD_DIM = 64
ROT = 32
LAYERS = 2


norm_epsilon = 1e-05
masked_score = -1e30


def sequence_labels(seq_lengths, seq_device, owner, count_rows):
    index = jnp.arange(seq_lengths.shape[0], dtype=jnp.int32)
    owned = jnp.where(seq_device == owner, seq_lengths, 0)
    earlier = index[None, :] < index[:, None]
    starts = jnp.sum(jnp.where(earlier, owned[None, :], 0), axis=1)
    places = jnp.arange(count_rows, dtype=jnp.int32)
    inside = (places[:, None] >= starts[None, :]) & (places[:, None] < (starts + owned)[None, :])
    return jnp.sum(jnp.where(inside, index[None, :] + 1, 0), axis=1)


def allowed_pairs(labels):
    places = jnp.arange(labels.shape[0], dtype=jnp.int32)
    same = (
        (labels[:, None] == labels[None, :])
        & (labels[:, None] > 0)
        & (places[None, :] <= places[:, None])
    )
    return same | (places[:, None] == places[None, :])


def rotate(field, positions):
    half = ROT // 2
    frequency = 10000.0 ** (-2.0 * jnp.arange(half, dtype=jnp.float32) / ROT)
    angles = positions.astype(jnp.float32)[:, None] * frequency[None, :]
    layout = (field.shape[0],) + (1,) * (field.ndim - 2) + (half,)
    cosine = jnp.cos(angles).reshape(layout)
    sine = jnp.sin(angles).reshape(layout)
    first = field[..., :half]
    second = field[..., half:ROT]
    return jnp.concatenate(
        [first * cosine - second * sine, second * cosine + first * sine, field[..., ROT:]], axis=-1
    )


def norm_piece(state, gain, shift):
    centre = jnp.mean(state, axis=1, keepdims=True)
    centered = state - centre
    spread = jnp.mean(centered * centered, axis=1, keepdims=True)
    return centered * lax.rsqrt(spread + norm_epsilon) * gain + shift


def per_device(
    hidden_in,
    seq_lengths,
    seq_device,
    positions,
    norm_gain,
    norm_bias,
    qkv_weight,
    qkv_bias,
    out_weight,
    fc1_weight,
    fc1_bias,
    fc2_weight,
    output_bias,
    out_cotangent,
):
    count_rows = hidden_in.shape[0]
    local_width = qkv_weight.shape[3]
    local_heads = local_width // HEAD_DIM
    scale = HEAD_DIM ** (-0.5)
    labels = sequence_labels(seq_lengths, seq_device, lax.axis_index("dp"), count_rows)
    allowed = allowed_pairs(labels)
    valid = (labels > 0).astype(jnp.float32)
    contract_last = (((1,), (1,)), ((), ()))
    contract_first = (((0,), (0,)), ((), ()))

    def head_forward(member):
        query_head, key_head, value_head = member
        scores = (
            lax.dot_general(query_head, key_head, contract_last, preferred_element_type=jnp.float32)
            * scale
        )
        masked = jnp.where(allowed, scores, masked_score)
        ceiling = jnp.max(masked, axis=1, keepdims=True)
        weights_exp = jnp.exp(masked - ceiling)
        totals = jnp.sum(weights_exp, axis=1, keepdims=True)
        chances = (weights_exp / totals).astype(jnp.bfloat16)
        mixed = jnp.dot(chances, value_head, preferred_element_type=jnp.float32)
        return (mixed.astype(jnp.bfloat16), ceiling[:, 0] + jnp.log(totals[:, 0]))

    def head_backward(member):
        query_head, key_head, value_head, grad_head, log_total = member
        scores = (
            lax.dot_general(query_head, key_head, contract_last, preferred_element_type=jnp.float32)
            * scale
        )
        masked = jnp.where(allowed, scores, masked_score)
        chances = jnp.exp(masked - log_total[:, None])
        grad_chances = lax.dot_general(
            grad_head, value_head, contract_last, preferred_element_type=jnp.float32
        )
        grad_value = lax.dot_general(
            chances.astype(jnp.bfloat16),
            grad_head,
            contract_first,
            preferred_element_type=jnp.float32,
        )
        centre = jnp.sum(grad_chances * chances, axis=1, keepdims=True)
        grad_scores = (chances * (grad_chances - centre)).astype(jnp.bfloat16)
        grad_query = jnp.dot(grad_scores, key_head, preferred_element_type=jnp.float32) * scale
        grad_key = (
            lax.dot_general(
                grad_scores, query_head, contract_first, preferred_element_type=jnp.float32
            )
            * scale
        )
        return (grad_query, grad_key, grad_value)

    state = hidden_in.astype(jnp.float32)
    kept = []
    for layer in range(LAYERS):
        gathered = (
            lax.all_gather(norm_gain[layer], "dp", axis=0, tiled=True),
            lax.all_gather(norm_bias[layer], "dp", axis=0, tiled=True),
            lax.all_gather(qkv_weight[layer], "dp", axis=0, tiled=True),
            lax.all_gather(qkv_bias[layer], "dp", axis=1, tiled=True),
            lax.all_gather(out_weight[layer], "dp", axis=1, tiled=True),
            lax.all_gather(fc1_weight[layer], "dp", axis=0, tiled=True),
            lax.all_gather(fc1_bias[layer], "dp", axis=0, tiled=True),
            lax.all_gather(fc2_weight[layer], "dp", axis=1, tiled=True),
            lax.all_gather(output_bias[layer], "dp", axis=0, tiled=True),
        )
        (
            gain_full,
            shift_full,
            proj_weight,
            proj_bias,
            mix_weight,
            up_weight,
            up_bias,
            down_weight,
            after_bias,
        ) = gathered
        normed_wide, norm_back = jax.vjp(
            norm_piece, state, gain_full.astype(jnp.float32), shift_full.astype(jnp.float32)
        )
        normed = normed_wide.astype(jnp.bfloat16)
        projected = jnp.einsum(
            "td,dpe->tpe", normed, proj_weight, preferred_element_type=jnp.float32
        ) + proj_bias.astype(jnp.float32)
        turned_wide, turn_back = jax.vjp(
            partial(rotate, positions=positions),
            projected[:, 0:2].reshape(count_rows, 2, local_heads, HEAD_DIM),
        )
        turned = turned_wide.astype(jnp.bfloat16).transpose(1, 2, 0, 3)
        value_heads = (
            projected[:, 2]
            .astype(jnp.bfloat16)
            .reshape(count_rows, local_heads, HEAD_DIM)
            .transpose(1, 0, 2)
        )
        mixed, log_totals = lax.map(head_forward, (turned[0], turned[1], value_heads))
        attended = mixed.transpose(1, 0, 2).reshape(count_rows, local_width)
        hidden_pre = jnp.dot(
            normed, up_weight, preferred_element_type=jnp.float32
        ) + up_bias.astype(jnp.float32)
        active_wide, gelu_back = jax.vjp(partial(jax.nn.gelu, approximate=True), hidden_pre)
        active = active_wide.astype(jnp.bfloat16)
        local_terms = jnp.dot(attended, mix_weight, preferred_element_type=jnp.float32) + jnp.dot(
            active, down_weight, preferred_element_type=jnp.float32
        )
        branch = lax.psum(local_terms.astype(jnp.bfloat16), "tensor").astype(jnp.float32)
        stored = None
        kept.append(
            (
                norm_back,
                normed,
                turned,
                turn_back,
                value_heads,
                log_totals,
                attended,
                gelu_back,
                active,
                stored,
            )
        )
        state = state + branch + after_bias.astype(jnp.float32)
    hidden_out = state.astype(jnp.bfloat16)
    grad_state = out_cotangent.astype(jnp.float32) * valid[:, None]
    collected = [None] * LAYERS
    for layer in reversed(range(LAYERS)):
        (
            norm_back,
            normed,
            turned,
            turn_back,
            value_heads,
            log_totals,
            attended,
            gelu_back,
            active,
            stored,
        ) = kept[layer]
        gathered = (
            lax.all_gather(norm_gain[layer], "dp", axis=0, tiled=True),
            lax.all_gather(norm_bias[layer], "dp", axis=0, tiled=True),
            lax.all_gather(qkv_weight[layer], "dp", axis=0, tiled=True),
            lax.all_gather(qkv_bias[layer], "dp", axis=1, tiled=True),
            lax.all_gather(out_weight[layer], "dp", axis=1, tiled=True),
            lax.all_gather(fc1_weight[layer], "dp", axis=0, tiled=True),
            lax.all_gather(fc1_bias[layer], "dp", axis=0, tiled=True),
            lax.all_gather(fc2_weight[layer], "dp", axis=1, tiled=True),
            lax.all_gather(output_bias[layer], "dp", axis=0, tiled=True),
        )
        (
            gain_full,
            shift_full,
            proj_weight,
            proj_bias,
            mix_weight,
            up_weight,
            up_bias,
            down_weight,
            after_bias,
        ) = gathered
        grad_branch = grad_state.astype(jnp.bfloat16)
        grad_after = jnp.sum(grad_state, axis=0)
        grad_down = jnp.einsum("tf,td->fd", active, grad_branch, preferred_element_type=jnp.float32)
        grad_mix = jnp.einsum(
            "te,td->ed", attended, grad_branch, preferred_element_type=jnp.float32
        )
        grad_active = jnp.einsum(
            "td,fd->tf", grad_branch, down_weight, preferred_element_type=jnp.float32
        )
        grad_pre = gelu_back(grad_active)[0].astype(jnp.bfloat16)
        grad_up_bias = jnp.sum(grad_pre, axis=0, dtype=jnp.float32)
        grad_up = jnp.einsum("td,tf->df", normed, grad_pre, preferred_element_type=jnp.float32)
        grad_normed = jnp.einsum(
            "tf,df->td", grad_pre, up_weight, preferred_element_type=jnp.float32
        )
        grad_attended = jnp.einsum(
            "td,ed->te", grad_branch, mix_weight, preferred_element_type=jnp.float32
        ).astype(jnp.bfloat16)
        grad_heads = grad_attended.reshape(count_rows, local_heads, HEAD_DIM).transpose(1, 0, 2)
        grad_query, grad_key, grad_value = lax.map(
            head_backward, (turned[0], turned[1], value_heads, grad_heads, log_totals)
        )
        grad_pair = jnp.stack([grad_query, grad_key], axis=0).transpose(2, 0, 1, 3)
        grad_turned = turn_back(grad_pair)[0].reshape(count_rows, 2, local_width)
        grad_values_rows = grad_value.transpose(1, 0, 2).reshape(count_rows, 1, local_width)
        grad_projected = jnp.concatenate([grad_turned, grad_values_rows], axis=1).astype(
            jnp.bfloat16
        )
        grad_proj_bias = jnp.sum(grad_projected, axis=0, dtype=jnp.float32)
        grad_proj_weight = jnp.einsum(
            "td,tpe->dpe", normed, grad_projected, preferred_element_type=jnp.float32
        )
        grad_normed = grad_normed + jnp.einsum(
            "tpe,dpe->td", grad_projected, proj_weight, preferred_element_type=jnp.float32
        )
        grad_normed = lax.psum(grad_normed.astype(jnp.bfloat16), "tensor").astype(jnp.float32)
        grad_input, grad_gain, grad_shift = norm_back(grad_normed)
        grad_state = grad_state + grad_input
        collected[layer] = (
            lax.psum_scatter(grad_gain, "dp", scatter_dimension=0, tiled=True),
            lax.psum_scatter(grad_shift, "dp", scatter_dimension=0, tiled=True),
            lax.psum_scatter(grad_proj_weight, "dp", scatter_dimension=0, tiled=True),
            lax.psum_scatter(grad_proj_bias, "dp", scatter_dimension=1, tiled=True),
            lax.psum_scatter(grad_mix, "dp", scatter_dimension=1, tiled=True),
            lax.psum_scatter(grad_up, "dp", scatter_dimension=0, tiled=True),
            lax.psum_scatter(grad_up_bias, "dp", scatter_dimension=0, tiled=True),
            lax.psum_scatter(grad_down, "dp", scatter_dimension=1, tiled=True),
            lax.psum_scatter(grad_after, "dp", scatter_dimension=0, tiled=True),
        )
    stacked = tuple(
        (
            jnp.stack([collected[layer][member] for layer in range(LAYERS)], axis=0)
            for member in range(9)
        )
    )
    return (
        hidden_out,
        grad_state,
        stacked[0],
        stacked[1],
        stacked[2],
        stacked[3],
        stacked[4],
        stacked[5],
        stacked[6],
        stacked[7],
        stacked[8],
    )


def solution(mesh):
    placed = (
        P("dp", None),
        P(),
        P(),
        P("dp"),
        P(None, "dp"),
        P(None, "dp"),
        P(None, "dp", None, "tensor"),
        P(None, None, ("tensor", "dp")),
        P(None, "tensor", "dp"),
        P(None, "dp", "tensor"),
        P(None, ("tensor", "dp")),
        P(None, "tensor", "dp"),
        P(None, "dp"),
        P("dp", None),
    )
    return jax.shard_map(
        per_device,
        mesh=mesh,
        in_specs=placed,
        out_specs=(
            P("dp", None),
            P("dp", None),
            P(None, "dp"),
            P(None, "dp"),
            P(None, "dp", None, "tensor"),
            P(None, None, ("tensor", "dp")),
            P(None, "tensor", "dp"),
            P(None, "dp", "tensor"),
            P(None, ("tensor", "dp")),
            P(None, "tensor", "dp"),
            P(None, "dp"),
        ),
        check_vma=False,
    )
```

profile of v0, /device:TPU:13, one launch (start us, length us, event | category | flops | bytes accessed | tf_op | source)
XLA Modules:
  0.0 3373.1 jit_solution(12605445387057670689)
XLA Ops:
  7.2 2.9 fusion.255
  11.8 3.0 fusion.254
  16.6 16.0 all-gather.6
  32.6 22.0 all-gather.1
  54.6 18.3 all-gather
  73.6 22.2 all-gather.3
  96.6 18.3 all-gather.27.cloned.1.call-done
  114.9 6.5 fusion.194
  123.2 8.0 while.56
  131.3 111.0 %all-gather.31.cloned.1.call-done = bf16[1,2048,4096]{2,1,0:T(8,128)(2,1)} async-done(((bf16[1,128,4096]{2,1,0:T(8,128)(2,1)}), bf16[1,2048,4096]{2,1,0:T(8,128)(2,1)}) %all-gather.31.cloned.1.call-update) | async-done | bytes 16777232 | tf_op jit(solution)/shard_map/all_gather | solution.py:135
  242.3 8.2 fusion.128
  250.6 122.4 %all-gather.33.cloned.1.call-done = bf16[1,4096,2048]{2,1,0:T(8,128)(2,1)} async-done(((bf16[1,4096,128]{2,1,0:T(8,128)(2,1)}), bf16[1,4096,2048]{2,1,0:T(8,128)(2,1)}) %all-gather.33.cloned.1.call-update) | async-done | bytes 16777232 | tf_op jit(solution)/shard_map/all_gather | solution.py:137
  373.0 9.4 fusion.114
  382.3 44.1 %all-gather.29.cloned.1.call-done = bf16[1,1024,2048]{2,1,0:T(8,128)(2,1)} async-done(((bf16[1,1024,128]{2,1,0:T(8,128)(2,1)}), bf16[1,1024,2048]{2,1,0:T(8,128)(2,1)}) %all-gather.29.cloned.1.call-update) | async-done | bytes 4194320 | tf_op jit(solution)/shard_map/all_gather | solution.py:134
  426.4 4.0 fusion.169
  433.0 17.8 all-gather.10
  450.8 19.0 all-gather.9
  470.3 17.6 all-gather.8
  487.9 18.8 all-gather.15
  506.9 19.5 all-gather.12
  526.8 3.7 fusion.206
  534.5 78.4 %all-gather.35.cloned.1.call-done = bf16[1,2048,3,1024]{3,1,2,0:T(8,128)(2,1)} async-done(((bf16[1,128,3,1024]{3,1,2,0:T(8,128)(2,1)}), bf16[1,2048,3,1024]{3,1,2,0:T(8,128)(2,1)}) %all-gather.35.cloned.1.call-update) | async-done | bytes 12582928 | tf_op jit(solution)/shard_map/all_gather | solution.py:132
  612.9 6.4 fusion.197
  620.4 2.5 copy.143
  628.6 32.2 while.57
  661.8 75.5 %while.58 = (s32[]{:T(128)}, f32[16,128,64]{1,2,0:T(8,128)S(1)}, f32[16,128,64]{1,2,0:T(8,128)S(1)}, bf16[16,128,64]{1,2,0:T(8,128)(2,1)S(1)}, bf16[16,128,64]{2...) while((s32[]{:T(128)}, f32[16,128,64]{1,2,0:T(8,128)S(1)}, ...), condition=%wide.region_18.19_spmd.clone, body=%wide.region_16.18_spmd.clone.sunk | while | flops 10747778 | bytes 795777 | solution.py:253
  739.8 9.6 fusion.131
  749.4 121.1 %all-gather.41.cloned.1.call-done = bf16[1,4096,2048]{2,1,0:T(8,128)(2,1)} async-done(((bf16[1,4096,128]{2,1,0:T(8,128)(2,1)}), bf16[1,4096,2048]{2,1,0:T(8,128)(2,1)}) %all-gather.41.cloned.1.call-update) | async-done | bytes 16777232 | tf_op jit(solution)/shard_map/all_gather | solution.py:137
  870.4 14.4 convert_reduce_fusion
  884.8 12.7 fusion.108
  897.5 10.2 fusion.163
  907.9 9.2 fusion.106
  918.7 18.3 all-reduce.23.cloned.1.call-done
  937.0 2.2 convert_reduce_fusion.5
  939.1 2.3 fusion.216
  946.1 75.4 %while.59 = (s32[]{:T(128)}, f32[16,128,64]{1,2,0:T(8,128)S(1)}, f32[16,128,64]{1,2,0:T(8,128)S(1)}, bf16[16,128,64]{1,2,0:T(8,128)(2,1)S(1)}, bf16[16,128,64]{2...) while((s32[]{:T(128)}, f32[16,128,64]{1,2,0:T(8,128)S(1)}, ...), condition=%wide.region_24.25_spmd.clone, body=%wide.region_22.24_spmd.clone.sunk | while | flops 10747778 | bytes 795777 | solution.py:253
  1025.8 2.1 add_convert_fusion
  1030.0 13.9 convert_reduce_fusion.1
  1043.9 12.7 fusion.116
  1056.6 10.3 fusion.160
  1071.7 35.5 %all-reduce.27.cloned.1.call-done = (bf16[128,2048]{1,0:T(8,128)(2,1)}, bf16[128,2048]{1,0:T(8,128)(2,1)}) async-done(((bf16[128,2048]{1,0:T(8,128)(2,1)}, bf16[128,2048]{1,0:T(8,128)(2,1)}), (bf16[128,2048]{1,0:T(8,128)(2,1)}, bf16[128,2048]{1,0:T(8,128)(2,1)})) %all-reduce.27.cloned.1.call-update) | async-done | bytes 1048592 | tf_op jit(solution)/shard_map/psum | solution.py:179
  1109.2 2.2 fusion.217
  1111.5 5.7 fusion.240
  1117.3 5.6 fusion.263
  1122.9 11.2 fusion.223
  1135.1 11.3 fusion.226
  1146.5 14.4 fusion.264
  1161.0 14.8 fusion.246
  1176.8 15.0 fusion.238
  1192.9 13.2 fusion.244
  1206.8 15.8 all-gather.17
  1228.6 89.3 %all-reduce.25.cloned.1.call-done = (f32[2048]{0:T(1024)}, f32[2048]{0:T(1024)}, f32[2048]{0:T(1024)}, f32[2048]{0:T(1024)}, f32[4096]{0:T(1024)}, /*index=5*/f32[4096]{0:T(1024)}, f32[2048]{0:T(1024)}, f32[2048]{0:T(1024)}) async-done(((f32[2048]{0:T(1024)}, f32[2048]{0:T(1024)}, f32[2048]{0:T(1024)}, f32[2048]{0:T(1024)}, f32[4096]{0:T(1024)}, /*index=5*/f32[4096]{0:T(1024)}, f32[2048]{0:T(1024)}, ...) | async-done | bytes 81936
  1324.0 102.9 %reduce-scatter.21.cloned.1.call-done = f32[1024,128]{1,0:T(8,128)} async-done(((f32[1024,2048]{1,0:T(8,128)}), f32[1024,128]{1,0:T(8,128)}) %reduce-scatter.21.cloned.1.call-update) | async-done | bytes 524304 | tf_op jit(solution)/shard_map/reduce_scatter | solution.py:277
  1426.9 107.2 %reduce-scatter.19.cloned.1.call-done = f32[1024,128]{1,0:T(8,128)} async-done(((f32[1024,2048]{1,0:T(8,128)}), f32[1024,128]{1,0:T(8,128)}) %reduce-scatter.19.cloned.1.call-update) | async-done | bytes 524304 | tf_op jit(solution)/shard_map/reduce_scatter | solution.py:277
  1534.1 2.2 pad_maximum_fusion.3
  1536.3 243.0 %reduce-scatter.17.cloned.1.call-done = f32[128,3,1024]{2,0,1:T(8,128)} async-done(((f32[2048,3,1024]{2,0,1:T(8,128)}), f32[128,3,1024]{2,0,1:T(8,128)}) %reduce-scatter.17.cloned.1.call-update) | async-done | bytes 1572880 | tf_op jit(solution)/shard_map/reduce_scatter | solution.py:275
  1779.3 246.4 %reduce-scatter.15.cloned.1.call-done = f32[128,3,1024]{2,0,1:T(8,128)} async-done(((f32[2048,3,1024]{2,0,1:T(8,128)}), f32[128,3,1024]{2,0,1:T(8,128)}) %reduce-scatter.15.cloned.1.call-update) | async-done | bytes 1572880 | tf_op jit(solution)/shard_map/reduce_scatter | solution.py:275
  2025.7 4.0 pad_maximum_fusion.2
  2029.7 330.6 %reduce-scatter.25.cloned.1.call-done = f32[128,4096]{1,0:T(8,128)} async-done(((f32[2048,4096]{1,0:T(8,128)}), f32[128,4096]{1,0:T(8,128)}) %reduce-scatter.25.cloned.1.call-update) | async-done | bytes 2097168 | tf_op jit(solution)/shard_map/reduce_scatter | solution.py:278
  2360.3 333.7 %reduce-scatter.23.cloned.1.call-done = f32[128,4096]{1,0:T(8,128)} async-done(((f32[2048,4096]{1,0:T(8,128)}), f32[128,4096]{1,0:T(8,128)}) %reduce-scatter.23.cloned.1.call-update) | async-done | bytes 2097168 | tf_op jit(solution)/shard_map/reduce_scatter | solution.py:278
  2694.0 4.7 pad_maximum_fusion
  2698.7 329.0 %reduce-scatter.29.cloned.1.call-done = f32[4096,128]{1,0:T(8,128)} async-done(((f32[4096,2048]{1,0:T(8,128)}), f32[4096,128]{1,0:T(8,128)}) %reduce-scatter.29.cloned.1.call-update) | async-done | bytes 2097168 | tf_op jit(solution)/shard_map/reduce_scatter | solution.py:280
  3027.7 333.7 %reduce-scatter.27.cloned.1.call-done = f32[4096,128]{1,0:T(8,128)} async-done(((f32[4096,2048]{1,0:T(8,128)}), f32[4096,128]{1,0:T(8,128)}) %reduce-scatter.27.cloned.1.call-update) | async-done | bytes 2097168 | tf_op jit(solution)/shard_map/reduce_scatter | solution.py:280
  3361.3 4.5 pad_maximum_fusion.1
  (635 shorter events, 246.7 us)
Async XLA Ops:
  7.2 3.1 copy-start.25
  7.2 107.7 %all-gather.27.cloned.1.call-start = ((), (), s32[]{:S(2)}) async-start(), calls=%async_computation.20 | async-start | bytes 13369344 | tf_op jit(solution)/shard_map/all_gather | solution.py:132
  10.2 232.1 %all-gather.31.cloned.1.call-start = ((), (), s32[]{:S(2)}) async-start(), calls=%async_computation.22 | async-start | bytes 17825792 | tf_op jit(solution)/shard_map/all_gather | solution.py:135
  11.7 3.2 copy-start.35
  11.7 361.2 %all-gather.33.cloned.1.call-start = ((), (), s32[]{:S(2)}) async-start(), calls=%async_computation.23 | async-start | bytes 17825792 | tf_op jit(solution)/shard_map/all_gather | solution.py:137
  14.8 1.7 copy-start.38
  14.8 1.7 copy-start.39
  14.8 1.7 copy-start.37
  14.8 58.1 %copy-start = (bf16[128,2048]{1,0:T(8,128)(2,1)S(1)}, bf16[128,2048]{1,0:T(8,128)(2,1)}, u32[]{:S(2)}) copy-start(bf16[128,2048]{1,0:T(8,128)(2,1)} %param.22) | copy-start | bytes 1572868
  14.8 58.6 %copy-start.36 = (bf16[2,3,64]{2,0,1:T(2,128)(2,1)S(1)}, bf16[2,3,64]{2,0,1:T(2,128)(2,1)}, u32[]{:S(2)}) copy-start(bf16[2,3,64]{2,0,1:T(2,128)(2,1)} %param.29) | copy-start | bytes 2308
  14.9 81.3 %copy-start.44 = (s32[128]{0:T(128)S(1)}, s32[128]{0:T(128)}, u32[]{:S(2)}) copy-start(s32[128]{0:T(128)} %param.25) | copy-start | bytes 1540
  14.9 81.3 %copy-start.42 = (s32[64]{0:T(128)S(1)}, s32[64]{0:T(128)}, u32[]{:S(2)}) copy-start(s32[64]{0:T(128)} %param.23) | copy-start | bytes 772
  14.9 81.3 %copy-start.43 = (s32[64]{0:T(128)S(1)}, s32[64]{0:T(128)}, u32[]{:S(2)}) copy-start(s32[64]{0:T(128)} %param.24) | copy-start | bytes 772
  14.9 411.5 %all-gather.29.cloned.1.call-start = ((), (), s32[]{:S(2)}) async-start(), calls=%async_computation.21 | async-start | bytes 4456448 | tf_op jit(solution)/shard_map/all_gather | solution.py:134
  15.8 510.9 %all-gather.37.cloned.1.call-start = ((), (), s32[]{:S(2)}) async-start(), calls=%async_computation.25 | async-start | bytes 4456448 | tf_op jit(solution)/shard_map/all_gather | solution.py:134
  16.4 515.0 %all-reduce.21.cloned.1.call-start = ((), (), s32[]{:S(2)}) async-start(), calls=%async_computation.10 | async-start | bytes 1048576 | tf_op jit(solution)/shard_map/psum | solution.py:179
  131.2 111.1 %copy-start.28 = (bf16[16,128,64]{2,1,0:T(8,128)(2,1)}, bf16[16,128,64]{2,1,0:T(8,128)(2,1)S(1)}, u32[]{:S(2)}) copy-start(bf16[16,128,64]{2,1,0:T(8,128)(2,1)S(1)} %get-tuple-element.1125) | copy-start | bytes 786436
  131.3 111.0 %copy-start.29 = (bf16[16,128,64]{2,1,0:T(8,128)(2,1)}, bf16[16,128,64]{2,1,0:T(8,128)(2,1)S(1)}, u32[]{:S(2)}) copy-start(bf16[16,128,64]{2,1,0:T(8,128)(2,1)S(1)} %get-tuple-element.1126) | copy-start | bytes 786436
  131.3 119.3 %copy-start.31 = (bf16[16,128,64]{2,1,0:T(8,128)(2,1)}, bf16[16,128,64]{2,1,0:T(8,128)(2,1)S(1)}, u32[]{:S(2)}) copy-start(bf16[16,128,64]{2,1,0:T(8,128)(2,1)S(1)} %get-tuple-element.1129) | copy-start | bytes 786436
  131.3 295.1 %copy-start.20 = (bf16[16,128,64]{1,2,0:T(8,128)(2,1)}, bf16[16,128,64]{1,2,0:T(8,128)(2,1)S(1)}, u32[]{:S(2)}) copy-start(bf16[16,128,64]{1,2,0:T(8,128)(2,1)S(1)} %get-tuple-element.195) | copy-start | bytes 786436
  250.6 131.8 %copy-start.5 = (f32[128,4096]{1,0:T(8,128)}, f32[128,4096]{1,0:T(8,128)S(1)}, u32[]{:S(2)}) copy-start(f32[128,4096]{1,0:T(8,128)S(1)} %fusion.128) | copy-start | bytes 6291460
  430.4 39.3 %copy-start.40 = (bf16[2,128]{1,0:T(2,128)(2,1)S(1)}, bf16[2,128]{1,0:T(2,128)(2,1)}, u32[]{:S(2)}) copy-start(bf16[2,128]{1,0:T(2,128)(2,1)} %param.34) | copy-start | bytes 1540
  430.5 182.5 %all-gather.35.cloned.1.call-start = ((), (), s32[]{:S(2)}) async-start(), calls=%async_computation.24 | async-start | bytes 13369344 | tf_op jit(solution)/shard_map/all_gather | solution.py:132
  431.2 95.6 %copy-start.11 = (bf16[128,2048]{1,0:T(8,128)(2,1)S(1)}, bf16[128,2048]{1,0:T(8,128)(2,1)}, u32[]{:S(2)}) copy-start(bf16[128,2048]{1,0:T(8,128)(2,1)} %param.35) | copy-start | bytes 1572868
  431.2 308.5 %all-gather.39.cloned.1.call-start = ((), (), s32[]{:S(2)}) async-start(), calls=%async_computation.26 | async-start | bytes 17825792 | tf_op jit(solution)/shard_map/all_gather | solution.py:135
  432.0 438.4 %all-gather.41.cloned.1.call-start = ((), (), s32[]{:S(2)}) async-start(), calls=%async_computation.27 | async-start | bytes 17825792 | tf_op jit(solution)/shard_map/all_gather | solution.py:137
  432.7 504.3 %all-reduce.23.cloned.1.call-start = ((), (), s32[]{:S(2)}) async-start(), calls=%async_computation.11 | async-start | bytes 1048576 | tf_op jit(solution)/shard_map/psum | solution.py:269
  433.0 97.5 %copy-start.21 = (bf16[16,128,64]{1,2,0:T(8,128)(2,1)}, bf16[16,128,64]{1,2,0:T(8,128)(2,1)S(1)}, u32[]{:S(2)}) copy-start(bf16[16,128,64]{1,2,0:T(8,128)(2,1)S(1)} %fusion.256) | copy-start | bytes 786436
  487.9 453.5 %copy-start.32 = (f32[1,2048]{1,0:T(1,128)}, f32[1,2048]{1,0:T(1,128)S(1)}, u32[]{:S(2)}) copy-start(f32[1,2048]{1,0:T(1,128)S(1)} %convert_element_type.197) | copy-start | bytes 24580
  531.4 2.8 copy-start.1
  626.0 1.4 copy-start.27
  628.6 33.1 copy-start.24
  660.9 0.9 copy-start.18
  739.7 157.8 %copy-start.14 = (bf16[128,2,1024]{2,0,1:T(8,128)(2,1)}, bf16[128,2,1024]{2,0,1:T(8,128)(2,1)S(1)}, u32[]{:S(2)}) copy-start(bf16[128,2,1024]{2,0,1:T(8,128)(2,1)S(1)} %copy.153) | copy-start | bytes 1572868
  739.7 130.7 %copy-start.12 = (bf16[128,2048]{1,0:T(8,128)(2,1)S(1)}, bf16[128,2048]{1,0:T(8,128)(2,1)}, u32[]{:S(2)}) copy-start(bf16[128,2048]{1,0:T(8,128)(2,1)} %param.35) | copy-start | bytes 1572868
  907.8 9.3 copy-start.19
  907.8 199.4 %all-reduce.27.cloned.1.call-start = ((), (), s32[]{:S(2)}) async-start(), calls=%async_computation.31 | async-start | bytes 2097152 | tf_op jit(solution)/shard_map/psum | solution.py:179
  907.9 9.2 copy-start.3
  937.0 4.4 copy-start.16
  941.4 2.2 copy-start.4
  942.8 2.4 copy-start.7
  943.6 1.5 copy-start.9
  943.6 2.5 copy-start.22
  1023.2 6.8 copy-start.6
  1066.9 157.5 %reduce-scatter.33.cloned.1.call-start = ((), (), s32[]{:S(2)}) async-start(), calls=%async_computation.29 | async-start | bytes 557056
  1069.2 156.1 %reduce-scatter.31.cloned.1.call-start = ((), (), s32[]{:S(2)}) async-start(), calls=%async_computation.28 | async-start | bytes 557056
  1071.6 246.3 %all-reduce.25.cloned.1.call-start = ((), (), s32[]{:S(2)}) async-start(), calls=%async_computation.30 | async-start | bytes 163840
  1111.5 315.4 %reduce-scatter.21.cloned.1.call-start = ((), (), s32[]{:S(2)}) async-start(), calls=%async_computation.15 | async-start | bytes 8912896 | tf_op jit(solution)/shard_map/reduce_scatter | solution.py:277
  1117.2 416.9 %reduce-scatter.19.cloned.1.call-start = ((), (), s32[]{:S(2)}) async-start(), calls=%async_computation.14 | async-start | bytes 8912896 | tf_op jit(solution)/shard_map/reduce_scatter | solution.py:277
  1122.9 656.4 %reduce-scatter.17.cloned.1.call-start = ((), (), s32[]{:S(2)}) async-start(), calls=%async_computation.13 | async-start | bytes 26738688 | tf_op jit(solution)/shard_map/reduce_scatter | solution.py:275
  1134.2 0.9 copy-start.17
  1134.2 891.5 %reduce-scatter.15.cloned.1.call-start = ((), (), s32[]{:S(2)}) async-start(), calls=%async_computation.12 | async-start | bytes 26738688 | tf_op jit(solution)/shard_map/reduce_scatter | solution.py:275
  1146.4 1213.9 %reduce-scatter.25.cloned.1.call-start = ((), (), s32[]{:S(2)}) async-start(), calls=%async_computation.17 | async-start | bytes 35651584 | tf_op jit(solution)/shard_map/reduce_scatter | solution.py:278
  1160.9 1533.1 %reduce-scatter.23.cloned.1.call-start = ((), (), s32[]{:S(2)}) async-start(), calls=%async_computation.16 | async-start | bytes 35651584 | tf_op jit(solution)/shard_map/reduce_scatter | solution.py:278
  1175.8 1.0 copy-start.13
  1175.8 1851.9 %reduce-scatter.29.cloned.1.call-start = ((), (), s32[]{:S(2)}) async-start(), calls=%async_computation.19 | async-start | bytes 35651584 | tf_op jit(solution)/shard_map/reduce_scatter | solution.py:280
  1191.9 1.0 copy-start.10
  1191.9 2169.5 %reduce-scatter.27.cloned.1.call-start = ((), (), s32[]{:S(2)}) async-start(), calls=%async_computation.18 | async-start | bytes 35651584 | tf_op jit(solution)/shard_map/reduce_scatter | solution.py:280
  1206.1 16.4 copy-start.45
  1206.1 20.6 copy-start.2
  1206.1 20.6 copy-start.8
  1206.1 20.6 copy-start.15
  1206.1 20.6 copy-start.33
  1206.1 20.6 copy-start.34
  (4 other events, 3.0 us)
Sparse Core Ops, SparseCore 0:
  10.3 104.5 all-gather.26
  117.6 124.6 all-gather.30
  245.0 127.8 all-gather.32
  375.6 50.8 all-gather.28
  428.4 50.6 all-gather.36
  481.8 28.8 all-reduce.20
  513.4 99.4 all-gather.34
  615.7 123.9 all-gather.38
  742.4 127.9 all-gather.40
  907.9 29.0 all-reduce.22
  1067.1 40.0 all-reduce.26
  1111.2 53.9 reduce-scatter.32
  1168.8 55.2 reduce-scatter.30
  1228.4 89.4 all-reduce.24
  1321.8 105.0 reduce-scatter.20
  1430.8 103.2 reduce-scatter.18
  1538.0 241.2 reduce-scatter.16
  1783.3 242.3 reduce-scatter.14
  2030.0 330.2 reduce-scatter.24
  2364.4 329.5 reduce-scatter.22
  2698.2 329.3 reduce-scatter.28
  3031.9 329.3 reduce-scatter.26
where the time goes:
time: 3400 us; the launch traced here: 3370 us
  waiting for transfers between devices  2670 us (79%)
  matrix products  411 us (12%)
  blocking collectives  187 us (6%)
  other arithmetic  43.9 us (1%)
  local copies, waits for them, and re-layouts  43.3 us (1%)
    reduce_scatter x2, waiting for transfers between devices, per_device(): lax.psum_scatter(grad_up, 'dp', scatter_dimension=0, tiled=True)  664 us
    reduce_scatter x2, waiting for transfers between devices, per_device(): lax.psum_scatter(grad_down, 'dp', scatter_dimension=1, tiled=True)  663 us
    reduce_scatter x2, waiting for transfers between devices, per_device(): lax.psum_scatter(grad_proj_weight, 'dp', scatter_dimension=0, tiled=True)  489 us
    all_gather x2, waiting for transfers between devices, per_device(): lax.all_gather(fc2_weight[layer], 'dp', axis=1, tiled=True)  243 us
    reduce_scatter x2, waiting for transfers between devices, per_device(): lax.psum_scatter(grad_mix, 'dp', scatter_dimension=1, tiled=True)  210 us
    all_gather x2, waiting for transfers between devices, per_device(): lax.all_gather(fc1_weight[layer], 'dp', axis=0, tiled=True)  111 us
    all_gather x2, waiting for transfers between devices, per_device(): lax.all_gather(qkv_weight[layer], 'dp', axis=0, tiled=True)  96.7 us
    unnamed x25, waiting for transfers between devices  92.2 us
  transfers between devices with their start and end apart: 22, of which 17 were waited for; matrix products, arithmetic and copies ran while one was open for 9% of the time, Pallas kernels for 0%

commit v1 on v0

v1 whole, which is shorter than its diff:
```python
from functools import partial

import jax
import jax.numpy as jnp
from jax import lax
from jax.experimental import pallas as pl
from jax.experimental.pallas import tpu as pltpu
from jax.sharding import PartitionSpec as P

HEAD_DIM = 64
ROT = 32
LAYERS = 2
GROUP = 16

norm_epsilon = 1e-05
masked_score = -1e30
bf16 = jnp.bfloat16
f32 = jnp.float32

contract_last = (((1,), (1,)), ((), ()))
contract_first = (((0,), (0,)), ((), ()))


def dot(a, b, dims=(((1,), (0,)), ((), ()))):
    return lax.dot_general(a, b, dims, preferred_element_type=f32)


def turn(x, cosine, up, down):
    return x * cosine + pltpu.roll(x, x.shape[1] - ROT // 2, 1) * up + pltpu.roll(x, ROT // 2, 1) * down


def stacked_heads(x):
    lane = lax.broadcasted_iota(jnp.int32, x.shape, 1)
    zero = jnp.zeros_like(x)
    return jnp.concatenate(
        [jnp.where(lane < HEAD_DIM, x, zero), jnp.where(lane < HEAD_DIM, zero, x)], axis=0
    )


def merged_heads(x):
    rows = x.shape[0] // 2
    lane = lax.broadcasted_iota(jnp.int32, (rows, x.shape[1]), 1)
    return jnp.where(lane < HEAD_DIM, x[:rows], x[rows:])


def softmax_rows(queries, keys, allowed):
    scores = dot(stacked_heads(queries), keys, contract_last) * HEAD_DIM ** (-0.5)
    masked = jnp.where(jnp.concatenate([allowed, allowed], axis=0) > 0, scores, masked_score)
    weights = jnp.exp(masked - jnp.max(masked, axis=1, keepdims=True))
    return weights / jnp.sum(weights, axis=1, keepdims=True)


def attention_forward(proj_ref, cos_ref, up_ref, down_ref, allowed_ref, kept_ref, out_ref):
    wide = 2 * HEAD_DIM
    tables = (cos_ref[...], up_ref[...], down_ref[...])
    queries = turn(proj_ref[:, :wide], *tables).astype(bf16)
    keys = turn(proj_ref[:, wide : 2 * wide], *tables).astype(bf16)
    values = proj_ref[:, 2 * wide :].astype(bf16)
    kept_ref[:, :wide] = queries
    kept_ref[:, wide : 2 * wide] = keys
    kept_ref[:, 2 * wide :] = values
    chances = softmax_rows(queries, keys, allowed_ref[...]).astype(bf16)
    out_ref[...] = merged_heads(dot(chances, values)).astype(bf16)


def attention_backward(kept_ref, grad_ref, cos_ref, up_ref, down_ref, allowed_ref, out_ref):
    wide = 2 * HEAD_DIM
    queries = kept_ref[:, :wide]
    keys = kept_ref[:, wide : 2 * wide]
    values = kept_ref[:, 2 * wide :]
    chances = softmax_rows(queries, keys, allowed_ref[...])
    grads = stacked_heads(grad_ref[...])
    grad_chances = dot(grads, values, contract_last)
    grad_values = dot(chances.astype(bf16), grads, contract_first)
    centre = jnp.sum(grad_chances * chances, axis=1, keepdims=True)
    grad_scores = (chances * (grad_chances - centre)).astype(bf16)
    scale = HEAD_DIM ** (-0.5)
    grad_queries = merged_heads(dot(grad_scores, keys)) * scale
    grad_keys = dot(grad_scores, stacked_heads(queries), contract_first) * scale
    tables = (cos_ref[...], -up_ref[...], -down_ref[...])
    out_ref[:, :wide] = turn(grad_queries, *tables).astype(bf16)
    out_ref[:, wide : 2 * wide] = turn(grad_keys, *tables).astype(bf16)
    out_ref[:, 2 * wide :] = grad_values.astype(bf16)


def row_blocks(rows, width):
    return pl.BlockSpec((rows, width), lambda i: (i, 0))


def call_forward(proj, tables, allowed, block):
    wide = 2 * HEAD_DIM
    rows = proj.shape[0]
    return pl.pallas_call(
        attention_forward,
        grid=(rows // block,),
        in_specs=[row_blocks(block, 3 * wide)] + [row_blocks(block, wide)] * 3 + [row_blocks(block, block)],
        out_specs=[row_blocks(block, 3 * wide), row_blocks(block, wide)],
        out_shape=[
            jax.ShapeDtypeStruct((rows, 3 * wide), bf16),
            jax.ShapeDtypeStruct((rows, wide), bf16),
        ],
        cost_estimate=pl.CostEstimate(flops=rows * block * wide * 8, bytes_accessed=rows * 6000, transcendentals=rows * block * 2),
        name="attention_forward",
    )(proj, *tables, allowed)


def call_backward(kept, grad, tables, allowed, block):
    wide = 2 * HEAD_DIM
    rows = kept.shape[0]
    return pl.pallas_call(
        attention_backward,
        grid=(rows // block,),
        in_specs=[row_blocks(block, 3 * wide), row_blocks(block, wide)]
        + [row_blocks(block, wide)] * 3
        + [row_blocks(block, block)],
        out_specs=row_blocks(block, 3 * wide),
        out_shape=jax.ShapeDtypeStruct((rows, 3 * wide), bf16),
        cost_estimate=pl.CostEstimate(flops=rows * block * wide * 20, bytes_accessed=rows * 6000, transcendentals=rows * block * 2),
        name="attention_backward",
    )(kept, grad, *tables, allowed)


def sequence_labels(seq_lengths, seq_device, owner, count_rows):
    index = jnp.arange(seq_lengths.shape[0], dtype=jnp.int32)
    owned = jnp.where(seq_device == owner, seq_lengths, 0)
    earlier = index[None, :] < index[:, None]
    starts = jnp.sum(jnp.where(earlier, owned[None, :], 0), axis=1)
    places = jnp.arange(count_rows, dtype=jnp.int32)
    inside = (places[:, None] >= starts[None, :]) & (places[:, None] < (starts + owned)[None, :])
    return jnp.sum(jnp.where(inside, index[None, :] + 1, 0), axis=1)


def gelu_parts(v):
    c = (2.0 / jnp.pi) ** 0.5
    inner = jnp.tanh(c * (v + 0.044715 * v * v * v))
    value = 0.5 * v * (1.0 + inner)
    slope = 0.5 * (1.0 + inner) + 0.5 * v * (1.0 - inner * inner) * c * (1.0 + 3.0 * 0.044715 * v * v)
    return value, slope


def per_device(
    n_dp,
    hidden_in,
    seq_lengths,
    seq_device,
    positions,
    norm_gain,
    norm_bias,
    qkv_weight,
    qkv_bias,
    out_weight,
    fc1_weight,
    fc1_bias,
    fc2_weight,
    output_bias,
    out_cotangent,
):
    block = hidden_in.shape[0]
    half = block // 2
    width = hidden_in.shape[1]
    piece = norm_gain.shape[1]
    hidden = fc1_weight.shape[2] // GROUP
    groups = n_dp // GROUP
    chips = GROUP // 2
    side = chips // 2 - 1

    if groups == 1:
        ring = [2 * a for a in range(chips // 2)] + [2 * a + 1 for a in reversed(range(chips // 2))]
    else:
        ring = list(range(chips // 2)) + list(reversed(range(chips // 2, chips)))
    ring_pairs = []
    for g in range(groups):
        for place in range(chips):
            for core, step in ((0, 1), (1, -1)):
                ring_pairs.append(
                    (
                        g * GROUP + ring[place] * 2 + core,
                        g * GROUP + ring[(place + step) % chips] * 2 + core,
                    )
                )
    core_pairs = [(i, i ^ 1) for i in range(n_dp)]
    inner = [[g * GROUP + i for i in range(GROUP)] for g in range(groups)]
    outer = [[g * GROUP + i for g in range(groups)] for i in range(GROUP)]
    if groups == 1:
        inner = None

    def along(x):
        return lax.ppermute(x, "dp", ring_pairs)

    def across(x):
        return lax.ppermute(x, "dp", core_pairs)

    def over(x):
        return lax.ppermute(x, "tensor", [(0, 1), (1, 0)])

    index = lax.axis_index("dp")
    group = index // GROUP
    chip = (index % GROUP) // 2
    core = index % 2
    tensor = lax.axis_index("tensor")
    is_first = core == 0
    at = core * half
    off = (1 - core) * half

    def my_half(x, start, axis=0):
        return lax.dynamic_slice_in_dim(x, start, half, axis)

    def in_order(own, other):
        return jnp.where(
            is_first, jnp.concatenate([own, other], 0), jnp.concatenate([other, own], 0)
        )

    def gather_rows(x):
        mine = in_order(x, across(x))
        behind, ahead = [], []
        moving = mine
        for _ in range(side):
            moving = along(moving)
            behind.append(moving)
            ahead.append(across(moving))
        moving = along(my_half(moving, at))
        far = in_order(moving, across(moving))
        return jnp.concatenate([mine] + behind + ahead + [far], axis=0)

    def scatter_rows(partial):
        slots = partial.reshape(chips, block, width)
        give = jnp.concatenate(
            [slots[1 : 1 + side].reshape(side * block, width), my_half(slots[chips - 1], off), my_half(slots[0], off)], 0
        ).astype(bf16)
        took = across(give).astype(f32)
        ahead = slots[1 + side : 1 + 2 * side].astype(f32) + took[: side * block].reshape(side, block, width)
        far = my_half(slots[chips - 1], at).astype(f32) + took[side * block : side * block + half]
        own = my_half(slots[0], at).astype(f32) + took[side * block + half :]
        moving = along(far.astype(bf16)).astype(f32)
        rows = lax.broadcasted_iota(jnp.int32, (block, 1), 0)
        mine_rows = (rows < half) == is_first
        moving = jnp.where(mine_rows, jnp.concatenate([moving, moving], 0), 0.0)
        for step in reversed(range(side)):
            moving = along((moving + ahead[step]).astype(bf16)).astype(f32)
        return own + my_half(moving, at) + across(my_half(moving, off).astype(bf16)).astype(f32)

    def spread(x):
        return lax.all_to_all(x, "dp", 0, 0, axis_index_groups=inner, tiled=True)

    def whole(x):
        if groups > 1:
            x = lax.all_gather(x, "dp", axis=0, axis_index_groups=outer, tiled=True)
        return x.transpose(1, 0, 2).reshape(x.shape[1], width)

    gathered_up, gathered_down = [], []
    for layer in range(LAYERS):
        up = jnp.concatenate(
            [
                qkv_weight[layer].reshape(piece, 3, GROUP, HEAD_DIM).transpose(2, 1, 3, 0).reshape(GROUP, 3 * HEAD_DIM, piece),
                fc1_weight[layer].reshape(piece, GROUP, hidden).transpose(1, 2, 0),
            ],
            axis=1,
        )
        down = jnp.concatenate(
            [
                out_weight[layer].reshape(GROUP, HEAD_DIM, piece),
                fc2_weight[layer].reshape(GROUP, hidden, piece),
            ],
            axis=1,
        )
        up = spread(up)
        up_other = over(up)
        down = spread(down)
        down_other = over(down)
        up, up_other, down, down_other = (whole(x) for x in (up, up_other, down, down_other))
        parts = []
        for p in range(3):
            parts += [up[p * HEAD_DIM : (p + 1) * HEAD_DIM], up_other[p * HEAD_DIM : (p + 1) * HEAD_DIM]]
        gathered_up.append(
            (
                jnp.concatenate(parts, 0),
                jnp.concatenate([up[3 * HEAD_DIM :], up_other[3 * HEAD_DIM :]], 0),
            )
        )
        gathered_down.append(
            (
                jnp.concatenate([down[:HEAD_DIM], down_other[:HEAD_DIM]], 0),
                jnp.concatenate([down[HEAD_DIM:], down_other[HEAD_DIM:]], 0),
            )
        )
    if groups == 1:
        biases = jnp.concatenate([qkv_bias.reshape(LAYERS, 3 * HEAD_DIM), fc1_bias], axis=1)
    else:
        full_qkv = lax.all_gather(qkv_bias, "dp", axis=2, tiled=True)
        full_up = lax.all_gather(fc1_bias, "dp", axis=1, tiled=True)
        member = index % GROUP
        biases = jnp.concatenate(
            [
                lax.dynamic_slice_in_dim(full_qkv, member * HEAD_DIM, HEAD_DIM, 2).reshape(LAYERS, 3 * HEAD_DIM),
                lax.dynamic_slice_in_dim(full_up, member * hidden, hidden, 1),
            ],
            axis=1,
        )
    biases_other = over(biases)
    small = jnp.concatenate(
        [
            norm_gain.reshape(-1),
            norm_bias.reshape(-1),
            output_bias.reshape(-1),
            (positions // 64).astype(bf16),
            (positions % 64).astype(bf16),
        ]
    )
    small = lax.all_gather(small, "dp", axis=0, tiled=False)
    vectors = small[:, : 6 * piece].reshape(n_dp, 3, LAYERS, piece).transpose(1, 2, 0, 3).reshape(3, LAYERS, width).astype(f32)
    gains, shifts, after = vectors[0], vectors[1], vectors[2]

    turned = jnp.where(is_first, 1, -1)
    place = jnp.sum(jnp.where(jnp.asarray(ring) == chip, jnp.arange(chips), 0))
    offsets = [0] + [-(s + 1) for s in range(side)] + [s + 1 for s in range(side)] + [chips // 2]
    places = (place + turned * jnp.asarray(offsets)) % chips
    chip_ids = jnp.sum(
        jnp.where(places[:, None] == jnp.arange(chips)[None, :], jnp.asarray(ring)[None, :], 0), axis=1
    )
    owners = group * GROUP + 2 * chip_ids + tensor
    labels = jax.vmap(lambda owner: sequence_labels(seq_lengths, seq_device, owner, block))(owners)
    rows_at = jnp.arange(block, dtype=jnp.int32)
    allowed = (
        (labels[:, :, None] == labels[:, None, :])
        & (labels[:, :, None] > 0)
        & (rows_at[None, None, :] <= rows_at[None, :, None])
    ) | (rows_at[None, None, :] == rows_at[None, :, None])
    allowed = allowed.astype(f32).reshape(chips * block, block)
    valid = my_half((labels[0] > 0).astype(f32)[:, None], at)
    picked = (owners[:, None] == jnp.arange(n_dp)[None, :]).astype(f32)
    place_parts = jnp.dot(picked, small[:, 6 * piece :].astype(f32), precision=lax.Precision.HIGHEST)
    row_places = (place_parts[:, :block] * 64.0 + place_parts[:, block:]).reshape(chips * block)
    pair = ROT // 2
    frequency = 10000.0 ** (-2.0 * jnp.arange(pair, dtype=f32) / ROT)
    angles = row_places[:, None] * frequency[None, :]
    cosine, sine = jnp.cos(angles), jnp.sin(angles)
    nought = jnp.zeros_like(sine)
    rest = jnp.zeros((chips * block, HEAD_DIM - ROT), f32)
    tables = (
        jnp.concatenate([cosine, cosine, rest + 1.0] * 2, axis=1),
        jnp.concatenate([-sine, nought, rest] * 2, axis=1),
        jnp.concatenate([nought, sine, rest] * 2, axis=1),
    )

    both = jnp.stack([hidden_in, out_cotangent])
    start = jnp.where(tensor == core, my_half(both, at, 1), across(my_half(both, off, 1)))
    state = start[0].astype(f32)
    kept = []
    for layer in range(LAYERS):
        weight_qkv, weight_up = gathered_up[layer]
        weight_out, weight_down = gathered_down[layer]
        mean = jnp.mean(state, axis=1, keepdims=True)
        centred = state - mean
        spread_rows = jnp.mean(centred * centred, axis=1, keepdims=True)
        inverse = lax.rsqrt(spread_rows + norm_epsilon)
        xhat = centred * inverse
        normed = gather_rows((xhat * gains[layer] + shifts[layer]).astype(bf16))
        bias_qkv = jnp.stack(
            [
                biases[layer, : 3 * HEAD_DIM].reshape(3, HEAD_DIM),
                biases_other[layer, : 3 * HEAD_DIM].reshape(3, HEAD_DIM),
            ],
            axis=1,
        ).reshape(6 * HEAD_DIM)
        bias_up = jnp.concatenate([biases[layer, 3 * HEAD_DIM :], biases_other[layer, 3 * HEAD_DIM :]])
        projected = dot(normed, weight_qkv, contract_last) + bias_qkv.astype(f32)
        heads, attended = call_forward(projected, tables, allowed, block)
        hidden_pre = dot(normed, weight_up, contract_last) + bias_up.astype(f32)
        active = gelu_parts(hidden_pre)[0].astype(bf16)
        branch = scatter_rows((dot(attended, weight_out) + dot(active, weight_down)).astype(bf16))
        kept.append((xhat, inverse, normed, heads, attended, hidden_pre, active))
        state = state + branch + after[layer]

    def handed_back(own_rows):
        filled = in_order(own_rows, across(own_rows))
        return jnp.where(tensor == core, filled, over(filled))

    hidden_out = handed_back(state.astype(bf16))

    grad_state = start[1].astype(f32) * valid
    vector_grads = [None] * LAYERS
    weight_grads = [None] * LAYERS
    bias_grads = [None] * LAYERS

    def summed(own, other):
        total = own + over(other.astype(bf16)).astype(f32)
        if groups > 1:
            total = lax.psum_scatter(total, "dp", scatter_dimension=1, axis_index_groups=outer, tiled=True)
        total = total.astype(bf16).reshape(total.shape[0], GROUP, piece).transpose(1, 0, 2)
        return spread(total)

    for layer in reversed(range(LAYERS)):
        xhat, inverse, normed, heads, attended, hidden_pre, active = kept[layer]
        weight_qkv, weight_up = gathered_up[layer]
        weight_out, weight_down = gathered_down[layer]
        grad_branch = gather_rows(grad_state.astype(bf16))
        grad_after = jnp.sum(grad_state, axis=0)
        grad_attended = dot(grad_branch, weight_out, contract_last).astype(bf16)
        grad_pre = (dot(grad_branch, weight_down, contract_last) * gelu_parts(hidden_pre)[1]).astype(bf16)
        grad_proj = call_backward(heads, grad_attended, tables, allowed, block)
        grad_normed = scatter_rows((dot(grad_proj, weight_qkv) + dot(grad_pre, weight_up)).astype(bf16))
        grad_out = dot(attended, grad_branch, contract_first)
        grad_down = dot(active, grad_branch, contract_first)
        grad_qkv = dot(grad_proj, normed, contract_first).reshape(3, 2, HEAD_DIM, width)
        grad_up = dot(grad_pre, normed, contract_first)
        down = summed(
            jnp.concatenate([grad_out[:HEAD_DIM], grad_down[:hidden]], 0),
            jnp.concatenate([grad_out[HEAD_DIM:], grad_down[hidden:]], 0),
        )
        up = summed(
            jnp.concatenate([grad_qkv[:, 0].reshape(3 * HEAD_DIM, width), grad_up[:hidden]], 0),
            jnp.concatenate([grad_qkv[:, 1].reshape(3 * HEAD_DIM, width), grad_up[hidden:]], 0),
        )
        up, down = up.astype(f32), down.astype(f32)
        weight_grads[layer] = (
            up[:, : 3 * HEAD_DIM].reshape(GROUP, 3, HEAD_DIM, piece).transpose(3, 1, 0, 2).reshape(piece, 3, GROUP * HEAD_DIM),
            down[:, :HEAD_DIM].reshape(GROUP * HEAD_DIM, piece),
            up[:, 3 * HEAD_DIM :].transpose(2, 0, 1).reshape(piece, GROUP * hidden),
            down[:, HEAD_DIM:].reshape(GROUP * hidden, piece),
        )
        sums_qkv = jnp.sum(grad_proj, axis=0, dtype=f32).reshape(3, 2, HEAD_DIM)
        sums_up = jnp.sum(grad_pre, axis=0, dtype=f32)
        bias_grads[layer] = (
            jnp.concatenate([sums_qkv[:, 0].reshape(-1), sums_up[:hidden]]),
            jnp.concatenate([sums_qkv[:, 1].reshape(-1), sums_up[hidden:]]),
        )
        vector_grads[layer] = jnp.stack(
            [jnp.sum(grad_normed * xhat, axis=0), jnp.sum(grad_normed, axis=0), grad_after]
        )
        scaled = grad_normed * gains[layer]
        grad_state = grad_state + (
            scaled
            - jnp.mean(scaled, axis=1, keepdims=True)
            - xhat * jnp.mean(scaled * xhat, axis=1, keepdims=True)
        ) * inverse

    grad_hidden = handed_back(grad_state.astype(bf16)).astype(f32)
    vectors = jnp.stack(vector_grads).reshape(LAYERS * 3, n_dp, piece).transpose(1, 0, 2)
    vectors = jnp.sum(lax.all_to_all(vectors, "dp", 0, 0, tiled=True), axis=0)
    vectors = (vectors + over(vectors)).reshape(LAYERS, 3, piece)
    bias_own = jnp.stack([bias_grads[layer][0] for layer in range(LAYERS)])
    bias_other = jnp.stack([bias_grads[layer][1] for layer in range(LAYERS)])
    bias_sums = bias_own + over(bias_other)
    bias_qkv, bias_up = bias_sums[:, : 3 * HEAD_DIM].reshape(LAYERS, 3, HEAD_DIM), bias_sums[:, 3 * HEAD_DIM :]
    if groups > 1:
        bias_qkv = lax.all_gather(lax.psum(bias_qkv, "dp", axis_index_groups=outer), "dp", axis=2, axis_index_groups=inner, tiled=True)
        bias_up = lax.all_gather(lax.psum(bias_up, "dp", axis_index_groups=outer), "dp", axis=1, axis_index_groups=inner, tiled=True)
        bias_qkv = lax.dynamic_slice_in_dim(bias_qkv, index * qkv_bias.shape[2], qkv_bias.shape[2], 2)
        bias_up = lax.dynamic_slice_in_dim(bias_up, index * fc1_bias.shape[1], fc1_bias.shape[1], 1)
    stacked = [jnp.stack([weight_grads[layer][i] for layer in range(LAYERS)]) for i in range(4)]
    return (
        hidden_out,
        grad_hidden,
        vectors[:, 0],
        vectors[:, 1],
        stacked[0],
        bias_qkv,
        stacked[1],
        stacked[2],
        bias_up,
        stacked[3],
        vectors[:, 2],
    )


def solution(mesh):
    placed = (
        P("dp", None),
        P(),
        P(),
        P("dp"),
        P(None, "dp"),
        P(None, "dp"),
        P(None, "dp", None, "tensor"),
        P(None, None, ("tensor", "dp")),
        P(None, "tensor", "dp"),
        P(None, "dp", "tensor"),
        P(None, ("tensor", "dp")),
        P(None, "tensor", "dp"),
        P(None, "dp"),
        P("dp", None),
    )
    return jax.shard_map(
        partial(per_device, mesh.shape["dp"]),
        mesh=mesh,
        in_specs=placed,
        out_specs=(
            P("dp", None),
            P("dp", None),
            P(None, "dp"),
            P(None, "dp"),
            P(None, "dp", None, "tensor"),
            P(None, None, ("tensor", "dp")),
            P(None, "tensor", "dp"),
            P(None, "dp", "tensor"),
            P(None, ("tensor", "dp")),
            P(None, "tensor", "dp"),
            P(None, "dp"),
        ),
        check_vma=False,
    )
```

time: 3400 us -> 886 us (0.26)
  waiting for transfers between devices: 2670 us -> 318 us
  matrix products: 411 us -> 97.6 us
  blocking collectives: 187 us -> 36.8 us
  starting transfers between devices: 1.07 us -> 128 us
  local copies, waits for them, and re-layouts: 43.3 us -> 158 us
  other arithmetic: 43.9 us -> 98.9 us
    reduce_scatter x8 -> x0, waiting for transfers between devices: 2030 us -> none  [the longest x2 664 us: per_device(): lax.psum_scatter(grad_up, 'dp', scatter_dimension=0, tiled=True)]
    all_gather x8 -> x0, waiting for transfers between devices: 495 us -> none  [the longest x2 243 us: per_device(): lax.all_gather(fc2_weight[layer], 'dp', axis=1, tiled=True)]
    dot_general x248 -> x25, matrix products: 411 us -> 97.6 us  [the longest x24 97.4 us: dot(): return lax.dot_general(a, b, dims, preferred_element_type=f32)]
    ppermute x0 -> x76, waiting for transfers between devices: none -> 285 us  [the longest x32 184 us: along(): return lax.ppermute(x, 'dp', ring_pairs)]
    all_gather x10 -> x1, blocking collectives: 187 us -> 36.8 us  [per_device(): small = lax.all_gather(small, 'dp', axis=0, tiled=False)]
    unnamed x25 -> x0, waiting for transfers between devices: 92.2 us -> none
    ppermute x0 -> x76, starting transfers between devices: none -> 79.4 us  [the longest x31 37.2 us: across(): return lax.ppermute(x, 'dp', core_pairs)]
    unnamed x110 -> x261, local copies, waits for them, and re-layouts: 16.2 us -> 78.5 us
  transfers between devices with their start and end apart: 22 -> 85, of which waited for: 17 -> 37; matrix products, arithmetic and copies ran while one was open for 9% -> 33% of each run, Pallas kernels for 0% -> 3%
where the time goes in v1:
time: 886 us; the launch traced here: 874 us
  waiting for transfers between devices  318 us (36%)
  local copies, waits for them, and re-layouts  158 us (18%)
  starting transfers between devices  128 us (14%)
  other arithmetic  98.9 us (11%)
  matrix products  97.6 us (11%)
  blocking collectives  36.8 us (4%)
  Pallas kernels  33 us (4%)
    ppermute x32, waiting for transfers between devices, along(): return lax.ppermute(x, 'dp', ring_pairs)  184 us
    ppermute x13, waiting for transfers between devices, over(): return lax.ppermute(x, 'tensor', [(0, 1), (1, 0)])  98 us
    dot_general x24, matrix products, dot(): return lax.dot_general(a, b, dims, preferred_element_type=f32)  97.4 us
    unnamed x261, local copies, waits for them, and re-layouts  78.5 us
    all_to_all x8, starting transfers between devices, spread(): return lax.all_to_all(x, 'dp', 0, 0, axis_index_groups=inner, tiled=True)  44.5 us
    ppermute x31, starting transfers between devices, across(): return lax.ppermute(x, 'dp', core_pairs)  37.2 us
    all_gather x1, blocking collectives, per_device(): small = lax.all_gather(small, 'dp', axis=0, tiled=False)  36.8 us
    ppermute x32, starting transfers between devices, along(): return lax.ppermute(x, 'dp', ring_pairs)  35 us
  transfers between devices with their start and end apart: 85, of which 37 were waited for; matrix products, arithmetic and copies ran while one was open for 33% of the time, Pallas kernels for 3%

profile of v1, /device:TPU:13, one launch (start us, length us, event | category | flops | bytes accessed | tf_op | source)
XLA Modules:
  0.0 874.5 jit_solution(348519598480081532)
XLA Ops:
  9.5 6.0 all-to-all-start.1
  18.8 36.8 %all-gather = bf16[16384]{0:T(1024)(128)(2,1)S(1)} all-gather(bf16[1024]{0:T(1024)(128)(2,1)S(1)} %dynamic-update-slice.52), channel_id=2, replica_groups=mesh['dp'=16,'tensor'=2] {'dp'}, dimensions={0}, use_global_device_ids=true | all-gather | bytes 34816 | tf_op jit(solution)/shard_map/all_gather | solution.py:309
  60.7 3.1 fusion.119
  71.2 4.9 all-to-all-start
  82.1 39.8 %collective-permute-done.2 = bf16[128,2048]{1,0:T(8,128)(2,1)} collective-permute-done((bf16[128,2048]{1,0:T(8,128)(2,1)S(1)}, bf16[128,2048]{1,0:T(8,128)(2,1)}, u32[]{:S(2)}, u32[]{:S(2)}) %collective-permute-start.2) | collective-permute-done | bytes 524320 | tf_op jit(solution)/shard_map/ppermute | solution.py:188
  150.9 4.2 all-to-all-start.3
  170.8 7.6 collective-permute-done.12
  182.7 35.0 %collective-permute-done.10 = bf16[16,448,128]{2,1,0:T(8,128)(2,1)} collective-permute-done((bf16[16,448,128]{2,1,0:T(8,128)(2,1)}, bf16[16,448,128]{2,1,0:T(8,128)(2,1)}, u32[]{:S(2)}, u32[]{:S(2)}) %collective-permute-start.10) | collective-permute-done | bytes 1835040 | tf_op jit(solution)/shard_map/ppermute | solution.py:194
  229.0 6.3 convolution_add_fusion.1.proj_ref
  239.0 5.9 fusion.23
  245.0 7.7 attention_forward.2
  252.6 4.8 add_convert_fusion.3
  265.7 6.8 collective-permute-done.39
  301.5 5.5 all-to-all-start.2
  317.3 35.4 %collective-permute-done.15 = bf16[128,2048]{1,0:T(8,128)(2,1)S(1)} collective-permute-done((bf16[128,2048]{1,0:T(8,128)(2,1)S(1)}, bf16[128,2048]{1,0:T(8,128)(2,1)S(1)}, u32[]{:S(2)}, u32[]{:S(2)}) %collective-permute-start.15) | collective-permute-done | bytes 524320 | tf_op jit(solution)/shard_map/ppermute | solution.py:188
  375.1 3.3 collective-permute-start.18
  378.5 10.6 %collective-permute-done.29 = bf16[16,320,128]{2,1,0:T(8,128)(2,1)} collective-permute-done((bf16[16,320,128]{2,1,0:T(8,128)(2,1)}, bf16[16,320,128]{2,1,0:T(8,128)(2,1)}, u32[]{:S(2)}, u32[]{:S(2)}) %collective-permute-start.29) | collective-permute-done | bytes 1310752 | tf_op jit(solution)/shard_map/ppermute | solution.py:194
  403.3 25.1 %collective-permute-done.28 = bf16[16,448,128]{2,1,0:T(8,128)(2,1)} collective-permute-done((bf16[16,448,128]{2,1,0:T(8,128)(2,1)S(1)}, bf16[16,448,128]{2,1,0:T(8,128)(2,1)}, u32[]{:S(2)}, u32[]{:S(2)}) %collective-permute-start.28) | collective-permute-done | bytes 1835040 | tf_op jit(solution)/shard_map/ppermute | solution.py:194
  433.2 6.8 collective-permute-done.20
  441.6 6.9 collective-permute-done.21
  451.9 3.0 collective-permute-start.23
  463.1 4.4 collective-permute-start.27
  470.1 4.7 fusion.22
  474.9 3.5 convert_reduce_fusion
  478.4 5.9 fusion.20
  484.3 4.9 convolution_add_fusion.proj_ref
  489.2 7.8 attention_forward.3
  497.0 4.8 add_convert_fusion.2
  506.5 5.8 fusion.21
  512.2 8.7 attention_backward.2
  520.9 6.6 add_convert_fusion.1
  539.9 7.4 collective-permute-done.49
  547.6 5.4 collective-permute-done.32
  553.2 5.4 collective-permute-done.50
  558.8 5.4 collective-permute-done.33
  564.8 5.0 collective-permute-done.51
  593.7 4.4 collective-permute-done.55
  601.6 5.0 collective-permute-done.56
  612.4 3.4 collective-permute-start.61
  617.1 3.5 convert_reduce_fusion.1
  622.6 5.8 fusion.24
  628.3 8.8 %attention_backward.3 = bf16[1024,384]{1,0:T(8,128)(2,1)} custom-call(bf16[1024,384]{1,0:T(8,128)(2,1)} %get-tuple-element.18.kept_ref, bf16[1024,128]{1,0:T(8,128)(2,1)} %convolution_convert_fusion.grad_ref, f32[1024,128]{1,0:T(8,128)} %concatenate.230.cos_ref, f32[1024,128]{1,0:T(8,128)} %concatenate.231.up_ref, f32[1024,128]{1,0:T(8,128)} %concatenate.232.down_ref, ...), custom_call_target="tpu_custom_call" | custom-call | flops 335544320 | bytes 6144000 | tf_op jit(solution)/shard_map/attention_backward/pallas_call | solution.py:110
  637.2 6.0 add_convert_fusion
  650.8 5.7 all-to-all-start.8
  659.2 3.1 slice.767
  662.9 4.4 bitcast_bitcast_fusion
  668.0 4.7 fusion.107
  678.9 8.6 all-to-all-done.8
  688.6 4.4 all-to-all-start.6
  693.0 3.0 slice_add_fusion
  703.5 35.3 %collective-permute-done.64 = bf16[128,2048]{1,0:T(8,128)(2,1)S(1)} collective-permute-done((bf16[128,2048]{1,0:T(8,128)(2,1)S(1)}, bf16[128,2048]{1,0:T(8,128)(2,1)S(1)}, u32[]{:S(2)}, u32[]{:S(2)}) %collective-permute-start.64) | collective-permute-done | bytes 524320 | tf_op jit(solution)/shard_map/ppermute | solution.py:188
  741.3 4.5 fusion.129
  750.3 6.8 all-to-all-start.7
  757.1 4.2 fusion.128
  784.9 3.8 all-to-all-done.7
  788.7 4.5 all-to-all-start.4
  793.2 12.9 %collective-permute-done.71 = bf16[448,2048]{1,0:T(8,128)(2,1)} collective-permute-done((bf16[448,2048]{1,0:T(8,128)(2,1)}, bf16[448,2048]{1,0:T(8,128)(2,1)}, u32[]{:S(2)}, u32[]{:S(2)}) %collective-permute-start.71) | collective-permute-done | bytes 1835040 | tf_op jit(solution)/shard_map/ppermute | solution.py:194
  806.0 3.6 bitcast_bitcast_fusion.1
  809.7 7.0 all-to-all-start.5
  828.8 6.5 collective-permute-done.70
  838.0 20.5 %all-to-all-done.5 = bf16[16,448,128]{2,1,0:T(8,128)(2,1)S(1)} async-done(((bf16[16,448,128]{2,1,0:T(8,128)(2,1)}), bf16[16,448,128]{2,1,0:T(8,128)(2,1)S(1)}, u32[]{:S(2)}, u32[]{:S(2)}) %all-to-all-start.5) | async-done | bytes 1835040 | tf_op jit(solution)/shard_map/all_to_all | solution.py:243
  861.9 3.5 copy.252
  867.0 3.1 copy.250
  870.0 4.0 pad_maximum_fusion
  (638 shorter events, 329.3 us)
Async XLA Ops:
  2.3 128.2 %collective-permute-start.11 = (bf16[2,448]{1,0:T(2,128)(2,1)S(1)}, bf16[2,448]{1,0:T(2,128)(2,1)S(1)}, u32[]{:S(2)}, u32[]{:S(2)}) collective-permute-start(bf16[2,448]{1,0:T(2,128)(2,1)S(1)} %pad_maximum_fusion.30), channel_id=1, source_target_pairs={{0,1},{1,0},{2,3},{3,2},{4,5},{5,4},{6,7},{7,6},{8,9},{9,8},{10,11... | collective-permute-start | bytes 5384 | tf_op jit(solution)/shard_map/ppermute | solution.py:194
  5.4 64.0 %collective-permute-start = (bf16[2,64,2048]{2,1,0:T(8,128)(2,1)}, bf16[2,64,2048]{2,1,0:T(8,128)(2,1)}, u32[]{:S(2)}, u32[]{:S(2)}) collective-permute-start(bf16[2,64,2048]{2,1,0:T(8,128)(2,1)} %fusion.58), channel_id=1, source_target_pairs={{0,2},{2,0},{4,6},{6,4},{8,10},{10,8},{12,14},{14,12},{16,18},{18,... | collective-permute-start | bytes 1572872 | tf_op jit(solution)/shard_map/ppermute | solution.py:191
  9.5 61.7 %all-to-all-start.1 = ((bf16[16,320,128]{2,1,0:T(8,128)(2,1)}), bf16[16,320,128]{2,1,0:T(8,128)(2,1)S(1)}, u32[]{:S(2)}, u32[]{:S(2)}) async-start(bf16[16,320,128]{2,1,0:T(8,128)(2,1)} %pad_maximum_fusion.23), calls=%async_computation.1 | async-start | bytes 2621440 | tf_op jit(solution)/shard_map/all_to_all | solution.py:243
  71.2 79.6 %all-to-all-start = ((bf16[16,448,128]{2,1,0:T(8,128)(2,1)}), bf16[16,448,128]{2,1,0:T(8,128)(2,1)}, u32[]{:S(2)}, u32[]{:S(2)}) async-start(bf16[16,448,128]{2,1,0:T(8,128)(2,1)} %pad_maximum_fusion.11), calls=%async_computation | async-start | bytes 3670016 | tf_op jit(solution)/shard_map/all_to_all | solution.py:243
  79.0 42.9 %collective-permute-start.2 = (bf16[128,2048]{1,0:T(8,128)(2,1)S(1)}, bf16[128,2048]{1,0:T(8,128)(2,1)}, u32[]{:S(2)}, u32[]{:S(2)}) collective-permute-start(bf16[128,2048]{1,0:T(8,128)(2,1)S(1)} %get-tuple-element.106), channel_id=1, source_target_pairs={{0,8},{2,6},{8,16},{10,2},{16,24},{18,10},{24,28},{26,18},{28,20},... | collective-permute-start | bytes 1572872 | tf_op jit(solution)/shard_map/ppermute | solution.py:188
  121.9 8.8 %collective-permute-start.3 = (bf16[128,2048]{1,0:T(8,128)(2,1)}, bf16[128,2048]{1,0:T(8,128)(2,1)}, u32[]{:S(2)}, u32[]{:S(2)}) collective-permute-start(bf16[128,2048]{1,0:T(8,128)(2,1)} %collective-permute-done.2), channel_id=1, source_target_pairs={{0,8},{2,6},{8,16},{10,2},{16,24},{18,10},{24,28},{26,18},{28,20},... | collective-permute-start | bytes 1572872 | tf_op jit(solution)/shard_map/ppermute | solution.py:188
  130.7 8.7 collective-permute-start.4
  132.6 129.4 %collective-permute-start.38 = (bf16[64,2048]{1,0:T(8,128)(2,1)S(1)}, bf16[64,2048]{1,0:T(8,128)(2,1)}, u32[]{:S(2)}, u32[]{:S(2)}) collective-permute-start(bf16[64,2048]{1,0:T(8,128)(2,1)S(1)} %get-tuple-element.134), channel_id=1, source_target_pairs={{0,2},{2,0},{4,6},{6,4},{8,10},{10,8},{12,14},{14,12},{16,18},{18,... | collective-permute-start | bytes 786440 | tf_op jit(solution)/shard_map/ppermute | solution.py:191
  134.0 12.4 %collective-permute-start.5 = (bf16[128,2048]{1,0:T(8,128)(2,1)}, bf16[128,2048]{1,0:T(8,128)(2,1)S(1)}, u32[]{:S(2)}, u32[]{:S(2)}) collective-permute-start(bf16[128,2048]{1,0:T(8,128)(2,1)} %collective-permute-done.2), channel_id=1, source_target_pairs={{0,2},{2,0},{4,6},{6,4},{8,10},{10,8},{12,14},{14,12},{16,18},{18,... | collective-permute-start | bytes 1572872 | tf_op jit(solution)/shard_map/ppermute | solution.py:191
  135.9 11.3 %collective-permute-start.6 = (bf16[128,2048]{1,0:T(8,128)(2,1)}, bf16[128,2048]{1,0:T(8,128)(2,1)S(1)}, u32[]{:S(2)}, u32[]{:S(2)}) collective-permute-start(bf16[128,2048]{1,0:T(8,128)(2,1)} %collective-permute-done.3), channel_id=1, source_target_pairs={{0,2},{2,0},{4,6},{6,4},{8,10},{10,8},{12,14},{14,12},{16,18},{18,... | collective-permute-start | bytes 1572872 | tf_op jit(solution)/shard_map/ppermute | solution.py:191
  142.2 17.4 %collective-permute-start.7 = (bf16[128,2048]{1,0:T(8,128)(2,1)}, bf16[128,2048]{1,0:T(8,128)(2,1)}, u32[]{:S(2)}, u32[]{:S(2)}) collective-permute-start(bf16[128,2048]{1,0:T(8,128)(2,1)} %collective-permute-done.4), channel_id=1, source_target_pairs={{0,2},{2,0},{4,6},{6,4},{8,10},{10,8},{12,14},{14,12},{16,18},{18,... | collective-permute-start | bytes 1572872 | tf_op jit(solution)/shard_map/ppermute | solution.py:191
  148.0 30.4 %collective-permute-start.12 = (bf16[16,320,128]{2,1,0:T(8,128)(2,1)S(1)}, bf16[16,320,128]{2,1,0:T(8,128)(2,1)}, u32[]{:S(2)}, u32[]{:S(2)}) collective-permute-start(bf16[16,320,128]{2,1,0:T(8,128)(2,1)S(1)} %copy-done.30), channel_id=1, source_target_pairs={{0,1},{1,0},{2,3},{3,2},{4,5},{5,4},{6,7},{7,6},{8,9},{9,8},{10,11... | collective-permute-start | bytes 3932168 | tf_op jit(solution)/shard_map/ppermute | solution.py:194
  148.3 13.2 %collective-permute-start.9 = (bf16[64,2048]{1,0:T(8,128)(2,1)}, bf16[64,2048]{1,0:T(8,128)(2,1)}, u32[]{:S(2)}, u32[]{:S(2)}) collective-permute-start(bf16[64,2048]{1,0:T(8,128)(2,1)} %collective-permute-done.8), channel_id=1, source_target_pairs={{0,2},{2,0},{4,6},{6,4},{8,10},{10,8},{12,14},{14,12},{16,18},{18,... | collective-permute-start | bytes 786440 | tf_op jit(solution)/shard_map/ppermute | solution.py:191
  150.9 149.6 %all-to-all-start.3 = ((bf16[16,320,128]{2,1,0:T(8,128)(2,1)}), bf16[16,320,128]{2,1,0:T(8,128)(2,1)S(1)}, u32[]{:S(2)}, u32[]{:S(2)}) async-start(bf16[16,320,128]{2,1,0:T(8,128)(2,1)} %pad_maximum_fusion.24), calls=%async_computation.3 | async-start | bytes 2621440 | tf_op jit(solution)/shard_map/all_to_all | solution.py:243
  155.1 62.6 %collective-permute-start.10 = (bf16[16,448,128]{2,1,0:T(8,128)(2,1)}, bf16[16,448,128]{2,1,0:T(8,128)(2,1)}, u32[]{:S(2)}, u32[]{:S(2)}) collective-permute-start(bf16[16,448,128]{2,1,0:T(8,128)(2,1)} %all-to-all-done), channel_id=1, source_target_pairs={{0,1},{1,0},{2,3},{3,2},{4,5},{5,4},{6,7},{7,6},{8,9},{9,8},{10,11... | collective-permute-start | bytes 5505032 | tf_op jit(solution)/shard_map/ppermute | solution.py:194
  261.2 32.7 %collective-permute-start.13 = (bf16[512,2048]{1,0:T(8,128)(2,1)}, bf16[512,2048]{1,0:T(8,128)(2,1)}, u32[]{:S(2)}, u32[]{:S(2)}) collective-permute-start(bf16[512,2048]{1,0:T(8,128)(2,1)} %pad_maximum_fusion.5), channel_id=1, source_target_pairs={{0,2},{2,0},{4,6},{6,4},{8,10},{10,8},{12,14},{14,12},{16,18},{18,... | collective-permute-start | bytes 6291464 | tf_op jit(solution)/shard_map/ppermute | solution.py:191
  272.5 8.6 collective-permute-start.40
  281.1 8.6 collective-permute-start.41
  282.9 31.7 %collective-permute-start.42 = (bf16[128,2048]{1,0:T(8,128)(2,1)}, bf16[128,2048]{1,0:T(8,128)(2,1)S(1)}, u32[]{:S(2)}, u32[]{:S(2)}) collective-permute-start(bf16[128,2048]{1,0:T(8,128)(2,1)} %collective-permute-done.39), channel_id=1, source_target_pairs={{0,2},{2,0},{4,6},{6,4},{8,10},{10,8},{12,14},{14,12},{16,18},{18,... | collective-permute-start | bytes 1572872 | tf_op jit(solution)/shard_map/ppermute | solution.py:191
  284.8 30.6 %collective-permute-start.43 = (bf16[128,2048]{1,0:T(8,128)(2,1)}, bf16[128,2048]{1,0:T(8,128)(2,1)}, u32[]{:S(2)}, u32[]{:S(2)}) collective-permute-start(bf16[128,2048]{1,0:T(8,128)(2,1)} %collective-permute-done.40), channel_id=1, source_target_pairs={{0,2},{2,0},{4,6},{6,4},{8,10},{10,8},{12,14},{14,12},{16,18},{18,... | collective-permute-start | bytes 1572872 | tf_op jit(solution)/shard_map/ppermute | solution.py:191
  290.8 26.6 %collective-permute-start.45 = (bf16[64,2048]{1,0:T(8,128)(2,1)S(1)}, bf16[64,2048]{1,0:T(8,128)(2,1)}, u32[]{:S(2)}, u32[]{:S(2)}) collective-permute-start(bf16[64,2048]{1,0:T(8,128)(2,1)S(1)} %constant_dynamic-slice_fusion.3), channel_id=1, source_target_pairs={{0,8},{2,6},{8,16},{10,2},{16,24},{18,10},{24,28},{26,18},{28,20},... | collective-permute-start | bytes 786440 | tf_op jit(solution)/shard_map/ppermute | solution.py:188
  292.9 66.3 %collective-permute-start.44 = (bf16[128,2048]{1,0:T(8,128)(2,1)}, bf16[128,2048]{1,0:T(8,128)(2,1)}, u32[]{:S(2)}, u32[]{:S(2)}) collective-permute-start(bf16[128,2048]{1,0:T(8,128)(2,1)} %collective-permute-done.41), channel_id=1, source_target_pairs={{0,2},{2,0},{4,6},{6,4},{8,10},{10,8},{12,14},{14,12},{16,18},{18,... | collective-permute-start | bytes 1572872 | tf_op jit(solution)/shard_map/ppermute | solution.py:191
  298.7 11.1 %collective-permute-start.14 = (bf16[64,2048]{1,0:T(8,128)(2,1)}, bf16[64,2048]{1,0:T(8,128)(2,1)}, u32[]{:S(2)}, u32[]{:S(2)}) collective-permute-start(bf16[64,2048]{1,0:T(8,128)(2,1)} %fusion.73), channel_id=1, source_target_pairs={{0,8},{2,6},{8,16},{10,2},{16,24},{18,10},{24,28},{26,18},{28,20},... | collective-permute-start | bytes 786440 | tf_op jit(solution)/shard_map/ppermute | solution.py:188
  301.5 65.0 %all-to-all-start.2 = ((bf16[16,448,128]{2,1,0:T(8,128)(2,1)}), bf16[16,448,128]{2,1,0:T(8,128)(2,1)S(1)}, u32[]{:S(2)}, u32[]{:S(2)}) async-start(bf16[16,448,128]{2,1,0:T(8,128)(2,1)} %pad_maximum_fusion.12), calls=%async_computation.2 | async-start | bytes 3670016 | tf_op jit(solution)/shard_map/all_to_all | solution.py:243
  311.5 41.2 %collective-permute-start.15 = (bf16[128,2048]{1,0:T(8,128)(2,1)S(1)}, bf16[128,2048]{1,0:T(8,128)(2,1)S(1)}, u32[]{:S(2)}, u32[]{:S(2)}) collective-permute-start(bf16[128,2048]{1,0:T(8,128)(2,1)S(1)} %fusion.39), channel_id=1, source_target_pairs={{0,8},{2,6},{8,16},{10,2},{16,24},{18,10},{24,28},{26,18},{28,20},... | collective-permute-start | bytes 1572872 | tf_op jit(solution)/shard_map/ppermute | solution.py:188
  317.3 43.8 %collective-permute-start.46 = (bf16[64,2048]{1,0:T(8,128)(2,1)}, bf16[64,2048]{1,0:T(8,128)(2,1)S(1)}, u32[]{:S(2)}, u32[]{:S(2)}) collective-permute-start(bf16[64,2048]{1,0:T(8,128)(2,1)} %collective-permute-done.45), channel_id=1, source_target_pairs={{0,2},{2,0},{4,6},{6,4},{8,10},{10,8},{12,14},{14,12},{16,18},{18,... | collective-permute-start | bytes 786440 | tf_op jit(solution)/shard_map/ppermute | solution.py:191
  353.6 9.4 %collective-permute-start.16 = (bf16[128,2048]{1,0:T(8,128)(2,1)}, bf16[128,2048]{1,0:T(8,128)(2,1)}, u32[]{:S(2)}, u32[]{:S(2)}) collective-permute-start(bf16[128,2048]{1,0:T(8,128)(2,1)} %fusion.38), channel_id=1, source_target_pairs={{0,8},{2,6},{8,16},{10,2},{16,24},{18,10},{24,28},{26,18},{28,20},... | collective-permute-start | bytes 1572872 | tf_op jit(solution)/shard_map/ppermute | solution.py:188
  358.9 30.2 %collective-permute-start.29 = (bf16[16,320,128]{2,1,0:T(8,128)(2,1)}, bf16[16,320,128]{2,1,0:T(8,128)(2,1)}, u32[]{:S(2)}, u32[]{:S(2)}) collective-permute-start(bf16[16,320,128]{2,1,0:T(8,128)(2,1)} %copy-done.31), channel_id=1, source_target_pairs={{0,1},{1,0},{2,3},{3,2},{4,5},{5,4},{6,7},{7,6},{8,9},{9,8},{10,11... | collective-permute-start | bytes 3932168 | tf_op jit(solution)/shard_map/ppermute | solution.py:194
  365.3 8.6 collective-permute-start.17
  370.5 57.9 %collective-permute-start.28 = (bf16[16,448,128]{2,1,0:T(8,128)(2,1)S(1)}, bf16[16,448,128]{2,1,0:T(8,128)(2,1)}, u32[]{:S(2)}, u32[]{:S(2)}) collective-permute-start(bf16[16,448,128]{2,1,0:T(8,128)(2,1)S(1)} %all-to-all-done.2), channel_id=1, source_target_pairs={{0,1},{1,0},{2,3},{3,2},{4,5},{5,4},{6,7},{7,6},{8,9},{9,8},{10,11... | collective-permute-start | bytes 5505032 | tf_op jit(solution)/shard_map/ppermute | solution.py:194
  375.1 15.1 %collective-permute-start.18 = (bf16[64,2048]{1,0:T(8,128)(2,1)S(1)}, bf16[64,2048]{1,0:T(8,128)(2,1)S(1)}, u32[]{:S(2)}, u32[]{:S(2)}) collective-permute-start(bf16[64,2048]{1,0:T(8,128)(2,1)S(1)} %dynamic-slice_convert_fusion.3), channel_id=1, source_target_pairs={{0,2},{2,0},{4,6},{6,4},{8,10},{10,8},{12,14},{14,12},{16,18},{18,... | collective-permute-start | bytes 786440 | tf_op jit(solution)/shard_map/ppermute | solution.py:191
  393.5 36.1 %collective-permute-start.19 = (bf16[64,2048]{1,0:T(8,128)(2,1)}, bf16[64,2048]{1,0:T(8,128)(2,1)}, u32[]{:S(2)}, u32[]{:S(2)}) collective-permute-start(bf16[64,2048]{1,0:T(8,128)(2,1)} %add_convert_fusion.4), channel_id=1, source_target_pairs={{0,2},{2,0},{4,6},{6,4},{8,10},{10,8},{12,14},{14,12},{16,18},{18,... | collective-permute-start | bytes 786440 | tf_op jit(solution)/shard_map/ppermute | solution.py:191
  448.5 9.2 %collective-permute-start.22 = (bf16[128,2048]{1,0:T(8,128)(2,1)}, bf16[128,2048]{1,0:T(8,128)(2,1)S(1)}, u32[]{:S(2)}, u32[]{:S(2)}) collective-permute-start(bf16[128,2048]{1,0:T(8,128)(2,1)} %collective-permute-done.21), channel_id=1, source_target_pairs={{0,8},{2,6},{8,16},{10,2},{16,24},{18,10},{24,28},{26,18},{28,20},... | collective-permute-start | bytes 1572872 | tf_op jit(solution)/shard_map/ppermute | solution.py:188
  451.9 10.2 %collective-permute-start.23 = (bf16[128,2048]{1,0:T(8,128)(2,1)S(1)}, bf16[128,2048]{1,0:T(8,128)(2,1)S(1)}, u32[]{:S(2)}, u32[]{:S(2)}) collective-permute-start(bf16[128,2048]{1,0:T(8,128)(2,1)S(1)} %copy-done.82), channel_id=1, source_target_pairs={{0,2},{2,0},{4,6},{6,4},{8,10},{10,8},{12,14},{14,12},{16,18},{18,... | collective-permute-start | bytes 1572872 | tf_op jit(solution)/shard_map/ppermute | solution.py:191
  455.8 11.8 %collective-permute-start.24 = (bf16[128,2048]{1,0:T(8,128)(2,1)}, bf16[128,2048]{1,0:T(8,128)(2,1)S(1)}, u32[]{:S(2)}, u32[]{:S(2)}) collective-permute-start(bf16[128,2048]{1,0:T(8,128)(2,1)} %collective-permute-done.21), channel_id=1, source_target_pairs={{0,2},{2,0},{4,6},{6,4},{8,10},{10,8},{12,14},{14,12},{16,18},{18,... | collective-permute-start | bytes 1572872 | tf_op jit(solution)/shard_map/ppermute | solution.py:191
  459.6 8.7 collective-permute-start.25
  505.6 22.4 %collective-permute-start.30 = (bf16[512,2048]{1,0:T(8,128)(2,1)}, bf16[512,2048]{1,0:T(8,128)(2,1)}, u32[]{:S(2)}, u32[]{:S(2)}) collective-permute-start(bf16[512,2048]{1,0:T(8,128)(2,1)} %pad_maximum_fusion.8), channel_id=1, source_target_pairs={{0,2},{2,0},{4,6},{6,4},{8,10},{10,8},{12,14},{14,12},{16,18},{18,... | collective-permute-start | bytes 6291464 | tf_op jit(solution)/shard_map/ppermute | solution.py:191
  539.0 13.9 %collective-permute-start.32 = (bf16[128,2048]{1,0:T(8,128)(2,1)S(1)}, bf16[128,2048]{1,0:T(8,128)(2,1)S(1)}, u32[]{:S(2)}, u32[]{:S(2)}) collective-permute-start(bf16[128,2048]{1,0:T(8,128)(2,1)S(1)} %get-tuple-element.157), channel_id=1, source_target_pairs={{0,8},{2,6},{8,16},{10,2},{16,24},{18,10},{24,28},{26,18},{28,20},... | collective-permute-start | bytes 1572872 | tf_op jit(solution)/shard_map/ppermute | solution.py:188
  547.5 11.1 %collective-permute-start.50 = (bf16[128,2048]{1,0:T(8,128)(2,1)S(1)}, bf16[128,2048]{1,0:T(8,128)(2,1)S(1)}, u32[]{:S(2)}, u32[]{:S(2)}) collective-permute-start(bf16[128,2048]{1,0:T(8,128)(2,1)S(1)} %fusion.32), channel_id=1, source_target_pairs={{0,8},{2,6},{8,16},{10,2},{16,24},{18,10},{24,28},{26,18},{28,20},... | collective-permute-start | bytes 1572872 | tf_op jit(solution)/shard_map/ppermute | solution.py:188
  553.1 11.1 %collective-permute-start.33 = (bf16[128,2048]{1,0:T(8,128)(2,1)S(1)}, bf16[128,2048]{1,0:T(8,128)(2,1)S(1)}, u32[]{:S(2)}, u32[]{:S(2)}) collective-permute-start(bf16[128,2048]{1,0:T(8,128)(2,1)S(1)} %fusion.35), channel_id=1, source_target_pairs={{0,8},{2,6},{8,16},{10,2},{16,24},{18,10},{24,28},{26,18},{28,20},... | collective-permute-start | bytes 1572872 | tf_op jit(solution)/shard_map/ppermute | solution.py:188
  558.7 11.1 %collective-permute-start.51 = (bf16[128,2048]{1,0:T(8,128)(2,1)S(1)}, bf16[128,2048]{1,0:T(8,128)(2,1)S(1)}, u32[]{:S(2)}, u32[]{:S(2)}) collective-permute-start(bf16[128,2048]{1,0:T(8,128)(2,1)S(1)} %fusion.31), channel_id=1, source_target_pairs={{0,8},{2,6},{8,16},{10,2},{16,24},{18,10},{24,28},{26,18},{28,20},... | collective-permute-start | bytes 1572872 | tf_op jit(solution)/shard_map/ppermute | solution.py:188
  564.4 11.1 %collective-permute-start.34 = (bf16[128,2048]{1,0:T(8,128)(2,1)S(1)}, bf16[128,2048]{1,0:T(8,128)(2,1)S(1)}, u32[]{:S(2)}, u32[]{:S(2)}) collective-permute-start(bf16[128,2048]{1,0:T(8,128)(2,1)S(1)} %fusion.34), channel_id=1, source_target_pairs={{0,8},{2,6},{8,16},{10,2},{16,24},{18,10},{24,28},{26,18},{28,20},... | collective-permute-start | bytes 1572872 | tf_op jit(solution)/shard_map/ppermute | solution.py:188
  581.2 8.5 collective-permute-start.54
  583.9 63.6 %collective-permute-start.75 = (bf16[320,2048]{1,0:T(8,128)(2,1)}, bf16[320,2048]{1,0:T(8,128)(2,1)}, u32[]{:S(2)}, u32[]{:S(2)}) collective-permute-start(bf16[320,2048]{1,0:T(8,128)(2,1)} %pad_maximum_fusion.26), channel_id=1, source_target_pairs={{0,1},{1,0},{2,3},{3,2},{4,5},{5,4},{6,7},{7,6},{8,9},{9,8},{10,11... | collective-permute-start | bytes 3932168 | tf_op jit(solution)/shard_map/ppermute | solution.py:194
  589.7 8.4 collective-permute-start.55
  600.9 8.7 collective-permute-start.57
  601.3 14.4 %collective-permute-start.58 = (bf16[128,2048]{1,0:T(8,128)(2,1)S(1)}, bf16[128,2048]{1,0:T(8,128)(2,1)S(1)}, u32[]{:S(2)}, u32[]{:S(2)}) collective-permute-start(bf16[128,2048]{1,0:T(8,128)(2,1)S(1)} %collective-permute-done.55), channel_id=1, source_target_pairs={{0,2},{2,0},{4,6},{6,4},{8,10},{10,8},{12,14},{14,12},{16,18},{18,... | collective-permute-start | bytes 1572872 | tf_op jit(solution)/shard_map/ppermute | solution.py:191
  609.6 53.3 %collective-permute-start.72 = (bf16[448,2048]{1,0:T(8,128)(2,1)}, bf16[448,2048]{1,0:T(8,128)(2,1)}, u32[]{:S(2)}, u32[]{:S(2)}) collective-permute-start(bf16[448,2048]{1,0:T(8,128)(2,1)} %pad_maximum_fusion.14), channel_id=1, source_target_pairs={{0,1},{1,0},{2,3},{3,2},{4,5},{5,4},{6,7},{7,6},{8,9},{9,8},{10,11... | collective-permute-start | bytes 5505032 | tf_op jit(solution)/shard_map/ppermute | solution.py:194
  647.0 25.7 %collective-permute-start.62 = (bf16[512,2048]{1,0:T(8,128)(2,1)}, bf16[512,2048]{1,0:T(8,128)(2,1)}, u32[]{:S(2)}, u32[]{:S(2)}) collective-permute-start(bf16[512,2048]{1,0:T(8,128)(2,1)} %pad_maximum_fusion.10), channel_id=1, source_target_pairs={{0,2},{2,0},{4,6},{6,4},{8,10},{10,8},{12,14},{14,12},{16,18},{18,... | collective-permute-start | bytes 6291464 | tf_op jit(solution)/shard_map/ppermute | solution.py:191
  650.8 36.7 %all-to-all-start.8 = ((bf16[16,320,128]{2,1,0:T(8,128)(2,1)}), bf16[16,320,128]{2,1,0:T(8,128)(2,1)S(1)}, u32[]{:S(2)}, u32[]{:S(2)}) async-start(bf16[16,320,128]{2,1,0:T(8,128)(2,1)} %bitcast_bitcast_fusion.2), calls=%async_computation.8 | async-start | bytes 2621440 | tf_op jit(solution)/shard_map/all_to_all | solution.py:243
  667.3 32.8 %collective-permute-start.36 = (bf16[64,2048]{1,0:T(8,128)(2,1)S(1)}, bf16[64,2048]{1,0:T(8,128)(2,1)}, u32[]{:S(2)}, u32[]{:S(2)}) collective-permute-start(bf16[64,2048]{1,0:T(8,128)(2,1)S(1)} %get-tuple-element.133), channel_id=1, source_target_pairs={{0,2},{2,0},{4,6},{6,4},{8,10},{10,8},{12,14},{14,12},{16,18},{18,... | collective-permute-start | bytes 786440 | tf_op jit(solution)/shard_map/ppermute | solution.py:191
  677.7 18.3 %collective-permute-start.63 = (bf16[64,2048]{1,0:T(8,128)(2,1)}, bf16[64,2048]{1,0:T(8,128)(2,1)}, u32[]{:S(2)}, u32[]{:S(2)}) collective-permute-start(bf16[64,2048]{1,0:T(8,128)(2,1)} %fusion.61), channel_id=1, source_target_pairs={{0,8},{2,6},{8,16},{10,2},{16,24},{18,10},{24,28},{26,18},{28,20},... | collective-permute-start | bytes 786440 | tf_op jit(solution)/shard_map/ppermute | solution.py:188
  688.6 61.7 %all-to-all-start.6 = ((bf16[16,448,128]{2,1,0:T(8,128)(2,1)}), bf16[16,448,128]{2,1,0:T(8,128)(2,1)S(1)}, u32[]{:S(2)}, u32[]{:S(2)}) async-start(bf16[16,448,128]{2,1,0:T(8,128)(2,1)} %bitcast_bitcast_fusion), calls=%async_computation.6 | async-start | bytes 3670016 | tf_op jit(solution)/shard_map/all_to_all | solution.py:243
  697.3 41.5 %collective-permute-start.64 = (bf16[128,2048]{1,0:T(8,128)(2,1)S(1)}, bf16[128,2048]{1,0:T(8,128)(2,1)S(1)}, u32[]{:S(2)}, u32[]{:S(2)}) collective-permute-start(bf16[128,2048]{1,0:T(8,128)(2,1)S(1)} %fusion.30), channel_id=1, source_target_pairs={{0,8},{2,6},{8,16},{10,2},{16,24},{18,10},{24,28},{26,18},{28,20},... | collective-permute-start | bytes 1572872 | tf_op jit(solution)/shard_map/ppermute | solution.py:188
  699.7 46.0 %collective-permute-start.74 = (bf16[320,2048]{1,0:T(8,128)(2,1)S(1)}, bf16[320,2048]{1,0:T(8,128)(2,1)S(1)}, u32[]{:S(2)}, u32[]{:S(2)}) collective-permute-start(bf16[320,2048]{1,0:T(8,128)(2,1)S(1)} %pad_maximum_fusion.25), channel_id=1, source_target_pairs={{0,1},{1,0},{2,3},{3,2},{4,5},{5,4},{6,7},{7,6},{8,9},{9,8},{10,11... | collective-permute-start | bytes 3932168 | tf_op jit(solution)/shard_map/ppermute | solution.py:194
  702.3 67.9 %collective-permute-start.37 = (bf16[128,2048]{1,0:T(8,128)(2,1)}, bf16[128,2048]{1,0:T(8,128)(2,1)}, u32[]{:S(2)}, u32[]{:S(2)}) collective-permute-start(bf16[128,2048]{1,0:T(8,128)(2,1)} %maximum_select_fusion.4), channel_id=1, source_target_pairs={{0,1},{1,0},{2,3},{3,2},{4,5},{5,4},{6,7},{7,6},{8,9},{9,8},{10,11... | collective-permute-start | bytes 1572872 | tf_op jit(solution)/shard_map/ppermute | solution.py:194
  738.9 10.0 %collective-permute-start.65 = (bf16[128,2048]{1,0:T(8,128)(2,1)S(1)}, bf16[128,2048]{1,0:T(8,128)(2,1)S(1)}, u32[]{:S(2)}, u32[]{:S(2)}) collective-permute-start(bf16[128,2048]{1,0:T(8,128)(2,1)S(1)} %fusion.29), channel_id=1, source_target_pairs={{0,8},{2,6},{8,16},{10,2},{16,24},{18,10},{24,28},{26,18},{28,20},... | collective-permute-start | bytes 1572872 | tf_op jit(solution)/shard_map/ppermute | solution.py:188
  749.8 17.8 %collective-permute-start.66 = (bf16[128,2048]{1,0:T(8,128)(2,1)}, bf16[128,2048]{1,0:T(8,128)(2,1)}, u32[]{:S(2)}, u32[]{:S(2)}) collective-permute-start(bf16[128,2048]{1,0:T(8,128)(2,1)} %fusion.28), channel_id=1, source_target_pairs={{0,8},{2,6},{8,16},{10,2},{16,24},{18,10},{24,28},{26,18},{28,20},... | collective-permute-start | bytes 1572872 | tf_op jit(solution)/shard_map/ppermute | solution.py:188
  750.3 38.4 %all-to-all-start.7 = ((bf16[16,320,128]{2,1,0:T(8,128)(2,1)}), bf16[16,320,128]{2,1,0:T(8,128)(2,1)}, u32[]{:S(2)}, u32[]{:S(2)}) async-start(bf16[16,320,128]{2,1,0:T(8,128)(2,1)} %bitcast_bitcast_fusion.3), calls=%async_computation.7 | async-start | bytes 2621440 | tf_op jit(solution)/shard_map/all_to_all | solution.py:243
  764.5 41.5 %collective-permute-start.71 = (bf16[448,2048]{1,0:T(8,128)(2,1)}, bf16[448,2048]{1,0:T(8,128)(2,1)}, u32[]{:S(2)}, u32[]{:S(2)}) collective-permute-start(bf16[448,2048]{1,0:T(8,128)(2,1)} %pad_maximum_fusion.13), channel_id=1, source_target_pairs={{0,1},{1,0},{2,3},{3,2},{4,5},{5,4},{6,7},{7,6},{8,9},{9,8},{10,11... | collective-permute-start | bytes 5505032 | tf_op jit(solution)/shard_map/ppermute | solution.py:194
  769.7 11.3 %collective-permute-start.67 = (bf16[64,2048]{1,0:T(8,128)(2,1)S(1)}, bf16[64,2048]{1,0:T(8,128)(2,1)}, u32[]{:S(2)}, u32[]{:S(2)}) collective-permute-start(bf16[64,2048]{1,0:T(8,128)(2,1)S(1)} %dynamic-slice_convert_fusion), channel_id=1, source_target_pairs={{0,2},{2,0},{4,6},{6,4},{8,10},{10,8},{12,14},{14,12},{16,18},{18,... | collective-permute-start | bytes 786440 | tf_op jit(solution)/shard_map/ppermute | solution.py:191
  788.7 21.0 %all-to-all-start.4 = ((f32[16,6,128]{2,1,0:T(8,128)}), f32[16,6,128]{2,1,0:T(8,128)S(1)}, u32[]{:S(2)}, u32[]{:S(2)}) async-start(f32[16,6,128]{2,1,0:T(8,128)} %copy.243), calls=%async_computation.4 | async-start | bytes 131072 | tf_op jit(solution)/shard_map/all_to_all | solution.py:439
  809.7 48.8 %all-to-all-start.5 = ((bf16[16,448,128]{2,1,0:T(8,128)(2,1)}), bf16[16,448,128]{2,1,0:T(8,128)(2,1)S(1)}, u32[]{:S(2)}, u32[]{:S(2)}) async-start(bf16[16,448,128]{2,1,0:T(8,128)(2,1)} %bitcast_bitcast_fusion.1), calls=%async_computation.5 | async-start | bytes 3670016 | tf_op jit(solution)/shard_map/all_to_all | solution.py:243
  822.8 13.1 %collective-permute-start.69 = (bf16[128,2048]{1,0:T(8,128)(2,1)S(1)}, bf16[128,2048]{1,0:T(8,128)(2,1)}, u32[]{:S(2)}, u32[]{:S(2)}) collective-permute-start(bf16[128,2048]{1,0:T(8,128)(2,1)S(1)} %maximum_select_fusion.9), channel_id=1, source_target_pairs={{0,1},{1,0},{2,3},{3,2},{4,5},{5,4},{6,7},{7,6},{8,9},{9,8},{10,11... | collective-permute-start | bytes 1572872 | tf_op jit(solution)/shard_map/ppermute | solution.py:194
  (130 other events, 918.5 us)

commit v2 on v1

v2 whole, which is shorter than its diff:
```python
from functools import partial

import jax
import jax.numpy as jnp
from jax import lax
from jax.experimental import pallas as pl
from jax.experimental.pallas import tpu as pltpu
from jax.sharding import PartitionSpec as P

HEAD_DIM = 64
ROT = 32
LAYERS = 2
GROUP = 16

norm_epsilon = 1e-05
masked_score = -1e30
bf16 = jnp.bfloat16
f32 = jnp.float32

contract_last = (((1,), (1,)), ((), ()))
contract_first = (((0,), (0,)), ((), ()))


def dot(a, b, dims=(((1,), (0,)), ((), ()))):
    return lax.dot_general(a, b, dims, preferred_element_type=f32)


def turn(x, cosine, up, down):
    return x * cosine + pltpu.roll(x, x.shape[1] - ROT // 2, 1) * up + pltpu.roll(x, ROT // 2, 1) * down


def stacked_heads(x):
    lane = lax.broadcasted_iota(jnp.int32, x.shape, 1)
    zero = jnp.zeros_like(x)
    return jnp.concatenate(
        [jnp.where(lane < HEAD_DIM, x, zero), jnp.where(lane < HEAD_DIM, zero, x)], axis=0
    )


def merged_heads(x):
    rows = x.shape[0] // 2
    lane = lax.broadcasted_iota(jnp.int32, (rows, x.shape[1]), 1)
    return jnp.where(lane < HEAD_DIM, x[:rows], x[rows:])


def softmax_rows(queries, keys, allowed):
    scores = dot(stacked_heads(queries), keys, contract_last) * HEAD_DIM ** (-0.5)
    masked = jnp.where(jnp.concatenate([allowed, allowed], axis=0) > 0, scores, masked_score)
    weights = jnp.exp(masked - jnp.max(masked, axis=1, keepdims=True))
    return weights / jnp.sum(weights, axis=1, keepdims=True)


def sequence_labels(seq_lengths, seq_device, owner, count_rows):
    index = jnp.arange(seq_lengths.shape[0], dtype=jnp.int32)
    owned = jnp.where(seq_device == owner, seq_lengths, 0)
    earlier = index[None, :] < index[:, None]
    starts = jnp.sum(jnp.where(earlier, owned[None, :], 0), axis=1)
    places = jnp.arange(count_rows, dtype=jnp.int32)
    inside = (places[:, None] >= starts[None, :]) & (places[:, None] < (starts + owned)[None, :])
    return jnp.sum(jnp.where(inside, index[None, :] + 1, 0), axis=1)


def gelu_parts(v):
    c = (2.0 / jnp.pi) ** 0.5
    inner = jnp.tanh(c * (v + 0.044715 * v * v * v))
    value = 0.5 * v * (1.0 + inner)
    slope = 0.5 * (1.0 + inner) + 0.5 * v * (1.0 - inner * inner) * c * (1.0 + 3.0 * 0.044715 * v * v)
    return value, slope


VMEM_SPEC = pl.BlockSpec(memory_space=pltpu.VMEM)
ANY_SPEC = pl.BlockSpec(memory_space=pl.ANY)
SMEM_SPEC = pl.BlockSpec(memory_space=pltpu.SMEM)
WIDE = 2 * HEAD_DIM


def left_lanes(x):
    return lax.broadcasted_iota(jnp.int32, x.shape, 1) < HEAD_DIM


def swapped(x):
    return pltpu.roll(x, HEAD_DIM, 1)


def zipped(a, b):
    left = left_lanes(a)
    return jnp.where(left, a, swapped(b)).astype(bf16), jnp.where(left, swapped(a), b).astype(bf16)


def pack_up(qkv_ref, fc1_ref, *rest):
    out_ref = rest[-1]
    q, k, v = (qkv_ref[0, p].astype(f32) for p in range(3))
    out_ref[0, :WIDE], out_ref[1, :WIDE] = zipped(q, k)
    rows = q.shape[0] // 2
    out_ref[0, WIDE : WIDE + rows], out_ref[1, WIDE : WIDE + rows] = zipped(v[:rows], v[rows:])
    base = WIDE + rows
    for d in range(2):
        for h in range(2):
            out_ref[d, base + h * 128 : base + (h + 1) * 128] = fc1_ref[0, :, (2 * d + h) * 128 : (2 * d + h + 1) * 128]
        if len(rest) > 1:
            out_ref[d, base + 256 :] = rest[0][...]


def call_pack_up(qkv, fc1, layer, small):
    rows = 3 * HEAD_DIM + 256 + (0 if small is None else small.shape[0])
    specs = [
        pl.BlockSpec((1, 3, 128, 128), lambda i: (layer, 0, 0, i)),
        pl.BlockSpec((1, 128, 512), lambda i: (layer, 0, i)),
    ]
    if small is not None:
        specs.append(pl.BlockSpec(small.shape, lambda i: (0, 0)))
    return pl.pallas_call(
        pack_up,
        grid=(GROUP // 2,),
        in_specs=specs,
        out_specs=pl.BlockSpec((2, rows, 128), lambda i: (i, 0, 0)),
        out_shape=jax.ShapeDtypeStruct((GROUP, rows, 128), bf16),
        name="pack_up",
    )(*([qkv, fc1] + ([] if small is None else [small])))


def pack_down(out_w_ref, fc2_ref, out_ref):
    for d in range(2):
        out_ref[d, :HEAD_DIM] = out_w_ref[0, d * HEAD_DIM : (d + 1) * HEAD_DIM]
        out_ref[d, HEAD_DIM:] = fc2_ref[0, d * 256 : (d + 1) * 256]


def call_pack_down(out_w, fc2, layer):
    return pl.pallas_call(
        pack_down,
        grid=(GROUP // 2,),
        in_specs=[
            pl.BlockSpec((1, 128, 128), lambda i: (layer, i, 0)),
            pl.BlockSpec((1, 512, 128), lambda i: (layer, i, 0)),
        ],
        out_specs=pl.BlockSpec((2, HEAD_DIM + 256, 128), lambda i: (i, 0, 0)),
        out_shape=jax.ShapeDtypeStruct((GROUP, HEAD_DIM + 256, 128), bf16),
        name="pack_down",
    )(out_w, fc2)


def join_up(own_ref, other_ref, out_ref):
    for e in range(2):
        rows = slice(e * 128, (e + 1) * 128)
        a, b = own_ref[e, :WIDE].astype(f32), other_ref[e, :WIDE].astype(f32)
        out_ref[rows, :WIDE], out_ref[rows, WIDE : 2 * WIDE] = zipped(a, b)
        a, b = own_ref[e, WIDE : WIDE + 64].astype(f32), other_ref[e, WIDE : WIDE + 64].astype(f32)
        top, bottom = zipped(a, b)
        out_ref[e * 128 : e * 128 + 64, 2 * WIDE : 3 * WIDE] = top
        out_ref[e * 128 + 64 : (e + 1) * 128, 2 * WIDE : 3 * WIDE] = bottom
        for n, ref in enumerate((own_ref, other_ref)):
            for h in range(2):
                lanes = 3 * WIDE + n * 256 + h * 128
                out_ref[rows, lanes : lanes + 128] = ref[e, WIDE + 64 + h * 128 : WIDE + 64 + (h + 1) * 128]


def call_join_up(own, other):
    rows = own.shape[1]
    return pl.pallas_call(
        join_up,
        grid=(GROUP // 2,),
        in_specs=[pl.BlockSpec((2, rows, 128), lambda i: (i, 0, 0))] * 2,
        out_specs=pl.BlockSpec((256, 3 * WIDE + 512), lambda i: (i, 0)),
        out_shape=jax.ShapeDtypeStruct((GROUP * 128, 3 * WIDE + 512), bf16),
        name="join_up",
    )(own, other)


def join_down(own_ref, other_ref, out_ref):
    for e in range(2):
        lanes = slice(e * 128, (e + 1) * 128)
        for n, ref in enumerate((own_ref, other_ref)):
            out_ref[n * HEAD_DIM : (n + 1) * HEAD_DIM, lanes] = ref[e, :HEAD_DIM]
            out_ref[WIDE + n * 256 : WIDE + (n + 1) * 256, lanes] = ref[e, HEAD_DIM:]


def call_join_down(own, other):
    rows = own.shape[1]
    return pl.pallas_call(
        join_down,
        grid=(GROUP // 2,),
        in_specs=[pl.BlockSpec((2, rows, 128), lambda i: (i, 0, 0))] * 2,
        out_specs=pl.BlockSpec((2 * rows, 256), lambda i: (0, i)),
        out_shape=jax.ShapeDtypeStruct((2 * rows, GROUP * 128), bf16),
        name="join_down",
    )(own, other)


def slot_copies(refs, which, target, core):
    block = target.shape[0] // 8
    half = block // 2
    pairs = []
    for slot in range(7):
        ref = refs[slot] if which is None else refs[slot].at[which]
        pairs.append((ref, target.at[pl.ds(slot * block, block)]))
    for n, at in ((7, core * half), (8, (1 - core) * half)):
        ref = refs[n] if which is None else refs[n].at[which]
        pairs.append((ref, target.at[pl.ds(pl.multiple_of(7 * block + at, half), half)]))
    return pairs


def split_copies(part, far_ref, give_ref, keep_ref, core):
    block = part.shape[0] // 8
    half = block // 2
    at, off = core * half, (1 - core) * half

    def rows(slot, start):
        return part.at[pl.ds(pl.multiple_of(slot * block + start, half), half)]

    return [
        (rows(7, off), far_ref),
        (part.at[pl.ds(block, 3 * block)], give_ref.at[pl.ds(0, 3 * block)]),
        (rows(0, off), give_ref.at[pl.ds(3 * block, half)]),
        (part.at[pl.ds(4 * block, 3 * block)], keep_ref.at[pl.ds(0, 3 * block)]),
        (rows(7, at), keep_ref.at[pl.ds(3 * block, half)]),
        (rows(0, at), keep_ref.at[pl.ds(3 * block + half, half)]),
    ]


def run_copies(pairs, sems, first):
    made = [pltpu.make_async_copy(a, b, sems.at[first + n]) for n, (a, b) in enumerate(pairs)]
    for copy in made:
        copy.start()
    return made


def heads_forward(chances, values):
    return merged_heads(dot(chances.astype(bf16), values)).astype(bf16)


def heads_backward(chances, queries, keys, values, grad, tables):
    grads = stacked_heads(grad)
    grad_chances = dot(grads, values, contract_last)
    grad_values = dot(chances.astype(bf16), grads, contract_first)
    centre = jnp.sum(grad_chances * chances, axis=1, keepdims=True)
    grad_scores = (chances * (grad_chances - centre)).astype(bf16)
    scale = HEAD_DIM ** (-0.5)
    grad_queries = merged_heads(dot(grad_scores, keys)) * scale
    grad_keys = dot(grad_scores, stacked_heads(queries), contract_first) * scale
    cosine, up, down = tables
    back = (cosine, -up, -down)
    return turn(grad_queries, *back).astype(bf16), turn(grad_keys, *back).astype(bf16), grad_values.astype(bf16)


def layer_pass(mode, *refs):
    refs = list(refs)

    def take(n):
        out = refs[:n]
        del refs[:n]
        return out

    forward, backward = mode != "last", mode != "first"
    core_ref, up_ref, down_ref, cos_ref, sin_up_ref, sin_down_ref, allowed_ref = take(7)
    core = core_ref[0]
    if mode == "first":
        bias_ref, gain_ref, shift_ref = take(3)
        rows_in = take(9)
    elif mode == "middle":
        (bias_ref,) = take(1)
        rows_in = take(9)
        grads_in = take(9)
    else:
        heads_ref, hidden_ref = take(2)
        grads_in = take(9)
    if mode == "first":
        normed_ref, heads_ref, hidden_ref, wide_ref = take(4)
        outs = take(3)
        raw, part, sems = take(3)
    elif mode == "middle":
        normed_ref, grad_rows_ref, wide_ref, slim_ref = take(4)
        outs = take(3)
        grad_outs = take(3)
        part, grad_part, sems = take(3)
    else:
        grad_rows_ref, slim_ref = take(2)
        grad_outs = take(3)
        grad_part, sems = take(2)

    pairs = []
    if mode == "first":
        pairs += slot_copies(rows_in, 0, raw, core)
    if mode == "middle":
        pairs += slot_copies(rows_in, None, normed_ref, core)
        pairs += slot_copies(grads_in, 1, grad_rows_ref, core)
    if mode == "last":
        pairs += slot_copies(grads_in, None, grad_rows_ref, core)
    for copy in run_copies(pairs, sems, 0):
        copy.wait()

    total = allowed_ref.shape[0]
    block = allowed_ref.shape[1]
    step = 2 * block

    if mode == "first":
        tile = 32

        def norm_tile(i, carry):
            at = pl.ds(pl.multiple_of(i * tile, tile), tile)
            x = raw[at, :].astype(f32)
            centred = x - jnp.mean(x, axis=1, keepdims=True)
            inverse = lax.rsqrt(jnp.mean(centred * centred, axis=1, keepdims=True) + norm_epsilon)
            normed_ref[at, :] = (centred * inverse * gain_ref[...] + shift_ref[...]).astype(bf16)
            return carry

        lax.fori_loop(0, total // tile, norm_tile, 0)

    def one(p, carry):
        at = pl.ds(pl.multiple_of(p * step, step), step)
        if forward:
            before = dot(normed_ref[at, :], up_ref[...]) + bias_ref[...]
            hidden_pre = before[:, 3 * WIDE :]
        else:
            hidden_pre = hidden_ref[at, :]
        value, slope = gelu_parts(hidden_pre)
        if backward:
            grad_wide = dot(grad_rows_ref[at, :], down_ref[...], contract_last)
            slim_ref[at, 3 * WIDE :] = (grad_wide[:, WIDE:] * slope).astype(bf16)
        if forward:
            wide_ref[at, WIDE:] = value.astype(bf16)
        if mode == "first":
            hidden_ref[at, :] = hidden_pre
        for b in range(2):
            mine = slice(b * block, (b + 1) * block)
            own = pl.ds(pl.multiple_of(p * step + b * block, block), block)
            tables = (cos_ref[own, :], sin_up_ref[own, :], sin_down_ref[own, :])
            if forward:
                queries = turn(before[mine, :WIDE], *tables).astype(bf16)
                keys = turn(before[mine, WIDE : 2 * WIDE], *tables).astype(bf16)
                values = before[mine, 2 * WIDE : 3 * WIDE].astype(bf16)
            else:
                queries = heads_ref[own, :WIDE]
                keys = heads_ref[own, WIDE : 2 * WIDE]
                values = heads_ref[own, 2 * WIDE :]
            if mode == "first":
                heads_ref[own, :WIDE] = queries
                heads_ref[own, WIDE : 2 * WIDE] = keys
                heads_ref[own, 2 * WIDE :] = values
            chances = softmax_rows(queries, keys, allowed_ref[own, :])
            if forward:
                wide_ref[own, :WIDE] = heads_forward(chances, values)
            if backward:
                grads = heads_backward(
                    chances, queries, keys, values, grad_wide[mine, :WIDE].astype(bf16), tables
                )
                for n in range(3):
                    slim_ref[own, n * WIDE : (n + 1) * WIDE] = grads[n]
        if forward:
            part[at, :] = dot(wide_ref[at, :], down_ref[...]).astype(bf16)
        if backward:
            grad_part[at, :] = dot(slim_ref[at, :], up_ref[...], contract_last).astype(bf16)
        return carry

    lax.fori_loop(0, total // step, one, 0)
    pairs = []
    if backward:
        pairs += split_copies(grad_part, *grad_outs, core)
    if forward:
        pairs += split_copies(part, *outs, core)
    for copy in run_copies(pairs, sems, 0):
        copy.wait()


def call_pass(mode, core, weights, tables, allowed, extra, chunks):
    total, block = allowed.shape
    half = block // 2
    width = weights[0].shape[0]
    slim = weights[0].shape[1]
    wide = weights[1].shape[0]
    parts = [
        jax.ShapeDtypeStruct((half, width), bf16),
        jax.ShapeDtypeStruct((3 * block + half, width), bf16),
        jax.ShapeDtypeStruct((4 * block, width), bf16),
    ]
    full = jax.ShapeDtypeStruct((total, width), bf16)
    slim_rows = jax.ShapeDtypeStruct((total, slim), bf16)
    wide_rows = jax.ShapeDtypeStruct((total, wide), bf16)
    if mode == "first":
        kept = [
            full,
            jax.ShapeDtypeStruct((total, 3 * WIDE), bf16),
            jax.ShapeDtypeStruct((total, slim - 3 * WIDE), f32),
            wide_rows,
        ]
        buffers = 2
    elif mode == "middle":
        kept = [full, full, wide_rows, slim_rows]
        parts = parts * 2
        buffers = 2
    else:
        kept = [full, slim_rows]
        buffers = 1
    passes = 2 if mode == "middle" else 1
    return pl.pallas_call(
        partial(layer_pass, mode),
        in_specs=[SMEM_SPEC] + [VMEM_SPEC] * (6 + len(extra)) + [ANY_SPEC] * len(chunks),
        out_specs=[VMEM_SPEC] * len(kept) + [ANY_SPEC] * len(parts),
        out_shape=kept + parts,
        scratch_shapes=[pltpu.VMEM((total, width), bf16)] * buffers + [pltpu.SemaphoreType.DMA((18,))],
        cost_estimate=pl.CostEstimate(
            flops=2 * total * width * (slim + wide) * passes,
            bytes_accessed=20_000_000 * passes,
            transcendentals=total * slim,
        ),
        name="pass_" + mode,
    )(core, *weights, *tables, allowed, *extra, *chunks)


def gradient_slabs(own_rows, other_rows, with_sums, left_ref, right_ref, own_ref, other_ref, *rest):
    turned_ref = rest[-1]

    @pl.when(pl.program_id(0) == 0)
    def _():
        width = left_ref.shape[1]
        for n in range(width // 128):
            lanes = slice(n * 128, (n + 1) * 128)
            left = left_ref[:, lanes].astype(f32)
            if with_sums:
                rest[0][:, lanes] = jnp.sum(left, axis=0, keepdims=True)
            turned_ref[lanes, :] = left.T.astype(bf16)

    product = dot(turned_ref[...], right_ref[...]).astype(bf16)
    for ref, pieces in ((own_ref, own_rows), (other_ref, other_rows)):
        place = 0
        for first, last in pieces:
            for e in range(2):
                ref[e, place : place + last - first] = product[first:last, e * 128 : (e + 1) * 128]
            place += last - first


def call_gradients(left, right, own_rows, other_rows, with_sums, name):
    total, height = left.shape
    width = right.shape[1]
    rows = height // 2
    slab = pl.BlockSpec((2, rows, 128), lambda i: (i, 0, 0))
    shape = jax.ShapeDtypeStruct((width // 128, rows, 128), bf16)
    out_specs, out_shape = [slab, slab], [shape, shape]
    if with_sums:
        out_specs.append(pl.BlockSpec((1, height), lambda i: (0, 0)))
        out_shape.append(jax.ShapeDtypeStruct((1, height), f32))
    return pl.pallas_call(
        partial(gradient_slabs, own_rows, other_rows, with_sums),
        grid=(width // 256,),
        in_specs=[pl.BlockSpec((total, height), lambda i: (0, 0)), pl.BlockSpec((total, 256), lambda i: (0, i))],
        out_specs=out_specs,
        out_shape=out_shape,
        scratch_shapes=[pltpu.VMEM((height, total), bf16)],
        cost_estimate=pl.CostEstimate(
            flops=2 * total * height * width, bytes_accessed=2 * (total * (width + height) + 2 * height * width), transcendentals=0
        ),
        name=name,
    )(left, right)


def spread_gradients(up_ref, down_ref, *rest):
    qkv_ref, out_w_ref, fc1_ref, fc2_ref = rest[-4:]
    for p in range(3):
        rows = slice(p * HEAD_DIM, (p + 1) * HEAD_DIM)
        both = jnp.concatenate([up_ref[0, rows].astype(f32), up_ref[1, rows].astype(f32)], axis=0)
        qkv_ref[0, p] = both.T
    base = 3 * HEAD_DIM
    for d in range(2):
        for h in range(2):
            fc1_ref[0, :, (2 * d + h) * 128 : (2 * d + h + 1) * 128] = (
                up_ref[d, base + h * 128 : base + (h + 1) * 128].astype(f32).T
            )
        out_w_ref[0, d * HEAD_DIM : (d + 1) * HEAD_DIM] = down_ref[d, :HEAD_DIM].astype(f32)
        fc2_ref[0, d * 256 : (d + 1) * 256] = down_ref[d, HEAD_DIM:].astype(f32)


def call_spread(up, down, layer, filled):
    shapes = [
        jax.ShapeDtypeStruct((LAYERS, 3, 128, GROUP * HEAD_DIM), f32),
        jax.ShapeDtypeStruct((LAYERS, GROUP * HEAD_DIM, 128), f32),
        jax.ShapeDtypeStruct((LAYERS, 128, GROUP * 256), f32),
        jax.ShapeDtypeStruct((LAYERS, GROUP * 256, 128), f32),
    ]
    return pl.pallas_call(
        spread_gradients,
        grid=(GROUP // 2,),
        in_specs=[
            pl.BlockSpec((2, up.shape[1], 128), lambda i: (i, 0, 0)),
            pl.BlockSpec((2, down.shape[1], 128), lambda i: (i, 0, 0)),
        ]
        + [ANY_SPEC] * len(filled),
        out_specs=[
            pl.BlockSpec((1, 3, 128, 128), lambda i: (layer, 0, 0, i)),
            pl.BlockSpec((1, 128, 128), lambda i: (layer, i, 0)),
            pl.BlockSpec((1, 128, 512), lambda i: (layer, 0, i)),
            pl.BlockSpec((1, 512, 128), lambda i: (layer, i, 0)),
        ],
        out_shape=shapes,
        input_output_aliases={2 + n: n for n in range(len(filled))},
        name="spread_gradients",
    )(up, down, *filled)


def ring_total(core_ref, keep_ref, took_ref, moving_ref, got_ref):
    half = got_ref.shape[0]
    arrived = moving_ref[pl.ds(pl.multiple_of(core_ref[0] * half, half), half), :]
    return keep_ref[...].astype(f32) + took_ref[...].astype(f32) + arrived.astype(f32) + got_ref[...].astype(f32)


def centred_rows(state):
    centred = state - jnp.mean(state, axis=1, keepdims=True)
    return centred, lax.rsqrt(jnp.mean(centred * centred, axis=1, keepdims=True) + norm_epsilon)


def forward_end(last, core_ref, keep_ref, took_ref, moving_ref, got_ref, state_ref, after_ref, *rest):
    state = state_ref[...].astype(f32) + ring_total(core_ref, keep_ref, took_ref, moving_ref, got_ref) + after_ref[...]
    if last:
        rest[0][...] = state.astype(bf16)
        return
    gain_ref, shift_ref, state_out, normed_ref = rest
    state_out[...] = state
    centred, inverse = centred_rows(state)
    normed_ref[...] = (centred * inverse * gain_ref[...] + shift_ref[...]).astype(bf16)


def backward_end(core_ref, keep_ref, took_ref, moving_ref, got_ref, state_ref, grad_ref, gain_ref, grad_out, low_ref, sums_ref):
    grad_normed = ring_total(core_ref, keep_ref, took_ref, moving_ref, got_ref)
    centred, inverse = centred_rows(state_ref[...].astype(f32))
    xhat = centred * inverse
    before = grad_ref[...].astype(f32)
    sums_ref[0:1] = jnp.sum(grad_normed * xhat, axis=0, keepdims=True)
    sums_ref[1:2] = jnp.sum(grad_normed, axis=0, keepdims=True)
    sums_ref[2:3] = jnp.sum(before, axis=0, keepdims=True)
    scaled = grad_normed * gain_ref[...]
    after = before + (
        scaled - jnp.mean(scaled, axis=1, keepdims=True) - xhat * jnp.mean(scaled * xhat, axis=1, keepdims=True)
    ) * inverse
    grad_out[...] = after
    low_ref[...] = after.astype(bf16)


def call_end(body, core, ring, extra, shapes, name):
    keep, took, moving, got = ring
    half, width = got.shape

    def rows_of(array):
        n = array.shape[0] // half - 1
        return pl.BlockSpec((half, width), lambda i: (n, 0))

    def whole_of(array):
        return pl.BlockSpec(array.shape, lambda i: (0,) * len(array.shape))

    return pl.pallas_call(
        body,
        grid=(1,),
        in_specs=[SMEM_SPEC, rows_of(keep), rows_of(took)] + [whole_of(x) for x in (moving, got, *extra)],
        out_specs=[whole_of(x) for x in shapes],
        out_shape=shapes,
        name=name,
    )(core, keep, took, moving, got, *extra)


def per_device(
    n_dp,
    hidden_in,
    seq_lengths,
    seq_device,
    positions,
    norm_gain,
    norm_bias,
    qkv_weight,
    qkv_bias,
    out_weight,
    fc1_weight,
    fc1_bias,
    fc2_weight,
    output_bias,
    out_cotangent,
):
    block = hidden_in.shape[0]
    half = block // 2
    width = hidden_in.shape[1]
    piece = norm_gain.shape[1]
    hidden = fc1_weight.shape[2] // GROUP
    groups = n_dp // GROUP
    chips = GROUP // 2
    side = chips // 2 - 1

    if groups == 1:
        ring = [2 * a for a in range(chips // 2)] + [2 * a + 1 for a in reversed(range(chips // 2))]
    else:
        ring = list(range(chips // 2)) + list(reversed(range(chips // 2, chips)))
    ring_pairs = []
    for g in range(groups):
        for place in range(chips):
            for core, step in ((0, 1), (1, -1)):
                ring_pairs.append(
                    (
                        g * GROUP + ring[place] * 2 + core,
                        g * GROUP + ring[(place + step) % chips] * 2 + core,
                    )
                )
    core_pairs = [(i, i ^ 1) for i in range(n_dp)]
    inner = [[g * GROUP + i for i in range(GROUP)] for g in range(groups)]
    outer = [[g * GROUP + i for g in range(groups)] for i in range(GROUP)]
    if groups == 1:
        inner = None

    def along(x):
        return lax.ppermute(x, "dp", ring_pairs)

    def across(x):
        return lax.ppermute(x, "dp", core_pairs)

    def over(x):
        return lax.ppermute(x, "tensor", [(0, 1), (1, 0)])

    index = lax.axis_index("dp")
    group = index // GROUP
    chip = (index % GROUP) // 2
    core = index % 2
    tensor = lax.axis_index("tensor")
    is_first = core == 0
    at = core * half
    off = (1 - core) * half
    core_word = core.astype(jnp.int32).reshape(1)

    def my_half(x, start, axis=0):
        return lax.dynamic_slice_in_dim(x, start, half, axis)

    def in_order(own, other):
        return jnp.where(
            is_first, jnp.concatenate([own, other], 0), jnp.concatenate([other, own], 0)
        )

    def gather_rows(mine):
        behind, ahead = [], []
        moving = mine
        for _ in range(side):
            moving = along(moving)
            behind.append(moving)
            ahead.append(across(moving))
        far = along(my_half(moving, at, moving.ndim - 2))
        return [mine] + behind + ahead + [far, across(far)]

    rows = lax.broadcasted_iota(jnp.int32, (block, 1), 0)
    mine_rows = (rows < half) == is_first

    def ring_sum(give_far, give, keep):
        took_far = across(give_far)
        took = across(give)
        far = keep[side * block : side * block + half].astype(f32) + took_far.astype(f32)
        moving = along(far.astype(bf16))
        moving = jnp.where(mine_rows, jnp.concatenate([moving, moving], 0), 0).astype(f32)
        for step in reversed(range(side)):
            here = slice(step * block, (step + 1) * block)
            moving = along((moving + keep[here].astype(f32) + took[here].astype(f32)).astype(bf16))
            if step:
                moving = moving.astype(f32)
        return keep, took, moving, across(my_half(moving, off))

    def spread(x):
        return lax.all_to_all(x, "dp", 0, 0, axis_index_groups=inner, tiled=True)

    small = jnp.concatenate(
        [
            norm_gain.reshape(-1),
            norm_bias.reshape(-1),
            output_bias.reshape(-1),
            (positions // 64).astype(bf16),
            (positions % 64).astype(bf16),
        ]
    )
    slab_rows = 3 * HEAD_DIM + hidden
    small_all = None
    weights = []
    if groups == 1:
        qkv_turned = qkv_weight.transpose(0, 2, 1, 3)
        for layer in range(LAYERS):
            extra = None
            if layer == 0:
                extra = jnp.concatenate([small, jnp.zeros_like(small)]).reshape(-1, 128)
            up = spread(call_pack_up(qkv_turned, fc1_weight, layer, extra))
            if layer == 0:
                small_all = up[:, slab_rows:].reshape(GROUP, -1)[:, : small.shape[0]]
            up_other = over(up)
            down = spread(call_pack_down(out_weight, fc2_weight, layer))
            down_other = over(down)
            weights.append((call_join_up(up, up_other), call_join_down(down, down_other)))
    else:
        small_all = lax.all_gather(small, "dp", axis=0, tiled=False)
        for layer in range(LAYERS):
            up = jnp.concatenate(
                [
                    qkv_weight[layer].reshape(piece, 3, GROUP, HEAD_DIM).transpose(2, 0, 1, 3).reshape(GROUP, piece, -1),
                    fc1_weight[layer].reshape(piece, GROUP, hidden).transpose(1, 0, 2),
                ],
                axis=2,
            )
            up = lax.all_gather(spread(up), "dp", axis=0, axis_index_groups=outer, tiled=True)
            up = up.reshape(width // 128, 128, slab_rows)
            value = up[:, :, WIDE : WIDE + HEAD_DIM]
            first = WIDE + HEAD_DIM
            up = jnp.concatenate(
                [
                    up[:, :, :WIDE],
                    jnp.concatenate([value[:, :HEAD_DIM], value[:, HEAD_DIM:]], axis=2),
                    up[:, :, first : first + 128],
                    up[:, :, first + 128 :],
                ],
                axis=1,
            )
            down = jnp.concatenate(
                [out_weight[layer].reshape(GROUP, HEAD_DIM, piece), fc2_weight[layer].reshape(GROUP, hidden, piece)],
                axis=1,
            )
            down = lax.all_gather(spread(down), "dp", axis=0, axis_index_groups=outer, tiled=True)
            down = down.transpose(1, 0, 2).reshape(-1, width // 128, 128).transpose(1, 0, 2)
            weights.append((call_join_up(up, over(up)), call_join_down(down, over(down))))
    if groups == 1:
        biases = jnp.concatenate([qkv_bias.reshape(LAYERS, 3 * HEAD_DIM), fc1_bias], axis=1)
    else:
        full_qkv = lax.all_gather(qkv_bias, "dp", axis=2, tiled=True)
        full_up = lax.all_gather(fc1_bias, "dp", axis=1, tiled=True)
        member = index % GROUP
        biases = jnp.concatenate(
            [
                lax.dynamic_slice_in_dim(full_qkv, member * HEAD_DIM, HEAD_DIM, 2).reshape(LAYERS, 3 * HEAD_DIM),
                lax.dynamic_slice_in_dim(full_up, member * hidden, hidden, 1),
            ],
            axis=1,
        )
    biases_other = over(biases)
    both_biases = jnp.stack([biases, biases_other], axis=1).astype(f32)
    bias_rows = jnp.concatenate(
        [
            both_biases[:, :, : 3 * HEAD_DIM].reshape(LAYERS, 2, 3, HEAD_DIM).transpose(0, 2, 1, 3).reshape(LAYERS, -1),
            both_biases[:, :, 3 * HEAD_DIM :].reshape(LAYERS, -1),
        ],
        axis=1,
    )
    vectors = small_all[:, : 6 * piece].reshape(n_dp, 3, LAYERS, piece).transpose(1, 2, 0, 3).reshape(3, LAYERS, 1, width).astype(f32)
    gains, shifts, after = vectors[0], vectors[1], vectors[2]

    turned = jnp.where(is_first, 1, -1)
    place = jnp.sum(jnp.where(jnp.asarray(ring) == chip, jnp.arange(chips), 0))
    offsets = [0] + [-(s + 1) for s in range(side)] + [s + 1 for s in range(side)] + [chips // 2]
    places = (place + turned * jnp.asarray(offsets)) % chips
    chip_ids = jnp.sum(
        jnp.where(places[:, None] == jnp.arange(chips)[None, :], jnp.asarray(ring)[None, :], 0), axis=1
    )
    owners = group * GROUP + 2 * chip_ids + tensor
    labels = jax.vmap(lambda owner: sequence_labels(seq_lengths, seq_device, owner, block))(owners)
    rows_at = jnp.arange(block, dtype=jnp.int32)
    allowed = (
        (labels[:, :, None] == labels[:, None, :])
        & (labels[:, :, None] > 0)
        & (rows_at[None, None, :] <= rows_at[None, :, None])
    ) | (rows_at[None, None, :] == rows_at[None, :, None])
    allowed = allowed.astype(f32).reshape(chips * block, block)
    picked = (owners[:, None] == jnp.arange(n_dp)[None, :]).astype(f32)
    place_parts = jnp.dot(picked, small_all[:, 6 * piece :].astype(f32), precision=lax.Precision.HIGHEST)
    row_places = (place_parts[:, :block] * 64.0 + place_parts[:, block:]).reshape(chips * block)
    pair = ROT // 2
    frequency = 10000.0 ** (-2.0 * jnp.arange(pair, dtype=f32) / ROT)
    angles = row_places[:, None] * frequency[None, :]
    cosine, sine = jnp.cos(angles), jnp.sin(angles)
    nought = jnp.zeros_like(sine)
    rest = jnp.zeros((chips * block, HEAD_DIM - ROT), f32)
    tables = (
        jnp.concatenate([cosine, cosine, rest + 1.0] * 2, axis=1),
        jnp.concatenate([-sine, nought, rest] * 2, axis=1),
        jnp.concatenate([nought, sine, rest] * 2, axis=1),
    )

    both = jnp.stack([hidden_in, out_cotangent])
    both = jnp.where(tensor == core, both, across(both))
    keeps = jnp.stack([jnp.ones_like(labels[0]), (labels[0] > 0).astype(labels.dtype)]).astype(bf16)
    both = both * keeps[:, :, None]
    inputs = gather_rows(both)
    mine_inputs = my_half(both, at, 1)
    state, grad_state = mine_inputs[0], mine_inputs[1]

    normed, heads, hidden_pre, wide, *parts = call_pass(
        "first", core_word, weights[0], tables, allowed, [bias_rows[0:1], gains[0], shifts[0]], inputs
    )
    rows_shape = (half, width)
    next_state, normed_own = call_end(
        partial(forward_end, False),
        core_word,
        ring_sum(*parts),
        [state, after[0], gains[1], shifts[1]],
        [jax.ShapeDtypeStruct(rows_shape, f32), jax.ShapeDtypeStruct(rows_shape, bf16)],
        "forward_end",
    )
    normed_chunks = gather_rows(in_order(normed_own, across(normed_own)))

    def handed_back(own_rows):
        filled = in_order(own_rows, across(own_rows))
        return jnp.where(tensor == core, filled, over(filled))

    def summed(own, other):
        total = own.astype(f32) + over(other).astype(f32)
        if groups > 1:
            total = total.transpose(1, 0, 2).reshape(total.shape[1], width)
            total = lax.psum_scatter(total, "dp", scatter_dimension=1, axis_index_groups=outer, tiled=True)
            total = total.reshape(total.shape[0], GROUP, piece).transpose(1, 0, 2)
        return spread(total.astype(bf16))

    down_own = [(0, HEAD_DIM), (WIDE, WIDE + hidden)]
    down_other = [(HEAD_DIM, WIDE), (WIDE + hidden, WIDE + 2 * hidden)]
    up_own = [(p * WIDE, p * WIDE + HEAD_DIM) for p in range(3)] + [(3 * WIDE, 3 * WIDE + hidden)]
    up_other = [(p * WIDE + HEAD_DIM, (p + 1) * WIDE) for p in range(3)] + [(3 * WIDE + hidden, 3 * WIDE + 2 * hidden)]

    def down_gradients(wide_rows, grad_rows):
        own, other = call_gradients(wide_rows, grad_rows, down_own, down_other, False, "down_gradients")
        return summed(own, other)

    def up_gradients(slim_rows, normed_rows):
        own, other, sums = call_gradients(slim_rows, normed_rows, up_own, up_other, True, "up_gradients")
        return summed(own, other), sums

    def backward_finish(parts, state, grad_state, layer):
        return call_end(
            backward_end,
            core_word,
            ring_sum(*parts),
            [state, grad_state, gains[layer]],
            [
                jax.ShapeDtypeStruct(rows_shape, f32),
                jax.ShapeDtypeStruct(rows_shape, bf16),
                jax.ShapeDtypeStruct((3, width), f32),
            ],
            "backward_end",
        )

    normed_last, grad_rows, wide_last, slim, *parts = call_pass(
        "middle", core_word, weights[1], tables, allowed, [bias_rows[1:2]], normed_chunks + inputs
    )
    grad_state, grad_low, sums_last = backward_finish(parts[3:], next_state, grad_state, 1)
    grad_chunks = gather_rows(in_order(grad_low, across(grad_low)))
    down_last = down_gradients(wide_last, grad_rows)
    up_last, bias_last = up_gradients(slim, normed_last)
    (hidden_out,) = call_end(
        partial(forward_end, True),
        core_word,
        ring_sum(*parts[:3]),
        [next_state, after[1]],
        [jax.ShapeDtypeStruct(rows_shape, bf16)],
        "forward_out",
    )
    hidden_out = handed_back(hidden_out)

    grad_rows, slim, *parts = call_pass(
        "last", core_word, weights[0], tables, allowed, [heads, hidden_pre], grad_chunks
    )
    down_first = down_gradients(wide, grad_rows)
    up_first, bias_first = up_gradients(slim, normed)
    _, grad_low, sums_first = backward_finish(parts, state, grad_state, 0)
    grad_hidden = handed_back(grad_low).astype(f32)

    vectors = jnp.stack([sums_first, sums_last]).reshape(LAYERS * 3, n_dp, piece).transpose(1, 0, 2)
    vectors = jnp.sum(lax.all_to_all(vectors, "dp", 0, 0, tiled=True), axis=0)
    vectors = (vectors + over(vectors)).reshape(LAYERS, 3, piece)
    sums = jnp.concatenate([bias_first, bias_last], axis=0)
    sums_qkv = sums[:, : 3 * WIDE].reshape(LAYERS, 3, 2, HEAD_DIM)
    sums_up = sums[:, 3 * WIDE :].reshape(LAYERS, 2, hidden)
    bias_own, bias_other = (
        jnp.concatenate([sums_qkv[:, :, n].reshape(LAYERS, -1), sums_up[:, n]], axis=1) for n in range(2)
    )
    bias_sums = bias_own + over(bias_other)
    bias_qkv, bias_up = bias_sums[:, : 3 * HEAD_DIM].reshape(LAYERS, 3, HEAD_DIM), bias_sums[:, 3 * HEAD_DIM :]
    if groups == 1:
        filled = call_spread(up_last, down_last, 1, [])
        grad_qkv, grad_out, grad_up, grad_down = call_spread(up_first, down_first, 0, filled)
        grad_qkv = grad_qkv.transpose(0, 2, 1, 3)
    else:
        bias_qkv = lax.all_gather(lax.psum(bias_qkv, "dp", axis_index_groups=outer), "dp", axis=2, axis_index_groups=inner, tiled=True)
        bias_up = lax.all_gather(lax.psum(bias_up, "dp", axis_index_groups=outer), "dp", axis=1, axis_index_groups=inner, tiled=True)
        bias_qkv = lax.dynamic_slice_in_dim(bias_qkv, index * qkv_bias.shape[2], qkv_bias.shape[2], 2)
        bias_up = lax.dynamic_slice_in_dim(bias_up, index * fc1_bias.shape[1], fc1_bias.shape[1], 1)
        ups = jnp.stack([up_first, up_last]).astype(f32)
        downs = jnp.stack([down_first, down_last]).astype(f32)
        grad_qkv = ups[:, :, : 3 * HEAD_DIM].reshape(LAYERS, GROUP, 3, HEAD_DIM, piece).transpose(0, 4, 2, 1, 3).reshape(LAYERS, piece, 3, -1)
        grad_up = ups[:, :, 3 * HEAD_DIM :].transpose(0, 3, 1, 2).reshape(LAYERS, piece, -1)
        grad_out = downs[:, :, :HEAD_DIM].reshape(LAYERS, -1, piece)
        grad_down = downs[:, :, HEAD_DIM:].reshape(LAYERS, -1, piece)
    return (
        hidden_out,
        grad_hidden,
        vectors[:, 0],
        vectors[:, 1],
        grad_qkv,
        bias_qkv,
        grad_out,
        grad_up,
        bias_up,
        grad_down,
        vectors[:, 2],
    )


def solution(mesh):
    placed = (
        P("dp", None),
        P(),
        P(),
        P("dp"),
        P(None, "dp"),
        P(None, "dp"),
        P(None, "dp", None, "tensor"),
        P(None, None, ("tensor", "dp")),
        P(None, "tensor", "dp"),
        P(None, "dp", "tensor"),
        P(None, ("tensor", "dp")),
        P(None, "tensor", "dp"),
        P(None, "dp"),
        P("dp", None),
    )
    return jax.shard_map(
        partial(per_device, mesh.shape["dp"]),
        mesh=mesh,
        in_specs=placed,
        out_specs=(
            P("dp", None),
            P("dp", None),
            P(None, "dp"),
            P(None, "dp"),
            P(None, "dp", None, "tensor"),
            P(None, None, ("tensor", "dp")),
            P(None, "tensor", "dp"),
            P(None, "dp", "tensor"),
            P(None, ("tensor", "dp")),
            P(None, "tensor", "dp"),
            P(None, "dp"),
        ),
        check_vma=False,
    )
```

time: 886 us -> 896 us (1.011)
  waiting for transfers between devices: 318 us -> 487 us
  Pallas kernels: 33 us -> 200 us
  local copies, waits for them, and re-layouts: 158 us -> 26.1 us
  matrix products: 97.6 us -> 0.19 us
  other arithmetic: 98.9 us -> 49.2 us
  blocking collectives: 36.8 us -> 0 us
    pallas_call x4 -> x21, Pallas kernels: 33 us -> 200 us  [the longest x3 89.1 us: call_pass(): pl.pallas_call(partial(layer_pass, mode), in_specs=[SMEM_SPEC] + [VMEM_SP...]
    ppermute x32 -> x28, waiting for transfers between devices: 184 us -> 318 us  [along(): return lax.ppermute(x, 'dp', ring_pairs)]
    dot_general x25 -> x1, matrix products: 97.6 us -> 0.19 us  [per_device(): jnp.dot(picked, small_all[:, 6 * piece:].astype(f32), precision=lax.Preci...]
    unnamed x261 -> x104, local copies, waits for them, and re-layouts: 78.5 us -> 11.5 us
    slice x66 -> x5, local copies, waits for them, and re-layouts: 55.6 us -> 0.12 us  [the longest x1 0.07 us: per_device(): both_biases[:, :, 3 * HEAD_DIM:].reshape(LAYERS, -1)]
    all_gather x1 -> x0, blocking collectives: 36.8 us -> none  [per_device(): small = lax.all_gather(small, 'dp', axis=0, tiled=False)]
    ppermute x13, waiting for transfers between devices: 98 us -> 134 us  [over(): return lax.ppermute(x, 'tensor', [(0, 1), (1, 0)])]
    concatenate x20 -> x3, other arithmetic: 21.3 us -> 0.7 us  [the longest x1 0.61 us: per_device(): jnp.concatenate([both_biases[:, :, :3 * HEAD_DIM].reshape(LAYERS, 2, 3, H...]
  transfers between devices with their start and end apart: 85 -> 79, of which waited for: 37 -> 37; matrix products, arithmetic and copies ran while one was open for 33% -> 7% of each run, Pallas kernels for 3% -> 14%
where the time goes in v2:
time: 896 us; the launch traced here: 889 us
  waiting for transfers between devices  487 us (54%)
  Pallas kernels  200 us (22%)
  starting transfers between devices  124 us (14%)
  other arithmetic  49.2 us (5%)
  local copies, waits for them, and re-layouts  26.1 us (3%)
    ppermute x28, waiting for transfers between devices, along(): return lax.ppermute(x, 'dp', ring_pairs)  318 us
    ppermute x13, waiting for transfers between devices, over(): return lax.ppermute(x, 'tensor', [(0, 1), (1, 0)])  134 us
    pallas_call x3, Pallas kernels, call_pass(): pl.pallas_call(partial(layer_pass, mode), in_specs=[SMEM_SPEC] + [VMEM_SP...  89.1 us
    all_to_all x8, starting transfers between devices, spread(): return lax.all_to_all(x, 'dp', 0, 0, axis_index_groups=inner, tiled=True)  55.2 us
    pallas_call x4, Pallas kernels, call_gradients(): pl.pallas_call(partial(gradient_slabs, own_rows, other_rows, with_sums),...  37.1 us
    ppermute x29, starting transfers between devices, across(): return lax.ppermute(x, 'dp', core_pairs)  27.5 us
    ppermute x28, starting transfers between devices, along(): return lax.ppermute(x, 'dp', ring_pairs)  23.7 us
    all_to_all x8, waiting for transfers between devices, spread(): return lax.all_to_all(x, 'dp', 0, 0, axis_index_groups=inner, tiled=True)  19.9 us
  transfers between devices with their start and end apart: 79, of which 37 were waited for; matrix products, arithmetic and copies ran while one was open for 7% of the time, Pallas kernels for 14%

profile of v2, /device:TPU:13, one launch (start us, length us, event | category | flops | bytes accessed | tf_op | source)
XLA Modules:
  0.0 888.8 jit_solution(1916752482125759716)
XLA Ops:
  0.6 5.3 pack_down.3
  6.1 6.7 all-to-all-start.3
  16.9 5.9 pack_up.3
  23.4 19.9 %all-to-all-done.3.own_ref = bf16[16,320,128]{2,1,0:T(8,128)(2,1)S(1)} async-done(((bf16[16,320,128]{2,1,0:T(8,128)(2,1)}), bf16[16,320,128]{2,1,0:T(8,128)(2,1)S(1)}, u32[]{:S(2)}, u32[]{:S(2)}) %all-to-all-start.3) | async-done | bytes 1310752 | tf_op jit(solution)/shard_map/all_to_all | solution.py:657
  43.3 4.7 all-to-all-start.2
  51.9 48.9 %collective-permute-done.6.refs_11_.refs_18_ = bf16[2,128,2048]{2,1,0:T(8,128)(2,1)S(1)} collective-permute-done((bf16[2,128,2048]{2,1,0:T(8,128)(2,1)S(1)}, bf16[2,128,2048]{2,1,0:T(8,128)(2,1)S(1)}, u32[]{:S(2)}, u32[]{:S(2)}) %collective-permute-start.6) | collective-permute-done | bytes 1048608 | tf_op jit(solution)/shard_map/ppermute | solution.py:604
  102.7 12.1 %collective-permute-done.7.refs_12_.refs_19_ = bf16[2,128,2048]{2,1,0:T(8,128)(2,1)} collective-permute-done((bf16[2,128,2048]{2,1,0:T(8,128)(2,1)S(1)}, bf16[2,128,2048]{2,1,0:T(8,128)(2,1)}, u32[]{:S(2)}, u32[]{:S(2)}) %collective-permute-start.7) | collective-permute-done | bytes 1048608 | tf_op jit(solution)/shard_map/ppermute | solution.py:604
  121.0 25.1 %collective-permute-done.2 = bf16[2,448]{1,0:T(2,128)(2,1)S(1)} collective-permute-done((bf16[2,448]{1,0:T(2,128)(2,1)S(1)}, bf16[2,448]{1,0:T(2,128)(2,1)S(1)}, u32[]{:S(2)}, u32[]{:S(2)}) %collective-permute-start.2) | collective-permute-done | bytes 1824 | tf_op jit(solution)/shard_map/ppermute | solution.py:610
  147.0 3.8 collective-permute-start.9
  153.9 3.1 multiply_sine_fusion
  157.0 3.4 collective-permute-done.12.refs_17_.refs_24_
  169.8 6.3 join_down.3.refs_2_
  176.1 10.8 %collective-permute-done.3.other_ref = bf16[16,464,128]{2,1,0:T(8,128)(2,1)} collective-permute-done((bf16[16,464,128]{2,1,0:T(8,128)(2,1)S(1)}, bf16[16,464,128]{2,1,0:T(8,128)(2,1)}, u32[]{:S(2)}, u32[]{:S(2)}) %collective-permute-start.3) | collective-permute-done | bytes 1900576 | tf_op jit(solution)/shard_map/ppermute | solution.py:610
  186.8 7.0 join_up.3.refs_1_
  193.8 29.3 %pass_first.1 = (bf16[1024,2048]{1,0:T(8,128)(2,1)}, bf16[1024,384]{1,0:T(8,128)(2,1)}, f32[1024,512]{1,0:T(8,128)}, bf16[1024,640]{1,0:T(8,128)(2,1)}, bf16[64,...) custom-call(s32[1]{0:T(128)} %bitcast.refs_0_.core_ref, bf16[2048,896]{1,0:T(8,128)(2,1)} %join_up.3.refs_1_, ...), custom_call_target="tpu_custom_call" | custom-call | flops 6442450944 | bytes 20000000 | tf_op jit(solution)/shard_map/pass_first/pallas_call | solution.py:394
  225.3 5.9 pack_up.2
  231.2 4.4 all-to-all-start
  238.4 40.0 %collective-permute-done.16 = bf16[64,2048]{1,0:T(8,128)(2,1)S(1)} collective-permute-done((bf16[64,2048]{1,0:T(8,128)(2,1)S(1)}, bf16[64,2048]{1,0:T(8,128)(2,1)S(1)}, u32[]{:S(2)}, u32[]{:S(2)}) %collective-permute-start.16) | collective-permute-done | bytes 262176 | tf_op jit(solution)/shard_map/ppermute | solution.py:604
  281.7 6.4 collective-permute-done.17
  292.1 5.3 pack_down.2
  297.5 6.4 all-to-all-start.1
  307.6 31.0 %collective-permute-done.19.moving_ref = bf16[128,2048]{1,0:T(8,128)(2,1)S(1)} collective-permute-done((bf16[128,2048]{1,0:T(8,128)(2,1)}, bf16[128,2048]{1,0:T(8,128)(2,1)S(1)}, u32[]{:S(2)}, u32[]{:S(2)}) %collective-permute-start.19) | collective-permute-done | bytes 524320 | tf_op jit(solution)/shard_map/ppermute | solution.py:604
  351.1 7.2 collective-permute-done.22.refs_9_
  358.3 8.6 collective-permute-done.23.refs_10_
  368.8 6.8 collective-permute-done.24.refs_11_
  376.6 42.8 %collective-permute-done.1.other_ref = bf16[16,320,128]{2,1,0:T(8,128)(2,1)S(1)} collective-permute-done((bf16[16,320,128]{2,1,0:T(8,128)(2,1)S(1)}, bf16[16,320,128]{2,1,0:T(8,128)(2,1)S(1)}, u32[]{:S(2)}, u32[]{:S(2)}) %collective-permute-start.1) | collective-permute-done | bytes 1310752 | tf_op jit(solution)/shard_map/ppermute | solution.py:610
  421.5 6.1 join_down.2.refs_2_
  428.8 6.9 join_up.2.refs_1_
  436.5 35.4 %pass_middle.1 = (bf16[1024,2048]{1,0:T(8,128)(2,1)}, bf16[1024,2048]{1,0:T(8,128)(2,1)}, bf16[1024,640]{1,0:T(8,128)(2,1)}, bf16[1024,896]{1,0:T(8,128)(2,1)}, ...) custom-call(s32[1]{0:T(128)} %bitcast.refs_0_.core_ref, ...), custom_call_target="tpu_custom_call" | custom-call | flops 12884901888 | bytes 40000000 | tf_op jit(solution)/shard_map/pass_middle/pallas_call | solution.py:394
  472.5 3.9 collective-permute-done.40
  477.5 5.5 collective-permute-done.41
  484.8 8.3 collective-permute-done.42
  493.4 8.3 collective-permute-done.43
  502.0 8.3 collective-permute-done.44.moving_ref
  510.4 3.9 collective-permute-start.45
  516.1 3.0 backward_end.2
  522.1 8.7 down_gradients.3
  532.1 8.3 collective-permute-done.48.refs_11_
  542.4 6.3 collective-permute-done.49.refs_12_
  548.8 12.2 %collective-permute-done.68 = bf16[16,320,128]{2,1,0:T(8,128)(2,1)S(1)} collective-permute-done((bf16[16,320,128]{2,1,0:T(8,128)(2,1)}, bf16[16,320,128]{2,1,0:T(8,128)(2,1)S(1)}, u32[]{:S(2)}, u32[]{:S(2)}) %collective-permute-start.68) | collective-permute-done | bytes 1310752 | tf_op jit(solution)/shard_map/ppermute | solution.py:610
  565.0 14.2 %all-to-all-start.8 = ((bf16[16,320,128]{2,1,0:T(8,128)(2,1)}), bf16[16,320,128]{2,1,0:T(8,128)(2,1)S(1)}, u32[]{:S(2)}, u32[]{:S(2)}) async-start(bf16[16,320,128]{2,1,0:T(8,128)(2,1)} %add_convert_fusion.2), calls=%async_computation.8 | async-start | bytes 2621440 | tf_op jit(solution)/shard_map/all_to_all | solution.py:657
  579.7 9.9 %up_gradients.3 = (bf16[16,448,128]{2,1,0:T(8,128)(2,1)}, bf16[16,448,128]{2,1,0:T(8,128)(2,1)}, f32[1,896]{1,0:T(1,128)}) custom-call(bf16[1024,896]{1,0:T(8,128)(2,1)} %get-tuple-element.87.left_ref, bf16[1024,2048]{1,0:T(8,128)(2,1)} %get-tuple-element.88.right_ref), custom_call_target="tpu_custom_call" | custom-call | flops 3758096384 | bytes 13369344 | tf_op jit(solution)/shard_map/up_gradients/pallas_call | solution.py:441
  591.5 24.4 %pass_last.1 = (bf16[1024,2048]{1,0:T(8,128)(2,1)}, bf16[1024,896]{1,0:T(8,128)(2,1)}, bf16[64,2048]{1,0:T(8,128)(2,1)}, bf16[448,2048]{1,0:T(8,128)(2,1)}, bf16[512,2048]{1,0:T(8,128)(2,1)}) custom-call(s32[1]{0:T(128)} %bitcast.refs_0_.core_ref, bf16[2048,896]{1,0:T(8,128)(2,1)} %join_up.3.refs_1_, bf16[640,2048]{1,0:T(8,128)(2,1)} %join_down.3.refs_2_, ...), custom_call_target="tpu_custom_call" | custom-call | flops 6442450944 | bytes 20000000 | tf_op jit(solution)/shard_map/pass_last/pallas_call | solution.py:394
  617.0 3.5 collective-permute-done.31
  625.4 6.0 collective-permute-done.67
  631.4 3.8 add_convert_fusion
  636.4 6.6 all-to-all-start.7
  643.1 3.1 add_convert_fusion.6
  647.4 41.4 %collective-permute-done.58 = bf16[128,2048]{1,0:T(8,128)(2,1)S(1)} collective-permute-done((bf16[128,2048]{1,0:T(8,128)(2,1)S(1)}, bf16[128,2048]{1,0:T(8,128)(2,1)S(1)}, u32[]{:S(2)}, u32[]{:S(2)}) %collective-permute-start.58) | collective-permute-done | bytes 524320 | tf_op jit(solution)/shard_map/ppermute | solution.py:604
  692.2 8.6 down_gradients.2
  703.5 8.4 collective-permute-done.60.moving_ref
  715.4 3.1 backward_end.3
  720.0 5.6 all-to-all-start.4
  725.6 5.4 collective-permute-done.66
  733.7 5.2 all-to-all-start.6
  738.9 9.9 %up_gradients.2 = (bf16[16,448,128]{2,1,0:T(8,128)(2,1)}, bf16[16,448,128]{2,1,0:T(8,128)(2,1)}, f32[1,896]{1,0:T(1,128)}) custom-call(bf16[1024,896]{1,0:T(8,128)(2,1)} %get-tuple-element.79.left_ref, bf16[1024,2048]{1,0:T(8,128)(2,1)} %get-tuple-element.80.right_ref), custom_call_target="tpu_custom_call" | custom-call | flops 3758096384 | bytes 13369344 | tf_op jit(solution)/shard_map/up_gradients/pallas_call | solution.py:441
  751.2 22.4 %collective-permute-done.33 = bf16[128,2048]{1,0:T(8,128)(2,1)S(1)} collective-permute-done((bf16[128,2048]{1,0:T(8,128)(2,1)}, bf16[128,2048]{1,0:T(8,128)(2,1)S(1)}, u32[]{:S(2)}, u32[]{:S(2)}) %collective-permute-start.33) | collective-permute-done | bytes 524320 | tf_op jit(solution)/shard_map/ppermute | solution.py:604
  777.7 12.4 %collective-permute-done.65 = bf16[16,448,128]{2,1,0:T(8,128)(2,1)S(1)} collective-permute-done((bf16[16,448,128]{2,1,0:T(8,128)(2,1)}, bf16[16,448,128]{2,1,0:T(8,128)(2,1)S(1)}, u32[]{:S(2)}, u32[]{:S(2)}) %collective-permute-start.65) | collective-permute-done | bytes 1835040 | tf_op jit(solution)/shard_map/ppermute | solution.py:610
  793.0 6.9 all-to-all-start.5
  802.6 7.2 spread_gradients.2
  809.8 35.8 %collective-permute-done.35.moving_ref = bf16[128,2048]{1,0:T(8,128)(2,1)S(1)} collective-permute-done((bf16[128,2048]{1,0:T(8,128)(2,1)S(1)}, bf16[128,2048]{1,0:T(8,128)(2,1)S(1)}, u32[]{:S(2)}, u32[]{:S(2)}) %collective-permute-start.35) | collective-permute-done | bytes 524320 | tf_op jit(solution)/shard_map/ppermute | solution.py:604
  859.6 9.5 %collective-permute-done.38 = bf16[128,2048]{1,0:T(8,128)(2,1)S(1)} collective-permute-done((bf16[128,2048]{1,0:T(8,128)(2,1)S(1)}, bf16[128,2048]{1,0:T(8,128)(2,1)S(1)}, u32[]{:S(2)}, u32[]{:S(2)}) %collective-permute-start.38) | collective-permute-done | bytes 524320 | tf_op jit(solution)/shard_map/ppermute | solution.py:610
  869.9 10.4 %collective-permute-done.63 = bf16[128,2048]{1,0:T(8,128)(2,1)S(1)} collective-permute-done((bf16[128,2048]{1,0:T(8,128)(2,1)S(1)}, bf16[128,2048]{1,0:T(8,128)(2,1)S(1)}, u32[]{:S(2)}, u32[]{:S(2)}) %collective-permute-start.63) | collective-permute-done | bytes 524320 | tf_op jit(solution)/shard_map/ppermute | solution.py:610
  881.3 7.2 spread_gradients.3
  (319 shorter events, 133.9 us)
Async XLA Ops:
  6.1 37.2 %all-to-all-start.3 = ((bf16[16,320,128]{2,1,0:T(8,128)(2,1)}), bf16[16,320,128]{2,1,0:T(8,128)(2,1)S(1)}, u32[]{:S(2)}, u32[]{:S(2)}) async-start(bf16[16,320,128]{2,1,0:T(8,128)(2,1)} %pack_down.3), calls=%async_computation.3 | async-start | bytes 2621440 | tf_op jit(solution)/shard_map/all_to_all | solution.py:657
  13.8 34.3 %collective-permute-start.5 = (bf16[2,128,2048]{2,1,0:T(8,128)(2,1)}, bf16[2,128,2048]{2,1,0:T(8,128)(2,1)}, u32[]{:S(2)}, u32[]{:S(2)}) collective-permute-start(bf16[2,128,2048]{2,1,0:T(8,128)(2,1)} %pad_maximum_fusion), channel_id=1, source_target_pairs={{0,2},{2,0},{4,6},{6,4},{8,10},{10,8},{12,14},{14,12},{16,18},{18,... | collective-permute-start | bytes 3145736 | tf_op jit(solution)/shard_map/ppermute | solution.py:607
  43.3 75.3 %all-to-all-start.2 = ((bf16[16,464,128]{2,1,0:T(8,128)(2,1)}), bf16[16,464,128]{2,1,0:T(8,128)(2,1)S(1)}, u32[]{:S(2)}, u32[]{:S(2)}) async-start(bf16[16,464,128]{2,1,0:T(8,128)(2,1)} %pack_up.3), calls=%async_computation.2 | async-start | bytes 3801088 | tf_op jit(solution)/shard_map/all_to_all | solution.py:657
  50.8 50.1 %collective-permute-start.6 = (bf16[2,128,2048]{2,1,0:T(8,128)(2,1)S(1)}, bf16[2,128,2048]{2,1,0:T(8,128)(2,1)S(1)}, u32[]{:S(2)}, u32[]{:S(2)}) collective-permute-start(bf16[2,128,2048]{2,1,0:T(8,128)(2,1)S(1)} %select_multiply_fusion.refs_10_.refs_17_), channel_id=1, source_target_pairs={{0,8},{2,6},{8,16},{10,2},{16,24},{18,10},{24,28},{26,18},{28,20},... | collective-permute-start | bytes 3145736 | tf_op jit(solution)/shard_map/ppermute | solution.py:604
  100.8 14.0 %collective-permute-start.7 = (bf16[2,128,2048]{2,1,0:T(8,128)(2,1)S(1)}, bf16[2,128,2048]{2,1,0:T(8,128)(2,1)}, u32[]{:S(2)}, u32[]{:S(2)}) collective-permute-start(bf16[2,128,2048]{2,1,0:T(8,128)(2,1)S(1)} %collective-permute-done.6.refs_11_.refs_18_), channel_id=1, source_target_pairs={{0,8},{2,6},{8,16},{10,2},{16,24},{18,10},{24,28},{26,18},{28,20},... | collective-permute-start | bytes 3145736 | tf_op jit(solution)/shard_map/ppermute | solution.py:604
  114.9 36.0 %collective-permute-start.8 = (bf16[2,128,2048]{2,1,0:T(8,128)(2,1)}, bf16[2,128,2048]{2,1,0:T(8,128)(2,1)}, u32[]{:S(2)}, u32[]{:S(2)}) collective-permute-start(bf16[2,128,2048]{2,1,0:T(8,128)(2,1)} %collective-permute-done.7.refs_12_.refs_19_), channel_id=1, source_target_pairs={{0,8},{2,6},{8,16},{10,2},{16,24},{18,10},{24,28},{26,18},{28,20},... | collective-permute-start | bytes 3145736 | tf_op jit(solution)/shard_map/ppermute | solution.py:604
  116.9 37.0 %collective-permute-start.4 = (bf16[16,320,128]{2,1,0:T(8,128)(2,1)S(1)}, bf16[16,320,128]{2,1,0:T(8,128)(2,1)}, u32[]{:S(2)}, u32[]{:S(2)}) collective-permute-start(bf16[16,320,128]{2,1,0:T(8,128)(2,1)S(1)} %all-to-all-done.3.own_ref), channel_id=1, source_target_pairs={{0,1},{1,0},{2,3},{3,2},{4,5},{5,4},{6,7},{7,6},{8,9},{9,8},{10,11... | collective-permute-start | bytes 3932168 | tf_op jit(solution)/shard_map/ppermute | solution.py:610
  118.2 27.9 %collective-permute-start.2 = (bf16[2,448]{1,0:T(2,128)(2,1)S(1)}, bf16[2,448]{1,0:T(2,128)(2,1)S(1)}, u32[]{:S(2)}, u32[]{:S(2)}) collective-permute-start(bf16[2,448]{1,0:T(2,128)(2,1)S(1)} %pad_maximum_fusion.6), channel_id=1, source_target_pairs={{0,1},{1,0},{2,3},{3,2},{4,5},{5,4},{6,7},{7,6},{8,9},{9,8},{10,11... | collective-permute-start | bytes 5384 | tf_op jit(solution)/shard_map/ppermute | solution.py:610
  118.6 68.2 %collective-permute-start.3 = (bf16[16,464,128]{2,1,0:T(8,128)(2,1)S(1)}, bf16[16,464,128]{2,1,0:T(8,128)(2,1)}, u32[]{:S(2)}, u32[]{:S(2)}) collective-permute-start(bf16[16,464,128]{2,1,0:T(8,128)(2,1)S(1)} %all-to-all-done.2.own_ref), channel_id=1, source_target_pairs={{0,1},{1,0},{2,3},{3,2},{4,5},{5,4},{6,7},{7,6},{8,9},{9,8},{10,11... | collective-permute-start | bytes 5701640 | tf_op jit(solution)/shard_map/ppermute | solution.py:610
  147.0 46.8 %collective-permute-start.9 = (bf16[2,128,2048]{2,1,0:T(8,128)(2,1)}, bf16[2,128,2048]{2,1,0:T(8,128)(2,1)}, u32[]{:S(2)}, u32[]{:S(2)}) collective-permute-start(bf16[2,128,2048]{2,1,0:T(8,128)(2,1)} %copy-done.39), channel_id=1, source_target_pairs={{0,2},{2,0},{4,6},{6,4},{8,10},{10,8},{12,14},{14,12},{16,18},{18,... | collective-permute-start | bytes 3145736 | tf_op jit(solution)/shard_map/ppermute | solution.py:607
  150.8 43.0 %collective-permute-start.10 = (bf16[2,128,2048]{2,1,0:T(8,128)(2,1)}, bf16[2,128,2048]{2,1,0:T(8,128)(2,1)}, u32[]{:S(2)}, u32[]{:S(2)}) collective-permute-start(bf16[2,128,2048]{2,1,0:T(8,128)(2,1)} %collective-permute-done.7.refs_12_.refs_19_), channel_id=1, source_target_pairs={{0,2},{2,0},{4,6},{6,4},{8,10},{10,8},{12,14},{14,12},{16,18},{18,... | collective-permute-start | bytes 3145736 | tf_op jit(solution)/shard_map/ppermute | solution.py:607
  152.0 8.5 collective-permute-start.12
  153.9 39.9 %collective-permute-start.11 = (bf16[2,128,2048]{2,1,0:T(8,128)(2,1)}, bf16[2,128,2048]{2,1,0:T(8,128)(2,1)}, u32[]{:S(2)}, u32[]{:S(2)}) collective-permute-start(bf16[2,128,2048]{2,1,0:T(8,128)(2,1)} %collective-permute-done.8.refs_13_.refs_20_), channel_id=1, source_target_pairs={{0,2},{2,0},{4,6},{6,4},{8,10},{10,8},{12,14},{14,12},{16,18},{18,... | collective-permute-start | bytes 3145736 | tf_op jit(solution)/shard_map/ppermute | solution.py:607
  160.4 33.4 %collective-permute-start.13 = (bf16[2,64,2048]{2,1,0:T(8,128)(2,1)}, bf16[2,64,2048]{2,1,0:T(8,128)(2,1)}, u32[]{:S(2)}, u32[]{:S(2)}) collective-permute-start(bf16[2,64,2048]{2,1,0:T(8,128)(2,1)} %collective-permute-done.12.refs_17_.refs_24_), channel_id=1, source_target_pairs={{0,2},{2,0},{4,6},{6,4},{8,10},{10,8},{12,14},{14,12},{16,18},{18,... | collective-permute-start | bytes 1572872 | tf_op jit(solution)/shard_map/ppermute | solution.py:607
  223.1 55.3 %collective-permute-start.14 = (bf16[448,2048]{1,0:T(8,128)(2,1)}, bf16[448,2048]{1,0:T(8,128)(2,1)}, u32[]{:S(2)}, u32[]{:S(2)}) collective-permute-start(bf16[448,2048]{1,0:T(8,128)(2,1)} %get-tuple-element.59), channel_id=1, source_target_pairs={{0,2},{2,0},{4,6},{6,4},{8,10},{10,8},{12,14},{14,12},{16,18},{18,... | collective-permute-start | bytes 5505032 | tf_op jit(solution)/shard_map/ppermute | solution.py:607
  231.2 66.3 %all-to-all-start = ((bf16[16,448,128]{2,1,0:T(8,128)(2,1)}), bf16[16,448,128]{2,1,0:T(8,128)(2,1)}, u32[]{:S(2)}, u32[]{:S(2)}) async-start(bf16[16,448,128]{2,1,0:T(8,128)(2,1)} %pack_up.2), calls=%async_computation | async-start | bytes 3670016 | tf_op jit(solution)/shard_map/all_to_all | solution.py:657
  237.3 41.0 %collective-permute-start.16 = (bf16[64,2048]{1,0:T(8,128)(2,1)S(1)}, bf16[64,2048]{1,0:T(8,128)(2,1)S(1)}, u32[]{:S(2)}, u32[]{:S(2)}) collective-permute-start(bf16[64,2048]{1,0:T(8,128)(2,1)S(1)} %add_convert_fusion.19), channel_id=1, source_target_pairs={{0,8},{2,6},{8,16},{10,2},{16,24},{18,10},{24,28},{26,18},{28,20},... | collective-permute-start | bytes 786440 | tf_op jit(solution)/shard_map/ppermute | solution.py:604
  279.8 8.4 collective-permute-start.17
  290.2 13.7 %collective-permute-start.18 = (bf16[128,2048]{1,0:T(8,128)(2,1)}, bf16[128,2048]{1,0:T(8,128)(2,1)}, u32[]{:S(2)}, u32[]{:S(2)}) collective-permute-start(bf16[128,2048]{1,0:T(8,128)(2,1)} %add_convert_fusion.14), channel_id=1, source_target_pairs={{0,8},{2,6},{8,16},{10,2},{16,24},{18,10},{24,28},{26,18},{28,20},... | collective-permute-start | bytes 1572872 | tf_op jit(solution)/shard_map/ppermute | solution.py:604
  297.5 53.4 %all-to-all-start.1 = ((bf16[16,320,128]{2,1,0:T(8,128)(2,1)}), bf16[16,320,128]{2,1,0:T(8,128)(2,1)S(1)}, u32[]{:S(2)}, u32[]{:S(2)}) async-start(bf16[16,320,128]{2,1,0:T(8,128)(2,1)} %pack_down.2), calls=%async_computation.1 | async-start | bytes 2621440 | tf_op jit(solution)/shard_map/all_to_all | solution.py:657
  306.1 32.4 %collective-permute-start.19 = (bf16[128,2048]{1,0:T(8,128)(2,1)}, bf16[128,2048]{1,0:T(8,128)(2,1)S(1)}, u32[]{:S(2)}, u32[]{:S(2)}) collective-permute-start(bf16[128,2048]{1,0:T(8,128)(2,1)} %add_convert_fusion.13), channel_id=1, source_target_pairs={{0,8},{2,6},{8,16},{10,2},{16,24},{18,10},{24,28},{26,18},{28,20},... | collective-permute-start | bytes 1572872 | tf_op jit(solution)/shard_map/ppermute | solution.py:604
  349.7 8.6 collective-permute-start.22
  349.7 77.9 %collective-permute-start = (bf16[16,448,128]{2,1,0:T(8,128)(2,1)}, bf16[16,448,128]{2,1,0:T(8,128)(2,1)S(1)}, u32[]{:S(2)}, u32[]{:S(2)}) collective-permute-start(bf16[16,448,128]{2,1,0:T(8,128)(2,1)} %all-to-all-done.own_ref), channel_id=1, source_target_pairs={{0,1},{1,0},{2,3},{3,2},{4,5},{5,4},{6,7},{7,6},{8,9},{9,8},{10,11... | collective-permute-start | bytes 5505032 | tf_op jit(solution)/shard_map/ppermute | solution.py:610
  350.9 68.5 %collective-permute-start.1 = (bf16[16,320,128]{2,1,0:T(8,128)(2,1)S(1)}, bf16[16,320,128]{2,1,0:T(8,128)(2,1)S(1)}, u32[]{:S(2)}, u32[]{:S(2)}) collective-permute-start(bf16[16,320,128]{2,1,0:T(8,128)(2,1)S(1)} %all-to-all-done.1.own_ref), channel_id=1, source_target_pairs={{0,1},{1,0},{2,3},{3,2},{4,5},{5,4},{6,7},{7,6},{8,9},{9,8},{10,11... | collective-permute-start | bytes 3932168 | tf_op jit(solution)/shard_map/ppermute | solution.py:610
  358.3 8.6 collective-permute-start.23
  366.9 8.6 collective-permute-start.24
  366.9 68.8 %collective-permute-start.25 = (bf16[128,2048]{1,0:T(8,128)(2,1)}, bf16[128,2048]{1,0:T(8,128)(2,1)}, u32[]{:S(2)}, u32[]{:S(2)}) collective-permute-start(bf16[128,2048]{1,0:T(8,128)(2,1)} %collective-permute-done.22.refs_9_), channel_id=1, source_target_pairs={{0,2},{2,0},{4,6},{6,4},{8,10},{10,8},{12,14},{14,12},{16,18},{18,... | collective-permute-start | bytes 1572872 | tf_op jit(solution)/shard_map/ppermute | solution.py:607
  368.8 67.0 %collective-permute-start.26 = (bf16[128,2048]{1,0:T(8,128)(2,1)}, bf16[128,2048]{1,0:T(8,128)(2,1)}, u32[]{:S(2)}, u32[]{:S(2)}) collective-permute-start(bf16[128,2048]{1,0:T(8,128)(2,1)} %collective-permute-done.23.refs_10_), channel_id=1, source_target_pairs={{0,2},{2,0},{4,6},{6,4},{8,10},{10,8},{12,14},{14,12},{16,18},{18,... | collective-permute-start | bytes 1572872 | tf_op jit(solution)/shard_map/ppermute | solution.py:607
  376.6 44.9 %collective-permute-start.28 = (bf16[64,2048]{1,0:T(8,128)(2,1)S(1)}, bf16[64,2048]{1,0:T(8,128)(2,1)}, u32[]{:S(2)}, u32[]{:S(2)}) collective-permute-start(bf16[64,2048]{1,0:T(8,128)(2,1)S(1)} %constant_dynamic-slice_fusion.4), channel_id=1, source_target_pairs={{0,8},{2,6},{8,16},{10,2},{16,24},{18,10},{24,28},{26,18},{28,20},... | collective-permute-start | bytes 786440 | tf_op jit(solution)/shard_map/ppermute | solution.py:604
  420.4 15.3 %collective-permute-start.27 = (bf16[128,2048]{1,0:T(8,128)(2,1)}, bf16[128,2048]{1,0:T(8,128)(2,1)}, u32[]{:S(2)}, u32[]{:S(2)}) collective-permute-start(bf16[128,2048]{1,0:T(8,128)(2,1)} %collective-permute-done.24.refs_11_), channel_id=1, source_target_pairs={{0,2},{2,0},{4,6},{6,4},{8,10},{10,8},{12,14},{14,12},{16,18},{18,... | collective-permute-start | bytes 1572872 | tf_op jit(solution)/shard_map/ppermute | solution.py:607
  421.4 14.3 %collective-permute-start.29 = (bf16[64,2048]{1,0:T(8,128)(2,1)}, bf16[64,2048]{1,0:T(8,128)(2,1)S(1)}, u32[]{:S(2)}, u32[]{:S(2)}) collective-permute-start(bf16[64,2048]{1,0:T(8,128)(2,1)} %collective-permute-done.28.refs_15_), channel_id=1, source_target_pairs={{0,2},{2,0},{4,6},{6,4},{8,10},{10,8},{12,14},{14,12},{16,18},{18,... | collective-permute-start | bytes 786440 | tf_op jit(solution)/shard_map/ppermute | solution.py:607
  471.8 11.2 %collective-permute-start.39 = (bf16[448,2048]{1,0:T(8,128)(2,1)}, bf16[448,2048]{1,0:T(8,128)(2,1)S(1)}, u32[]{:S(2)}, u32[]{:S(2)}) collective-permute-start(bf16[448,2048]{1,0:T(8,128)(2,1)} %get-tuple-element.69), channel_id=1, source_target_pairs={{0,2},{2,0},{4,6},{6,4},{8,10},{10,8},{12,14},{14,12},{16,18},{18,... | collective-permute-start | bytes 5505032 | tf_op jit(solution)/shard_map/ppermute | solution.py:607
  484.7 8.4 collective-permute-start.42
  493.3 8.4 collective-permute-start.43
  502.0 8.4 collective-permute-start.44
  522.0 10.0 %collective-permute-start.47 = (bf16[128,2048]{1,0:T(8,128)(2,1)S(1)}, bf16[128,2048]{1,0:T(8,128)(2,1)S(1)}, u32[]{:S(2)}, u32[]{:S(2)}) collective-permute-start(bf16[128,2048]{1,0:T(8,128)(2,1)S(1)} %maximum_select_fusion.5.refs_9_), channel_id=1, source_target_pairs={{0,8},{2,6},{8,16},{10,2},{16,24},{18,10},{24,28},{26,18},{28,20},... | collective-permute-start | bytes 1572872 | tf_op jit(solution)/shard_map/ppermute | solution.py:604
  530.8 30.2 %collective-permute-start.68 = (bf16[16,320,128]{2,1,0:T(8,128)(2,1)}, bf16[16,320,128]{2,1,0:T(8,128)(2,1)S(1)}, u32[]{:S(2)}, u32[]{:S(2)}) collective-permute-start(bf16[16,320,128]{2,1,0:T(8,128)(2,1)} %get-tuple-element.94), channel_id=1, source_target_pairs={{0,1},{1,0},{2,3},{3,2},{4,5},{5,4},{6,7},{7,6},{8,9},{9,8},{10,11... | collective-permute-start | bytes 3932168 | tf_op jit(solution)/shard_map/ppermute | solution.py:610
  532.1 8.3 collective-permute-start.48
  540.4 8.3 collective-permute-start.49
  540.4 102.6 %collective-permute-start.30 = (bf16[448,2048]{1,0:T(8,128)(2,1)}, bf16[448,2048]{1,0:T(8,128)(2,1)}, u32[]{:S(2)}, u32[]{:S(2)}) collective-permute-start(bf16[448,2048]{1,0:T(8,128)(2,1)} %get-tuple-element.63), channel_id=1, source_target_pairs={{0,2},{2,0},{4,6},{6,4},{8,10},{10,8},{12,14},{14,12},{16,18},{18,... | collective-permute-start | bytes 5505032 | tf_op jit(solution)/shard_map/ppermute | solution.py:607
  541.9 47.7 %collective-permute-start.50 = (bf16[128,2048]{1,0:T(8,128)(2,1)S(1)}, bf16[128,2048]{1,0:T(8,128)(2,1)}, u32[]{:S(2)}, u32[]{:S(2)}) collective-permute-start(bf16[128,2048]{1,0:T(8,128)(2,1)S(1)} %collective-permute-done.47.refs_10_), channel_id=1, source_target_pairs={{0,2},{2,0},{4,6},{6,4},{8,10},{10,8},{12,14},{14,12},{16,18},{18,... | collective-permute-start | bytes 1572872 | tf_op jit(solution)/shard_map/ppermute | solution.py:607
  542.0 48.9 %collective-permute-start.51 = (bf16[128,2048]{1,0:T(8,128)(2,1)S(1)}, bf16[128,2048]{1,0:T(8,128)(2,1)}, u32[]{:S(2)}, u32[]{:S(2)}) collective-permute-start(bf16[128,2048]{1,0:T(8,128)(2,1)S(1)} %collective-permute-done.48.refs_11_), channel_id=1, source_target_pairs={{0,2},{2,0},{4,6},{6,4},{8,10},{10,8},{12,14},{14,12},{16,18},{18,... | collective-permute-start | bytes 1572872 | tf_op jit(solution)/shard_map/ppermute | solution.py:607
  548.7 30.5 %collective-permute-start.53 = (bf16[64,2048]{1,0:T(8,128)(2,1)S(1)}, bf16[64,2048]{1,0:T(8,128)(2,1)S(1)}, u32[]{:S(2)}, u32[]{:S(2)}) collective-permute-start(bf16[64,2048]{1,0:T(8,128)(2,1)S(1)} %constant_dynamic-slice_fusion.1), channel_id=1, source_target_pairs={{0,8},{2,6},{8,16},{10,2},{16,24},{18,10},{24,28},{26,18},{28,20},... | collective-permute-start | bytes 786440 | tf_op jit(solution)/shard_map/ppermute | solution.py:604
  561.0 29.8 %collective-permute-start.52 = (bf16[128,2048]{1,0:T(8,128)(2,1)S(1)}, bf16[128,2048]{1,0:T(8,128)(2,1)}, u32[]{:S(2)}, u32[]{:S(2)}) collective-permute-start(bf16[128,2048]{1,0:T(8,128)(2,1)S(1)} %collective-permute-done.49.refs_12_), channel_id=1, source_target_pairs={{0,2},{2,0},{4,6},{6,4},{8,10},{10,8},{12,14},{14,12},{16,18},{18,... | collective-permute-start | bytes 1572872 | tf_op jit(solution)/shard_map/ppermute | solution.py:607
  565.0 70.2 %all-to-all-start.8 = ((bf16[16,320,128]{2,1,0:T(8,128)(2,1)}), bf16[16,320,128]{2,1,0:T(8,128)(2,1)S(1)}, u32[]{:S(2)}, u32[]{:S(2)}) async-start(bf16[16,320,128]{2,1,0:T(8,128)(2,1)} %add_convert_fusion.2), calls=%async_computation.8 | async-start | bytes 2621440 | tf_op jit(solution)/shard_map/all_to_all | solution.py:657
  579.2 11.6 %collective-permute-start.54 = (bf16[64,2048]{1,0:T(8,128)(2,1)S(1)}, bf16[64,2048]{1,0:T(8,128)(2,1)S(1)}, u32[]{:S(2)}, u32[]{:S(2)}) collective-permute-start(bf16[64,2048]{1,0:T(8,128)(2,1)S(1)} %collective-permute-done.53.refs_16_), channel_id=1, source_target_pairs={{0,2},{2,0},{4,6},{6,4},{8,10},{10,8},{12,14},{14,12},{16,18},{18,... | collective-permute-start | bytes 786440 | tf_op jit(solution)/shard_map/ppermute | solution.py:607
  589.6 41.8 %collective-permute-start.67 = (bf16[16,448,128]{2,1,0:T(8,128)(2,1)}, bf16[16,448,128]{2,1,0:T(8,128)(2,1)}, u32[]{:S(2)}, u32[]{:S(2)}) collective-permute-start(bf16[16,448,128]{2,1,0:T(8,128)(2,1)} %get-tuple-element.90), channel_id=1, source_target_pairs={{0,1},{1,0},{2,3},{3,2},{4,5},{5,4},{6,7},{7,6},{8,9},{9,8},{10,11... | collective-permute-start | bytes 5505032 | tf_op jit(solution)/shard_map/ppermute | solution.py:610
  616.0 27.1 %collective-permute-start.55 = (bf16[448,2048]{1,0:T(8,128)(2,1)}, bf16[448,2048]{1,0:T(8,128)(2,1)}, u32[]{:S(2)}, u32[]{:S(2)}) collective-permute-start(bf16[448,2048]{1,0:T(8,128)(2,1)} %get-tuple-element.73), channel_id=1, source_target_pairs={{0,2},{2,0},{4,6},{6,4},{8,10},{10,8},{12,14},{14,12},{16,18},{18,... | collective-permute-start | bytes 5505032 | tf_op jit(solution)/shard_map/ppermute | solution.py:607
  621.2 21.8 %collective-permute-start.32 = (bf16[64,2048]{1,0:T(8,128)(2,1)}, bf16[64,2048]{1,0:T(8,128)(2,1)}, u32[]{:S(2)}, u32[]{:S(2)}) collective-permute-start(bf16[64,2048]{1,0:T(8,128)(2,1)} %add_convert_fusion.18), channel_id=1, source_target_pairs={{0,8},{2,6},{8,16},{10,2},{16,24},{18,10},{24,28},{26,18},{28,20},... | collective-permute-start | bytes 786440 | tf_op jit(solution)/shard_map/ppermute | solution.py:604
  624.2 18.9 %collective-permute-start.57 = (bf16[64,2048]{1,0:T(8,128)(2,1)}, bf16[64,2048]{1,0:T(8,128)(2,1)}, u32[]{:S(2)}, u32[]{:S(2)}) collective-permute-start(bf16[64,2048]{1,0:T(8,128)(2,1)} %add_convert_fusion.16), channel_id=1, source_target_pairs={{0,8},{2,6},{8,16},{10,2},{16,24},{18,10},{24,28},{26,18},{28,20},... | collective-permute-start | bytes 786440 | tf_op jit(solution)/shard_map/ppermute | solution.py:604
  636.4 83.6 %all-to-all-start.7 = ((bf16[16,448,128]{2,1,0:T(8,128)(2,1)}), bf16[16,448,128]{2,1,0:T(8,128)(2,1)}, u32[]{:S(2)}, u32[]{:S(2)}) async-start(bf16[16,448,128]{2,1,0:T(8,128)(2,1)} %add_convert_fusion), calls=%async_computation.7 | async-start | bytes 3670016 | tf_op jit(solution)/shard_map/all_to_all | solution.py:657
  646.2 42.6 %collective-permute-start.58 = (bf16[128,2048]{1,0:T(8,128)(2,1)S(1)}, bf16[128,2048]{1,0:T(8,128)(2,1)S(1)}, u32[]{:S(2)}, u32[]{:S(2)}) collective-permute-start(bf16[128,2048]{1,0:T(8,128)(2,1)S(1)} %get-tuple-element.180), channel_id=1, source_target_pairs={{0,8},{2,6},{8,16},{10,2},{16,24},{18,10},{24,28},{26,18},{28,20},... | collective-permute-start | bytes 1572872 | tf_op jit(solution)/shard_map/ppermute | solution.py:604
  690.2 11.8 %collective-permute-start.59 = (bf16[128,2048]{1,0:T(8,128)(2,1)S(1)}, bf16[128,2048]{1,0:T(8,128)(2,1)S(1)}, u32[]{:S(2)}, u32[]{:S(2)}) collective-permute-start(bf16[128,2048]{1,0:T(8,128)(2,1)S(1)} %add_convert_fusion.5), channel_id=1, source_target_pairs={{0,8},{2,6},{8,16},{10,2},{16,24},{18,10},{24,28},{26,18},{28,20},... | collective-permute-start | bytes 1572872 | tf_op jit(solution)/shard_map/ppermute | solution.py:604
  700.8 30.2 %collective-permute-start.66 = (bf16[16,320,128]{2,1,0:T(8,128)(2,1)}, bf16[16,320,128]{2,1,0:T(8,128)(2,1)}, u32[]{:S(2)}, u32[]{:S(2)}) collective-permute-start(bf16[16,320,128]{2,1,0:T(8,128)(2,1)} %get-tuple-element.86), channel_id=1, source_target_pairs={{0,1},{1,0},{2,3},{3,2},{4,5},{5,4},{6,7},{7,6},{8,9},{9,8},{10,11... | collective-permute-start | bytes 3932168 | tf_op jit(solution)/shard_map/ppermute | solution.py:610
  703.5 8.5 collective-permute-start.60
  720.0 13.8 %all-to-all-start.4 = ((f32[16,6,128]{2,1,0:T(8,128)}), f32[16,6,128]{2,1,0:T(8,128)S(1)}, u32[]{:S(2)}, u32[]{:S(2)}) async-start(f32[16,6,128]{2,1,0:T(8,128)} %copy.70), calls=%async_computation.4 | async-start | bytes 131072 | tf_op jit(solution)/shard_map/all_to_all | solution.py:857
  733.7 58.2 %all-to-all-start.6 = ((bf16[16,320,128]{2,1,0:T(8,128)(2,1)}), bf16[16,320,128]{2,1,0:T(8,128)(2,1)S(1)}, u32[]{:S(2)}, u32[]{:S(2)}) async-start(bf16[16,320,128]{2,1,0:T(8,128)(2,1)} %add_convert_fusion.3), calls=%async_computation.6 | async-start | bytes 2621440 | tf_op jit(solution)/shard_map/all_to_all | solution.py:657
  748.8 41.4 %collective-permute-start.65 = (bf16[16,448,128]{2,1,0:T(8,128)(2,1)}, bf16[16,448,128]{2,1,0:T(8,128)(2,1)S(1)}, u32[]{:S(2)}, u32[]{:S(2)}) collective-permute-start(bf16[16,448,128]{2,1,0:T(8,128)(2,1)} %get-tuple-element.82), channel_id=1, source_target_pairs={{0,1},{1,0},{2,3},{3,2},{4,5},{5,4},{6,7},{7,6},{8,9},{9,8},{10,11... | collective-permute-start | bytes 5505032 | tf_op jit(solution)/shard_map/ppermute | solution.py:610
  750.0 23.6 %collective-permute-start.33 = (bf16[128,2048]{1,0:T(8,128)(2,1)}, bf16[128,2048]{1,0:T(8,128)(2,1)S(1)}, u32[]{:S(2)}, u32[]{:S(2)}) collective-permute-start(bf16[128,2048]{1,0:T(8,128)(2,1)} %get-tuple-element.181), channel_id=1, source_target_pairs={{0,8},{2,6},{8,16},{10,2},{16,24},{18,10},{24,28},{26,18},{28,20},... | collective-permute-start | bytes 1572872 | tf_op jit(solution)/shard_map/ppermute | solution.py:604
  775.6 24.3 %collective-permute-start.34 = (bf16[128,2048]{1,0:T(8,128)(2,1)}, bf16[128,2048]{1,0:T(8,128)(2,1)}, u32[]{:S(2)}, u32[]{:S(2)}) collective-permute-start(bf16[128,2048]{1,0:T(8,128)(2,1)} %add_convert_fusion.11), channel_id=1, source_target_pairs={{0,8},{2,6},{8,16},{10,2},{16,24},{18,10},{24,28},{26,18},{28,20},... | collective-permute-start | bytes 1572872 | tf_op jit(solution)/shard_map/ppermute | solution.py:604
  793.0 88.3 %all-to-all-start.5 = ((bf16[16,448,128]{2,1,0:T(8,128)(2,1)}), bf16[16,448,128]{2,1,0:T(8,128)(2,1)}, u32[]{:S(2)}, u32[]{:S(2)}) async-start(bf16[16,448,128]{2,1,0:T(8,128)(2,1)} %add_convert_fusion.1), calls=%async_computation.5 | async-start | bytes 3670016 | tf_op jit(solution)/shard_map/all_to_all | solution.py:657
  801.4 44.3 %collective-permute-start.35 = (bf16[128,2048]{1,0:T(8,128)(2,1)S(1)}, bf16[128,2048]{1,0:T(8,128)(2,1)S(1)}, u32[]{:S(2)}, u32[]{:S(2)}) collective-permute-start(bf16[128,2048]{1,0:T(8,128)(2,1)S(1)} %add_convert_fusion.10), channel_id=1, source_target_pairs={{0,8},{2,6},{8,16},{10,2},{16,24},{18,10},{24,28},{26,18},{28,20},... | collective-permute-start | bytes 1572872 | tf_op jit(solution)/shard_map/ppermute | solution.py:604
  855.9 13.2 %collective-permute-start.38 = (bf16[128,2048]{1,0:T(8,128)(2,1)S(1)}, bf16[128,2048]{1,0:T(8,128)(2,1)S(1)}, u32[]{:S(2)}, u32[]{:S(2)}) collective-permute-start(bf16[128,2048]{1,0:T(8,128)(2,1)S(1)} %maximum_select_fusion.3), channel_id=1, source_target_pairs={{0,1},{1,0},{2,3},{3,2},{4,5},{5,4},{6,7},{7,6},{8,9},{9,8},{10,11... | collective-permute-start | bytes 1572872 | tf_op jit(solution)/shard_map/ppermute | solution.py:610
  858.7 21.6 %collective-permute-start.63 = (bf16[128,2048]{1,0:T(8,128)(2,1)S(1)}, bf16[128,2048]{1,0:T(8,128)(2,1)S(1)}, u32[]{:S(2)}, u32[]{:S(2)}) collective-permute-start(bf16[128,2048]{1,0:T(8,128)(2,1)S(1)} %maximum_select_fusion.7), channel_id=1, source_target_pairs={{0,1},{1,0},{2,3},{3,2},{4,5},{5,4},{6,7},{7,6},{8,9},{9,8},{10,11... | collective-permute-start | bytes 1572872 | tf_op jit(solution)/shard_map/ppermute | solution.py:610
  (63 other events, 831.4 us)

commit v3 on v2

--- a/solution.py
+++ b/solution.py
@@ -72,6 +72,10 @@
 ANY_SPEC = pl.BlockSpec(memory_space=pl.ANY)
 SMEM_SPEC = pl.BlockSpec(memory_space=pltpu.SMEM)
 WIDE = 2 * HEAD_DIM
+
+
+def after(x, *others):
+    return lax.optimization_barrier((x, *others))[0]
 
 
 def left_lanes(x):
@@ -398,7 +402,7 @@
         out_shape=kept + parts,
         scratch_shapes=[pltpu.VMEM((total, width), bf16)] * buffers + [pltpu.SemaphoreType.DMA((18,))],
         cost_estimate=pl.CostEstimate(
-            flops=2 * total * width * (slim + wide) * passes,
+            flops=6 * total * width * (slim + wide) * passes,
             bytes_accessed=20_000_000 * passes,
             transcendentals=total * slim,
         ),
@@ -406,8 +410,16 @@
     )(core, *weights, *tables, allowed, *extra, *chunks)
 
 
-def gradient_slabs(own_rows, other_rows, with_sums, left_ref, right_ref, own_ref, other_ref, *rest):
+def gradient_slabs(own_rows, other_rows, with_sums, pieces_in, core_ref, left_ref, *rest):
+    right_refs, (own_ref, other_ref, *rest) = rest[:pieces_in], rest[pieces_in:]
     turned_ref = rest[-1]
+    if pieces_in == 1:
+        right = right_refs[0][...]
+    else:
+        a, b = right_refs[-2][...], right_refs[-1][...]
+        first = jnp.full(a.shape, core_ref[0]) == 0
+        halves = [jnp.where(first, a, b), jnp.where(first, b, a)]
+        right = jnp.concatenate([ref[...] for ref in right_refs[:-2]] + halves, axis=0)
 
     @pl.when(pl.program_id(0) == 0)
     def _():
@@ -419,7 +431,7 @@
                 rest[0][:, lanes] = jnp.sum(left, axis=0, keepdims=True)
             turned_ref[lanes, :] = left.T.astype(bf16)
 
-    product = dot(turned_ref[...], right_ref[...]).astype(bf16)
+    product = dot(turned_ref[...], right).astype(bf16)
     for ref, pieces in ((own_ref, own_rows), (other_ref, other_rows)):
         place = 0
         for first, last in pieces:
@@ -428,9 +440,9 @@
             place += last - first
 
 
-def call_gradients(left, right, own_rows, other_rows, with_sums, name):
+def call_gradients(core, left, right, own_rows, other_rows, with_sums, name):
     total, height = left.shape
-    width = right.shape[1]
+    width = right[0].shape[1]
     rows = height // 2
     slab = pl.BlockSpec((2, rows, 128), lambda i: (i, 0, 0))
     shape = jax.ShapeDtypeStruct((width // 128, rows, 128), bf16)
@@ -439,17 +451,18 @@
         out_specs.append(pl.BlockSpec((1, height), lambda i: (0, 0)))
         out_shape.append(jax.ShapeDtypeStruct((1, height), f32))
     return pl.pallas_call(
-        partial(gradient_slabs, own_rows, other_rows, with_sums),
+        partial(gradient_slabs, own_rows, other_rows, with_sums, len(right)),
         grid=(width // 256,),
-        in_specs=[pl.BlockSpec((total, height), lambda i: (0, 0)), pl.BlockSpec((total, 256), lambda i: (0, i))],
+        in_specs=[SMEM_SPEC, pl.BlockSpec((total, height), lambda i: (0, 0))]
+        + [pl.BlockSpec((x.shape[0], 256), lambda i: (0, i)) for x in right],
         out_specs=out_specs,
         out_shape=out_shape,
         scratch_shapes=[pltpu.VMEM((height, total), bf16)],
         cost_estimate=pl.CostEstimate(
-            flops=2 * total * height * width, bytes_accessed=2 * (total * (width + height) + 2 * height * width), transcendentals=0
+            flops=4 * total * height * width, bytes_accessed=2 * (total * (width + height) + 2 * height * width), transcendentals=0
         ),
         name=name,
-    )(left, right)
+    )(core, left, *right)
 
 
 def spread_gradients(up_ref, down_ref, *rest):
@@ -534,8 +547,8 @@
 
 
 def call_end(body, core, ring, extra, shapes, name):
-    keep, took, moving, got = ring
-    half, width = got.shape
+    keep, took, moving, got, n_sum = ring
+    _, half, width = got.shape
 
     def rows_of(array):
         n = array.shape[0] // half - 1
@@ -544,10 +557,13 @@
     def whole_of(array):
         return pl.BlockSpec(array.shape, lambda i: (0,) * len(array.shape))
 
+    def one_of(array):
+        return pl.BlockSpec((None,) + array.shape[1:], lambda i: (n_sum, 0, 0))
+
     return pl.pallas_call(
         body,
         grid=(1,),
-        in_specs=[SMEM_SPEC, rows_of(keep), rows_of(took)] + [whole_of(x) for x in (moving, got, *extra)],
+        in_specs=[SMEM_SPEC, rows_of(keep), rows_of(took), one_of(moving), one_of(got)] + [whole_of(x) for x in extra],
         out_specs=[whole_of(x) for x in shapes],
         out_shape=shapes,
         name=name,
@@ -640,18 +656,21 @@
     rows = lax.broadcasted_iota(jnp.int32, (block, 1), 0)
     mine_rows = (rows < half) == is_first
 
-    def ring_sum(give_far, give, keep):
-        took_far = across(give_far)
-        took = across(give)
-        far = keep[side * block : side * block + half].astype(f32) + took_far.astype(f32)
-        moving = along(far.astype(bf16))
-        moving = jnp.where(mine_rows, jnp.concatenate([moving, moving], 0), 0).astype(f32)
+    def ring_sum(*sets):
+        took_far = [across(give_far) for give_far, _, _ in sets]
+        took = [across(give) for _, give, _ in sets]
+        keep = [x for _, _, x in sets]
+        far = [k[side * block : side * block + half].astype(f32) + t.astype(f32) for k, t in zip(keep, took_far)]
+        moving = along(jnp.stack(far).astype(bf16))
+        moving = jnp.where(mine_rows, jnp.concatenate([moving, moving], 1), 0).astype(f32)
         for step in reversed(range(side)):
             here = slice(step * block, (step + 1) * block)
-            moving = along((moving + keep[here].astype(f32) + took[here].astype(f32)).astype(bf16))
+            added = [k[here].astype(f32) + t[here].astype(f32) for k, t in zip(keep, took)]
+            moving = along((moving + jnp.stack(added)).astype(bf16))
             if step:
                 moving = moving.astype(f32)
-        return keep, took, moving, across(my_half(moving, off))
+        got = across(my_half(moving, off, 1))
+        return [(k, t, moving, got, n) for n, (k, t) in enumerate(zip(keep, took))]
 
     def spread(x):
         return lax.all_to_all(x, "dp", 0, 0, axis_index_groups=inner, tiled=True)
@@ -668,18 +687,22 @@
     slab_rows = 3 * HEAD_DIM + hidden
     small_all = None
     weights = []
+    arrivals = []
     if groups == 1:
         qkv_turned = qkv_weight.transpose(0, 2, 1, 3)
+        previous = ()
         for layer in range(LAYERS):
             extra = None
             if layer == 0:
                 extra = jnp.concatenate([small, jnp.zeros_like(small)]).reshape(-1, 128)
-            up = spread(call_pack_up(qkv_turned, fc1_weight, layer, extra))
+            up = spread(after(call_pack_up(qkv_turned, fc1_weight, layer, extra), *previous))
             if layer == 0:
                 small_all = up[:, slab_rows:].reshape(GROUP, -1)[:, : small.shape[0]]
             up_other = over(up)
-            down = spread(call_pack_down(out_weight, fc2_weight, layer))
+            down = spread(after(call_pack_down(out_weight, fc2_weight, layer), up))
             down_other = over(down)
+            previous = (down,)
+            arrivals.append((up, down))
             weights.append((call_join_up(up, up_other), call_join_down(down, down_other)))
     else:
         small_all = lax.all_gather(small, "dp", axis=0, tiled=False)
@@ -710,6 +733,7 @@
             )
             down = lax.all_gather(spread(down), "dp", axis=0, axis_index_groups=outer, tiled=True)
             down = down.transpose(1, 0, 2).reshape(-1, width // 128, 128).transpose(1, 0, 2)
+            arrivals.append((up, down))
             weights.append((call_join_up(up, over(up)), call_join_down(down, over(down))))
     if groups == 1:
         biases = jnp.concatenate([qkv_bias.reshape(LAYERS, 3 * HEAD_DIM), fc1_bias], axis=1)
@@ -734,7 +758,7 @@
         axis=1,
     )
     vectors = small_all[:, : 6 * piece].reshape(n_dp, 3, LAYERS, piece).transpose(1, 2, 0, 3).reshape(3, LAYERS, 1, width).astype(f32)
-    gains, shifts, after = vectors[0], vectors[1], vectors[2]
+    gains, shifts, added_bias = vectors[0], vectors[1], vectors[2]
 
     turned = jnp.where(is_first, 1, -1)
     place = jnp.sum(jnp.where(jnp.asarray(ring) == chip, jnp.arange(chips), 0))
@@ -782,24 +806,25 @@
     next_state, normed_own = call_end(
         partial(forward_end, False),
         core_word,
-        ring_sum(*parts),
-        [state, after[0], gains[1], shifts[1]],
+        ring_sum((after(parts[0], arrivals[1][0]), parts[1], parts[2]))[0],
+        [state, added_bias[0], gains[1], shifts[1]],
         [jax.ShapeDtypeStruct(rows_shape, f32), jax.ShapeDtypeStruct(rows_shape, bf16)],
         "forward_end",
     )
+    normed_own = after(normed_own, arrivals[1][1])
     normed_chunks = gather_rows(in_order(normed_own, across(normed_own)))
 
     def handed_back(own_rows):
         filled = in_order(own_rows, across(own_rows))
         return jnp.where(tensor == core, filled, over(filled))
 
-    def summed(own, other):
+    def summed(own, other, *earlier):
         total = own.astype(f32) + over(other).astype(f32)
         if groups > 1:
             total = total.transpose(1, 0, 2).reshape(total.shape[1], width)
             total = lax.psum_scatter(total, "dp", scatter_dimension=1, axis_index_groups=outer, tiled=True)
             total = total.reshape(total.shape[0], GROUP, piece).transpose(1, 0, 2)
-        return spread(total.astype(bf16))
+        return spread(after(total.astype(bf16), *earlier))
 
     down_own = [(0, HEAD_DIM), (WIDE, WIDE + hidden)]
     down_other = [(HEAD_DIM, WIDE), (WIDE + hidden, WIDE + 2 * hidden)]
@@ -807,18 +832,16 @@
     up_other = [(p * WIDE + HEAD_DIM, (p + 1) * WIDE) for p in range(3)] + [(3 * WIDE + hidden, 3 * WIDE + 2 * hidden)]
 
     def down_gradients(wide_rows, grad_rows):
-        own, other = call_gradients(wide_rows, grad_rows, down_own, down_other, False, "down_gradients")
-        return summed(own, other)
+        return call_gradients(core_word, wide_rows, grad_rows, down_own, down_other, False, "down_gradients")
 
     def up_gradients(slim_rows, normed_rows):
-        own, other, sums = call_gradients(slim_rows, normed_rows, up_own, up_other, True, "up_gradients")
-        return summed(own, other), sums
-
-    def backward_finish(parts, state, grad_state, layer):
+        return call_gradients(core_word, slim_rows, [normed_rows], up_own, up_other, True, "up_gradients")
+
+    def backward_finish(ring_end, state, grad_state, layer):
         return call_end(
             backward_end,
             core_word,
-            ring_sum(*parts),
+            ring_end,
             [state, grad_state, gains[layer]],
             [
                 jax.ShapeDtypeStruct(rows_shape, f32),
@@ -831,27 +854,35 @@
     normed_last, grad_rows, wide_last, slim, *parts = call_pass(
         "middle", core_word, weights[1], tables, allowed, [bias_rows[1:2]], normed_chunks + inputs
     )
-    grad_state, grad_low, sums_last = backward_finish(parts[3:], next_state, grad_state, 1)
+    out_parts = parts[:3]
+    down_pair = down_gradients(wide_last, [grad_rows])
+    *up_pair, bias_last = up_gradients(slim, normed_last)
+    grad_state, grad_low, sums_last = backward_finish(
+        ring_sum(parts[3:])[0], after(next_state, down_pair[0], up_pair[0]), grad_state, 1
+    )
     grad_chunks = gather_rows(in_order(grad_low, across(grad_low)))
-    down_last = down_gradients(wide_last, grad_rows)
-    up_last, bias_last = up_gradients(slim, normed_last)
+    down_last = summed(*down_pair)
+    up_last = summed(*up_pair, down_last)
+
+    down_pair = down_gradients(wide, grad_chunks)
+    grad_rows, slim, *parts = call_pass(
+        "last", core_word, weights[0], tables, allowed, [heads, after(hidden_pre, down_pair[0], down_last)], grad_chunks
+    )
+    down_first = summed(*down_pair, up_last)
+    *up_pair, bias_first = up_gradients(slim, normed)
+    up_first = summed(*up_pair, down_first)
+    grad_end, out_end = ring_sum((after(parts[0], up_pair[0]), parts[1], parts[2]), out_parts)
+    _, grad_low, sums_first = backward_finish(grad_end, state, grad_state, 0)
+    grad_hidden = handed_back(grad_low).astype(f32)
     (hidden_out,) = call_end(
         partial(forward_end, True),
         core_word,
-        ring_sum(*parts[:3]),
-        [next_state, after[1]],
+        out_end,
+        [next_state, added_bias[1]],
         [jax.ShapeDtypeStruct(rows_shape, bf16)],
         "forward_out",
     )
     hidden_out = handed_back(hidden_out)
-
-    grad_rows, slim, *parts = call_pass(
-        "last", core_word, weights[0], tables, allowed, [heads, hidden_pre], grad_chunks
-    )
-    down_first = down_gradients(wide, grad_rows)
-    up_first, bias_first = up_gradients(slim, normed)
-    _, grad_low, sums_first = backward_finish(parts, state, grad_state, 0)
-    grad_hidden = handed_back(grad_low).astype(f32)
 
     vectors = jnp.stack([sums_first, sums_last]).reshape(LAYERS * 3, n_dp, piece).transpose(1, 0, 2)
     vectors = jnp.sum(lax.all_to_all(vectors, "dp", 0, 0, tiled=True), axis=0)

time: 896 us -> 789 us (0.88)
  waiting for transfers between devices: 487 us -> 388 us
  starting transfers between devices: 124 us -> 115 us
    ppermute x13, waiting for transfers between devices: 134 us -> 65.3 us  [over(): return lax.ppermute(x, 'tensor', [(0, 1), (1, 0)])]
    ppermute x28 -> x24, waiting for transfers between devices: 318 us -> 300 us  [along(): return lax.ppermute(x, 'dp', ring_pairs)]
    all_to_all x8, waiting for transfers between devices: 19.9 us -> 10.1 us  [spread(): return lax.all_to_all(x, 'dp', 0, 0, axis_index_groups=inner, tiled=True)]
    all_to_all x8, starting transfers between devices: 55.2 us -> 45.6 us  [spread(): return lax.all_to_all(x, 'dp', 0, 0, axis_index_groups=inner, tiled=True)]
    convert_element_type x19 -> x15, other arithmetic: 32.1 us -> 23.9 us  [the longest x9 12.1 us: ring_sum(): moving = along((moving + jnp.stack(added)).astype(bf16))]
    ppermute x28 -> x24, starting transfers between devices: 23.7 us -> 27.6 us  [along(): return lax.ppermute(x, 'dp', ring_pairs)]
    ppermute x29 -> x28, starting transfers between devices: 27.5 us -> 25 us  [across(): return lax.ppermute(x, 'dp', core_pairs)]
  transfers between devices with their start and end apart: 79 -> 74, of which waited for: 37 -> 32; matrix products, arithmetic and copies ran while one was open for 7% -> 7% of each run, Pallas kernels for 14% -> 20%
where the time goes in v3:
time: 789 us; the launch traced here: 776 us
  waiting for transfers between devices  388 us (49%)
  Pallas kernels  201 us (25%)
  starting transfers between devices  115 us (15%)
  other arithmetic  47.9 us (6%)
  local copies, waits for them, and re-layouts  22.7 us (3%)
    ppermute x24, waiting for transfers between devices, along(): return lax.ppermute(x, 'dp', ring_pairs)  300 us
    pallas_call x3, Pallas kernels, call_pass(): pl.pallas_call(partial(layer_pass, mode), in_specs=[SMEM_SPEC] + [VMEM_SP...  89.3 us
    ppermute x13, waiting for transfers between devices, over(): return lax.ppermute(x, 'tensor', [(0, 1), (1, 0)])  65.3 us
    all_to_all x8, starting transfers between devices, spread(): return lax.all_to_all(x, 'dp', 0, 0, axis_index_groups=inner, tiled=True)  45.6 us
    pallas_call x4, Pallas kernels, call_gradients(): pl.pallas_call(partial(gradient_slabs, own_rows, other_rows, with_sums, l...  37.9 us
    ppermute x24, starting transfers between devices, along(): return lax.ppermute(x, 'dp', ring_pairs)  27.6 us
    ppermute x28, starting transfers between devices, across(): return lax.ppermute(x, 'dp', core_pairs)  25 us
  transfers between devices with their start and end apart: 74, of which 32 were waited for; matrix products, arithmetic and copies ran while one was open for 7% of the time, Pallas kernels for 20%

profile of v3, /device:TPU:13, one launch (start us, length us, event | category | flops | bytes accessed | tf_op | source)
XLA Modules:
  0.0 776.5 jit_solution(6384616240446353705)
XLA Ops:
  0.7 2.3 pad_maximum_fusion
  5.4 5.9 pack_up.3
  11.4 6.1 all-to-all-start
  23.3 47.0 %collective-permute-done.6.refs_11_.refs_18_ = bf16[2,128,2048]{2,1,0:T(8,128)(2,1)} collective-permute-done((bf16[2,128,2048]{2,1,0:T(8,128)(2,1)S(1)}, bf16[2,128,2048]{2,1,0:T(8,128)(2,1)}, u32[]{:S(2)}, u32[]{:S(2)}) %collective-permute-start.6) | collective-permute-done | bytes 1048608 | tf_op jit(solution)/shard_map/ppermute | solution.py:620
  72.3 5.3 pack_down.2
  77.6 5.7 all-to-all-start.1
  88.3 35.5 %collective-permute-done.8.refs_13_.refs_20_ = bf16[2,128,2048]{2,1,0:T(8,128)(2,1)} collective-permute-done((bf16[2,128,2048]{2,1,0:T(8,128)(2,1)}, bf16[2,128,2048]{2,1,0:T(8,128)(2,1)}, u32[]{:S(2)}, u32[]{:S(2)}) %collective-permute-start.8) | collective-permute-done | bytes 1048608 | tf_op jit(solution)/shard_map/ppermute | solution.py:620
  127.1 5.9 pack_up.2
  138.6 5.4 all-to-all-start.2
  152.4 7.0 join_up.3.refs_1_
  159.4 7.1 collective-permute-done.4.other_ref
  166.5 6.2 join_down.3.refs_2_
  173.5 29.2 %pass_first.1 = (bf16[1024,2048]{1,0:T(8,128)(2,1)}, bf16[1024,384]{1,0:T(8,128)(2,1)}, f32[1024,512]{1,0:T(8,128)}, bf16[1024,640]{1,0:T(8,128)(2,1)}, bf16[64,...) custom-call(s32[1]{0:T(128)} %bitcast.refs_0_.core_ref, bf16[2048,896]{1,0:T(8,128)(2,1)} %join_up.3.refs_1_, ...), custom_call_target="tpu_custom_call" | custom-call | flops 19327352832 | bytes 20000000 | tf_op jit(solution)/shard_map/pass_first/pallas_call | solution.py:398
  204.3 3.9 collective-permute-done.15
  211.0 3.8 collective-permute-done.16
  218.7 5.3 pack_down.3
  224.0 6.5 all-to-all-start.3
  233.2 31.8 %collective-permute-done.18 = bf16[1,128,2048]{2,1,0:T(8,128)(2,1)S(1)} collective-permute-done((bf16[1,128,2048]{2,1,0:T(8,128)(2,1)S(1)}, bf16[1,128,2048]{2,1,0:T(8,128)(2,1)S(1)}, u32[]{:S(2)}, u32[]{:S(2)}) %collective-permute-start.18) | collective-permute-done | bytes 524320 | tf_op jit(solution)/shard_map/ppermute | solution.py:620
  269.1 6.6 collective-permute-done.19.moving_ref
  275.8 3.2 collective-permute-start.20
  281.6 2.5 forward_end.1
  287.1 8.4 %collective-permute-done.22.refs_9_ = bf16[128,2048]{1,0:T(8,128)(2,1)} collective-permute-done((bf16[128,2048]{1,0:T(8,128)(2,1)S(1)}, bf16[128,2048]{1,0:T(8,128)(2,1)}, u32[]{:S(2)}, u32[]{:S(2)}) %collective-permute-start.22) | collective-permute-done | bytes 524320 | tf_op jit(solution)/shard_map/ppermute | solution.py:620
  296.8 7.4 collective-permute-done.23.refs_10_
  306.2 6.7 collective-permute-done.24.refs_11_
  313.9 11.8 %collective-permute-done.other_ref = bf16[16,448,128]{2,1,0:T(8,128)(2,1)S(1)} collective-permute-done((bf16[16,448,128]{2,1,0:T(8,128)(2,1)}, bf16[16,448,128]{2,1,0:T(8,128)(2,1)S(1)}, u32[]{:S(2)}, u32[]{:S(2)}) %collective-permute-start) | collective-permute-done | bytes 1835040 | tf_op jit(solution)/shard_map/ppermute | solution.py:626
  327.9 6.9 join_up.2.refs_1_
  334.8 19.1 %collective-permute-done.1.other_ref = bf16[16,320,128]{2,1,0:T(8,128)(2,1)} collective-permute-done((bf16[16,320,128]{2,1,0:T(8,128)(2,1)S(1)}, bf16[16,320,128]{2,1,0:T(8,128)(2,1)}, u32[]{:S(2)}, u32[]{:S(2)}) %collective-permute-start.1) | collective-permute-done | bytes 1310752 | tf_op jit(solution)/shard_map/ppermute | solution.py:626
  353.8 6.1 join_down.2.refs_2_
  360.7 35.4 %pass_middle.1 = (bf16[1024,2048]{1,0:T(8,128)(2,1)}, bf16[1024,2048]{1,0:T(8,128)(2,1)}, bf16[1024,640]{1,0:T(8,128)(2,1)}, bf16[1024,896]{1,0:T(8,128)(2,1)}, ...) custom-call(s32[1]{0:T(128)} %bitcast.refs_0_.core_ref, ...), custom_call_target="tpu_custom_call" | custom-call | flops 38654705664 | bytes 40000000 | tf_op jit(solution)/shard_map/pass_middle/pallas_call | solution.py:398
  397.5 3.9 collective-permute-done.32
  402.5 5.5 collective-permute-done.33
  409.7 8.3 %collective-permute-done.34 = bf16[1,128,2048]{2,1,0:T(8,128)(2,1)S(1)} collective-permute-done((bf16[1,128,2048]{2,1,0:T(8,128)(2,1)S(1)}, bf16[1,128,2048]{2,1,0:T(8,128)(2,1)S(1)}, u32[]{:S(2)}, u32[]{:S(2)}) %collective-permute-start.34) | collective-permute-done | bytes 524320 | tf_op jit(solution)/shard_map/ppermute | solution.py:620
  418.3 8.3 %collective-permute-done.35 = bf16[1,128,2048]{2,1,0:T(8,128)(2,1)S(1)} collective-permute-done((bf16[1,128,2048]{2,1,0:T(8,128)(2,1)S(1)}, bf16[1,128,2048]{2,1,0:T(8,128)(2,1)S(1)}, u32[]{:S(2)}, u32[]{:S(2)}) %collective-permute-start.35) | collective-permute-done | bytes 524320 | tf_op jit(solution)/shard_map/ppermute | solution.py:620
  427.9 8.8 %down_gradients.2 = (bf16[16,320,128]{2,1,0:T(8,128)(2,1)}, bf16[16,320,128]{2,1,0:T(8,128)(2,1)}) custom-call(s32[1]{0:T(128)} %bitcast.refs_0_.core_ref, bf16[1024,640]{1,0:T(8,128)(2,1)} %get-tuple-element.86.left_ref, bf16[1024,2048]{1,0:T(8,128)(2,1)} %get-tuple-element.87.rest_0_), custom_call_target="tpu_custom_call" | custom-call | flops 5368709120 | bytes 10747904 | tf_op jit(solution)/shard_map/down_gradients/pallas_call | solution.py:453
  437.9 3.3 collective-permute-start.37
  441.2 10.0 %up_gradients.2 = (bf16[16,448,128]{2,1,0:T(8,128)(2,1)}, bf16[16,448,128]{2,1,0:T(8,128)(2,1)}, f32[1,896]{1,0:T(1,128)}) custom-call(s32[1]{0:T(128)} %bitcast.refs_0_.core_ref, bf16[1024,896]{1,0:T(8,128)(2,1)} %get-tuple-element.89.left_ref, bf16[1024,2048]{1,0:T(8,128)(2,1)} %get-tuple-element.90.rest_0_), custom_call_target="tpu_custom_call" | custom-call | flops 7516192768 | bytes 13369344 | tf_op jit(solution)/shard_map/up_gradients/pallas_call | solution.py:453
  452.0 3.2 backward_end.2
  459.8 6.7 collective-permute-done.39.rest_1_.refs_10_
  469.6 6.1 all-to-all-start.4
  477.0 33.4 %collective-permute-done.41.rest_3_.refs_12_ = bf16[128,2048]{1,0:T(8,128)(2,1)S(1)} collective-permute-done((bf16[128,2048]{1,0:T(8,128)(2,1)}, bf16[128,2048]{1,0:T(8,128)(2,1)S(1)}, u32[]{:S(2)}, u32[]{:S(2)}) %collective-permute-start.41) | collective-permute-done | bytes 524320 | tf_op jit(solution)/shard_map/ppermute | solution.py:620
  513.4 2.6 collective-permute-done.45.rest_7_.refs_16_
  516.0 3.1 collective-permute-start.46
  521.9 8.9 %down_gradients.3 = (bf16[16,320,128]{2,1,0:T(8,128)(2,1)}, bf16[16,320,128]{2,1,0:T(8,128)(2,1)}) custom-call(s32[1]{0:T(128)} %bitcast.refs_0_.core_ref, bf16[1024,640]{1,0:T(8,128)(2,1)} %get-tuple-element.81.left_ref, bf16[128,2048]{1,0:T(8,128)(2,1)} %copy-done.25, bf16[128,2048]{1,0:T(8,128)(2,1)} %collective-permute-done.39.rest_1_.refs_10_, ...), custom_call_target="tpu_custom_call" | custom-call | flops 5368709120 | bytes 10747904 | tf_op jit(solution)/shard_map/down_gradients/pallas_call | solution.py:453
  530.8 24.7 %pass_last.1 = (bf16[1024,2048]{1,0:T(8,128)(2,1)}, bf16[1024,896]{1,0:T(8,128)(2,1)}, bf16[64,2048]{1,0:T(8,128)(2,1)}, bf16[448,2048]{1,0:T(8,128)(2,1)}, bf16[512,2048]{1,0:T(8,128)(2,1)}) custom-call(s32[1]{0:T(128)} %bitcast.refs_0_.core_ref, bf16[2048,896]{1,0:T(8,128)(2,1)} %join_up.3.refs_1_, bf16[640,2048]{1,0:T(8,128)(2,1)} %join_down.3.refs_2_, ...), custom_call_target="tpu_custom_call" | custom-call | flops 19327352832 | bytes 20000000 | tf_op jit(solution)/shard_map/pass_last/pallas_call | solution.py:398
  556.0 3.2 add_bitcast_fusion.4
  559.3 10.2 %up_gradients.3 = (bf16[16,448,128]{2,1,0:T(8,128)(2,1)}, bf16[16,448,128]{2,1,0:T(8,128)(2,1)}, f32[1,896]{1,0:T(1,128)}) custom-call(s32[1]{0:T(128)} %bitcast.refs_0_.core_ref, bf16[1024,896]{1,0:T(8,128)(2,1)} %get-tuple-element.99.left_ref, bf16[1024,2048]{1,0:T(8,128)(2,1)} %get-tuple-element.100.rest_0_), custom_call_target="tpu_custom_call" | custom-call | flops 7516192768 | bytes 13369344 | tf_op jit(solution)/shard_map/up_gradients/pallas_call | solution.py:453
  569.6 3.2 add_convert_fusion
  572.8 4.4 all-to-all-start.6
  579.7 2.9 add_bitcast_fusion.5
  582.6 40.3 %collective-permute-done.50 = bf16[2,64,2048]{2,1,0:T(8,128)(2,1)S(1)} collective-permute-done((bf16[2,64,2048]{2,1,0:T(8,128)(2,1)S(1)}, bf16[2,64,2048]{2,1,0:T(8,128)(2,1)S(1)}, u32[]{:S(2)}, u32[]{:S(2)}) %collective-permute-start.50) | collective-permute-done | bytes 524320 | tf_op jit(solution)/shard_map/ppermute | solution.py:620
  626.4 10.9 %collective-permute-done.52 = bf16[2,128,2048]{2,1,0:T(8,128)(2,1)S(1)} collective-permute-done((bf16[2,128,2048]{2,1,0:T(8,128)(2,1)S(1)}, bf16[2,128,2048]{2,1,0:T(8,128)(2,1)S(1)}, u32[]{:S(2)}, u32[]{:S(2)}) %collective-permute-start.52) | collective-permute-done | bytes 1048608 | tf_op jit(solution)/shard_map/ppermute | solution.py:620
  640.4 14.7 %collective-permute-done.62 = bf16[16,320,128]{2,1,0:T(8,128)(2,1)S(1)} collective-permute-done((bf16[16,320,128]{2,1,0:T(8,128)(2,1)S(1)}, bf16[16,320,128]{2,1,0:T(8,128)(2,1)S(1)}, u32[]{:S(2)}, u32[]{:S(2)}) %collective-permute-start.62) | collective-permute-done | bytes 1310752 | tf_op jit(solution)/shard_map/ppermute | solution.py:626
  656.5 5.1 all-to-all-start.7
  665.9 35.9 %collective-permute-done.54.moving_ref = bf16[2,128,2048]{2,1,0:T(8,128)(2,1)S(1)} collective-permute-done((bf16[2,128,2048]{2,1,0:T(8,128)(2,1)S(1)}, bf16[2,128,2048]{2,1,0:T(8,128)(2,1)S(1)}, u32[]{:S(2)}, u32[]{:S(2)}) %collective-permute-start.54) | collective-permute-done | bytes 1048608 | tf_op jit(solution)/shard_map/ppermute | solution.py:620
  701.9 2.4 collective-permute-start.55
  706.6 3.0 backward_end.3
  711.1 4.2 all-to-all-start.5
  715.3 3.8 add_convert_fusion.1
  719.5 6.3 all-to-all-start.8
  726.1 2.3 forward_out.1
  734.7 7.2 spread_gradients.2
  746.1 10.4 %collective-permute-done.59 = bf16[128,2048]{1,0:T(8,128)(2,1)S(1)} collective-permute-done((bf16[128,2048]{1,0:T(8,128)(2,1)S(1)}, bf16[128,2048]{1,0:T(8,128)(2,1)S(1)}, u32[]{:S(2)}, u32[]{:S(2)}) %collective-permute-start.59) | collective-permute-done | bytes 524320 | tf_op jit(solution)/shard_map/ppermute | solution.py:626
  757.5 10.1 %all-to-all-done.8.up_ref = bf16[16,448,128]{2,1,0:T(8,128)(2,1)S(1)} async-done(((bf16[16,448,128]{2,1,0:T(8,128)(2,1)}), bf16[16,448,128]{2,1,0:T(8,128)(2,1)S(1)}, u32[]{:S(2)}, u32[]{:S(2)}) %all-to-all-start.8) | async-done | bytes 1835040 | tf_op jit(solution)/shard_map/all_to_all | solution.py:676
  768.8 7.2 spread_gradients.3
  (319 shorter events, 115.8 us)
Async XLA Ops:
  3.0 16.7 %collective-permute-start.5 = (bf16[2,128,2048]{2,1,0:T(8,128)(2,1)}, bf16[2,128,2048]{2,1,0:T(8,128)(2,1)}, u32[]{:S(2)}, u32[]{:S(2)}) collective-permute-start(bf16[2,128,2048]{2,1,0:T(8,128)(2,1)} %pad_maximum_fusion), channel_id=1, source_target_pairs={{0,2},{2,0},{4,6},{6,4},{8,10},{10,8},{12,14},{14,12},{16,18},{18,... | collective-permute-start | bytes 3145736 | tf_op jit(solution)/shard_map/ppermute | solution.py:623
  11.4 66.3 %all-to-all-start = ((bf16[16,464,128]{2,1,0:T(8,128)(2,1)}), bf16[16,464,128]{2,1,0:T(8,128)(2,1)S(1)}, u32[]{:S(2)}, u32[]{:S(2)}) async-start(bf16[16,464,128]{2,1,0:T(8,128)(2,1)} %pack_up.3), calls=%async_computation | async-start | bytes 3801088 | tf_op jit(solution)/shard_map/all_to_all | solution.py:676
  22.1 48.2 %collective-permute-start.6 = (bf16[2,128,2048]{2,1,0:T(8,128)(2,1)S(1)}, bf16[2,128,2048]{2,1,0:T(8,128)(2,1)}, u32[]{:S(2)}, u32[]{:S(2)}) collective-permute-start(bf16[2,128,2048]{2,1,0:T(8,128)(2,1)S(1)} %select_multiply_fusion.refs_10_.refs_17_), channel_id=1, source_target_pairs={{0,8},{2,6},{8,16},{10,2},{16,24},{18,10},{24,28},{26,18},{28,20},... | collective-permute-start | bytes 3145736 | tf_op jit(solution)/shard_map/ppermute | solution.py:620
  70.3 14.3 %collective-permute-start.7 = (bf16[2,128,2048]{2,1,0:T(8,128)(2,1)}, bf16[2,128,2048]{2,1,0:T(8,128)(2,1)}, u32[]{:S(2)}, u32[]{:S(2)}) collective-permute-start(bf16[2,128,2048]{2,1,0:T(8,128)(2,1)} %collective-permute-done.6.refs_11_.refs_18_), channel_id=1, source_target_pairs={{0,8},{2,6},{8,16},{10,2},{16,24},{18,10},{24,28},{26,18},{28,20},... | collective-permute-start | bytes 3145736 | tf_op jit(solution)/shard_map/ppermute | solution.py:620
  77.6 58.7 %all-to-all-start.1 = ((bf16[16,320,128]{2,1,0:T(8,128)(2,1)}), bf16[16,320,128]{2,1,0:T(8,128)(2,1)}, u32[]{:S(2)}, u32[]{:S(2)}) async-start(bf16[16,320,128]{2,1,0:T(8,128)(2,1)} %pack_down.2), calls=%async_computation.1 | async-start | bytes 2621440 | tf_op jit(solution)/shard_map/all_to_all | solution.py:676
  84.5 39.3 %collective-permute-start.8 = (bf16[2,128,2048]{2,1,0:T(8,128)(2,1)}, bf16[2,128,2048]{2,1,0:T(8,128)(2,1)}, u32[]{:S(2)}, u32[]{:S(2)}) collective-permute-start(bf16[2,128,2048]{2,1,0:T(8,128)(2,1)} %collective-permute-done.7.refs_12_.refs_19_), channel_id=1, source_target_pairs={{0,8},{2,6},{8,16},{10,2},{16,24},{18,10},{24,28},{26,18},{28,20},... | collective-permute-start | bytes 3145736 | tf_op jit(solution)/shard_map/ppermute | solution.py:620
  86.5 59.3 %collective-permute-start.3 = (bf16[16,464,128]{2,1,0:T(8,128)(2,1)S(1)}, bf16[16,464,128]{2,1,0:T(8,128)(2,1)}, u32[]{:S(2)}, u32[]{:S(2)}) collective-permute-start(bf16[16,464,128]{2,1,0:T(8,128)(2,1)S(1)} %all-to-all-done.own_ref), channel_id=1, source_target_pairs={{0,1},{1,0},{2,3},{3,2},{4,5},{5,4},{6,7},{7,6},{8,9},{9,8},{10,11... | collective-permute-start | bytes 5701640 | tf_op jit(solution)/shard_map/ppermute | solution.py:626
  87.9 46.3 %collective-permute-start.2 = (bf16[2,448]{1,0:T(2,128)(2,1)S(1)}, bf16[2,448]{1,0:T(2,128)(2,1)S(1)}, u32[]{:S(2)}, u32[]{:S(2)}) collective-permute-start(bf16[2,448]{1,0:T(2,128)(2,1)S(1)} %pad_maximum_fusion.7), channel_id=1, source_target_pairs={{0,1},{1,0},{2,3},{3,2},{4,5},{5,4},{6,7},{7,6},{8,9},{9,8},{10,11... | collective-permute-start | bytes 5384 | tf_op jit(solution)/shard_map/ppermute | solution.py:626
  124.9 12.9 %collective-permute-start.12 = (bf16[2,64,2048]{2,1,0:T(8,128)(2,1)S(1)}, bf16[2,64,2048]{2,1,0:T(8,128)(2,1)}, u32[]{:S(2)}, u32[]{:S(2)}) collective-permute-start(bf16[2,64,2048]{2,1,0:T(8,128)(2,1)S(1)} %constant_dynamic-slice_fusion.4), channel_id=1, source_target_pairs={{0,8},{2,6},{8,16},{10,2},{16,24},{18,10},{24,28},{26,18},{28,20},... | collective-permute-start | bytes 1572872 | tf_op jit(solution)/shard_map/ppermute | solution.py:620
  135.1 37.6 %collective-permute-start.9 = (bf16[2,128,2048]{2,1,0:T(8,128)(2,1)}, bf16[2,128,2048]{2,1,0:T(8,128)(2,1)}, u32[]{:S(2)}, u32[]{:S(2)}) collective-permute-start(bf16[2,128,2048]{2,1,0:T(8,128)(2,1)} %collective-permute-done.6.refs_11_.refs_18_), channel_id=1, source_target_pairs={{0,2},{2,0},{4,6},{6,4},{8,10},{10,8},{12,14},{14,12},{16,18},{18,... | collective-permute-start | bytes 3145736 | tf_op jit(solution)/shard_map/ppermute | solution.py:623
  136.3 36.5 %collective-permute-start.10 = (bf16[2,128,2048]{2,1,0:T(8,128)(2,1)}, bf16[2,128,2048]{2,1,0:T(8,128)(2,1)}, u32[]{:S(2)}, u32[]{:S(2)}) collective-permute-start(bf16[2,128,2048]{2,1,0:T(8,128)(2,1)} %collective-permute-done.7.refs_12_.refs_19_), channel_id=1, source_target_pairs={{0,2},{2,0},{4,6},{6,4},{8,10},{10,8},{12,14},{14,12},{16,18},{18,... | collective-permute-start | bytes 3145736 | tf_op jit(solution)/shard_map/ppermute | solution.py:623
  136.3 30.2 %collective-permute-start.4 = (bf16[16,320,128]{2,1,0:T(8,128)(2,1)}, bf16[16,320,128]{2,1,0:T(8,128)(2,1)}, u32[]{:S(2)}, u32[]{:S(2)}) collective-permute-start(bf16[16,320,128]{2,1,0:T(8,128)(2,1)} %all-to-all-done.1.own_ref), channel_id=1, source_target_pairs={{0,1},{1,0},{2,3},{3,2},{4,5},{5,4},{6,7},{7,6},{8,9},{9,8},{10,11... | collective-permute-start | bytes 3932168 | tf_op jit(solution)/shard_map/ppermute | solution.py:626
  137.8 35.0 %collective-permute-start.11 = (bf16[2,128,2048]{2,1,0:T(8,128)(2,1)}, bf16[2,128,2048]{2,1,0:T(8,128)(2,1)}, u32[]{:S(2)}, u32[]{:S(2)}) collective-permute-start(bf16[2,128,2048]{2,1,0:T(8,128)(2,1)} %collective-permute-done.8.refs_13_.refs_20_), channel_id=1, source_target_pairs={{0,2},{2,0},{4,6},{6,4},{8,10},{10,8},{12,14},{14,12},{16,18},{18,... | collective-permute-start | bytes 3145736 | tf_op jit(solution)/shard_map/ppermute | solution.py:623
  138.6 65.7 %all-to-all-start.2 = ((bf16[16,448,128]{2,1,0:T(8,128)(2,1)}), bf16[16,448,128]{2,1,0:T(8,128)(2,1)}, u32[]{:S(2)}, u32[]{:S(2)}) async-start(bf16[16,448,128]{2,1,0:T(8,128)(2,1)} %pack_up.2), calls=%async_computation.2 | async-start | bytes 3670016 | tf_op jit(solution)/shard_map/all_to_all | solution.py:676
  145.8 26.9 %collective-permute-start.13 = (bf16[2,64,2048]{2,1,0:T(8,128)(2,1)}, bf16[2,64,2048]{2,1,0:T(8,128)(2,1)S(1)}, u32[]{:S(2)}, u32[]{:S(2)}) collective-permute-start(bf16[2,64,2048]{2,1,0:T(8,128)(2,1)} %collective-permute-done.12.refs_17_.refs_24_), channel_id=1, source_target_pairs={{0,2},{2,0},{4,6},{6,4},{8,10},{10,8},{12,14},{14,12},{16,18},{18,... | collective-permute-start | bytes 1572872 | tf_op jit(solution)/shard_map/ppermute | solution.py:623
  202.8 8.2 %collective-permute-start.14 = (bf16[448,2048]{1,0:T(8,128)(2,1)}, bf16[448,2048]{1,0:T(8,128)(2,1)S(1)}, u32[]{:S(2)}, u32[]{:S(2)}) collective-permute-start(bf16[448,2048]{1,0:T(8,128)(2,1)} %get-tuple-element.72), channel_id=1, source_target_pairs={{0,2},{2,0},{4,6},{6,4},{8,10},{10,8},{12,14},{14,12},{16,18},{18,... | collective-permute-start | bytes 5505032 | tf_op jit(solution)/shard_map/ppermute | solution.py:623
  209.2 5.6 collective-permute-start.16
  216.9 13.6 %collective-permute-start.17 = (bf16[1,128,2048]{2,1,0:T(8,128)(2,1)}, bf16[1,128,2048]{2,1,0:T(8,128)(2,1)}, u32[]{:S(2)}, u32[]{:S(2)}) collective-permute-start(bf16[1,128,2048]{2,1,0:T(8,128)(2,1)} %fusion.7), channel_id=1, source_target_pairs={{0,8},{2,6},{8,16},{10,2},{16,24},{18,10},{24,28},{26,18},{28,20},... | collective-permute-start | bytes 1572872 | tf_op jit(solution)/shard_map/ppermute | solution.py:620
  224.0 60.1 %all-to-all-start.3 = ((bf16[16,320,128]{2,1,0:T(8,128)(2,1)}), bf16[16,320,128]{2,1,0:T(8,128)(2,1)S(1)}, u32[]{:S(2)}, u32[]{:S(2)}) async-start(bf16[16,320,128]{2,1,0:T(8,128)(2,1)} %pack_down.3), calls=%async_computation.3 | async-start | bytes 2621440 | tf_op jit(solution)/shard_map/all_to_all | solution.py:676
  232.0 33.1 %collective-permute-start.18 = (bf16[1,128,2048]{2,1,0:T(8,128)(2,1)S(1)}, bf16[1,128,2048]{2,1,0:T(8,128)(2,1)S(1)}, u32[]{:S(2)}, u32[]{:S(2)}) collective-permute-start(bf16[1,128,2048]{2,1,0:T(8,128)(2,1)S(1)} %fusion.6), channel_id=1, source_target_pairs={{0,8},{2,6},{8,16},{10,2},{16,24},{18,10},{24,28},{26,18},{28,20},... | collective-permute-start | bytes 1572872 | tf_op jit(solution)/shard_map/ppermute | solution.py:620
  267.2 8.5 %collective-permute-start.19 = (bf16[1,128,2048]{2,1,0:T(8,128)(2,1)}, bf16[1,128,2048]{2,1,0:T(8,128)(2,1)S(1)}, u32[]{:S(2)}, u32[]{:S(2)}) collective-permute-start(bf16[1,128,2048]{2,1,0:T(8,128)(2,1)} %fusion.5), channel_id=1, source_target_pairs={{0,8},{2,6},{8,16},{10,2},{16,24},{18,10},{24,28},{26,18},{28,20},... | collective-permute-start | bytes 1572872 | tf_op jit(solution)/shard_map/ppermute | solution.py:620
  284.3 41.4 %collective-permute-start = (bf16[16,448,128]{2,1,0:T(8,128)(2,1)}, bf16[16,448,128]{2,1,0:T(8,128)(2,1)S(1)}, u32[]{:S(2)}, u32[]{:S(2)}) collective-permute-start(bf16[16,448,128]{2,1,0:T(8,128)(2,1)} %all-to-all-done.2.own_ref), channel_id=1, source_target_pairs={{0,1},{1,0},{2,3},{3,2},{4,5},{5,4},{6,7},{7,6},{8,9},{9,8},{10,11... | collective-permute-start | bytes 5505032 | tf_op jit(solution)/shard_map/ppermute | solution.py:626
  287.1 8.5 %collective-permute-start.22 = (bf16[128,2048]{1,0:T(8,128)(2,1)S(1)}, bf16[128,2048]{1,0:T(8,128)(2,1)}, u32[]{:S(2)}, u32[]{:S(2)}) collective-permute-start(bf16[128,2048]{1,0:T(8,128)(2,1)S(1)} %maximum_select_fusion.2.refs_8_), channel_id=1, source_target_pairs={{0,8},{2,6},{8,16},{10,2},{16,24},{18,10},{24,28},{26,18},{28,20},... | collective-permute-start | bytes 1572872 | tf_op jit(solution)/shard_map/ppermute | solution.py:620
  295.6 8.6 %collective-permute-start.23 = (bf16[128,2048]{1,0:T(8,128)(2,1)}, bf16[128,2048]{1,0:T(8,128)(2,1)}, u32[]{:S(2)}, u32[]{:S(2)}) collective-permute-start(bf16[128,2048]{1,0:T(8,128)(2,1)} %collective-permute-done.22.refs_9_), channel_id=1, source_target_pairs={{0,8},{2,6},{8,16},{10,2},{16,24},{18,10},{24,28},{26,18},{28,20},... | collective-permute-start | bytes 1572872 | tf_op jit(solution)/shard_map/ppermute | solution.py:620
  295.6 58.3 %collective-permute-start.1 = (bf16[16,320,128]{2,1,0:T(8,128)(2,1)S(1)}, bf16[16,320,128]{2,1,0:T(8,128)(2,1)}, u32[]{:S(2)}, u32[]{:S(2)}) collective-permute-start(bf16[16,320,128]{2,1,0:T(8,128)(2,1)S(1)} %all-to-all-done.3.own_ref), channel_id=1, source_target_pairs={{0,1},{1,0},{2,3},{3,2},{4,5},{5,4},{6,7},{7,6},{8,9},{9,8},{10,11... | collective-permute-start | bytes 3932168 | tf_op jit(solution)/shard_map/ppermute | solution.py:626
  304.2 8.6 %collective-permute-start.24 = (bf16[128,2048]{1,0:T(8,128)(2,1)}, bf16[128,2048]{1,0:T(8,128)(2,1)}, u32[]{:S(2)}, u32[]{:S(2)}) collective-permute-start(bf16[128,2048]{1,0:T(8,128)(2,1)} %collective-permute-done.23.refs_10_), channel_id=1, source_target_pairs={{0,8},{2,6},{8,16},{10,2},{16,24},{18,10},{24,28},{26,18},{28,20},... | collective-permute-start | bytes 1572872 | tf_op jit(solution)/shard_map/ppermute | solution.py:620
  304.2 55.8 %collective-permute-start.25 = (bf16[128,2048]{1,0:T(8,128)(2,1)}, bf16[128,2048]{1,0:T(8,128)(2,1)}, u32[]{:S(2)}, u32[]{:S(2)}) collective-permute-start(bf16[128,2048]{1,0:T(8,128)(2,1)} %collective-permute-done.22.refs_9_), channel_id=1, source_target_pairs={{0,2},{2,0},{4,6},{6,4},{8,10},{10,8},{12,14},{14,12},{16,18},{18,... | collective-permute-start | bytes 1572872 | tf_op jit(solution)/shard_map/ppermute | solution.py:623
  306.2 53.8 %collective-permute-start.26 = (bf16[128,2048]{1,0:T(8,128)(2,1)}, bf16[128,2048]{1,0:T(8,128)(2,1)}, u32[]{:S(2)}, u32[]{:S(2)}) collective-permute-start(bf16[128,2048]{1,0:T(8,128)(2,1)} %collective-permute-done.23.refs_10_), channel_id=1, source_target_pairs={{0,2},{2,0},{4,6},{6,4},{8,10},{10,8},{12,14},{14,12},{16,18},{18,... | collective-permute-start | bytes 1572872 | tf_op jit(solution)/shard_map/ppermute | solution.py:623
  313.8 14.0 %collective-permute-start.28 = (bf16[64,2048]{1,0:T(8,128)(2,1)S(1)}, bf16[64,2048]{1,0:T(8,128)(2,1)}, u32[]{:S(2)}, u32[]{:S(2)}) collective-permute-start(bf16[64,2048]{1,0:T(8,128)(2,1)S(1)} %constant_dynamic-slice_fusion.2), channel_id=1, source_target_pairs={{0,8},{2,6},{8,16},{10,2},{16,24},{18,10},{24,28},{26,18},{28,20},... | collective-permute-start | bytes 786440 | tf_op jit(solution)/shard_map/ppermute | solution.py:620
  325.7 34.3 %collective-permute-start.27 = (bf16[128,2048]{1,0:T(8,128)(2,1)}, bf16[128,2048]{1,0:T(8,128)(2,1)}, u32[]{:S(2)}, u32[]{:S(2)}) collective-permute-start(bf16[128,2048]{1,0:T(8,128)(2,1)} %collective-permute-done.24.refs_11_), channel_id=1, source_target_pairs={{0,2},{2,0},{4,6},{6,4},{8,10},{10,8},{12,14},{14,12},{16,18},{18,... | collective-permute-start | bytes 1572872 | tf_op jit(solution)/shard_map/ppermute | solution.py:623
  327.8 32.2 %collective-permute-start.29 = (bf16[64,2048]{1,0:T(8,128)(2,1)}, bf16[64,2048]{1,0:T(8,128)(2,1)S(1)}, u32[]{:S(2)}, u32[]{:S(2)}) collective-permute-start(bf16[64,2048]{1,0:T(8,128)(2,1)} %collective-permute-done.28.refs_15_), channel_id=1, source_target_pairs={{0,2},{2,0},{4,6},{6,4},{8,10},{10,8},{12,14},{14,12},{16,18},{18,... | collective-permute-start | bytes 786440 | tf_op jit(solution)/shard_map/ppermute | solution.py:623
  396.1 11.9 %collective-permute-start.31 = (bf16[448,2048]{1,0:T(8,128)(2,1)}, bf16[448,2048]{1,0:T(8,128)(2,1)S(1)}, u32[]{:S(2)}, u32[]{:S(2)}) collective-permute-start(bf16[448,2048]{1,0:T(8,128)(2,1)} %get-tuple-element.83), channel_id=1, source_target_pairs={{0,2},{2,0},{4,6},{6,4},{8,10},{10,8},{12,14},{14,12},{16,18},{18,... | collective-permute-start | bytes 5505032 | tf_op jit(solution)/shard_map/ppermute | solution.py:623
  402.4 5.6 collective-permute-start.33
  409.6 8.4 %collective-permute-start.34 = (bf16[1,128,2048]{2,1,0:T(8,128)(2,1)S(1)}, bf16[1,128,2048]{2,1,0:T(8,128)(2,1)S(1)}, u32[]{:S(2)}, u32[]{:S(2)}) collective-permute-start(bf16[1,128,2048]{2,1,0:T(8,128)(2,1)S(1)} %fusion.8), channel_id=1, source_target_pairs={{0,8},{2,6},{8,16},{10,2},{16,24},{18,10},{24,28},{26,18},{28,20},... | collective-permute-start | bytes 1572872 | tf_op jit(solution)/shard_map/ppermute | solution.py:620
  418.3 8.4 %collective-permute-start.35 = (bf16[1,128,2048]{2,1,0:T(8,128)(2,1)S(1)}, bf16[1,128,2048]{2,1,0:T(8,128)(2,1)S(1)}, u32[]{:S(2)}, u32[]{:S(2)}) collective-permute-start(bf16[1,128,2048]{2,1,0:T(8,128)(2,1)S(1)} %fusion.4), channel_id=1, source_target_pairs={{0,8},{2,6},{8,16},{10,2},{16,24},{18,10},{24,28},{26,18},{28,20},... | collective-permute-start | bytes 1572872 | tf_op jit(solution)/shard_map/ppermute | solution.py:620
  427.7 10.2 %collective-permute-start.36 = (bf16[1,128,2048]{2,1,0:T(8,128)(2,1)}, bf16[1,128,2048]{2,1,0:T(8,128)(2,1)S(1)}, u32[]{:S(2)}, u32[]{:S(2)}) collective-permute-start(bf16[1,128,2048]{2,1,0:T(8,128)(2,1)} %fusion.3), channel_id=1, source_target_pairs={{0,8},{2,6},{8,16},{10,2},{16,24},{18,10},{24,28},{26,18},{28,20},... | collective-permute-start | bytes 1572872 | tf_op jit(solution)/shard_map/ppermute | solution.py:620
  436.7 31.6 %collective-permute-start.47 = (bf16[16,320,128]{2,1,0:T(8,128)(2,1)}, bf16[16,320,128]{2,1,0:T(8,128)(2,1)S(1)}, u32[]{:S(2)}, u32[]{:S(2)}) collective-permute-start(bf16[16,320,128]{2,1,0:T(8,128)(2,1)} %get-tuple-element.95), channel_id=1, source_target_pairs={{0,1},{1,0},{2,3},{3,2},{4,5},{5,4},{6,7},{7,6},{8,9},{9,8},{10,11... | collective-permute-start | bytes 3932168 | tf_op jit(solution)/shard_map/ppermute | solution.py:626
  437.9 13.3 %collective-permute-start.37 = (bf16[1,64,2048]{2,1,0:T(8,128)(2,1)S(1)}, bf16[1,64,2048]{2,1,0:T(8,128)(2,1)S(1)}, u32[]{:S(2)}, u32[]{:S(2)}) collective-permute-start(bf16[1,64,2048]{2,1,0:T(8,128)(2,1)S(1)} %constant_dynamic-slice_fusion.1), channel_id=1, source_target_pairs={{0,2},{2,0},{4,6},{6,4},{8,10},{10,8},{12,14},{14,12},{16,18},{18,... | collective-permute-start | bytes 786440 | tf_op jit(solution)/shard_map/ppermute | solution.py:623
  458.0 8.5 %collective-permute-start.39 = (bf16[128,2048]{1,0:T(8,128)(2,1)S(1)}, bf16[128,2048]{1,0:T(8,128)(2,1)}, u32[]{:S(2)}, u32[]{:S(2)}) collective-permute-start(bf16[128,2048]{1,0:T(8,128)(2,1)S(1)} %maximum_select_fusion.4.rest_0_.refs_9_), channel_id=1, source_target_pairs={{0,8},{2,6},{8,16},{10,2},{16,24},{18,10},{24,28},{26,18},{28,20},... | collective-permute-start | bytes 1572872 | tf_op jit(solution)/shard_map/ppermute | solution.py:620
  466.5 9.2 %collective-permute-start.40 = (bf16[128,2048]{1,0:T(8,128)(2,1)}, bf16[128,2048]{1,0:T(8,128)(2,1)}, u32[]{:S(2)}, u32[]{:S(2)}) collective-permute-start(bf16[128,2048]{1,0:T(8,128)(2,1)} %collective-permute-done.39.rest_1_.refs_10_), channel_id=1, source_target_pairs={{0,8},{2,6},{8,16},{10,2},{16,24},{18,10},{24,28},{26,18},{28,20},... | collective-permute-start | bytes 1572872 | tf_op jit(solution)/shard_map/ppermute | solution.py:620
  469.6 61.2 %all-to-all-start.4 = ((bf16[16,320,128]{2,1,0:T(8,128)(2,1)}), bf16[16,320,128]{2,1,0:T(8,128)(2,1)S(1)}, u32[]{:S(2)}, u32[]{:S(2)}) async-start(bf16[16,320,128]{2,1,0:T(8,128)(2,1)} %add_convert_fusion.3), calls=%async_computation.4 | async-start | bytes 2621440 | tf_op jit(solution)/shard_map/all_to_all | solution.py:676
  475.8 34.6 %collective-permute-start.41 = (bf16[128,2048]{1,0:T(8,128)(2,1)}, bf16[128,2048]{1,0:T(8,128)(2,1)S(1)}, u32[]{:S(2)}, u32[]{:S(2)}) collective-permute-start(bf16[128,2048]{1,0:T(8,128)(2,1)} %collective-permute-done.40.rest_2_.refs_11_), channel_id=1, source_target_pairs={{0,8},{2,6},{8,16},{10,2},{16,24},{18,10},{24,28},{26,18},{28,20},... | collective-permute-start | bytes 1572872 | tf_op jit(solution)/shard_map/ppermute | solution.py:620
  477.0 36.3 %collective-permute-start.49 = (bf16[64,2048]{1,0:T(8,128)(2,1)}, bf16[64,2048]{1,0:T(8,128)(2,1)S(1)}, u32[]{:S(2)}, u32[]{:S(2)}) collective-permute-start(bf16[64,2048]{1,0:T(8,128)(2,1)} %get-tuple-element.103), channel_id=1, source_target_pairs={{0,2},{2,0},{4,6},{6,4},{8,10},{10,8},{12,14},{14,12},{16,18},{18,... | collective-permute-start | bytes 786440 | tf_op jit(solution)/shard_map/ppermute | solution.py:623
  512.3 7.6 collective-permute-start.42
  512.8 7.4 collective-permute-start.43
  512.9 7.4 collective-permute-start.44
  513.3 42.7 %collective-permute-start.30 = (bf16[448,2048]{1,0:T(8,128)(2,1)}, bf16[448,2048]{1,0:T(8,128)(2,1)}, u32[]{:S(2)}, u32[]{:S(2)}) collective-permute-start(bf16[448,2048]{1,0:T(8,128)(2,1)} %get-tuple-element.78), channel_id=1, source_target_pairs={{0,2},{2,0},{4,6},{6,4},{8,10},{10,8},{12,14},{14,12},{16,18},{18,... | collective-permute-start | bytes 5505032 | tf_op jit(solution)/shard_map/ppermute | solution.py:623
  519.9 49.7 %collective-permute-start.63 = (bf16[16,448,128]{2,1,0:T(8,128)(2,1)}, bf16[16,448,128]{2,1,0:T(8,128)(2,1)}, u32[]{:S(2)}, u32[]{:S(2)}) collective-permute-start(bf16[16,448,128]{2,1,0:T(8,128)(2,1)} %get-tuple-element.111), channel_id=1, source_target_pairs={{0,1},{1,0},{2,3},{3,2},{4,5},{5,4},{6,7},{7,6},{8,9},{9,8},{10,11... | collective-permute-start | bytes 5505032 | tf_op jit(solution)/shard_map/ppermute | solution.py:626
  555.6 24.1 %collective-permute-start.51 = (bf16[448,2048]{1,0:T(8,128)(2,1)}, bf16[448,2048]{1,0:T(8,128)(2,1)}, u32[]{:S(2)}, u32[]{:S(2)}) collective-permute-start(bf16[448,2048]{1,0:T(8,128)(2,1)} %get-tuple-element.104), channel_id=1, source_target_pairs={{0,2},{2,0},{4,6},{6,4},{8,10},{10,8},{12,14},{14,12},{16,18},{18,... | collective-permute-start | bytes 5505032 | tf_op jit(solution)/shard_map/ppermute | solution.py:623
  569.4 7.8 %collective-permute-start.48 = (bf16[64,2048]{1,0:T(8,128)(2,1)}, bf16[64,2048]{1,0:T(8,128)(2,1)}, u32[]{:S(2)}, u32[]{:S(2)}) collective-permute-start(bf16[64,2048]{1,0:T(8,128)(2,1)} %get-tuple-element.102), channel_id=1, source_target_pairs={{0,2},{2,0},{4,6},{6,4},{8,10},{10,8},{12,14},{14,12},{16,18},{18,... | collective-permute-start | bytes 786440 | tf_op jit(solution)/shard_map/ppermute | solution.py:623
  572.8 83.7 %all-to-all-start.6 = ((bf16[16,448,128]{2,1,0:T(8,128)(2,1)}), bf16[16,448,128]{2,1,0:T(8,128)(2,1)}, u32[]{:S(2)}, u32[]{:S(2)}) async-start(bf16[16,448,128]{2,1,0:T(8,128)(2,1)} %add_convert_fusion), calls=%async_computation.6 | async-start | bytes 3670016 | tf_op jit(solution)/shard_map/all_to_all | solution.py:676
  578.4 44.5 %collective-permute-start.50 = (bf16[2,64,2048]{2,1,0:T(8,128)(2,1)S(1)}, bf16[2,64,2048]{2,1,0:T(8,128)(2,1)S(1)}, u32[]{:S(2)}, u32[]{:S(2)}) collective-permute-start(bf16[2,64,2048]{2,1,0:T(8,128)(2,1)S(1)} %pad_maximum_fusion.1), channel_id=1, source_target_pairs={{0,8},{2,6},{8,16},{10,2},{16,24},{18,10},{24,28},{26,18},{28,20},... | collective-permute-start | bytes 1572872 | tf_op jit(solution)/shard_map/ppermute | solution.py:620
  623.3 14.0 %collective-permute-start.52 = (bf16[2,128,2048]{2,1,0:T(8,128)(2,1)S(1)}, bf16[2,128,2048]{2,1,0:T(8,128)(2,1)S(1)}, u32[]{:S(2)}, u32[]{:S(2)}) collective-permute-start(bf16[2,128,2048]{2,1,0:T(8,128)(2,1)S(1)} %fusion), channel_id=1, source_target_pairs={{0,8},{2,6},{8,16},{10,2},{16,24},{18,10},{24,28},{26,18},{28,20},... | collective-permute-start | bytes 3145736 | tf_op jit(solution)/shard_map/ppermute | solution.py:620
  625.2 29.9 %collective-permute-start.62 = (bf16[16,320,128]{2,1,0:T(8,128)(2,1)S(1)}, bf16[16,320,128]{2,1,0:T(8,128)(2,1)S(1)}, u32[]{:S(2)}, u32[]{:S(2)}) collective-permute-start(bf16[16,320,128]{2,1,0:T(8,128)(2,1)S(1)} %copy-done.43), channel_id=1, source_target_pairs={{0,1},{1,0},{2,3},{3,2},{4,5},{5,4},{6,7},{7,6},{8,9},{9,8},{10,11... | collective-permute-start | bytes 3932168 | tf_op jit(solution)/shard_map/ppermute | solution.py:626
  638.5 23.1 %collective-permute-start.53 = (bf16[2,128,2048]{2,1,0:T(8,128)(2,1)}, bf16[2,128,2048]{2,1,0:T(8,128)(2,1)}, u32[]{:S(2)}, u32[]{:S(2)}) collective-permute-start(bf16[2,128,2048]{2,1,0:T(8,128)(2,1)} %fusion.1), channel_id=1, source_target_pairs={{0,8},{2,6},{8,16},{10,2},{16,24},{18,10},{24,28},{26,18},{28,20},... | collective-permute-start | bytes 3145736 | tf_op jit(solution)/shard_map/ppermute | solution.py:620
  656.5 54.5 %all-to-all-start.7 = ((bf16[16,320,128]{2,1,0:T(8,128)(2,1)}), bf16[16,320,128]{2,1,0:T(8,128)(2,1)S(1)}, u32[]{:S(2)}, u32[]{:S(2)}) async-start(bf16[16,320,128]{2,1,0:T(8,128)(2,1)} %add_convert_fusion.2), calls=%async_computation.7 | async-start | bytes 2621440 | tf_op jit(solution)/shard_map/all_to_all | solution.py:676
  663.5 38.3 %collective-permute-start.54 = (bf16[2,128,2048]{2,1,0:T(8,128)(2,1)S(1)}, bf16[2,128,2048]{2,1,0:T(8,128)(2,1)S(1)}, u32[]{:S(2)}, u32[]{:S(2)}) collective-permute-start(bf16[2,128,2048]{2,1,0:T(8,128)(2,1)S(1)} %fusion.2), channel_id=1, source_target_pairs={{0,8},{2,6},{8,16},{10,2},{16,24},{18,10},{24,28},{26,18},{28,20},... | collective-permute-start | bytes 3145736 | tf_op jit(solution)/shard_map/ppermute | solution.py:620
  664.7 50.6 %collective-permute-start.61 = (bf16[16,448,128]{2,1,0:T(8,128)(2,1)}, bf16[16,448,128]{2,1,0:T(8,128)(2,1)}, u32[]{:S(2)}, u32[]{:S(2)}) collective-permute-start(bf16[16,448,128]{2,1,0:T(8,128)(2,1)} %get-tuple-element.109), channel_id=1, source_target_pairs={{0,1},{1,0},{2,3},{3,2},{4,5},{5,4},{6,7},{7,6},{8,9},{9,8},{10,11... | collective-permute-start | bytes 5505032 | tf_op jit(solution)/shard_map/ppermute | solution.py:626
  711.1 8.5 %all-to-all-start.5 = ((f32[16,6,128]{2,1,0:T(8,128)}), f32[16,6,128]{2,1,0:T(8,128)S(1)}, u32[]{:S(2)}, u32[]{:S(2)}) async-start(f32[16,6,128]{2,1,0:T(8,128)} %copy.70), calls=%async_computation.5 | async-start | bytes 131072 | tf_op jit(solution)/shard_map/all_to_all | solution.py:888
  719.5 48.1 %all-to-all-start.8 = ((bf16[16,448,128]{2,1,0:T(8,128)(2,1)}), bf16[16,448,128]{2,1,0:T(8,128)(2,1)S(1)}, u32[]{:S(2)}, u32[]{:S(2)}) async-start(bf16[16,448,128]{2,1,0:T(8,128)(2,1)} %add_convert_fusion.1), calls=%async_computation.8 | async-start | bytes 3670016 | tf_op jit(solution)/shard_map/all_to_all | solution.py:676
  730.1 11.8 %collective-permute-start.58 = (bf16[64,2048]{1,0:T(8,128)(2,1)S(1)}, bf16[64,2048]{1,0:T(8,128)(2,1)S(1)}, u32[]{:S(2)}, u32[]{:S(2)}) collective-permute-start(bf16[64,2048]{1,0:T(8,128)(2,1)S(1)} %copy-done.29), channel_id=1, source_target_pairs={{0,2},{2,0},{4,6},{6,4},{8,10},{10,8},{12,14},{14,12},{16,18},{18,... | collective-permute-start | bytes 786440 | tf_op jit(solution)/shard_map/ppermute | solution.py:623
  730.5 11.4 %collective-permute-start.60 = (f32[6,128]{1,0:T(8,128)S(1)}, f32[6,128]{1,0:T(8,128)S(1)}, u32[]{:S(2)}, u32[]{:S(2)}) collective-permute-start(f32[6,128]{1,0:T(8,128)S(1)} %reduce_sum.49), channel_id=1, source_target_pairs={{0,1},{1,0},{2,3},{3,2},{4,5},{5,4},{6,7},{7,6},{8,9},{9,8},{10,11... | collective-permute-start | bytes 9224 | tf_op jit(solution)/shard_map/ppermute | solution.py:626
  732.0 13.2 %collective-permute-start.57 = (bf16[128,2048]{1,0:T(8,128)(2,1)S(1)}, bf16[128,2048]{1,0:T(8,128)(2,1)S(1)}, u32[]{:S(2)}, u32[]{:S(2)}) collective-permute-start(bf16[128,2048]{1,0:T(8,128)(2,1)S(1)} %maximum_select_fusion.5), channel_id=1, source_target_pairs={{0,1},{1,0},{2,3},{3,2},{4,5},{5,4},{6,7},{7,6},{8,9},{9,8},{10,11... | collective-permute-start | bytes 1572872 | tf_op jit(solution)/shard_map/ppermute | solution.py:626
  742.1 14.4 %collective-permute-start.59 = (bf16[128,2048]{1,0:T(8,128)(2,1)S(1)}, bf16[128,2048]{1,0:T(8,128)(2,1)S(1)}, u32[]{:S(2)}, u32[]{:S(2)}) collective-permute-start(bf16[128,2048]{1,0:T(8,128)(2,1)S(1)} %maximum_select_fusion.6), channel_id=1, source_target_pairs={{0,1},{1,0},{2,3},{3,2},{4,5},{5,4},{6,7},{7,6},{8,9},{9,8},{10,11... | collective-permute-start | bytes 1572872 | tf_op jit(solution)/shard_map/ppermute | solution.py:626
  (63 other events, 674.0 us)

commit v4 on v3

--- a/solution.py
+++ b/solution.py
@@ -72,9 +72,14 @@
 ANY_SPEC = pl.BlockSpec(memory_space=pl.ANY)
 SMEM_SPEC = pl.BlockSpec(memory_space=pltpu.SMEM)
 WIDE = 2 * HEAD_DIM
+UP_ROWS = 3 * HEAD_DIM + 256
+DOWN_ROWS = HEAD_DIM + 256
+MEMBERS = 4
 
 
 def after(x, *others):
+    if not others:
+        return x
     return lax.optimization_barrier((x, *others))[0]
 
 
@@ -93,58 +98,66 @@
 
 def pack_up(qkv_ref, fc1_ref, *rest):
     out_ref = rest[-1]
-    q, k, v = (qkv_ref[0, p].astype(f32) for p in range(3))
-    out_ref[0, :WIDE], out_ref[1, :WIDE] = zipped(q, k)
-    rows = q.shape[0] // 2
-    out_ref[0, WIDE : WIDE + rows], out_ref[1, WIDE : WIDE + rows] = zipped(v[:rows], v[rows:])
-    base = WIDE + rows
-    for d in range(2):
-        for h in range(2):
-            out_ref[d, base + h * 128 : base + (h + 1) * 128] = fc1_ref[0, :, (2 * d + h) * 128 : (2 * d + h + 1) * 128]
-        if len(rest) > 1:
-            out_ref[d, base + 256 :] = rest[0][...]
-
-
-def call_pack_up(qkv, fc1, layer, small):
-    rows = 3 * HEAD_DIM + 256 + (0 if small is None else small.shape[0])
-    specs = [
-        pl.BlockSpec((1, 3, 128, 128), lambda i: (layer, 0, 0, i)),
-        pl.BlockSpec((1, 128, 512), lambda i: (layer, 0, i)),
-    ]
-    if small is not None:
-        specs.append(pl.BlockSpec(small.shape, lambda i: (0, 0)))
-    return pl.pallas_call(
-        pack_up,
-        grid=(GROUP // 2,),
-        in_specs=specs,
-        out_specs=pl.BlockSpec((2, rows, 128), lambda i: (i, 0, 0)),
-        out_shape=jax.ShapeDtypeStruct((GROUP, rows, 128), bf16),
-        name="pack_up",
-    )(*([qkv, fc1] + ([] if small is None else [small])))
+    for pair in range(MEMBERS // 2):
+        lanes = slice(pair * 128, (pair + 1) * 128)
+        q, k, v = (qkv_ref[0, p, :, lanes].astype(f32) for p in range(3))
+        here, there = 2 * pair, 2 * pair + 1
+        out_ref[here, :WIDE], out_ref[there, :WIDE] = zipped(q, k)
+        rows = q.shape[0] // 2
+        out_ref[here, WIDE : WIDE + rows], out_ref[there, WIDE : WIDE + rows] = zipped(v[:rows], v[rows:])
+        base = WIDE + rows
+        for d in (here, there):
+            for h in range(2):
+                out_ref[d, base + h * 128 : base + (h + 1) * 128] = fc1_ref[0, :, (2 * d + h) * 128 : (2 * d + h + 1) * 128]
+
+
+def pack_first(qkv_ref, fc1_ref, small_ref, out_ref):
+    pack_up(qkv_ref, fc1_ref, out_ref)
+    for d in range(MEMBERS):
+        out_ref[d, UP_ROWS:] = small_ref[...]
+
+
+def pack_both(qkv_ref, fc1_ref, out_w_ref, fc2_ref, out_ref):
+    pack_up(qkv_ref, fc1_ref, out_ref)
+    pack_down(out_w_ref, fc2_ref, out_ref.at[:, UP_ROWS:])
 
 
 def pack_down(out_w_ref, fc2_ref, out_ref):
-    for d in range(2):
+    for d in range(MEMBERS):
         out_ref[d, :HEAD_DIM] = out_w_ref[0, d * HEAD_DIM : (d + 1) * HEAD_DIM]
         out_ref[d, HEAD_DIM:] = fc2_ref[0, d * 256 : (d + 1) * 256]
 
 
-def call_pack_down(out_w, fc2, layer):
+def call_pack(body, layer, ups, downs, small):
+    rows, specs = 0, []
+    if ups:
+        rows += UP_ROWS
+        specs += [
+            pl.BlockSpec((1, 3, 128, MEMBERS * HEAD_DIM), lambda i: (layer, 0, 0, i)),
+            pl.BlockSpec((1, 128, MEMBERS * 256), lambda i: (layer, 0, i)),
+        ]
+    if downs:
+        rows += DOWN_ROWS
+        specs += [
+            pl.BlockSpec((1, MEMBERS * HEAD_DIM, 128), lambda i: (layer, i, 0)),
+            pl.BlockSpec((1, MEMBERS * 256, 128), lambda i: (layer, i, 0)),
+        ]
+    if small:
+        rows += small[0].shape[0]
+        specs.append(pl.BlockSpec(small[0].shape, lambda i: (0, 0)))
     return pl.pallas_call(
-        pack_down,
-        grid=(GROUP // 2,),
-        in_specs=[
-            pl.BlockSpec((1, 128, 128), lambda i: (layer, i, 0)),
-            pl.BlockSpec((1, 512, 128), lambda i: (layer, i, 0)),
-        ],
-        out_specs=pl.BlockSpec((2, HEAD_DIM + 256, 128), lambda i: (i, 0, 0)),
-        out_shape=jax.ShapeDtypeStruct((GROUP, HEAD_DIM + 256, 128), bf16),
-        name="pack_down",
-    )(out_w, fc2)
+        body,
+        grid=(GROUP // MEMBERS,),
+        in_specs=specs,
+        out_specs=pl.BlockSpec((MEMBERS, rows, 128), lambda i: (i, 0, 0)),
+        out_shape=jax.ShapeDtypeStruct((GROUP, rows, 128), bf16),
+        cost_estimate=pl.CostEstimate(flops=0, bytes_accessed=GROUP * rows * 128 * 8, transcendentals=0),
+        name=body.__name__,
+    )(*ups, *downs, *small)
 
 
 def join_up(own_ref, other_ref, out_ref):
-    for e in range(2):
+    for e in range(MEMBERS):
         rows = slice(e * 128, (e + 1) * 128)
         a, b = own_ref[e, :WIDE].astype(f32), other_ref[e, :WIDE].astype(f32)
         out_ref[rows, :WIDE], out_ref[rows, WIDE : 2 * WIDE] = zipped(a, b)
@@ -158,35 +171,37 @@
                 out_ref[rows, lanes : lanes + 128] = ref[e, WIDE + 64 + h * 128 : WIDE + 64 + (h + 1) * 128]
 
 
-def call_join_up(own, other):
-    rows = own.shape[1]
-    return pl.pallas_call(
-        join_up,
-        grid=(GROUP // 2,),
-        in_specs=[pl.BlockSpec((2, rows, 128), lambda i: (i, 0, 0))] * 2,
-        out_specs=pl.BlockSpec((256, 3 * WIDE + 512), lambda i: (i, 0)),
-        out_shape=jax.ShapeDtypeStruct((GROUP * 128, 3 * WIDE + 512), bf16),
-        name="join_up",
-    )(own, other)
-
-
 def join_down(own_ref, other_ref, out_ref):
-    for e in range(2):
+    base = own_ref.shape[1] - DOWN_ROWS
+    for e in range(MEMBERS):
         lanes = slice(e * 128, (e + 1) * 128)
         for n, ref in enumerate((own_ref, other_ref)):
-            out_ref[n * HEAD_DIM : (n + 1) * HEAD_DIM, lanes] = ref[e, :HEAD_DIM]
-            out_ref[WIDE + n * 256 : WIDE + (n + 1) * 256, lanes] = ref[e, HEAD_DIM:]
-
-
-def call_join_down(own, other):
+            out_ref[n * HEAD_DIM : (n + 1) * HEAD_DIM, lanes] = ref[e, base : base + HEAD_DIM]
+            out_ref[WIDE + n * 256 : WIDE + (n + 1) * 256, lanes] = ref[e, base + HEAD_DIM :]
+
+
+def join_both(own_ref, other_ref, up_ref, down_ref):
+    join_up(own_ref, other_ref, up_ref)
+    join_down(own_ref, other_ref, down_ref)
+
+
+def call_join(body, own, other, ups, downs):
     rows = own.shape[1]
+    specs, shapes = [], []
+    if ups:
+        specs.append(pl.BlockSpec((MEMBERS * 128, 2 * UP_ROWS), lambda i: (i, 0)))
+        shapes.append(jax.ShapeDtypeStruct((GROUP * 128, 2 * UP_ROWS), bf16))
+    if downs:
+        specs.append(pl.BlockSpec((2 * DOWN_ROWS, MEMBERS * 128), lambda i: (0, i)))
+        shapes.append(jax.ShapeDtypeStruct((2 * DOWN_ROWS, GROUP * 128), bf16))
     return pl.pallas_call(
-        join_down,
-        grid=(GROUP // 2,),
-        in_specs=[pl.BlockSpec((2, rows, 128), lambda i: (i, 0, 0))] * 2,
-        out_specs=pl.BlockSpec((2 * rows, 256), lambda i: (0, i)),
-        out_shape=jax.ShapeDtypeStruct((2 * rows, GROUP * 128), bf16),
-        name="join_down",
+        body,
+        grid=(GROUP // MEMBERS,),
+        in_specs=[pl.BlockSpec((MEMBERS, rows, 128), lambda i: (i, 0, 0))] * 2,
+        out_specs=specs,
+        out_shape=shapes,
+        cost_estimate=pl.CostEstimate(flops=0, bytes_accessed=GROUP * rows * 128 * 12, transcendentals=0),
+        name=body.__name__,
     )(own, other)
 
 
@@ -643,20 +658,20 @@
             is_first, jnp.concatenate([own, other], 0), jnp.concatenate([other, own], 0)
         )
 
-    def gather_rows(mine):
+    def gather_rows(mine, needed={}):
         behind, ahead = [], []
         moving = mine
-        for _ in range(side):
-            moving = along(moving)
+        for step in range(side):
+            moving = along(after(moving, *needed.get(step, ())))
             behind.append(moving)
             ahead.append(across(moving))
-        far = along(my_half(moving, at, moving.ndim - 2))
+        far = along(after(my_half(moving, at, moving.ndim - 2), *needed.get(side, ())))
         return [mine] + behind + ahead + [far, across(far)]
 
     rows = lax.broadcasted_iota(jnp.int32, (block, 1), 0)
     mine_rows = (rows < half) == is_first
 
-    def ring_sum(*sets):
+    def ring_sum(*sets, needed=()):
         took_far = [across(give_far) for give_far, _, _ in sets]
         took = [across(give) for _, give, _ in sets]
         keep = [x for _, _, x in sets]
@@ -665,6 +680,8 @@
         moving = jnp.where(mine_rows, jnp.concatenate([moving, moving], 1), 0).astype(f32)
         for step in reversed(range(side)):
             here = slice(step * block, (step + 1) * block)
+            if step == side - 2 and needed:
+                moving = after(moving, *needed)
             added = [k[here].astype(f32) + t[here].astype(f32) for k, t in zip(keep, took)]
             moving = along((moving + jnp.stack(added)).astype(bf16))
             if step:
@@ -684,26 +701,20 @@
             (positions % 64).astype(bf16),
         ]
     )
-    slab_rows = 3 * HEAD_DIM + hidden
-    small_all = None
     weights = []
-    arrivals = []
     if groups == 1:
         qkv_turned = qkv_weight.transpose(0, 2, 1, 3)
-        previous = ()
-        for layer in range(LAYERS):
-            extra = None
-            if layer == 0:
-                extra = jnp.concatenate([small, jnp.zeros_like(small)]).reshape(-1, 128)
-            up = spread(after(call_pack_up(qkv_turned, fc1_weight, layer, extra), *previous))
-            if layer == 0:
-                small_all = up[:, slab_rows:].reshape(GROUP, -1)[:, : small.shape[0]]
-            up_other = over(up)
-            down = spread(after(call_pack_down(out_weight, fc2_weight, layer), up))
-            down_other = over(down)
-            previous = (down,)
-            arrivals.append((up, down))
-            weights.append((call_join_up(up, up_other), call_join_down(down, down_other)))
+        ups, downs = (qkv_turned, fc1_weight), (out_weight, fc2_weight)
+        extra = jnp.concatenate([small, jnp.zeros_like(small)]).reshape(-1, 128)
+        up = spread(call_pack(pack_first, 0, ups, (), (extra,)))
+        small_all = up[:, UP_ROWS:].reshape(GROUP, -1)[:, : small.shape[0]]
+        up_other = over(up)
+        packed_down = call_pack(pack_down, 0, (), downs, ())
+        down = spread(after(packed_down, up))
+        down_other = over(down)
+        weights.append(call_join(join_up, up, up_other, True, False) + call_join(join_down, down, down_other, False, True))
+        packed_last = call_pack(pack_both, 1, ups, downs, ())
+        first_up, first_other, first_down = up, up_other, down
     else:
         small_all = lax.all_gather(small, "dp", axis=0, tiled=False)
         for layer in range(LAYERS):
@@ -715,7 +726,7 @@
                 axis=2,
             )
             up = lax.all_gather(spread(up), "dp", axis=0, axis_index_groups=outer, tiled=True)
-            up = up.reshape(width // 128, 128, slab_rows)
+            up = up.reshape(width // 128, 128, UP_ROWS)
             value = up[:, :, WIDE : WIDE + HEAD_DIM]
             first = WIDE + HEAD_DIM
             up = jnp.concatenate(
@@ -733,8 +744,7 @@
             )
             down = lax.all_gather(spread(down), "dp", axis=0, axis_index_groups=outer, tiled=True)
             down = down.transpose(1, 0, 2).reshape(-1, width // 128, 128).transpose(1, 0, 2)
-            arrivals.append((up, down))
-            weights.append((call_join_up(up, over(up)), call_join_down(down, over(down))))
+            weights.append(call_join(join_up, up, over(up), True, False) + call_join(join_down, down, over(down), False, True))
     if groups == 1:
         biases = jnp.concatenate([qkv_bias.reshape(LAYERS, 3 * HEAD_DIM), fc1_bias], axis=1)
     else:
@@ -795,7 +805,15 @@
     both = jnp.where(tensor == core, both, across(both))
     keeps = jnp.stack([jnp.ones_like(labels[0]), (labels[0] > 0).astype(labels.dtype)]).astype(bf16)
     both = both * keeps[:, :, None]
-    inputs = gather_rows(both)
+    if groups == 1:
+        inputs = gather_rows(after(both, packed_down, packed_last, first_up), {side: (first_other,)})
+        slab = spread(after(packed_last, first_down, inputs[-2]))
+        slab_other = over(slab)
+        weights.append(call_join(join_both, slab, slab_other, True, True))
+        slabs, others = (slab,), (slab_other,)
+    else:
+        inputs = gather_rows(both)
+        slabs, others = (), ()
     mine_inputs = my_half(both, at, 1)
     state, grad_state = mine_inputs[0], mine_inputs[1]
 
@@ -806,25 +824,27 @@
     next_state, normed_own = call_end(
         partial(forward_end, False),
         core_word,
-        ring_sum((after(parts[0], arrivals[1][0]), parts[1], parts[2]))[0],
+        ring_sum((after(parts[0], *slabs), parts[1], parts[2]))[0],
         [state, added_bias[0], gains[1], shifts[1]],
         [jax.ShapeDtypeStruct(rows_shape, f32), jax.ShapeDtypeStruct(rows_shape, bf16)],
         "forward_end",
     )
-    normed_own = after(normed_own, arrivals[1][1])
-    normed_chunks = gather_rows(in_order(normed_own, across(normed_own)))
+    normed_chunks = gather_rows(in_order(normed_own, across(normed_own)), {1: others})
 
     def handed_back(own_rows):
         filled = in_order(own_rows, across(own_rows))
         return jnp.where(tensor == core, filled, over(filled))
 
-    def summed(own, other, *earlier):
+    def summed(own, other, *earlier, extra=None):
         total = own.astype(f32) + over(other).astype(f32)
         if groups > 1:
             total = total.transpose(1, 0, 2).reshape(total.shape[1], width)
             total = lax.psum_scatter(total, "dp", scatter_dimension=1, axis_index_groups=outer, tiled=True)
             total = total.reshape(total.shape[0], GROUP, piece).transpose(1, 0, 2)
-        return spread(after(total.astype(bf16), *earlier))
+        total = total.astype(bf16)
+        if extra is not None:
+            total = jnp.concatenate([total, extra], axis=1)
+        return spread(after(total, *earlier))
 
     down_own = [(0, HEAD_DIM), (WIDE, WIDE + hidden)]
     down_other = [(HEAD_DIM, WIDE), (WIDE + hidden, WIDE + 2 * hidden)]
@@ -857,9 +877,8 @@
     out_parts = parts[:3]
     down_pair = down_gradients(wide_last, [grad_rows])
     *up_pair, bias_last = up_gradients(slim, normed_last)
-    grad_state, grad_low, sums_last = backward_finish(
-        ring_sum(parts[3:])[0], after(next_state, down_pair[0], up_pair[0]), grad_state, 1
-    )
+    grad_end, out_end = ring_sum(parts[3:], out_parts, needed=(down_pair[0], up_pair[0]))
+    grad_state, grad_low, sums_last = backward_finish(grad_end, next_state, grad_state, 1)
     grad_chunks = gather_rows(in_order(grad_low, across(grad_low)))
     down_last = summed(*down_pair)
     up_last = summed(*up_pair, down_last)
@@ -869,9 +888,8 @@
         "last", core_word, weights[0], tables, allowed, [heads, after(hidden_pre, down_pair[0], down_last)], grad_chunks
     )
     down_first = summed(*down_pair, up_last)
-    *up_pair, bias_first = up_gradients(slim, normed)
-    up_first = summed(*up_pair, down_first)
-    grad_end, out_end = ring_sum((after(parts[0], up_pair[0]), parts[1], parts[2]), out_parts)
+    *up_pair, bias_first = up_gradients(slim, after(normed, up_last))
+    (grad_end,) = ring_sum((after(parts[0], up_pair[0]), parts[1], parts[2]), needed=(down_first,))
     _, grad_low, sums_first = backward_finish(grad_end, state, grad_state, 0)
     grad_hidden = handed_back(grad_low).astype(f32)
     (hidden_out,) = call_end(
@@ -885,7 +903,14 @@
     hidden_out = handed_back(hidden_out)
 
     vectors = jnp.stack([sums_first, sums_last]).reshape(LAYERS * 3, n_dp, piece).transpose(1, 0, 2)
-    vectors = jnp.sum(lax.all_to_all(vectors, "dp", 0, 0, tiled=True), axis=0)
+    if groups == 1:
+        extra = jnp.pad(vectors, ((0, 0), (0, 16 - LAYERS * 3), (0, 0))).astype(bf16)
+        up_first = summed(*up_pair, down_first, extra=extra)
+        vectors = up_first[:, UP_ROWS : UP_ROWS + LAYERS * 3].astype(f32)
+    else:
+        up_first = summed(*up_pair, down_first)
+        vectors = lax.all_to_all(vectors, "dp", 0, 0, tiled=True)
+    vectors = jnp.sum(vectors, axis=0)
     vectors = (vectors + over(vectors)).reshape(LAYERS, 3, piece)
     sums = jnp.concatenate([bias_first, bias_last], axis=0)
     sums_qkv = sums[:, : 3 * WIDE].reshape(LAYERS, 3, 2, HEAD_DIM)

time: 789 us -> 762 us (0.966)
  Pallas kernels: 201 us -> 179 us
  waiting for transfers between devices: 388 us -> 368 us
  starting transfers between devices: 115 us -> 134 us
    ppermute x24, waiting for transfers between devices: 300 us -> 191 us  [along(): return lax.ppermute(x, 'dp', ring_pairs)]
    ppermute x13 -> x12, waiting for transfers between devices: 65.3 us -> 114 us  [over(): return lax.ppermute(x, 'tensor', [(0, 1), (1, 0)])]
    all_to_all x8 -> x7, waiting for transfers between devices: 10.1 us -> 45.2 us  [spread(): return lax.all_to_all(x, 'dp', 0, 0, axis_index_groups=inner, tiled=True)]
    pallas_call x8 -> x6, Pallas kernels: 48.7 us -> 27 us  [the longest x3 15.1 us: call_join(): pl.pallas_call(body, grid=(GROUP // MEMBERS,), in_specs=[pl.BlockSpec((ME...]
    ppermute x28, starting transfers between devices: 25 us -> 34.5 us  [across(): return lax.ppermute(x, 'dp', core_pairs)]
    all_to_all x8 -> x7, starting transfers between devices: 45.6 us -> 53.8 us  [spread(): return lax.all_to_all(x, 'dp', 0, 0, axis_index_groups=inner, tiled=True)]
  transfers between devices with their start and end apart: 74 -> 71, of which waited for: 32 -> 42; matrix products, arithmetic and copies ran while one was open for 7% -> 8% of each run, Pallas kernels for 20% -> 17%
where the time goes in v4:
time: 762 us; the launch traced here: 755 us
  waiting for transfers between devices  368 us (48%)
  Pallas kernels  179 us (23%)
  starting transfers between devices  134 us (18%)
  other arithmetic  49.8 us (7%)
  local copies, waits for them, and re-layouts  22.6 us (3%)
    ppermute x24, waiting for transfers between devices, along(): return lax.ppermute(x, 'dp', ring_pairs)  191 us
    ppermute x12, waiting for transfers between devices, over(): return lax.ppermute(x, 'tensor', [(0, 1), (1, 0)])  114 us
    pallas_call x3, Pallas kernels, call_pass(): pl.pallas_call(partial(layer_pass, mode), in_specs=[SMEM_SPEC] + [VMEM_SP...  88.9 us
    all_to_all x7, starting transfers between devices, spread(): return lax.all_to_all(x, 'dp', 0, 0, axis_index_groups=inner, tiled=True)  53.8 us
    all_to_all x7, waiting for transfers between devices, spread(): return lax.all_to_all(x, 'dp', 0, 0, axis_index_groups=inner, tiled=True)  45.2 us
    pallas_call x4, Pallas kernels, call_gradients(): pl.pallas_call(partial(gradient_slabs, own_rows, other_rows, with_sums, l...  37.9 us
    ppermute x28, starting transfers between devices, across(): return lax.ppermute(x, 'dp', core_pairs)  34.5 us
    ppermute x24, starting transfers between devices, along(): return lax.ppermute(x, 'dp', ring_pairs)  32.5 us
  transfers between devices with their start and end apart: 71, of which 42 were waited for; matrix products, arithmetic and copies ran while one was open for 8% of the time, Pallas kernels for 17%

profile of v4, /device:TPU:13, one launch (start us, length us, event | category | flops | bytes accessed | tf_op | source)
XLA Modules:
  0.0 755.3 jit_solution(17732501540063472368)
XLA Ops:
  4.8 4.0 pack_first.1
  8.8 6.7 all-to-all-start
  18.5 3.5 pack_down.1
  22.0 4.4 pack_both.1
  28.6 30.1 %all-to-all-done.own_ref = bf16[16,464,128]{2,1,0:T(8,128)(2,1)S(1)} async-done(((bf16[16,464,128]{2,1,0:T(8,128)(2,1)}), bf16[16,464,128]{2,1,0:T(8,128)(2,1)S(1)}, u32[]{:S(2)}, u32[]{:S(2)}) %all-to-all-start) | async-done | bytes 1900576 | tf_op jit(solution)/shard_map/all_to_all | solution.py:693
  58.7 14.0 %collective-permute-done.1.refs_11_.refs_18_ = bf16[2,128,2048]{2,1,0:T(8,128)(2,1)} collective-permute-done((bf16[2,128,2048]{2,1,0:T(8,128)(2,1)S(1)}, bf16[2,128,2048]{2,1,0:T(8,128)(2,1)}, u32[]{:S(2)}, u32[]{:S(2)}) %collective-permute-start.1) | collective-permute-done | bytes 1048608 | tf_op jit(solution)/shard_map/ppermute | solution.py:635
  72.8 6.2 all-to-all-start.1
  80.2 12.5 %collective-permute-done.2.refs_12_.refs_19_ = bf16[2,128,2048]{2,1,0:T(8,128)(2,1)} collective-permute-done((bf16[2,128,2048]{2,1,0:T(8,128)(2,1)}, bf16[2,128,2048]{2,1,0:T(8,128)(2,1)}, u32[]{:S(2)}, u32[]{:S(2)}) %collective-permute-start.2) | collective-permute-done | bytes 1048608 | tf_op jit(solution)/shard_map/ppermute | solution.py:635
  95.0 29.3 %collective-permute-done.3.refs_13_.refs_20_ = bf16[2,128,2048]{2,1,0:T(8,128)(2,1)} collective-permute-done((bf16[2,128,2048]{2,1,0:T(8,128)(2,1)}, bf16[2,128,2048]{2,1,0:T(8,128)(2,1)}, u32[]{:S(2)}, u32[]{:S(2)}) %collective-permute-start.3) | collective-permute-done | bytes 1048608 | tf_op jit(solution)/shard_map/ppermute | solution.py:635
  128.1 6.7 collective-permute-done.5.refs_17_.refs_24_
  134.9 9.1 %all-to-all-start.2 = ((bf16[16,768,128]{2,1,0:T(8,128)(2,1)}), bf16[16,768,128]{2,1,0:T(8,128)(2,1)}, u32[]{:S(2)}, u32[]{:S(2)}) async-start(bf16[16,768,128]{2,1,0:T(8,128)(2,1)} %pack_both.1), calls=%async_computation.2 | async-start | bytes 6291456 | tf_op jit(solution)/shard_map/all_to_all | solution.py:693
  151.3 3.0 multiply_sine_fusion
  154.5 2.7 concatenate.72.refs_5_
  157.2 2.7 concatenate.71.refs_4_
  162.3 4.8 join_up.1.refs_1_
  167.1 10.1 %collective-permute-done.8.other_ref = bf16[16,320,128]{2,1,0:T(8,128)(2,1)} collective-permute-done((bf16[16,320,128]{2,1,0:T(8,128)(2,1)S(1)}, bf16[16,320,128]{2,1,0:T(8,128)(2,1)}, u32[]{:S(2)}, u32[]{:S(2)}) %collective-permute-start.8) | collective-permute-done | bytes 1310752 | tf_op jit(solution)/shard_map/ppermute | solution.py:641
  177.3 4.2 join_down.1.refs_2_
  181.5 29.4 %pass_first.1 = (bf16[1024,2048]{1,0:T(8,128)(2,1)}, bf16[1024,384]{1,0:T(8,128)(2,1)}, f32[1024,512]{1,0:T(8,128)}, bf16[1024,640]{1,0:T(8,128)(2,1)}, bf16[64,...) custom-call(s32[1]{0:T(128)} %bitcast.refs_0_.core_ref, bf16[2048,896]{1,0:T(8,128)(2,1)} %join_up.1.refs_1_, ...), custom_call_target="tpu_custom_call" | custom-call | flops 19327352832 | bytes 20000000 | tf_op jit(solution)/shard_map/pass_first/pallas_call | solution.py:413
  214.1 2.9 collective-permute-done.14
  219.2 4.3 collective-permute-done.15
  227.4 6.0 collective-permute-done.16
  236.0 7.2 collective-permute-done.17
  246.7 7.5 collective-permute-done.18.moving_ref
  254.2 3.5 collective-permute-start.19
  259.6 2.5 forward_end.1
  266.2 29.3 %collective-permute-done.6.other_ref = bf16[16,768,128]{2,1,0:T(8,128)(2,1)} collective-permute-done((bf16[16,768,128]{2,1,0:T(8,128)(2,1)}, bf16[16,768,128]{2,1,0:T(8,128)(2,1)}, u32[]{:S(2)}, u32[]{:S(2)}) %collective-permute-start.6) | collective-permute-done | bytes 3145760 | tf_op jit(solution)/shard_map/ppermute | solution.py:641
  296.8 7.1 collective-permute-done.22.refs_10_
  306.8 5.4 collective-permute-done.23.refs_11_
  313.5 2.6 collective-permute-start.26
  317.6 4.3 collective-permute-start.28
  321.9 6.1 join_both.1
  329.0 35.2 %pass_middle.1 = (bf16[1024,2048]{1,0:T(8,128)(2,1)}, bf16[1024,2048]{1,0:T(8,128)(2,1)}, bf16[1024,640]{1,0:T(8,128)(2,1)}, bf16[1024,896]{1,0:T(8,128)(2,1)}, ...) custom-call(s32[1]{0:T(128)} %bitcast.refs_0_.core_ref, ...), custom_call_target="tpu_custom_call" | custom-call | flops 38654705664 | bytes 40000000 | tf_op jit(solution)/shard_map/pass_middle/pallas_call | solution.py:413
  365.3 3.3 collective-permute-done.30
  376.8 4.3 collective-permute-done.32
  383.7 8.8 %down_gradients.2 = (bf16[16,320,128]{2,1,0:T(8,128)(2,1)}, bf16[16,320,128]{2,1,0:T(8,128)(2,1)}) custom-call(s32[1]{0:T(128)} %bitcast.refs_0_.core_ref, bf16[1024,640]{1,0:T(8,128)(2,1)} %get-tuple-element.91.left_ref, bf16[1024,2048]{1,0:T(8,128)(2,1)} %get-tuple-element.92.rest_0_), custom_call_target="tpu_custom_call" | custom-call | flops 5368709120 | bytes 10747904 | tf_op jit(solution)/shard_map/down_gradients/pallas_call | solution.py:468
  393.7 10.0 %up_gradients.2 = (bf16[16,448,128]{2,1,0:T(8,128)(2,1)}, bf16[16,448,128]{2,1,0:T(8,128)(2,1)}, f32[1,896]{1,0:T(1,128)}) custom-call(s32[1]{0:T(128)} %bitcast.refs_0_.core_ref, bf16[1024,896]{1,0:T(8,128)(2,1)} %get-tuple-element.94.left_ref, bf16[1024,2048]{1,0:T(8,128)(2,1)} %get-tuple-element.95.rest_0_), custom_call_target="tpu_custom_call" | custom-call | flops 7516192768 | bytes 13369344 | tf_op jit(solution)/shard_map/up_gradients/pallas_call | solution.py:468
  406.7 16.0 %collective-permute-done.49 = bf16[16,320,128]{2,1,0:T(8,128)(2,1)} collective-permute-done((bf16[16,320,128]{2,1,0:T(8,128)(2,1)}, bf16[16,320,128]{2,1,0:T(8,128)(2,1)}, u32[]{:S(2)}, u32[]{:S(2)}) %collective-permute-start.49) | collective-permute-done | bytes 1310752 | tf_op jit(solution)/shard_map/ppermute | solution.py:641
  422.7 2.7 add_convert_fusion.3
  425.5 14.7 %all-to-all-start.3 = ((bf16[16,320,128]{2,1,0:T(8,128)(2,1)}), bf16[16,320,128]{2,1,0:T(8,128)(2,1)S(1)}, u32[]{:S(2)}, u32[]{:S(2)}) async-start(bf16[16,320,128]{2,1,0:T(8,128)(2,1)} %add_convert_fusion.3), calls=%async_computation.3 | async-start | bytes 2621440 | tf_op jit(solution)/shard_map/all_to_all | solution.py:693
  441.4 2.9 fusion.3
  445.6 36.1 %collective-permute-done.51 = bf16[16,448,128]{2,1,0:T(8,128)(2,1)S(1)} collective-permute-done((bf16[16,448,128]{2,1,0:T(8,128)(2,1)}, bf16[16,448,128]{2,1,0:T(8,128)(2,1)S(1)}, u32[]{:S(2)}, u32[]{:S(2)}) %collective-permute-start.51) | collective-permute-done | bytes 1835040 | tf_op jit(solution)/shard_map/ppermute | solution.py:641
  484.4 6.9 all-to-all-start.4
  494.2 3.0 backward_end.2
  501.4 35.6 %collective-permute-done.41.rest_1_.refs_10_ = bf16[128,2048]{1,0:T(8,128)(2,1)} collective-permute-done((bf16[128,2048]{1,0:T(8,128)(2,1)S(1)}, bf16[128,2048]{1,0:T(8,128)(2,1)}, u32[]{:S(2)}, u32[]{:S(2)}) %collective-permute-start.41) | collective-permute-done | bytes 524320 | tf_op jit(solution)/shard_map/ppermute | solution.py:635
  539.0 6.6 collective-permute-done.42.rest_2_.refs_11_
  549.0 5.2 collective-permute-done.43.rest_3_.refs_12_
  559.6 5.2 collective-permute-start.48
  566.7 8.9 %down_gradients.3 = (bf16[16,320,128]{2,1,0:T(8,128)(2,1)}, bf16[16,320,128]{2,1,0:T(8,128)(2,1)}) custom-call(s32[1]{0:T(128)} %bitcast.refs_0_.core_ref, bf16[1024,640]{1,0:T(8,128)(2,1)} %get-tuple-element.101.left_ref, bf16[128,2048]{1,0:T(8,128)(2,1)} %copy-done.25, bf16[128,2048]{1,0:T(8,128)(2,1)} %collective-permute-done.41.rest_1_.refs_10_, ...), custom_call_target="tpu_custom_call" | custom-call | flops 5368709120 | bytes 10747904 | tf_op jit(solution)/shard_map/down_gradients/pallas_call | solution.py:468
  576.9 24.3 %pass_last.1 = (bf16[1024,2048]{1,0:T(8,128)(2,1)}, bf16[1024,896]{1,0:T(8,128)(2,1)}, bf16[64,2048]{1,0:T(8,128)(2,1)}, bf16[448,2048]{1,0:T(8,128)(2,1)}, bf16[512,2048]{1,0:T(8,128)(2,1)}) custom-call(s32[1]{0:T(128)} %bitcast.refs_0_.core_ref, bf16[2048,896]{1,0:T(8,128)(2,1)} %join_up.1.refs_1_, bf16[640,2048]{1,0:T(8,128)(2,1)} %join_down.1.refs_2_, ...), custom_call_target="tpu_custom_call" | custom-call | flops 19327352832 | bytes 20000000 | tf_op jit(solution)/shard_map/pass_last/pallas_call | solution.py:413
  601.9 3.9 collective-permute-done.55
  607.2 5.1 all-to-all-start.5
  612.3 10.2 %up_gradients.3 = (bf16[16,448,128]{2,1,0:T(8,128)(2,1)}, bf16[16,448,128]{2,1,0:T(8,128)(2,1)}, f32[1,896]{1,0:T(1,128)}) custom-call(s32[1]{0:T(128)} %bitcast.refs_0_.core_ref, bf16[1024,896]{1,0:T(8,128)(2,1)} %get-tuple-element.109.left_ref, bf16[1024,2048]{1,0:T(8,128)(2,1)} %get-tuple-element.113.rest_0_), custom_call_target="tpu_custom_call" | custom-call | flops 7516192768 | bytes 13369344 | tf_op jit(solution)/shard_map/up_gradients/pallas_call | solution.py:468
  625.6 18.4 %collective-permute-done.53 = bf16[1,64,2048]{2,1,0:T(8,128)(2,1)S(1)} collective-permute-done((bf16[1,64,2048]{2,1,0:T(8,128)(2,1)S(1)}, bf16[1,64,2048]{2,1,0:T(8,128)(2,1)S(1)}, u32[]{:S(2)}, u32[]{:S(2)}) %collective-permute-start.53) | collective-permute-done | bytes 262176 | tf_op jit(solution)/shard_map/ppermute | solution.py:635
  648.4 5.3 collective-permute-done.54
  658.9 6.5 collective-permute-done.56
  668.6 6.5 collective-permute-done.57.moving_ref
  675.2 4.7 collective-permute-start.58
  679.9 8.7 %collective-permute-done.61 = bf16[16,448,128]{2,1,0:T(8,128)(2,1)} collective-permute-done((bf16[16,448,128]{2,1,0:T(8,128)(2,1)}, bf16[16,448,128]{2,1,0:T(8,128)(2,1)}, u32[]{:S(2)}, u32[]{:S(2)}) %collective-permute-start.61) | collective-permute-done | bytes 1835040 | tf_op jit(solution)/shard_map/ppermute | solution.py:641
  691.3 3.0 backward_end.3
  696.5 5.2 all-to-all-start.6
  711.0 9.3 %collective-permute-done.39 = bf16[128,2048]{1,0:T(8,128)(2,1)} collective-permute-done((bf16[128,2048]{1,0:T(8,128)(2,1)S(1)}, bf16[128,2048]{1,0:T(8,128)(2,1)}, u32[]{:S(2)}, u32[]{:S(2)}) %collective-permute-start.39) | collective-permute-done | bytes 524320 | tf_op jit(solution)/shard_map/ppermute | solution.py:641
  722.2 7.2 spread_gradients.2
  730.9 14.0 %all-to-all-done.6.up_ref = bf16[16,464,128]{2,1,0:T(8,128)(2,1)S(1)} async-done(((bf16[16,464,128]{2,1,0:T(8,128)(2,1)}), bf16[16,464,128]{2,1,0:T(8,128)(2,1)S(1)}, u32[]{:S(2)}, u32[]{:S(2)}) %all-to-all-start.6) | async-done | bytes 1900576 | tf_op jit(solution)/shard_map/all_to_all | solution.py:693
  747.3 7.3 spread_gradients.3
  (306 shorter events, 136.2 us)
Async XLA Ops:
  8.8 49.9 %all-to-all-start = ((bf16[16,464,128]{2,1,0:T(8,128)(2,1)}), bf16[16,464,128]{2,1,0:T(8,128)(2,1)S(1)}, u32[]{:S(2)}, u32[]{:S(2)}) async-start(bf16[16,464,128]{2,1,0:T(8,128)(2,1)} %pack_first.1), calls=%async_computation | async-start | bytes 3801088 | tf_op jit(solution)/shard_map/all_to_all | solution.py:693
  16.6 10.5 %collective-permute-start = (bf16[2,128,2048]{2,1,0:T(8,128)(2,1)}, bf16[2,128,2048]{2,1,0:T(8,128)(2,1)}, u32[]{:S(2)}, u32[]{:S(2)}) collective-permute-start(bf16[2,128,2048]{2,1,0:T(8,128)(2,1)} %pad_maximum_fusion), channel_id=1, source_target_pairs={{0,2},{2,0},{4,6},{6,4},{8,10},{10,8},{12,14},{14,12},{16,18},{18,... | collective-permute-start | bytes 3145736 | tf_op jit(solution)/shard_map/ppermute | solution.py:638
  58.7 14.0 %collective-permute-start.1 = (bf16[2,128,2048]{2,1,0:T(8,128)(2,1)S(1)}, bf16[2,128,2048]{2,1,0:T(8,128)(2,1)}, u32[]{:S(2)}, u32[]{:S(2)}) collective-permute-start(bf16[2,128,2048]{2,1,0:T(8,128)(2,1)S(1)} %select_multiply_fusion.refs_10_.refs_17_), channel_id=1, source_target_pairs={{0,8},{2,6},{8,16},{10,2},{16,24},{18,10},{24,28},{26,18},{28,20},... | collective-permute-start | bytes 3145736 | tf_op jit(solution)/shard_map/ppermute | solution.py:635
  72.8 20.0 %collective-permute-start.2 = (bf16[2,128,2048]{2,1,0:T(8,128)(2,1)}, bf16[2,128,2048]{2,1,0:T(8,128)(2,1)}, u32[]{:S(2)}, u32[]{:S(2)}) collective-permute-start(bf16[2,128,2048]{2,1,0:T(8,128)(2,1)} %collective-permute-done.1.refs_11_.refs_18_), channel_id=1, source_target_pairs={{0,8},{2,6},{8,16},{10,2},{16,24},{18,10},{24,28},{26,18},{28,20},... | collective-permute-start | bytes 3145736 | tf_op jit(solution)/shard_map/ppermute | solution.py:635
  72.8 55.4 %all-to-all-start.1 = ((bf16[16,320,128]{2,1,0:T(8,128)(2,1)}), bf16[16,320,128]{2,1,0:T(8,128)(2,1)S(1)}, u32[]{:S(2)}, u32[]{:S(2)}) async-start(bf16[16,320,128]{2,1,0:T(8,128)(2,1)} %pack_down.1), calls=%async_computation.1 | async-start | bytes 2621440 | tf_op jit(solution)/shard_map/all_to_all | solution.py:693
  79.0 47.2 %collective-permute-start.4 = (bf16[16,464,128]{2,1,0:T(8,128)(2,1)S(1)}, bf16[16,464,128]{2,1,0:T(8,128)(2,1)}, u32[]{:S(2)}, u32[]{:S(2)}) collective-permute-start(bf16[16,464,128]{2,1,0:T(8,128)(2,1)S(1)} %all-to-all-done.own_ref), channel_id=1, source_target_pairs={{0,1},{1,0},{2,3},{3,2},{4,5},{5,4},{6,7},{7,6},{8,9},{9,8},{10,11... | collective-permute-start | bytes 5701640 | tf_op jit(solution)/shard_map/ppermute | solution.py:641
  92.7 31.5 %collective-permute-start.3 = (bf16[2,128,2048]{2,1,0:T(8,128)(2,1)}, bf16[2,128,2048]{2,1,0:T(8,128)(2,1)}, u32[]{:S(2)}, u32[]{:S(2)}) collective-permute-start(bf16[2,128,2048]{2,1,0:T(8,128)(2,1)} %collective-permute-done.2.refs_12_.refs_19_), channel_id=1, source_target_pairs={{0,8},{2,6},{8,16},{10,2},{16,24},{18,10},{24,28},{26,18},{28,20},... | collective-permute-start | bytes 3145736 | tf_op jit(solution)/shard_map/ppermute | solution.py:635
  126.2 8.7 %collective-permute-start.5 = (bf16[2,64,2048]{2,1,0:T(8,128)(2,1)}, bf16[2,64,2048]{2,1,0:T(8,128)(2,1)}, u32[]{:S(2)}, u32[]{:S(2)}) collective-permute-start(bf16[2,64,2048]{2,1,0:T(8,128)(2,1)} %constant_dynamic-slice_fusion.4), channel_id=1, source_target_pairs={{0,8},{2,6},{8,16},{10,2},{16,24},{18,10},{24,28},{26,18},{28,20},... | collective-permute-start | bytes 1572872 | tf_op jit(solution)/shard_map/ppermute | solution.py:635
  134.9 79.1 %all-to-all-start.2 = ((bf16[16,768,128]{2,1,0:T(8,128)(2,1)}), bf16[16,768,128]{2,1,0:T(8,128)(2,1)}, u32[]{:S(2)}, u32[]{:S(2)}) async-start(bf16[16,768,128]{2,1,0:T(8,128)(2,1)} %pack_both.1), calls=%async_computation.2 | async-start | bytes 6291456 | tf_op jit(solution)/shard_map/all_to_all | solution.py:693
  147.9 29.4 %collective-permute-start.8 = (bf16[16,320,128]{2,1,0:T(8,128)(2,1)S(1)}, bf16[16,320,128]{2,1,0:T(8,128)(2,1)}, u32[]{:S(2)}, u32[]{:S(2)}) collective-permute-start(bf16[16,320,128]{2,1,0:T(8,128)(2,1)S(1)} %all-to-all-done.1.own_ref), channel_id=1, source_target_pairs={{0,1},{1,0},{2,3},{3,2},{4,5},{5,4},{6,7},{7,6},{8,9},{9,8},{10,11... | collective-permute-start | bytes 3932168 | tf_op jit(solution)/shard_map/ppermute | solution.py:641
  149.4 32.1 %collective-permute-start.9 = (bf16[2,128,2048]{2,1,0:T(8,128)(2,1)}, bf16[2,128,2048]{2,1,0:T(8,128)(2,1)}, u32[]{:S(2)}, u32[]{:S(2)}) collective-permute-start(bf16[2,128,2048]{2,1,0:T(8,128)(2,1)} %collective-permute-done.1.refs_11_.refs_18_), channel_id=1, source_target_pairs={{0,2},{2,0},{4,6},{6,4},{8,10},{10,8},{12,14},{14,12},{16,18},{18,... | collective-permute-start | bytes 3145736 | tf_op jit(solution)/shard_map/ppermute | solution.py:638
  150.8 30.7 %collective-permute-start.10 = (bf16[2,128,2048]{2,1,0:T(8,128)(2,1)}, bf16[2,128,2048]{2,1,0:T(8,128)(2,1)}, u32[]{:S(2)}, u32[]{:S(2)}) collective-permute-start(bf16[2,128,2048]{2,1,0:T(8,128)(2,1)} %collective-permute-done.2.refs_12_.refs_19_), channel_id=1, source_target_pairs={{0,2},{2,0},{4,6},{6,4},{8,10},{10,8},{12,14},{14,12},{16,18},{18,... | collective-permute-start | bytes 3145736 | tf_op jit(solution)/shard_map/ppermute | solution.py:638
  150.8 30.7 %collective-permute-start.11 = (bf16[2,128,2048]{2,1,0:T(8,128)(2,1)}, bf16[2,128,2048]{2,1,0:T(8,128)(2,1)}, u32[]{:S(2)}, u32[]{:S(2)}) collective-permute-start(bf16[2,128,2048]{2,1,0:T(8,128)(2,1)} %collective-permute-done.3.refs_13_.refs_20_), channel_id=1, source_target_pairs={{0,2},{2,0},{4,6},{6,4},{8,10},{10,8},{12,14},{14,12},{16,18},{18,... | collective-permute-start | bytes 3145736 | tf_op jit(solution)/shard_map/ppermute | solution.py:638
  154.3 27.1 %collective-permute-start.12 = (bf16[2,64,2048]{2,1,0:T(8,128)(2,1)}, bf16[2,64,2048]{2,1,0:T(8,128)(2,1)}, u32[]{:S(2)}, u32[]{:S(2)}) collective-permute-start(bf16[2,64,2048]{2,1,0:T(8,128)(2,1)} %collective-permute-done.5.refs_17_.refs_24_), channel_id=1, source_target_pairs={{0,2},{2,0},{4,6},{6,4},{8,10},{10,8},{12,14},{14,12},{16,18},{18,... | collective-permute-start | bytes 1572872 | tf_op jit(solution)/shard_map/ppermute | solution.py:638
  210.9 8.3 %collective-permute-start.13 = (bf16[448,2048]{1,0:T(8,128)(2,1)}, bf16[448,2048]{1,0:T(8,128)(2,1)}, u32[]{:S(2)}, u32[]{:S(2)}) collective-permute-start(bf16[448,2048]{1,0:T(8,128)(2,1)} %get-tuple-element.80), channel_id=1, source_target_pairs={{0,2},{2,0},{4,6},{6,4},{8,10},{10,8},{12,14},{14,12},{16,18},{18,... | collective-permute-start | bytes 5505032 | tf_op jit(solution)/shard_map/ppermute | solution.py:638
  213.9 3.0 collective-permute-start.14
  218.0 5.6 collective-permute-start.15
  225.0 8.5 %collective-permute-start.16 = (bf16[1,128,2048]{2,1,0:T(8,128)(2,1)S(1)}, bf16[1,128,2048]{2,1,0:T(8,128)(2,1)S(1)}, u32[]{:S(2)}, u32[]{:S(2)}) collective-permute-start(bf16[1,128,2048]{2,1,0:T(8,128)(2,1)S(1)} %fusion.9), channel_id=1, source_target_pairs={{0,8},{2,6},{8,16},{10,2},{16,24},{18,10},{24,28},{26,18},{28,20},... | collective-permute-start | bytes 1572872 | tf_op jit(solution)/shard_map/ppermute | solution.py:635
  226.2 69.4 %collective-permute-start.6 = (bf16[16,768,128]{2,1,0:T(8,128)(2,1)}, bf16[16,768,128]{2,1,0:T(8,128)(2,1)}, u32[]{:S(2)}, u32[]{:S(2)}) collective-permute-start(bf16[16,768,128]{2,1,0:T(8,128)(2,1)} %all-to-all-done.2.own_ref), channel_id=1, source_target_pairs={{0,1},{1,0},{2,3},{3,2},{4,5},{5,4},{6,7},{7,6},{8,9},{9,8},{10,11... | collective-permute-start | bytes 9437192 | tf_op jit(solution)/shard_map/ppermute | solution.py:641
  234.8 8.5 %collective-permute-start.17 = (bf16[1,128,2048]{2,1,0:T(8,128)(2,1)S(1)}, bf16[1,128,2048]{2,1,0:T(8,128)(2,1)S(1)}, u32[]{:S(2)}, u32[]{:S(2)}) collective-permute-start(bf16[1,128,2048]{2,1,0:T(8,128)(2,1)S(1)} %fusion.8), channel_id=1, source_target_pairs={{0,8},{2,6},{8,16},{10,2},{16,24},{18,10},{24,28},{26,18},{28,20},... | collective-permute-start | bytes 1572872 | tf_op jit(solution)/shard_map/ppermute | solution.py:635
  245.3 8.9 %collective-permute-start.18 = (bf16[1,128,2048]{2,1,0:T(8,128)(2,1)}, bf16[1,128,2048]{2,1,0:T(8,128)(2,1)S(1)}, u32[]{:S(2)}, u32[]{:S(2)}) collective-permute-start(bf16[1,128,2048]{2,1,0:T(8,128)(2,1)} %fusion.7), channel_id=1, source_target_pairs={{0,8},{2,6},{8,16},{10,2},{16,24},{18,10},{24,28},{26,18},{28,20},... | collective-permute-start | bytes 1572872 | tf_op jit(solution)/shard_map/ppermute | solution.py:635
  254.2 4.7 collective-permute-start.19
  265.0 30.6 %collective-permute-start.21 = (bf16[128,2048]{1,0:T(8,128)(2,1)S(1)}, bf16[128,2048]{1,0:T(8,128)(2,1)S(1)}, u32[]{:S(2)}, u32[]{:S(2)}) collective-permute-start(bf16[128,2048]{1,0:T(8,128)(2,1)S(1)} %maximum_select_fusion.2.refs_8_), channel_id=1, source_target_pairs={{0,8},{2,6},{8,16},{10,2},{16,24},{18,10},{24,28},{26,18},{28,20},... | collective-permute-start | bytes 1572872 | tf_op jit(solution)/shard_map/ppermute | solution.py:635
  295.6 8.3 %collective-permute-start.22 = (bf16[128,2048]{1,0:T(8,128)(2,1)S(1)}, bf16[128,2048]{1,0:T(8,128)(2,1)S(1)}, u32[]{:S(2)}, u32[]{:S(2)}) collective-permute-start(bf16[128,2048]{1,0:T(8,128)(2,1)S(1)} %collective-permute-done.21.refs_9_), channel_id=1, source_target_pairs={{0,8},{2,6},{8,16},{10,2},{16,24},{18,10},{24,28},{26,18},{28,20},... | collective-permute-start | bytes 1572872 | tf_op jit(solution)/shard_map/ppermute | solution.py:635
  303.9 8.3 %collective-permute-start.23 = (bf16[128,2048]{1,0:T(8,128)(2,1)S(1)}, bf16[128,2048]{1,0:T(8,128)(2,1)S(1)}, u32[]{:S(2)}, u32[]{:S(2)}) collective-permute-start(bf16[128,2048]{1,0:T(8,128)(2,1)S(1)} %collective-permute-done.22.refs_10_), channel_id=1, source_target_pairs={{0,8},{2,6},{8,16},{10,2},{16,24},{18,10},{24,28},{26,18},{28,20},... | collective-permute-start | bytes 1572872 | tf_op jit(solution)/shard_map/ppermute | solution.py:635
  305.1 22.9 %collective-permute-start.24 = (bf16[128,2048]{1,0:T(8,128)(2,1)S(1)}, bf16[128,2048]{1,0:T(8,128)(2,1)S(1)}, u32[]{:S(2)}, u32[]{:S(2)}) collective-permute-start(bf16[128,2048]{1,0:T(8,128)(2,1)S(1)} %collective-permute-done.21.refs_9_), channel_id=1, source_target_pairs={{0,2},{2,0},{4,6},{6,4},{8,10},{10,8},{12,14},{14,12},{16,18},{18,... | collective-permute-start | bytes 1572872 | tf_op jit(solution)/shard_map/ppermute | solution.py:638
  306.8 21.2 %collective-permute-start.25 = (bf16[128,2048]{1,0:T(8,128)(2,1)S(1)}, bf16[128,2048]{1,0:T(8,128)(2,1)S(1)}, u32[]{:S(2)}, u32[]{:S(2)}) collective-permute-start(bf16[128,2048]{1,0:T(8,128)(2,1)S(1)} %collective-permute-done.22.refs_10_), channel_id=1, source_target_pairs={{0,2},{2,0},{4,6},{6,4},{8,10},{10,8},{12,14},{14,12},{16,18},{18,... | collective-permute-start | bytes 1572872 | tf_op jit(solution)/shard_map/ppermute | solution.py:638
  312.3 5.3 collective-permute-start.27
  313.5 14.6 %collective-permute-start.26 = (bf16[128,2048]{1,0:T(8,128)(2,1)S(1)}, bf16[128,2048]{1,0:T(8,128)(2,1)}, u32[]{:S(2)}, u32[]{:S(2)}) collective-permute-start(bf16[128,2048]{1,0:T(8,128)(2,1)S(1)} %collective-permute-done.23.refs_11_), channel_id=1, source_target_pairs={{0,2},{2,0},{4,6},{6,4},{8,10},{10,8},{12,14},{14,12},{16,18},{18,... | collective-permute-start | bytes 1572872 | tf_op jit(solution)/shard_map/ppermute | solution.py:638
  317.6 10.5 %collective-permute-start.28 = (bf16[64,2048]{1,0:T(8,128)(2,1)S(1)}, bf16[64,2048]{1,0:T(8,128)(2,1)}, u32[]{:S(2)}, u32[]{:S(2)}) collective-permute-start(bf16[64,2048]{1,0:T(8,128)(2,1)S(1)} %collective-permute-done.27.refs_15_), channel_id=1, source_target_pairs={{0,2},{2,0},{4,6},{6,4},{8,10},{10,8},{12,14},{14,12},{16,18},{18,... | collective-permute-start | bytes 786440 | tf_op jit(solution)/shard_map/ppermute | solution.py:638
  364.3 9.8 %collective-permute-start.33 = (bf16[448,2048]{1,0:T(8,128)(2,1)}, bf16[448,2048]{1,0:T(8,128)(2,1)S(1)}, u32[]{:S(2)}, u32[]{:S(2)}) collective-permute-start(bf16[448,2048]{1,0:T(8,128)(2,1)} %get-tuple-element.90), channel_id=1, source_target_pairs={{0,2},{2,0},{4,6},{6,4},{8,10},{10,8},{12,14},{14,12},{16,18},{18,... | collective-permute-start | bytes 5505032 | tf_op jit(solution)/shard_map/ppermute | solution.py:638
  364.4 4.3 collective-permute-start.30
  364.8 10.4 %collective-permute-start.29 = (bf16[448,2048]{1,0:T(8,128)(2,1)}, bf16[448,2048]{1,0:T(8,128)(2,1)S(1)}, u32[]{:S(2)}, u32[]{:S(2)}) collective-permute-start(bf16[448,2048]{1,0:T(8,128)(2,1)} %get-tuple-element.86), channel_id=1, source_target_pairs={{0,2},{2,0},{4,6},{6,4},{8,10},{10,8},{12,14},{14,12},{16,18},{18,... | collective-permute-start | bytes 5505032 | tf_op jit(solution)/shard_map/ppermute | solution.py:638
  364.9 6.8 collective-permute-start.31
  372.8 8.4 %collective-permute-start.32 = (bf16[2,64,2048]{2,1,0:T(8,128)(2,1)S(1)}, bf16[2,64,2048]{2,1,0:T(8,128)(2,1)S(1)}, u32[]{:S(2)}, u32[]{:S(2)}) collective-permute-start(bf16[2,64,2048]{2,1,0:T(8,128)(2,1)S(1)} %pad_maximum_fusion.1), channel_id=1, source_target_pairs={{0,8},{2,6},{8,16},{10,2},{16,24},{18,10},{24,28},{26,18},{28,20},... | collective-permute-start | bytes 1572872 | tf_op jit(solution)/shard_map/ppermute | solution.py:635
  382.5 21.2 %collective-permute-start.34 = (bf16[2,128,2048]{2,1,0:T(8,128)(2,1)}, bf16[2,128,2048]{2,1,0:T(8,128)(2,1)}, u32[]{:S(2)}, u32[]{:S(2)}) collective-permute-start(bf16[2,128,2048]{2,1,0:T(8,128)(2,1)} %fusion.1), channel_id=1, source_target_pairs={{0,8},{2,6},{8,16},{10,2},{16,24},{18,10},{24,28},{26,18},{28,20},... | collective-permute-start | bytes 3145736 | tf_op jit(solution)/shard_map/ppermute | solution.py:635
  392.5 30.3 %collective-permute-start.49 = (bf16[16,320,128]{2,1,0:T(8,128)(2,1)}, bf16[16,320,128]{2,1,0:T(8,128)(2,1)}, u32[]{:S(2)}, u32[]{:S(2)}) collective-permute-start(bf16[16,320,128]{2,1,0:T(8,128)(2,1)} %get-tuple-element.104), channel_id=1, source_target_pairs={{0,1},{1,0},{2,3},{3,2},{4,5},{5,4},{6,7},{7,6},{8,9},{9,8},{10,11... | collective-permute-start | bytes 3932168 | tf_op jit(solution)/shard_map/ppermute | solution.py:641
  406.4 35.0 %collective-permute-start.35 = (bf16[2,128,2048]{2,1,0:T(8,128)(2,1)}, bf16[2,128,2048]{2,1,0:T(8,128)(2,1)}, u32[]{:S(2)}, u32[]{:S(2)}) collective-permute-start(bf16[2,128,2048]{2,1,0:T(8,128)(2,1)} %fusion.2), channel_id=1, source_target_pairs={{0,8},{2,6},{8,16},{10,2},{16,24},{18,10},{24,28},{26,18},{28,20},... | collective-permute-start | bytes 3145736 | tf_op jit(solution)/shard_map/ppermute | solution.py:635
  425.5 57.9 %all-to-all-start.3 = ((bf16[16,320,128]{2,1,0:T(8,128)(2,1)}), bf16[16,320,128]{2,1,0:T(8,128)(2,1)S(1)}, u32[]{:S(2)}, u32[]{:S(2)}) async-start(bf16[16,320,128]{2,1,0:T(8,128)(2,1)} %add_convert_fusion.3), calls=%async_computation.3 | async-start | bytes 2621440 | tf_op jit(solution)/shard_map/all_to_all | solution.py:693
  440.2 41.5 %collective-permute-start.51 = (bf16[16,448,128]{2,1,0:T(8,128)(2,1)}, bf16[16,448,128]{2,1,0:T(8,128)(2,1)S(1)}, u32[]{:S(2)}, u32[]{:S(2)}) collective-permute-start(bf16[16,448,128]{2,1,0:T(8,128)(2,1)} %get-tuple-element.111), channel_id=1, source_target_pairs={{0,1},{1,0},{2,3},{3,2},{4,5},{5,4},{6,7},{7,6},{8,9},{9,8},{10,11... | collective-permute-start | bytes 5505032 | tf_op jit(solution)/shard_map/ppermute | solution.py:641
  444.4 46.9 %collective-permute-start.36 = (bf16[2,128,2048]{2,1,0:T(8,128)(2,1)}, bf16[2,128,2048]{2,1,0:T(8,128)(2,1)S(1)}, u32[]{:S(2)}, u32[]{:S(2)}) collective-permute-start(bf16[2,128,2048]{2,1,0:T(8,128)(2,1)} %fusion.3), channel_id=1, source_target_pairs={{0,8},{2,6},{8,16},{10,2},{16,24},{18,10},{24,28},{26,18},{28,20},... | collective-permute-start | bytes 3145736 | tf_op jit(solution)/shard_map/ppermute | solution.py:635
  484.4 80.4 %all-to-all-start.4 = ((bf16[16,448,128]{2,1,0:T(8,128)(2,1)}), bf16[16,448,128]{2,1,0:T(8,128)(2,1)S(1)}, u32[]{:S(2)}, u32[]{:S(2)}) async-start(bf16[16,448,128]{2,1,0:T(8,128)(2,1)} %add_convert_fusion.1), calls=%async_computation.4 | async-start | bytes 3670016 | tf_op jit(solution)/shard_map/all_to_all | solution.py:693
  500.1 36.9 %collective-permute-start.41 = (bf16[128,2048]{1,0:T(8,128)(2,1)S(1)}, bf16[128,2048]{1,0:T(8,128)(2,1)}, u32[]{:S(2)}, u32[]{:S(2)}) collective-permute-start(bf16[128,2048]{1,0:T(8,128)(2,1)S(1)} %maximum_select_fusion.4.rest_0_.refs_9_), channel_id=1, source_target_pairs={{0,8},{2,6},{8,16},{10,2},{16,24},{18,10},{24,28},{26,18},{28,20},... | collective-permute-start | bytes 1572872 | tf_op jit(solution)/shard_map/ppermute | solution.py:635
  537.0 8.6 %collective-permute-start.42 = (bf16[128,2048]{1,0:T(8,128)(2,1)}, bf16[128,2048]{1,0:T(8,128)(2,1)}, u32[]{:S(2)}, u32[]{:S(2)}) collective-permute-start(bf16[128,2048]{1,0:T(8,128)(2,1)} %collective-permute-done.41.rest_1_.refs_10_), channel_id=1, source_target_pairs={{0,8},{2,6},{8,16},{10,2},{16,24},{18,10},{24,28},{26,18},{28,20},... | collective-permute-start | bytes 1572872 | tf_op jit(solution)/shard_map/ppermute | solution.py:635
  545.7 8.5 %collective-permute-start.43 = (bf16[128,2048]{1,0:T(8,128)(2,1)}, bf16[128,2048]{1,0:T(8,128)(2,1)S(1)}, u32[]{:S(2)}, u32[]{:S(2)}) collective-permute-start(bf16[128,2048]{1,0:T(8,128)(2,1)} %collective-permute-done.42.rest_2_.refs_11_), channel_id=1, source_target_pairs={{0,8},{2,6},{8,16},{10,2},{16,24},{18,10},{24,28},{26,18},{28,20},... | collective-permute-start | bytes 1572872 | tf_op jit(solution)/shard_map/ppermute | solution.py:635
  547.7 17.2 %collective-permute-start.44 = (bf16[128,2048]{1,0:T(8,128)(2,1)}, bf16[128,2048]{1,0:T(8,128)(2,1)}, u32[]{:S(2)}, u32[]{:S(2)}) collective-permute-start(bf16[128,2048]{1,0:T(8,128)(2,1)} %collective-permute-done.41.rest_1_.refs_10_), channel_id=1, source_target_pairs={{0,2},{2,0},{4,6},{6,4},{8,10},{10,8},{12,14},{14,12},{16,18},{18,... | collective-permute-start | bytes 1572872 | tf_op jit(solution)/shard_map/ppermute | solution.py:638
  549.0 15.9 %collective-permute-start.45 = (bf16[128,2048]{1,0:T(8,128)(2,1)}, bf16[128,2048]{1,0:T(8,128)(2,1)}, u32[]{:S(2)}, u32[]{:S(2)}) collective-permute-start(bf16[128,2048]{1,0:T(8,128)(2,1)} %collective-permute-done.42.rest_2_.refs_11_), channel_id=1, source_target_pairs={{0,2},{2,0},{4,6},{6,4},{8,10},{10,8},{12,14},{14,12},{16,18},{18,... | collective-permute-start | bytes 1572872 | tf_op jit(solution)/shard_map/ppermute | solution.py:638
  554.2 5.4 collective-permute-start.47
  556.3 9.7 %collective-permute-start.46 = (bf16[128,2048]{1,0:T(8,128)(2,1)S(1)}, bf16[128,2048]{1,0:T(8,128)(2,1)}, u32[]{:S(2)}, u32[]{:S(2)}) collective-permute-start(bf16[128,2048]{1,0:T(8,128)(2,1)S(1)} %collective-permute-done.43.rest_3_.refs_12_), channel_id=1, source_target_pairs={{0,2},{2,0},{4,6},{6,4},{8,10},{10,8},{12,14},{14,12},{16,18},{18,... | collective-permute-start | bytes 1572872 | tf_op jit(solution)/shard_map/ppermute | solution.py:638
  559.6 6.4 collective-permute-start.48
  575.6 30.2 %collective-permute-start.55 = (bf16[16,320,128]{2,1,0:T(8,128)(2,1)}, bf16[16,320,128]{2,1,0:T(8,128)(2,1)S(1)}, u32[]{:S(2)}, u32[]{:S(2)}) collective-permute-start(bf16[16,320,128]{2,1,0:T(8,128)(2,1)} %get-tuple-element.116), channel_id=1, source_target_pairs={{0,1},{1,0},{2,3},{3,2},{4,5},{5,4},{6,7},{7,6},{8,9},{9,8},{10,11... | collective-permute-start | bytes 3932168 | tf_op jit(solution)/shard_map/ppermute | solution.py:641
  601.2 42.8 %collective-permute-start.50 = (bf16[448,2048]{1,0:T(8,128)(2,1)}, bf16[448,2048]{1,0:T(8,128)(2,1)}, u32[]{:S(2)}, u32[]{:S(2)}) collective-permute-start(bf16[448,2048]{1,0:T(8,128)(2,1)} %get-tuple-element.107), channel_id=1, source_target_pairs={{0,2},{2,0},{4,6},{6,4},{8,10},{10,8},{12,14},{14,12},{16,18},{18,... | collective-permute-start | bytes 5505032 | tf_op jit(solution)/shard_map/ppermute | solution.py:638
  607.2 47.6 %all-to-all-start.5 = ((bf16[16,320,128]{2,1,0:T(8,128)(2,1)}), bf16[16,320,128]{2,1,0:T(8,128)(2,1)S(1)}, u32[]{:S(2)}, u32[]{:S(2)}) async-start(bf16[16,320,128]{2,1,0:T(8,128)(2,1)} %add_convert_fusion.2), calls=%async_computation.5 | async-start | bytes 2621440 | tf_op jit(solution)/shard_map/all_to_all | solution.py:693
  624.3 19.7 %collective-permute-start.53 = (bf16[1,64,2048]{2,1,0:T(8,128)(2,1)S(1)}, bf16[1,64,2048]{2,1,0:T(8,128)(2,1)S(1)}, u32[]{:S(2)}, u32[]{:S(2)}) collective-permute-start(bf16[1,64,2048]{2,1,0:T(8,128)(2,1)S(1)} %fusion.18), channel_id=1, source_target_pairs={{0,8},{2,6},{8,16},{10,2},{16,24},{18,10},{24,28},{26,18},{28,20},... | collective-permute-start | bytes 786440 | tf_op jit(solution)/shard_map/ppermute | solution.py:635
  645.3 8.5 %collective-permute-start.54 = (bf16[1,128,2048]{2,1,0:T(8,128)(2,1)S(1)}, bf16[1,128,2048]{2,1,0:T(8,128)(2,1)S(1)}, u32[]{:S(2)}, u32[]{:S(2)}) collective-permute-start(bf16[1,128,2048]{2,1,0:T(8,128)(2,1)S(1)} %fusion.10), channel_id=1, source_target_pairs={{0,8},{2,6},{8,16},{10,2},{16,24},{18,10},{24,28},{26,18},{28,20},... | collective-permute-start | bytes 1572872 | tf_op jit(solution)/shard_map/ppermute | solution.py:635
  647.2 41.3 %collective-permute-start.61 = (bf16[16,448,128]{2,1,0:T(8,128)(2,1)}, bf16[16,448,128]{2,1,0:T(8,128)(2,1)}, u32[]{:S(2)}, u32[]{:S(2)}) collective-permute-start(bf16[16,448,128]{2,1,0:T(8,128)(2,1)} %get-tuple-element.121), channel_id=1, source_target_pairs={{0,1},{1,0},{2,3},{3,2},{4,5},{5,4},{6,7},{7,6},{8,9},{9,8},{10,11... | collective-permute-start | bytes 5505032 | tf_op jit(solution)/shard_map/ppermute | solution.py:641
  656.9 8.5 %collective-permute-start.56 = (bf16[1,128,2048]{2,1,0:T(8,128)(2,1)S(1)}, bf16[1,128,2048]{2,1,0:T(8,128)(2,1)S(1)}, u32[]{:S(2)}, u32[]{:S(2)}) collective-permute-start(bf16[1,128,2048]{2,1,0:T(8,128)(2,1)S(1)} %fusion.6), channel_id=1, source_target_pairs={{0,8},{2,6},{8,16},{10,2},{16,24},{18,10},{24,28},{26,18},{28,20},... | collective-permute-start | bytes 1572872 | tf_op jit(solution)/shard_map/ppermute | solution.py:635
  666.7 8.5 %collective-permute-start.57 = (bf16[1,128,2048]{2,1,0:T(8,128)(2,1)S(1)}, bf16[1,128,2048]{2,1,0:T(8,128)(2,1)S(1)}, u32[]{:S(2)}, u32[]{:S(2)}) collective-permute-start(bf16[1,128,2048]{2,1,0:T(8,128)(2,1)S(1)} %fusion.5), channel_id=1, source_target_pairs={{0,8},{2,6},{8,16},{10,2},{16,24},{18,10},{24,28},{26,18},{28,20},... | collective-permute-start | bytes 1572872 | tf_op jit(solution)/shard_map/ppermute | solution.py:635
  675.2 15.4 %collective-permute-start.58 = (bf16[1,64,2048]{2,1,0:T(8,128)(2,1)S(1)}, bf16[1,64,2048]{2,1,0:T(8,128)(2,1)S(1)}, u32[]{:S(2)}, u32[]{:S(2)}) collective-permute-start(bf16[1,64,2048]{2,1,0:T(8,128)(2,1)S(1)} %constant_dynamic-slice_fusion.5), channel_id=1, source_target_pairs={{0,2},{2,0},{4,6},{6,4},{8,10},{10,8},{12,14},{14,12},{16,18},{18,... | collective-permute-start | bytes 786440 | tf_op jit(solution)/shard_map/ppermute | solution.py:638
  696.5 48.4 %all-to-all-start.6 = ((bf16[16,464,128]{2,1,0:T(8,128)(2,1)}), bf16[16,464,128]{2,1,0:T(8,128)(2,1)S(1)}, u32[]{:S(2)}, u32[]{:S(2)}) async-start(bf16[16,464,128]{2,1,0:T(8,128)(2,1)} %fusion.4), calls=%async_computation.6 | async-start | bytes 3801088 | tf_op jit(solution)/shard_map/all_to_all | solution.py:693
  707.0 13.3 %collective-permute-start.39 = (bf16[128,2048]{1,0:T(8,128)(2,1)S(1)}, bf16[128,2048]{1,0:T(8,128)(2,1)}, u32[]{:S(2)}, u32[]{:S(2)}) collective-permute-start(bf16[128,2048]{1,0:T(8,128)(2,1)S(1)} %maximum_select_fusion.3), channel_id=1, source_target_pairs={{0,1},{1,0},{2,3},{3,2},{4,5},{5,4},{6,7},{7,6},{8,9},{9,8},{10,11... | collective-permute-start | bytes 1572872 | tf_op jit(solution)/shard_map/ppermute | solution.py:641
  709.3 20.2 %collective-permute-start.63 = (f32[2,448]{1,0:T(2,128)S(1)}, f32[2,448]{1,0:T(2,128)S(1)}, u32[]{:S(2)}, u32[]{:S(2)}) collective-permute-start(f32[2,448]{1,0:T(2,128)S(1)} %pad_maximum_fusion.4), channel_id=1, source_target_pairs={{0,1},{1,0},{2,3},{3,2},{4,5},{5,4},{6,7},{7,6},{8,9},{9,8},{10,11... | collective-permute-start | bytes 10760 | tf_op jit(solution)/shard_map/ppermute | solution.py:641
  710.5 35.7 %collective-permute-start.60 = (bf16[128,2048]{1,0:T(8,128)(2,1)S(1)}, bf16[128,2048]{1,0:T(8,128)(2,1)S(1)}, u32[]{:S(2)}, u32[]{:S(2)}) collective-permute-start(bf16[128,2048]{1,0:T(8,128)(2,1)S(1)} %maximum_select_fusion.6), channel_id=1, source_target_pairs={{0,1},{1,0},{2,3},{3,2},{4,5},{5,4},{6,7},{7,6},{8,9},{9,8},{10,11... | collective-permute-start | bytes 1572872 | tf_op jit(solution)/shard_map/ppermute | solution.py:641
  744.9 9.6 %collective-permute-start.62 = (f32[6,128]{1,0:T(8,128)S(1)}, f32[6,128]{1,0:T(8,128)S(1)}, u32[]{:S(2)}, u32[]{:S(2)}) collective-permute-start(f32[6,128]{1,0:T(8,128)S(1)} %convert_reduce_fusion), channel_id=1, source_target_pairs={{0,1},{1,0},{2,3},{3,2},{4,5},{5,4},{6,7},{7,6},{8,9},{9,8},{10,11... | collective-permute-start | bytes 9224 | tf_op jit(solution)/shard_map/ppermute | solution.py:641
  (55 other events, 751.1 us)

commit v5 on v4

--- a/solution.py
+++ b/solution.py
@@ -185,8 +185,28 @@
     join_down(own_ref, other_ref, down_ref)
 
 
-def call_join(body, own, other, ups, downs):
+def join_halves(own_ref, lower_ref, upper_ref, up_ref, down_ref):
+    lower = pl.program_id(0) < GROUP // MEMBERS // 2
+
+    @pl.when(lower)
+    def _():
+        join_both(own_ref, lower_ref, up_ref, down_ref)
+
+    @pl.when(jnp.logical_not(lower))
+    def _():
+        join_both(own_ref, upper_ref, up_ref, down_ref)
+
+
+def call_join(body, own, others, ups, downs):
     rows = own.shape[1]
+    steps = GROUP // MEMBERS
+    spec = pl.BlockSpec((MEMBERS, rows, 128), lambda i: (i, 0, 0))
+    other_specs = [spec]
+    if len(others) == 2:
+        other_specs = [
+            pl.BlockSpec((MEMBERS, rows, 128), lambda i: (jnp.minimum(i, steps // 2 - 1), 0, 0)),
+            pl.BlockSpec((MEMBERS, rows, 128), lambda i: (jnp.maximum(i - steps // 2, 0), 0, 0)),
+        ]
     specs, shapes = [], []
     if ups:
         specs.append(pl.BlockSpec((MEMBERS * 128, 2 * UP_ROWS), lambda i: (i, 0)))
@@ -197,12 +217,12 @@
     return pl.pallas_call(
         body,
         grid=(GROUP // MEMBERS,),
-        in_specs=[pl.BlockSpec((MEMBERS, rows, 128), lambda i: (i, 0, 0))] * 2,
+        in_specs=[spec] + other_specs,
         out_specs=specs,
         out_shape=shapes,
         cost_estimate=pl.CostEstimate(flops=0, bytes_accessed=GROUP * rows * 128 * 12, transcendentals=0),
         name=body.__name__,
-    )(own, other)
+    )(own, *others)
 
 
 def slot_copies(refs, which, target, core):
@@ -671,7 +691,7 @@
     rows = lax.broadcasted_iota(jnp.int32, (block, 1), 0)
     mine_rows = (rows < half) == is_first
 
-    def ring_sum(*sets, needed=()):
+    def ring_sum(*sets, needed={}):
         took_far = [across(give_far) for give_far, _, _ in sets]
         took = [across(give) for _, give, _ in sets]
         keep = [x for _, _, x in sets]
@@ -680,8 +700,7 @@
         moving = jnp.where(mine_rows, jnp.concatenate([moving, moving], 1), 0).astype(f32)
         for step in reversed(range(side)):
             here = slice(step * block, (step + 1) * block)
-            if step == side - 2 and needed:
-                moving = after(moving, *needed)
+            moving = after(moving, *needed.get(step, ()))
             added = [k[here].astype(f32) + t[here].astype(f32) for k, t in zip(keep, took)]
             moving = along((moving + jnp.stack(added)).astype(bf16))
             if step:
@@ -712,9 +731,9 @@
         packed_down = call_pack(pack_down, 0, (), downs, ())
         down = spread(after(packed_down, up))
         down_other = over(down)
-        weights.append(call_join(join_up, up, up_other, True, False) + call_join(join_down, down, down_other, False, True))
+        weights.append(call_join(join_up, up, [up_other], True, False) + call_join(join_down, down, [down_other], False, True))
         packed_last = call_pack(pack_both, 1, ups, downs, ())
-        first_up, first_other, first_down = up, up_other, down
+        firsts = (up, up_other, down)
     else:
         small_all = lax.all_gather(small, "dp", axis=0, tiled=False)
         for layer in range(LAYERS):
@@ -744,7 +763,7 @@
             )
             down = lax.all_gather(spread(down), "dp", axis=0, axis_index_groups=outer, tiled=True)
             down = down.transpose(1, 0, 2).reshape(-1, width // 128, 128).transpose(1, 0, 2)
-            weights.append(call_join(join_up, up, over(up), True, False) + call_join(join_down, down, over(down), False, True))
+            weights.append(call_join(join_up, up, [over(up)], True, False) + call_join(join_down, down, [over(down)], False, True))
     if groups == 1:
         biases = jnp.concatenate([qkv_bias.reshape(LAYERS, 3 * HEAD_DIM), fc1_bias], axis=1)
     else:
@@ -806,11 +825,11 @@
     keeps = jnp.stack([jnp.ones_like(labels[0]), (labels[0] > 0).astype(labels.dtype)]).astype(bf16)
     both = both * keeps[:, :, None]
     if groups == 1:
-        inputs = gather_rows(after(both, packed_down, packed_last, first_up), {side: (first_other,)})
-        slab = spread(after(packed_last, first_down, inputs[-2]))
-        slab_other = over(slab)
-        weights.append(call_join(join_both, slab, slab_other, True, True))
-        slabs, others = (slab,), (slab_other,)
+        inputs = gather_rows(after(both, packed_down, packed_last, *firsts), {side: (down_other,)})
+        slab = spread(after(packed_last, inputs[-2]))
+        others = tuple(over(slab[n * GROUP // 2 : (n + 1) * GROUP // 2]) for n in range(2))
+        weights.append(call_join(join_halves, slab, others, True, True))
+        slabs = (slab,)
     else:
         inputs = gather_rows(both)
         slabs, others = (), ()
@@ -824,19 +843,19 @@
     next_state, normed_own = call_end(
         partial(forward_end, False),
         core_word,
-        ring_sum((after(parts[0], *slabs), parts[1], parts[2]))[0],
+        ring_sum((after(parts[0], *slabs), parts[1], parts[2]), needed={0: others[:1]})[0],
         [state, added_bias[0], gains[1], shifts[1]],
         [jax.ShapeDtypeStruct(rows_shape, f32), jax.ShapeDtypeStruct(rows_shape, bf16)],
         "forward_end",
     )
-    normed_chunks = gather_rows(in_order(normed_own, across(normed_own)), {1: others})
+    normed_chunks = gather_rows(in_order(normed_own, across(normed_own)), {1: others[1:]})
 
     def handed_back(own_rows):
         filled = in_order(own_rows, across(own_rows))
         return jnp.where(tensor == core, filled, over(filled))
 
     def summed(own, other, *earlier, extra=None):
-        total = own.astype(f32) + over(other).astype(f32)
+        total = own.astype(f32) + other.astype(f32)
         if groups > 1:
             total = total.transpose(1, 0, 2).reshape(total.shape[1], width)
             total = lax.psum_scatter(total, "dp", scatter_dimension=1, axis_index_groups=outer, tiled=True)
@@ -877,21 +896,9 @@
     out_parts = parts[:3]
     down_pair = down_gradients(wide_last, [grad_rows])
     *up_pair, bias_last = up_gradients(slim, normed_last)
-    grad_end, out_end = ring_sum(parts[3:], out_parts, needed=(down_pair[0], up_pair[0]))
+    down_sent, up_sent = over(down_pair[1]), over(up_pair[1])
+    grad_end, out_end = ring_sum(parts[3:], out_parts, needed={1: (down_pair[0], up_pair[0]), 0: (down_sent,)})
     grad_state, grad_low, sums_last = backward_finish(grad_end, next_state, grad_state, 1)
-    grad_chunks = gather_rows(in_order(grad_low, across(grad_low)))
-    down_last = summed(*down_pair)
-    up_last = summed(*up_pair, down_last)
-
-    down_pair = down_gradients(wide, grad_chunks)
-    grad_rows, slim, *parts = call_pass(
-        "last", core_word, weights[0], tables, allowed, [heads, after(hidden_pre, down_pair[0], down_last)], grad_chunks
-    )
-    down_first = summed(*down_pair, up_last)
-    *up_pair, bias_first = up_gradients(slim, after(normed, up_last))
-    (grad_end,) = ring_sum((after(parts[0], up_pair[0]), parts[1], parts[2]), needed=(down_first,))
-    _, grad_low, sums_first = backward_finish(grad_end, state, grad_state, 0)
-    grad_hidden = handed_back(grad_low).astype(f32)
     (hidden_out,) = call_end(
         partial(forward_end, True),
         core_word,
@@ -901,14 +908,29 @@
         "forward_out",
     )
     hidden_out = handed_back(hidden_out)
+    down_last = summed(down_pair[0], after(down_sent, grad_low))
+    grad_chunks = gather_rows(in_order(grad_low, across(grad_low)), {2: (up_sent,), side: (down_last, hidden_out)})
+    up_last = summed(up_pair[0], after(up_sent, grad_chunks[-2]), down_last)
+
+    down_pair = down_gradients(wide, grad_chunks)
+    down_sent = over(down_pair[1])
+    grad_rows, slim, *parts = call_pass(
+        "last", core_word, weights[0], tables, allowed, [heads, after(hidden_pre, down_pair[0])], grad_chunks
+    )
+    down_first = summed(down_pair[0], after(down_sent, slim), up_last)
+    *up_pair, bias_first = up_gradients(slim, after(normed, up_last))
+    up_sent = over(up_pair[1])
+    (grad_end,) = ring_sum((after(parts[0], up_pair[0]), parts[1], parts[2]), needed={1: (down_first,)})
+    _, grad_low, sums_first = backward_finish(grad_end, state, grad_state, 0)
+    grad_hidden = handed_back(grad_low).astype(f32)
 
     vectors = jnp.stack([sums_first, sums_last]).reshape(LAYERS * 3, n_dp, piece).transpose(1, 0, 2)
     if groups == 1:
         extra = jnp.pad(vectors, ((0, 0), (0, 16 - LAYERS * 3), (0, 0))).astype(bf16)
-        up_first = summed(*up_pair, down_first, extra=extra)
+        up_first = summed(up_pair[0], up_sent, down_first, extra=extra)
         vectors = up_first[:, UP_ROWS : UP_ROWS + LAYERS * 3].astype(f32)
     else:
-        up_first = summed(*up_pair, down_first)
+        up_first = summed(up_pair[0], up_sent, down_first)
         vectors = lax.all_to_all(vectors, "dp", 0, 0, tiled=True)
     vectors = jnp.sum(vectors, axis=0)
     vectors = (vectors + over(vectors)).reshape(LAYERS, 3, piece)

time: 762 us -> 760 us (level)
  starting transfers between devices: 134 us -> 112 us
  local copies, waits for them, and re-layouts: 22.6 us -> 32.8 us
    all_to_all x7, waiting for transfers between devices: 45.2 us -> 73.9 us  [spread(): return lax.all_to_all(x, 'dp', 0, 0, axis_index_groups=inner, tiled=True)]
    ppermute x12 -> x13, waiting for transfers between devices: 114 us -> 89.4 us  [over(): return lax.ppermute(x, 'tensor', [(0, 1), (1, 0)])]
    ppermute x28, starting transfers between devices: 34.5 us -> 24.1 us  [across(): return lax.ppermute(x, 'dp', core_pairs)]
  transfers between devices with their start and end apart: 71 -> 72, of which waited for: 42 -> 46; matrix products, arithmetic and copies ran while one was open for 8% -> 8% of each run, Pallas kernels for 17% -> 18%
where the time goes in v5:
time: 760 us; the launch traced here: 749 us
  waiting for transfers between devices  370 us (49%)
  Pallas kernels  179 us (24%)
  starting transfers between devices  112 us (15%)
  other arithmetic  52.2 us (7%)
  local copies, waits for them, and re-layouts  32.8 us (4%)
    ppermute x24, waiting for transfers between devices, along(): return lax.ppermute(x, 'dp', ring_pairs)  192 us
    ppermute x13, waiting for transfers between devices, over(): return lax.ppermute(x, 'tensor', [(0, 1), (1, 0)])  89.4 us
    pallas_call x3, Pallas kernels, call_pass(): pl.pallas_call(partial(layer_pass, mode), in_specs=[SMEM_SPEC] + [VMEM_SP...  88.9 us
    all_to_all x7, waiting for transfers between devices, spread(): return lax.all_to_all(x, 'dp', 0, 0, axis_index_groups=inner, tiled=True)  73.9 us
    all_to_all x7, starting transfers between devices, spread(): return lax.all_to_all(x, 'dp', 0, 0, axis_index_groups=inner, tiled=True)  46.9 us
    pallas_call x4, Pallas kernels, call_gradients(): pl.pallas_call(partial(gradient_slabs, own_rows, other_rows, with_sums, l...  37.9 us
    ppermute x24, starting transfers between devices, along(): return lax.ppermute(x, 'dp', ring_pairs)  26.3 us
    ppermute x28, starting transfers between devices, across(): return lax.ppermute(x, 'dp', core_pairs)  24.1 us
  transfers between devices with their start and end apart: 72, of which 46 were waited for; matrix products, arithmetic and copies ran while one was open for 8% of the time, Pallas kernels for 18%

profile of v5, /device:TPU:13, one launch (start us, length us, event | category | flops | bytes accessed | tf_op | source)
XLA Modules:
  0.0 749.0 jit_solution(17395304411325826576)
XLA Ops:
  4.9 4.0 pack_first.1
  8.8 6.5 all-to-all-start
  15.3 3.5 pack_down.1
  18.8 39.7 %all-to-all-done.own_ref = bf16[16,464,128]{2,1,0:T(8,128)(2,1)S(1)} async-done(((bf16[16,464,128]{2,1,0:T(8,128)(2,1)}), bf16[16,464,128]{2,1,0:T(8,128)(2,1)S(1)}, u32[]{:S(2)}, u32[]{:S(2)}) %all-to-all-start) | async-done | bytes 1900576 | tf_op jit(solution)/shard_map/all_to_all | solution.py:712
  58.5 4.8 all-to-all-start.1
  68.8 4.4 pack_both.1
  76.5 34.0 %collective-permute-done.1.other_ref = bf16[16,464,128]{2,1,0:T(8,128)(2,1)} collective-permute-done((bf16[16,464,128]{2,1,0:T(8,128)(2,1)S(1)}, bf16[16,464,128]{2,1,0:T(8,128)(2,1)}, u32[]{:S(2)}, u32[]{:S(2)}) %collective-permute-start.1) | collective-permute-done | bytes 1900576 | tf_op jit(solution)/shard_map/ppermute | solution.py:661
  111.7 13.0 %collective-permute-done.2.refs_11_.refs_18_ = bf16[2,128,2048]{2,1,0:T(8,128)(2,1)S(1)} collective-permute-done((bf16[2,128,2048]{2,1,0:T(8,128)(2,1)}, bf16[2,128,2048]{2,1,0:T(8,128)(2,1)S(1)}, u32[]{:S(2)}, u32[]{:S(2)}) %collective-permute-start.2) | collective-permute-done | bytes 1048608 | tf_op jit(solution)/shard_map/ppermute | solution.py:655
  128.0 11.7 %collective-permute-done.3.refs_12_.refs_19_ = bf16[2,128,2048]{2,1,0:T(8,128)(2,1)} collective-permute-done((bf16[2,128,2048]{2,1,0:T(8,128)(2,1)S(1)}, bf16[2,128,2048]{2,1,0:T(8,128)(2,1)}, u32[]{:S(2)}, u32[]{:S(2)}) %collective-permute-start.3) | collective-permute-done | bytes 1048608 | tf_op jit(solution)/shard_map/ppermute | solution.py:655
  140.9 13.1 %collective-permute-done.4.refs_13_.refs_20_ = bf16[2,128,2048]{2,1,0:T(8,128)(2,1)} collective-permute-done((bf16[2,128,2048]{2,1,0:T(8,128)(2,1)}, bf16[2,128,2048]{2,1,0:T(8,128)(2,1)}, u32[]{:S(2)}, u32[]{:S(2)}) %collective-permute-start.4) | collective-permute-done | bytes 1048608 | tf_op jit(solution)/shard_map/ppermute | solution.py:655
  157.2 7.2 collective-permute-done.6.refs_17_.refs_24_
  164.5 9.1 %all-to-all-start.2 = ((bf16[16,768,128]{2,1,0:T(8,128)(2,1)}), bf16[16,768,128]{2,1,0:T(8,128)(2,1)S(1)}, u32[]{:S(2)}, u32[]{:S(2)}) async-start(bf16[16,768,128]{2,1,0:T(8,128)(2,1)} %pack_both.1), calls=%async_computation.2 | async-start | bytes 6291456 | tf_op jit(solution)/shard_map/all_to_all | solution.py:712
  180.2 3.1 multiply_sine_fusion
  185.1 3.4 concatenate.72.refs_5_
  188.5 3.3 concatenate.71.refs_4_
  192.6 3.5 concatenate.70.refs_3_
  196.8 4.8 join_up.1.refs_1_
  201.6 4.2 join_down.1.refs_2_
  205.9 29.3 %pass_first.1 = (bf16[1024,2048]{1,0:T(8,128)(2,1)}, bf16[1024,384]{1,0:T(8,128)(2,1)}, f32[1024,512]{1,0:T(8,128)}, bf16[1024,640]{1,0:T(8,128)(2,1)}, bf16[64,...) custom-call(s32[1]{0:T(128)} %bitcast.refs_0_.core_ref, bf16[2048,896]{1,0:T(8,128)(2,1)} %join_up.1.refs_1_, ...), custom_call_target="tpu_custom_call" | custom-call | flops 19327352832 | bytes 20000000 | tf_op jit(solution)/shard_map/pass_first/pallas_call | solution.py:433
  235.7 7.7 %all-to-all-done.2.own_ref = bf16[16,768,128]{2,1,0:T(8,128)(2,1)S(1)} async-done(((bf16[16,768,128]{2,1,0:T(8,128)(2,1)}), bf16[16,768,128]{2,1,0:T(8,128)(2,1)S(1)}, u32[]{:S(2)}, u32[]{:S(2)}) %all-to-all-start.2) | async-done | bytes 3145760 | tf_op jit(solution)/shard_map/all_to_all | solution.py:712
  249.0 2.9 collective-permute-done.16
  253.2 8.3 %collective-permute-done.17 = bf16[1,128,2048]{2,1,0:T(8,128)(2,1)S(1)} collective-permute-done((bf16[1,128,2048]{2,1,0:T(8,128)(2,1)S(1)}, bf16[1,128,2048]{2,1,0:T(8,128)(2,1)S(1)}, u32[]{:S(2)}, u32[]{:S(2)}) %collective-permute-start.17) | collective-permute-done | bytes 524320 | tf_op jit(solution)/shard_map/ppermute | solution.py:655
  262.9 8.3 %collective-permute-done.18 = bf16[1,128,2048]{2,1,0:T(8,128)(2,1)S(1)} collective-permute-done((bf16[1,128,2048]{2,1,0:T(8,128)(2,1)S(1)}, bf16[1,128,2048]{2,1,0:T(8,128)(2,1)S(1)}, u32[]{:S(2)}, u32[]{:S(2)}) %collective-permute-start.18) | collective-permute-done | bytes 524320 | tf_op jit(solution)/shard_map/ppermute | solution.py:655
  271.3 12.3 %collective-permute-done.7.lower_ref = bf16[8,768,128]{2,1,0:T(8,128)(2,1)S(1)} collective-permute-done((bf16[8,768,128]{2,1,0:T(8,128)(2,1)S(1)}, bf16[8,768,128]{2,1,0:T(8,128)(2,1)S(1)}, u32[]{:S(2)}, u32[]{:S(2)}) %collective-permute-start.7) | collective-permute-done | bytes 1572896 | tf_op jit(solution)/shard_map/ppermute | solution.py:661
  288.4 6.4 collective-permute-done.19.moving_ref
  306.2 17.3 %collective-permute-done.8.upper_ref = bf16[8,768,128]{2,1,0:T(8,128)(2,1)} collective-permute-done((bf16[8,768,128]{2,1,0:T(8,128)(2,1)}, bf16[8,768,128]{2,1,0:T(8,128)(2,1)}, u32[]{:S(2)}, u32[]{:S(2)}) %collective-permute-start.8) | collective-permute-done | bytes 1572896 | tf_op jit(solution)/shard_map/ppermute | solution.py:661
  323.4 8.3 %collective-permute-done.23.refs_10_ = bf16[128,2048]{1,0:T(8,128)(2,1)S(1)} collective-permute-done((bf16[128,2048]{1,0:T(8,128)(2,1)S(1)}, bf16[128,2048]{1,0:T(8,128)(2,1)S(1)}, u32[]{:S(2)}, u32[]{:S(2)}) %collective-permute-start.23) | collective-permute-done | bytes 524320 | tf_op jit(solution)/shard_map/ppermute | solution.py:655
  333.5 6.5 collective-permute-done.24.refs_11_
  345.4 3.7 collective-permute-start.29
  349.1 6.4 join_halves.1
  356.6 35.2 %pass_middle.1 = (bf16[1024,2048]{1,0:T(8,128)(2,1)}, bf16[1024,2048]{1,0:T(8,128)(2,1)}, bf16[1024,640]{1,0:T(8,128)(2,1)}, bf16[1024,896]{1,0:T(8,128)(2,1)}, ...) custom-call(s32[1]{0:T(128)} %bitcast.refs_0_.core_ref, ...), custom_call_target="tpu_custom_call" | custom-call | flops 38654705664 | bytes 40000000 | tf_op jit(solution)/shard_map/pass_middle/pallas_call | solution.py:433
  392.9 3.3 collective-permute-done.31
  404.4 4.3 collective-permute-done.33
  410.4 8.8 %down_gradients.2 = (bf16[16,320,128]{2,1,0:T(8,128)(2,1)}, bf16[16,320,128]{2,1,0:T(8,128)(2,1)}) custom-call(s32[1]{0:T(128)} %bitcast.refs_0_.core_ref, bf16[1024,640]{1,0:T(8,128)(2,1)} %get-tuple-element.99.left_ref, bf16[1024,2048]{1,0:T(8,128)(2,1)} %get-tuple-element.100.rest_0_), custom_call_target="tpu_custom_call" | custom-call | flops 5368709120 | bytes 10747904 | tf_op jit(solution)/shard_map/down_gradients/pallas_call | solution.py:488
  420.4 10.1 %up_gradients.2 = (bf16[16,448,128]{2,1,0:T(8,128)(2,1)}, bf16[16,448,128]{2,1,0:T(8,128)(2,1)}, f32[1,896]{1,0:T(1,128)}) custom-call(s32[1]{0:T(128)} %bitcast.refs_0_.core_ref, bf16[1024,896]{1,0:T(8,128)(2,1)} %get-tuple-element.102.left_ref, bf16[1024,2048]{1,0:T(8,128)(2,1)} %get-tuple-element.103.rest_0_), custom_call_target="tpu_custom_call" | custom-call | flops 7516192768 | bytes 13369344 | tf_op jit(solution)/shard_map/up_gradients/pallas_call | solution.py:488
  434.7 12.2 %collective-permute-done.36 = bf16[2,128,2048]{2,1,0:T(8,128)(2,1)S(1)} collective-permute-done((bf16[2,128,2048]{2,1,0:T(8,128)(2,1)S(1)}, bf16[2,128,2048]{2,1,0:T(8,128)(2,1)S(1)}, u32[]{:S(2)}, u32[]{:S(2)}) %collective-permute-start.36) | collective-permute-done | bytes 1048608 | tf_op jit(solution)/shard_map/ppermute | solution.py:655
  452.2 12.4 %collective-permute-done.38.moving_ref = bf16[2,128,2048]{2,1,0:T(8,128)(2,1)S(1)} collective-permute-done((bf16[2,128,2048]{2,1,0:T(8,128)(2,1)S(1)}, bf16[2,128,2048]{2,1,0:T(8,128)(2,1)S(1)}, u32[]{:S(2)}, u32[]{:S(2)}) %collective-permute-start.38) | collective-permute-done | bytes 1048608 | tf_op jit(solution)/shard_map/ppermute | solution.py:655
  469.3 3.1 backward_end.2
  472.7 2.7 add_convert_fusion.3
  475.5 5.5 all-to-all-start.3
  485.4 30.2 %collective-permute-done.43.rest_1_.refs_10_ = bf16[128,2048]{1,0:T(8,128)(2,1)} collective-permute-done((bf16[128,2048]{1,0:T(8,128)(2,1)}, bf16[128,2048]{1,0:T(8,128)(2,1)}, u32[]{:S(2)}, u32[]{:S(2)}) %collective-permute-start.43) | collective-permute-done | bytes 524320 | tf_op jit(solution)/shard_map/ppermute | solution.py:655
  520.0 4.2 collective-permute-done.44.rest_2_.refs_11_
  526.1 5.7 collective-permute-done.41
  535.3 3.6 collective-permute-done.50.rest_7_.refs_16_
  538.9 3.2 add_convert_fusion.1
  542.2 8.8 %all-to-all-start.4 = ((bf16[16,448,128]{2,1,0:T(8,128)(2,1)}), bf16[16,448,128]{2,1,0:T(8,128)(2,1)S(1)}, u32[]{:S(2)}, u32[]{:S(2)}) async-start(bf16[16,448,128]{2,1,0:T(8,128)(2,1)} %add_convert_fusion.1), calls=%async_computation.4 | async-start | bytes 3670016 | tf_op jit(solution)/shard_map/all_to_all | solution.py:712
  555.5 8.9 %down_gradients.3 = (bf16[16,320,128]{2,1,0:T(8,128)(2,1)}, bf16[16,320,128]{2,1,0:T(8,128)(2,1)}) custom-call(s32[1]{0:T(128)} %bitcast.refs_0_.core_ref, bf16[1024,640]{1,0:T(8,128)(2,1)} %get-tuple-element.111.left_ref, bf16[128,2048]{1,0:T(8,128)(2,1)} %maximum_select_fusion.4.rest_0_.refs_9_, ...), custom_call_target="tpu_custom_call" | custom-call | flops 5368709120 | bytes 10747904 | tf_op jit(solution)/shard_map/down_gradients/pallas_call | solution.py:488
  565.6 24.3 %pass_last.1 = (bf16[1024,2048]{1,0:T(8,128)(2,1)}, bf16[1024,896]{1,0:T(8,128)(2,1)}, bf16[64,2048]{1,0:T(8,128)(2,1)}, bf16[448,2048]{1,0:T(8,128)(2,1)}, bf16[512,2048]{1,0:T(8,128)(2,1)}) custom-call(s32[1]{0:T(128)} %bitcast.refs_0_.core_ref, bf16[2048,896]{1,0:T(8,128)(2,1)} %join_up.1.refs_1_, bf16[640,2048]{1,0:T(8,128)(2,1)} %join_down.1.refs_2_, ...), custom_call_target="tpu_custom_call" | custom-call | flops 19327352832 | bytes 20000000 | tf_op jit(solution)/shard_map/pass_last/pallas_call | solution.py:433
  590.6 4.1 collective-permute-done.56
  594.7 2.7 add_convert_fusion.2
  598.7 6.8 all-to-all-start.5
  605.6 10.2 %up_gradients.3 = (bf16[16,448,128]{2,1,0:T(8,128)(2,1)}, bf16[16,448,128]{2,1,0:T(8,128)(2,1)}, f32[1,896]{1,0:T(1,128)}) custom-call(s32[1]{0:T(128)} %bitcast.refs_0_.core_ref, bf16[1024,896]{1,0:T(8,128)(2,1)} %get-tuple-element.122.left_ref, bf16[1024,2048]{1,0:T(8,128)(2,1)} %get-tuple-element.126.rest_0_), custom_call_target="tpu_custom_call" | custom-call | flops 7516192768 | bytes 13369344 | tf_op jit(solution)/shard_map/up_gradients/pallas_call | solution.py:488
  618.8 18.4 %collective-permute-done.54 = bf16[1,64,2048]{2,1,0:T(8,128)(2,1)S(1)} collective-permute-done((bf16[1,64,2048]{2,1,0:T(8,128)(2,1)S(1)}, bf16[1,64,2048]{2,1,0:T(8,128)(2,1)S(1)}, u32[]{:S(2)}, u32[]{:S(2)}) %collective-permute-start.54) | collective-permute-done | bytes 262176 | tf_op jit(solution)/shard_map/ppermute | solution.py:655
  641.7 5.3 collective-permute-done.55
  652.1 6.5 collective-permute-done.57
  662.2 6.5 collective-permute-done.58.moving_ref
  668.7 4.7 collective-permute-start.59
  673.4 8.4 %collective-permute-done.62 = bf16[16,448,128]{2,1,0:T(8,128)(2,1)} collective-permute-done((bf16[16,448,128]{2,1,0:T(8,128)(2,1)}, bf16[16,448,128]{2,1,0:T(8,128)(2,1)}, u32[]{:S(2)}, u32[]{:S(2)}) %collective-permute-start.62) | collective-permute-done | bytes 1835040 | tf_op jit(solution)/shard_map/ppermute | solution.py:661
  684.6 3.0 backward_end.3
  689.8 5.4 all-to-all-start.6
  698.8 7.2 spread_gradients.2
  706.1 4.4 collective-permute-done.64
  711.8 26.5 %all-to-all-done.6.up_ref = bf16[16,464,128]{2,1,0:T(8,128)(2,1)S(1)} async-done(((bf16[16,464,128]{2,1,0:T(8,128)(2,1)}), bf16[16,464,128]{2,1,0:T(8,128)(2,1)S(1)}, u32[]{:S(2)}, u32[]{:S(2)}) %all-to-all-start.6) | async-done | bytes 1900576 | tf_op jit(solution)/shard_map/all_to_all | solution.py:712
  740.7 7.3 spread_gradients.3
  (325 shorter events, 142.3 us)
Async XLA Ops:
  8.8 49.7 %all-to-all-start = ((bf16[16,464,128]{2,1,0:T(8,128)(2,1)}), bf16[16,464,128]{2,1,0:T(8,128)(2,1)S(1)}, u32[]{:S(2)}, u32[]{:S(2)}) async-start(bf16[16,464,128]{2,1,0:T(8,128)(2,1)} %pack_first.1), calls=%async_computation | async-start | bytes 3801088 | tf_op jit(solution)/shard_map/all_to_all | solution.py:712
  58.5 52.0 %all-to-all-start.1 = ((bf16[16,320,128]{2,1,0:T(8,128)(2,1)}), bf16[16,320,128]{2,1,0:T(8,128)(2,1)S(1)}, u32[]{:S(2)}, u32[]{:S(2)}) async-start(bf16[16,320,128]{2,1,0:T(8,128)(2,1)} %pack_down.1), calls=%async_computation.1 | async-start | bytes 2621440 | tf_op jit(solution)/shard_map/all_to_all | solution.py:712
  65.6 8.3 %collective-permute-start = (bf16[2,128,2048]{2,1,0:T(8,128)(2,1)}, bf16[2,128,2048]{2,1,0:T(8,128)(2,1)}, u32[]{:S(2)}, u32[]{:S(2)}) collective-permute-start(bf16[2,128,2048]{2,1,0:T(8,128)(2,1)} %pad_maximum_fusion), channel_id=1, source_target_pairs={{0,2},{2,0},{4,6},{6,4},{8,10},{10,8},{12,14},{14,12},{16,18},{18,... | collective-permute-start | bytes 3145736 | tf_op jit(solution)/shard_map/ppermute | solution.py:658
  67.5 43.0 %collective-permute-start.1 = (bf16[16,464,128]{2,1,0:T(8,128)(2,1)S(1)}, bf16[16,464,128]{2,1,0:T(8,128)(2,1)}, u32[]{:S(2)}, u32[]{:S(2)}) collective-permute-start(bf16[16,464,128]{2,1,0:T(8,128)(2,1)S(1)} %all-to-all-done.own_ref), channel_id=1, source_target_pairs={{0,1},{1,0},{2,3},{3,2},{4,5},{5,4},{6,7},{7,6},{8,9},{9,8},{10,11... | collective-permute-start | bytes 5701640 | tf_op jit(solution)/shard_map/ppermute | solution.py:661
  110.5 14.2 %collective-permute-start.2 = (bf16[2,128,2048]{2,1,0:T(8,128)(2,1)}, bf16[2,128,2048]{2,1,0:T(8,128)(2,1)S(1)}, u32[]{:S(2)}, u32[]{:S(2)}) collective-permute-start(bf16[2,128,2048]{2,1,0:T(8,128)(2,1)} %select_multiply_fusion.refs_10_.refs_17_), channel_id=1, source_target_pairs={{0,8},{2,6},{8,16},{10,2},{16,24},{18,10},{24,28},{26,18},{28,20},... | collective-permute-start | bytes 3145736 | tf_op jit(solution)/shard_map/ppermute | solution.py:655
  125.6 14.0 %collective-permute-start.3 = (bf16[2,128,2048]{2,1,0:T(8,128)(2,1)S(1)}, bf16[2,128,2048]{2,1,0:T(8,128)(2,1)}, u32[]{:S(2)}, u32[]{:S(2)}) collective-permute-start(bf16[2,128,2048]{2,1,0:T(8,128)(2,1)S(1)} %collective-permute-done.2.refs_11_.refs_18_), channel_id=1, source_target_pairs={{0,8},{2,6},{8,16},{10,2},{16,24},{18,10},{24,28},{26,18},{28,20},... | collective-permute-start | bytes 3145736 | tf_op jit(solution)/shard_map/ppermute | solution.py:655
  126.8 29.2 %collective-permute-start.5 = (bf16[16,320,128]{2,1,0:T(8,128)(2,1)S(1)}, bf16[16,320,128]{2,1,0:T(8,128)(2,1)S(1)}, u32[]{:S(2)}, u32[]{:S(2)}) collective-permute-start(bf16[16,320,128]{2,1,0:T(8,128)(2,1)S(1)} %all-to-all-done.1.own_ref), channel_id=1, source_target_pairs={{0,1},{1,0},{2,3},{3,2},{4,5},{5,4},{6,7},{7,6},{8,9},{9,8},{10,11... | collective-permute-start | bytes 3932168 | tf_op jit(solution)/shard_map/ppermute | solution.py:661
  139.7 14.3 %collective-permute-start.4 = (bf16[2,128,2048]{2,1,0:T(8,128)(2,1)}, bf16[2,128,2048]{2,1,0:T(8,128)(2,1)}, u32[]{:S(2)}, u32[]{:S(2)}) collective-permute-start(bf16[2,128,2048]{2,1,0:T(8,128)(2,1)} %collective-permute-done.3.refs_12_.refs_19_), channel_id=1, source_target_pairs={{0,8},{2,6},{8,16},{10,2},{16,24},{18,10},{24,28},{26,18},{28,20},... | collective-permute-start | bytes 3145736 | tf_op jit(solution)/shard_map/ppermute | solution.py:655
  156.1 8.4 %collective-permute-start.6 = (bf16[2,64,2048]{2,1,0:T(8,128)(2,1)S(1)}, bf16[2,64,2048]{2,1,0:T(8,128)(2,1)}, u32[]{:S(2)}, u32[]{:S(2)}) collective-permute-start(bf16[2,64,2048]{2,1,0:T(8,128)(2,1)S(1)} %constant_dynamic-slice_fusion.4), channel_id=1, source_target_pairs={{0,8},{2,6},{8,16},{10,2},{16,24},{18,10},{24,28},{26,18},{28,20},... | collective-permute-start | bytes 1572872 | tf_op jit(solution)/shard_map/ppermute | solution.py:655
  164.5 79.0 %all-to-all-start.2 = ((bf16[16,768,128]{2,1,0:T(8,128)(2,1)}), bf16[16,768,128]{2,1,0:T(8,128)(2,1)S(1)}, u32[]{:S(2)}, u32[]{:S(2)}) async-start(bf16[16,768,128]{2,1,0:T(8,128)(2,1)} %pack_both.1), calls=%async_computation.2 | async-start | bytes 6291456 | tf_op jit(solution)/shard_map/all_to_all | solution.py:712
  178.4 27.4 %collective-permute-start.10 = (bf16[2,128,2048]{2,1,0:T(8,128)(2,1)}, bf16[2,128,2048]{2,1,0:T(8,128)(2,1)}, u32[]{:S(2)}, u32[]{:S(2)}) collective-permute-start(bf16[2,128,2048]{2,1,0:T(8,128)(2,1)} %copy-done.44), channel_id=1, source_target_pairs={{0,2},{2,0},{4,6},{6,4},{8,10},{10,8},{12,14},{14,12},{16,18},{18,... | collective-permute-start | bytes 3145736 | tf_op jit(solution)/shard_map/ppermute | solution.py:658
  179.7 26.2 %collective-permute-start.11 = (bf16[2,128,2048]{2,1,0:T(8,128)(2,1)}, bf16[2,128,2048]{2,1,0:T(8,128)(2,1)}, u32[]{:S(2)}, u32[]{:S(2)}) collective-permute-start(bf16[2,128,2048]{2,1,0:T(8,128)(2,1)} %collective-permute-done.3.refs_12_.refs_19_), channel_id=1, source_target_pairs={{0,2},{2,0},{4,6},{6,4},{8,10},{10,8},{12,14},{14,12},{16,18},{18,... | collective-permute-start | bytes 3145736 | tf_op jit(solution)/shard_map/ppermute | solution.py:658
  179.7 26.2 %collective-permute-start.12 = (bf16[2,128,2048]{2,1,0:T(8,128)(2,1)}, bf16[2,128,2048]{2,1,0:T(8,128)(2,1)}, u32[]{:S(2)}, u32[]{:S(2)}) collective-permute-start(bf16[2,128,2048]{2,1,0:T(8,128)(2,1)} %collective-permute-done.4.refs_13_.refs_20_), channel_id=1, source_target_pairs={{0,2},{2,0},{4,6},{6,4},{8,10},{10,8},{12,14},{14,12},{16,18},{18,... | collective-permute-start | bytes 3145736 | tf_op jit(solution)/shard_map/ppermute | solution.py:658
  183.3 22.6 %collective-permute-start.13 = (bf16[2,64,2048]{2,1,0:T(8,128)(2,1)}, bf16[2,64,2048]{2,1,0:T(8,128)(2,1)}, u32[]{:S(2)}, u32[]{:S(2)}) collective-permute-start(bf16[2,64,2048]{2,1,0:T(8,128)(2,1)} %collective-permute-done.6.refs_17_.refs_24_), channel_id=1, source_target_pairs={{0,2},{2,0},{4,6},{6,4},{8,10},{10,8},{12,14},{14,12},{16,18},{18,... | collective-permute-start | bytes 1572872 | tf_op jit(solution)/shard_map/ppermute | solution.py:658
  235.2 13.8 %collective-permute-start.14 = (bf16[448,2048]{1,0:T(8,128)(2,1)}, bf16[448,2048]{1,0:T(8,128)(2,1)}, u32[]{:S(2)}, u32[]{:S(2)}) collective-permute-start(bf16[448,2048]{1,0:T(8,128)(2,1)} %get-tuple-element.87), channel_id=1, source_target_pairs={{0,2},{2,0},{4,6},{6,4},{8,10},{10,8},{12,14},{14,12},{16,18},{18,... | collective-permute-start | bytes 5505032 | tf_op jit(solution)/shard_map/ppermute | solution.py:658
  246.2 5.6 collective-permute-start.16
  247.7 35.8 %collective-permute-start.7 = (bf16[8,768,128]{2,1,0:T(8,128)(2,1)S(1)}, bf16[8,768,128]{2,1,0:T(8,128)(2,1)S(1)}, u32[]{:S(2)}, u32[]{:S(2)}) collective-permute-start(bf16[8,768,128]{2,1,0:T(8,128)(2,1)S(1)} %get-tuple-element.202), channel_id=1, source_target_pairs={{0,1},{1,0},{2,3},{3,2},{4,5},{5,4},{6,7},{7,6},{8,9},{9,8},{10,11... | collective-permute-start | bytes 4718600 | tf_op jit(solution)/shard_map/ppermute | solution.py:661
  253.1 8.4 %collective-permute-start.17 = (bf16[1,128,2048]{2,1,0:T(8,128)(2,1)S(1)}, bf16[1,128,2048]{2,1,0:T(8,128)(2,1)S(1)}, u32[]{:S(2)}, u32[]{:S(2)}) collective-permute-start(bf16[1,128,2048]{2,1,0:T(8,128)(2,1)S(1)} %fusion.9), channel_id=1, source_target_pairs={{0,8},{2,6},{8,16},{10,2},{16,24},{18,10},{24,28},{26,18},{28,20},... | collective-permute-start | bytes 1572872 | tf_op jit(solution)/shard_map/ppermute | solution.py:655
  262.8 8.4 %collective-permute-start.18 = (bf16[1,128,2048]{2,1,0:T(8,128)(2,1)S(1)}, bf16[1,128,2048]{2,1,0:T(8,128)(2,1)S(1)}, u32[]{:S(2)}, u32[]{:S(2)}) collective-permute-start(bf16[1,128,2048]{2,1,0:T(8,128)(2,1)S(1)} %fusion.8), channel_id=1, source_target_pairs={{0,8},{2,6},{8,16},{10,2},{16,24},{18,10},{24,28},{26,18},{28,20},... | collective-permute-start | bytes 1572872 | tf_op jit(solution)/shard_map/ppermute | solution.py:655
  285.9 8.8 %collective-permute-start.19 = (bf16[1,128,2048]{2,1,0:T(8,128)(2,1)}, bf16[1,128,2048]{2,1,0:T(8,128)(2,1)S(1)}, u32[]{:S(2)}, u32[]{:S(2)}) collective-permute-start(bf16[1,128,2048]{2,1,0:T(8,128)(2,1)} %fusion.7), channel_id=1, source_target_pairs={{0,8},{2,6},{8,16},{10,2},{16,24},{18,10},{24,28},{26,18},{28,20},... | collective-permute-start | bytes 1572872 | tf_op jit(solution)/shard_map/ppermute | solution.py:655
  287.2 36.3 %collective-permute-start.8 = (bf16[8,768,128]{2,1,0:T(8,128)(2,1)}, bf16[8,768,128]{2,1,0:T(8,128)(2,1)}, u32[]{:S(2)}, u32[]{:S(2)}) collective-permute-start(bf16[8,768,128]{2,1,0:T(8,128)(2,1)} %get-tuple-element.201), channel_id=1, source_target_pairs={{0,1},{1,0},{2,3},{3,2},{4,5},{5,4},{6,7},{7,6},{8,9},{9,8},{10,11... | collective-permute-start | bytes 4718600 | tf_op jit(solution)/shard_map/ppermute | solution.py:661
  304.7 18.7 %collective-permute-start.22 = (bf16[128,2048]{1,0:T(8,128)(2,1)S(1)}, bf16[128,2048]{1,0:T(8,128)(2,1)S(1)}, u32[]{:S(2)}, u32[]{:S(2)}) collective-permute-start(bf16[128,2048]{1,0:T(8,128)(2,1)S(1)} %maximum_select_fusion.2.refs_8_), channel_id=1, source_target_pairs={{0,8},{2,6},{8,16},{10,2},{16,24},{18,10},{24,28},{26,18},{28,20},... | collective-permute-start | bytes 1572872 | tf_op jit(solution)/shard_map/ppermute | solution.py:655
  323.4 8.3 %collective-permute-start.23 = (bf16[128,2048]{1,0:T(8,128)(2,1)S(1)}, bf16[128,2048]{1,0:T(8,128)(2,1)S(1)}, u32[]{:S(2)}, u32[]{:S(2)}) collective-permute-start(bf16[128,2048]{1,0:T(8,128)(2,1)S(1)} %collective-permute-done.22.refs_9_), channel_id=1, source_target_pairs={{0,8},{2,6},{8,16},{10,2},{16,24},{18,10},{24,28},{26,18},{28,20},... | collective-permute-start | bytes 1572872 | tf_op jit(solution)/shard_map/ppermute | solution.py:655
  331.7 8.3 %collective-permute-start.24 = (bf16[128,2048]{1,0:T(8,128)(2,1)S(1)}, bf16[128,2048]{1,0:T(8,128)(2,1)S(1)}, u32[]{:S(2)}, u32[]{:S(2)}) collective-permute-start(bf16[128,2048]{1,0:T(8,128)(2,1)S(1)} %collective-permute-done.23.refs_10_), channel_id=1, source_target_pairs={{0,8},{2,6},{8,16},{10,2},{16,24},{18,10},{24,28},{26,18},{28,20},... | collective-permute-start | bytes 1572872 | tf_op jit(solution)/shard_map/ppermute | solution.py:655
  331.7 23.8 %collective-permute-start.25 = (bf16[128,2048]{1,0:T(8,128)(2,1)S(1)}, bf16[128,2048]{1,0:T(8,128)(2,1)S(1)}, u32[]{:S(2)}, u32[]{:S(2)}) collective-permute-start(bf16[128,2048]{1,0:T(8,128)(2,1)S(1)} %collective-permute-done.22.refs_9_), channel_id=1, source_target_pairs={{0,2},{2,0},{4,6},{6,4},{8,10},{10,8},{12,14},{14,12},{16,18},{18,... | collective-permute-start | bytes 1572872 | tf_op jit(solution)/shard_map/ppermute | solution.py:658
  333.5 22.1 %collective-permute-start.26 = (bf16[128,2048]{1,0:T(8,128)(2,1)S(1)}, bf16[128,2048]{1,0:T(8,128)(2,1)S(1)}, u32[]{:S(2)}, u32[]{:S(2)}) collective-permute-start(bf16[128,2048]{1,0:T(8,128)(2,1)S(1)} %collective-permute-done.23.refs_10_), channel_id=1, source_target_pairs={{0,2},{2,0},{4,6},{6,4},{8,10},{10,8},{12,14},{14,12},{16,18},{18,... | collective-permute-start | bytes 1572872 | tf_op jit(solution)/shard_map/ppermute | solution.py:658
  340.1 5.3 collective-permute-start.28
  340.2 15.4 %collective-permute-start.27 = (bf16[128,2048]{1,0:T(8,128)(2,1)S(1)}, bf16[128,2048]{1,0:T(8,128)(2,1)}, u32[]{:S(2)}, u32[]{:S(2)}) collective-permute-start(bf16[128,2048]{1,0:T(8,128)(2,1)S(1)} %collective-permute-done.24.refs_11_), channel_id=1, source_target_pairs={{0,2},{2,0},{4,6},{6,4},{8,10},{10,8},{12,14},{14,12},{16,18},{18,... | collective-permute-start | bytes 1572872 | tf_op jit(solution)/shard_map/ppermute | solution.py:658
  345.4 10.2 %collective-permute-start.29 = (bf16[64,2048]{1,0:T(8,128)(2,1)S(1)}, bf16[64,2048]{1,0:T(8,128)(2,1)}, u32[]{:S(2)}, u32[]{:S(2)}) collective-permute-start(bf16[64,2048]{1,0:T(8,128)(2,1)S(1)} %collective-permute-done.28.refs_15_), channel_id=1, source_target_pairs={{0,2},{2,0},{4,6},{6,4},{8,10},{10,8},{12,14},{14,12},{16,18},{18,... | collective-permute-start | bytes 786440 | tf_op jit(solution)/shard_map/ppermute | solution.py:658
  391.8 8.9 %collective-permute-start.34 = (bf16[448,2048]{1,0:T(8,128)(2,1)}, bf16[448,2048]{1,0:T(8,128)(2,1)S(1)}, u32[]{:S(2)}, u32[]{:S(2)}) collective-permute-start(bf16[448,2048]{1,0:T(8,128)(2,1)} %get-tuple-element.98), channel_id=1, source_target_pairs={{0,2},{2,0},{4,6},{6,4},{8,10},{10,8},{12,14},{14,12},{16,18},{18,... | collective-permute-start | bytes 5505032 | tf_op jit(solution)/shard_map/ppermute | solution.py:658
  392.0 4.3 collective-permute-start.31
  392.4 10.0 %collective-permute-start.30 = (bf16[448,2048]{1,0:T(8,128)(2,1)}, bf16[448,2048]{1,0:T(8,128)(2,1)S(1)}, u32[]{:S(2)}, u32[]{:S(2)}) collective-permute-start(bf16[448,2048]{1,0:T(8,128)(2,1)} %get-tuple-element.94), channel_id=1, source_target_pairs={{0,2},{2,0},{4,6},{6,4},{8,10},{10,8},{12,14},{14,12},{16,18},{18,... | collective-permute-start | bytes 5505032 | tf_op jit(solution)/shard_map/ppermute | solution.py:658
  392.5 6.7 collective-permute-start.32
  400.3 8.4 %collective-permute-start.33 = (bf16[2,64,2048]{2,1,0:T(8,128)(2,1)S(1)}, bf16[2,64,2048]{2,1,0:T(8,128)(2,1)S(1)}, u32[]{:S(2)}, u32[]{:S(2)}) collective-permute-start(bf16[2,64,2048]{2,1,0:T(8,128)(2,1)S(1)} %pad_maximum_fusion.1), channel_id=1, source_target_pairs={{0,8},{2,6},{8,16},{10,2},{16,24},{18,10},{24,28},{26,18},{28,20},... | collective-permute-start | bytes 1572872 | tf_op jit(solution)/shard_map/ppermute | solution.py:655
  410.1 20.4 %collective-permute-start.35 = (bf16[2,128,2048]{2,1,0:T(8,128)(2,1)}, bf16[2,128,2048]{2,1,0:T(8,128)(2,1)}, u32[]{:S(2)}, u32[]{:S(2)}) collective-permute-start(bf16[2,128,2048]{2,1,0:T(8,128)(2,1)} %fusion.1), channel_id=1, source_target_pairs={{0,8},{2,6},{8,16},{10,2},{16,24},{18,10},{24,28},{26,18},{28,20},... | collective-permute-start | bytes 3145736 | tf_op jit(solution)/shard_map/ppermute | solution.py:655
  419.2 29.9 %collective-permute-start.37 = (bf16[16,320,128]{2,1,0:T(8,128)(2,1)}, bf16[16,320,128]{2,1,0:T(8,128)(2,1)S(1)}, u32[]{:S(2)}, u32[]{:S(2)}) collective-permute-start(bf16[16,320,128]{2,1,0:T(8,128)(2,1)} %get-tuple-element.106), channel_id=1, source_target_pairs={{0,1},{1,0},{2,3},{3,2},{4,5},{5,4},{6,7},{7,6},{8,9},{9,8},{10,11... | collective-permute-start | bytes 3932168 | tf_op jit(solution)/shard_map/ppermute | solution.py:661
  432.7 14.2 %collective-permute-start.36 = (bf16[2,128,2048]{2,1,0:T(8,128)(2,1)S(1)}, bf16[2,128,2048]{2,1,0:T(8,128)(2,1)S(1)}, u32[]{:S(2)}, u32[]{:S(2)}) collective-permute-start(bf16[2,128,2048]{2,1,0:T(8,128)(2,1)S(1)} %fusion.2), channel_id=1, source_target_pairs={{0,8},{2,6},{8,16},{10,2},{16,24},{18,10},{24,28},{26,18},{28,20},... | collective-permute-start | bytes 3145736 | tf_op jit(solution)/shard_map/ppermute | solution.py:655
  450.4 14.2 %collective-permute-start.38 = (bf16[2,128,2048]{2,1,0:T(8,128)(2,1)S(1)}, bf16[2,128,2048]{2,1,0:T(8,128)(2,1)S(1)}, u32[]{:S(2)}, u32[]{:S(2)}) collective-permute-start(bf16[2,128,2048]{2,1,0:T(8,128)(2,1)S(1)} %fusion.3), channel_id=1, source_target_pairs={{0,8},{2,6},{8,16},{10,2},{16,24},{18,10},{24,28},{26,18},{28,20},... | collective-permute-start | bytes 3145736 | tf_op jit(solution)/shard_map/ppermute | solution.py:655
  464.7 3.8 collective-permute-start.39
  466.9 53.1 %collective-permute-start.45 = (bf16[16,448,128]{2,1,0:T(8,128)(2,1)}, bf16[16,448,128]{2,1,0:T(8,128)(2,1)}, u32[]{:S(2)}, u32[]{:S(2)}) collective-permute-start(bf16[16,448,128]{2,1,0:T(8,128)(2,1)} %get-tuple-element.113), channel_id=1, source_target_pairs={{0,1},{1,0},{2,3},{3,2},{4,5},{5,4},{6,7},{7,6},{8,9},{9,8},{10,11... | collective-permute-start | bytes 5505032 | tf_op jit(solution)/shard_map/ppermute | solution.py:661
  472.4 8.6 %collective-permute-start.42 = (bf16[64,2048]{1,0:T(8,128)(2,1)}, bf16[64,2048]{1,0:T(8,128)(2,1)S(1)}, u32[]{:S(2)}, u32[]{:S(2)}) collective-permute-start(bf16[64,2048]{1,0:T(8,128)(2,1)} %get-tuple-element.112), channel_id=1, source_target_pairs={{0,2},{2,0},{4,6},{6,4},{8,10},{10,8},{12,14},{14,12},{16,18},{18,... | collective-permute-start | bytes 786440 | tf_op jit(solution)/shard_map/ppermute | solution.py:658
  475.5 58.1 %all-to-all-start.3 = ((bf16[16,320,128]{2,1,0:T(8,128)(2,1)}), bf16[16,320,128]{2,1,0:T(8,128)(2,1)S(1)}, u32[]{:S(2)}, u32[]{:S(2)}) async-start(bf16[16,320,128]{2,1,0:T(8,128)(2,1)} %add_convert_fusion.3), calls=%async_computation.3 | async-start | bytes 2621440 | tf_op jit(solution)/shard_map/all_to_all | solution.py:712
  481.9 33.7 %collective-permute-start.43 = (bf16[128,2048]{1,0:T(8,128)(2,1)}, bf16[128,2048]{1,0:T(8,128)(2,1)}, u32[]{:S(2)}, u32[]{:S(2)}) collective-permute-start(bf16[128,2048]{1,0:T(8,128)(2,1)} %maximum_select_fusion.4.rest_0_.refs_9_), channel_id=1, source_target_pairs={{0,8},{2,6},{8,16},{10,2},{16,24},{18,10},{24,28},{26,18},{28,20},... | collective-permute-start | bytes 1572872 | tf_op jit(solution)/shard_map/ppermute | solution.py:655
  485.4 32.1 %collective-permute-start.40 = (bf16[64,2048]{1,0:T(8,128)(2,1)}, bf16[64,2048]{1,0:T(8,128)(2,1)S(1)}, u32[]{:S(2)}, u32[]{:S(2)}) collective-permute-start(bf16[64,2048]{1,0:T(8,128)(2,1)} %forward_out.1), channel_id=1, source_target_pairs={{0,2},{2,0},{4,6},{6,4},{8,10},{10,8},{12,14},{14,12},{16,18},{18,... | collective-permute-start | bytes 786440 | tf_op jit(solution)/shard_map/ppermute | solution.py:658
  515.7 8.5 %collective-permute-start.44 = (bf16[128,2048]{1,0:T(8,128)(2,1)}, bf16[128,2048]{1,0:T(8,128)(2,1)S(1)}, u32[]{:S(2)}, u32[]{:S(2)}) collective-permute-start(bf16[128,2048]{1,0:T(8,128)(2,1)} %collective-permute-done.43.rest_1_.refs_10_), channel_id=1, source_target_pairs={{0,8},{2,6},{8,16},{10,2},{16,24},{18,10},{24,28},{26,18},{28,20},... | collective-permute-start | bytes 1572872 | tf_op jit(solution)/shard_map/ppermute | solution.py:655
  518.7 13.1 %collective-permute-start.41 = (bf16[128,2048]{1,0:T(8,128)(2,1)S(1)}, bf16[128,2048]{1,0:T(8,128)(2,1)S(1)}, u32[]{:S(2)}, u32[]{:S(2)}) collective-permute-start(bf16[128,2048]{1,0:T(8,128)(2,1)S(1)} %maximum_select_fusion.3), channel_id=1, source_target_pairs={{0,1},{1,0},{2,3},{3,2},{4,5},{5,4},{6,7},{7,6},{8,9},{9,8},{10,11... | collective-permute-start | bytes 1572872 | tf_op jit(solution)/shard_map/ppermute | solution.py:661
  524.2 8.5 %collective-permute-start.46 = (bf16[128,2048]{1,0:T(8,128)(2,1)S(1)}, bf16[128,2048]{1,0:T(8,128)(2,1)S(1)}, u32[]{:S(2)}, u32[]{:S(2)}) collective-permute-start(bf16[128,2048]{1,0:T(8,128)(2,1)S(1)} %collective-permute-done.44.rest_2_.refs_11_), channel_id=1, source_target_pairs={{0,8},{2,6},{8,16},{10,2},{16,24},{18,10},{24,28},{26,18},{28,20},... | collective-permute-start | bytes 1572872 | tf_op jit(solution)/shard_map/ppermute | solution.py:655
  533.5 5.4 collective-permute-start.50
  542.2 55.3 %all-to-all-start.4 = ((bf16[16,448,128]{2,1,0:T(8,128)(2,1)}), bf16[16,448,128]{2,1,0:T(8,128)(2,1)S(1)}, u32[]{:S(2)}, u32[]{:S(2)}) async-start(bf16[16,448,128]{2,1,0:T(8,128)(2,1)} %add_convert_fusion.1), calls=%async_computation.4 | async-start | bytes 3670016 | tf_op jit(solution)/shard_map/all_to_all | solution.py:712
  551.5 3.2 collective-permute-start.49
  551.9 3.3 collective-permute-start.51
  564.4 30.3 %collective-permute-start.56 = (bf16[16,320,128]{2,1,0:T(8,128)(2,1)}, bf16[16,320,128]{2,1,0:T(8,128)(2,1)}, u32[]{:S(2)}, u32[]{:S(2)}) collective-permute-start(bf16[16,320,128]{2,1,0:T(8,128)(2,1)} %get-tuple-element.129), channel_id=1, source_target_pairs={{0,1},{1,0},{2,3},{3,2},{4,5},{5,4},{6,7},{7,6},{8,9},{9,8},{10,11... | collective-permute-start | bytes 3932168 | tf_op jit(solution)/shard_map/ppermute | solution.py:661
  590.0 28.9 %collective-permute-start.52 = (bf16[448,2048]{1,0:T(8,128)(2,1)}, bf16[448,2048]{1,0:T(8,128)(2,1)}, u32[]{:S(2)}, u32[]{:S(2)}) collective-permute-start(bf16[448,2048]{1,0:T(8,128)(2,1)} %get-tuple-element.120), channel_id=1, source_target_pairs={{0,2},{2,0},{4,6},{6,4},{8,10},{10,8},{12,14},{14,12},{16,18},{18,... | collective-permute-start | bytes 5505032 | tf_op jit(solution)/shard_map/ppermute | solution.py:658
  598.7 49.4 %all-to-all-start.5 = ((bf16[16,320,128]{2,1,0:T(8,128)(2,1)}), bf16[16,320,128]{2,1,0:T(8,128)(2,1)S(1)}, u32[]{:S(2)}, u32[]{:S(2)}) async-start(bf16[16,320,128]{2,1,0:T(8,128)(2,1)} %add_convert_fusion.2), calls=%async_computation.5 | async-start | bytes 2621440 | tf_op jit(solution)/shard_map/all_to_all | solution.py:712
  617.6 19.7 %collective-permute-start.54 = (bf16[1,64,2048]{2,1,0:T(8,128)(2,1)S(1)}, bf16[1,64,2048]{2,1,0:T(8,128)(2,1)S(1)}, u32[]{:S(2)}, u32[]{:S(2)}) collective-permute-start(bf16[1,64,2048]{2,1,0:T(8,128)(2,1)S(1)} %fusion.18), channel_id=1, source_target_pairs={{0,8},{2,6},{8,16},{10,2},{16,24},{18,10},{24,28},{26,18},{28,20},... | collective-permute-start | bytes 786440 | tf_op jit(solution)/shard_map/ppermute | solution.py:655
  638.5 8.5 %collective-permute-start.55 = (bf16[1,128,2048]{2,1,0:T(8,128)(2,1)S(1)}, bf16[1,128,2048]{2,1,0:T(8,128)(2,1)S(1)}, u32[]{:S(2)}, u32[]{:S(2)}) collective-permute-start(bf16[1,128,2048]{2,1,0:T(8,128)(2,1)S(1)} %fusion.10), channel_id=1, source_target_pairs={{0,8},{2,6},{8,16},{10,2},{16,24},{18,10},{24,28},{26,18},{28,20},... | collective-permute-start | bytes 1572872 | tf_op jit(solution)/shard_map/ppermute | solution.py:655
  640.5 41.3 %collective-permute-start.62 = (bf16[16,448,128]{2,1,0:T(8,128)(2,1)}, bf16[16,448,128]{2,1,0:T(8,128)(2,1)}, u32[]{:S(2)}, u32[]{:S(2)}) collective-permute-start(bf16[16,448,128]{2,1,0:T(8,128)(2,1)} %get-tuple-element.135), channel_id=1, source_target_pairs={{0,1},{1,0},{2,3},{3,2},{4,5},{5,4},{6,7},{7,6},{8,9},{9,8},{10,11... | collective-permute-start | bytes 5505032 | tf_op jit(solution)/shard_map/ppermute | solution.py:661
  650.2 8.5 %collective-permute-start.57 = (bf16[1,128,2048]{2,1,0:T(8,128)(2,1)S(1)}, bf16[1,128,2048]{2,1,0:T(8,128)(2,1)S(1)}, u32[]{:S(2)}, u32[]{:S(2)}) collective-permute-start(bf16[1,128,2048]{2,1,0:T(8,128)(2,1)S(1)} %fusion.6), channel_id=1, source_target_pairs={{0,8},{2,6},{8,16},{10,2},{16,24},{18,10},{24,28},{26,18},{28,20},... | collective-permute-start | bytes 1572872 | tf_op jit(solution)/shard_map/ppermute | solution.py:655
  660.0 8.7 %collective-permute-start.58 = (bf16[1,128,2048]{2,1,0:T(8,128)(2,1)S(1)}, bf16[1,128,2048]{2,1,0:T(8,128)(2,1)S(1)}, u32[]{:S(2)}, u32[]{:S(2)}) collective-permute-start(bf16[1,128,2048]{2,1,0:T(8,128)(2,1)S(1)} %fusion.5), channel_id=1, source_target_pairs={{0,8},{2,6},{8,16},{10,2},{16,24},{18,10},{24,28},{26,18},{28,20},... | collective-permute-start | bytes 1572872 | tf_op jit(solution)/shard_map/ppermute | solution.py:655
  668.7 15.1 %collective-permute-start.59 = (bf16[1,64,2048]{2,1,0:T(8,128)(2,1)S(1)}, bf16[1,64,2048]{2,1,0:T(8,128)(2,1)S(1)}, u32[]{:S(2)}, u32[]{:S(2)}) collective-permute-start(bf16[1,64,2048]{2,1,0:T(8,128)(2,1)S(1)} %constant_dynamic-slice_fusion.5), channel_id=1, source_target_pairs={{0,2},{2,0},{4,6},{6,4},{8,10},{10,8},{12,14},{14,12},{16,18},{18,... | collective-permute-start | bytes 786440 | tf_op jit(solution)/shard_map/ppermute | solution.py:658
  689.8 48.6 %all-to-all-start.6 = ((bf16[16,464,128]{2,1,0:T(8,128)(2,1)}), bf16[16,464,128]{2,1,0:T(8,128)(2,1)S(1)}, u32[]{:S(2)}, u32[]{:S(2)}) async-start(bf16[16,464,128]{2,1,0:T(8,128)(2,1)} %fusion.4), calls=%async_computation.6 | async-start | bytes 3801088 | tf_op jit(solution)/shard_map/all_to_all | solution.py:712
  697.0 42.6 %collective-permute-start.61 = (bf16[128,2048]{1,0:T(8,128)(2,1)S(1)}, bf16[128,2048]{1,0:T(8,128)(2,1)S(1)}, u32[]{:S(2)}, u32[]{:S(2)}) collective-permute-start(bf16[128,2048]{1,0:T(8,128)(2,1)S(1)} %maximum_select_fusion.6), channel_id=1, source_target_pairs={{0,1},{1,0},{2,3},{3,2},{4,5},{5,4},{6,7},{7,6},{8,9},{9,8},{10,11... | collective-permute-start | bytes 1572872 | tf_op jit(solution)/shard_map/ppermute | solution.py:661
  698.5 11.9 %collective-permute-start.64 = (f32[2,448]{1,0:T(2,128)S(1)}, f32[2,448]{1,0:T(2,128)S(1)}, u32[]{:S(2)}, u32[]{:S(2)}) collective-permute-start(f32[2,448]{1,0:T(2,128)S(1)} %pad_maximum_fusion.4), channel_id=1, source_target_pairs={{0,1},{1,0},{2,3},{3,2},{4,5},{5,4},{6,7},{7,6},{8,9},{9,8},{10,11... | collective-permute-start | bytes 10760 | tf_op jit(solution)/shard_map/ppermute | solution.py:661
  738.4 9.6 %collective-permute-start.63 = (f32[6,128]{1,0:T(8,128)S(1)}, f32[6,128]{1,0:T(8,128)S(1)}, u32[]{:S(2)}, u32[]{:S(2)}) collective-permute-start(f32[6,128]{1,0:T(8,128)S(1)} %convert_reduce_fusion), channel_id=1, source_target_pairs={{0,1},{1,0},{2,3},{3,2},{4,5},{5,4},{6,7},{7,6},{8,9},{9,8},{10,11... | collective-permute-start | bytes 9224 | tf_op jit(solution)/shard_map/ppermute | solution.py:661
  (63 other events, 680.5 us)

commit v6 on v5

--- a/solution.py
+++ b/solution.py
@@ -74,6 +74,7 @@
 WIDE = 2 * HEAD_DIM
 UP_ROWS = 3 * HEAD_DIM + 256
 DOWN_ROWS = HEAD_DIM + 256
+SUM_ROWS = 16
 MEMBERS = 4
 
 
@@ -300,19 +301,19 @@
         rows_in = take(9)
         grads_in = take(9)
     else:
-        heads_ref, hidden_ref = take(2)
+        heads_ref, hidden_ref, normed_ref = take(3)
         grads_in = take(9)
     if mode == "first":
         normed_ref, heads_ref, hidden_ref, wide_ref = take(4)
         outs = take(3)
         raw, part, sems = take(3)
     elif mode == "middle":
-        normed_ref, grad_rows_ref, wide_ref, slim_ref = take(4)
+        normed_ref, grad_rows_ref, wide_ref, slim_ref, sums_ref = take(5)
         outs = take(3)
         grad_outs = take(3)
         part, grad_part, sems = take(3)
     else:
-        grad_rows_ref, slim_ref = take(2)
+        grad_rows_ref, slim_ref, sums_ref = take(3)
         grad_outs = take(3)
         grad_part, sems = take(2)
 
@@ -343,6 +344,9 @@
             return carry
 
         lax.fori_loop(0, total // tile, norm_tile, 0)
+
+    if backward:
+        sums_ref[...] = jnp.zeros_like(sums_ref)
 
     def one(p, carry):
         at = pl.ds(pl.multiple_of(p * step, step), step)
@@ -387,7 +391,12 @@
         if forward:
             part[at, :] = dot(wide_ref[at, :], down_ref[...]).astype(bf16)
         if backward:
-            grad_part[at, :] = dot(slim_ref[at, :], up_ref[...], contract_last).astype(bf16)
+            grad_normed = dot(slim_ref[at, :], up_ref[...], contract_last)
+            grad_part[at, :] = grad_normed.astype(bf16)
+            for n, rows in enumerate(
+                (grad_normed, grad_normed * normed_ref[at, :].astype(f32), grad_rows_ref[at, :].astype(f32))
+            ):
+                sums_ref[n : n + 1] += jnp.sum(rows, axis=0, keepdims=True)
         return carry
 
     lax.fori_loop(0, total // step, one, 0)
@@ -412,6 +421,7 @@
         jax.ShapeDtypeStruct((4 * block, width), bf16),
     ]
     full = jax.ShapeDtypeStruct((total, width), bf16)
+    sums = jax.ShapeDtypeStruct((SUM_ROWS, width), f32)
     slim_rows = jax.ShapeDtypeStruct((total, slim), bf16)
     wide_rows = jax.ShapeDtypeStruct((total, wide), bf16)
     if mode == "first":
@@ -423,11 +433,11 @@
         ]
         buffers = 2
     elif mode == "middle":
-        kept = [full, full, wide_rows, slim_rows]
+        kept = [full, full, wide_rows, slim_rows, sums]
         parts = parts * 2
         buffers = 2
     else:
-        kept = [full, slim_rows]
+        kept = [full, slim_rows, sums]
         buffers = 1
     passes = 2 if mode == "middle" else 1
     return pl.pallas_call(
@@ -446,7 +456,10 @@
 
 
 def gradient_slabs(own_rows, other_rows, with_sums, pieces_in, core_ref, left_ref, *rest):
-    right_refs, (own_ref, other_ref, *rest) = rest[:pieces_in], rest[pieces_in:]
+    right_refs, rest = rest[:pieces_in], rest[pieces_in:]
+    if with_sums:
+        sums_ref, *rest = rest
+    own_ref, other_ref, *rest = rest
     turned_ref = rest[-1]
     if pieces_in == 1:
         right = right_refs[0][...]
@@ -473,12 +486,16 @@
             for e in range(2):
                 ref[e, place : place + last - first] = product[first:last, e * 128 : (e + 1) * 128]
             place += last - first
-
-
-def call_gradients(core, left, right, own_rows, other_rows, with_sums, name):
+        if with_sums:
+            for e in range(2):
+                ref[e, place:] = sums_ref[:, e * 128 : (e + 1) * 128].astype(bf16)
+
+
+def call_gradients(core, left, right, own_rows, other_rows, sums, name):
     total, height = left.shape
     width = right[0].shape[1]
-    rows = height // 2
+    with_sums = len(sums) > 0
+    rows = height // 2 + (SUM_ROWS if with_sums else 0)
     slab = pl.BlockSpec((2, rows, 128), lambda i: (i, 0, 0))
     shape = jax.ShapeDtypeStruct((width // 128, rows, 128), bf16)
     out_specs, out_shape = [slab, slab], [shape, shape]
@@ -489,7 +506,7 @@
         partial(gradient_slabs, own_rows, other_rows, with_sums, len(right)),
         grid=(width // 256,),
         in_specs=[SMEM_SPEC, pl.BlockSpec((total, height), lambda i: (0, 0))]
-        + [pl.BlockSpec((x.shape[0], 256), lambda i: (0, i)) for x in right],
+        + [pl.BlockSpec((x.shape[0], 256), lambda i: (0, i)) for x in (*right, *sums)],
         out_specs=out_specs,
         out_shape=out_shape,
         scratch_shapes=[pltpu.VMEM((height, total), bf16)],
@@ -497,7 +514,7 @@
             flops=4 * total * height * width, bytes_accessed=2 * (total * (width + height) + 2 * height * width), transcendentals=0
         ),
         name=name,
-    )(core, left, *right)
+    )(core, left, *right, *sums)
 
 
 def spread_gradients(up_ref, down_ref, *rest):
@@ -565,14 +582,11 @@
     normed_ref[...] = (centred * inverse * gain_ref[...] + shift_ref[...]).astype(bf16)
 
 
-def backward_end(core_ref, keep_ref, took_ref, moving_ref, got_ref, state_ref, grad_ref, gain_ref, grad_out, low_ref, sums_ref):
+def backward_end(core_ref, keep_ref, took_ref, moving_ref, got_ref, state_ref, grad_ref, gain_ref, grad_out, low_ref):
     grad_normed = ring_total(core_ref, keep_ref, took_ref, moving_ref, got_ref)
     centred, inverse = centred_rows(state_ref[...].astype(f32))
     xhat = centred * inverse
     before = grad_ref[...].astype(f32)
-    sums_ref[0:1] = jnp.sum(grad_normed * xhat, axis=0, keepdims=True)
-    sums_ref[1:2] = jnp.sum(grad_normed, axis=0, keepdims=True)
-    sums_ref[2:3] = jnp.sum(before, axis=0, keepdims=True)
     scaled = grad_normed * gain_ref[...]
     after = before + (
         scaled - jnp.mean(scaled, axis=1, keepdims=True) - xhat * jnp.mean(scaled * xhat, axis=1, keepdims=True)
@@ -825,7 +839,10 @@
     keeps = jnp.stack([jnp.ones_like(labels[0]), (labels[0] > 0).astype(labels.dtype)]).astype(bf16)
     both = both * keeps[:, :, None]
     if groups == 1:
-        inputs = gather_rows(after(both, packed_down, packed_last, *firsts), {side: (down_other,)})
+        inputs = gather_rows(
+            after(both, packed_down, packed_last, firsts[0], firsts[2]),
+            {1: (firsts[1], tables[0]), 2: (tables[1], tables[2], allowed), side: (down_other, weights[0][0])},
+        )
         slab = spread(after(packed_last, inputs[-2]))
         others = tuple(over(slab[n * GROUP // 2 : (n + 1) * GROUP // 2]) for n in range(2))
         weights.append(call_join(join_halves, slab, others, True, True))
@@ -843,27 +860,24 @@
     next_state, normed_own = call_end(
         partial(forward_end, False),
         core_word,
-        ring_sum((after(parts[0], *slabs), parts[1], parts[2]), needed={0: others[:1]})[0],
+        ring_sum((after(parts[0], *slabs), parts[1], parts[2]), needed={})[0],
         [state, added_bias[0], gains[1], shifts[1]],
         [jax.ShapeDtypeStruct(rows_shape, f32), jax.ShapeDtypeStruct(rows_shape, bf16)],
         "forward_end",
     )
-    normed_chunks = gather_rows(in_order(normed_own, across(normed_own)), {1: others[1:]})
+    normed_chunks = gather_rows(in_order(normed_own, across(normed_own)), {0: others[:1], 2: others[1:]})
 
     def handed_back(own_rows):
         filled = in_order(own_rows, across(own_rows))
         return jnp.where(tensor == core, filled, over(filled))
 
-    def summed(own, other, *earlier, extra=None):
+    def summed(own, other, *earlier):
         total = own.astype(f32) + other.astype(f32)
         if groups > 1:
             total = total.transpose(1, 0, 2).reshape(total.shape[1], width)
             total = lax.psum_scatter(total, "dp", scatter_dimension=1, axis_index_groups=outer, tiled=True)
             total = total.reshape(total.shape[0], GROUP, piece).transpose(1, 0, 2)
-        total = total.astype(bf16)
-        if extra is not None:
-            total = jnp.concatenate([total, extra], axis=1)
-        return spread(after(total, *earlier))
+        return spread(after(total.astype(bf16), *earlier))
 
     down_own = [(0, HEAD_DIM), (WIDE, WIDE + hidden)]
     down_other = [(HEAD_DIM, WIDE), (WIDE + hidden, WIDE + 2 * hidden)]
@@ -871,10 +885,10 @@
     up_other = [(p * WIDE + HEAD_DIM, (p + 1) * WIDE) for p in range(3)] + [(3 * WIDE + hidden, 3 * WIDE + 2 * hidden)]
 
     def down_gradients(wide_rows, grad_rows):
-        return call_gradients(core_word, wide_rows, grad_rows, down_own, down_other, False, "down_gradients")
-
-    def up_gradients(slim_rows, normed_rows):
-        return call_gradients(core_word, slim_rows, [normed_rows], up_own, up_other, True, "up_gradients")
+        return call_gradients(core_word, wide_rows, grad_rows, down_own, down_other, [], "down_gradients")
+
+    def up_gradients(slim_rows, normed_rows, sums):
+        return call_gradients(core_word, slim_rows, [normed_rows], up_own, up_other, [sums], "up_gradients")
 
     def backward_finish(ring_end, state, grad_state, layer):
         return call_end(
@@ -882,23 +896,19 @@
             core_word,
             ring_end,
             [state, grad_state, gains[layer]],
-            [
-                jax.ShapeDtypeStruct(rows_shape, f32),
-                jax.ShapeDtypeStruct(rows_shape, bf16),
-                jax.ShapeDtypeStruct((3, width), f32),
-            ],
+            [jax.ShapeDtypeStruct(rows_shape, f32), jax.ShapeDtypeStruct(rows_shape, bf16)],
             "backward_end",
         )
 
-    normed_last, grad_rows, wide_last, slim, *parts = call_pass(
+    normed_last, grad_rows, wide_last, slim, sums, *parts = call_pass(
         "middle", core_word, weights[1], tables, allowed, [bias_rows[1:2]], normed_chunks + inputs
     )
     out_parts = parts[:3]
     down_pair = down_gradients(wide_last, [grad_rows])
-    *up_pair, bias_last = up_gradients(slim, normed_last)
+    *up_pair, bias_last = up_gradients(slim, normed_last, sums)
     down_sent, up_sent = over(down_pair[1]), over(up_pair[1])
-    grad_end, out_end = ring_sum(parts[3:], out_parts, needed={1: (down_pair[0], up_pair[0]), 0: (down_sent,)})
-    grad_state, grad_low, sums_last = backward_finish(grad_end, next_state, grad_state, 1)
+    grad_end, out_end = ring_sum(parts[3:], out_parts, needed={1: (down_pair[0],), 0: (up_pair[0],)})
+    grad_state, grad_low = backward_finish(grad_end, next_state, grad_state, 1)
     (hidden_out,) = call_end(
         partial(forward_end, True),
         core_word,
@@ -909,31 +919,26 @@
     )
     hidden_out = handed_back(hidden_out)
     down_last = summed(down_pair[0], after(down_sent, grad_low))
-    grad_chunks = gather_rows(in_order(grad_low, across(grad_low)), {2: (up_sent,), side: (down_last, hidden_out)})
+    grad_chunks = gather_rows(in_order(grad_low, across(grad_low)), {0: (down_sent,), 2: (up_sent,), side: (down_last, hidden_out)})
     up_last = summed(up_pair[0], after(up_sent, grad_chunks[-2]), down_last)
 
     down_pair = down_gradients(wide, grad_chunks)
     down_sent = over(down_pair[1])
-    grad_rows, slim, *parts = call_pass(
-        "last", core_word, weights[0], tables, allowed, [heads, after(hidden_pre, down_pair[0])], grad_chunks
+    grad_rows, slim, sums, *parts = call_pass(
+        "last", core_word, weights[0], tables, allowed, [heads, after(hidden_pre, down_pair[0]), normed], grad_chunks
     )
     down_first = summed(down_pair[0], after(down_sent, slim), up_last)
-    *up_pair, bias_first = up_gradients(slim, after(normed, up_last))
+    *up_pair, bias_first = up_gradients(slim, after(normed, up_last), sums)
     up_sent = over(up_pair[1])
     (grad_end,) = ring_sum((after(parts[0], up_pair[0]), parts[1], parts[2]), needed={1: (down_first,)})
-    _, grad_low, sums_first = backward_finish(grad_end, state, grad_state, 0)
+    up_first = summed(up_pair[0], up_sent, down_first)
+    _, grad_low = backward_finish(grad_end, state, grad_state, 0)
     grad_hidden = handed_back(grad_low).astype(f32)
 
-    vectors = jnp.stack([sums_first, sums_last]).reshape(LAYERS * 3, n_dp, piece).transpose(1, 0, 2)
-    if groups == 1:
-        extra = jnp.pad(vectors, ((0, 0), (0, 16 - LAYERS * 3), (0, 0))).astype(bf16)
-        up_first = summed(up_pair[0], up_sent, down_first, extra=extra)
-        vectors = up_first[:, UP_ROWS : UP_ROWS + LAYERS * 3].astype(f32)
-    else:
-        up_first = summed(up_pair[0], up_sent, down_first)
-        vectors = lax.all_to_all(vectors, "dp", 0, 0, tiled=True)
-    vectors = jnp.sum(vectors, axis=0)
-    vectors = (vectors + over(vectors)).reshape(LAYERS, 3, piece)
+    ends = jnp.stack([jnp.sum(x[:, UP_ROWS : UP_ROWS + 3].astype(f32), axis=0) for x in (up_first, up_last)])
+    shift_grads = ends[:, 0]
+    gain_grads = (ends[:, 1] - norm_bias.astype(f32) * ends[:, 0]) / norm_gain.astype(f32)
+    after_grads = ends[:, 2] / GROUP
     sums = jnp.concatenate([bias_first, bias_last], axis=0)
     sums_qkv = sums[:, : 3 * WIDE].reshape(LAYERS, 3, 2, HEAD_DIM)
     sums_up = sums[:, 3 * WIDE :].reshape(LAYERS, 2, hidden)
@@ -954,21 +959,21 @@
         ups = jnp.stack([up_first, up_last]).astype(f32)
         downs = jnp.stack([down_first, down_last]).astype(f32)
         grad_qkv = ups[:, :, : 3 * HEAD_DIM].reshape(LAYERS, GROUP, 3, HEAD_DIM, piece).transpose(0, 4, 2, 1, 3).reshape(LAYERS, piece, 3, -1)
-        grad_up = ups[:, :, 3 * HEAD_DIM :].transpose(0, 3, 1, 2).reshape(LAYERS, piece, -1)
+        grad_up = ups[:, :, 3 * HEAD_DIM : UP_ROWS].transpose(0, 3, 1, 2).reshape(LAYERS, piece, -1)
         grad_out = downs[:, :, :HEAD_DIM].reshape(LAYERS, -1, piece)
         grad_down = downs[:, :, HEAD_DIM:].reshape(LAYERS, -1, piece)
     return (
         hidden_out,
         grad_hidden,
-        vectors[:, 0],
-        vectors[:, 1],
+        gain_grads,
+        shift_grads,
         grad_qkv,
         bias_qkv,
         grad_out,
         grad_up,
         bias_up,
         grad_down,
-        vectors[:, 2],
+        after_grads,
     )
 
 

time: 760 us -> 752 us (0.989)
  local copies, waits for them, and re-layouts: 32.8 us -> 22.7 us
  waiting for transfers between devices: 370 us -> 361 us
    ppermute x13 -> x12, waiting for transfers between devices: 89.4 us -> 66.1 us  [over(): return lax.ppermute(x, 'tensor', [(0, 1), (1, 0)])]
    all_to_all x7, waiting for transfers between devices: 73.9 us -> 87.4 us  [spread(): return lax.all_to_all(x, 'dp', 0, 0, axis_index_groups=inner, tiled=True)]
  transfers between devices with their start and end apart: 72 -> 71, of which waited for: 46 -> 44; matrix products, arithmetic and copies ran while one was open for 8% -> 8% of each run, Pallas kernels for 18% -> 18%
where the time goes in v6:
time: 752 us; the launch traced here: 740 us
  waiting for transfers between devices  361 us (48%)
  Pallas kernels  182 us (24%)
  starting transfers between devices  118 us (16%)
  other arithmetic  53.1 us (7%)
  local copies, waits for them, and re-layouts  22.7 us (3%)
    ppermute x24, waiting for transfers between devices, along(): return lax.ppermute(x, 'dp', ring_pairs)  194 us
    pallas_call x3, Pallas kernels, call_pass(): pl.pallas_call(partial(layer_pass, mode), in_specs=[SMEM_SPEC] + [VMEM_SP...  91.9 us
    all_to_all x7, waiting for transfers between devices, spread(): return lax.all_to_all(x, 'dp', 0, 0, axis_index_groups=inner, tiled=True)  87.4 us
    ppermute x12, waiting for transfers between devices, over(): return lax.ppermute(x, 'tensor', [(0, 1), (1, 0)])  66.1 us
    all_to_all x7, starting transfers between devices, spread(): return lax.all_to_all(x, 'dp', 0, 0, axis_index_groups=inner, tiled=True)  52.5 us
    pallas_call x4, Pallas kernels, call_gradients(): pl.pallas_call(partial(gradient_slabs, own_rows, other_rows, with_sums, l...  38 us
    ppermute x24, starting transfers between devices, along(): return lax.ppermute(x, 'dp', ring_pairs)  26.2 us
    ppermute x28, starting transfers between devices, across(): return lax.ppermute(x, 'dp', core_pairs)  25.8 us
  transfers between devices with their start and end apart: 71, of which 44 were waited for; matrix products, arithmetic and copies ran while one was open for 8% of the time, Pallas kernels for 18%

profile of v6, /device:TPU:13, one launch (start us, length us, event | category | flops | bytes accessed | tf_op | source)
XLA Modules:
  0.0 739.8 jit_solution(5279578489066028924)
XLA Ops:
  4.8 4.0 pack_first.1
  8.8 6.5 all-to-all-start
  15.3 3.5 pack_down.1
  18.9 39.7 %all-to-all-done.own_ref = bf16[16,464,128]{2,1,0:T(8,128)(2,1)S(1)} async-done(((bf16[16,464,128]{2,1,0:T(8,128)(2,1)}), bf16[16,464,128]{2,1,0:T(8,128)(2,1)S(1)}, u32[]{:S(2)}, u32[]{:S(2)}) %all-to-all-start) | async-done | bytes 1900576 | tf_op jit(solution)/shard_map/all_to_all | solution.py:726
  58.5 4.8 all-to-all-start.1
  69.3 4.4 pack_both.1
  76.4 17.9 %all-to-all-done.1.own_ref = bf16[16,320,128]{2,1,0:T(8,128)(2,1)S(1)} async-done(((bf16[16,320,128]{2,1,0:T(8,128)(2,1)}), bf16[16,320,128]{2,1,0:T(8,128)(2,1)S(1)}, u32[]{:S(2)}, u32[]{:S(2)}) %all-to-all-start.1) | async-done | bytes 1310752 | tf_op jit(solution)/shard_map/all_to_all | solution.py:726
  100.7 10.1 %collective-permute-done.2.other_ref = bf16[16,464,128]{2,1,0:T(8,128)(2,1)} collective-permute-done((bf16[16,464,128]{2,1,0:T(8,128)(2,1)S(1)}, bf16[16,464,128]{2,1,0:T(8,128)(2,1)}, u32[]{:S(2)}, u32[]{:S(2)}) %collective-permute-start.2) | collective-permute-done | bytes 1900576 | tf_op jit(solution)/shard_map/ppermute | solution.py:675
  118.0 7.1 collective-permute-done.3.refs_12_.refs_19_
  126.3 4.8 join_up.1.refs_1_
  131.1 8.1 %collective-permute-done.4.refs_13_.refs_20_ = bf16[2,128,2048]{2,1,0:T(8,128)(2,1)S(1)} collective-permute-done((bf16[2,128,2048]{2,1,0:T(8,128)(2,1)}, bf16[2,128,2048]{2,1,0:T(8,128)(2,1)S(1)}, u32[]{:S(2)}, u32[]{:S(2)}) %collective-permute-start.4) | collective-permute-done | bytes 1048608 | tf_op jit(solution)/shard_map/ppermute | solution.py:669
  139.3 2.9 collective-permute-done.5.other_ref
  143.4 7.1 collective-permute-done.6.refs_17_.refs_24_
  151.4 6.8 all-to-all-start.2
  164.6 4.2 join_down.1.refs_2_
  168.8 29.3 %pass_first.1 = (bf16[1024,2048]{1,0:T(8,128)(2,1)}, bf16[1024,384]{1,0:T(8,128)(2,1)}, f32[1024,512]{1,0:T(8,128)}, bf16[1024,640]{1,0:T(8,128)(2,1)}, bf16[64,...) custom-call(s32[1]{0:T(128)} %bitcast.refs_0_.core_ref, bf16[2048,896]{1,0:T(8,128)(2,1)} %join_up.1.refs_1_, ...), custom_call_target="tpu_custom_call" | custom-call | flops 19327352832 | bytes 20000000 | tf_op jit(solution)/shard_map/pass_first/pallas_call | solution.py:443
  198.2 29.8 %all-to-all-done.2.own_ref = bf16[16,768,128]{2,1,0:T(8,128)(2,1)S(1)} async-done(((bf16[16,768,128]{2,1,0:T(8,128)(2,1)}), bf16[16,768,128]{2,1,0:T(8,128)(2,1)S(1)}, u32[]{:S(2)}, u32[]{:S(2)}) %all-to-all-start.2) | async-done | bytes 3145760 | tf_op jit(solution)/shard_map/all_to_all | solution.py:726
  230.9 5.5 collective-permute-done.16
  238.1 8.3 %collective-permute-done.17 = bf16[1,128,2048]{2,1,0:T(8,128)(2,1)S(1)} collective-permute-done((bf16[1,128,2048]{2,1,0:T(8,128)(2,1)S(1)}, bf16[1,128,2048]{2,1,0:T(8,128)(2,1)S(1)}, u32[]{:S(2)}, u32[]{:S(2)}) %collective-permute-start.17) | collective-permute-done | bytes 524320 | tf_op jit(solution)/shard_map/ppermute | solution.py:669
  250.9 5.2 collective-permute-done.18
  258.2 8.5 %collective-permute-done.19.moving_ref = bf16[1,128,2048]{2,1,0:T(8,128)(2,1)S(1)} collective-permute-done((bf16[1,128,2048]{2,1,0:T(8,128)(2,1)}, bf16[1,128,2048]{2,1,0:T(8,128)(2,1)S(1)}, u32[]{:S(2)}, u32[]{:S(2)}) %collective-permute-start.19) | collective-permute-done | bytes 524320 | tf_op jit(solution)/shard_map/ppermute | solution.py:669
  267.5 3.5 collective-permute-start.20
  279.1 4.9 collective-permute-done.7.lower_ref
  285.1 9.1 %collective-permute-done.22.refs_9_ = bf16[128,2048]{1,0:T(8,128)(2,1)} collective-permute-done((bf16[128,2048]{1,0:T(8,128)(2,1)S(1)}, bf16[128,2048]{1,0:T(8,128)(2,1)}, u32[]{:S(2)}, u32[]{:S(2)}) %collective-permute-start.22) | collective-permute-done | bytes 524320 | tf_op jit(solution)/shard_map/ppermute | solution.py:669
  294.2 23.7 %collective-permute-done.8.upper_ref = bf16[8,768,128]{2,1,0:T(8,128)(2,1)} collective-permute-done((bf16[8,768,128]{2,1,0:T(8,128)(2,1)}, bf16[8,768,128]{2,1,0:T(8,128)(2,1)}, u32[]{:S(2)}, u32[]{:S(2)}) %collective-permute-start.8) | collective-permute-done | bytes 1572896 | tf_op jit(solution)/shard_map/ppermute | solution.py:675
  318.9 3.3 collective-permute-start.25
  322.3 5.8 collective-permute-done.24.refs_11_
  328.2 3.5 collective-permute-start.27
  333.7 2.7 collective-permute-start.29
  336.4 6.4 join_halves.1
  343.5 36.0 %pass_middle.1 = (bf16[1024,2048]{1,0:T(8,128)(2,1)}, bf16[1024,2048]{1,0:T(8,128)(2,1)}, bf16[1024,640]{1,0:T(8,128)(2,1)}, bf16[1024,896]{1,0:T(8,128)(2,1)}, ...) custom-call(s32[1]{0:T(128)} %bitcast.refs_0_.core_ref, ...), custom_call_target="tpu_custom_call" | custom-call | flops 38654705664 | bytes 40000000 | tf_op jit(solution)/shard_map/pass_middle/pallas_call | solution.py:443
  380.6 3.3 collective-permute-done.31
  393.1 3.4 collective-permute-done.33
  398.3 8.8 %down_gradients.2 = (bf16[16,320,128]{2,1,0:T(8,128)(2,1)}, bf16[16,320,128]{2,1,0:T(8,128)(2,1)}) custom-call(s32[1]{0:T(128)} %bitcast.refs_0_.core_ref, bf16[1024,640]{1,0:T(8,128)(2,1)} %get-tuple-element.104.left_ref, bf16[1024,2048]{1,0:T(8,128)(2,1)} %get-tuple-element.105.rest_0_), custom_call_target="tpu_custom_call" | custom-call | flops 5368709120 | bytes 10747904 | tf_op jit(solution)/shard_map/down_gradients/pallas_call | solution.py:505
  407.1 3.8 collective-permute-done.35
  413.1 10.1 %up_gradients.2 = (bf16[16,464,128]{2,1,0:T(8,128)(2,1)}, bf16[16,464,128]{2,1,0:T(8,128)(2,1)}, f32[1,896]{1,0:T(1,128)}) custom-call(s32[1]{0:T(128)} %bitcast.refs_0_.core_ref, bf16[1024,896]{1,0:T(8,128)(2,1)} %get-tuple-element.108.left_ref, bf16[1024,2048]{1,0:T(8,128)(2,1)} %get-tuple-element.109.rest_0_, f32[16,2048]{1,0:T(8,128)} %get-tuple-element.110.rest_1_), custom_call_target="tpu_custom_call" | custom-call | flops 7516192768 | bytes 13369344 | tf_op jit(solution)/shard_map/up_gradients/pallas_call | solution.py:505
  428.9 11.4 %collective-permute-done.37.moving_ref = bf16[2,128,2048]{2,1,0:T(8,128)(2,1)S(1)} collective-permute-done((bf16[2,128,2048]{2,1,0:T(8,128)(2,1)S(1)}, bf16[2,128,2048]{2,1,0:T(8,128)(2,1)S(1)}, u32[]{:S(2)}, u32[]{:S(2)}) %collective-permute-start.37) | collective-permute-done | bytes 1048608 | tf_op jit(solution)/shard_map/ppermute | solution.py:669
  440.4 3.5 collective-permute-start.38
  446.2 3.0 backward_end.2
  449.6 5.7 collective-permute-done.42
  455.3 2.7 add_convert_fusion.3
  458.0 12.2 %all-to-all-start.3 = ((bf16[16,320,128]{2,1,0:T(8,128)(2,1)}), bf16[16,320,128]{2,1,0:T(8,128)(2,1)S(1)}, u32[]{:S(2)}, u32[]{:S(2)}) async-start(bf16[16,320,128]{2,1,0:T(8,128)(2,1)} %add_convert_fusion.3), calls=%async_computation.3 | async-start | bytes 2621440 | tf_op jit(solution)/shard_map/all_to_all | solution.py:726
  474.6 30.2 %collective-permute-done.43.rest_1_.refs_11_ = bf16[128,2048]{1,0:T(8,128)(2,1)} collective-permute-done((bf16[128,2048]{1,0:T(8,128)(2,1)}, bf16[128,2048]{1,0:T(8,128)(2,1)}, u32[]{:S(2)}, u32[]{:S(2)}) %collective-permute-start.43) | collective-permute-done | bytes 524320 | tf_op jit(solution)/shard_map/ppermute | solution.py:669
  509.2 4.2 collective-permute-done.44.rest_2_.refs_12_
  515.3 5.7 collective-permute-done.40
  524.5 3.6 collective-permute-done.50.rest_7_.refs_17_
  528.1 3.3 add_convert_fusion.1
  531.4 8.8 %all-to-all-start.4 = ((bf16[16,464,128]{2,1,0:T(8,128)(2,1)}), bf16[16,464,128]{2,1,0:T(8,128)(2,1)S(1)}, u32[]{:S(2)}, u32[]{:S(2)}) async-start(bf16[16,464,128]{2,1,0:T(8,128)(2,1)} %add_convert_fusion.1), calls=%async_computation.4 | async-start | bytes 3801088 | tf_op jit(solution)/shard_map/all_to_all | solution.py:726
  544.7 8.9 %down_gradients.3 = (bf16[16,320,128]{2,1,0:T(8,128)(2,1)}, bf16[16,320,128]{2,1,0:T(8,128)(2,1)}) custom-call(s32[1]{0:T(128)} %bitcast.refs_0_.core_ref, bf16[1024,640]{1,0:T(8,128)(2,1)} %get-tuple-element.116.left_ref, bf16[128,2048]{1,0:T(8,128)(2,1)} %maximum_select_fusion.4.rest_0_.refs_10_, ...), custom_call_target="tpu_custom_call" | custom-call | flops 5368709120 | bytes 10747904 | tf_op jit(solution)/shard_map/down_gradients/pallas_call | solution.py:505
  554.9 26.6 %pass_last.1 = (bf16[1024,2048]{1,0:T(8,128)(2,1)}, bf16[1024,896]{1,0:T(8,128)(2,1)}, f32[16,2048]{1,0:T(8,128)}, bf16[64,2048]{1,0:T(8,128)(2,1)}, bf16[448,20...) custom-call(s32[1]{0:T(128)} %bitcast.refs_0_.core_ref, bf16[2048,896]{1,0:T(8,128)(2,1)} %join_up.1.refs_1_, ...), custom_call_target="tpu_custom_call" | custom-call | flops 19327352832 | bytes 20000000 | tf_op jit(solution)/shard_map/pass_last/pallas_call | solution.py:443
  584.0 2.8 add_convert_fusion.2
  586.7 6.8 all-to-all-start.5
  593.5 10.2 %up_gradients.3 = (bf16[16,464,128]{2,1,0:T(8,128)(2,1)}, bf16[16,464,128]{2,1,0:T(8,128)(2,1)}, f32[1,896]{1,0:T(1,128)}) custom-call(s32[1]{0:T(128)} %bitcast.refs_0_.core_ref, bf16[1024,896]{1,0:T(8,128)(2,1)} %get-tuple-element.130.left_ref, bf16[1024,2048]{1,0:T(8,128)(2,1)} %get-tuple-element.133.refs_9_.rest_0_, f32[16,2048]{1,0:T(8,128)} %get-tuple-element.134.rest_1_), custom_call_target="tpu_custom_call" | custom-call | flops 7516192768 | bytes 13369344 | tf_op jit(solution)/shard_map/up_gradients/pallas_call | solution.py:505
  607.9 17.4 %collective-permute-done.54 = bf16[1,64,2048]{2,1,0:T(8,128)(2,1)S(1)} collective-permute-done((bf16[1,64,2048]{2,1,0:T(8,128)(2,1)S(1)}, bf16[1,64,2048]{2,1,0:T(8,128)(2,1)S(1)}, u32[]{:S(2)}, u32[]{:S(2)}) %collective-permute-start.54) | collective-permute-done | bytes 262176 | tf_op jit(solution)/shard_map/ppermute | solution.py:669
  629.1 6.1 collective-permute-done.55
  636.3 3.0 fusion.4
  641.6 5.8 collective-permute-done.62
  647.3 3.3 add_convert_fusion
  650.6 6.6 all-to-all-start.6
  660.1 44.3 %collective-permute-done.58.moving_ref = bf16[1,128,2048]{2,1,0:T(8,128)(2,1)S(1)} collective-permute-done((bf16[1,128,2048]{2,1,0:T(8,128)(2,1)S(1)}, bf16[1,128,2048]{2,1,0:T(8,128)(2,1)S(1)}, u32[]{:S(2)}, u32[]{:S(2)}) %collective-permute-start.58) | collective-permute-done | bytes 524320 | tf_op jit(solution)/shard_map/ppermute | solution.py:669
  708.7 2.9 backward_end.3
  716.3 7.3 spread_gradients.2
  723.6 4.1 collective-permute-done.63
  732.1 7.3 spread_gradients.3
  (310 shorter events, 133.6 us)
Async XLA Ops:
  8.8 49.7 %all-to-all-start = ((bf16[16,464,128]{2,1,0:T(8,128)(2,1)}), bf16[16,464,128]{2,1,0:T(8,128)(2,1)S(1)}, u32[]{:S(2)}, u32[]{:S(2)}) async-start(bf16[16,464,128]{2,1,0:T(8,128)(2,1)} %pack_first.1), calls=%async_computation | async-start | bytes 3801088 | tf_op jit(solution)/shard_map/all_to_all | solution.py:726
  58.5 35.7 %all-to-all-start.1 = ((bf16[16,320,128]{2,1,0:T(8,128)(2,1)}), bf16[16,320,128]{2,1,0:T(8,128)(2,1)S(1)}, u32[]{:S(2)}, u32[]{:S(2)}) async-start(bf16[16,320,128]{2,1,0:T(8,128)(2,1)} %pack_down.1), calls=%async_computation.1 | async-start | bytes 2621440 | tf_op jit(solution)/shard_map/all_to_all | solution.py:726
  65.6 8.2 %collective-permute-start = (bf16[2,128,2048]{2,1,0:T(8,128)(2,1)}, bf16[2,128,2048]{2,1,0:T(8,128)(2,1)}, u32[]{:S(2)}, u32[]{:S(2)}) collective-permute-start(bf16[2,128,2048]{2,1,0:T(8,128)(2,1)} %pad_maximum_fusion), channel_id=1, source_target_pairs={{0,2},{2,0},{4,6},{6,4},{8,10},{10,8},{12,14},{14,12},{16,18},{18,... | collective-permute-start | bytes 3145736 | tf_op jit(solution)/shard_map/ppermute | solution.py:672
  67.9 43.0 %collective-permute-start.2 = (bf16[16,464,128]{2,1,0:T(8,128)(2,1)S(1)}, bf16[16,464,128]{2,1,0:T(8,128)(2,1)}, u32[]{:S(2)}, u32[]{:S(2)}) collective-permute-start(bf16[16,464,128]{2,1,0:T(8,128)(2,1)S(1)} %all-to-all-done.own_ref), channel_id=1, source_target_pairs={{0,1},{1,0},{2,3},{3,2},{4,5},{5,4},{6,7},{7,6},{8,9},{9,8},{10,11... | collective-permute-start | bytes 5701640 | tf_op jit(solution)/shard_map/ppermute | solution.py:675
  94.3 16.6 %collective-permute-start.1 = (bf16[2,128,2048]{2,1,0:T(8,128)(2,1)}, bf16[2,128,2048]{2,1,0:T(8,128)(2,1)}, u32[]{:S(2)}, u32[]{:S(2)}) collective-permute-start(bf16[2,128,2048]{2,1,0:T(8,128)(2,1)} %select_multiply_fusion.refs_10_.refs_17_), channel_id=1, source_target_pairs={{0,8},{2,6},{8,16},{10,2},{16,24},{18,10},{24,28},{26,18},{28,20},... | collective-permute-start | bytes 3145736 | tf_op jit(solution)/shard_map/ppermute | solution.py:669
  110.9 14.3 %collective-permute-start.3 = (bf16[2,128,2048]{2,1,0:T(8,128)(2,1)}, bf16[2,128,2048]{2,1,0:T(8,128)(2,1)}, u32[]{:S(2)}, u32[]{:S(2)}) collective-permute-start(bf16[2,128,2048]{2,1,0:T(8,128)(2,1)} %collective-permute-done.1.refs_11_.refs_18_), channel_id=1, source_target_pairs={{0,8},{2,6},{8,16},{10,2},{16,24},{18,10},{24,28},{26,18},{28,20},... | collective-permute-start | bytes 3145736 | tf_op jit(solution)/shard_map/ppermute | solution.py:669
  112.0 30.2 %collective-permute-start.5 = (bf16[16,320,128]{2,1,0:T(8,128)(2,1)}, bf16[16,320,128]{2,1,0:T(8,128)(2,1)S(1)}, u32[]{:S(2)}, u32[]{:S(2)}) collective-permute-start(bf16[16,320,128]{2,1,0:T(8,128)(2,1)} %copy-done.10), channel_id=1, source_target_pairs={{0,1},{1,0},{2,3},{3,2},{4,5},{5,4},{6,7},{7,6},{8,9},{9,8},{10,11... | collective-permute-start | bytes 3932168 | tf_op jit(solution)/shard_map/ppermute | solution.py:675
  125.1 14.2 %collective-permute-start.4 = (bf16[2,128,2048]{2,1,0:T(8,128)(2,1)}, bf16[2,128,2048]{2,1,0:T(8,128)(2,1)S(1)}, u32[]{:S(2)}, u32[]{:S(2)}) collective-permute-start(bf16[2,128,2048]{2,1,0:T(8,128)(2,1)} %collective-permute-done.3.refs_12_.refs_19_), channel_id=1, source_target_pairs={{0,8},{2,6},{8,16},{10,2},{16,24},{18,10},{24,28},{26,18},{28,20},... | collective-permute-start | bytes 3145736 | tf_op jit(solution)/shard_map/ppermute | solution.py:669
  142.2 8.3 %collective-permute-start.6 = (bf16[2,64,2048]{2,1,0:T(8,128)(2,1)S(1)}, bf16[2,64,2048]{2,1,0:T(8,128)(2,1)S(1)}, u32[]{:S(2)}, u32[]{:S(2)}) collective-permute-start(bf16[2,64,2048]{2,1,0:T(8,128)(2,1)S(1)} %constant_dynamic-slice_fusion.4), channel_id=1, source_target_pairs={{0,8},{2,6},{8,16},{10,2},{16,24},{18,10},{24,28},{26,18},{28,20},... | collective-permute-start | bytes 1572872 | tf_op jit(solution)/shard_map/ppermute | solution.py:669
  151.4 76.7 %all-to-all-start.2 = ((bf16[16,768,128]{2,1,0:T(8,128)(2,1)}), bf16[16,768,128]{2,1,0:T(8,128)(2,1)S(1)}, u32[]{:S(2)}, u32[]{:S(2)}) async-start(bf16[16,768,128]{2,1,0:T(8,128)(2,1)} %pack_both.1), calls=%async_computation.2 | async-start | bytes 6291456 | tf_op jit(solution)/shard_map/all_to_all | solution.py:726
  158.3 10.5 %collective-permute-start.10 = (bf16[2,128,2048]{2,1,0:T(8,128)(2,1)}, bf16[2,128,2048]{2,1,0:T(8,128)(2,1)}, u32[]{:S(2)}, u32[]{:S(2)}) collective-permute-start(bf16[2,128,2048]{2,1,0:T(8,128)(2,1)} %collective-permute-done.1.refs_11_.refs_18_), channel_id=1, source_target_pairs={{0,2},{2,0},{4,6},{6,4},{8,10},{10,8},{12,14},{14,12},{16,18},{18,... | collective-permute-start | bytes 3145736 | tf_op jit(solution)/shard_map/ppermute | solution.py:672
  158.6 10.1 %collective-permute-start.11 = (bf16[2,128,2048]{2,1,0:T(8,128)(2,1)}, bf16[2,128,2048]{2,1,0:T(8,128)(2,1)}, u32[]{:S(2)}, u32[]{:S(2)}) collective-permute-start(bf16[2,128,2048]{2,1,0:T(8,128)(2,1)} %collective-permute-done.3.refs_12_.refs_19_), channel_id=1, source_target_pairs={{0,2},{2,0},{4,6},{6,4},{8,10},{10,8},{12,14},{14,12},{16,18},{18,... | collective-permute-start | bytes 3145736 | tf_op jit(solution)/shard_map/ppermute | solution.py:672
  158.8 10.0 %collective-permute-start.12 = (bf16[2,128,2048]{2,1,0:T(8,128)(2,1)}, bf16[2,128,2048]{2,1,0:T(8,128)(2,1)}, u32[]{:S(2)}, u32[]{:S(2)}) collective-permute-start(bf16[2,128,2048]{2,1,0:T(8,128)(2,1)} %copy-done.28), channel_id=1, source_target_pairs={{0,2},{2,0},{4,6},{6,4},{8,10},{10,8},{12,14},{14,12},{16,18},{18,... | collective-permute-start | bytes 3145736 | tf_op jit(solution)/shard_map/ppermute | solution.py:672
  162.9 6.0 collective-permute-start.13
  198.1 32.8 %collective-permute-start.14 = (bf16[448,2048]{1,0:T(8,128)(2,1)}, bf16[448,2048]{1,0:T(8,128)(2,1)}, u32[]{:S(2)}, u32[]{:S(2)}) collective-permute-start(bf16[448,2048]{1,0:T(8,128)(2,1)} %get-tuple-element.92), channel_id=1, source_target_pairs={{0,2},{2,0},{4,6},{6,4},{8,10},{10,8},{12,14},{14,12},{16,18},{18,... | collective-permute-start | bytes 5505032 | tf_op jit(solution)/shard_map/ppermute | solution.py:672
  230.8 5.6 collective-permute-start.16
  237.9 8.6 %collective-permute-start.17 = (bf16[1,128,2048]{2,1,0:T(8,128)(2,1)S(1)}, bf16[1,128,2048]{2,1,0:T(8,128)(2,1)S(1)}, u32[]{:S(2)}, u32[]{:S(2)}) collective-permute-start(bf16[1,128,2048]{2,1,0:T(8,128)(2,1)S(1)} %fusion.7), channel_id=1, source_target_pairs={{0,8},{2,6},{8,16},{10,2},{16,24},{18,10},{24,28},{26,18},{28,20},... | collective-permute-start | bytes 1572872 | tf_op jit(solution)/shard_map/ppermute | solution.py:669
  247.7 8.4 %collective-permute-start.18 = (bf16[1,128,2048]{2,1,0:T(8,128)(2,1)S(1)}, bf16[1,128,2048]{2,1,0:T(8,128)(2,1)S(1)}, u32[]{:S(2)}, u32[]{:S(2)}) collective-permute-start(bf16[1,128,2048]{2,1,0:T(8,128)(2,1)S(1)} %fusion.6), channel_id=1, source_target_pairs={{0,8},{2,6},{8,16},{10,2},{16,24},{18,10},{24,28},{26,18},{28,20},... | collective-permute-start | bytes 1572872 | tf_op jit(solution)/shard_map/ppermute | solution.py:669
  249.7 34.3 %collective-permute-start.7 = (bf16[8,768,128]{2,1,0:T(8,128)(2,1)}, bf16[8,768,128]{2,1,0:T(8,128)(2,1)S(1)}, u32[]{:S(2)}, u32[]{:S(2)}) collective-permute-start(bf16[8,768,128]{2,1,0:T(8,128)(2,1)} %get-tuple-element.210), channel_id=1, source_target_pairs={{0,1},{1,0},{2,3},{3,2},{4,5},{5,4},{6,7},{7,6},{8,9},{9,8},{10,11... | collective-permute-start | bytes 4718600 | tf_op jit(solution)/shard_map/ppermute | solution.py:675
  258.2 8.5 %collective-permute-start.19 = (bf16[1,128,2048]{2,1,0:T(8,128)(2,1)}, bf16[1,128,2048]{2,1,0:T(8,128)(2,1)S(1)}, u32[]{:S(2)}, u32[]{:S(2)}) collective-permute-start(bf16[1,128,2048]{2,1,0:T(8,128)(2,1)} %fusion.5), channel_id=1, source_target_pairs={{0,8},{2,6},{8,16},{10,2},{16,24},{18,10},{24,28},{26,18},{28,20},... | collective-permute-start | bytes 1572872 | tf_op jit(solution)/shard_map/ppermute | solution.py:669
  267.5 5.6 collective-permute-start.20
  271.0 46.8 %collective-permute-start.8 = (bf16[8,768,128]{2,1,0:T(8,128)(2,1)}, bf16[8,768,128]{2,1,0:T(8,128)(2,1)}, u32[]{:S(2)}, u32[]{:S(2)}) collective-permute-start(bf16[8,768,128]{2,1,0:T(8,128)(2,1)} %get-tuple-element.209), channel_id=1, source_target_pairs={{0,1},{1,0},{2,3},{3,2},{4,5},{5,4},{6,7},{7,6},{8,9},{9,8},{10,11... | collective-permute-start | bytes 4718600 | tf_op jit(solution)/shard_map/ppermute | solution.py:675
  284.1 10.1 %collective-permute-start.22 = (bf16[128,2048]{1,0:T(8,128)(2,1)S(1)}, bf16[128,2048]{1,0:T(8,128)(2,1)}, u32[]{:S(2)}, u32[]{:S(2)}) collective-permute-start(bf16[128,2048]{1,0:T(8,128)(2,1)S(1)} %maximum_select_fusion.2.refs_8_), channel_id=1, source_target_pairs={{0,8},{2,6},{8,16},{10,2},{16,24},{18,10},{24,28},{26,18},{28,20},... | collective-permute-start | bytes 1572872 | tf_op jit(solution)/shard_map/ppermute | solution.py:669
  294.2 23.7 %collective-permute-start.23 = (bf16[128,2048]{1,0:T(8,128)(2,1)}, bf16[128,2048]{1,0:T(8,128)(2,1)}, u32[]{:S(2)}, u32[]{:S(2)}) collective-permute-start(bf16[128,2048]{1,0:T(8,128)(2,1)} %collective-permute-done.22.refs_9_), channel_id=1, source_target_pairs={{0,8},{2,6},{8,16},{10,2},{16,24},{18,10},{24,28},{26,18},{28,20},... | collective-permute-start | bytes 1572872 | tf_op jit(solution)/shard_map/ppermute | solution.py:669
  317.9 10.2 %collective-permute-start.24 = (bf16[128,2048]{1,0:T(8,128)(2,1)}, bf16[128,2048]{1,0:T(8,128)(2,1)S(1)}, u32[]{:S(2)}, u32[]{:S(2)}) collective-permute-start(bf16[128,2048]{1,0:T(8,128)(2,1)} %collective-permute-done.23.refs_10_), channel_id=1, source_target_pairs={{0,8},{2,6},{8,16},{10,2},{16,24},{18,10},{24,28},{26,18},{28,20},... | collective-permute-start | bytes 1572872 | tf_op jit(solution)/shard_map/ppermute | solution.py:669
  318.9 23.8 %collective-permute-start.25 = (bf16[128,2048]{1,0:T(8,128)(2,1)}, bf16[128,2048]{1,0:T(8,128)(2,1)}, u32[]{:S(2)}, u32[]{:S(2)}) collective-permute-start(bf16[128,2048]{1,0:T(8,128)(2,1)} %collective-permute-done.22.refs_9_), channel_id=1, source_target_pairs={{0,2},{2,0},{4,6},{6,4},{8,10},{10,8},{12,14},{14,12},{16,18},{18,... | collective-permute-start | bytes 1572872 | tf_op jit(solution)/shard_map/ppermute | solution.py:672
  322.3 20.5 %collective-permute-start.26 = (bf16[128,2048]{1,0:T(8,128)(2,1)}, bf16[128,2048]{1,0:T(8,128)(2,1)}, u32[]{:S(2)}, u32[]{:S(2)}) collective-permute-start(bf16[128,2048]{1,0:T(8,128)(2,1)} %collective-permute-done.23.refs_10_), channel_id=1, source_target_pairs={{0,2},{2,0},{4,6},{6,4},{8,10},{10,8},{12,14},{14,12},{16,18},{18,... | collective-permute-start | bytes 1572872 | tf_op jit(solution)/shard_map/ppermute | solution.py:672
  328.1 5.6 collective-permute-start.28
  328.2 14.6 %collective-permute-start.27 = (bf16[128,2048]{1,0:T(8,128)(2,1)S(1)}, bf16[128,2048]{1,0:T(8,128)(2,1)}, u32[]{:S(2)}, u32[]{:S(2)}) collective-permute-start(bf16[128,2048]{1,0:T(8,128)(2,1)S(1)} %collective-permute-done.24.refs_11_), channel_id=1, source_target_pairs={{0,2},{2,0},{4,6},{6,4},{8,10},{10,8},{12,14},{14,12},{16,18},{18,... | collective-permute-start | bytes 1572872 | tf_op jit(solution)/shard_map/ppermute | solution.py:672
  333.7 9.1 %collective-permute-start.29 = (bf16[64,2048]{1,0:T(8,128)(2,1)S(1)}, bf16[64,2048]{1,0:T(8,128)(2,1)S(1)}, u32[]{:S(2)}, u32[]{:S(2)}) collective-permute-start(bf16[64,2048]{1,0:T(8,128)(2,1)S(1)} %collective-permute-done.28.refs_15_), channel_id=1, source_target_pairs={{0,2},{2,0},{4,6},{6,4},{8,10},{10,8},{12,14},{14,12},{16,18},{18,... | collective-permute-start | bytes 786440 | tf_op jit(solution)/shard_map/ppermute | solution.py:672
  379.5 10.0 %collective-permute-start.34 = (bf16[448,2048]{1,0:T(8,128)(2,1)}, bf16[448,2048]{1,0:T(8,128)(2,1)S(1)}, u32[]{:S(2)}, u32[]{:S(2)}) collective-permute-start(bf16[448,2048]{1,0:T(8,128)(2,1)} %get-tuple-element.103), channel_id=1, source_target_pairs={{0,2},{2,0},{4,6},{6,4},{8,10},{10,8},{12,14},{14,12},{16,18},{18,... | collective-permute-start | bytes 5505032 | tf_op jit(solution)/shard_map/ppermute | solution.py:672
  379.7 4.3 collective-permute-start.31
  380.1 11.0 %collective-permute-start.30 = (bf16[448,2048]{1,0:T(8,128)(2,1)}, bf16[448,2048]{1,0:T(8,128)(2,1)S(1)}, u32[]{:S(2)}, u32[]{:S(2)}) collective-permute-start(bf16[448,2048]{1,0:T(8,128)(2,1)} %get-tuple-element.99), channel_id=1, source_target_pairs={{0,2},{2,0},{4,6},{6,4},{8,10},{10,8},{12,14},{14,12},{16,18},{18,... | collective-permute-start | bytes 5505032 | tf_op jit(solution)/shard_map/ppermute | solution.py:672
  380.2 6.8 collective-permute-start.32
  388.1 8.4 %collective-permute-start.33 = (bf16[2,64,2048]{2,1,0:T(8,128)(2,1)S(1)}, bf16[2,64,2048]{2,1,0:T(8,128)(2,1)S(1)}, u32[]{:S(2)}, u32[]{:S(2)}) collective-permute-start(bf16[2,64,2048]{2,1,0:T(8,128)(2,1)S(1)} %pad_maximum_fusion.1), channel_id=1, source_target_pairs={{0,8},{2,6},{8,16},{10,2},{16,24},{18,10},{24,28},{26,18},{28,20},... | collective-permute-start | bytes 1572872 | tf_op jit(solution)/shard_map/ppermute | solution.py:669
  396.8 14.0 %collective-permute-start.35 = (bf16[2,128,2048]{2,1,0:T(8,128)(2,1)S(1)}, bf16[2,128,2048]{2,1,0:T(8,128)(2,1)S(1)}, u32[]{:S(2)}, u32[]{:S(2)}) collective-permute-start(bf16[2,128,2048]{2,1,0:T(8,128)(2,1)S(1)} %fusion), channel_id=1, source_target_pairs={{0,8},{2,6},{8,16},{10,2},{16,24},{18,10},{24,28},{26,18},{28,20},... | collective-permute-start | bytes 3145736 | tf_op jit(solution)/shard_map/ppermute | solution.py:669
  411.4 14.2 %collective-permute-start.36 = (bf16[2,128,2048]{2,1,0:T(8,128)(2,1)S(1)}, bf16[2,128,2048]{2,1,0:T(8,128)(2,1)S(1)}, u32[]{:S(2)}, u32[]{:S(2)}) collective-permute-start(bf16[2,128,2048]{2,1,0:T(8,128)(2,1)S(1)} %fusion.1), channel_id=1, source_target_pairs={{0,8},{2,6},{8,16},{10,2},{16,24},{18,10},{24,28},{26,18},{28,20},... | collective-permute-start | bytes 3145736 | tf_op jit(solution)/shard_map/ppermute | solution.py:669
  426.2 14.1 %collective-permute-start.37 = (bf16[2,128,2048]{2,1,0:T(8,128)(2,1)S(1)}, bf16[2,128,2048]{2,1,0:T(8,128)(2,1)S(1)}, u32[]{:S(2)}, u32[]{:S(2)}) collective-permute-start(bf16[2,128,2048]{2,1,0:T(8,128)(2,1)S(1)} %fusion.2), channel_id=1, source_target_pairs={{0,8},{2,6},{8,16},{10,2},{16,24},{18,10},{24,28},{26,18},{28,20},... | collective-permute-start | bytes 3145736 | tf_op jit(solution)/shard_map/ppermute | solution.py:669
  427.6 27.6 %collective-permute-start.42 = (bf16[16,320,128]{2,1,0:T(8,128)(2,1)}, bf16[16,320,128]{2,1,0:T(8,128)(2,1)}, u32[]{:S(2)}, u32[]{:S(2)}) collective-permute-start(bf16[16,320,128]{2,1,0:T(8,128)(2,1)} %get-tuple-element.118), channel_id=1, source_target_pairs={{0,1},{1,0},{2,3},{3,2},{4,5},{5,4},{6,7},{7,6},{8,9},{9,8},{10,11... | collective-permute-start | bytes 3932168 | tf_op jit(solution)/shard_map/ppermute | solution.py:675
  440.4 5.1 collective-permute-start.38
  443.9 65.3 %collective-permute-start.45 = (bf16[16,464,128]{2,1,0:T(8,128)(2,1)}, bf16[16,464,128]{2,1,0:T(8,128)(2,1)}, u32[]{:S(2)}, u32[]{:S(2)}) collective-permute-start(bf16[16,464,128]{2,1,0:T(8,128)(2,1)} %get-tuple-element.120), channel_id=1, source_target_pairs={{0,1},{1,0},{2,3},{3,2},{4,5},{5,4},{6,7},{7,6},{8,9},{9,8},{10,11... | collective-permute-start | bytes 5701640 | tf_op jit(solution)/shard_map/ppermute | solution.py:675
  449.2 20.9 %collective-permute-start.41 = (bf16[64,2048]{1,0:T(8,128)(2,1)}, bf16[64,2048]{1,0:T(8,128)(2,1)S(1)}, u32[]{:S(2)}, u32[]{:S(2)}) collective-permute-start(bf16[64,2048]{1,0:T(8,128)(2,1)} %get-tuple-element.117), channel_id=1, source_target_pairs={{0,2},{2,0},{4,6},{6,4},{8,10},{10,8},{12,14},{14,12},{16,18},{18,... | collective-permute-start | bytes 786440 | tf_op jit(solution)/shard_map/ppermute | solution.py:672
  458.0 64.7 %all-to-all-start.3 = ((bf16[16,320,128]{2,1,0:T(8,128)(2,1)}), bf16[16,320,128]{2,1,0:T(8,128)(2,1)S(1)}, u32[]{:S(2)}, u32[]{:S(2)}) async-start(bf16[16,320,128]{2,1,0:T(8,128)(2,1)} %add_convert_fusion.3), calls=%async_computation.3 | async-start | bytes 2621440 | tf_op jit(solution)/shard_map/all_to_all | solution.py:726
  471.1 33.7 %collective-permute-start.43 = (bf16[128,2048]{1,0:T(8,128)(2,1)}, bf16[128,2048]{1,0:T(8,128)(2,1)}, u32[]{:S(2)}, u32[]{:S(2)}) collective-permute-start(bf16[128,2048]{1,0:T(8,128)(2,1)} %maximum_select_fusion.4.rest_0_.refs_10_), channel_id=1, source_target_pairs={{0,8},{2,6},{8,16},{10,2},{16,24},{18,10},{24,28},{26,18},{28,20},... | collective-permute-start | bytes 1572872 | tf_op jit(solution)/shard_map/ppermute | solution.py:669
  474.6 32.1 %collective-permute-start.39 = (bf16[64,2048]{1,0:T(8,128)(2,1)}, bf16[64,2048]{1,0:T(8,128)(2,1)S(1)}, u32[]{:S(2)}, u32[]{:S(2)}) collective-permute-start(bf16[64,2048]{1,0:T(8,128)(2,1)} %forward_out.1), channel_id=1, source_target_pairs={{0,2},{2,0},{4,6},{6,4},{8,10},{10,8},{12,14},{14,12},{16,18},{18,... | collective-permute-start | bytes 786440 | tf_op jit(solution)/shard_map/ppermute | solution.py:672
  504.8 8.5 %collective-permute-start.44 = (bf16[128,2048]{1,0:T(8,128)(2,1)}, bf16[128,2048]{1,0:T(8,128)(2,1)S(1)}, u32[]{:S(2)}, u32[]{:S(2)}) collective-permute-start(bf16[128,2048]{1,0:T(8,128)(2,1)} %collective-permute-done.43.rest_1_.refs_11_), channel_id=1, source_target_pairs={{0,8},{2,6},{8,16},{10,2},{16,24},{18,10},{24,28},{26,18},{28,20},... | collective-permute-start | bytes 1572872 | tf_op jit(solution)/shard_map/ppermute | solution.py:669
  507.9 13.1 %collective-permute-start.40 = (bf16[128,2048]{1,0:T(8,128)(2,1)S(1)}, bf16[128,2048]{1,0:T(8,128)(2,1)S(1)}, u32[]{:S(2)}, u32[]{:S(2)}) collective-permute-start(bf16[128,2048]{1,0:T(8,128)(2,1)S(1)} %maximum_select_fusion.3), channel_id=1, source_target_pairs={{0,1},{1,0},{2,3},{3,2},{4,5},{5,4},{6,7},{7,6},{8,9},{9,8},{10,11... | collective-permute-start | bytes 1572872 | tf_op jit(solution)/shard_map/ppermute | solution.py:675
  513.4 8.5 %collective-permute-start.46 = (bf16[128,2048]{1,0:T(8,128)(2,1)S(1)}, bf16[128,2048]{1,0:T(8,128)(2,1)S(1)}, u32[]{:S(2)}, u32[]{:S(2)}) collective-permute-start(bf16[128,2048]{1,0:T(8,128)(2,1)S(1)} %collective-permute-done.44.rest_2_.refs_12_), channel_id=1, source_target_pairs={{0,8},{2,6},{8,16},{10,2},{16,24},{18,10},{24,28},{26,18},{28,20},... | collective-permute-start | bytes 1572872 | tf_op jit(solution)/shard_map/ppermute | solution.py:669
  522.7 5.4 collective-permute-start.50
  531.4 55.3 %all-to-all-start.4 = ((bf16[16,464,128]{2,1,0:T(8,128)(2,1)}), bf16[16,464,128]{2,1,0:T(8,128)(2,1)S(1)}, u32[]{:S(2)}, u32[]{:S(2)}) async-start(bf16[16,464,128]{2,1,0:T(8,128)(2,1)} %add_convert_fusion.1), calls=%async_computation.4 | async-start | bytes 3801088 | tf_op jit(solution)/shard_map/all_to_all | solution.py:726
  540.7 3.2 collective-permute-start.49
  541.1 3.3 collective-permute-start.51
  553.6 30.3 %collective-permute-start.56 = (bf16[16,320,128]{2,1,0:T(8,128)(2,1)}, bf16[16,320,128]{2,1,0:T(8,128)(2,1)}, u32[]{:S(2)}, u32[]{:S(2)}) collective-permute-start(bf16[16,320,128]{2,1,0:T(8,128)(2,1)} %get-tuple-element.137), channel_id=1, source_target_pairs={{0,1},{1,0},{2,3},{3,2},{4,5},{5,4},{6,7},{7,6},{8,9},{9,8},{10,11... | collective-permute-start | bytes 3932168 | tf_op jit(solution)/shard_map/ppermute | solution.py:675
  581.5 26.4 %collective-permute-start.52 = (bf16[448,2048]{1,0:T(8,128)(2,1)}, bf16[448,2048]{1,0:T(8,128)(2,1)}, u32[]{:S(2)}, u32[]{:S(2)}) collective-permute-start(bf16[448,2048]{1,0:T(8,128)(2,1)} %get-tuple-element.128), channel_id=1, source_target_pairs={{0,2},{2,0},{4,6},{6,4},{8,10},{10,8},{12,14},{14,12},{16,18},{18,... | collective-permute-start | bytes 5505032 | tf_op jit(solution)/shard_map/ppermute | solution.py:672
  586.7 49.5 %all-to-all-start.5 = ((bf16[16,320,128]{2,1,0:T(8,128)(2,1)}), bf16[16,320,128]{2,1,0:T(8,128)(2,1)S(1)}, u32[]{:S(2)}, u32[]{:S(2)}) async-start(bf16[16,320,128]{2,1,0:T(8,128)(2,1)} %add_convert_fusion.2), calls=%async_computation.5 | async-start | bytes 2621440 | tf_op jit(solution)/shard_map/all_to_all | solution.py:726
  604.1 43.2 %collective-permute-start.62 = (bf16[16,464,128]{2,1,0:T(8,128)(2,1)}, bf16[16,464,128]{2,1,0:T(8,128)(2,1)}, u32[]{:S(2)}, u32[]{:S(2)}) collective-permute-start(bf16[16,464,128]{2,1,0:T(8,128)(2,1)} %get-tuple-element.143), channel_id=1, source_target_pairs={{0,1},{1,0},{2,3},{3,2},{4,5},{5,4},{6,7},{7,6},{8,9},{9,8},{10,11... | collective-permute-start | bytes 5701640 | tf_op jit(solution)/shard_map/ppermute | solution.py:675
  606.4 18.9 %collective-permute-start.54 = (bf16[1,64,2048]{2,1,0:T(8,128)(2,1)S(1)}, bf16[1,64,2048]{2,1,0:T(8,128)(2,1)S(1)}, u32[]{:S(2)}, u32[]{:S(2)}) collective-permute-start(bf16[1,64,2048]{2,1,0:T(8,128)(2,1)S(1)} %fusion.16), channel_id=1, source_target_pairs={{0,8},{2,6},{8,16},{10,2},{16,24},{18,10},{24,28},{26,18},{28,20},... | collective-permute-start | bytes 786440 | tf_op jit(solution)/shard_map/ppermute | solution.py:669
  626.7 8.5 %collective-permute-start.55 = (bf16[1,128,2048]{2,1,0:T(8,128)(2,1)S(1)}, bf16[1,128,2048]{2,1,0:T(8,128)(2,1)S(1)}, u32[]{:S(2)}, u32[]{:S(2)}) collective-permute-start(bf16[1,128,2048]{2,1,0:T(8,128)(2,1)S(1)} %fusion.8), channel_id=1, source_target_pairs={{0,8},{2,6},{8,16},{10,2},{16,24},{18,10},{24,28},{26,18},{28,20},... | collective-permute-start | bytes 1572872 | tf_op jit(solution)/shard_map/ppermute | solution.py:669
  639.3 18.0 %collective-permute-start.57 = (bf16[1,128,2048]{2,1,0:T(8,128)(2,1)}, bf16[1,128,2048]{2,1,0:T(8,128)(2,1)}, u32[]{:S(2)}, u32[]{:S(2)}) collective-permute-start(bf16[1,128,2048]{2,1,0:T(8,128)(2,1)} %fusion.4), channel_id=1, source_target_pairs={{0,8},{2,6},{8,16},{10,2},{16,24},{18,10},{24,28},{26,18},{28,20},... | collective-permute-start | bytes 1572872 | tf_op jit(solution)/shard_map/ppermute | solution.py:669
  650.6 79.6 %all-to-all-start.6 = ((bf16[16,464,128]{2,1,0:T(8,128)(2,1)}), bf16[16,464,128]{2,1,0:T(8,128)(2,1)}, u32[]{:S(2)}, u32[]{:S(2)}) async-start(bf16[16,464,128]{2,1,0:T(8,128)(2,1)} %add_convert_fusion), calls=%async_computation.6 | async-start | bytes 3801088 | tf_op jit(solution)/shard_map/all_to_all | solution.py:726
  658.8 45.5 %collective-permute-start.58 = (bf16[1,128,2048]{2,1,0:T(8,128)(2,1)S(1)}, bf16[1,128,2048]{2,1,0:T(8,128)(2,1)S(1)}, u32[]{:S(2)}, u32[]{:S(2)}) collective-permute-start(bf16[1,128,2048]{2,1,0:T(8,128)(2,1)S(1)} %fusion.3), channel_id=1, source_target_pairs={{0,8},{2,6},{8,16},{10,2},{16,24},{18,10},{24,28},{26,18},{28,20},... | collective-permute-start | bytes 1572872 | tf_op jit(solution)/shard_map/ppermute | solution.py:669
  704.4 3.6 collective-permute-start.59
  714.5 14.7 %collective-permute-start.61 = (bf16[128,2048]{1,0:T(8,128)(2,1)S(1)}, bf16[128,2048]{1,0:T(8,128)(2,1)S(1)}, u32[]{:S(2)}, u32[]{:S(2)}) collective-permute-start(bf16[128,2048]{1,0:T(8,128)(2,1)S(1)} %maximum_select_fusion.6), channel_id=1, source_target_pairs={{0,1},{1,0},{2,3},{3,2},{4,5},{5,4},{6,7},{7,6},{8,9},{9,8},{10,11... | collective-permute-start | bytes 1572872 | tf_op jit(solution)/shard_map/ppermute | solution.py:675
  715.9 11.8 %collective-permute-start.63 = (f32[2,448]{1,0:T(2,128)S(1)}, f32[2,448]{1,0:T(2,128)S(1)}, u32[]{:S(2)}, u32[]{:S(2)}) collective-permute-start(f32[2,448]{1,0:T(2,128)S(1)} %pad_maximum_fusion.3), channel_id=1, source_target_pairs={{0,1},{1,0},{2,3},{3,2},{4,5},{5,4},{6,7},{7,6},{8,9},{9,8},{10,11... | collective-permute-start | bytes 10760 | tf_op jit(solution)/shard_map/ppermute | solution.py:675
  (58 other events, 969.4 us)

commit v7 on v6

--- a/solution.py
+++ b/solution.py
@@ -299,7 +299,6 @@
     elif mode == "middle":
         (bias_ref,) = take(1)
         rows_in = take(9)
-        grads_in = take(9)
     else:
         heads_ref, hidden_ref, normed_ref = take(3)
         grads_in = take(9)
@@ -319,10 +318,10 @@
 
     pairs = []
     if mode == "first":
-        pairs += slot_copies(rows_in, 0, raw, core)
+        pairs += slot_copies(rows_in, None, raw, core)
     if mode == "middle":
-        pairs += slot_copies(rows_in, None, normed_ref, core)
-        pairs += slot_copies(grads_in, 1, grad_rows_ref, core)
+        pairs += slot_copies(rows_in, 0, normed_ref, core)
+        pairs += slot_copies(rows_in, 1, grad_rows_ref, core)
     if mode == "last":
         pairs += slot_copies(grads_in, None, grad_rows_ref, core)
     for copy in run_copies(pairs, sems, 0):
@@ -519,6 +518,7 @@
 
 def spread_gradients(up_ref, down_ref, *rest):
     qkv_ref, out_w_ref, fc1_ref, fc2_ref = rest[-4:]
+    down = down_ref.shape[1] - DOWN_ROWS
     for p in range(3):
         rows = slice(p * HEAD_DIM, (p + 1) * HEAD_DIM)
         both = jnp.concatenate([up_ref[0, rows].astype(f32), up_ref[1, rows].astype(f32)], axis=0)
@@ -529,8 +529,8 @@
             fc1_ref[0, :, (2 * d + h) * 128 : (2 * d + h + 1) * 128] = (
                 up_ref[d, base + h * 128 : base + (h + 1) * 128].astype(f32).T
             )
-        out_w_ref[0, d * HEAD_DIM : (d + 1) * HEAD_DIM] = down_ref[d, :HEAD_DIM].astype(f32)
-        fc2_ref[0, d * 256 : (d + 1) * 256] = down_ref[d, HEAD_DIM:].astype(f32)
+        out_w_ref[0, d * HEAD_DIM : (d + 1) * HEAD_DIM] = down_ref[d, down : down + HEAD_DIM].astype(f32)
+        fc2_ref[0, d * 256 : (d + 1) * 256] = down_ref[d, down + HEAD_DIM :].astype(f32)
 
 
 def call_spread(up, down, layer, filled):
@@ -615,6 +615,7 @@
         in_specs=[SMEM_SPEC, rows_of(keep), rows_of(took), one_of(moving), one_of(got)] + [whole_of(x) for x in extra],
         out_specs=[whole_of(x) for x in shapes],
         out_shape=shapes,
+        cost_estimate=pl.CostEstimate(flops=0, bytes_accessed=half * width, transcendentals=0),
         name=name,
     )(core, keep, took, moving, got, *extra)
 
@@ -834,13 +835,12 @@
         jnp.concatenate([nought, sine, rest] * 2, axis=1),
     )
 
-    both = jnp.stack([hidden_in, out_cotangent])
-    both = jnp.where(tensor == core, both, across(both))
-    keeps = jnp.stack([jnp.ones_like(labels[0]), (labels[0] > 0).astype(labels.dtype)]).astype(bf16)
-    both = both * keeps[:, :, None]
+    mine = jnp.where(tensor == core, hidden_in, across(hidden_in))
+    cotangent = jnp.where(tensor == core, out_cotangent, across(out_cotangent))
+    cotangent = jnp.where(labels[0][:, None] > 0, cotangent, jnp.zeros_like(cotangent))
     if groups == 1:
         inputs = gather_rows(
-            after(both, packed_down, packed_last, firsts[0], firsts[2]),
+            after(mine, packed_down, packed_last, firsts[0], firsts[2]),
             {1: (firsts[1], tables[0]), 2: (tables[1], tables[2], allowed), side: (down_other, weights[0][0])},
         )
         slab = spread(after(packed_last, inputs[-2]))
@@ -848,10 +848,9 @@
         weights.append(call_join(join_halves, slab, others, True, True))
         slabs = (slab,)
     else:
-        inputs = gather_rows(both)
+        inputs = gather_rows(mine)
         slabs, others = (), ()
-    mine_inputs = my_half(both, at, 1)
-    state, grad_state = mine_inputs[0], mine_inputs[1]
+    state, grad_state = my_half(mine, at), my_half(cotangent, at)
 
     normed, heads, hidden_pre, wide, *parts = call_pass(
         "first", core_word, weights[0], tables, allowed, [bias_rows[0:1], gains[0], shifts[0]], inputs
@@ -865,14 +864,16 @@
         [jax.ShapeDtypeStruct(rows_shape, f32), jax.ShapeDtypeStruct(rows_shape, bf16)],
         "forward_end",
     )
-    normed_chunks = gather_rows(in_order(normed_own, across(normed_own)), {0: others[:1], 2: others[1:]})
+    normed_chunks = gather_rows(
+        jnp.stack([in_order(normed_own, across(normed_own)), cotangent]), {0: others[:1], 2: others[1:]}
+    )
 
     def handed_back(own_rows):
         filled = in_order(own_rows, across(own_rows))
         return jnp.where(tensor == core, filled, over(filled))
 
-    def summed(own, other, *earlier):
-        total = own.astype(f32) + other.astype(f32)
+    def summed(pairs, *earlier):
+        total = jnp.concatenate([own.astype(f32) + other.astype(f32) for own, other in pairs], axis=1)
         if groups > 1:
             total = total.transpose(1, 0, 2).reshape(total.shape[1], width)
             total = lax.psum_scatter(total, "dp", scatter_dimension=1, axis_index_groups=outer, tiled=True)
@@ -901,7 +902,7 @@
         )
 
     normed_last, grad_rows, wide_last, slim, sums, *parts = call_pass(
-        "middle", core_word, weights[1], tables, allowed, [bias_rows[1:2]], normed_chunks + inputs
+        "middle", core_word, weights[1], tables, allowed, [bias_rows[1:2]], normed_chunks
     )
     out_parts = parts[:3]
     down_pair = down_gradients(wide_last, [grad_rows])
@@ -918,20 +919,24 @@
         "forward_out",
     )
     hidden_out = handed_back(hidden_out)
-    down_last = summed(down_pair[0], after(down_sent, grad_low))
-    grad_chunks = gather_rows(in_order(grad_low, across(grad_low)), {0: (down_sent,), 2: (up_sent,), side: (down_last, hidden_out)})
-    up_last = summed(up_pair[0], after(up_sent, grad_chunks[-2]), down_last)
+    grad_chunks = gather_rows(in_order(grad_low, across(grad_low)), {0: (down_sent,), side: (up_sent, hidden_out)})
+    both_last = summed([(up_pair[0], after(up_sent, grad_chunks[-2])), (down_pair[0], down_sent)])
+    up_last, down_last = both_last[:, : UP_ROWS + SUM_ROWS], both_last[:, UP_ROWS + SUM_ROWS :]
 
     down_pair = down_gradients(wide, grad_chunks)
     down_sent = over(down_pair[1])
     grad_rows, slim, sums, *parts = call_pass(
         "last", core_word, weights[0], tables, allowed, [heads, after(hidden_pre, down_pair[0]), normed], grad_chunks
     )
-    down_first = summed(down_pair[0], after(down_sent, slim), up_last)
-    *up_pair, bias_first = up_gradients(slim, after(normed, up_last), sums)
+    *up_pair, bias_first = up_gradients(slim, normed, sums)
     up_sent = over(up_pair[1])
-    (grad_end,) = ring_sum((after(parts[0], up_pair[0]), parts[1], parts[2]), needed={1: (down_first,)})
-    up_first = summed(up_pair[0], up_sent, down_first)
+    down_first = summed([(down_pair[0], after(down_sent, up_pair[0]))], both_last)
+    needed = {1: (down_first,)}
+    if groups == 1:
+        filled = call_spread(both_last, both_last, 1, [])
+        needed[0] = (filled[1][:, :8],)
+    (grad_end,) = ring_sum((after(parts[0], up_pair[0], both_last), parts[1], parts[2]), needed=needed)
+    up_first = summed([(up_pair[0], up_sent)], down_first)
     _, grad_low = backward_finish(grad_end, state, grad_state, 0)
     grad_hidden = handed_back(grad_low).astype(f32)
 
@@ -948,7 +953,6 @@
     bias_sums = bias_own + over(bias_other)
     bias_qkv, bias_up = bias_sums[:, : 3 * HEAD_DIM].reshape(LAYERS, 3, HEAD_DIM), bias_sums[:, 3 * HEAD_DIM :]
     if groups == 1:
-        filled = call_spread(up_last, down_last, 1, [])
         grad_qkv, grad_out, grad_up, grad_down = call_spread(up_first, down_first, 0, filled)
         grad_qkv = grad_qkv.transpose(0, 2, 1, 3)
     else:

time: 752 us -> 784 us (1.043)
  waiting for transfers between devices: 361 us -> 403 us
  starting transfers between devices: 118 us -> 104 us
    ppermute x12, waiting for transfers between devices: 66.1 us -> 109 us  [over(): return lax.ppermute(x, 'tensor', [(0, 1), (1, 0)])]
    ppermute x24, waiting for transfers between devices: 194 us -> 174 us  [along(): return lax.ppermute(x, 'dp', ring_pairs)]
    all_to_all x7 -> x6, waiting for transfers between devices: 87.4 us -> 104 us  [spread(): return lax.all_to_all(x, 'dp', 0, 0, axis_index_groups=inner, tiled=True)]
    all_to_all x7 -> x6, starting transfers between devices: 52.5 us -> 39.6 us  [spread(): return lax.all_to_all(x, 'dp', 0, 0, axis_index_groups=inner, tiled=True)]
    ppermute x28 -> x29, starting transfers between devices: 25.8 us -> 27.5 us  [across(): return lax.ppermute(x, 'dp', core_pairs)]
  transfers between devices with their start and end apart: 71 -> 71, of which waited for: 44 -> 46; matrix products, arithmetic and copies ran while one was open for 8% -> 8% of each run, Pallas kernels for 18% -> 18%
where the time goes in v7:
time: 784 us; the launch traced here: 772 us
  waiting for transfers between devices  403 us (51%)
  Pallas kernels  183 us (23%)
  starting transfers between devices  104 us (13%)
  other arithmetic  55.8 us (7%)
  local copies, waits for them, and re-layouts  24.9 us (3%)
    ppermute x24, waiting for transfers between devices, along(): return lax.ppermute(x, 'dp', ring_pairs)  174 us
    ppermute x12, waiting for transfers between devices, over(): return lax.ppermute(x, 'tensor', [(0, 1), (1, 0)])  109 us
    all_to_all x6, waiting for transfers between devices, spread(): return lax.all_to_all(x, 'dp', 0, 0, axis_index_groups=inner, tiled=True)  104 us
    pallas_call x3, Pallas kernels, call_pass(): pl.pallas_call(partial(layer_pass, mode), in_specs=[SMEM_SPEC] + [VMEM_SP...  91.8 us
    all_to_all x6, starting transfers between devices, spread(): return lax.all_to_all(x, 'dp', 0, 0, axis_index_groups=inner, tiled=True)  39.6 us
    pallas_call x4, Pallas kernels, call_gradients(): pl.pallas_call(partial(gradient_slabs, own_rows, other_rows, with_sums, l...  37.9 us
    ppermute x29, starting transfers between devices, across(): return lax.ppermute(x, 'dp', core_pairs)  27.5 us
    ppermute x24, starting transfers between devices, along(): return lax.ppermute(x, 'dp', ring_pairs)  23.2 us
  transfers between devices with their start and end apart: 71, of which 46 were waited for; matrix products, arithmetic and copies ran while one was open for 8% of the time, Pallas kernels for 18%

profile of v7, /device:TPU:13, one launch (start us, length us, event | category | flops | bytes accessed | tf_op | source)
XLA Modules:
  0.0 772.4 jit_solution(15967864597427956682)
XLA Ops:
  4.8 4.0 pack_first.1
  8.8 6.5 all-to-all-start
  15.3 3.5 pack_down.1
  18.8 39.7 %all-to-all-done.own_ref = bf16[16,464,128]{2,1,0:T(8,128)(2,1)S(1)} async-done(((bf16[16,464,128]{2,1,0:T(8,128)(2,1)}), bf16[16,464,128]{2,1,0:T(8,128)(2,1)S(1)}, u32[]{:S(2)}, u32[]{:S(2)}) %all-to-all-start) | async-done | bytes 1900576 | tf_op jit(solution)/shard_map/all_to_all | solution.py:727
  58.5 4.8 all-to-all-start.1
  68.0 4.4 pack_both.1
  74.8 19.5 %all-to-all-done.1.own_ref = bf16[16,320,128]{2,1,0:T(8,128)(2,1)S(1)} async-done(((bf16[16,320,128]{2,1,0:T(8,128)(2,1)}), bf16[16,320,128]{2,1,0:T(8,128)(2,1)S(1)}, u32[]{:S(2)}, u32[]{:S(2)}) %all-to-all-start.1) | async-done | bytes 1310752 | tf_op jit(solution)/shard_map/all_to_all | solution.py:727
  95.3 2.6 multiply_sine_fusion
  98.7 2.6 concatenate.89.refs_3_
  102.6 6.6 collective-permute-done.2.other_ref
  119.0 4.8 join_up.1.refs_1_
  123.9 2.4 collective-permute-done.4.refs_13_
  126.3 11.0 %collective-permute-done.5.other_ref = bf16[16,320,128]{2,1,0:T(8,128)(2,1)} collective-permute-done((bf16[16,320,128]{2,1,0:T(8,128)(2,1)}, bf16[16,320,128]{2,1,0:T(8,128)(2,1)}, u32[]{:S(2)}, u32[]{:S(2)}) %collective-permute-start.5) | collective-permute-done | bytes 1310752 | tf_op jit(solution)/shard_map/ppermute | solution.py:676
  138.5 4.3 collective-permute-done.6.refs_17_
  143.5 7.4 all-to-all-start.2
  157.3 4.2 join_down.1.refs_2_
  162.3 29.3 %pass_first.1 = (bf16[1024,2048]{1,0:T(8,128)(2,1)}, bf16[1024,384]{1,0:T(8,128)(2,1)}, f32[1024,512]{1,0:T(8,128)}, bf16[1024,640]{1,0:T(8,128)(2,1)}, bf16[64,...) custom-call(s32[1]{0:T(128)} %bitcast.refs_0_.core_ref, bf16[2048,896]{1,0:T(8,128)(2,1)} %join_up.1.refs_1_, ...), custom_call_target="tpu_custom_call" | custom-call | flops 19327352832 | bytes 20000000 | tf_op jit(solution)/shard_map/pass_first/pallas_call | solution.py:442
  192.2 28.7 %all-to-all-done.2.own_ref = bf16[16,768,128]{2,1,0:T(8,128)(2,1)S(1)} async-done(((bf16[16,768,128]{2,1,0:T(8,128)(2,1)}), bf16[16,768,128]{2,1,0:T(8,128)(2,1)S(1)}, u32[]{:S(2)}, u32[]{:S(2)}) %all-to-all-start.2) | async-done | bytes 3145760 | tf_op jit(solution)/shard_map/all_to_all | solution.py:727
  223.8 5.5 collective-permute-done.16
  230.9 8.3 %collective-permute-done.17 = bf16[1,128,2048]{2,1,0:T(8,128)(2,1)S(1)} collective-permute-done((bf16[1,128,2048]{2,1,0:T(8,128)(2,1)S(1)}, bf16[1,128,2048]{2,1,0:T(8,128)(2,1)S(1)}, u32[]{:S(2)}, u32[]{:S(2)}) %collective-permute-start.17) | collective-permute-done | bytes 524320 | tf_op jit(solution)/shard_map/ppermute | solution.py:670
  240.6 8.3 %collective-permute-done.18 = bf16[1,128,2048]{2,1,0:T(8,128)(2,1)S(1)} collective-permute-done((bf16[1,128,2048]{2,1,0:T(8,128)(2,1)S(1)}, bf16[1,128,2048]{2,1,0:T(8,128)(2,1)S(1)}, u32[]{:S(2)}, u32[]{:S(2)}) %collective-permute-start.18) | collective-permute-done | bytes 524320 | tf_op jit(solution)/shard_map/ppermute | solution.py:670
  251.0 2.7 collective-permute-start.22
  256.8 2.8 collective-permute-done.19.moving_ref
  260.6 3.6 collective-permute-start.20
  266.1 2.5 forward_end.1
  271.6 20.1 %collective-permute-done.7.lower_ref = bf16[8,768,128]{2,1,0:T(8,128)(2,1)S(1)} collective-permute-done((bf16[8,768,128]{2,1,0:T(8,128)(2,1)}, bf16[8,768,128]{2,1,0:T(8,128)(2,1)S(1)}, u32[]{:S(2)}, u32[]{:S(2)}) %collective-permute-start.7) | collective-permute-done | bytes 1572896 | tf_op jit(solution)/shard_map/ppermute | solution.py:676
  294.7 11.1 %collective-permute-done.23.refs_9_ = bf16[2,128,2048]{2,1,0:T(8,128)(2,1)} collective-permute-done((bf16[2,128,2048]{2,1,0:T(8,128)(2,1)S(1)}, bf16[2,128,2048]{2,1,0:T(8,128)(2,1)}, u32[]{:S(2)}, u32[]{:S(2)}) %collective-permute-start.23) | collective-permute-done | bytes 1048608 | tf_op jit(solution)/shard_map/ppermute | solution.py:670
  307.5 21.7 %collective-permute-done.8.upper_ref = bf16[8,768,128]{2,1,0:T(8,128)(2,1)S(1)} collective-permute-done((bf16[8,768,128]{2,1,0:T(8,128)(2,1)S(1)}, bf16[8,768,128]{2,1,0:T(8,128)(2,1)S(1)}, u32[]{:S(2)}, u32[]{:S(2)}) %collective-permute-start.8) | collective-permute-done | bytes 1572896 | tf_op jit(solution)/shard_map/ppermute | solution.py:676
  330.3 13.2 %collective-permute-done.25.refs_11_ = bf16[2,128,2048]{2,1,0:T(8,128)(2,1)} collective-permute-done((bf16[2,128,2048]{2,1,0:T(8,128)(2,1)}, bf16[2,128,2048]{2,1,0:T(8,128)(2,1)}, u32[]{:S(2)}, u32[]{:S(2)}) %collective-permute-start.25) | collective-permute-done | bytes 1048608 | tf_op jit(solution)/shard_map/ppermute | solution.py:670
  346.6 6.5 collective-permute-done.29.refs_15_
  355.2 6.4 join_halves.1
  361.6 36.0 %pass_middle.1 = (bf16[1024,2048]{1,0:T(8,128)(2,1)}, bf16[1024,2048]{1,0:T(8,128)(2,1)}, bf16[1024,640]{1,0:T(8,128)(2,1)}, bf16[1024,896]{1,0:T(8,128)(2,1)}, ...) custom-call(s32[1]{0:T(128)} %bitcast.refs_0_.core_ref, ...), custom_call_target="tpu_custom_call" | custom-call | flops 38654705664 | bytes 40000000 | tf_op jit(solution)/shard_map/pass_middle/pallas_call | solution.py:442
  398.7 3.3 collective-permute-done.32
  410.5 4.0 collective-permute-done.34
  415.7 8.8 %down_gradients.2 = (bf16[16,320,128]{2,1,0:T(8,128)(2,1)}, bf16[16,320,128]{2,1,0:T(8,128)(2,1)}) custom-call(s32[1]{0:T(128)} %bitcast.refs_0_.core_ref, bf16[1024,640]{1,0:T(8,128)(2,1)} %get-tuple-element.100.left_ref, bf16[1024,2048]{1,0:T(8,128)(2,1)} %get-tuple-element.101.rest_0_), custom_call_target="tpu_custom_call" | custom-call | flops 5368709120 | bytes 10747904 | tf_op jit(solution)/shard_map/down_gradients/pallas_call | solution.py:504
  424.5 4.4 collective-permute-done.36
  430.5 10.1 %up_gradients.2 = (bf16[16,464,128]{2,1,0:T(8,128)(2,1)}, bf16[16,464,128]{2,1,0:T(8,128)(2,1)}, f32[1,896]{1,0:T(1,128)}) custom-call(s32[1]{0:T(128)} %bitcast.refs_0_.core_ref, bf16[1024,896]{1,0:T(8,128)(2,1)} %get-tuple-element.104.left_ref, bf16[1024,2048]{1,0:T(8,128)(2,1)} %get-tuple-element.105.rest_0_, f32[16,2048]{1,0:T(8,128)} %get-tuple-element.106.rest_1_), custom_call_target="tpu_custom_call" | custom-call | flops 7516192768 | bytes 13369344 | tf_op jit(solution)/shard_map/up_gradients/pallas_call | solution.py:504
  440.6 3.1 collective-permute-done.37
  446.3 12.0 %collective-permute-done.38.moving_ref = bf16[2,128,2048]{2,1,0:T(8,128)(2,1)S(1)} collective-permute-done((bf16[2,128,2048]{2,1,0:T(8,128)(2,1)S(1)}, bf16[2,128,2048]{2,1,0:T(8,128)(2,1)S(1)}, u32[]{:S(2)}, u32[]{:S(2)}) %collective-permute-start.38) | collective-permute-done | bytes 1048608 | tf_op jit(solution)/shard_map/ppermute | solution.py:670
  458.3 3.6 collective-permute-start.39
  464.3 2.9 backward_end.2
  478.2 3.1 collective-permute-start.40
  485.7 4.5 collective-permute-done.45.rest_2_.refs_12_
  491.8 34.4 %collective-permute-done.41 = bf16[128,2048]{1,0:T(8,128)(2,1)S(1)} collective-permute-done((bf16[128,2048]{1,0:T(8,128)(2,1)S(1)}, bf16[128,2048]{1,0:T(8,128)(2,1)S(1)}, u32[]{:S(2)}, u32[]{:S(2)}) %collective-permute-start.41) | collective-permute-done | bytes 524320 | tf_op jit(solution)/shard_map/ppermute | solution.py:676
  528.3 5.0 collective-permute-done.51.rest_7_.refs_17_
  535.6 10.0 %all-to-all-start.3 = ((bf16[16,784,128]{2,1,0:T(8,128)(2,1)}), bf16[16,784,128]{2,1,0:T(8,128)(2,1)S(1)}, u32[]{:S(2)}, u32[]{:S(2)}) async-start(bf16[16,784,128]{2,1,0:T(8,128)(2,1)} %pad_maximum_fusion), calls=%async_computation.3 | async-start | bytes 6422528 | tf_op jit(solution)/shard_map/all_to_all | solution.py:727
  549.9 8.9 %down_gradients.3 = (bf16[16,320,128]{2,1,0:T(8,128)(2,1)}, bf16[16,320,128]{2,1,0:T(8,128)(2,1)}) custom-call(s32[1]{0:T(128)} %bitcast.refs_0_.core_ref, bf16[1024,640]{1,0:T(8,128)(2,1)} %get-tuple-element.112.left_ref, bf16[128,2048]{1,0:T(8,128)(2,1)} %maximum_select_fusion.4.rest_0_.refs_10_, ...), custom_call_target="tpu_custom_call" | custom-call | flops 5368709120 | bytes 10747904 | tf_op jit(solution)/shard_map/down_gradients/pallas_call | solution.py:504
  560.1 26.5 %pass_last.1 = (bf16[1024,2048]{1,0:T(8,128)(2,1)}, bf16[1024,896]{1,0:T(8,128)(2,1)}, f32[16,2048]{1,0:T(8,128)}, bf16[64,2048]{1,0:T(8,128)(2,1)}, bf16[448,20...) custom-call(s32[1]{0:T(128)} %bitcast.refs_0_.core_ref, bf16[2048,896]{1,0:T(8,128)(2,1)} %join_up.1.refs_1_, ...), custom_call_target="tpu_custom_call" | custom-call | flops 19327352832 | bytes 20000000 | tf_op jit(solution)/shard_map/pass_last/pallas_call | solution.py:442
  587.2 10.1 %up_gradients.3 = (bf16[16,464,128]{2,1,0:T(8,128)(2,1)}, bf16[16,464,128]{2,1,0:T(8,128)(2,1)}, f32[1,896]{1,0:T(1,128)}) custom-call(s32[1]{0:T(128)} %bitcast.refs_0_.core_ref, bf16[1024,896]{1,0:T(8,128)(2,1)} %get-tuple-element.124.left_ref, bf16[1024,2048]{1,0:T(8,128)(2,1)} %get-tuple-element.120.refs_9_.rest_0_, f32[16,2048]{1,0:T(8,128)} %get-tuple-element.125.rest_1_), custom_call_target="tpu_custom_call" | custom-call | flops 7516192768 | bytes 13369344 | tf_op jit(solution)/shard_map/up_gradients/pallas_call | solution.py:504
  597.3 3.1 add_convert_fusion.2
  600.4 16.5 %all-to-all-done.3.up_ref.down_ref = bf16[16,784,128]{2,1,0:T(8,128)(2,1)S(1)} async-done(((bf16[16,784,128]{2,1,0:T(8,128)(2,1)}), bf16[16,784,128]{2,1,0:T(8,128)(2,1)S(1)}, u32[]{:S(2)}, u32[]{:S(2)}) %all-to-all-start.3) | async-done | bytes 3211296 | tf_op jit(solution)/shard_map/all_to_all | solution.py:727
  616.9 4.8 all-to-all-start.4
  626.0 27.4 %collective-permute-done.55 = bf16[1,64,2048]{2,1,0:T(8,128)(2,1)S(1)} collective-permute-done((bf16[1,64,2048]{2,1,0:T(8,128)(2,1)S(1)}, bf16[1,64,2048]{2,1,0:T(8,128)(2,1)S(1)}, u32[]{:S(2)}, u32[]{:S(2)}) %collective-permute-start.55) | collective-permute-done | bytes 262176 | tf_op jit(solution)/shard_map/ppermute | solution.py:670
  654.9 2.4 collective-permute-start.56
  657.2 6.1 collective-permute-done.56
  664.4 2.6 fusion.4
  669.4 3.3 add_convert_fusion
  672.7 6.1 all-to-all-start.5
  682.6 43.4 %collective-permute-done.59.moving_ref = bf16[1,128,2048]{2,1,0:T(8,128)(2,1)S(1)} collective-permute-done((bf16[1,128,2048]{2,1,0:T(8,128)(2,1)S(1)}, bf16[1,128,2048]{2,1,0:T(8,128)(2,1)S(1)}, u32[]{:S(2)}, u32[]{:S(2)}) %collective-permute-start.59) | collective-permute-done | bytes 524320 | tf_op jit(solution)/shard_map/ppermute | solution.py:670
  726.8 2.4 collective-permute-start.60
  731.1 2.9 backward_end.3
  739.4 11.8 %collective-permute-done.64 = f32[2,448]{1,0:T(2,128)S(1)} collective-permute-done((f32[2,448]{1,0:T(2,128)S(1)}, f32[2,448]{1,0:T(2,128)S(1)}, u32[]{:S(2)}, u32[]{:S(2)}) %collective-permute-start.64) | collective-permute-done | bytes 3616 | tf_op jit(solution)/shard_map/ppermute | solution.py:676
  752.6 8.0 %spread_gradients.2 = (f32[2,3,128,1024]{3,2,1,0:T(8,128)}, f32[2,1024,128]{2,1,0:T(8,128)}, f32[2,128,4096]{2,1,0:T(8,128)}, f32[2,4096,128]{2,1,0:T(8,128)}) custom-call(bf16[16,784,128]{2,1,0:T(8,128)(2,1)} %copy-done, bf16[16,784,128]{2,1,0:T(8,128)(2,1)} %copy-done), custom_call_target="tpu_custom_call" | custom-call | tf_op jit(solution)/shard_map/spread_gradients/pallas_call | solution.py:543
  764.7 7.3 spread_gradients.3
  (301 shorter events, 132.9 us)
Async XLA Ops:
  8.8 49.7 %all-to-all-start = ((bf16[16,464,128]{2,1,0:T(8,128)(2,1)}), bf16[16,464,128]{2,1,0:T(8,128)(2,1)S(1)}, u32[]{:S(2)}, u32[]{:S(2)}) async-start(bf16[16,464,128]{2,1,0:T(8,128)(2,1)} %pack_first.1), calls=%async_computation | async-start | bytes 3801088 | tf_op jit(solution)/shard_map/all_to_all | solution.py:727
  58.5 35.7 %all-to-all-start.1 = ((bf16[16,320,128]{2,1,0:T(8,128)(2,1)}), bf16[16,320,128]{2,1,0:T(8,128)(2,1)S(1)}, u32[]{:S(2)}, u32[]{:S(2)}) async-start(bf16[16,320,128]{2,1,0:T(8,128)(2,1)} %pack_down.1), calls=%async_computation.1 | async-start | bytes 2621440 | tf_op jit(solution)/shard_map/all_to_all | solution.py:727
  63.3 9.5 %collective-permute-start = (bf16[128,2048]{1,0:T(8,128)(2,1)}, bf16[128,2048]{1,0:T(8,128)(2,1)}, u32[]{:S(2)}, u32[]{:S(2)}) collective-permute-start(bf16[128,2048]{1,0:T(8,128)(2,1)} %param.17), channel_id=1, source_target_pairs={{0,2},{2,0},{4,6},{6,4},{8,10},{10,8},{12,14},{14,12},{16,18},{18,... | collective-permute-start | bytes 1572872 | tf_op jit(solution)/shard_map/ppermute | solution.py:673
  66.2 43.0 %collective-permute-start.2 = (bf16[16,464,128]{2,1,0:T(8,128)(2,1)S(1)}, bf16[16,464,128]{2,1,0:T(8,128)(2,1)}, u32[]{:S(2)}, u32[]{:S(2)}) collective-permute-start(bf16[16,464,128]{2,1,0:T(8,128)(2,1)S(1)} %all-to-all-done.own_ref), channel_id=1, source_target_pairs={{0,1},{1,0},{2,3},{3,2},{4,5},{5,4},{6,7},{7,6},{8,9},{9,8},{10,11... | collective-permute-start | bytes 5701640 | tf_op jit(solution)/shard_map/ppermute | solution.py:676
  94.3 14.9 %collective-permute-start.1 = (bf16[128,2048]{1,0:T(8,128)(2,1)}, bf16[128,2048]{1,0:T(8,128)(2,1)}, u32[]{:S(2)}, u32[]{:S(2)}) collective-permute-start(bf16[128,2048]{1,0:T(8,128)(2,1)} %broadcast_select_fusion.1.refs_10_), channel_id=1, source_target_pairs={{0,8},{2,6},{8,16},{10,2},{16,24},{18,10},{24,28},{26,18},{28,20},... | collective-permute-start | bytes 1572872 | tf_op jit(solution)/shard_map/ppermute | solution.py:670
  101.4 35.9 %collective-permute-start.5 = (bf16[16,320,128]{2,1,0:T(8,128)(2,1)}, bf16[16,320,128]{2,1,0:T(8,128)(2,1)}, u32[]{:S(2)}, u32[]{:S(2)}) collective-permute-start(bf16[16,320,128]{2,1,0:T(8,128)(2,1)} %copy-done.9), channel_id=1, source_target_pairs={{0,1},{1,0},{2,3},{3,2},{4,5},{5,4},{6,7},{7,6},{8,9},{9,8},{10,11... | collective-permute-start | bytes 3932168 | tf_op jit(solution)/shard_map/ppermute | solution.py:676
  109.2 8.6 %collective-permute-start.3 = (bf16[128,2048]{1,0:T(8,128)(2,1)}, bf16[128,2048]{1,0:T(8,128)(2,1)S(1)}, u32[]{:S(2)}, u32[]{:S(2)}) collective-permute-start(bf16[128,2048]{1,0:T(8,128)(2,1)} %collective-permute-done.1.refs_11_), channel_id=1, source_target_pairs={{0,8},{2,6},{8,16},{10,2},{16,24},{18,10},{24,28},{26,18},{28,20},... | collective-permute-start | bytes 1572872 | tf_op jit(solution)/shard_map/ppermute | solution.py:670
  117.9 8.4 %collective-permute-start.4 = (bf16[128,2048]{1,0:T(8,128)(2,1)S(1)}, bf16[128,2048]{1,0:T(8,128)(2,1)S(1)}, u32[]{:S(2)}, u32[]{:S(2)}) collective-permute-start(bf16[128,2048]{1,0:T(8,128)(2,1)S(1)} %collective-permute-done.3.refs_12_), channel_id=1, source_target_pairs={{0,8},{2,6},{8,16},{10,2},{16,24},{18,10},{24,28},{26,18},{28,20},... | collective-permute-start | bytes 1572872 | tf_op jit(solution)/shard_map/ppermute | solution.py:670
  137.3 5.5 collective-permute-start.6
  143.5 77.3 %all-to-all-start.2 = ((bf16[16,768,128]{2,1,0:T(8,128)(2,1)}), bf16[16,768,128]{2,1,0:T(8,128)(2,1)S(1)}, u32[]{:S(2)}, u32[]{:S(2)}) async-start(bf16[16,768,128]{2,1,0:T(8,128)(2,1)} %pack_both.1), calls=%async_computation.2 | async-start | bytes 6291456 | tf_op jit(solution)/shard_map/all_to_all | solution.py:727
  154.8 6.8 collective-permute-start.10
  156.0 5.6 collective-permute-start.11
  156.0 5.6 collective-permute-start.12
  156.6 5.0 collective-permute-start.13
  191.6 32.2 %collective-permute-start.14 = (bf16[448,2048]{1,0:T(8,128)(2,1)}, bf16[448,2048]{1,0:T(8,128)(2,1)}, u32[]{:S(2)}, u32[]{:S(2)}) collective-permute-start(bf16[448,2048]{1,0:T(8,128)(2,1)} %get-tuple-element.88), channel_id=1, source_target_pairs={{0,2},{2,0},{4,6},{6,4},{8,10},{10,8},{12,14},{14,12},{16,18},{18,... | collective-permute-start | bytes 5505032 | tf_op jit(solution)/shard_map/ppermute | solution.py:673
  223.7 5.6 collective-permute-start.16
  230.7 8.6 %collective-permute-start.17 = (bf16[1,128,2048]{2,1,0:T(8,128)(2,1)S(1)}, bf16[1,128,2048]{2,1,0:T(8,128)(2,1)S(1)}, u32[]{:S(2)}, u32[]{:S(2)}) collective-permute-start(bf16[1,128,2048]{2,1,0:T(8,128)(2,1)S(1)} %fusion.7), channel_id=1, source_target_pairs={{0,8},{2,6},{8,16},{10,2},{16,24},{18,10},{24,28},{26,18},{28,20},... | collective-permute-start | bytes 1572872 | tf_op jit(solution)/shard_map/ppermute | solution.py:670
  240.5 8.4 %collective-permute-start.18 = (bf16[1,128,2048]{2,1,0:T(8,128)(2,1)S(1)}, bf16[1,128,2048]{2,1,0:T(8,128)(2,1)S(1)}, u32[]{:S(2)}, u32[]{:S(2)}) collective-permute-start(bf16[1,128,2048]{2,1,0:T(8,128)(2,1)S(1)} %fusion.6), channel_id=1, source_target_pairs={{0,8},{2,6},{8,16},{10,2},{16,24},{18,10},{24,28},{26,18},{28,20},... | collective-permute-start | bytes 1572872 | tf_op jit(solution)/shard_map/ppermute | solution.py:670
  251.0 8.6 %collective-permute-start.19 = (bf16[1,128,2048]{2,1,0:T(8,128)(2,1)}, bf16[1,128,2048]{2,1,0:T(8,128)(2,1)}, u32[]{:S(2)}, u32[]{:S(2)}) collective-permute-start(bf16[1,128,2048]{2,1,0:T(8,128)(2,1)} %fusion.5), channel_id=1, source_target_pairs={{0,8},{2,6},{8,16},{10,2},{16,24},{18,10},{24,28},{26,18},{28,20},... | collective-permute-start | bytes 1572872 | tf_op jit(solution)/shard_map/ppermute | solution.py:670
  251.0 17.9 %collective-permute-start.22 = (bf16[128,2048]{1,0:T(8,128)(2,1)}, bf16[128,2048]{1,0:T(8,128)(2,1)}, u32[]{:S(2)}, u32[]{:S(2)}) collective-permute-start(bf16[128,2048]{1,0:T(8,128)(2,1)} %param.30), channel_id=1, source_target_pairs={{0,2},{2,0},{4,6},{6,4},{8,10},{10,8},{12,14},{14,12},{16,18},{18,... | collective-permute-start | bytes 1572872 | tf_op jit(solution)/shard_map/ppermute | solution.py:673
  255.6 36.1 %collective-permute-start.7 = (bf16[8,768,128]{2,1,0:T(8,128)(2,1)}, bf16[8,768,128]{2,1,0:T(8,128)(2,1)S(1)}, u32[]{:S(2)}, u32[]{:S(2)}) collective-permute-start(bf16[8,768,128]{2,1,0:T(8,128)(2,1)} %get-tuple-element.202), channel_id=1, source_target_pairs={{0,1},{1,0},{2,3},{3,2},{4,5},{5,4},{6,7},{7,6},{8,9},{9,8},{10,11... | collective-permute-start | bytes 4718600 | tf_op jit(solution)/shard_map/ppermute | solution.py:676
  260.6 4.8 collective-permute-start.20
  291.7 14.0 %collective-permute-start.23 = (bf16[2,128,2048]{2,1,0:T(8,128)(2,1)S(1)}, bf16[2,128,2048]{2,1,0:T(8,128)(2,1)}, u32[]{:S(2)}, u32[]{:S(2)}) collective-permute-start(bf16[2,128,2048]{2,1,0:T(8,128)(2,1)S(1)} %pad_maximum_fusion.1.refs_8_), channel_id=1, source_target_pairs={{0,8},{2,6},{8,16},{10,2},{16,24},{18,10},{24,28},{26,18},{28,20},... | collective-permute-start | bytes 3145736 | tf_op jit(solution)/shard_map/ppermute | solution.py:670
  293.5 35.8 %collective-permute-start.8 = (bf16[8,768,128]{2,1,0:T(8,128)(2,1)S(1)}, bf16[8,768,128]{2,1,0:T(8,128)(2,1)S(1)}, u32[]{:S(2)}, u32[]{:S(2)}) collective-permute-start(bf16[8,768,128]{2,1,0:T(8,128)(2,1)S(1)} %copy-done.19), channel_id=1, source_target_pairs={{0,1},{1,0},{2,3},{3,2},{4,5},{5,4},{6,7},{7,6},{8,9},{9,8},{10,11... | collective-permute-start | bytes 4718600 | tf_op jit(solution)/shard_map/ppermute | solution.py:676
  305.8 23.5 %collective-permute-start.24 = (bf16[2,128,2048]{2,1,0:T(8,128)(2,1)}, bf16[2,128,2048]{2,1,0:T(8,128)(2,1)}, u32[]{:S(2)}, u32[]{:S(2)}) collective-permute-start(bf16[2,128,2048]{2,1,0:T(8,128)(2,1)} %collective-permute-done.23.refs_9_), channel_id=1, source_target_pairs={{0,8},{2,6},{8,16},{10,2},{16,24},{18,10},{24,28},{26,18},{28,20},... | collective-permute-start | bytes 3145736 | tf_op jit(solution)/shard_map/ppermute | solution.py:670
  329.3 14.3 %collective-permute-start.25 = (bf16[2,128,2048]{2,1,0:T(8,128)(2,1)}, bf16[2,128,2048]{2,1,0:T(8,128)(2,1)}, u32[]{:S(2)}, u32[]{:S(2)}) collective-permute-start(bf16[2,128,2048]{2,1,0:T(8,128)(2,1)} %collective-permute-done.24.refs_10_), channel_id=1, source_target_pairs={{0,8},{2,6},{8,16},{10,2},{16,24},{18,10},{24,28},{26,18},{28,20},... | collective-permute-start | bytes 3145736 | tf_op jit(solution)/shard_map/ppermute | solution.py:670
  329.3 32.3 %collective-permute-start.26 = (bf16[2,128,2048]{2,1,0:T(8,128)(2,1)}, bf16[2,128,2048]{2,1,0:T(8,128)(2,1)}, u32[]{:S(2)}, u32[]{:S(2)}) collective-permute-start(bf16[2,128,2048]{2,1,0:T(8,128)(2,1)} %collective-permute-done.23.refs_9_), channel_id=1, source_target_pairs={{0,2},{2,0},{4,6},{6,4},{8,10},{10,8},{12,14},{14,12},{16,18},{18,... | collective-permute-start | bytes 3145736 | tf_op jit(solution)/shard_map/ppermute | solution.py:673
  330.3 31.2 %collective-permute-start.27 = (bf16[2,128,2048]{2,1,0:T(8,128)(2,1)}, bf16[2,128,2048]{2,1,0:T(8,128)(2,1)}, u32[]{:S(2)}, u32[]{:S(2)}) collective-permute-start(bf16[2,128,2048]{2,1,0:T(8,128)(2,1)} %collective-permute-done.24.refs_10_), channel_id=1, source_target_pairs={{0,2},{2,0},{4,6},{6,4},{8,10},{10,8},{12,14},{14,12},{16,18},{18,... | collective-permute-start | bytes 3145736 | tf_op jit(solution)/shard_map/ppermute | solution.py:673
  344.6 8.5 %collective-permute-start.29 = (bf16[2,64,2048]{2,1,0:T(8,128)(2,1)S(1)}, bf16[2,64,2048]{2,1,0:T(8,128)(2,1)}, u32[]{:S(2)}, u32[]{:S(2)}) collective-permute-start(bf16[2,64,2048]{2,1,0:T(8,128)(2,1)S(1)} %constant_dynamic-slice_fusion.1), channel_id=1, source_target_pairs={{0,8},{2,6},{8,16},{10,2},{16,24},{18,10},{24,28},{26,18},{28,20},... | collective-permute-start | bytes 1572872 | tf_op jit(solution)/shard_map/ppermute | solution.py:670
  344.7 16.9 %collective-permute-start.28 = (bf16[2,128,2048]{2,1,0:T(8,128)(2,1)}, bf16[2,128,2048]{2,1,0:T(8,128)(2,1)}, u32[]{:S(2)}, u32[]{:S(2)}) collective-permute-start(bf16[2,128,2048]{2,1,0:T(8,128)(2,1)} %collective-permute-done.25.refs_11_), channel_id=1, source_target_pairs={{0,2},{2,0},{4,6},{6,4},{8,10},{10,8},{12,14},{14,12},{16,18},{18,... | collective-permute-start | bytes 3145736 | tf_op jit(solution)/shard_map/ppermute | solution.py:673
  353.1 8.4 %collective-permute-start.30 = (bf16[2,64,2048]{2,1,0:T(8,128)(2,1)}, bf16[2,64,2048]{2,1,0:T(8,128)(2,1)}, u32[]{:S(2)}, u32[]{:S(2)}) collective-permute-start(bf16[2,64,2048]{2,1,0:T(8,128)(2,1)} %collective-permute-done.29.refs_15_), channel_id=1, source_target_pairs={{0,2},{2,0},{4,6},{6,4},{8,10},{10,8},{12,14},{14,12},{16,18},{18,... | collective-permute-start | bytes 1572872 | tf_op jit(solution)/shard_map/ppermute | solution.py:673
  397.6 9.4 %collective-permute-start.35 = (bf16[448,2048]{1,0:T(8,128)(2,1)}, bf16[448,2048]{1,0:T(8,128)(2,1)S(1)}, u32[]{:S(2)}, u32[]{:S(2)}) collective-permute-start(bf16[448,2048]{1,0:T(8,128)(2,1)} %get-tuple-element.99), channel_id=1, source_target_pairs={{0,2},{2,0},{4,6},{6,4},{8,10},{10,8},{12,14},{14,12},{16,18},{18,... | collective-permute-start | bytes 5505032 | tf_op jit(solution)/shard_map/ppermute | solution.py:673
  397.7 4.4 collective-permute-start.32
  398.2 10.4 %collective-permute-start.31 = (bf16[448,2048]{1,0:T(8,128)(2,1)}, bf16[448,2048]{1,0:T(8,128)(2,1)S(1)}, u32[]{:S(2)}, u32[]{:S(2)}) collective-permute-start(bf16[448,2048]{1,0:T(8,128)(2,1)} %get-tuple-element.95), channel_id=1, source_target_pairs={{0,2},{2,0},{4,6},{6,4},{8,10},{10,8},{12,14},{14,12},{16,18},{18,... | collective-permute-start | bytes 5505032 | tf_op jit(solution)/shard_map/ppermute | solution.py:673
  398.3 6.8 collective-permute-start.33
  406.1 8.4 %collective-permute-start.34 = (bf16[2,64,2048]{2,1,0:T(8,128)(2,1)S(1)}, bf16[2,64,2048]{2,1,0:T(8,128)(2,1)S(1)}, u32[]{:S(2)}, u32[]{:S(2)}) collective-permute-start(bf16[2,64,2048]{2,1,0:T(8,128)(2,1)S(1)} %pad_maximum_fusion.2), channel_id=1, source_target_pairs={{0,8},{2,6},{8,16},{10,2},{16,24},{18,10},{24,28},{26,18},{28,20},... | collective-permute-start | bytes 1572872 | tf_op jit(solution)/shard_map/ppermute | solution.py:670
  414.9 14.0 %collective-permute-start.36 = (bf16[2,128,2048]{2,1,0:T(8,128)(2,1)S(1)}, bf16[2,128,2048]{2,1,0:T(8,128)(2,1)S(1)}, u32[]{:S(2)}, u32[]{:S(2)}) collective-permute-start(bf16[2,128,2048]{2,1,0:T(8,128)(2,1)S(1)} %fusion), channel_id=1, source_target_pairs={{0,8},{2,6},{8,16},{10,2},{16,24},{18,10},{24,28},{26,18},{28,20},... | collective-permute-start | bytes 3145736 | tf_op jit(solution)/shard_map/ppermute | solution.py:670
  429.5 14.2 %collective-permute-start.37 = (bf16[2,128,2048]{2,1,0:T(8,128)(2,1)S(1)}, bf16[2,128,2048]{2,1,0:T(8,128)(2,1)S(1)}, u32[]{:S(2)}, u32[]{:S(2)}) collective-permute-start(bf16[2,128,2048]{2,1,0:T(8,128)(2,1)S(1)} %fusion.1), channel_id=1, source_target_pairs={{0,8},{2,6},{8,16},{10,2},{16,24},{18,10},{24,28},{26,18},{28,20},... | collective-permute-start | bytes 3145736 | tf_op jit(solution)/shard_map/ppermute | solution.py:670
  444.3 14.0 %collective-permute-start.38 = (bf16[2,128,2048]{2,1,0:T(8,128)(2,1)S(1)}, bf16[2,128,2048]{2,1,0:T(8,128)(2,1)S(1)}, u32[]{:S(2)}, u32[]{:S(2)}) collective-permute-start(bf16[2,128,2048]{2,1,0:T(8,128)(2,1)S(1)} %fusion.2), channel_id=1, source_target_pairs={{0,8},{2,6},{8,16},{10,2},{16,24},{18,10},{24,28},{26,18},{28,20},... | collective-permute-start | bytes 3145736 | tf_op jit(solution)/shard_map/ppermute | solution.py:670
  445.1 27.9 %collective-permute-start.43 = (bf16[16,320,128]{2,1,0:T(8,128)(2,1)}, bf16[16,320,128]{2,1,0:T(8,128)(2,1)S(1)}, u32[]{:S(2)}, u32[]{:S(2)}) collective-permute-start(bf16[16,320,128]{2,1,0:T(8,128)(2,1)} %get-tuple-element.114), channel_id=1, source_target_pairs={{0,1},{1,0},{2,3},{3,2},{4,5},{5,4},{6,7},{7,6},{8,9},{9,8},{10,11... | collective-permute-start | bytes 3932168 | tf_op jit(solution)/shard_map/ppermute | solution.py:676
  458.3 5.2 collective-permute-start.39
  473.0 8.6 %collective-permute-start.44 = (bf16[128,2048]{1,0:T(8,128)(2,1)}, bf16[128,2048]{1,0:T(8,128)(2,1)}, u32[]{:S(2)}, u32[]{:S(2)}) collective-permute-start(bf16[128,2048]{1,0:T(8,128)(2,1)} %maximum_select_fusion.4.rest_0_.refs_10_), channel_id=1, source_target_pairs={{0,8},{2,6},{8,16},{10,2},{16,24},{18,10},{24,28},{26,18},{28,20},... | collective-permute-start | bytes 1572872 | tf_op jit(solution)/shard_map/ppermute | solution.py:670
  474.7 52.5 %collective-permute-start.50 = (bf16[16,464,128]{2,1,0:T(8,128)(2,1)}, bf16[16,464,128]{2,1,0:T(8,128)(2,1)S(1)}, u32[]{:S(2)}, u32[]{:S(2)}) collective-permute-start(bf16[16,464,128]{2,1,0:T(8,128)(2,1)} %get-tuple-element.116), channel_id=1, source_target_pairs={{0,1},{1,0},{2,3},{3,2},{4,5},{5,4},{6,7},{7,6},{8,9},{9,8},{10,11... | collective-permute-start | bytes 5701640 | tf_op jit(solution)/shard_map/ppermute | solution.py:676
  478.2 5.1 collective-permute-start.40
  481.7 8.5 %collective-permute-start.45 = (bf16[128,2048]{1,0:T(8,128)(2,1)}, bf16[128,2048]{1,0:T(8,128)(2,1)S(1)}, u32[]{:S(2)}, u32[]{:S(2)}) collective-permute-start(bf16[128,2048]{1,0:T(8,128)(2,1)} %collective-permute-done.44.rest_1_.refs_11_), channel_id=1, source_target_pairs={{0,8},{2,6},{8,16},{10,2},{16,24},{18,10},{24,28},{26,18},{28,20},... | collective-permute-start | bytes 1572872 | tf_op jit(solution)/shard_map/ppermute | solution.py:670
  484.5 41.8 %collective-permute-start.41 = (bf16[128,2048]{1,0:T(8,128)(2,1)S(1)}, bf16[128,2048]{1,0:T(8,128)(2,1)S(1)}, u32[]{:S(2)}, u32[]{:S(2)}) collective-permute-start(bf16[128,2048]{1,0:T(8,128)(2,1)S(1)} %maximum_select_fusion.3), channel_id=1, source_target_pairs={{0,1},{1,0},{2,3},{3,2},{4,5},{5,4},{6,7},{7,6},{8,9},{9,8},{10,11... | collective-permute-start | bytes 1572872 | tf_op jit(solution)/shard_map/ppermute | solution.py:676
  490.2 36.9 %collective-permute-start.46 = (bf16[128,2048]{1,0:T(8,128)(2,1)S(1)}, bf16[128,2048]{1,0:T(8,128)(2,1)S(1)}, u32[]{:S(2)}, u32[]{:S(2)}) collective-permute-start(bf16[128,2048]{1,0:T(8,128)(2,1)S(1)} %collective-permute-done.45.rest_2_.refs_12_), channel_id=1, source_target_pairs={{0,8},{2,6},{8,16},{10,2},{16,24},{18,10},{24,28},{26,18},{28,20},... | collective-permute-start | bytes 1572872 | tf_op jit(solution)/shard_map/ppermute | solution.py:670
  527.9 5.3 collective-permute-start.51
  535.6 81.3 %all-to-all-start.3 = ((bf16[16,784,128]{2,1,0:T(8,128)(2,1)}), bf16[16,784,128]{2,1,0:T(8,128)(2,1)S(1)}, u32[]{:S(2)}, u32[]{:S(2)}) async-start(bf16[16,784,128]{2,1,0:T(8,128)(2,1)} %pad_maximum_fusion), calls=%async_computation.3 | async-start | bytes 6422528 | tf_op jit(solution)/shard_map/all_to_all | solution.py:727
  546.0 2.8 collective-permute-start.48
  546.2 3.4 collective-permute-start.49
  546.5 3.4 collective-permute-start.52
  558.9 38.4 %collective-permute-start.57 = (bf16[16,320,128]{2,1,0:T(8,128)(2,1)}, bf16[16,320,128]{2,1,0:T(8,128)(2,1)}, u32[]{:S(2)}, u32[]{:S(2)}) collective-permute-start(bf16[16,320,128]{2,1,0:T(8,128)(2,1)} %get-tuple-element.129), channel_id=1, source_target_pairs={{0,1},{1,0},{2,3},{3,2},{4,5},{5,4},{6,7},{7,6},{8,9},{9,8},{10,11... | collective-permute-start | bytes 3932168 | tf_op jit(solution)/shard_map/ppermute | solution.py:676
  586.6 39.4 %collective-permute-start.53 = (bf16[448,2048]{1,0:T(8,128)(2,1)}, bf16[448,2048]{1,0:T(8,128)(2,1)}, u32[]{:S(2)}, u32[]{:S(2)}) collective-permute-start(bf16[448,2048]{1,0:T(8,128)(2,1)} %get-tuple-element.122), channel_id=1, source_target_pairs={{0,2},{2,0},{4,6},{6,4},{8,10},{10,8},{12,14},{14,12},{16,18},{18,... | collective-permute-start | bytes 5505032 | tf_op jit(solution)/shard_map/ppermute | solution.py:673
  616.9 47.5 %all-to-all-start.4 = ((bf16[16,320,128]{2,1,0:T(8,128)(2,1)}), bf16[16,320,128]{2,1,0:T(8,128)(2,1)}, u32[]{:S(2)}, u32[]{:S(2)}) async-start(bf16[16,320,128]{2,1,0:T(8,128)(2,1)} %add_convert_fusion.2), calls=%async_computation.4 | async-start | bytes 2621440 | tf_op jit(solution)/shard_map/all_to_all | solution.py:727
  622.1 47.2 %collective-permute-start.63 = (bf16[16,464,128]{2,1,0:T(8,128)(2,1)}, bf16[16,464,128]{2,1,0:T(8,128)(2,1)}, u32[]{:S(2)}, u32[]{:S(2)}) collective-permute-start(bf16[16,464,128]{2,1,0:T(8,128)(2,1)} %get-tuple-element.135), channel_id=1, source_target_pairs={{0,1},{1,0},{2,3},{3,2},{4,5},{5,4},{6,7},{7,6},{8,9},{9,8},{10,11... | collective-permute-start | bytes 5701640 | tf_op jit(solution)/shard_map/ppermute | solution.py:676
  624.5 28.9 %collective-permute-start.55 = (bf16[1,64,2048]{2,1,0:T(8,128)(2,1)S(1)}, bf16[1,64,2048]{2,1,0:T(8,128)(2,1)S(1)}, u32[]{:S(2)}, u32[]{:S(2)}) collective-permute-start(bf16[1,64,2048]{2,1,0:T(8,128)(2,1)S(1)} %fusion.16), channel_id=1, source_target_pairs={{0,8},{2,6},{8,16},{10,2},{16,24},{18,10},{24,28},{26,18},{28,20},... | collective-permute-start | bytes 786440 | tf_op jit(solution)/shard_map/ppermute | solution.py:670
  654.9 8.5 %collective-permute-start.56 = (bf16[1,128,2048]{2,1,0:T(8,128)(2,1)S(1)}, bf16[1,128,2048]{2,1,0:T(8,128)(2,1)S(1)}, u32[]{:S(2)}, u32[]{:S(2)}) collective-permute-start(bf16[1,128,2048]{2,1,0:T(8,128)(2,1)S(1)} %fusion.8), channel_id=1, source_target_pairs={{0,8},{2,6},{8,16},{10,2},{16,24},{18,10},{24,28},{26,18},{28,20},... | collective-permute-start | bytes 1572872 | tf_op jit(solution)/shard_map/ppermute | solution.py:670
  667.0 11.8 %collective-permute-start.58 = (bf16[1,128,2048]{2,1,0:T(8,128)(2,1)}, bf16[1,128,2048]{2,1,0:T(8,128)(2,1)}, u32[]{:S(2)}, u32[]{:S(2)}) collective-permute-start(bf16[1,128,2048]{2,1,0:T(8,128)(2,1)} %fusion.4), channel_id=1, source_target_pairs={{0,8},{2,6},{8,16},{10,2},{16,24},{18,10},{24,28},{26,18},{28,20},... | collective-permute-start | bytes 1572872 | tf_op jit(solution)/shard_map/ppermute | solution.py:670
  672.7 90.0 %all-to-all-start.5 = ((bf16[16,464,128]{2,1,0:T(8,128)(2,1)}), bf16[16,464,128]{2,1,0:T(8,128)(2,1)}, u32[]{:S(2)}, u32[]{:S(2)}) async-start(bf16[16,464,128]{2,1,0:T(8,128)(2,1)} %add_convert_fusion), calls=%async_computation.5 | async-start | bytes 3801088 | tf_op jit(solution)/shard_map/all_to_all | solution.py:727
  681.4 44.6 %collective-permute-start.59 = (bf16[1,128,2048]{2,1,0:T(8,128)(2,1)S(1)}, bf16[1,128,2048]{2,1,0:T(8,128)(2,1)S(1)}, u32[]{:S(2)}, u32[]{:S(2)}) collective-permute-start(bf16[1,128,2048]{2,1,0:T(8,128)(2,1)S(1)} %fusion.3), channel_id=1, source_target_pairs={{0,8},{2,6},{8,16},{10,2},{16,24},{18,10},{24,28},{26,18},{28,20},... | collective-permute-start | bytes 1572872 | tf_op jit(solution)/shard_map/ppermute | solution.py:670
  726.8 3.6 collective-permute-start.60
  737.7 23.0 %collective-permute-start.62 = (bf16[128,2048]{1,0:T(8,128)(2,1)}, bf16[128,2048]{1,0:T(8,128)(2,1)}, u32[]{:S(2)}, u32[]{:S(2)}) collective-permute-start(bf16[128,2048]{1,0:T(8,128)(2,1)} %maximum_select_fusion.6), channel_id=1, source_target_pairs={{0,1},{1,0},{2,3},{3,2},{4,5},{5,4},{6,7},{7,6},{8,9},{9,8},{10,11... | collective-permute-start | bytes 1572872 | tf_op jit(solution)/shard_map/ppermute | solution.py:676
  739.1 12.1 %collective-permute-start.64 = (f32[2,448]{1,0:T(2,128)S(1)}, f32[2,448]{1,0:T(2,128)S(1)}, u32[]{:S(2)}, u32[]{:S(2)}) collective-permute-start(f32[2,448]{1,0:T(2,128)S(1)} %pad_maximum_fusion.4), channel_id=1, source_target_pairs={{0,1},{1,0},{2,3},{3,2},{4,5},{5,4},{6,7},{7,6},{8,9},{9,8},{10,11... | collective-permute-start | bytes 10760 | tf_op jit(solution)/shard_map/ppermute | solution.py:676
  (52 other events, 938.6 us)

commit v8 on v7

--- a/solution.py
+++ b/solution.py
@@ -299,6 +299,7 @@
     elif mode == "middle":
         (bias_ref,) = take(1)
         rows_in = take(9)
+        grads_in = take(9)
     else:
         heads_ref, hidden_ref, normed_ref = take(3)
         grads_in = take(9)
@@ -318,10 +319,10 @@
 
     pairs = []
     if mode == "first":
-        pairs += slot_copies(rows_in, None, raw, core)
+        pairs += slot_copies(rows_in, 0, raw, core)
     if mode == "middle":
-        pairs += slot_copies(rows_in, 0, normed_ref, core)
-        pairs += slot_copies(rows_in, 1, grad_rows_ref, core)
+        pairs += slot_copies(rows_in, None, normed_ref, core)
+        pairs += slot_copies(grads_in, 1, grad_rows_ref, core)
     if mode == "last":
         pairs += slot_copies(grads_in, None, grad_rows_ref, core)
     for copy in run_copies(pairs, sems, 0):
@@ -517,7 +518,8 @@
 
 
 def spread_gradients(up_ref, down_ref, *rest):
-    qkv_ref, out_w_ref, fc1_ref, fc2_ref = rest[-4:]
+    qkv_ref, out_w_ref, fc1_ref, fc2_ref, mark_ref = rest[-5:]
+    mark_ref[...] = jnp.zeros_like(mark_ref)
     down = down_ref.shape[1] - DOWN_ROWS
     for p in range(3):
         rows = slice(p * HEAD_DIM, (p + 1) * HEAD_DIM)
@@ -539,6 +541,7 @@
         jax.ShapeDtypeStruct((LAYERS, GROUP * HEAD_DIM, 128), f32),
         jax.ShapeDtypeStruct((LAYERS, 128, GROUP * 256), f32),
         jax.ShapeDtypeStruct((LAYERS, GROUP * 256, 128), f32),
+        jax.ShapeDtypeStruct((8, 128), f32),
     ]
     return pl.pallas_call(
         spread_gradients,
@@ -553,6 +556,7 @@
             pl.BlockSpec((1, 128, 128), lambda i: (layer, i, 0)),
             pl.BlockSpec((1, 128, 512), lambda i: (layer, 0, i)),
             pl.BlockSpec((1, 512, 128), lambda i: (layer, i, 0)),
+            pl.BlockSpec((8, 128), lambda i: (0, 0)),
         ],
         out_shape=shapes,
         input_output_aliases={2 + n: n for n in range(len(filled))},
@@ -835,12 +839,13 @@
         jnp.concatenate([nought, sine, rest] * 2, axis=1),
     )
 
-    mine = jnp.where(tensor == core, hidden_in, across(hidden_in))
-    cotangent = jnp.where(tensor == core, out_cotangent, across(out_cotangent))
-    cotangent = jnp.where(labels[0][:, None] > 0, cotangent, jnp.zeros_like(cotangent))
+    both = jnp.stack([hidden_in, out_cotangent])
+    both = jnp.where(tensor == core, both, across(both))
+    keeps = jnp.stack([jnp.ones_like(labels[0]), (labels[0] > 0).astype(labels.dtype)]).astype(bf16)
+    both = both * keeps[:, :, None]
     if groups == 1:
         inputs = gather_rows(
-            after(mine, packed_down, packed_last, firsts[0], firsts[2]),
+            after(both, packed_down, packed_last, firsts[0], firsts[2]),
             {1: (firsts[1], tables[0]), 2: (tables[1], tables[2], allowed), side: (down_other, weights[0][0])},
         )
         slab = spread(after(packed_last, inputs[-2]))
@@ -848,9 +853,9 @@
         weights.append(call_join(join_halves, slab, others, True, True))
         slabs = (slab,)
     else:
-        inputs = gather_rows(mine)
+        inputs = gather_rows(both)
         slabs, others = (), ()
-    state, grad_state = my_half(mine, at), my_half(cotangent, at)
+    state, grad_state = my_half(both, at, 1)
 
     normed, heads, hidden_pre, wide, *parts = call_pass(
         "first", core_word, weights[0], tables, allowed, [bias_rows[0:1], gains[0], shifts[0]], inputs
@@ -859,14 +864,12 @@
     next_state, normed_own = call_end(
         partial(forward_end, False),
         core_word,
-        ring_sum((after(parts[0], *slabs), parts[1], parts[2]), needed={})[0],
+        ring_sum((after(parts[0], *slabs), parts[1], parts[2]), needed={0: others[:1]})[0],
         [state, added_bias[0], gains[1], shifts[1]],
         [jax.ShapeDtypeStruct(rows_shape, f32), jax.ShapeDtypeStruct(rows_shape, bf16)],
         "forward_end",
     )
-    normed_chunks = gather_rows(
-        jnp.stack([in_order(normed_own, across(normed_own)), cotangent]), {0: others[:1], 2: others[1:]}
-    )
+    normed_chunks = gather_rows(in_order(normed_own, across(normed_own)), {1: others[1:]})
 
     def handed_back(own_rows):
         filled = in_order(own_rows, across(own_rows))
@@ -902,7 +905,7 @@
         )
 
     normed_last, grad_rows, wide_last, slim, sums, *parts = call_pass(
-        "middle", core_word, weights[1], tables, allowed, [bias_rows[1:2]], normed_chunks
+        "middle", core_word, weights[1], tables, allowed, [bias_rows[1:2]], normed_chunks + inputs
     )
     out_parts = parts[:3]
     down_pair = down_gradients(wide_last, [grad_rows])
@@ -919,7 +922,7 @@
         "forward_out",
     )
     hidden_out = handed_back(hidden_out)
-    grad_chunks = gather_rows(in_order(grad_low, across(grad_low)), {0: (down_sent,), side: (up_sent, hidden_out)})
+    grad_chunks = gather_rows(in_order(grad_low, across(grad_low)), {0: (down_sent,), 2: (up_sent,)})
     both_last = summed([(up_pair[0], after(up_sent, grad_chunks[-2])), (down_pair[0], down_sent)])
     up_last, down_last = both_last[:, : UP_ROWS + SUM_ROWS], both_last[:, UP_ROWS + SUM_ROWS :]
 
@@ -933,8 +936,8 @@
     down_first = summed([(down_pair[0], after(down_sent, up_pair[0]))], both_last)
     needed = {1: (down_first,)}
     if groups == 1:
-        filled = call_spread(both_last, both_last, 1, [])
-        needed[0] = (filled[1][:, :8],)
+        *filled, mark = call_spread(both_last, both_last, 1, [])
+        needed[0] = (mark, hidden_out)
     (grad_end,) = ring_sum((after(parts[0], up_pair[0], both_last), parts[1], parts[2]), needed=needed)
     up_first = summed([(up_pair[0], up_sent)], down_first)
     _, grad_low = backward_finish(grad_end, state, grad_state, 0)
@@ -953,7 +956,7 @@
     bias_sums = bias_own + over(bias_other)
     bias_qkv, bias_up = bias_sums[:, : 3 * HEAD_DIM].reshape(LAYERS, 3, HEAD_DIM), bias_sums[:, 3 * HEAD_DIM :]
     if groups == 1:
-        grad_qkv, grad_out, grad_up, grad_down = call_spread(up_first, down_first, 0, filled)
+        grad_qkv, grad_out, grad_up, grad_down, _ = call_spread(up_first, down_first, 0, filled)
         grad_qkv = grad_qkv.transpose(0, 2, 1, 3)
     else:
         bias_qkv = lax.all_gather(lax.psum(bias_qkv, "dp", axis_index_groups=outer), "dp", axis=2, axis_index_groups=inner, tiled=True)

time: 784 us -> 765 us (0.976)
  waiting for transfers between devices: 403 us -> 389 us
  starting transfers between devices: 104 us -> 94.5 us
    ppermute x12, waiting for transfers between devices: 109 us -> 89.1 us  [over(): return lax.ppermute(x, 'tensor', [(0, 1), (1, 0)])]
    ppermute x29 -> x28, starting transfers between devices: 27.5 us -> 22.4 us  [across(): return lax.ppermute(x, 'dp', core_pairs)]
    ppermute x29 -> x28, waiting for transfers between devices: 15.6 us -> 17.9 us  [across(): return lax.ppermute(x, 'dp', core_pairs)]
  transfers between devices with their start and end apart: 71 -> 70, of which waited for: 46 -> 45; matrix products, arithmetic and copies ran while one was open for 8% -> 8% of each run, Pallas kernels for 18% -> 18%
where the time goes in v8:
time: 765 us; the launch traced here: 753 us
  waiting for transfers between devices  389 us (51%)
  Pallas kernels  183 us (24%)
  starting transfers between devices  94.5 us (12%)
  other arithmetic  60.9 us (8%)
  local copies, waits for them, and re-layouts  23.9 us (3%)
    ppermute x24, waiting for transfers between devices, along(): return lax.ppermute(x, 'dp', ring_pairs)  179 us
    all_to_all x6, waiting for transfers between devices, spread(): return lax.all_to_all(x, 'dp', 0, 0, axis_index_groups=inner, tiled=True)  103 us
    pallas_call x3, Pallas kernels, call_pass(): pl.pallas_call(partial(layer_pass, mode), in_specs=[SMEM_SPEC] + [VMEM_SP...  91.8 us
    ppermute x12, waiting for transfers between devices, over(): return lax.ppermute(x, 'tensor', [(0, 1), (1, 0)])  89.1 us
    all_to_all x6, starting transfers between devices, spread(): return lax.all_to_all(x, 'dp', 0, 0, axis_index_groups=inner, tiled=True)  38.5 us
    pallas_call x4, Pallas kernels, call_gradients(): pl.pallas_call(partial(gradient_slabs, own_rows, other_rows, with_sums, l...  37.9 us
    ppermute x28, starting transfers between devices, across(): return lax.ppermute(x, 'dp', core_pairs)  22.4 us
    ppermute x24, starting transfers between devices, along(): return lax.ppermute(x, 'dp', ring_pairs)  20 us
  transfers between devices with their start and end apart: 70, of which 45 were waited for; matrix products, arithmetic and copies ran while one was open for 8% of the time, Pallas kernels for 18%

profile of v8, /device:TPU:13, one launch (start us, length us, event | category | flops | bytes accessed | tf_op | source)
XLA Modules:
  0.0 753.2 jit_solution(16895155302746816243)
XLA Ops:
  4.8 4.0 pack_first.1
  8.8 6.5 all-to-all-start
  15.3 3.5 pack_down.1
  18.9 39.7 %all-to-all-done.own_ref = bf16[16,464,128]{2,1,0:T(8,128)(2,1)S(1)} async-done(((bf16[16,464,128]{2,1,0:T(8,128)(2,1)}), bf16[16,464,128]{2,1,0:T(8,128)(2,1)S(1)}, u32[]{:S(2)}, u32[]{:S(2)}) %all-to-all-start) | async-done | bytes 1900576 | tf_op jit(solution)/shard_map/all_to_all | solution.py:731
  58.5 4.8 all-to-all-start.1
  69.3 4.4 pack_both.1
  73.8 2.7 select_multiply_fusion.refs_10_.refs_17_
  76.4 17.9 %all-to-all-done.1.own_ref = bf16[16,320,128]{2,1,0:T(8,128)(2,1)S(1)} async-done(((bf16[16,320,128]{2,1,0:T(8,128)(2,1)}), bf16[16,320,128]{2,1,0:T(8,128)(2,1)S(1)}, u32[]{:S(2)}, u32[]{:S(2)}) %all-to-all-start.1) | async-done | bytes 1310752 | tf_op jit(solution)/shard_map/all_to_all | solution.py:731
  98.1 2.7 concatenate.71.refs_3_
  100.7 10.1 %collective-permute-done.2.other_ref = bf16[16,464,128]{2,1,0:T(8,128)(2,1)} collective-permute-done((bf16[16,464,128]{2,1,0:T(8,128)(2,1)S(1)}, bf16[16,464,128]{2,1,0:T(8,128)(2,1)}, u32[]{:S(2)}, u32[]{:S(2)}) %collective-permute-start.2) | collective-permute-done | bytes 1900576 | tf_op jit(solution)/shard_map/ppermute | solution.py:680
  118.0 7.1 collective-permute-done.3.refs_12_.refs_19_
  126.3 4.8 join_up.1.refs_1_
  131.1 8.2 %collective-permute-done.4.refs_13_.refs_20_ = bf16[2,128,2048]{2,1,0:T(8,128)(2,1)S(1)} collective-permute-done((bf16[2,128,2048]{2,1,0:T(8,128)(2,1)}, bf16[2,128,2048]{2,1,0:T(8,128)(2,1)S(1)}, u32[]{:S(2)}, u32[]{:S(2)}) %collective-permute-start.4) | collective-permute-done | bytes 1048608 | tf_op jit(solution)/shard_map/ppermute | solution.py:674
  139.3 2.9 collective-permute-done.5.other_ref
  143.4 7.1 collective-permute-done.6.refs_17_.refs_24_
  151.4 6.8 all-to-all-start.2
  164.5 4.2 join_down.1.refs_2_
  168.8 29.3 %pass_first.1 = (bf16[1024,2048]{1,0:T(8,128)(2,1)}, bf16[1024,384]{1,0:T(8,128)(2,1)}, f32[1024,512]{1,0:T(8,128)}, bf16[1024,640]{1,0:T(8,128)(2,1)}, bf16[64,...) custom-call(s32[1]{0:T(128)} %bitcast.refs_0_.core_ref, bf16[2048,896]{1,0:T(8,128)(2,1)} %join_up.1.refs_1_, ...), custom_call_target="tpu_custom_call" | custom-call | flops 19327352832 | bytes 20000000 | tf_op jit(solution)/shard_map/pass_first/pallas_call | solution.py:443
  198.2 29.8 %all-to-all-done.2.own_ref = bf16[16,768,128]{2,1,0:T(8,128)(2,1)S(1)} async-done(((bf16[16,768,128]{2,1,0:T(8,128)(2,1)}), bf16[16,768,128]{2,1,0:T(8,128)(2,1)S(1)}, u32[]{:S(2)}, u32[]{:S(2)}) %all-to-all-start.2) | async-done | bytes 3145760 | tf_op jit(solution)/shard_map/all_to_all | solution.py:731
  233.7 2.8 collective-permute-done.16
  237.9 8.3 %collective-permute-done.17 = bf16[1,128,2048]{2,1,0:T(8,128)(2,1)S(1)} collective-permute-done((bf16[1,128,2048]{2,1,0:T(8,128)(2,1)S(1)}, bf16[1,128,2048]{2,1,0:T(8,128)(2,1)S(1)}, u32[]{:S(2)}, u32[]{:S(2)}) %collective-permute-start.17) | collective-permute-done | bytes 524320 | tf_op jit(solution)/shard_map/ppermute | solution.py:674
  247.6 8.3 %collective-permute-done.18 = bf16[1,128,2048]{2,1,0:T(8,128)(2,1)S(1)} collective-permute-done((bf16[1,128,2048]{2,1,0:T(8,128)(2,1)S(1)}, bf16[1,128,2048]{2,1,0:T(8,128)(2,1)S(1)}, u32[]{:S(2)}, u32[]{:S(2)}) %collective-permute-start.18) | collective-permute-done | bytes 524320 | tf_op jit(solution)/shard_map/ppermute | solution.py:674
  256.0 12.3 %collective-permute-done.7.lower_ref = bf16[8,768,128]{2,1,0:T(8,128)(2,1)S(1)} collective-permute-done((bf16[8,768,128]{2,1,0:T(8,128)(2,1)S(1)}, bf16[8,768,128]{2,1,0:T(8,128)(2,1)S(1)}, u32[]{:S(2)}, u32[]{:S(2)}) %collective-permute-start.7) | collective-permute-done | bytes 1572896 | tf_op jit(solution)/shard_map/ppermute | solution.py:680
  273.0 6.4 collective-permute-done.19.moving_ref
  284.0 2.5 forward_end.1
  290.8 17.3 %collective-permute-done.8.upper_ref = bf16[8,768,128]{2,1,0:T(8,128)(2,1)} collective-permute-done((bf16[8,768,128]{2,1,0:T(8,128)(2,1)}, bf16[8,768,128]{2,1,0:T(8,128)(2,1)}, u32[]{:S(2)}, u32[]{:S(2)}) %collective-permute-start.8) | collective-permute-done | bytes 1572896 | tf_op jit(solution)/shard_map/ppermute | solution.py:680
  308.1 8.3 %collective-permute-done.23.refs_10_ = bf16[128,2048]{1,0:T(8,128)(2,1)S(1)} collective-permute-done((bf16[128,2048]{1,0:T(8,128)(2,1)S(1)}, bf16[128,2048]{1,0:T(8,128)(2,1)S(1)}, u32[]{:S(2)}, u32[]{:S(2)}) %collective-permute-start.23) | collective-permute-done | bytes 524320 | tf_op jit(solution)/shard_map/ppermute | solution.py:674
  318.2 6.6 collective-permute-done.24.refs_11_
  324.8 2.6 collective-permute-start.27
  327.4 2.6 collective-permute-done.28.refs_15_
  330.0 3.7 collective-permute-start.29
  333.7 6.3 join_halves.1
  341.1 36.0 %pass_middle.1 = (bf16[1024,2048]{1,0:T(8,128)(2,1)}, bf16[1024,2048]{1,0:T(8,128)(2,1)}, bf16[1024,640]{1,0:T(8,128)(2,1)}, bf16[1024,896]{1,0:T(8,128)(2,1)}, ...) custom-call(s32[1]{0:T(128)} %bitcast.refs_0_.core_ref, ...), custom_call_target="tpu_custom_call" | custom-call | flops 38654705664 | bytes 40000000 | tf_op jit(solution)/shard_map/pass_middle/pallas_call | solution.py:443
  378.3 3.3 collective-permute-done.31
  389.4 4.7 collective-permute-done.33
  395.8 8.8 %down_gradients.2 = (bf16[16,320,128]{2,1,0:T(8,128)(2,1)}, bf16[16,320,128]{2,1,0:T(8,128)(2,1)}) custom-call(s32[1]{0:T(128)} %bitcast.refs_0_.core_ref, bf16[1024,640]{1,0:T(8,128)(2,1)} %get-tuple-element.101.left_ref, bf16[1024,2048]{1,0:T(8,128)(2,1)} %get-tuple-element.102.rest_0_), custom_call_target="tpu_custom_call" | custom-call | flops 5368709120 | bytes 10747904 | tf_op jit(solution)/shard_map/down_gradients/pallas_call | solution.py:505
  404.6 5.2 collective-permute-done.35
  413.0 10.1 %up_gradients.2 = (bf16[16,464,128]{2,1,0:T(8,128)(2,1)}, bf16[16,464,128]{2,1,0:T(8,128)(2,1)}, f32[1,896]{1,0:T(1,128)}) custom-call(s32[1]{0:T(128)} %bitcast.refs_0_.core_ref, bf16[1024,896]{1,0:T(8,128)(2,1)} %get-tuple-element.105.left_ref, bf16[1024,2048]{1,0:T(8,128)(2,1)} %get-tuple-element.106.rest_0_, f32[16,2048]{1,0:T(8,128)} %get-tuple-element.107.rest_1_), custom_call_target="tpu_custom_call" | custom-call | flops 7516192768 | bytes 13369344 | tf_op jit(solution)/shard_map/up_gradients/pallas_call | solution.py:505
  423.1 3.7 collective-permute-done.36
  429.0 12.5 %collective-permute-done.37.moving_ref = bf16[2,128,2048]{2,1,0:T(8,128)(2,1)S(1)} collective-permute-done((bf16[2,128,2048]{2,1,0:T(8,128)(2,1)S(1)}, bf16[2,128,2048]{2,1,0:T(8,128)(2,1)S(1)}, u32[]{:S(2)}, u32[]{:S(2)}) %collective-permute-start.37) | collective-permute-done | bytes 1048608 | tf_op jit(solution)/shard_map/ppermute | solution.py:674
  441.5 3.5 collective-permute-start.38
  447.3 2.9 backward_end.2
  453.2 2.8 collective-permute-done.42
  457.8 7.5 collective-permute-done.43.rest_1_.refs_11_
  466.2 30.5 %collective-permute-done.45 = bf16[16,464,128]{2,1,0:T(8,128)(2,1)S(1)} collective-permute-done((bf16[16,464,128]{2,1,0:T(8,128)(2,1)}, bf16[16,464,128]{2,1,0:T(8,128)(2,1)S(1)}, u32[]{:S(2)}, u32[]{:S(2)}) %collective-permute-start.45) | collective-permute-done | bytes 1900576 | tf_op jit(solution)/shard_map/ppermute | solution.py:680
  498.5 7.5 collective-permute-done.46.rest_3_.refs_13_
  509.3 2.8 collective-permute-done.50.rest_7_.refs_17_
  514.5 9.5 %all-to-all-start.3 = ((bf16[16,784,128]{2,1,0:T(8,128)(2,1)}), bf16[16,784,128]{2,1,0:T(8,128)(2,1)S(1)}, u32[]{:S(2)}, u32[]{:S(2)}) async-start(bf16[16,784,128]{2,1,0:T(8,128)(2,1)} %pad_maximum_fusion), calls=%async_computation.3 | async-start | bytes 6422528 | tf_op jit(solution)/shard_map/all_to_all | solution.py:731
  529.0 8.9 %down_gradients.3 = (bf16[16,320,128]{2,1,0:T(8,128)(2,1)}, bf16[16,320,128]{2,1,0:T(8,128)(2,1)}) custom-call(s32[1]{0:T(128)} %bitcast.refs_0_.core_ref, bf16[1024,640]{1,0:T(8,128)(2,1)} %get-tuple-element.113.left_ref, bf16[128,2048]{1,0:T(8,128)(2,1)} %copy-done.21, bf16[128,2048]{1,0:T(8,128)(2,1)} %copy-done.39, bf16[128,2048]{1,0:T(8,128)(2,1)} %copy-done.40, ...), custom_call_target="tpu_custom_call" | custom-call | flops 5368709120 | bytes 10747904 | tf_op jit(solution)/shard_map/down_gradients/pallas_call | solution.py:505
  539.1 26.5 %pass_last.1 = (bf16[1024,2048]{1,0:T(8,128)(2,1)}, bf16[1024,896]{1,0:T(8,128)(2,1)}, f32[16,2048]{1,0:T(8,128)}, bf16[64,2048]{1,0:T(8,128)(2,1)}, bf16[448,20...) custom-call(s32[1]{0:T(128)} %bitcast.refs_0_.core_ref, bf16[2048,896]{1,0:T(8,128)(2,1)} %join_up.1.refs_1_, ...), custom_call_target="tpu_custom_call" | custom-call | flops 19327352832 | bytes 20000000 | tf_op jit(solution)/shard_map/pass_last/pallas_call | solution.py:443
  566.2 10.1 %up_gradients.3 = (bf16[16,464,128]{2,1,0:T(8,128)(2,1)}, bf16[16,464,128]{2,1,0:T(8,128)(2,1)}, f32[1,896]{1,0:T(1,128)}) custom-call(s32[1]{0:T(128)} %bitcast.refs_0_.core_ref, bf16[1024,896]{1,0:T(8,128)(2,1)} %get-tuple-element.125.left_ref, bf16[1024,2048]{1,0:T(8,128)(2,1)} %get-tuple-element.121.refs_9_.rest_0_, f32[16,2048]{1,0:T(8,128)} %get-tuple-element.126.rest_1_), custom_call_target="tpu_custom_call" | custom-call | flops 7516192768 | bytes 13369344 | tf_op jit(solution)/shard_map/up_gradients/pallas_call | solution.py:505
  576.3 3.1 add_convert_fusion.2
  579.4 16.0 %all-to-all-done.3.up_ref.down_ref = bf16[16,784,128]{2,1,0:T(8,128)(2,1)S(1)} async-done(((bf16[16,784,128]{2,1,0:T(8,128)(2,1)}), bf16[16,784,128]{2,1,0:T(8,128)(2,1)S(1)}, u32[]{:S(2)}, u32[]{:S(2)}) %all-to-all-start.3) | async-done | bytes 3211296 | tf_op jit(solution)/shard_map/all_to_all | solution.py:731
  595.4 4.8 all-to-all-start.4
  604.2 27.7 %collective-permute-done.54 = bf16[1,64,2048]{2,1,0:T(8,128)(2,1)S(1)} collective-permute-done((bf16[1,64,2048]{2,1,0:T(8,128)(2,1)S(1)}, bf16[1,64,2048]{2,1,0:T(8,128)(2,1)S(1)}, u32[]{:S(2)}, u32[]{:S(2)}) %collective-permute-start.54) | collective-permute-done | bytes 262176 | tf_op jit(solution)/shard_map/ppermute | solution.py:674
  634.1 2.5 collective-permute-start.55
  646.1 2.6 fusion.4
  650.2 3.4 add_convert_fusion
  653.5 6.1 all-to-all-start.5
  665.3 41.5 %collective-permute-done.58.moving_ref = bf16[1,128,2048]{2,1,0:T(8,128)(2,1)S(1)} collective-permute-done((bf16[1,128,2048]{2,1,0:T(8,128)(2,1)S(1)}, bf16[1,128,2048]{2,1,0:T(8,128)(2,1)S(1)}, u32[]{:S(2)}, u32[]{:S(2)}) %collective-permute-start.58) | collective-permute-done | bytes 524320 | tf_op jit(solution)/shard_map/ppermute | solution.py:674
  711.9 2.9 backward_end.3
  720.3 11.8 %collective-permute-done.63 = f32[2,448]{1,0:T(2,128)S(1)} collective-permute-done((f32[2,448]{1,0:T(2,128)S(1)}, f32[2,448]{1,0:T(2,128)S(1)}, u32[]{:S(2)}, u32[]{:S(2)}) %collective-permute-start.63) | collective-permute-done | bytes 3616 | tf_op jit(solution)/shard_map/ppermute | solution.py:680
  733.5 7.9 %spread_gradients.2 = (f32[2,3,128,1024]{3,2,1,0:T(8,128)}, f32[2,1024,128]{2,1,0:T(8,128)}, f32[2,128,4096]{2,1,0:T(8,128)}, f32[2,4096,128]{2,1,0:T(8,128)}, f32[8,128]{1,0:T(8,128)}) custom-call(bf16[16,784,128]{2,1,0:T(8,128)(2,1)} %copy-done, bf16[16,784,128]{2,1,0:T(8,128)(2,1)} %copy-done), custom_call_target="tpu_custom_call" | custom-call | tf_op jit(solution)/shard_map/spread_gradients/pallas_call | solution.py:546
  745.4 7.3 spread_gradients.3
  (307 shorter events, 132.6 us)
Async XLA Ops:
  8.8 49.7 %all-to-all-start = ((bf16[16,464,128]{2,1,0:T(8,128)(2,1)}), bf16[16,464,128]{2,1,0:T(8,128)(2,1)S(1)}, u32[]{:S(2)}, u32[]{:S(2)}) async-start(bf16[16,464,128]{2,1,0:T(8,128)(2,1)} %pack_first.1), calls=%async_computation | async-start | bytes 3801088 | tf_op jit(solution)/shard_map/all_to_all | solution.py:731
  58.5 35.7 %all-to-all-start.1 = ((bf16[16,320,128]{2,1,0:T(8,128)(2,1)}), bf16[16,320,128]{2,1,0:T(8,128)(2,1)S(1)}, u32[]{:S(2)}, u32[]{:S(2)}) async-start(bf16[16,320,128]{2,1,0:T(8,128)(2,1)} %pack_down.1), calls=%async_computation.1 | async-start | bytes 2621440 | tf_op jit(solution)/shard_map/all_to_all | solution.py:731
  65.6 8.2 %collective-permute-start = (bf16[2,128,2048]{2,1,0:T(8,128)(2,1)}, bf16[2,128,2048]{2,1,0:T(8,128)(2,1)}, u32[]{:S(2)}, u32[]{:S(2)}) collective-permute-start(bf16[2,128,2048]{2,1,0:T(8,128)(2,1)} %pad_maximum_fusion.1), channel_id=1, source_target_pairs={{0,2},{2,0},{4,6},{6,4},{8,10},{10,8},{12,14},{14,12},{16,18},{18,... | collective-permute-start | bytes 3145736 | tf_op jit(solution)/shard_map/ppermute | solution.py:677
  67.9 43.0 %collective-permute-start.2 = (bf16[16,464,128]{2,1,0:T(8,128)(2,1)S(1)}, bf16[16,464,128]{2,1,0:T(8,128)(2,1)}, u32[]{:S(2)}, u32[]{:S(2)}) collective-permute-start(bf16[16,464,128]{2,1,0:T(8,128)(2,1)S(1)} %all-to-all-done.own_ref), channel_id=1, source_target_pairs={{0,1},{1,0},{2,3},{3,2},{4,5},{5,4},{6,7},{7,6},{8,9},{9,8},{10,11... | collective-permute-start | bytes 5701640 | tf_op jit(solution)/shard_map/ppermute | solution.py:680
  94.3 16.6 %collective-permute-start.1 = (bf16[2,128,2048]{2,1,0:T(8,128)(2,1)}, bf16[2,128,2048]{2,1,0:T(8,128)(2,1)}, u32[]{:S(2)}, u32[]{:S(2)}) collective-permute-start(bf16[2,128,2048]{2,1,0:T(8,128)(2,1)} %select_multiply_fusion.refs_10_.refs_17_), channel_id=1, source_target_pairs={{0,8},{2,6},{8,16},{10,2},{16,24},{18,10},{24,28},{26,18},{28,20},... | collective-permute-start | bytes 3145736 | tf_op jit(solution)/shard_map/ppermute | solution.py:674
  110.9 14.3 %collective-permute-start.3 = (bf16[2,128,2048]{2,1,0:T(8,128)(2,1)}, bf16[2,128,2048]{2,1,0:T(8,128)(2,1)}, u32[]{:S(2)}, u32[]{:S(2)}) collective-permute-start(bf16[2,128,2048]{2,1,0:T(8,128)(2,1)} %collective-permute-done.1.refs_11_.refs_18_), channel_id=1, source_target_pairs={{0,8},{2,6},{8,16},{10,2},{16,24},{18,10},{24,28},{26,18},{28,20},... | collective-permute-start | bytes 3145736 | tf_op jit(solution)/shard_map/ppermute | solution.py:674
  112.0 30.2 %collective-permute-start.5 = (bf16[16,320,128]{2,1,0:T(8,128)(2,1)}, bf16[16,320,128]{2,1,0:T(8,128)(2,1)S(1)}, u32[]{:S(2)}, u32[]{:S(2)}) collective-permute-start(bf16[16,320,128]{2,1,0:T(8,128)(2,1)} %copy-done.9), channel_id=1, source_target_pairs={{0,1},{1,0},{2,3},{3,2},{4,5},{5,4},{6,7},{7,6},{8,9},{9,8},{10,11... | collective-permute-start | bytes 3932168 | tf_op jit(solution)/shard_map/ppermute | solution.py:680
  125.1 14.2 %collective-permute-start.4 = (bf16[2,128,2048]{2,1,0:T(8,128)(2,1)}, bf16[2,128,2048]{2,1,0:T(8,128)(2,1)S(1)}, u32[]{:S(2)}, u32[]{:S(2)}) collective-permute-start(bf16[2,128,2048]{2,1,0:T(8,128)(2,1)} %collective-permute-done.3.refs_12_.refs_19_), channel_id=1, source_target_pairs={{0,8},{2,6},{8,16},{10,2},{16,24},{18,10},{24,28},{26,18},{28,20},... | collective-permute-start | bytes 3145736 | tf_op jit(solution)/shard_map/ppermute | solution.py:674
  142.2 8.3 %collective-permute-start.6 = (bf16[2,64,2048]{2,1,0:T(8,128)(2,1)S(1)}, bf16[2,64,2048]{2,1,0:T(8,128)(2,1)S(1)}, u32[]{:S(2)}, u32[]{:S(2)}) collective-permute-start(bf16[2,64,2048]{2,1,0:T(8,128)(2,1)S(1)} %constant_dynamic-slice_fusion.4), channel_id=1, source_target_pairs={{0,8},{2,6},{8,16},{10,2},{16,24},{18,10},{24,28},{26,18},{28,20},... | collective-permute-start | bytes 1572872 | tf_op jit(solution)/shard_map/ppermute | solution.py:674
  151.4 76.7 %all-to-all-start.2 = ((bf16[16,768,128]{2,1,0:T(8,128)(2,1)}), bf16[16,768,128]{2,1,0:T(8,128)(2,1)S(1)}, u32[]{:S(2)}, u32[]{:S(2)}) async-start(bf16[16,768,128]{2,1,0:T(8,128)(2,1)} %pack_both.1), calls=%async_computation.2 | async-start | bytes 6291456 | tf_op jit(solution)/shard_map/all_to_all | solution.py:731
  158.2 10.5 %collective-permute-start.10 = (bf16[2,128,2048]{2,1,0:T(8,128)(2,1)}, bf16[2,128,2048]{2,1,0:T(8,128)(2,1)}, u32[]{:S(2)}, u32[]{:S(2)}) collective-permute-start(bf16[2,128,2048]{2,1,0:T(8,128)(2,1)} %collective-permute-done.1.refs_11_.refs_18_), channel_id=1, source_target_pairs={{0,2},{2,0},{4,6},{6,4},{8,10},{10,8},{12,14},{14,12},{16,18},{18,... | collective-permute-start | bytes 3145736 | tf_op jit(solution)/shard_map/ppermute | solution.py:677
  158.6 10.1 %collective-permute-start.11 = (bf16[2,128,2048]{2,1,0:T(8,128)(2,1)}, bf16[2,128,2048]{2,1,0:T(8,128)(2,1)}, u32[]{:S(2)}, u32[]{:S(2)}) collective-permute-start(bf16[2,128,2048]{2,1,0:T(8,128)(2,1)} %collective-permute-done.3.refs_12_.refs_19_), channel_id=1, source_target_pairs={{0,2},{2,0},{4,6},{6,4},{8,10},{10,8},{12,14},{14,12},{16,18},{18,... | collective-permute-start | bytes 3145736 | tf_op jit(solution)/shard_map/ppermute | solution.py:677
  158.8 10.0 %collective-permute-start.12 = (bf16[2,128,2048]{2,1,0:T(8,128)(2,1)}, bf16[2,128,2048]{2,1,0:T(8,128)(2,1)}, u32[]{:S(2)}, u32[]{:S(2)}) collective-permute-start(bf16[2,128,2048]{2,1,0:T(8,128)(2,1)} %copy-done.25), channel_id=1, source_target_pairs={{0,2},{2,0},{4,6},{6,4},{8,10},{10,8},{12,14},{14,12},{16,18},{18,... | collective-permute-start | bytes 3145736 | tf_op jit(solution)/shard_map/ppermute | solution.py:677
  159.2 2.7 collective-permute-start.9
  162.8 5.9 collective-permute-start.13
  198.1 35.6 %collective-permute-start.14 = (bf16[448,2048]{1,0:T(8,128)(2,1)}, bf16[448,2048]{1,0:T(8,128)(2,1)}, u32[]{:S(2)}, u32[]{:S(2)}) collective-permute-start(bf16[448,2048]{1,0:T(8,128)(2,1)} %get-tuple-element.89), channel_id=1, source_target_pairs={{0,2},{2,0},{4,6},{6,4},{8,10},{10,8},{12,14},{14,12},{16,18},{18,... | collective-permute-start | bytes 5505032 | tf_op jit(solution)/shard_map/ppermute | solution.py:677
  230.8 5.7 collective-permute-start.16
  232.5 35.8 %collective-permute-start.7 = (bf16[8,768,128]{2,1,0:T(8,128)(2,1)S(1)}, bf16[8,768,128]{2,1,0:T(8,128)(2,1)S(1)}, u32[]{:S(2)}, u32[]{:S(2)}) collective-permute-start(bf16[8,768,128]{2,1,0:T(8,128)(2,1)S(1)} %get-tuple-element.204), channel_id=1, source_target_pairs={{0,1},{1,0},{2,3},{3,2},{4,5},{5,4},{6,7},{7,6},{8,9},{9,8},{10,11... | collective-permute-start | bytes 4718600 | tf_op jit(solution)/shard_map/ppermute | solution.py:680
  237.9 8.4 %collective-permute-start.17 = (bf16[1,128,2048]{2,1,0:T(8,128)(2,1)S(1)}, bf16[1,128,2048]{2,1,0:T(8,128)(2,1)S(1)}, u32[]{:S(2)}, u32[]{:S(2)}) collective-permute-start(bf16[1,128,2048]{2,1,0:T(8,128)(2,1)S(1)} %fusion.7), channel_id=1, source_target_pairs={{0,8},{2,6},{8,16},{10,2},{16,24},{18,10},{24,28},{26,18},{28,20},... | collective-permute-start | bytes 1572872 | tf_op jit(solution)/shard_map/ppermute | solution.py:674
  247.5 8.4 %collective-permute-start.18 = (bf16[1,128,2048]{2,1,0:T(8,128)(2,1)S(1)}, bf16[1,128,2048]{2,1,0:T(8,128)(2,1)S(1)}, u32[]{:S(2)}, u32[]{:S(2)}) collective-permute-start(bf16[1,128,2048]{2,1,0:T(8,128)(2,1)S(1)} %fusion.6), channel_id=1, source_target_pairs={{0,8},{2,6},{8,16},{10,2},{16,24},{18,10},{24,28},{26,18},{28,20},... | collective-permute-start | bytes 1572872 | tf_op jit(solution)/shard_map/ppermute | solution.py:674
  270.7 8.6 %collective-permute-start.19 = (bf16[1,128,2048]{2,1,0:T(8,128)(2,1)}, bf16[1,128,2048]{2,1,0:T(8,128)(2,1)S(1)}, u32[]{:S(2)}, u32[]{:S(2)}) collective-permute-start(bf16[1,128,2048]{2,1,0:T(8,128)(2,1)} %fusion.5), channel_id=1, source_target_pairs={{0,8},{2,6},{8,16},{10,2},{16,24},{18,10},{24,28},{26,18},{28,20},... | collective-permute-start | bytes 1572872 | tf_op jit(solution)/shard_map/ppermute | solution.py:674
  271.8 36.3 %collective-permute-start.8 = (bf16[8,768,128]{2,1,0:T(8,128)(2,1)}, bf16[8,768,128]{2,1,0:T(8,128)(2,1)}, u32[]{:S(2)}, u32[]{:S(2)}) collective-permute-start(bf16[8,768,128]{2,1,0:T(8,128)(2,1)} %get-tuple-element.203), channel_id=1, source_target_pairs={{0,1},{1,0},{2,3},{3,2},{4,5},{5,4},{6,7},{7,6},{8,9},{9,8},{10,11... | collective-permute-start | bytes 4718600 | tf_op jit(solution)/shard_map/ppermute | solution.py:680
  280.1 3.1 collective-permute-start.20
  289.3 18.7 %collective-permute-start.22 = (bf16[128,2048]{1,0:T(8,128)(2,1)S(1)}, bf16[128,2048]{1,0:T(8,128)(2,1)S(1)}, u32[]{:S(2)}, u32[]{:S(2)}) collective-permute-start(bf16[128,2048]{1,0:T(8,128)(2,1)S(1)} %maximum_select_fusion.2.refs_8_), channel_id=1, source_target_pairs={{0,8},{2,6},{8,16},{10,2},{16,24},{18,10},{24,28},{26,18},{28,20},... | collective-permute-start | bytes 1572872 | tf_op jit(solution)/shard_map/ppermute | solution.py:674
  308.1 8.3 %collective-permute-start.23 = (bf16[128,2048]{1,0:T(8,128)(2,1)S(1)}, bf16[128,2048]{1,0:T(8,128)(2,1)S(1)}, u32[]{:S(2)}, u32[]{:S(2)}) collective-permute-start(bf16[128,2048]{1,0:T(8,128)(2,1)S(1)} %collective-permute-done.22.refs_9_), channel_id=1, source_target_pairs={{0,8},{2,6},{8,16},{10,2},{16,24},{18,10},{24,28},{26,18},{28,20},... | collective-permute-start | bytes 1572872 | tf_op jit(solution)/shard_map/ppermute | solution.py:674
  316.4 8.3 %collective-permute-start.24 = (bf16[128,2048]{1,0:T(8,128)(2,1)S(1)}, bf16[128,2048]{1,0:T(8,128)(2,1)S(1)}, u32[]{:S(2)}, u32[]{:S(2)}) collective-permute-start(bf16[128,2048]{1,0:T(8,128)(2,1)S(1)} %collective-permute-done.23.refs_10_), channel_id=1, source_target_pairs={{0,8},{2,6},{8,16},{10,2},{16,24},{18,10},{24,28},{26,18},{28,20},... | collective-permute-start | bytes 1572872 | tf_op jit(solution)/shard_map/ppermute | solution.py:674
  316.4 23.7 %collective-permute-start.25 = (bf16[128,2048]{1,0:T(8,128)(2,1)S(1)}, bf16[128,2048]{1,0:T(8,128)(2,1)S(1)}, u32[]{:S(2)}, u32[]{:S(2)}) collective-permute-start(bf16[128,2048]{1,0:T(8,128)(2,1)S(1)} %collective-permute-done.22.refs_9_), channel_id=1, source_target_pairs={{0,2},{2,0},{4,6},{6,4},{8,10},{10,8},{12,14},{14,12},{16,18},{18,... | collective-permute-start | bytes 1572872 | tf_op jit(solution)/shard_map/ppermute | solution.py:677
  318.1 22.0 %collective-permute-start.26 = (bf16[128,2048]{1,0:T(8,128)(2,1)S(1)}, bf16[128,2048]{1,0:T(8,128)(2,1)S(1)}, u32[]{:S(2)}, u32[]{:S(2)}) collective-permute-start(bf16[128,2048]{1,0:T(8,128)(2,1)S(1)} %collective-permute-done.23.refs_10_), channel_id=1, source_target_pairs={{0,2},{2,0},{4,6},{6,4},{8,10},{10,8},{12,14},{14,12},{16,18},{18,... | collective-permute-start | bytes 1572872 | tf_op jit(solution)/shard_map/ppermute | solution.py:677
  324.8 5.3 collective-permute-start.28
  324.8 15.3 %collective-permute-start.27 = (bf16[128,2048]{1,0:T(8,128)(2,1)S(1)}, bf16[128,2048]{1,0:T(8,128)(2,1)}, u32[]{:S(2)}, u32[]{:S(2)}) collective-permute-start(bf16[128,2048]{1,0:T(8,128)(2,1)S(1)} %collective-permute-done.24.refs_11_), channel_id=1, source_target_pairs={{0,2},{2,0},{4,6},{6,4},{8,10},{10,8},{12,14},{14,12},{16,18},{18,... | collective-permute-start | bytes 1572872 | tf_op jit(solution)/shard_map/ppermute | solution.py:677
  330.0 10.1 %collective-permute-start.29 = (bf16[64,2048]{1,0:T(8,128)(2,1)S(1)}, bf16[64,2048]{1,0:T(8,128)(2,1)}, u32[]{:S(2)}, u32[]{:S(2)}) collective-permute-start(bf16[64,2048]{1,0:T(8,128)(2,1)S(1)} %collective-permute-done.28.refs_15_), channel_id=1, source_target_pairs={{0,2},{2,0},{4,6},{6,4},{8,10},{10,8},{12,14},{14,12},{16,18},{18,... | collective-permute-start | bytes 786440 | tf_op jit(solution)/shard_map/ppermute | solution.py:677
  377.2 8.9 %collective-permute-start.34 = (bf16[448,2048]{1,0:T(8,128)(2,1)}, bf16[448,2048]{1,0:T(8,128)(2,1)S(1)}, u32[]{:S(2)}, u32[]{:S(2)}) collective-permute-start(bf16[448,2048]{1,0:T(8,128)(2,1)} %get-tuple-element.100), channel_id=1, source_target_pairs={{0,2},{2,0},{4,6},{6,4},{8,10},{10,8},{12,14},{14,12},{16,18},{18,... | collective-permute-start | bytes 5505032 | tf_op jit(solution)/shard_map/ppermute | solution.py:677
  377.4 4.3 collective-permute-start.31
  377.8 9.9 %collective-permute-start.30 = (bf16[448,2048]{1,0:T(8,128)(2,1)}, bf16[448,2048]{1,0:T(8,128)(2,1)S(1)}, u32[]{:S(2)}, u32[]{:S(2)}) collective-permute-start(bf16[448,2048]{1,0:T(8,128)(2,1)} %get-tuple-element.96), channel_id=1, source_target_pairs={{0,2},{2,0},{4,6},{6,4},{8,10},{10,8},{12,14},{14,12},{16,18},{18,... | collective-permute-start | bytes 5505032 | tf_op jit(solution)/shard_map/ppermute | solution.py:677
  377.9 6.7 collective-permute-start.32
  385.7 8.4 %collective-permute-start.33 = (bf16[2,64,2048]{2,1,0:T(8,128)(2,1)S(1)}, bf16[2,64,2048]{2,1,0:T(8,128)(2,1)S(1)}, u32[]{:S(2)}, u32[]{:S(2)}) collective-permute-start(bf16[2,64,2048]{2,1,0:T(8,128)(2,1)S(1)} %pad_maximum_fusion.2), channel_id=1, source_target_pairs={{0,8},{2,6},{8,16},{10,2},{16,24},{18,10},{24,28},{26,18},{28,20},... | collective-permute-start | bytes 1572872 | tf_op jit(solution)/shard_map/ppermute | solution.py:674
  395.5 14.3 %collective-permute-start.35 = (bf16[2,128,2048]{2,1,0:T(8,128)(2,1)}, bf16[2,128,2048]{2,1,0:T(8,128)(2,1)}, u32[]{:S(2)}, u32[]{:S(2)}) collective-permute-start(bf16[2,128,2048]{2,1,0:T(8,128)(2,1)} %fusion), channel_id=1, source_target_pairs={{0,8},{2,6},{8,16},{10,2},{16,24},{18,10},{24,28},{26,18},{28,20},... | collective-permute-start | bytes 3145736 | tf_op jit(solution)/shard_map/ppermute | solution.py:674
  412.4 14.3 %collective-permute-start.36 = (bf16[2,128,2048]{2,1,0:T(8,128)(2,1)}, bf16[2,128,2048]{2,1,0:T(8,128)(2,1)S(1)}, u32[]{:S(2)}, u32[]{:S(2)}) collective-permute-start(bf16[2,128,2048]{2,1,0:T(8,128)(2,1)} %fusion.1), channel_id=1, source_target_pairs={{0,8},{2,6},{8,16},{10,2},{16,24},{18,10},{24,28},{26,18},{28,20},... | collective-permute-start | bytes 3145736 | tf_op jit(solution)/shard_map/ppermute | solution.py:674
  427.3 14.1 %collective-permute-start.37 = (bf16[2,128,2048]{2,1,0:T(8,128)(2,1)S(1)}, bf16[2,128,2048]{2,1,0:T(8,128)(2,1)S(1)}, u32[]{:S(2)}, u32[]{:S(2)}) collective-permute-start(bf16[2,128,2048]{2,1,0:T(8,128)(2,1)S(1)} %fusion.2), channel_id=1, source_target_pairs={{0,8},{2,6},{8,16},{10,2},{16,24},{18,10},{24,28},{26,18},{28,20},... | collective-permute-start | bytes 3145736 | tf_op jit(solution)/shard_map/ppermute | solution.py:674
  427.8 28.2 %collective-permute-start.42 = (bf16[16,320,128]{2,1,0:T(8,128)(2,1)}, bf16[16,320,128]{2,1,0:T(8,128)(2,1)}, u32[]{:S(2)}, u32[]{:S(2)}) collective-permute-start(bf16[16,320,128]{2,1,0:T(8,128)(2,1)} %get-tuple-element.115), channel_id=1, source_target_pairs={{0,1},{1,0},{2,3},{3,2},{4,5},{5,4},{6,7},{7,6},{8,9},{9,8},{10,11... | collective-permute-start | bytes 3932168 | tf_op jit(solution)/shard_map/ppermute | solution.py:680
  441.5 5.1 collective-permute-start.38
  445.0 51.6 %collective-permute-start.45 = (bf16[16,464,128]{2,1,0:T(8,128)(2,1)}, bf16[16,464,128]{2,1,0:T(8,128)(2,1)S(1)}, u32[]{:S(2)}, u32[]{:S(2)}) collective-permute-start(bf16[16,464,128]{2,1,0:T(8,128)(2,1)} %get-tuple-element.117), channel_id=1, source_target_pairs={{0,1},{1,0},{2,3},{3,2},{4,5},{5,4},{6,7},{7,6},{8,9},{9,8},{10,11... | collective-permute-start | bytes 5701640 | tf_op jit(solution)/shard_map/ppermute | solution.py:680
  456.0 9.3 %collective-permute-start.43 = (bf16[128,2048]{1,0:T(8,128)(2,1)S(1)}, bf16[128,2048]{1,0:T(8,128)(2,1)S(1)}, u32[]{:S(2)}, u32[]{:S(2)}) collective-permute-start(bf16[128,2048]{1,0:T(8,128)(2,1)S(1)} %maximum_select_fusion.4.rest_0_.refs_10_), channel_id=1, source_target_pairs={{0,8},{2,6},{8,16},{10,2},{16,24},{18,10},{24,28},{26,18},{28,20},... | collective-permute-start | bytes 1572872 | tf_op jit(solution)/shard_map/ppermute | solution.py:674
  465.3 31.3 %collective-permute-start.44 = (bf16[128,2048]{1,0:T(8,128)(2,1)S(1)}, bf16[128,2048]{1,0:T(8,128)(2,1)S(1)}, u32[]{:S(2)}, u32[]{:S(2)}) collective-permute-start(bf16[128,2048]{1,0:T(8,128)(2,1)S(1)} %collective-permute-done.43.rest_1_.refs_11_), channel_id=1, source_target_pairs={{0,8},{2,6},{8,16},{10,2},{16,24},{18,10},{24,28},{26,18},{28,20},... | collective-permute-start | bytes 1572872 | tf_op jit(solution)/shard_map/ppermute | solution.py:674
  496.6 9.4 %collective-permute-start.46 = (bf16[128,2048]{1,0:T(8,128)(2,1)S(1)}, bf16[128,2048]{1,0:T(8,128)(2,1)S(1)}, u32[]{:S(2)}, u32[]{:S(2)}) collective-permute-start(bf16[128,2048]{1,0:T(8,128)(2,1)S(1)} %collective-permute-done.44.rest_2_.refs_12_), channel_id=1, source_target_pairs={{0,8},{2,6},{8,16},{10,2},{16,24},{18,10},{24,28},{26,18},{28,20},... | collective-permute-start | bytes 1572872 | tf_op jit(solution)/shard_map/ppermute | solution.py:674
  506.8 5.3 collective-permute-start.50
  514.5 80.8 %all-to-all-start.3 = ((bf16[16,784,128]{2,1,0:T(8,128)(2,1)}), bf16[16,784,128]{2,1,0:T(8,128)(2,1)S(1)}, u32[]{:S(2)}, u32[]{:S(2)}) async-start(bf16[16,784,128]{2,1,0:T(8,128)(2,1)} %pad_maximum_fusion), calls=%async_computation.3 | async-start | bytes 6422528 | tf_op jit(solution)/shard_map/all_to_all | solution.py:731
  524.1 2.4 collective-permute-start.47
  524.5 2.8 collective-permute-start.48
  524.6 3.7 collective-permute-start.49
  525.0 3.3 collective-permute-start.51
  537.9 38.4 %collective-permute-start.56 = (bf16[16,320,128]{2,1,0:T(8,128)(2,1)}, bf16[16,320,128]{2,1,0:T(8,128)(2,1)}, u32[]{:S(2)}, u32[]{:S(2)}) collective-permute-start(bf16[16,320,128]{2,1,0:T(8,128)(2,1)} %get-tuple-element.130), channel_id=1, source_target_pairs={{0,1},{1,0},{2,3},{3,2},{4,5},{5,4},{6,7},{7,6},{8,9},{9,8},{10,11... | collective-permute-start | bytes 3932168 | tf_op jit(solution)/shard_map/ppermute | solution.py:680
  565.6 38.6 %collective-permute-start.52 = (bf16[448,2048]{1,0:T(8,128)(2,1)}, bf16[448,2048]{1,0:T(8,128)(2,1)}, u32[]{:S(2)}, u32[]{:S(2)}) collective-permute-start(bf16[448,2048]{1,0:T(8,128)(2,1)} %get-tuple-element.123), channel_id=1, source_target_pairs={{0,2},{2,0},{4,6},{6,4},{8,10},{10,8},{12,14},{14,12},{16,18},{18,... | collective-permute-start | bytes 5505032 | tf_op jit(solution)/shard_map/ppermute | solution.py:677
  595.4 50.7 %all-to-all-start.4 = ((bf16[16,320,128]{2,1,0:T(8,128)(2,1)}), bf16[16,320,128]{2,1,0:T(8,128)(2,1)}, u32[]{:S(2)}, u32[]{:S(2)}) async-start(bf16[16,320,128]{2,1,0:T(8,128)(2,1)} %add_convert_fusion.2), calls=%async_computation.4 | async-start | bytes 2621440 | tf_op jit(solution)/shard_map/all_to_all | solution.py:731
  600.6 49.5 %collective-permute-start.62 = (bf16[16,464,128]{2,1,0:T(8,128)(2,1)}, bf16[16,464,128]{2,1,0:T(8,128)(2,1)}, u32[]{:S(2)}, u32[]{:S(2)}) collective-permute-start(bf16[16,464,128]{2,1,0:T(8,128)(2,1)} %get-tuple-element.137), channel_id=1, source_target_pairs={{0,1},{1,0},{2,3},{3,2},{4,5},{5,4},{6,7},{7,6},{8,9},{9,8},{10,11... | collective-permute-start | bytes 5701640 | tf_op jit(solution)/shard_map/ppermute | solution.py:680
  602.9 28.9 %collective-permute-start.54 = (bf16[1,64,2048]{2,1,0:T(8,128)(2,1)S(1)}, bf16[1,64,2048]{2,1,0:T(8,128)(2,1)S(1)}, u32[]{:S(2)}, u32[]{:S(2)}) collective-permute-start(bf16[1,64,2048]{2,1,0:T(8,128)(2,1)S(1)} %fusion.16), channel_id=1, source_target_pairs={{0,8},{2,6},{8,16},{10,2},{16,24},{18,10},{24,28},{26,18},{28,20},... | collective-permute-start | bytes 786440 | tf_op jit(solution)/shard_map/ppermute | solution.py:674
  634.1 9.8 %collective-permute-start.55 = (bf16[1,128,2048]{2,1,0:T(8,128)(2,1)}, bf16[1,128,2048]{2,1,0:T(8,128)(2,1)}, u32[]{:S(2)}, u32[]{:S(2)}) collective-permute-start(bf16[1,128,2048]{2,1,0:T(8,128)(2,1)} %fusion.8), channel_id=1, source_target_pairs={{0,8},{2,6},{8,16},{10,2},{16,24},{18,10},{24,28},{26,18},{28,20},... | collective-permute-start | bytes 1572872 | tf_op jit(solution)/shard_map/ppermute | solution.py:674
  642.7 16.9 %collective-permute-start.40 = (bf16[128,2048]{1,0:T(8,128)(2,1)}, bf16[128,2048]{1,0:T(8,128)(2,1)}, u32[]{:S(2)}, u32[]{:S(2)}) collective-permute-start(bf16[128,2048]{1,0:T(8,128)(2,1)} %maximum_select_fusion.3), channel_id=1, source_target_pairs={{0,1},{1,0},{2,3},{3,2},{4,5},{5,4},{6,7},{7,6},{8,9},{9,8},{10,11... | collective-permute-start | bytes 1572872 | tf_op jit(solution)/shard_map/ppermute | solution.py:680
  648.7 12.8 %collective-permute-start.57 = (bf16[1,128,2048]{2,1,0:T(8,128)(2,1)}, bf16[1,128,2048]{2,1,0:T(8,128)(2,1)}, u32[]{:S(2)}, u32[]{:S(2)}) collective-permute-start(bf16[1,128,2048]{2,1,0:T(8,128)(2,1)} %fusion.4), channel_id=1, source_target_pairs={{0,8},{2,6},{8,16},{10,2},{16,24},{18,10},{24,28},{26,18},{28,20},... | collective-permute-start | bytes 1572872 | tf_op jit(solution)/shard_map/ppermute | solution.py:674
  653.5 90.0 %all-to-all-start.5 = ((bf16[16,464,128]{2,1,0:T(8,128)(2,1)}), bf16[16,464,128]{2,1,0:T(8,128)(2,1)}, u32[]{:S(2)}, u32[]{:S(2)}) async-start(bf16[16,464,128]{2,1,0:T(8,128)(2,1)} %add_convert_fusion), calls=%async_computation.5 | async-start | bytes 3801088 | tf_op jit(solution)/shard_map/all_to_all | solution.py:731
  664.1 42.7 %collective-permute-start.58 = (bf16[1,128,2048]{2,1,0:T(8,128)(2,1)S(1)}, bf16[1,128,2048]{2,1,0:T(8,128)(2,1)S(1)}, u32[]{:S(2)}, u32[]{:S(2)}) collective-permute-start(bf16[1,128,2048]{2,1,0:T(8,128)(2,1)S(1)} %fusion.3), channel_id=1, source_target_pairs={{0,8},{2,6},{8,16},{10,2},{16,24},{18,10},{24,28},{26,18},{28,20},... | collective-permute-start | bytes 1572872 | tf_op jit(solution)/shard_map/ppermute | solution.py:674
  707.6 3.6 collective-permute-start.59
  718.5 22.9 %collective-permute-start.61 = (bf16[128,2048]{1,0:T(8,128)(2,1)}, bf16[128,2048]{1,0:T(8,128)(2,1)}, u32[]{:S(2)}, u32[]{:S(2)}) collective-permute-start(bf16[128,2048]{1,0:T(8,128)(2,1)} %maximum_select_fusion.6), channel_id=1, source_target_pairs={{0,1},{1,0},{2,3},{3,2},{4,5},{5,4},{6,7},{7,6},{8,9},{9,8},{10,11... | collective-permute-start | bytes 1572872 | tf_op jit(solution)/shard_map/ppermute | solution.py:680
  719.9 12.1 %collective-permute-start.63 = (f32[2,448]{1,0:T(2,128)S(1)}, f32[2,448]{1,0:T(2,128)S(1)}, u32[]{:S(2)}, u32[]{:S(2)}) collective-permute-start(f32[2,448]{1,0:T(2,128)S(1)} %pad_maximum_fusion.4), channel_id=1, source_target_pairs={{0,1},{1,0},{2,3},{3,2},{4,5},{5,4},{6,7},{7,6},{8,9},{9,8},{10,11... | collective-permute-start | bytes 10760 | tf_op jit(solution)/shard_map/ppermute | solution.py:680
  (55 other events, 955.8 us)

commit v9 on v6

--- a/solution.py
+++ b/solution.py
@@ -518,7 +518,8 @@
 
 
 def spread_gradients(up_ref, down_ref, *rest):
-    qkv_ref, out_w_ref, fc1_ref, fc2_ref = rest[-4:]
+    qkv_ref, out_w_ref, fc1_ref, fc2_ref, mark_ref = rest[-5:]
+    mark_ref[...] = jnp.zeros_like(mark_ref)
     for p in range(3):
         rows = slice(p * HEAD_DIM, (p + 1) * HEAD_DIM)
         both = jnp.concatenate([up_ref[0, rows].astype(f32), up_ref[1, rows].astype(f32)], axis=0)
@@ -539,6 +540,7 @@
         jax.ShapeDtypeStruct((LAYERS, GROUP * HEAD_DIM, 128), f32),
         jax.ShapeDtypeStruct((LAYERS, 128, GROUP * 256), f32),
         jax.ShapeDtypeStruct((LAYERS, GROUP * 256, 128), f32),
+        jax.ShapeDtypeStruct((8, 128), f32),
     ]
     return pl.pallas_call(
         spread_gradients,
@@ -553,6 +555,7 @@
             pl.BlockSpec((1, 128, 128), lambda i: (layer, i, 0)),
             pl.BlockSpec((1, 128, 512), lambda i: (layer, 0, i)),
             pl.BlockSpec((1, 512, 128), lambda i: (layer, i, 0)),
+            pl.BlockSpec((8, 128), lambda i: (0, 0)),
         ],
         out_shape=shapes,
         input_output_aliases={2 + n: n for n in range(len(filled))},
@@ -582,7 +585,8 @@
     normed_ref[...] = (centred * inverse * gain_ref[...] + shift_ref[...]).astype(bf16)
 
 
-def backward_end(core_ref, keep_ref, took_ref, moving_ref, got_ref, state_ref, grad_ref, gain_ref, grad_out, low_ref):
+def backward_end(core_ref, keep_ref, took_ref, moving_ref, got_ref, state_ref, grad_ref, gain_ref, *rest):
+    grad_out, low_ref = rest[-2:]
     grad_normed = ring_total(core_ref, keep_ref, took_ref, moving_ref, got_ref)
     centred, inverse = centred_rows(state_ref[...].astype(f32))
     xhat = centred * inverse
@@ -711,14 +715,13 @@
         keep = [x for _, _, x in sets]
         far = [k[side * block : side * block + half].astype(f32) + t.astype(f32) for k, t in zip(keep, took_far)]
         moving = along(jnp.stack(far).astype(bf16))
-        moving = jnp.where(mine_rows, jnp.concatenate([moving, moving], 1), 0).astype(f32)
         for step in reversed(range(side)):
             here = slice(step * block, (step + 1) * block)
-            moving = after(moving, *needed.get(step, ()))
             added = [k[here].astype(f32) + t[here].astype(f32) for k, t in zip(keep, took)]
-            moving = along((moving + jnp.stack(added)).astype(bf16))
-            if step:
-                moving = moving.astype(f32)
+            arrived = after(moving, *needed.get(step, ())).astype(f32)
+            if step == side - 1:
+                arrived = jnp.where(mine_rows, jnp.concatenate([arrived, arrived], 1), 0)
+            moving = along((arrived + jnp.stack(added)).astype(bf16))
         got = across(my_half(moving, off, 1))
         return [(k, t, moving, got, n) for n, (k, t) in enumerate(zip(keep, took))]
 
@@ -860,12 +863,12 @@
     next_state, normed_own = call_end(
         partial(forward_end, False),
         core_word,
-        ring_sum((after(parts[0], *slabs), parts[1], parts[2]), needed={})[0],
+        ring_sum((after(parts[0], *slabs), parts[1], parts[2]), needed={0: others[:1]})[0],
         [state, added_bias[0], gains[1], shifts[1]],
         [jax.ShapeDtypeStruct(rows_shape, f32), jax.ShapeDtypeStruct(rows_shape, bf16)],
         "forward_end",
     )
-    normed_chunks = gather_rows(in_order(normed_own, across(normed_own)), {0: others[:1], 2: others[1:]})
+    normed_chunks = gather_rows(in_order(normed_own, across(normed_own)), {1: others[1:]})
 
     def handed_back(own_rows):
         filled = in_order(own_rows, across(own_rows))
@@ -890,12 +893,12 @@
     def up_gradients(slim_rows, normed_rows, sums):
         return call_gradients(core_word, slim_rows, [normed_rows], up_own, up_other, [sums], "up_gradients")
 
-    def backward_finish(ring_end, state, grad_state, layer):
+    def backward_finish(ring_end, state, grad_state, layer, *needed):
         return call_end(
             backward_end,
             core_word,
             ring_end,
-            [state, grad_state, gains[layer]],
+            [state, grad_state, gains[layer], *needed],
             [jax.ShapeDtypeStruct(rows_shape, f32), jax.ShapeDtypeStruct(rows_shape, bf16)],
             "backward_end",
         )
@@ -932,24 +935,28 @@
     up_sent = over(up_pair[1])
     (grad_end,) = ring_sum((after(parts[0], up_pair[0]), parts[1], parts[2]), needed={1: (down_first,)})
     up_first = summed(up_pair[0], up_sent, down_first)
-    _, grad_low = backward_finish(grad_end, state, grad_state, 0)
-    grad_hidden = handed_back(grad_low).astype(f32)
-
-    ends = jnp.stack([jnp.sum(x[:, UP_ROWS : UP_ROWS + 3].astype(f32), axis=0) for x in (up_first, up_last)])
-    shift_grads = ends[:, 0]
-    gain_grads = (ends[:, 1] - norm_bias.astype(f32) * ends[:, 0]) / norm_gain.astype(f32)
-    after_grads = ends[:, 2] / GROUP
     sums = jnp.concatenate([bias_first, bias_last], axis=0)
     sums_qkv = sums[:, : 3 * WIDE].reshape(LAYERS, 3, 2, HEAD_DIM)
     sums_up = sums[:, 3 * WIDE :].reshape(LAYERS, 2, hidden)
     bias_own, bias_other = (
         jnp.concatenate([sums_qkv[:, :, n].reshape(LAYERS, -1), sums_up[:, n]], axis=1) for n in range(2)
     )
-    bias_sums = bias_own + over(bias_other)
+    bias_sent = over(bias_other)
+    needed = [bias_sent]
+    if groups == 1:
+        *filled, mark = call_spread(up_last, down_last, 1, [])
+        needed.append(mark)
+    _, grad_low = backward_finish(grad_end, state, grad_state, 0, *needed)
+    grad_hidden = handed_back(grad_low).astype(f32)
+
+    ends = jnp.stack([jnp.sum(x[:, UP_ROWS : UP_ROWS + 3].astype(f32), axis=0) for x in (up_first, up_last)])
+    shift_grads = ends[:, 0]
+    gain_grads = (ends[:, 1] - norm_bias.astype(f32) * ends[:, 0]) / norm_gain.astype(f32)
+    after_grads = ends[:, 2] / GROUP
+    bias_sums = bias_own + bias_sent
     bias_qkv, bias_up = bias_sums[:, : 3 * HEAD_DIM].reshape(LAYERS, 3, HEAD_DIM), bias_sums[:, 3 * HEAD_DIM :]
     if groups == 1:
-        filled = call_spread(up_last, down_last, 1, [])
-        grad_qkv, grad_out, grad_up, grad_down = call_spread(up_first, down_first, 0, filled)
+        grad_qkv, grad_out, grad_up, grad_down, _ = call_spread(up_first, down_first, 0, filled)
         grad_qkv = grad_qkv.transpose(0, 2, 1, 3)
     else:
         bias_qkv = lax.all_gather(lax.psum(bias_qkv, "dp", axis_index_groups=outer), "dp", axis=2, axis_index_groups=inner, tiled=True)

time: 752 us -> 757 us (level)
  waiting for transfers between devices: 361 us -> 372 us
    ppermute x12, waiting for transfers between devices: 66.1 us -> 82 us  [over(): return lax.ppermute(x, 'tensor', [(0, 1), (1, 0)])]
  transfers between devices with their start and end apart: 71 -> 71, of which waited for: 44 -> 43; matrix products, arithmetic and copies ran while one was open for 8% -> 8% of each run, Pallas kernels for 18% -> 18%
where the time goes in v9:
time: 757 us; the launch traced here: 746 us
  waiting for transfers between devices  372 us (49%)
  Pallas kernels  182 us (24%)
  starting transfers between devices  111 us (15%)
  other arithmetic  55.3 us (7%)
  local copies, waits for them, and re-layouts  22.7 us (3%)
    ppermute x24, waiting for transfers between devices, along(): return lax.ppermute(x, 'dp', ring_pairs)  189 us
    pallas_call x3, Pallas kernels, call_pass(): pl.pallas_call(partial(layer_pass, mode), in_specs=[SMEM_SPEC] + [VMEM_SP...  91.8 us
    all_to_all x7, waiting for transfers between devices, spread(): return lax.all_to_all(x, 'dp', 0, 0, axis_index_groups=inner, tiled=True)  87.4 us
    ppermute x12, waiting for transfers between devices, over(): return lax.ppermute(x, 'tensor', [(0, 1), (1, 0)])  82 us
    all_to_all x7, starting transfers between devices, spread(): return lax.all_to_all(x, 'dp', 0, 0, axis_index_groups=inner, tiled=True)  52.6 us
    pallas_call x4, Pallas kernels, call_gradients(): pl.pallas_call(partial(gradient_slabs, own_rows, other_rows, with_sums, l...  38.1 us
    ppermute x28, starting transfers between devices, across(): return lax.ppermute(x, 'dp', core_pairs)  22.5 us
    ppermute x24, starting transfers between devices, along(): return lax.ppermute(x, 'dp', ring_pairs)  22.3 us
  transfers between devices with their start and end apart: 71, of which 43 were waited for; matrix products, arithmetic and copies ran while one was open for 8% of the time, Pallas kernels for 18%

profile of v9, /device:TPU:13, one launch (start us, length us, event | category | flops | bytes accessed | tf_op | source)
XLA Modules:
  0.0 745.6 jit_solution(334493455203413110)
XLA Ops:
  4.8 4.0 pack_first.1
  8.8 6.5 all-to-all-start
  15.3 3.5 pack_down.1
  18.9 39.7 %all-to-all-done.own_ref = bf16[16,464,128]{2,1,0:T(8,128)(2,1)S(1)} async-done(((bf16[16,464,128]{2,1,0:T(8,128)(2,1)}), bf16[16,464,128]{2,1,0:T(8,128)(2,1)S(1)}, u32[]{:S(2)}, u32[]{:S(2)}) %all-to-all-start) | async-done | bytes 1900576 | tf_op jit(solution)/shard_map/all_to_all | solution.py:729
  58.5 4.8 all-to-all-start.1
  69.3 4.4 pack_both.1
  73.8 2.7 select_multiply_fusion.refs_10_.refs_17_
  76.4 17.9 %all-to-all-done.1.own_ref = bf16[16,320,128]{2,1,0:T(8,128)(2,1)S(1)} async-done(((bf16[16,320,128]{2,1,0:T(8,128)(2,1)}), bf16[16,320,128]{2,1,0:T(8,128)(2,1)S(1)}, u32[]{:S(2)}, u32[]{:S(2)}) %all-to-all-start.1) | async-done | bytes 1310752 | tf_op jit(solution)/shard_map/all_to_all | solution.py:729
  98.1 2.7 concatenate.76.refs_3_
  100.8 10.1 %collective-permute-done.2.other_ref = bf16[16,464,128]{2,1,0:T(8,128)(2,1)} collective-permute-done((bf16[16,464,128]{2,1,0:T(8,128)(2,1)S(1)}, bf16[16,464,128]{2,1,0:T(8,128)(2,1)}, u32[]{:S(2)}, u32[]{:S(2)}) %collective-permute-start.2) | collective-permute-done | bytes 1900576 | tf_op jit(solution)/shard_map/ppermute | solution.py:679
  118.0 7.1 collective-permute-done.3.refs_12_.refs_19_
  126.3 4.8 join_up.1.refs_1_
  131.1 8.2 %collective-permute-done.4.refs_13_.refs_20_ = bf16[2,128,2048]{2,1,0:T(8,128)(2,1)S(1)} collective-permute-done((bf16[2,128,2048]{2,1,0:T(8,128)(2,1)}, bf16[2,128,2048]{2,1,0:T(8,128)(2,1)S(1)}, u32[]{:S(2)}, u32[]{:S(2)}) %collective-permute-start.4) | collective-permute-done | bytes 1048608 | tf_op jit(solution)/shard_map/ppermute | solution.py:673
  139.3 2.9 collective-permute-done.5.other_ref
  143.4 7.1 collective-permute-done.6.refs_17_.refs_24_
  151.4 6.8 all-to-all-start.2
  164.6 4.2 join_down.1.refs_2_
  168.8 29.3 %pass_first.1 = (bf16[1024,2048]{1,0:T(8,128)(2,1)}, bf16[1024,384]{1,0:T(8,128)(2,1)}, f32[1024,512]{1,0:T(8,128)}, bf16[1024,640]{1,0:T(8,128)(2,1)}, bf16[64,...) custom-call(s32[1]{0:T(128)} %bitcast.refs_0_.core_ref, bf16[2048,896]{1,0:T(8,128)(2,1)} %join_up.1.refs_1_, ...), custom_call_target="tpu_custom_call" | custom-call | flops 19327352832 | bytes 20000000 | tf_op jit(solution)/shard_map/pass_first/pallas_call | solution.py:443
  198.2 29.9 %all-to-all-done.2.own_ref = bf16[16,768,128]{2,1,0:T(8,128)(2,1)S(1)} async-done(((bf16[16,768,128]{2,1,0:T(8,128)(2,1)}), bf16[16,768,128]{2,1,0:T(8,128)(2,1)S(1)}, u32[]{:S(2)}, u32[]{:S(2)}) %all-to-all-start.2) | async-done | bytes 3145760 | tf_op jit(solution)/shard_map/all_to_all | solution.py:729
  233.7 2.8 collective-permute-done.16
  238.0 8.3 %collective-permute-done.17 = bf16[1,128,2048]{2,1,0:T(8,128)(2,1)S(1)} collective-permute-done((bf16[1,128,2048]{2,1,0:T(8,128)(2,1)S(1)}, bf16[1,128,2048]{2,1,0:T(8,128)(2,1)S(1)}, u32[]{:S(2)}, u32[]{:S(2)}) %collective-permute-start.17) | collective-permute-done | bytes 524320 | tf_op jit(solution)/shard_map/ppermute | solution.py:673
  247.6 20.7 %collective-permute-done.7.lower_ref = bf16[8,768,128]{2,1,0:T(8,128)(2,1)S(1)} collective-permute-done((bf16[8,768,128]{2,1,0:T(8,128)(2,1)S(1)}, bf16[8,768,128]{2,1,0:T(8,128)(2,1)S(1)}, u32[]{:S(2)}, u32[]{:S(2)}) %collective-permute-start.7) | collective-permute-done | bytes 1572896 | tf_op jit(solution)/shard_map/ppermute | solution.py:679
  273.0 6.4 collective-permute-done.19.moving_ref
  290.8 17.3 %collective-permute-done.8.upper_ref = bf16[8,768,128]{2,1,0:T(8,128)(2,1)} collective-permute-done((bf16[8,768,128]{2,1,0:T(8,128)(2,1)}, bf16[8,768,128]{2,1,0:T(8,128)(2,1)}, u32[]{:S(2)}, u32[]{:S(2)}) %collective-permute-start.8) | collective-permute-done | bytes 1572896 | tf_op jit(solution)/shard_map/ppermute | solution.py:679
  308.2 8.3 %collective-permute-done.23.refs_10_ = bf16[128,2048]{1,0:T(8,128)(2,1)S(1)} collective-permute-done((bf16[128,2048]{1,0:T(8,128)(2,1)S(1)}, bf16[128,2048]{1,0:T(8,128)(2,1)S(1)}, u32[]{:S(2)}, u32[]{:S(2)}) %collective-permute-start.23) | collective-permute-done | bytes 524320 | tf_op jit(solution)/shard_map/ppermute | solution.py:673
  318.2 6.6 collective-permute-done.24.refs_11_
  327.5 2.6 collective-permute-done.28.refs_15_
  330.1 3.7 collective-permute-start.29
  333.8 6.4 join_halves.1
  341.2 36.0 %pass_middle.1 = (bf16[1024,2048]{1,0:T(8,128)(2,1)}, bf16[1024,2048]{1,0:T(8,128)(2,1)}, bf16[1024,640]{1,0:T(8,128)(2,1)}, bf16[1024,896]{1,0:T(8,128)(2,1)}, ...) custom-call(s32[1]{0:T(128)} %bitcast.refs_0_.core_ref, ...), custom_call_target="tpu_custom_call" | custom-call | flops 38654705664 | bytes 40000000 | tf_op jit(solution)/shard_map/pass_middle/pallas_call | solution.py:443
  378.3 3.3 collective-permute-done.31
  389.8 4.4 collective-permute-done.33
  395.8 8.9 %down_gradients.2 = (bf16[16,320,128]{2,1,0:T(8,128)(2,1)}, bf16[16,320,128]{2,1,0:T(8,128)(2,1)}) custom-call(s32[1]{0:T(128)} %bitcast.refs_0_.core_ref, bf16[1024,640]{1,0:T(8,128)(2,1)} %get-tuple-element.105.left_ref, bf16[1024,2048]{1,0:T(8,128)(2,1)} %get-tuple-element.106.rest_0_), custom_call_target="tpu_custom_call" | custom-call | flops 5368709120 | bytes 10747904 | tf_op jit(solution)/shard_map/down_gradients/pallas_call | solution.py:505
  404.7 5.0 collective-permute-done.35
  412.8 10.2 %up_gradients.2 = (bf16[16,464,128]{2,1,0:T(8,128)(2,1)}, bf16[16,464,128]{2,1,0:T(8,128)(2,1)}, f32[1,896]{1,0:T(1,128)}) custom-call(s32[1]{0:T(128)} %bitcast.refs_0_.core_ref, bf16[1024,896]{1,0:T(8,128)(2,1)} %get-tuple-element.109.left_ref, bf16[1024,2048]{1,0:T(8,128)(2,1)} %get-tuple-element.110.rest_0_, f32[16,2048]{1,0:T(8,128)} %get-tuple-element.111.rest_1_), custom_call_target="tpu_custom_call" | custom-call | flops 7516192768 | bytes 13369344 | tf_op jit(solution)/shard_map/up_gradients/pallas_call | solution.py:505
  422.9 3.6 collective-permute-done.36
  428.5 12.5 %collective-permute-done.37.moving_ref = bf16[2,128,2048]{2,1,0:T(8,128)(2,1)S(1)} collective-permute-done((bf16[2,128,2048]{2,1,0:T(8,128)(2,1)S(1)}, bf16[2,128,2048]{2,1,0:T(8,128)(2,1)S(1)}, u32[]{:S(2)}, u32[]{:S(2)}) %collective-permute-start.37) | collective-permute-done | bytes 1048608 | tf_op jit(solution)/shard_map/ppermute | solution.py:673
  441.0 3.5 collective-permute-start.38
  446.9 3.0 backward_end.2
  450.3 5.2 collective-permute-done.42
  455.5 2.7 add_convert_fusion.3
  458.2 12.1 %all-to-all-start.3 = ((bf16[16,320,128]{2,1,0:T(8,128)(2,1)}), bf16[16,320,128]{2,1,0:T(8,128)(2,1)S(1)}, u32[]{:S(2)}, u32[]{:S(2)}) async-start(bf16[16,320,128]{2,1,0:T(8,128)(2,1)} %add_convert_fusion.3), calls=%async_computation.3 | async-start | bytes 2621440 | tf_op jit(solution)/shard_map/all_to_all | solution.py:729
  474.8 30.2 %collective-permute-done.43.rest_1_.refs_11_ = bf16[128,2048]{1,0:T(8,128)(2,1)} collective-permute-done((bf16[128,2048]{1,0:T(8,128)(2,1)}, bf16[128,2048]{1,0:T(8,128)(2,1)}, u32[]{:S(2)}, u32[]{:S(2)}) %collective-permute-start.43) | collective-permute-done | bytes 524320 | tf_op jit(solution)/shard_map/ppermute | solution.py:673
  509.3 4.2 collective-permute-done.44.rest_2_.refs_12_
  515.4 5.7 collective-permute-done.40
  524.6 3.6 collective-permute-done.50.rest_7_.refs_17_
  528.2 3.3 add_convert_fusion.1
  531.5 8.8 %all-to-all-start.4 = ((bf16[16,464,128]{2,1,0:T(8,128)(2,1)}), bf16[16,464,128]{2,1,0:T(8,128)(2,1)S(1)}, u32[]{:S(2)}, u32[]{:S(2)}) async-start(bf16[16,464,128]{2,1,0:T(8,128)(2,1)} %add_convert_fusion.1), calls=%async_computation.4 | async-start | bytes 3801088 | tf_op jit(solution)/shard_map/all_to_all | solution.py:729
  544.9 8.9 %down_gradients.3 = (bf16[16,320,128]{2,1,0:T(8,128)(2,1)}, bf16[16,320,128]{2,1,0:T(8,128)(2,1)}) custom-call(s32[1]{0:T(128)} %bitcast.refs_0_.core_ref, bf16[1024,640]{1,0:T(8,128)(2,1)} %get-tuple-element.117.left_ref, bf16[128,2048]{1,0:T(8,128)(2,1)} %maximum_select_fusion.2.rest_0_.refs_10_, ...), custom_call_target="tpu_custom_call" | custom-call | flops 5368709120 | bytes 10747904 | tf_op jit(solution)/shard_map/down_gradients/pallas_call | solution.py:505
  555.0 26.5 %pass_last.1 = (bf16[1024,2048]{1,0:T(8,128)(2,1)}, bf16[1024,896]{1,0:T(8,128)(2,1)}, f32[16,2048]{1,0:T(8,128)}, bf16[64,2048]{1,0:T(8,128)(2,1)}, bf16[448,20...) custom-call(s32[1]{0:T(128)} %bitcast.refs_0_.core_ref, bf16[2048,896]{1,0:T(8,128)(2,1)} %join_up.1.refs_1_, ...), custom_call_target="tpu_custom_call" | custom-call | flops 19327352832 | bytes 20000000 | tf_op jit(solution)/shard_map/pass_last/pallas_call | solution.py:443
  584.1 2.7 add_convert_fusion.2
  586.8 6.8 all-to-all-start.5
  593.7 10.1 %up_gradients.3 = (bf16[16,464,128]{2,1,0:T(8,128)(2,1)}, bf16[16,464,128]{2,1,0:T(8,128)(2,1)}, f32[1,896]{1,0:T(1,128)}) custom-call(s32[1]{0:T(128)} %bitcast.refs_0_.core_ref, bf16[1024,896]{1,0:T(8,128)(2,1)} %get-tuple-element.131.left_ref, bf16[1024,2048]{1,0:T(8,128)(2,1)} %get-tuple-element.134.refs_9_.rest_0_, f32[16,2048]{1,0:T(8,128)} %get-tuple-element.135.rest_1_), custom_call_target="tpu_custom_call" | custom-call | flops 7516192768 | bytes 13369344 | tf_op jit(solution)/shard_map/up_gradients/pallas_call | solution.py:505
  607.8 17.6 %collective-permute-done.54 = bf16[1,64,2048]{2,1,0:T(8,128)(2,1)S(1)} collective-permute-done((bf16[1,64,2048]{2,1,0:T(8,128)(2,1)S(1)}, bf16[1,64,2048]{2,1,0:T(8,128)(2,1)S(1)}, u32[]{:S(2)}, u32[]{:S(2)}) %collective-permute-start.54) | collective-permute-done | bytes 262176 | tf_op jit(solution)/shard_map/ppermute | solution.py:673
  629.4 6.1 collective-permute-done.55
  635.5 2.9 fusion.4
  640.7 6.7 collective-permute-done.63
  647.4 3.3 add_convert_fusion
  650.7 6.7 all-to-all-start.6
  660.5 44.1 %collective-permute-done.58.moving_ref = bf16[1,128,2048]{2,1,0:T(8,128)(2,1)S(1)} collective-permute-done((bf16[1,128,2048]{2,1,0:T(8,128)(2,1)S(1)}, bf16[1,128,2048]{2,1,0:T(8,128)(2,1)S(1)}, u32[]{:S(2)}, u32[]{:S(2)}) %collective-permute-start.58) | collective-permute-done | bytes 524320 | tf_op jit(solution)/shard_map/ppermute | solution.py:673
  708.4 7.3 spread_gradients.2
  716.4 2.9 backward_end.3
  725.6 10.0 %collective-permute-done.62 = bf16[128,2048]{1,0:T(8,128)(2,1)S(1)} collective-permute-done((bf16[128,2048]{1,0:T(8,128)(2,1)S(1)}, bf16[128,2048]{1,0:T(8,128)(2,1)S(1)}, u32[]{:S(2)}, u32[]{:S(2)}) %collective-permute-start.62) | collective-permute-done | bytes 524320 | tf_op jit(solution)/shard_map/ppermute | solution.py:679
  737.8 7.3 spread_gradients.3
  (317 shorter events, 127.9 us)
Async XLA Ops:
  8.8 49.7 %all-to-all-start = ((bf16[16,464,128]{2,1,0:T(8,128)(2,1)}), bf16[16,464,128]{2,1,0:T(8,128)(2,1)S(1)}, u32[]{:S(2)}, u32[]{:S(2)}) async-start(bf16[16,464,128]{2,1,0:T(8,128)(2,1)} %pack_first.1), calls=%async_computation | async-start | bytes 3801088 | tf_op jit(solution)/shard_map/all_to_all | solution.py:729
  58.5 35.7 %all-to-all-start.1 = ((bf16[16,320,128]{2,1,0:T(8,128)(2,1)}), bf16[16,320,128]{2,1,0:T(8,128)(2,1)S(1)}, u32[]{:S(2)}, u32[]{:S(2)}) async-start(bf16[16,320,128]{2,1,0:T(8,128)(2,1)} %pack_down.1), calls=%async_computation.1 | async-start | bytes 2621440 | tf_op jit(solution)/shard_map/all_to_all | solution.py:729
  65.6 8.2 %collective-permute-start = (bf16[2,128,2048]{2,1,0:T(8,128)(2,1)}, bf16[2,128,2048]{2,1,0:T(8,128)(2,1)}, u32[]{:S(2)}, u32[]{:S(2)}) collective-permute-start(bf16[2,128,2048]{2,1,0:T(8,128)(2,1)} %pad_maximum_fusion), channel_id=1, source_target_pairs={{0,2},{2,0},{4,6},{6,4},{8,10},{10,8},{12,14},{14,12},{16,18},{18,... | collective-permute-start | bytes 3145736 | tf_op jit(solution)/shard_map/ppermute | solution.py:676
  67.9 43.0 %collective-permute-start.2 = (bf16[16,464,128]{2,1,0:T(8,128)(2,1)S(1)}, bf16[16,464,128]{2,1,0:T(8,128)(2,1)}, u32[]{:S(2)}, u32[]{:S(2)}) collective-permute-start(bf16[16,464,128]{2,1,0:T(8,128)(2,1)S(1)} %all-to-all-done.own_ref), channel_id=1, source_target_pairs={{0,1},{1,0},{2,3},{3,2},{4,5},{5,4},{6,7},{7,6},{8,9},{9,8},{10,11... | collective-permute-start | bytes 5701640 | tf_op jit(solution)/shard_map/ppermute | solution.py:679
  94.3 16.6 %collective-permute-start.1 = (bf16[2,128,2048]{2,1,0:T(8,128)(2,1)}, bf16[2,128,2048]{2,1,0:T(8,128)(2,1)}, u32[]{:S(2)}, u32[]{:S(2)}) collective-permute-start(bf16[2,128,2048]{2,1,0:T(8,128)(2,1)} %select_multiply_fusion.refs_10_.refs_17_), channel_id=1, source_target_pairs={{0,8},{2,6},{8,16},{10,2},{16,24},{18,10},{24,28},{26,18},{28,20},... | collective-permute-start | bytes 3145736 | tf_op jit(solution)/shard_map/ppermute | solution.py:673
  110.9 14.3 %collective-permute-start.3 = (bf16[2,128,2048]{2,1,0:T(8,128)(2,1)}, bf16[2,128,2048]{2,1,0:T(8,128)(2,1)}, u32[]{:S(2)}, u32[]{:S(2)}) collective-permute-start(bf16[2,128,2048]{2,1,0:T(8,128)(2,1)} %collective-permute-done.1.refs_11_.refs_18_), channel_id=1, source_target_pairs={{0,8},{2,6},{8,16},{10,2},{16,24},{18,10},{24,28},{26,18},{28,20},... | collective-permute-start | bytes 3145736 | tf_op jit(solution)/shard_map/ppermute | solution.py:673
  112.0 30.2 %collective-permute-start.5 = (bf16[16,320,128]{2,1,0:T(8,128)(2,1)}, bf16[16,320,128]{2,1,0:T(8,128)(2,1)S(1)}, u32[]{:S(2)}, u32[]{:S(2)}) collective-permute-start(bf16[16,320,128]{2,1,0:T(8,128)(2,1)} %copy-done.10), channel_id=1, source_target_pairs={{0,1},{1,0},{2,3},{3,2},{4,5},{5,4},{6,7},{7,6},{8,9},{9,8},{10,11... | collective-permute-start | bytes 3932168 | tf_op jit(solution)/shard_map/ppermute | solution.py:679
  125.1 14.2 %collective-permute-start.4 = (bf16[2,128,2048]{2,1,0:T(8,128)(2,1)}, bf16[2,128,2048]{2,1,0:T(8,128)(2,1)S(1)}, u32[]{:S(2)}, u32[]{:S(2)}) collective-permute-start(bf16[2,128,2048]{2,1,0:T(8,128)(2,1)} %collective-permute-done.3.refs_12_.refs_19_), channel_id=1, source_target_pairs={{0,8},{2,6},{8,16},{10,2},{16,24},{18,10},{24,28},{26,18},{28,20},... | collective-permute-start | bytes 3145736 | tf_op jit(solution)/shard_map/ppermute | solution.py:673
  142.2 8.3 %collective-permute-start.6 = (bf16[2,64,2048]{2,1,0:T(8,128)(2,1)S(1)}, bf16[2,64,2048]{2,1,0:T(8,128)(2,1)S(1)}, u32[]{:S(2)}, u32[]{:S(2)}) collective-permute-start(bf16[2,64,2048]{2,1,0:T(8,128)(2,1)S(1)} %constant_dynamic-slice_fusion.4), channel_id=1, source_target_pairs={{0,8},{2,6},{8,16},{10,2},{16,24},{18,10},{24,28},{26,18},{28,20},... | collective-permute-start | bytes 1572872 | tf_op jit(solution)/shard_map/ppermute | solution.py:673
  151.4 76.7 %all-to-all-start.2 = ((bf16[16,768,128]{2,1,0:T(8,128)(2,1)}), bf16[16,768,128]{2,1,0:T(8,128)(2,1)S(1)}, u32[]{:S(2)}, u32[]{:S(2)}) async-start(bf16[16,768,128]{2,1,0:T(8,128)(2,1)} %pack_both.1), calls=%async_computation.2 | async-start | bytes 6291456 | tf_op jit(solution)/shard_map/all_to_all | solution.py:729
  158.3 10.5 %collective-permute-start.10 = (bf16[2,128,2048]{2,1,0:T(8,128)(2,1)}, bf16[2,128,2048]{2,1,0:T(8,128)(2,1)}, u32[]{:S(2)}, u32[]{:S(2)}) collective-permute-start(bf16[2,128,2048]{2,1,0:T(8,128)(2,1)} %collective-permute-done.1.refs_11_.refs_18_), channel_id=1, source_target_pairs={{0,2},{2,0},{4,6},{6,4},{8,10},{10,8},{12,14},{14,12},{16,18},{18,... | collective-permute-start | bytes 3145736 | tf_op jit(solution)/shard_map/ppermute | solution.py:676
  158.6 10.1 %collective-permute-start.11 = (bf16[2,128,2048]{2,1,0:T(8,128)(2,1)}, bf16[2,128,2048]{2,1,0:T(8,128)(2,1)}, u32[]{:S(2)}, u32[]{:S(2)}) collective-permute-start(bf16[2,128,2048]{2,1,0:T(8,128)(2,1)} %collective-permute-done.3.refs_12_.refs_19_), channel_id=1, source_target_pairs={{0,2},{2,0},{4,6},{6,4},{8,10},{10,8},{12,14},{14,12},{16,18},{18,... | collective-permute-start | bytes 3145736 | tf_op jit(solution)/shard_map/ppermute | solution.py:676
  158.8 10.0 %collective-permute-start.12 = (bf16[2,128,2048]{2,1,0:T(8,128)(2,1)}, bf16[2,128,2048]{2,1,0:T(8,128)(2,1)}, u32[]{:S(2)}, u32[]{:S(2)}) collective-permute-start(bf16[2,128,2048]{2,1,0:T(8,128)(2,1)} %copy-done.29), channel_id=1, source_target_pairs={{0,2},{2,0},{4,6},{6,4},{8,10},{10,8},{12,14},{14,12},{16,18},{18,... | collective-permute-start | bytes 3145736 | tf_op jit(solution)/shard_map/ppermute | solution.py:676
  162.8 5.9 collective-permute-start.13
  198.1 35.7 %collective-permute-start.14 = (bf16[448,2048]{1,0:T(8,128)(2,1)}, bf16[448,2048]{1,0:T(8,128)(2,1)}, u32[]{:S(2)}, u32[]{:S(2)}) collective-permute-start(bf16[448,2048]{1,0:T(8,128)(2,1)} %get-tuple-element.93), channel_id=1, source_target_pairs={{0,2},{2,0},{4,6},{6,4},{8,10},{10,8},{12,14},{14,12},{16,18},{18,... | collective-permute-start | bytes 5505032 | tf_op jit(solution)/shard_map/ppermute | solution.py:676
  230.8 5.7 collective-permute-start.16
  232.5 35.8 %collective-permute-start.7 = (bf16[8,768,128]{2,1,0:T(8,128)(2,1)S(1)}, bf16[8,768,128]{2,1,0:T(8,128)(2,1)S(1)}, u32[]{:S(2)}, u32[]{:S(2)}) collective-permute-start(bf16[8,768,128]{2,1,0:T(8,128)(2,1)S(1)} %get-tuple-element.223), channel_id=1, source_target_pairs={{0,1},{1,0},{2,3},{3,2},{4,5},{5,4},{6,7},{7,6},{8,9},{9,8},{10,11... | collective-permute-start | bytes 4718600 | tf_op jit(solution)/shard_map/ppermute | solution.py:679
  237.9 8.4 %collective-permute-start.17 = (bf16[1,128,2048]{2,1,0:T(8,128)(2,1)S(1)}, bf16[1,128,2048]{2,1,0:T(8,128)(2,1)S(1)}, u32[]{:S(2)}, u32[]{:S(2)}) collective-permute-start(bf16[1,128,2048]{2,1,0:T(8,128)(2,1)S(1)} %fusion.7), channel_id=1, source_target_pairs={{0,8},{2,6},{8,16},{10,2},{16,24},{18,10},{24,28},{26,18},{28,20},... | collective-permute-start | bytes 1572872 | tf_op jit(solution)/shard_map/ppermute | solution.py:673
  247.6 20.8 %collective-permute-start.18 = (bf16[1,128,2048]{2,1,0:T(8,128)(2,1)S(1)}, bf16[1,128,2048]{2,1,0:T(8,128)(2,1)S(1)}, u32[]{:S(2)}, u32[]{:S(2)}) collective-permute-start(bf16[1,128,2048]{2,1,0:T(8,128)(2,1)S(1)} %fusion.6), channel_id=1, source_target_pairs={{0,8},{2,6},{8,16},{10,2},{16,24},{18,10},{24,28},{26,18},{28,20},... | collective-permute-start | bytes 1572872 | tf_op jit(solution)/shard_map/ppermute | solution.py:673
  270.8 8.6 %collective-permute-start.19 = (bf16[1,128,2048]{2,1,0:T(8,128)(2,1)}, bf16[1,128,2048]{2,1,0:T(8,128)(2,1)S(1)}, u32[]{:S(2)}, u32[]{:S(2)}) collective-permute-start(bf16[1,128,2048]{2,1,0:T(8,128)(2,1)} %fusion.5), channel_id=1, source_target_pairs={{0,8},{2,6},{8,16},{10,2},{16,24},{18,10},{24,28},{26,18},{28,20},... | collective-permute-start | bytes 1572872 | tf_op jit(solution)/shard_map/ppermute | solution.py:673
  271.8 36.3 %collective-permute-start.8 = (bf16[8,768,128]{2,1,0:T(8,128)(2,1)}, bf16[8,768,128]{2,1,0:T(8,128)(2,1)}, u32[]{:S(2)}, u32[]{:S(2)}) collective-permute-start(bf16[8,768,128]{2,1,0:T(8,128)(2,1)} %get-tuple-element.222), channel_id=1, source_target_pairs={{0,1},{1,0},{2,3},{3,2},{4,5},{5,4},{6,7},{7,6},{8,9},{9,8},{10,11... | collective-permute-start | bytes 4718600 | tf_op jit(solution)/shard_map/ppermute | solution.py:679
  280.2 3.1 collective-permute-start.20
  289.4 18.8 %collective-permute-start.22 = (bf16[128,2048]{1,0:T(8,128)(2,1)S(1)}, bf16[128,2048]{1,0:T(8,128)(2,1)S(1)}, u32[]{:S(2)}, u32[]{:S(2)}) collective-permute-start(bf16[128,2048]{1,0:T(8,128)(2,1)S(1)} %maximum_select_fusion.refs_8_), channel_id=1, source_target_pairs={{0,8},{2,6},{8,16},{10,2},{16,24},{18,10},{24,28},{26,18},{28,20},... | collective-permute-start | bytes 1572872 | tf_op jit(solution)/shard_map/ppermute | solution.py:673
  308.2 8.3 %collective-permute-start.23 = (bf16[128,2048]{1,0:T(8,128)(2,1)S(1)}, bf16[128,2048]{1,0:T(8,128)(2,1)S(1)}, u32[]{:S(2)}, u32[]{:S(2)}) collective-permute-start(bf16[128,2048]{1,0:T(8,128)(2,1)S(1)} %collective-permute-done.22.refs_9_), channel_id=1, source_target_pairs={{0,8},{2,6},{8,16},{10,2},{16,24},{18,10},{24,28},{26,18},{28,20},... | collective-permute-start | bytes 1572872 | tf_op jit(solution)/shard_map/ppermute | solution.py:673
  316.5 8.3 %collective-permute-start.24 = (bf16[128,2048]{1,0:T(8,128)(2,1)S(1)}, bf16[128,2048]{1,0:T(8,128)(2,1)S(1)}, u32[]{:S(2)}, u32[]{:S(2)}) collective-permute-start(bf16[128,2048]{1,0:T(8,128)(2,1)S(1)} %collective-permute-done.23.refs_10_), channel_id=1, source_target_pairs={{0,8},{2,6},{8,16},{10,2},{16,24},{18,10},{24,28},{26,18},{28,20},... | collective-permute-start | bytes 1572872 | tf_op jit(solution)/shard_map/ppermute | solution.py:673
  316.5 23.7 %collective-permute-start.25 = (bf16[128,2048]{1,0:T(8,128)(2,1)S(1)}, bf16[128,2048]{1,0:T(8,128)(2,1)S(1)}, u32[]{:S(2)}, u32[]{:S(2)}) collective-permute-start(bf16[128,2048]{1,0:T(8,128)(2,1)S(1)} %collective-permute-done.22.refs_9_), channel_id=1, source_target_pairs={{0,2},{2,0},{4,6},{6,4},{8,10},{10,8},{12,14},{14,12},{16,18},{18,... | collective-permute-start | bytes 1572872 | tf_op jit(solution)/shard_map/ppermute | solution.py:676
  318.2 22.1 %collective-permute-start.26 = (bf16[128,2048]{1,0:T(8,128)(2,1)S(1)}, bf16[128,2048]{1,0:T(8,128)(2,1)S(1)}, u32[]{:S(2)}, u32[]{:S(2)}) collective-permute-start(bf16[128,2048]{1,0:T(8,128)(2,1)S(1)} %collective-permute-done.23.refs_10_), channel_id=1, source_target_pairs={{0,2},{2,0},{4,6},{6,4},{8,10},{10,8},{12,14},{14,12},{16,18},{18,... | collective-permute-start | bytes 1572872 | tf_op jit(solution)/shard_map/ppermute | solution.py:676
  324.8 5.3 collective-permute-start.28
  324.9 15.3 %collective-permute-start.27 = (bf16[128,2048]{1,0:T(8,128)(2,1)S(1)}, bf16[128,2048]{1,0:T(8,128)(2,1)}, u32[]{:S(2)}, u32[]{:S(2)}) collective-permute-start(bf16[128,2048]{1,0:T(8,128)(2,1)S(1)} %collective-permute-done.24.refs_11_), channel_id=1, source_target_pairs={{0,2},{2,0},{4,6},{6,4},{8,10},{10,8},{12,14},{14,12},{16,18},{18,... | collective-permute-start | bytes 1572872 | tf_op jit(solution)/shard_map/ppermute | solution.py:676
  330.1 10.1 %collective-permute-start.29 = (bf16[64,2048]{1,0:T(8,128)(2,1)S(1)}, bf16[64,2048]{1,0:T(8,128)(2,1)}, u32[]{:S(2)}, u32[]{:S(2)}) collective-permute-start(bf16[64,2048]{1,0:T(8,128)(2,1)S(1)} %collective-permute-done.28.refs_15_), channel_id=1, source_target_pairs={{0,2},{2,0},{4,6},{6,4},{8,10},{10,8},{12,14},{14,12},{16,18},{18,... | collective-permute-start | bytes 786440 | tf_op jit(solution)/shard_map/ppermute | solution.py:676
  377.2 8.9 %collective-permute-start.34 = (bf16[448,2048]{1,0:T(8,128)(2,1)}, bf16[448,2048]{1,0:T(8,128)(2,1)S(1)}, u32[]{:S(2)}, u32[]{:S(2)}) collective-permute-start(bf16[448,2048]{1,0:T(8,128)(2,1)} %get-tuple-element.104), channel_id=1, source_target_pairs={{0,2},{2,0},{4,6},{6,4},{8,10},{10,8},{12,14},{14,12},{16,18},{18,... | collective-permute-start | bytes 5505032 | tf_op jit(solution)/shard_map/ppermute | solution.py:676
  377.4 4.3 collective-permute-start.31
  377.8 9.9 %collective-permute-start.30 = (bf16[448,2048]{1,0:T(8,128)(2,1)}, bf16[448,2048]{1,0:T(8,128)(2,1)S(1)}, u32[]{:S(2)}, u32[]{:S(2)}) collective-permute-start(bf16[448,2048]{1,0:T(8,128)(2,1)} %get-tuple-element.100), channel_id=1, source_target_pairs={{0,2},{2,0},{4,6},{6,4},{8,10},{10,8},{12,14},{14,12},{16,18},{18,... | collective-permute-start | bytes 5505032 | tf_op jit(solution)/shard_map/ppermute | solution.py:676
  377.9 6.7 collective-permute-start.32
  385.8 8.4 %collective-permute-start.33 = (bf16[2,64,2048]{2,1,0:T(8,128)(2,1)S(1)}, bf16[2,64,2048]{2,1,0:T(8,128)(2,1)S(1)}, u32[]{:S(2)}, u32[]{:S(2)}) collective-permute-start(bf16[2,64,2048]{2,1,0:T(8,128)(2,1)S(1)} %pad_maximum_fusion.1), channel_id=1, source_target_pairs={{0,8},{2,6},{8,16},{10,2},{16,24},{18,10},{24,28},{26,18},{28,20},... | collective-permute-start | bytes 1572872 | tf_op jit(solution)/shard_map/ppermute | solution.py:673
  395.5 14.3 %collective-permute-start.35 = (bf16[2,128,2048]{2,1,0:T(8,128)(2,1)}, bf16[2,128,2048]{2,1,0:T(8,128)(2,1)}, u32[]{:S(2)}, u32[]{:S(2)}) collective-permute-start(bf16[2,128,2048]{2,1,0:T(8,128)(2,1)} %fusion), channel_id=1, source_target_pairs={{0,8},{2,6},{8,16},{10,2},{16,24},{18,10},{24,28},{26,18},{28,20},... | collective-permute-start | bytes 3145736 | tf_op jit(solution)/shard_map/ppermute | solution.py:673
  412.2 14.3 %collective-permute-start.36 = (bf16[2,128,2048]{2,1,0:T(8,128)(2,1)}, bf16[2,128,2048]{2,1,0:T(8,128)(2,1)S(1)}, u32[]{:S(2)}, u32[]{:S(2)}) collective-permute-start(bf16[2,128,2048]{2,1,0:T(8,128)(2,1)} %fusion.1), channel_id=1, source_target_pairs={{0,8},{2,6},{8,16},{10,2},{16,24},{18,10},{24,28},{26,18},{28,20},... | collective-permute-start | bytes 3145736 | tf_op jit(solution)/shard_map/ppermute | solution.py:673
  426.9 14.1 %collective-permute-start.37 = (bf16[2,128,2048]{2,1,0:T(8,128)(2,1)S(1)}, bf16[2,128,2048]{2,1,0:T(8,128)(2,1)S(1)}, u32[]{:S(2)}, u32[]{:S(2)}) collective-permute-start(bf16[2,128,2048]{2,1,0:T(8,128)(2,1)S(1)} %fusion.2), channel_id=1, source_target_pairs={{0,8},{2,6},{8,16},{10,2},{16,24},{18,10},{24,28},{26,18},{28,20},... | collective-permute-start | bytes 3145736 | tf_op jit(solution)/shard_map/ppermute | solution.py:673
  427.3 28.2 %collective-permute-start.42 = (bf16[16,320,128]{2,1,0:T(8,128)(2,1)}, bf16[16,320,128]{2,1,0:T(8,128)(2,1)}, u32[]{:S(2)}, u32[]{:S(2)}) collective-permute-start(bf16[16,320,128]{2,1,0:T(8,128)(2,1)} %get-tuple-element.119), channel_id=1, source_target_pairs={{0,1},{1,0},{2,3},{3,2},{4,5},{5,4},{6,7},{7,6},{8,9},{9,8},{10,11... | collective-permute-start | bytes 3932168 | tf_op jit(solution)/shard_map/ppermute | solution.py:679
  441.0 5.1 collective-permute-start.38
  444.5 64.8 %collective-permute-start.45 = (bf16[16,464,128]{2,1,0:T(8,128)(2,1)}, bf16[16,464,128]{2,1,0:T(8,128)(2,1)}, u32[]{:S(2)}, u32[]{:S(2)}) collective-permute-start(bf16[16,464,128]{2,1,0:T(8,128)(2,1)} %get-tuple-element.121), channel_id=1, source_target_pairs={{0,1},{1,0},{2,3},{3,2},{4,5},{5,4},{6,7},{7,6},{8,9},{9,8},{10,11... | collective-permute-start | bytes 5701640 | tf_op jit(solution)/shard_map/ppermute | solution.py:679
  449.9 20.5 %collective-permute-start.41 = (bf16[64,2048]{1,0:T(8,128)(2,1)}, bf16[64,2048]{1,0:T(8,128)(2,1)S(1)}, u32[]{:S(2)}, u32[]{:S(2)}) collective-permute-start(bf16[64,2048]{1,0:T(8,128)(2,1)} %get-tuple-element.118), channel_id=1, source_target_pairs={{0,2},{2,0},{4,6},{6,4},{8,10},{10,8},{12,14},{14,12},{16,18},{18,... | collective-permute-start | bytes 786440 | tf_op jit(solution)/shard_map/ppermute | solution.py:676
  458.2 64.6 %all-to-all-start.3 = ((bf16[16,320,128]{2,1,0:T(8,128)(2,1)}), bf16[16,320,128]{2,1,0:T(8,128)(2,1)S(1)}, u32[]{:S(2)}, u32[]{:S(2)}) async-start(bf16[16,320,128]{2,1,0:T(8,128)(2,1)} %add_convert_fusion.3), calls=%async_computation.3 | async-start | bytes 2621440 | tf_op jit(solution)/shard_map/all_to_all | solution.py:729
  471.3 33.7 %collective-permute-start.43 = (bf16[128,2048]{1,0:T(8,128)(2,1)}, bf16[128,2048]{1,0:T(8,128)(2,1)}, u32[]{:S(2)}, u32[]{:S(2)}) collective-permute-start(bf16[128,2048]{1,0:T(8,128)(2,1)} %maximum_select_fusion.2.rest_0_.refs_10_), channel_id=1, source_target_pairs={{0,8},{2,6},{8,16},{10,2},{16,24},{18,10},{24,28},{26,18},{28,20},... | collective-permute-start | bytes 1572872 | tf_op jit(solution)/shard_map/ppermute | solution.py:673
  474.7 32.1 %collective-permute-start.39 = (bf16[64,2048]{1,0:T(8,128)(2,1)}, bf16[64,2048]{1,0:T(8,128)(2,1)S(1)}, u32[]{:S(2)}, u32[]{:S(2)}) collective-permute-start(bf16[64,2048]{1,0:T(8,128)(2,1)} %forward_out.1), channel_id=1, source_target_pairs={{0,2},{2,0},{4,6},{6,4},{8,10},{10,8},{12,14},{14,12},{16,18},{18,... | collective-permute-start | bytes 786440 | tf_op jit(solution)/shard_map/ppermute | solution.py:676
  505.0 8.5 %collective-permute-start.44 = (bf16[128,2048]{1,0:T(8,128)(2,1)}, bf16[128,2048]{1,0:T(8,128)(2,1)S(1)}, u32[]{:S(2)}, u32[]{:S(2)}) collective-permute-start(bf16[128,2048]{1,0:T(8,128)(2,1)} %collective-permute-done.43.rest_1_.refs_11_), channel_id=1, source_target_pairs={{0,8},{2,6},{8,16},{10,2},{16,24},{18,10},{24,28},{26,18},{28,20},... | collective-permute-start | bytes 1572872 | tf_op jit(solution)/shard_map/ppermute | solution.py:673
  508.0 13.1 %collective-permute-start.40 = (bf16[128,2048]{1,0:T(8,128)(2,1)S(1)}, bf16[128,2048]{1,0:T(8,128)(2,1)S(1)}, u32[]{:S(2)}, u32[]{:S(2)}) collective-permute-start(bf16[128,2048]{1,0:T(8,128)(2,1)S(1)} %maximum_select_fusion.1), channel_id=1, source_target_pairs={{0,1},{1,0},{2,3},{3,2},{4,5},{5,4},{6,7},{7,6},{8,9},{9,8},{10,11... | collective-permute-start | bytes 1572872 | tf_op jit(solution)/shard_map/ppermute | solution.py:679
  513.5 8.5 %collective-permute-start.46 = (bf16[128,2048]{1,0:T(8,128)(2,1)S(1)}, bf16[128,2048]{1,0:T(8,128)(2,1)S(1)}, u32[]{:S(2)}, u32[]{:S(2)}) collective-permute-start(bf16[128,2048]{1,0:T(8,128)(2,1)S(1)} %collective-permute-done.44.rest_2_.refs_12_), channel_id=1, source_target_pairs={{0,8},{2,6},{8,16},{10,2},{16,24},{18,10},{24,28},{26,18},{28,20},... | collective-permute-start | bytes 1572872 | tf_op jit(solution)/shard_map/ppermute | solution.py:673
  522.9 5.4 collective-permute-start.50
  531.5 55.3 %all-to-all-start.4 = ((bf16[16,464,128]{2,1,0:T(8,128)(2,1)}), bf16[16,464,128]{2,1,0:T(8,128)(2,1)S(1)}, u32[]{:S(2)}, u32[]{:S(2)}) async-start(bf16[16,464,128]{2,1,0:T(8,128)(2,1)} %add_convert_fusion.1), calls=%async_computation.4 | async-start | bytes 3801088 | tf_op jit(solution)/shard_map/all_to_all | solution.py:729
  540.9 3.2 collective-permute-start.49
  541.3 3.3 collective-permute-start.51
  553.7 30.3 %collective-permute-start.56 = (bf16[16,320,128]{2,1,0:T(8,128)(2,1)}, bf16[16,320,128]{2,1,0:T(8,128)(2,1)}, u32[]{:S(2)}, u32[]{:S(2)}) collective-permute-start(bf16[16,320,128]{2,1,0:T(8,128)(2,1)} %get-tuple-element.138), channel_id=1, source_target_pairs={{0,1},{1,0},{2,3},{3,2},{4,5},{5,4},{6,7},{7,6},{8,9},{9,8},{10,11... | collective-permute-start | bytes 3932168 | tf_op jit(solution)/shard_map/ppermute | solution.py:679
  581.5 26.2 %collective-permute-start.52 = (bf16[448,2048]{1,0:T(8,128)(2,1)}, bf16[448,2048]{1,0:T(8,128)(2,1)}, u32[]{:S(2)}, u32[]{:S(2)}) collective-permute-start(bf16[448,2048]{1,0:T(8,128)(2,1)} %get-tuple-element.129), channel_id=1, source_target_pairs={{0,2},{2,0},{4,6},{6,4},{8,10},{10,8},{12,14},{14,12},{16,18},{18,... | collective-permute-start | bytes 5505032 | tf_op jit(solution)/shard_map/ppermute | solution.py:676
  586.8 48.7 %all-to-all-start.5 = ((bf16[16,320,128]{2,1,0:T(8,128)(2,1)}), bf16[16,320,128]{2,1,0:T(8,128)(2,1)S(1)}, u32[]{:S(2)}, u32[]{:S(2)}) async-start(bf16[16,320,128]{2,1,0:T(8,128)(2,1)} %add_convert_fusion.2), calls=%async_computation.5 | async-start | bytes 2621440 | tf_op jit(solution)/shard_map/all_to_all | solution.py:729
  604.3 43.2 %collective-permute-start.63 = (bf16[16,464,128]{2,1,0:T(8,128)(2,1)}, bf16[16,464,128]{2,1,0:T(8,128)(2,1)}, u32[]{:S(2)}, u32[]{:S(2)}) collective-permute-start(bf16[16,464,128]{2,1,0:T(8,128)(2,1)} %get-tuple-element.147), channel_id=1, source_target_pairs={{0,1},{1,0},{2,3},{3,2},{4,5},{5,4},{6,7},{7,6},{8,9},{9,8},{10,11... | collective-permute-start | bytes 5701640 | tf_op jit(solution)/shard_map/ppermute | solution.py:679
  606.5 18.8 %collective-permute-start.54 = (bf16[1,64,2048]{2,1,0:T(8,128)(2,1)S(1)}, bf16[1,64,2048]{2,1,0:T(8,128)(2,1)S(1)}, u32[]{:S(2)}, u32[]{:S(2)}) collective-permute-start(bf16[1,64,2048]{2,1,0:T(8,128)(2,1)S(1)} %fusion.16), channel_id=1, source_target_pairs={{0,8},{2,6},{8,16},{10,2},{16,24},{18,10},{24,28},{26,18},{28,20},... | collective-permute-start | bytes 786440 | tf_op jit(solution)/shard_map/ppermute | solution.py:673
  626.8 8.7 %collective-permute-start.55 = (bf16[1,128,2048]{2,1,0:T(8,128)(2,1)S(1)}, bf16[1,128,2048]{2,1,0:T(8,128)(2,1)}, u32[]{:S(2)}, u32[]{:S(2)}) collective-permute-start(bf16[1,128,2048]{2,1,0:T(8,128)(2,1)S(1)} %fusion.8), channel_id=1, source_target_pairs={{0,8},{2,6},{8,16},{10,2},{16,24},{18,10},{24,28},{26,18},{28,20},... | collective-permute-start | bytes 1572872 | tf_op jit(solution)/shard_map/ppermute | solution.py:673
  638.4 19.1 %collective-permute-start.57 = (bf16[1,128,2048]{2,1,0:T(8,128)(2,1)}, bf16[1,128,2048]{2,1,0:T(8,128)(2,1)}, u32[]{:S(2)}, u32[]{:S(2)}) collective-permute-start(bf16[1,128,2048]{2,1,0:T(8,128)(2,1)} %fusion.4), channel_id=1, source_target_pairs={{0,8},{2,6},{8,16},{10,2},{16,24},{18,10},{24,28},{26,18},{28,20},... | collective-permute-start | bytes 1572872 | tf_op jit(solution)/shard_map/ppermute | solution.py:673
  650.7 85.8 %all-to-all-start.6 = ((bf16[16,464,128]{2,1,0:T(8,128)(2,1)}), bf16[16,464,128]{2,1,0:T(8,128)(2,1)S(1)}, u32[]{:S(2)}, u32[]{:S(2)}) async-start(bf16[16,464,128]{2,1,0:T(8,128)(2,1)} %add_convert_fusion), calls=%async_computation.6 | async-start | bytes 3801088 | tf_op jit(solution)/shard_map/all_to_all | solution.py:729
  659.1 45.5 %collective-permute-start.58 = (bf16[1,128,2048]{2,1,0:T(8,128)(2,1)S(1)}, bf16[1,128,2048]{2,1,0:T(8,128)(2,1)S(1)}, u32[]{:S(2)}, u32[]{:S(2)}) collective-permute-start(bf16[1,128,2048]{2,1,0:T(8,128)(2,1)S(1)} %fusion.3), channel_id=1, source_target_pairs={{0,8},{2,6},{8,16},{10,2},{16,24},{18,10},{24,28},{26,18},{28,20},... | collective-permute-start | bytes 1572872 | tf_op jit(solution)/shard_map/ppermute | solution.py:673
  704.6 11.1 %collective-permute-start.59 = (bf16[1,64,2048]{2,1,0:T(8,128)(2,1)S(1)}, bf16[1,64,2048]{2,1,0:T(8,128)(2,1)S(1)}, u32[]{:S(2)}, u32[]{:S(2)}) collective-permute-start(bf16[1,64,2048]{2,1,0:T(8,128)(2,1)S(1)} %constant_dynamic-slice_fusion.5), channel_id=1, source_target_pairs={{0,2},{2,0},{4,6},{6,4},{8,10},{10,8},{12,14},{14,12},{16,18},{18,... | collective-permute-start | bytes 786440 | tf_op jit(solution)/shard_map/ppermute | solution.py:676
  707.1 8.5 %collective-permute-start.60 = (f32[2,448]{1,0:T(2,128)S(1)}, f32[2,448]{1,0:T(2,128)S(1)}, u32[]{:S(2)}, u32[]{:S(2)}) collective-permute-start(f32[2,448]{1,0:T(2,128)S(1)} %pad_maximum_fusion.3), channel_id=1, source_target_pairs={{0,1},{1,0},{2,3},{3,2},{4,5},{5,4},{6,7},{7,6},{8,9},{9,8},{10,11... | collective-permute-start | bytes 10760 | tf_op jit(solution)/shard_map/ppermute | solution.py:679
  722.3 13.2 %collective-permute-start.62 = (bf16[128,2048]{1,0:T(8,128)(2,1)S(1)}, bf16[128,2048]{1,0:T(8,128)(2,1)S(1)}, u32[]{:S(2)}, u32[]{:S(2)}) collective-permute-start(bf16[128,2048]{1,0:T(8,128)(2,1)S(1)} %maximum_select_fusion.3), channel_id=1, source_target_pairs={{0,1},{1,0},{2,3},{3,2},{4,5},{5,4},{6,7},{7,6},{8,9},{9,8},{10,11... | collective-permute-start | bytes 1572872 | tf_op jit(solution)/shard_map/ppermute | solution.py:679
  (63 other events, 853.2 us)

commit v10 on v9

--- a/solution.py
+++ b/solution.py
@@ -934,7 +934,7 @@
     *up_pair, bias_first = up_gradients(slim, after(normed, up_last), sums)
     up_sent = over(up_pair[1])
     (grad_end,) = ring_sum((after(parts[0], up_pair[0]), parts[1], parts[2]), needed={1: (down_first,)})
-    up_first = summed(up_pair[0], up_sent, down_first)
+    up_first = summed(up_pair[0], up_sent, down_first, grad_end[2])
     sums = jnp.concatenate([bias_first, bias_last], axis=0)
     sums_qkv = sums[:, : 3 * WIDE].reshape(LAYERS, 3, 2, HEAD_DIM)
     sums_up = sums[:, 3 * WIDE :].reshape(LAYERS, 2, hidden)

time: 757 us -> 745 us (0.984)
  waiting for transfers between devices: 372 us -> 363 us
    ppermute x24, waiting for transfers between devices: 189 us -> 151 us  [along(): return lax.ppermute(x, 'dp', ring_pairs)]
    ppermute x12, waiting for transfers between devices: 82 us -> 97.6 us  [over(): return lax.ppermute(x, 'tensor', [(0, 1), (1, 0)])]
    all_to_all x7, waiting for transfers between devices: 87.4 us -> 99.5 us  [spread(): return lax.all_to_all(x, 'dp', 0, 0, axis_index_groups=inner, tiled=True)]
  transfers between devices with their start and end apart: 71 -> 71, of which waited for: 43 -> 45; matrix products, arithmetic and copies ran while one was open for 8% -> 8% of each run, Pallas kernels for 18% -> 18%
where the time goes in v10:
time: 745 us; the launch traced here: 734 us
  waiting for transfers between devices  363 us (49%)
  Pallas kernels  183 us (25%)
  starting transfers between devices  108 us (14%)
  other arithmetic  54.1 us (7%)
  local copies, waits for them, and re-layouts  24.8 us (3%)
    ppermute x24, waiting for transfers between devices, along(): return lax.ppermute(x, 'dp', ring_pairs)  151 us
    all_to_all x7, waiting for transfers between devices, spread(): return lax.all_to_all(x, 'dp', 0, 0, axis_index_groups=inner, tiled=True)  99.5 us
    ppermute x12, waiting for transfers between devices, over(): return lax.ppermute(x, 'tensor', [(0, 1), (1, 0)])  97.6 us
    pallas_call x3, Pallas kernels, call_pass(): pl.pallas_call(partial(layer_pass, mode), in_specs=[SMEM_SPEC] + [VMEM_SP...  91.9 us
    all_to_all x7, starting transfers between devices, spread(): return lax.all_to_all(x, 'dp', 0, 0, axis_index_groups=inner, tiled=True)  51.2 us
    pallas_call x4, Pallas kernels, call_gradients(): pl.pallas_call(partial(gradient_slabs, own_rows, other_rows, with_sums, l...  38.1 us
    ppermute x24, starting transfers between devices, along(): return lax.ppermute(x, 'dp', ring_pairs)  22.2 us
    ppermute x28, starting transfers between devices, across(): return lax.ppermute(x, 'dp', core_pairs)  20.6 us
  transfers between devices with their start and end apart: 71, of which 45 were waited for; matrix products, arithmetic and copies ran while one was open for 8% of the time, Pallas kernels for 18%

profile of v10, /device:TPU:13, one launch (start us, length us, event | category | flops | bytes accessed | tf_op | source)
XLA Modules:
  0.0 733.8 jit_solution(13097865683027835381)
XLA Ops:
  4.8 4.0 pack_first.1
  8.8 6.5 all-to-all-start
  15.3 3.5 pack_down.1
  18.9 39.7 %all-to-all-done.own_ref = bf16[16,464,128]{2,1,0:T(8,128)(2,1)S(1)} async-done(((bf16[16,464,128]{2,1,0:T(8,128)(2,1)}), bf16[16,464,128]{2,1,0:T(8,128)(2,1)S(1)}, u32[]{:S(2)}, u32[]{:S(2)}) %all-to-all-start) | async-done | bytes 1900576 | tf_op jit(solution)/shard_map/all_to_all | solution.py:729
  58.5 4.8 all-to-all-start.1
  69.3 4.4 pack_both.1
  73.8 2.7 select_multiply_fusion.refs_10_.refs_17_
  76.4 17.9 %all-to-all-done.1.own_ref = bf16[16,320,128]{2,1,0:T(8,128)(2,1)S(1)} async-done(((bf16[16,320,128]{2,1,0:T(8,128)(2,1)}), bf16[16,320,128]{2,1,0:T(8,128)(2,1)S(1)}, u32[]{:S(2)}, u32[]{:S(2)}) %all-to-all-start.1) | async-done | bytes 1310752 | tf_op jit(solution)/shard_map/all_to_all | solution.py:729
  98.1 2.7 concatenate.76.refs_3_
  100.8 10.1 %collective-permute-done.2.other_ref = bf16[16,464,128]{2,1,0:T(8,128)(2,1)} collective-permute-done((bf16[16,464,128]{2,1,0:T(8,128)(2,1)S(1)}, bf16[16,464,128]{2,1,0:T(8,128)(2,1)}, u32[]{:S(2)}, u32[]{:S(2)}) %collective-permute-start.2) | collective-permute-done | bytes 1900576 | tf_op jit(solution)/shard_map/ppermute | solution.py:679
  118.0 7.1 collective-permute-done.3.refs_12_.refs_19_
  126.3 4.8 join_up.1.refs_1_
  131.1 8.2 %collective-permute-done.4.refs_13_.refs_20_ = bf16[2,128,2048]{2,1,0:T(8,128)(2,1)S(1)} collective-permute-done((bf16[2,128,2048]{2,1,0:T(8,128)(2,1)}, bf16[2,128,2048]{2,1,0:T(8,128)(2,1)S(1)}, u32[]{:S(2)}, u32[]{:S(2)}) %collective-permute-start.4) | collective-permute-done | bytes 1048608 | tf_op jit(solution)/shard_map/ppermute | solution.py:673
  139.3 2.9 collective-permute-done.5.other_ref
  143.4 7.1 collective-permute-done.6.refs_17_.refs_24_
  151.4 6.8 all-to-all-start.2
  164.6 4.2 join_down.1.refs_2_
  168.8 29.3 %pass_first.1 = (bf16[1024,2048]{1,0:T(8,128)(2,1)}, bf16[1024,384]{1,0:T(8,128)(2,1)}, f32[1024,512]{1,0:T(8,128)}, bf16[1024,640]{1,0:T(8,128)(2,1)}, bf16[64,...) custom-call(s32[1]{0:T(128)} %bitcast.refs_0_.core_ref, bf16[2048,896]{1,0:T(8,128)(2,1)} %join_up.1.refs_1_, ...), custom_call_target="tpu_custom_call" | custom-call | flops 19327352832 | bytes 20000000 | tf_op jit(solution)/shard_map/pass_first/pallas_call | solution.py:443
  198.2 29.8 %all-to-all-done.2.own_ref = bf16[16,768,128]{2,1,0:T(8,128)(2,1)S(1)} async-done(((bf16[16,768,128]{2,1,0:T(8,128)(2,1)}), bf16[16,768,128]{2,1,0:T(8,128)(2,1)S(1)}, u32[]{:S(2)}, u32[]{:S(2)}) %all-to-all-start.2) | async-done | bytes 3145760 | tf_op jit(solution)/shard_map/all_to_all | solution.py:729
  233.7 2.8 collective-permute-done.16
  238.0 8.3 %collective-permute-done.17 = bf16[1,128,2048]{2,1,0:T(8,128)(2,1)S(1)} collective-permute-done((bf16[1,128,2048]{2,1,0:T(8,128)(2,1)S(1)}, bf16[1,128,2048]{2,1,0:T(8,128)(2,1)S(1)}, u32[]{:S(2)}, u32[]{:S(2)}) %collective-permute-start.17) | collective-permute-done | bytes 524320 | tf_op jit(solution)/shard_map/ppermute | solution.py:673
  247.6 20.7 %collective-permute-done.7.lower_ref = bf16[8,768,128]{2,1,0:T(8,128)(2,1)S(1)} collective-permute-done((bf16[8,768,128]{2,1,0:T(8,128)(2,1)S(1)}, bf16[8,768,128]{2,1,0:T(8,128)(2,1)S(1)}, u32[]{:S(2)}, u32[]{:S(2)}) %collective-permute-start.7) | collective-permute-done | bytes 1572896 | tf_op jit(solution)/shard_map/ppermute | solution.py:679
  273.1 6.4 collective-permute-done.19.moving_ref
  290.8 17.3 %collective-permute-done.8.upper_ref = bf16[8,768,128]{2,1,0:T(8,128)(2,1)} collective-permute-done((bf16[8,768,128]{2,1,0:T(8,128)(2,1)}, bf16[8,768,128]{2,1,0:T(8,128)(2,1)}, u32[]{:S(2)}, u32[]{:S(2)}) %collective-permute-start.8) | collective-permute-done | bytes 1572896 | tf_op jit(solution)/shard_map/ppermute | solution.py:679
  308.2 8.3 %collective-permute-done.23.refs_10_ = bf16[128,2048]{1,0:T(8,128)(2,1)S(1)} collective-permute-done((bf16[128,2048]{1,0:T(8,128)(2,1)S(1)}, bf16[128,2048]{1,0:T(8,128)(2,1)S(1)}, u32[]{:S(2)}, u32[]{:S(2)}) %collective-permute-start.23) | collective-permute-done | bytes 524320 | tf_op jit(solution)/shard_map/ppermute | solution.py:673
  318.2 6.6 collective-permute-done.24.refs_11_
  327.5 2.6 collective-permute-done.28.refs_15_
  330.1 3.7 collective-permute-start.29
  333.8 6.3 join_halves.1
  341.2 36.0 %pass_middle.1 = (bf16[1024,2048]{1,0:T(8,128)(2,1)}, bf16[1024,2048]{1,0:T(8,128)(2,1)}, bf16[1024,640]{1,0:T(8,128)(2,1)}, bf16[1024,896]{1,0:T(8,128)(2,1)}, ...) custom-call(s32[1]{0:T(128)} %bitcast.refs_0_.core_ref, ...), custom_call_target="tpu_custom_call" | custom-call | flops 38654705664 | bytes 40000000 | tf_op jit(solution)/shard_map/pass_middle/pallas_call | solution.py:443
  378.3 3.3 collective-permute-done.31
  389.8 4.4 collective-permute-done.33
  395.8 8.9 %down_gradients.2 = (bf16[16,320,128]{2,1,0:T(8,128)(2,1)}, bf16[16,320,128]{2,1,0:T(8,128)(2,1)}) custom-call(s32[1]{0:T(128)} %bitcast.refs_0_.core_ref, bf16[1024,640]{1,0:T(8,128)(2,1)} %get-tuple-element.105.left_ref, bf16[1024,2048]{1,0:T(8,128)(2,1)} %get-tuple-element.106.rest_0_), custom_call_target="tpu_custom_call" | custom-call | flops 5368709120 | bytes 10747904 | tf_op jit(solution)/shard_map/down_gradients/pallas_call | solution.py:505
  404.8 5.0 collective-permute-done.35
  412.8 10.2 %up_gradients.2 = (bf16[16,464,128]{2,1,0:T(8,128)(2,1)}, bf16[16,464,128]{2,1,0:T(8,128)(2,1)}, f32[1,896]{1,0:T(1,128)}) custom-call(s32[1]{0:T(128)} %bitcast.refs_0_.core_ref, bf16[1024,896]{1,0:T(8,128)(2,1)} %get-tuple-element.109.left_ref, bf16[1024,2048]{1,0:T(8,128)(2,1)} %get-tuple-element.110.rest_0_, f32[16,2048]{1,0:T(8,128)} %get-tuple-element.111.rest_1_), custom_call_target="tpu_custom_call" | custom-call | flops 7516192768 | bytes 13369344 | tf_op jit(solution)/shard_map/up_gradients/pallas_call | solution.py:505
  422.9 3.6 collective-permute-done.36
  428.5 12.5 %collective-permute-done.37.moving_ref = bf16[2,128,2048]{2,1,0:T(8,128)(2,1)S(1)} collective-permute-done((bf16[2,128,2048]{2,1,0:T(8,128)(2,1)S(1)}, bf16[2,128,2048]{2,1,0:T(8,128)(2,1)S(1)}, u32[]{:S(2)}, u32[]{:S(2)}) %collective-permute-start.37) | collective-permute-done | bytes 1048608 | tf_op jit(solution)/shard_map/ppermute | solution.py:673
  441.0 3.5 collective-permute-start.38
  446.9 3.0 backward_end.2
  450.3 5.2 collective-permute-done.42
  455.5 2.7 add_convert_fusion.3
  458.2 12.1 %all-to-all-start.3 = ((bf16[16,320,128]{2,1,0:T(8,128)(2,1)}), bf16[16,320,128]{2,1,0:T(8,128)(2,1)S(1)}, u32[]{:S(2)}, u32[]{:S(2)}) async-start(bf16[16,320,128]{2,1,0:T(8,128)(2,1)} %add_convert_fusion.3), calls=%async_computation.3 | async-start | bytes 2621440 | tf_op jit(solution)/shard_map/all_to_all | solution.py:729
  474.8 30.2 %collective-permute-done.43.rest_1_.refs_11_ = bf16[128,2048]{1,0:T(8,128)(2,1)} collective-permute-done((bf16[128,2048]{1,0:T(8,128)(2,1)}, bf16[128,2048]{1,0:T(8,128)(2,1)}, u32[]{:S(2)}, u32[]{:S(2)}) %collective-permute-start.43) | collective-permute-done | bytes 524320 | tf_op jit(solution)/shard_map/ppermute | solution.py:673
  509.3 4.2 collective-permute-done.44.rest_2_.refs_12_
  515.4 5.7 collective-permute-done.40
  525.3 3.8 collective-permute-done.50.rest_7_.refs_17_
  529.1 3.3 add_convert_fusion.1
  532.4 8.8 %all-to-all-start.4 = ((bf16[16,464,128]{2,1,0:T(8,128)(2,1)}), bf16[16,464,128]{2,1,0:T(8,128)(2,1)S(1)}, u32[]{:S(2)}, u32[]{:S(2)}) async-start(bf16[16,464,128]{2,1,0:T(8,128)(2,1)} %add_convert_fusion.1), calls=%async_computation.4 | async-start | bytes 3801088 | tf_op jit(solution)/shard_map/all_to_all | solution.py:729
  546.0 8.9 %down_gradients.3 = (bf16[16,320,128]{2,1,0:T(8,128)(2,1)}, bf16[16,320,128]{2,1,0:T(8,128)(2,1)}) custom-call(s32[1]{0:T(128)} %bitcast.refs_0_.core_ref, bf16[1024,640]{1,0:T(8,128)(2,1)} %get-tuple-element.117.left_ref, bf16[128,2048]{1,0:T(8,128)(2,1)} %maximum_select_fusion.2.rest_0_.refs_10_, ...), custom_call_target="tpu_custom_call" | custom-call | flops 5368709120 | bytes 10747904 | tf_op jit(solution)/shard_map/down_gradients/pallas_call | solution.py:505
  556.1 26.6 %pass_last.1 = (bf16[1024,2048]{1,0:T(8,128)(2,1)}, bf16[1024,896]{1,0:T(8,128)(2,1)}, f32[16,2048]{1,0:T(8,128)}, bf16[64,2048]{1,0:T(8,128)(2,1)}, bf16[448,20...) custom-call(s32[1]{0:T(128)} %bitcast.refs_0_.core_ref, bf16[2048,896]{1,0:T(8,128)(2,1)} %join_up.1.refs_1_, ...), custom_call_target="tpu_custom_call" | custom-call | flops 19327352832 | bytes 20000000 | tf_op jit(solution)/shard_map/pass_last/pallas_call | solution.py:443
  585.2 2.7 add_convert_fusion.2
  588.0 6.8 all-to-all-start.5
  594.8 10.1 %up_gradients.3 = (bf16[16,464,128]{2,1,0:T(8,128)(2,1)}, bf16[16,464,128]{2,1,0:T(8,128)(2,1)}, f32[1,896]{1,0:T(1,128)}) custom-call(s32[1]{0:T(128)} %bitcast.refs_0_.core_ref, bf16[1024,896]{1,0:T(8,128)(2,1)} %get-tuple-element.131.left_ref, bf16[1024,2048]{1,0:T(8,128)(2,1)} %get-tuple-element.134.refs_9_.rest_0_, f32[16,2048]{1,0:T(8,128)} %get-tuple-element.135.rest_1_), custom_call_target="tpu_custom_call" | custom-call | flops 7516192768 | bytes 13369344 | tf_op jit(solution)/shard_map/up_gradients/pallas_call | solution.py:505
  609.0 17.5 %collective-permute-done.54 = bf16[1,64,2048]{2,1,0:T(8,128)(2,1)S(1)} collective-permute-done((bf16[1,64,2048]{2,1,0:T(8,128)(2,1)S(1)}, bf16[1,64,2048]{2,1,0:T(8,128)(2,1)S(1)}, u32[]{:S(2)}, u32[]{:S(2)}) %collective-permute-start.54) | collective-permute-done | bytes 262176 | tf_op jit(solution)/shard_map/ppermute | solution.py:673
  631.4 5.3 collective-permute-done.55
  640.6 6.5 collective-permute-done.57
  650.4 22.5 %collective-permute-done.63 = bf16[16,464,128]{2,1,0:T(8,128)(2,1)} collective-permute-done((bf16[16,464,128]{2,1,0:T(8,128)(2,1)}, bf16[16,464,128]{2,1,0:T(8,128)(2,1)}, u32[]{:S(2)}, u32[]{:S(2)}) %collective-permute-start.63) | collective-permute-done | bytes 1900576 | tf_op jit(solution)/shard_map/ppermute | solution.py:679
  672.9 3.3 add_convert_fusion
  676.2 5.4 all-to-all-start.6
  684.5 7.3 spread_gradients.2
  692.6 2.9 backward_end.3
  701.7 9.9 %collective-permute-done.62 = bf16[128,2048]{1,0:T(8,128)(2,1)S(1)} collective-permute-done((bf16[128,2048]{1,0:T(8,128)(2,1)S(1)}, bf16[128,2048]{1,0:T(8,128)(2,1)S(1)}, u32[]{:S(2)}, u32[]{:S(2)}) %collective-permute-start.62) | collective-permute-done | bytes 524320 | tf_op jit(solution)/shard_map/ppermute | solution.py:679
  712.7 12.1 %all-to-all-done.6.up_ref = bf16[16,464,128]{2,1,0:T(8,128)(2,1)S(1)} async-done(((bf16[16,464,128]{2,1,0:T(8,128)(2,1)}), bf16[16,464,128]{2,1,0:T(8,128)(2,1)S(1)}, u32[]{:S(2)}, u32[]{:S(2)}) %all-to-all-start.6) | async-done | bytes 1900576 | tf_op jit(solution)/shard_map/all_to_all | solution.py:729
  726.0 7.3 spread_gradients.3
  (315 shorter events, 130.7 us)
Async XLA Ops:
  8.8 49.7 %all-to-all-start = ((bf16[16,464,128]{2,1,0:T(8,128)(2,1)}), bf16[16,464,128]{2,1,0:T(8,128)(2,1)S(1)}, u32[]{:S(2)}, u32[]{:S(2)}) async-start(bf16[16,464,128]{2,1,0:T(8,128)(2,1)} %pack_first.1), calls=%async_computation | async-start | bytes 3801088 | tf_op jit(solution)/shard_map/all_to_all | solution.py:729
  58.5 35.7 %all-to-all-start.1 = ((bf16[16,320,128]{2,1,0:T(8,128)(2,1)}), bf16[16,320,128]{2,1,0:T(8,128)(2,1)S(1)}, u32[]{:S(2)}, u32[]{:S(2)}) async-start(bf16[16,320,128]{2,1,0:T(8,128)(2,1)} %pack_down.1), calls=%async_computation.1 | async-start | bytes 2621440 | tf_op jit(solution)/shard_map/all_to_all | solution.py:729
  65.6 8.2 %collective-permute-start = (bf16[2,128,2048]{2,1,0:T(8,128)(2,1)}, bf16[2,128,2048]{2,1,0:T(8,128)(2,1)}, u32[]{:S(2)}, u32[]{:S(2)}) collective-permute-start(bf16[2,128,2048]{2,1,0:T(8,128)(2,1)} %pad_maximum_fusion), channel_id=1, source_target_pairs={{0,2},{2,0},{4,6},{6,4},{8,10},{10,8},{12,14},{14,12},{16,18},{18,... | collective-permute-start | bytes 3145736 | tf_op jit(solution)/shard_map/ppermute | solution.py:676
  67.9 43.0 %collective-permute-start.2 = (bf16[16,464,128]{2,1,0:T(8,128)(2,1)S(1)}, bf16[16,464,128]{2,1,0:T(8,128)(2,1)}, u32[]{:S(2)}, u32[]{:S(2)}) collective-permute-start(bf16[16,464,128]{2,1,0:T(8,128)(2,1)S(1)} %all-to-all-done.own_ref), channel_id=1, source_target_pairs={{0,1},{1,0},{2,3},{3,2},{4,5},{5,4},{6,7},{7,6},{8,9},{9,8},{10,11... | collective-permute-start | bytes 5701640 | tf_op jit(solution)/shard_map/ppermute | solution.py:679
  94.3 16.6 %collective-permute-start.1 = (bf16[2,128,2048]{2,1,0:T(8,128)(2,1)}, bf16[2,128,2048]{2,1,0:T(8,128)(2,1)}, u32[]{:S(2)}, u32[]{:S(2)}) collective-permute-start(bf16[2,128,2048]{2,1,0:T(8,128)(2,1)} %select_multiply_fusion.refs_10_.refs_17_), channel_id=1, source_target_pairs={{0,8},{2,6},{8,16},{10,2},{16,24},{18,10},{24,28},{26,18},{28,20},... | collective-permute-start | bytes 3145736 | tf_op jit(solution)/shard_map/ppermute | solution.py:673
  110.9 14.3 %collective-permute-start.3 = (bf16[2,128,2048]{2,1,0:T(8,128)(2,1)}, bf16[2,128,2048]{2,1,0:T(8,128)(2,1)}, u32[]{:S(2)}, u32[]{:S(2)}) collective-permute-start(bf16[2,128,2048]{2,1,0:T(8,128)(2,1)} %collective-permute-done.1.refs_11_.refs_18_), channel_id=1, source_target_pairs={{0,8},{2,6},{8,16},{10,2},{16,24},{18,10},{24,28},{26,18},{28,20},... | collective-permute-start | bytes 3145736 | tf_op jit(solution)/shard_map/ppermute | solution.py:673
  112.0 30.2 %collective-permute-start.5 = (bf16[16,320,128]{2,1,0:T(8,128)(2,1)}, bf16[16,320,128]{2,1,0:T(8,128)(2,1)S(1)}, u32[]{:S(2)}, u32[]{:S(2)}) collective-permute-start(bf16[16,320,128]{2,1,0:T(8,128)(2,1)} %copy-done.11), channel_id=1, source_target_pairs={{0,1},{1,0},{2,3},{3,2},{4,5},{5,4},{6,7},{7,6},{8,9},{9,8},{10,11... | collective-permute-start | bytes 3932168 | tf_op jit(solution)/shard_map/ppermute | solution.py:679
  125.1 14.2 %collective-permute-start.4 = (bf16[2,128,2048]{2,1,0:T(8,128)(2,1)}, bf16[2,128,2048]{2,1,0:T(8,128)(2,1)S(1)}, u32[]{:S(2)}, u32[]{:S(2)}) collective-permute-start(bf16[2,128,2048]{2,1,0:T(8,128)(2,1)} %collective-permute-done.3.refs_12_.refs_19_), channel_id=1, source_target_pairs={{0,8},{2,6},{8,16},{10,2},{16,24},{18,10},{24,28},{26,18},{28,20},... | collective-permute-start | bytes 3145736 | tf_op jit(solution)/shard_map/ppermute | solution.py:673
  142.2 8.3 %collective-permute-start.6 = (bf16[2,64,2048]{2,1,0:T(8,128)(2,1)S(1)}, bf16[2,64,2048]{2,1,0:T(8,128)(2,1)S(1)}, u32[]{:S(2)}, u32[]{:S(2)}) collective-permute-start(bf16[2,64,2048]{2,1,0:T(8,128)(2,1)S(1)} %constant_dynamic-slice_fusion.4), channel_id=1, source_target_pairs={{0,8},{2,6},{8,16},{10,2},{16,24},{18,10},{24,28},{26,18},{28,20},... | collective-permute-start | bytes 1572872 | tf_op jit(solution)/shard_map/ppermute | solution.py:673
  151.4 76.7 %all-to-all-start.2 = ((bf16[16,768,128]{2,1,0:T(8,128)(2,1)}), bf16[16,768,128]{2,1,0:T(8,128)(2,1)S(1)}, u32[]{:S(2)}, u32[]{:S(2)}) async-start(bf16[16,768,128]{2,1,0:T(8,128)(2,1)} %pack_both.1), calls=%async_computation.2 | async-start | bytes 6291456 | tf_op jit(solution)/shard_map/all_to_all | solution.py:729
  158.3 10.5 %collective-permute-start.10 = (bf16[2,128,2048]{2,1,0:T(8,128)(2,1)}, bf16[2,128,2048]{2,1,0:T(8,128)(2,1)}, u32[]{:S(2)}, u32[]{:S(2)}) collective-permute-start(bf16[2,128,2048]{2,1,0:T(8,128)(2,1)} %collective-permute-done.1.refs_11_.refs_18_), channel_id=1, source_target_pairs={{0,2},{2,0},{4,6},{6,4},{8,10},{10,8},{12,14},{14,12},{16,18},{18,... | collective-permute-start | bytes 3145736 | tf_op jit(solution)/shard_map/ppermute | solution.py:676
  158.6 10.2 %collective-permute-start.11 = (bf16[2,128,2048]{2,1,0:T(8,128)(2,1)}, bf16[2,128,2048]{2,1,0:T(8,128)(2,1)}, u32[]{:S(2)}, u32[]{:S(2)}) collective-permute-start(bf16[2,128,2048]{2,1,0:T(8,128)(2,1)} %collective-permute-done.3.refs_12_.refs_19_), channel_id=1, source_target_pairs={{0,2},{2,0},{4,6},{6,4},{8,10},{10,8},{12,14},{14,12},{16,18},{18,... | collective-permute-start | bytes 3145736 | tf_op jit(solution)/shard_map/ppermute | solution.py:676
  158.8 10.0 %collective-permute-start.12 = (bf16[2,128,2048]{2,1,0:T(8,128)(2,1)}, bf16[2,128,2048]{2,1,0:T(8,128)(2,1)}, u32[]{:S(2)}, u32[]{:S(2)}) collective-permute-start(bf16[2,128,2048]{2,1,0:T(8,128)(2,1)} %copy-done.29), channel_id=1, source_target_pairs={{0,2},{2,0},{4,6},{6,4},{8,10},{10,8},{12,14},{14,12},{16,18},{18,... | collective-permute-start | bytes 3145736 | tf_op jit(solution)/shard_map/ppermute | solution.py:676
  162.9 6.0 collective-permute-start.13
  198.1 35.6 %collective-permute-start.14 = (bf16[448,2048]{1,0:T(8,128)(2,1)}, bf16[448,2048]{1,0:T(8,128)(2,1)}, u32[]{:S(2)}, u32[]{:S(2)}) collective-permute-start(bf16[448,2048]{1,0:T(8,128)(2,1)} %get-tuple-element.93), channel_id=1, source_target_pairs={{0,2},{2,0},{4,6},{6,4},{8,10},{10,8},{12,14},{14,12},{16,18},{18,... | collective-permute-start | bytes 5505032 | tf_op jit(solution)/shard_map/ppermute | solution.py:676
  230.8 5.7 collective-permute-start.16
  232.5 35.8 %collective-permute-start.7 = (bf16[8,768,128]{2,1,0:T(8,128)(2,1)S(1)}, bf16[8,768,128]{2,1,0:T(8,128)(2,1)S(1)}, u32[]{:S(2)}, u32[]{:S(2)}) collective-permute-start(bf16[8,768,128]{2,1,0:T(8,128)(2,1)S(1)} %get-tuple-element.223), channel_id=1, source_target_pairs={{0,1},{1,0},{2,3},{3,2},{4,5},{5,4},{6,7},{7,6},{8,9},{9,8},{10,11... | collective-permute-start | bytes 4718600 | tf_op jit(solution)/shard_map/ppermute | solution.py:679
  237.9 8.4 %collective-permute-start.17 = (bf16[1,128,2048]{2,1,0:T(8,128)(2,1)S(1)}, bf16[1,128,2048]{2,1,0:T(8,128)(2,1)S(1)}, u32[]{:S(2)}, u32[]{:S(2)}) collective-permute-start(bf16[1,128,2048]{2,1,0:T(8,128)(2,1)S(1)} %fusion.7), channel_id=1, source_target_pairs={{0,8},{2,6},{8,16},{10,2},{16,24},{18,10},{24,28},{26,18},{28,20},... | collective-permute-start | bytes 1572872 | tf_op jit(solution)/shard_map/ppermute | solution.py:673
  247.6 20.8 %collective-permute-start.18 = (bf16[1,128,2048]{2,1,0:T(8,128)(2,1)S(1)}, bf16[1,128,2048]{2,1,0:T(8,128)(2,1)S(1)}, u32[]{:S(2)}, u32[]{:S(2)}) collective-permute-start(bf16[1,128,2048]{2,1,0:T(8,128)(2,1)S(1)} %fusion.6), channel_id=1, source_target_pairs={{0,8},{2,6},{8,16},{10,2},{16,24},{18,10},{24,28},{26,18},{28,20},... | collective-permute-start | bytes 1572872 | tf_op jit(solution)/shard_map/ppermute | solution.py:673
  270.8 8.6 %collective-permute-start.19 = (bf16[1,128,2048]{2,1,0:T(8,128)(2,1)}, bf16[1,128,2048]{2,1,0:T(8,128)(2,1)S(1)}, u32[]{:S(2)}, u32[]{:S(2)}) collective-permute-start(bf16[1,128,2048]{2,1,0:T(8,128)(2,1)} %fusion.5), channel_id=1, source_target_pairs={{0,8},{2,6},{8,16},{10,2},{16,24},{18,10},{24,28},{26,18},{28,20},... | collective-permute-start | bytes 1572872 | tf_op jit(solution)/shard_map/ppermute | solution.py:673
  271.8 36.3 %collective-permute-start.8 = (bf16[8,768,128]{2,1,0:T(8,128)(2,1)}, bf16[8,768,128]{2,1,0:T(8,128)(2,1)}, u32[]{:S(2)}, u32[]{:S(2)}) collective-permute-start(bf16[8,768,128]{2,1,0:T(8,128)(2,1)} %get-tuple-element.222), channel_id=1, source_target_pairs={{0,1},{1,0},{2,3},{3,2},{4,5},{5,4},{6,7},{7,6},{8,9},{9,8},{10,11... | collective-permute-start | bytes 4718600 | tf_op jit(solution)/shard_map/ppermute | solution.py:679
  280.2 3.1 collective-permute-start.20
  289.4 18.8 %collective-permute-start.22 = (bf16[128,2048]{1,0:T(8,128)(2,1)S(1)}, bf16[128,2048]{1,0:T(8,128)(2,1)S(1)}, u32[]{:S(2)}, u32[]{:S(2)}) collective-permute-start(bf16[128,2048]{1,0:T(8,128)(2,1)S(1)} %maximum_select_fusion.refs_8_), channel_id=1, source_target_pairs={{0,8},{2,6},{8,16},{10,2},{16,24},{18,10},{24,28},{26,18},{28,20},... | collective-permute-start | bytes 1572872 | tf_op jit(solution)/shard_map/ppermute | solution.py:673
  308.2 8.3 %collective-permute-start.23 = (bf16[128,2048]{1,0:T(8,128)(2,1)S(1)}, bf16[128,2048]{1,0:T(8,128)(2,1)S(1)}, u32[]{:S(2)}, u32[]{:S(2)}) collective-permute-start(bf16[128,2048]{1,0:T(8,128)(2,1)S(1)} %collective-permute-done.22.refs_9_), channel_id=1, source_target_pairs={{0,8},{2,6},{8,16},{10,2},{16,24},{18,10},{24,28},{26,18},{28,20},... | collective-permute-start | bytes 1572872 | tf_op jit(solution)/shard_map/ppermute | solution.py:673
  316.5 8.3 %collective-permute-start.24 = (bf16[128,2048]{1,0:T(8,128)(2,1)S(1)}, bf16[128,2048]{1,0:T(8,128)(2,1)S(1)}, u32[]{:S(2)}, u32[]{:S(2)}) collective-permute-start(bf16[128,2048]{1,0:T(8,128)(2,1)S(1)} %collective-permute-done.23.refs_10_), channel_id=1, source_target_pairs={{0,8},{2,6},{8,16},{10,2},{16,24},{18,10},{24,28},{26,18},{28,20},... | collective-permute-start | bytes 1572872 | tf_op jit(solution)/shard_map/ppermute | solution.py:673
  316.5 23.7 %collective-permute-start.25 = (bf16[128,2048]{1,0:T(8,128)(2,1)S(1)}, bf16[128,2048]{1,0:T(8,128)(2,1)S(1)}, u32[]{:S(2)}, u32[]{:S(2)}) collective-permute-start(bf16[128,2048]{1,0:T(8,128)(2,1)S(1)} %collective-permute-done.22.refs_9_), channel_id=1, source_target_pairs={{0,2},{2,0},{4,6},{6,4},{8,10},{10,8},{12,14},{14,12},{16,18},{18,... | collective-permute-start | bytes 1572872 | tf_op jit(solution)/shard_map/ppermute | solution.py:676
  318.2 22.0 %collective-permute-start.26 = (bf16[128,2048]{1,0:T(8,128)(2,1)S(1)}, bf16[128,2048]{1,0:T(8,128)(2,1)S(1)}, u32[]{:S(2)}, u32[]{:S(2)}) collective-permute-start(bf16[128,2048]{1,0:T(8,128)(2,1)S(1)} %collective-permute-done.23.refs_10_), channel_id=1, source_target_pairs={{0,2},{2,0},{4,6},{6,4},{8,10},{10,8},{12,14},{14,12},{16,18},{18,... | collective-permute-start | bytes 1572872 | tf_op jit(solution)/shard_map/ppermute | solution.py:676
  324.9 5.3 collective-permute-start.28
  324.9 15.3 %collective-permute-start.27 = (bf16[128,2048]{1,0:T(8,128)(2,1)S(1)}, bf16[128,2048]{1,0:T(8,128)(2,1)}, u32[]{:S(2)}, u32[]{:S(2)}) collective-permute-start(bf16[128,2048]{1,0:T(8,128)(2,1)S(1)} %collective-permute-done.24.refs_11_), channel_id=1, source_target_pairs={{0,2},{2,0},{4,6},{6,4},{8,10},{10,8},{12,14},{14,12},{16,18},{18,... | collective-permute-start | bytes 1572872 | tf_op jit(solution)/shard_map/ppermute | solution.py:676
  330.1 10.1 %collective-permute-start.29 = (bf16[64,2048]{1,0:T(8,128)(2,1)S(1)}, bf16[64,2048]{1,0:T(8,128)(2,1)}, u32[]{:S(2)}, u32[]{:S(2)}) collective-permute-start(bf16[64,2048]{1,0:T(8,128)(2,1)S(1)} %collective-permute-done.28.refs_15_), channel_id=1, source_target_pairs={{0,2},{2,0},{4,6},{6,4},{8,10},{10,8},{12,14},{14,12},{16,18},{18,... | collective-permute-start | bytes 786440 | tf_op jit(solution)/shard_map/ppermute | solution.py:676
  377.2 8.9 %collective-permute-start.34 = (bf16[448,2048]{1,0:T(8,128)(2,1)}, bf16[448,2048]{1,0:T(8,128)(2,1)S(1)}, u32[]{:S(2)}, u32[]{:S(2)}) collective-permute-start(bf16[448,2048]{1,0:T(8,128)(2,1)} %get-tuple-element.104), channel_id=1, source_target_pairs={{0,2},{2,0},{4,6},{6,4},{8,10},{10,8},{12,14},{14,12},{16,18},{18,... | collective-permute-start | bytes 5505032 | tf_op jit(solution)/shard_map/ppermute | solution.py:676
  377.4 4.3 collective-permute-start.31
  377.8 9.9 %collective-permute-start.30 = (bf16[448,2048]{1,0:T(8,128)(2,1)}, bf16[448,2048]{1,0:T(8,128)(2,1)S(1)}, u32[]{:S(2)}, u32[]{:S(2)}) collective-permute-start(bf16[448,2048]{1,0:T(8,128)(2,1)} %get-tuple-element.100), channel_id=1, source_target_pairs={{0,2},{2,0},{4,6},{6,4},{8,10},{10,8},{12,14},{14,12},{16,18},{18,... | collective-permute-start | bytes 5505032 | tf_op jit(solution)/shard_map/ppermute | solution.py:676
  377.9 6.7 collective-permute-start.32
  385.8 8.4 %collective-permute-start.33 = (bf16[2,64,2048]{2,1,0:T(8,128)(2,1)S(1)}, bf16[2,64,2048]{2,1,0:T(8,128)(2,1)S(1)}, u32[]{:S(2)}, u32[]{:S(2)}) collective-permute-start(bf16[2,64,2048]{2,1,0:T(8,128)(2,1)S(1)} %pad_maximum_fusion.1), channel_id=1, source_target_pairs={{0,8},{2,6},{8,16},{10,2},{16,24},{18,10},{24,28},{26,18},{28,20},... | collective-permute-start | bytes 1572872 | tf_op jit(solution)/shard_map/ppermute | solution.py:673
  395.5 14.3 %collective-permute-start.35 = (bf16[2,128,2048]{2,1,0:T(8,128)(2,1)}, bf16[2,128,2048]{2,1,0:T(8,128)(2,1)}, u32[]{:S(2)}, u32[]{:S(2)}) collective-permute-start(bf16[2,128,2048]{2,1,0:T(8,128)(2,1)} %fusion), channel_id=1, source_target_pairs={{0,8},{2,6},{8,16},{10,2},{16,24},{18,10},{24,28},{26,18},{28,20},... | collective-permute-start | bytes 3145736 | tf_op jit(solution)/shard_map/ppermute | solution.py:673
  412.2 14.3 %collective-permute-start.36 = (bf16[2,128,2048]{2,1,0:T(8,128)(2,1)}, bf16[2,128,2048]{2,1,0:T(8,128)(2,1)S(1)}, u32[]{:S(2)}, u32[]{:S(2)}) collective-permute-start(bf16[2,128,2048]{2,1,0:T(8,128)(2,1)} %fusion.1), channel_id=1, source_target_pairs={{0,8},{2,6},{8,16},{10,2},{16,24},{18,10},{24,28},{26,18},{28,20},... | collective-permute-start | bytes 3145736 | tf_op jit(solution)/shard_map/ppermute | solution.py:673
  426.9 14.1 %collective-permute-start.37 = (bf16[2,128,2048]{2,1,0:T(8,128)(2,1)S(1)}, bf16[2,128,2048]{2,1,0:T(8,128)(2,1)S(1)}, u32[]{:S(2)}, u32[]{:S(2)}) collective-permute-start(bf16[2,128,2048]{2,1,0:T(8,128)(2,1)S(1)} %fusion.2), channel_id=1, source_target_pairs={{0,8},{2,6},{8,16},{10,2},{16,24},{18,10},{24,28},{26,18},{28,20},... | collective-permute-start | bytes 3145736 | tf_op jit(solution)/shard_map/ppermute | solution.py:673
  427.3 28.2 %collective-permute-start.42 = (bf16[16,320,128]{2,1,0:T(8,128)(2,1)}, bf16[16,320,128]{2,1,0:T(8,128)(2,1)}, u32[]{:S(2)}, u32[]{:S(2)}) collective-permute-start(bf16[16,320,128]{2,1,0:T(8,128)(2,1)} %get-tuple-element.119), channel_id=1, source_target_pairs={{0,1},{1,0},{2,3},{3,2},{4,5},{5,4},{6,7},{7,6},{8,9},{9,8},{10,11... | collective-permute-start | bytes 3932168 | tf_op jit(solution)/shard_map/ppermute | solution.py:679
  441.0 5.1 collective-permute-start.38
  444.5 64.8 %collective-permute-start.45 = (bf16[16,464,128]{2,1,0:T(8,128)(2,1)}, bf16[16,464,128]{2,1,0:T(8,128)(2,1)}, u32[]{:S(2)}, u32[]{:S(2)}) collective-permute-start(bf16[16,464,128]{2,1,0:T(8,128)(2,1)} %get-tuple-element.121), channel_id=1, source_target_pairs={{0,1},{1,0},{2,3},{3,2},{4,5},{5,4},{6,7},{7,6},{8,9},{9,8},{10,11... | collective-permute-start | bytes 5701640 | tf_op jit(solution)/shard_map/ppermute | solution.py:679
  449.9 20.5 %collective-permute-start.41 = (bf16[64,2048]{1,0:T(8,128)(2,1)}, bf16[64,2048]{1,0:T(8,128)(2,1)S(1)}, u32[]{:S(2)}, u32[]{:S(2)}) collective-permute-start(bf16[64,2048]{1,0:T(8,128)(2,1)} %get-tuple-element.118), channel_id=1, source_target_pairs={{0,2},{2,0},{4,6},{6,4},{8,10},{10,8},{12,14},{14,12},{16,18},{18,... | collective-permute-start | bytes 786440 | tf_op jit(solution)/shard_map/ppermute | solution.py:676
  458.2 65.4 %all-to-all-start.3 = ((bf16[16,320,128]{2,1,0:T(8,128)(2,1)}), bf16[16,320,128]{2,1,0:T(8,128)(2,1)S(1)}, u32[]{:S(2)}, u32[]{:S(2)}) async-start(bf16[16,320,128]{2,1,0:T(8,128)(2,1)} %add_convert_fusion.3), calls=%async_computation.3 | async-start | bytes 2621440 | tf_op jit(solution)/shard_map/all_to_all | solution.py:729
  471.3 33.7 %collective-permute-start.43 = (bf16[128,2048]{1,0:T(8,128)(2,1)}, bf16[128,2048]{1,0:T(8,128)(2,1)}, u32[]{:S(2)}, u32[]{:S(2)}) collective-permute-start(bf16[128,2048]{1,0:T(8,128)(2,1)} %maximum_select_fusion.2.rest_0_.refs_10_), channel_id=1, source_target_pairs={{0,8},{2,6},{8,16},{10,2},{16,24},{18,10},{24,28},{26,18},{28,20},... | collective-permute-start | bytes 1572872 | tf_op jit(solution)/shard_map/ppermute | solution.py:673
  474.8 32.2 %collective-permute-start.39 = (bf16[64,2048]{1,0:T(8,128)(2,1)}, bf16[64,2048]{1,0:T(8,128)(2,1)S(1)}, u32[]{:S(2)}, u32[]{:S(2)}) collective-permute-start(bf16[64,2048]{1,0:T(8,128)(2,1)} %forward_out.1), channel_id=1, source_target_pairs={{0,2},{2,0},{4,6},{6,4},{8,10},{10,8},{12,14},{14,12},{16,18},{18,... | collective-permute-start | bytes 786440 | tf_op jit(solution)/shard_map/ppermute | solution.py:676
  505.0 8.5 %collective-permute-start.44 = (bf16[128,2048]{1,0:T(8,128)(2,1)}, bf16[128,2048]{1,0:T(8,128)(2,1)S(1)}, u32[]{:S(2)}, u32[]{:S(2)}) collective-permute-start(bf16[128,2048]{1,0:T(8,128)(2,1)} %collective-permute-done.43.rest_1_.refs_11_), channel_id=1, source_target_pairs={{0,8},{2,6},{8,16},{10,2},{16,24},{18,10},{24,28},{26,18},{28,20},... | collective-permute-start | bytes 1572872 | tf_op jit(solution)/shard_map/ppermute | solution.py:673
  508.1 13.1 %collective-permute-start.40 = (bf16[128,2048]{1,0:T(8,128)(2,1)S(1)}, bf16[128,2048]{1,0:T(8,128)(2,1)S(1)}, u32[]{:S(2)}, u32[]{:S(2)}) collective-permute-start(bf16[128,2048]{1,0:T(8,128)(2,1)S(1)} %maximum_select_fusion.1), channel_id=1, source_target_pairs={{0,1},{1,0},{2,3},{3,2},{4,5},{5,4},{6,7},{7,6},{8,9},{9,8},{10,11... | collective-permute-start | bytes 1572872 | tf_op jit(solution)/shard_map/ppermute | solution.py:679
  513.5 8.5 %collective-permute-start.46 = (bf16[128,2048]{1,0:T(8,128)(2,1)S(1)}, bf16[128,2048]{1,0:T(8,128)(2,1)S(1)}, u32[]{:S(2)}, u32[]{:S(2)}) collective-permute-start(bf16[128,2048]{1,0:T(8,128)(2,1)S(1)} %collective-permute-done.44.rest_2_.refs_12_), channel_id=1, source_target_pairs={{0,8},{2,6},{8,16},{10,2},{16,24},{18,10},{24,28},{26,18},{28,20},... | collective-permute-start | bytes 1572872 | tf_op jit(solution)/shard_map/ppermute | solution.py:673
  523.6 5.5 collective-permute-start.50
  532.4 55.6 %all-to-all-start.4 = ((bf16[16,464,128]{2,1,0:T(8,128)(2,1)}), bf16[16,464,128]{2,1,0:T(8,128)(2,1)S(1)}, u32[]{:S(2)}, u32[]{:S(2)}) async-start(bf16[16,464,128]{2,1,0:T(8,128)(2,1)} %add_convert_fusion.1), calls=%async_computation.4 | async-start | bytes 3801088 | tf_op jit(solution)/shard_map/all_to_all | solution.py:729
  541.7 3.3 collective-permute-start.49
  542.1 3.1 collective-permute-start.51
  554.9 30.3 %collective-permute-start.56 = (bf16[16,320,128]{2,1,0:T(8,128)(2,1)}, bf16[16,320,128]{2,1,0:T(8,128)(2,1)}, u32[]{:S(2)}, u32[]{:S(2)}) collective-permute-start(bf16[16,320,128]{2,1,0:T(8,128)(2,1)} %get-tuple-element.138), channel_id=1, source_target_pairs={{0,1},{1,0},{2,3},{3,2},{4,5},{5,4},{6,7},{7,6},{8,9},{9,8},{10,11... | collective-permute-start | bytes 3932168 | tf_op jit(solution)/shard_map/ppermute | solution.py:679
  582.7 26.3 %collective-permute-start.52 = (bf16[448,2048]{1,0:T(8,128)(2,1)}, bf16[448,2048]{1,0:T(8,128)(2,1)}, u32[]{:S(2)}, u32[]{:S(2)}) collective-permute-start(bf16[448,2048]{1,0:T(8,128)(2,1)} %get-tuple-element.129), channel_id=1, source_target_pairs={{0,2},{2,0},{4,6},{6,4},{8,10},{10,8},{12,14},{14,12},{16,18},{18,... | collective-permute-start | bytes 5505032 | tf_op jit(solution)/shard_map/ppermute | solution.py:676
  588.0 48.7 %all-to-all-start.5 = ((bf16[16,320,128]{2,1,0:T(8,128)(2,1)}), bf16[16,320,128]{2,1,0:T(8,128)(2,1)S(1)}, u32[]{:S(2)}, u32[]{:S(2)}) async-start(bf16[16,320,128]{2,1,0:T(8,128)(2,1)} %add_convert_fusion.2), calls=%async_computation.5 | async-start | bytes 2621440 | tf_op jit(solution)/shard_map/all_to_all | solution.py:729
  607.8 18.7 %collective-permute-start.54 = (bf16[1,64,2048]{2,1,0:T(8,128)(2,1)S(1)}, bf16[1,64,2048]{2,1,0:T(8,128)(2,1)S(1)}, u32[]{:S(2)}, u32[]{:S(2)}) collective-permute-start(bf16[1,64,2048]{2,1,0:T(8,128)(2,1)S(1)} %fusion.16), channel_id=1, source_target_pairs={{0,8},{2,6},{8,16},{10,2},{16,24},{18,10},{24,28},{26,18},{28,20},... | collective-permute-start | bytes 786440 | tf_op jit(solution)/shard_map/ppermute | solution.py:673
  627.9 8.7 %collective-permute-start.55 = (bf16[1,128,2048]{2,1,0:T(8,128)(2,1)S(1)}, bf16[1,128,2048]{2,1,0:T(8,128)(2,1)}, u32[]{:S(2)}, u32[]{:S(2)}) collective-permute-start(bf16[1,128,2048]{2,1,0:T(8,128)(2,1)S(1)} %fusion.8), channel_id=1, source_target_pairs={{0,8},{2,6},{8,16},{10,2},{16,24},{18,10},{24,28},{26,18},{28,20},... | collective-permute-start | bytes 1572872 | tf_op jit(solution)/shard_map/ppermute | solution.py:673
  630.2 42.7 %collective-permute-start.63 = (bf16[16,464,128]{2,1,0:T(8,128)(2,1)}, bf16[16,464,128]{2,1,0:T(8,128)(2,1)}, u32[]{:S(2)}, u32[]{:S(2)}) collective-permute-start(bf16[16,464,128]{2,1,0:T(8,128)(2,1)} %get-tuple-element.147), channel_id=1, source_target_pairs={{0,1},{1,0},{2,3},{3,2},{4,5},{5,4},{6,7},{7,6},{8,9},{9,8},{10,11... | collective-permute-start | bytes 5701640 | tf_op jit(solution)/shard_map/ppermute | solution.py:679
  638.7 8.5 %collective-permute-start.57 = (bf16[1,128,2048]{2,1,0:T(8,128)(2,1)S(1)}, bf16[1,128,2048]{2,1,0:T(8,128)(2,1)S(1)}, u32[]{:S(2)}, u32[]{:S(2)}) collective-permute-start(bf16[1,128,2048]{2,1,0:T(8,128)(2,1)S(1)} %fusion.4), channel_id=1, source_target_pairs={{0,8},{2,6},{8,16},{10,2},{16,24},{18,10},{24,28},{26,18},{28,20},... | collective-permute-start | bytes 1572872 | tf_op jit(solution)/shard_map/ppermute | solution.py:673
  648.4 27.8 %collective-permute-start.58 = (bf16[1,128,2048]{2,1,0:T(8,128)(2,1)S(1)}, bf16[1,128,2048]{2,1,0:T(8,128)(2,1)}, u32[]{:S(2)}, u32[]{:S(2)}) collective-permute-start(bf16[1,128,2048]{2,1,0:T(8,128)(2,1)S(1)} %fusion.3), channel_id=1, source_target_pairs={{0,8},{2,6},{8,16},{10,2},{16,24},{18,10},{24,28},{26,18},{28,20},... | collective-permute-start | bytes 1572872 | tf_op jit(solution)/shard_map/ppermute | solution.py:673
  676.2 48.6 %all-to-all-start.6 = ((bf16[16,464,128]{2,1,0:T(8,128)(2,1)}), bf16[16,464,128]{2,1,0:T(8,128)(2,1)S(1)}, u32[]{:S(2)}, u32[]{:S(2)}) async-start(bf16[16,464,128]{2,1,0:T(8,128)(2,1)} %add_convert_fusion), calls=%async_computation.6 | async-start | bytes 3801088 | tf_op jit(solution)/shard_map/all_to_all | solution.py:729
  682.8 9.1 %collective-permute-start.59 = (bf16[1,64,2048]{2,1,0:T(8,128)(2,1)S(1)}, bf16[1,64,2048]{2,1,0:T(8,128)(2,1)S(1)}, u32[]{:S(2)}, u32[]{:S(2)}) collective-permute-start(bf16[1,64,2048]{2,1,0:T(8,128)(2,1)S(1)} %constant_dynamic-slice_fusion.5), channel_id=1, source_target_pairs={{0,2},{2,0},{4,6},{6,4},{8,10},{10,8},{12,14},{14,12},{16,18},{18,... | collective-permute-start | bytes 786440 | tf_op jit(solution)/shard_map/ppermute | solution.py:676
  683.3 8.5 %collective-permute-start.60 = (f32[2,448]{1,0:T(2,128)S(1)}, f32[2,448]{1,0:T(2,128)S(1)}, u32[]{:S(2)}, u32[]{:S(2)}) collective-permute-start(f32[2,448]{1,0:T(2,128)S(1)} %pad_maximum_fusion.3), channel_id=1, source_target_pairs={{0,1},{1,0},{2,3},{3,2},{4,5},{5,4},{6,7},{7,6},{8,9},{9,8},{10,11... | collective-permute-start | bytes 10760 | tf_op jit(solution)/shard_map/ppermute | solution.py:679
  698.5 13.2 %collective-permute-start.62 = (bf16[128,2048]{1,0:T(8,128)(2,1)S(1)}, bf16[128,2048]{1,0:T(8,128)(2,1)S(1)}, u32[]{:S(2)}, u32[]{:S(2)}) collective-permute-start(bf16[128,2048]{1,0:T(8,128)(2,1)S(1)} %maximum_select_fusion.3), channel_id=1, source_target_pairs={{0,1},{1,0},{2,3},{3,2},{4,5},{5,4},{6,7},{7,6},{8,9},{9,8},{10,11... | collective-permute-start | bytes 1572872 | tf_op jit(solution)/shard_map/ppermute | solution.py:679
  (62 other events, 872.0 us)

commit v11 on v10

--- a/solution.py
+++ b/solution.py
@@ -933,7 +933,7 @@
     down_first = summed(down_pair[0], after(down_sent, slim), up_last)
     *up_pair, bias_first = up_gradients(slim, after(normed, up_last), sums)
     up_sent = over(up_pair[1])
-    (grad_end,) = ring_sum((after(parts[0], up_pair[0]), parts[1], parts[2]), needed={1: (down_first,)})
+    (grad_end,) = ring_sum((after(parts[0], up_pair[0]), parts[1], parts[2]), needed={1: (down_first,), 0: (up_sent,)})
     up_first = summed(up_pair[0], up_sent, down_first, grad_end[2])
     sums = jnp.concatenate([bias_first, bias_last], axis=0)
     sums_qkv = sums[:, : 3 * WIDE].reshape(LAYERS, 3, 2, HEAD_DIM)

time: 745 us -> 732 us (0.983)
  waiting for transfers between devices: 363 us -> 349 us
    ppermute x12, waiting for transfers between devices: 97.6 us -> 86.7 us  [over(): return lax.ppermute(x, 'tensor', [(0, 1), (1, 0)])]
  transfers between devices with their start and end apart: 71 -> 71, of which waited for: 45 -> 45; matrix products, arithmetic and copies ran while one was open for 8% -> 8% of each run, Pallas kernels for 18% -> 19%
where the time goes in v11:
time: 732 us; the launch traced here: 721 us
  waiting for transfers between devices  349 us (48%)
  Pallas kernels  182 us (25%)
  starting transfers between devices  109 us (15%)
  other arithmetic  54.1 us (7%)
  local copies, waits for them, and re-layouts  24.8 us (3%)
    ppermute x24, waiting for transfers between devices, along(): return lax.ppermute(x, 'dp', ring_pairs)  148 us
    all_to_all x7, waiting for transfers between devices, spread(): return lax.all_to_all(x, 'dp', 0, 0, axis_index_groups=inner, tiled=True)  99.5 us
    pallas_call x3, Pallas kernels, call_pass(): pl.pallas_call(partial(layer_pass, mode), in_specs=[SMEM_SPEC] + [VMEM_SP...  91.8 us
    ppermute x12, waiting for transfers between devices, over(): return lax.ppermute(x, 'tensor', [(0, 1), (1, 0)])  86.7 us
    all_to_all x7, starting transfers between devices, spread(): return lax.all_to_all(x, 'dp', 0, 0, axis_index_groups=inner, tiled=True)  52.1 us
    pallas_call x4, Pallas kernels, call_gradients(): pl.pallas_call(partial(gradient_slabs, own_rows, other_rows, with_sums, l...  38.1 us
    ppermute x24, starting transfers between devices, along(): return lax.ppermute(x, 'dp', ring_pairs)  22.3 us
    ppermute x28, starting transfers between devices, across(): return lax.ppermute(x, 'dp', core_pairs)  20.6 us
  transfers between devices with their start and end apart: 71, of which 45 were waited for; matrix products, arithmetic and copies ran while one was open for 8% of the time, Pallas kernels for 19%

profile of v11, /device:TPU:13, one launch (start us, length us, event | category | flops | bytes accessed | tf_op | source)
XLA Modules:
  0.0 720.7 jit_solution(8085867189178269006)
XLA Ops:
  4.8 4.0 pack_first.1
  8.8 6.5 all-to-all-start
  15.3 3.5 pack_down.1
  18.9 39.7 %all-to-all-done.own_ref = bf16[16,464,128]{2,1,0:T(8,128)(2,1)S(1)} async-done(((bf16[16,464,128]{2,1,0:T(8,128)(2,1)}), bf16[16,464,128]{2,1,0:T(8,128)(2,1)S(1)}, u32[]{:S(2)}, u32[]{:S(2)}) %all-to-all-start) | async-done | bytes 1900576 | tf_op jit(solution)/shard_map/all_to_all | solution.py:729
  58.5 4.8 all-to-all-start.1
  69.3 4.4 pack_both.1
  73.8 2.7 select_multiply_fusion.refs_10_.refs_17_
  76.4 17.9 %all-to-all-done.1.own_ref = bf16[16,320,128]{2,1,0:T(8,128)(2,1)S(1)} async-done(((bf16[16,320,128]{2,1,0:T(8,128)(2,1)}), bf16[16,320,128]{2,1,0:T(8,128)(2,1)S(1)}, u32[]{:S(2)}, u32[]{:S(2)}) %all-to-all-start.1) | async-done | bytes 1310752 | tf_op jit(solution)/shard_map/all_to_all | solution.py:729
  98.1 2.7 concatenate.76.refs_3_
  100.8 10.1 %collective-permute-done.2.other_ref = bf16[16,464,128]{2,1,0:T(8,128)(2,1)} collective-permute-done((bf16[16,464,128]{2,1,0:T(8,128)(2,1)S(1)}, bf16[16,464,128]{2,1,0:T(8,128)(2,1)}, u32[]{:S(2)}, u32[]{:S(2)}) %collective-permute-start.2) | collective-permute-done | bytes 1900576 | tf_op jit(solution)/shard_map/ppermute | solution.py:679
  118.0 7.1 collective-permute-done.3.refs_12_.refs_19_
  126.3 4.8 join_up.1.refs_1_
  131.1 8.2 %collective-permute-done.4.refs_13_.refs_20_ = bf16[2,128,2048]{2,1,0:T(8,128)(2,1)S(1)} collective-permute-done((bf16[2,128,2048]{2,1,0:T(8,128)(2,1)}, bf16[2,128,2048]{2,1,0:T(8,128)(2,1)S(1)}, u32[]{:S(2)}, u32[]{:S(2)}) %collective-permute-start.4) | collective-permute-done | bytes 1048608 | tf_op jit(solution)/shard_map/ppermute | solution.py:673
  139.3 2.9 collective-permute-done.5.other_ref
  143.4 7.1 collective-permute-done.6.refs_17_.refs_24_
  151.4 6.8 all-to-all-start.2
  164.6 4.2 join_down.1.refs_2_
  168.8 29.3 %pass_first.1 = (bf16[1024,2048]{1,0:T(8,128)(2,1)}, bf16[1024,384]{1,0:T(8,128)(2,1)}, f32[1024,512]{1,0:T(8,128)}, bf16[1024,640]{1,0:T(8,128)(2,1)}, bf16[64,...) custom-call(s32[1]{0:T(128)} %bitcast.refs_0_.core_ref, bf16[2048,896]{1,0:T(8,128)(2,1)} %join_up.1.refs_1_, ...), custom_call_target="tpu_custom_call" | custom-call | flops 19327352832 | bytes 20000000 | tf_op jit(solution)/shard_map/pass_first/pallas_call | solution.py:443
  198.2 29.8 %all-to-all-done.2.own_ref = bf16[16,768,128]{2,1,0:T(8,128)(2,1)S(1)} async-done(((bf16[16,768,128]{2,1,0:T(8,128)(2,1)}), bf16[16,768,128]{2,1,0:T(8,128)(2,1)S(1)}, u32[]{:S(2)}, u32[]{:S(2)}) %all-to-all-start.2) | async-done | bytes 3145760 | tf_op jit(solution)/shard_map/all_to_all | solution.py:729
  233.7 2.8 collective-permute-done.16
  238.0 8.3 %collective-permute-done.17 = bf16[1,128,2048]{2,1,0:T(8,128)(2,1)S(1)} collective-permute-done((bf16[1,128,2048]{2,1,0:T(8,128)(2,1)S(1)}, bf16[1,128,2048]{2,1,0:T(8,128)(2,1)S(1)}, u32[]{:S(2)}, u32[]{:S(2)}) %collective-permute-start.17) | collective-permute-done | bytes 524320 | tf_op jit(solution)/shard_map/ppermute | solution.py:673
  247.6 20.7 %collective-permute-done.7.lower_ref = bf16[8,768,128]{2,1,0:T(8,128)(2,1)S(1)} collective-permute-done((bf16[8,768,128]{2,1,0:T(8,128)(2,1)S(1)}, bf16[8,768,128]{2,1,0:T(8,128)(2,1)S(1)}, u32[]{:S(2)}, u32[]{:S(2)}) %collective-permute-start.7) | collective-permute-done | bytes 1572896 | tf_op jit(solution)/shard_map/ppermute | solution.py:679
  273.1 6.4 collective-permute-done.19.moving_ref
  290.8 17.3 %collective-permute-done.8.upper_ref = bf16[8,768,128]{2,1,0:T(8,128)(2,1)} collective-permute-done((bf16[8,768,128]{2,1,0:T(8,128)(2,1)}, bf16[8,768,128]{2,1,0:T(8,128)(2,1)}, u32[]{:S(2)}, u32[]{:S(2)}) %collective-permute-start.8) | collective-permute-done | bytes 1572896 | tf_op jit(solution)/shard_map/ppermute | solution.py:679
  308.2 8.3 %collective-permute-done.23.refs_10_ = bf16[128,2048]{1,0:T(8,128)(2,1)S(1)} collective-permute-done((bf16[128,2048]{1,0:T(8,128)(2,1)S(1)}, bf16[128,2048]{1,0:T(8,128)(2,1)S(1)}, u32[]{:S(2)}, u32[]{:S(2)}) %collective-permute-start.23) | collective-permute-done | bytes 524320 | tf_op jit(solution)/shard_map/ppermute | solution.py:673
  318.2 6.6 collective-permute-done.24.refs_11_
  327.5 2.6 collective-permute-done.28.refs_15_
  330.1 3.7 collective-permute-start.29
  333.8 6.3 join_halves.1
  341.2 36.0 %pass_middle.1 = (bf16[1024,2048]{1,0:T(8,128)(2,1)}, bf16[1024,2048]{1,0:T(8,128)(2,1)}, bf16[1024,640]{1,0:T(8,128)(2,1)}, bf16[1024,896]{1,0:T(8,128)(2,1)}, ...) custom-call(s32[1]{0:T(128)} %bitcast.refs_0_.core_ref, ...), custom_call_target="tpu_custom_call" | custom-call | flops 38654705664 | bytes 40000000 | tf_op jit(solution)/shard_map/pass_middle/pallas_call | solution.py:443
  378.3 3.3 collective-permute-done.31
  389.8 4.4 collective-permute-done.33
  395.8 8.9 %down_gradients.2 = (bf16[16,320,128]{2,1,0:T(8,128)(2,1)}, bf16[16,320,128]{2,1,0:T(8,128)(2,1)}) custom-call(s32[1]{0:T(128)} %bitcast.refs_0_.core_ref, bf16[1024,640]{1,0:T(8,128)(2,1)} %get-tuple-element.106.left_ref, bf16[1024,2048]{1,0:T(8,128)(2,1)} %get-tuple-element.107.rest_0_), custom_call_target="tpu_custom_call" | custom-call | flops 5368709120 | bytes 10747904 | tf_op jit(solution)/shard_map/down_gradients/pallas_call | solution.py:505
  404.8 5.0 collective-permute-done.35
  412.8 10.2 %up_gradients.2 = (bf16[16,464,128]{2,1,0:T(8,128)(2,1)}, bf16[16,464,128]{2,1,0:T(8,128)(2,1)}, f32[1,896]{1,0:T(1,128)}) custom-call(s32[1]{0:T(128)} %bitcast.refs_0_.core_ref, bf16[1024,896]{1,0:T(8,128)(2,1)} %get-tuple-element.110.left_ref, bf16[1024,2048]{1,0:T(8,128)(2,1)} %get-tuple-element.111.rest_0_, f32[16,2048]{1,0:T(8,128)} %get-tuple-element.112.rest_1_), custom_call_target="tpu_custom_call" | custom-call | flops 7516192768 | bytes 13369344 | tf_op jit(solution)/shard_map/up_gradients/pallas_call | solution.py:505
  422.9 3.6 collective-permute-done.36
  428.5 12.5 %collective-permute-done.37.moving_ref = bf16[2,128,2048]{2,1,0:T(8,128)(2,1)S(1)} collective-permute-done((bf16[2,128,2048]{2,1,0:T(8,128)(2,1)S(1)}, bf16[2,128,2048]{2,1,0:T(8,128)(2,1)S(1)}, u32[]{:S(2)}, u32[]{:S(2)}) %collective-permute-start.37) | collective-permute-done | bytes 1048608 | tf_op jit(solution)/shard_map/ppermute | solution.py:673
  441.0 3.5 collective-permute-start.38
  446.9 3.0 backward_end.2
  450.3 5.2 collective-permute-done.42
  455.5 2.7 add_convert_fusion.3
  458.2 12.1 %all-to-all-start.3 = ((bf16[16,320,128]{2,1,0:T(8,128)(2,1)}), bf16[16,320,128]{2,1,0:T(8,128)(2,1)S(1)}, u32[]{:S(2)}, u32[]{:S(2)}) async-start(bf16[16,320,128]{2,1,0:T(8,128)(2,1)} %add_convert_fusion.3), calls=%async_computation.3 | async-start | bytes 2621440 | tf_op jit(solution)/shard_map/all_to_all | solution.py:729
  474.8 30.2 %collective-permute-done.43.rest_1_.refs_11_ = bf16[128,2048]{1,0:T(8,128)(2,1)} collective-permute-done((bf16[128,2048]{1,0:T(8,128)(2,1)}, bf16[128,2048]{1,0:T(8,128)(2,1)}, u32[]{:S(2)}, u32[]{:S(2)}) %collective-permute-start.43) | collective-permute-done | bytes 524320 | tf_op jit(solution)/shard_map/ppermute | solution.py:673
  509.3 4.2 collective-permute-done.44.rest_2_.refs_12_
  515.4 5.7 collective-permute-done.40
  525.3 3.8 collective-permute-done.50.rest_7_.refs_17_
  529.1 3.3 add_convert_fusion.1
  532.4 8.8 %all-to-all-start.4 = ((bf16[16,464,128]{2,1,0:T(8,128)(2,1)}), bf16[16,464,128]{2,1,0:T(8,128)(2,1)S(1)}, u32[]{:S(2)}, u32[]{:S(2)}) async-start(bf16[16,464,128]{2,1,0:T(8,128)(2,1)} %add_convert_fusion.1), calls=%async_computation.4 | async-start | bytes 3801088 | tf_op jit(solution)/shard_map/all_to_all | solution.py:729
  546.0 8.9 %down_gradients.3 = (bf16[16,320,128]{2,1,0:T(8,128)(2,1)}, bf16[16,320,128]{2,1,0:T(8,128)(2,1)}) custom-call(s32[1]{0:T(128)} %bitcast.refs_0_.core_ref, bf16[1024,640]{1,0:T(8,128)(2,1)} %get-tuple-element.118.left_ref, bf16[128,2048]{1,0:T(8,128)(2,1)} %maximum_select_fusion.2.rest_0_.refs_10_, ...), custom_call_target="tpu_custom_call" | custom-call | flops 5368709120 | bytes 10747904 | tf_op jit(solution)/shard_map/down_gradients/pallas_call | solution.py:505
  556.1 26.5 %pass_last.1 = (bf16[1024,2048]{1,0:T(8,128)(2,1)}, bf16[1024,896]{1,0:T(8,128)(2,1)}, f32[16,2048]{1,0:T(8,128)}, bf16[64,2048]{1,0:T(8,128)(2,1)}, bf16[448,20...) custom-call(s32[1]{0:T(128)} %bitcast.refs_0_.core_ref, bf16[2048,896]{1,0:T(8,128)(2,1)} %join_up.1.refs_1_, ...), custom_call_target="tpu_custom_call" | custom-call | flops 19327352832 | bytes 20000000 | tf_op jit(solution)/shard_map/pass_last/pallas_call | solution.py:443
  585.2 2.7 add_convert_fusion.2
  588.0 6.8 all-to-all-start.5
  594.8 10.1 %up_gradients.3 = (bf16[16,464,128]{2,1,0:T(8,128)(2,1)}, bf16[16,464,128]{2,1,0:T(8,128)(2,1)}, f32[1,896]{1,0:T(1,128)}) custom-call(s32[1]{0:T(128)} %bitcast.refs_0_.core_ref, bf16[1024,896]{1,0:T(8,128)(2,1)} %get-tuple-element.132.left_ref, bf16[1024,2048]{1,0:T(8,128)(2,1)} %get-tuple-element.135.refs_9_.rest_0_, f32[16,2048]{1,0:T(8,128)} %get-tuple-element.136.rest_1_), custom_call_target="tpu_custom_call" | custom-call | flops 7516192768 | bytes 13369344 | tf_op jit(solution)/shard_map/up_gradients/pallas_call | solution.py:505
  610.2 16.3 %collective-permute-done.54 = bf16[1,64,2048]{2,1,0:T(8,128)(2,1)S(1)} collective-permute-done((bf16[1,64,2048]{2,1,0:T(8,128)(2,1)S(1)}, bf16[1,64,2048]{2,1,0:T(8,128)(2,1)S(1)}, u32[]{:S(2)}, u32[]{:S(2)}) %collective-permute-start.54) | collective-permute-done | bytes 262176 | tf_op jit(solution)/shard_map/ppermute | solution.py:673
  630.6 6.1 collective-permute-done.55
  641.0 11.5 %collective-permute-done.58 = bf16[16,464,128]{2,1,0:T(8,128)(2,1)} collective-permute-done((bf16[16,464,128]{2,1,0:T(8,128)(2,1)}, bf16[16,464,128]{2,1,0:T(8,128)(2,1)}, u32[]{:S(2)}, u32[]{:S(2)}) %collective-permute-start.58) | collective-permute-done | bytes 1900576 | tf_op jit(solution)/shard_map/ppermute | solution.py:679
  655.1 3.3 add_convert_fusion
  658.4 3.9 collective-permute-done.59.moving_ref
  662.3 6.2 all-to-all-start.6
  671.5 7.3 %spread_gradients.2 = (f32[2,3,128,1024]{3,2,1,0:T(8,128)}, f32[2,1024,128]{2,1,0:T(8,128)}, f32[2,128,4096]{2,1,0:T(8,128)}, f32[2,4096,128]{2,1,0:T(8,128)}, f32[8,128]{1,0:T(8,128)}) custom-call(bf16[16,464,128]{2,1,0:T(8,128)(2,1)} %copy-done.2, bf16[16,320,128]{2,1,0:T(8,128)(2,1)} %copy-done.12), custom_call_target="tpu_custom_call" | custom-call | tf_op jit(solution)/shard_map/spread_gradients/pallas_call | solution.py:545
  679.5 2.9 backward_end.3
  688.7 9.9 %collective-permute-done.63 = bf16[128,2048]{1,0:T(8,128)(2,1)S(1)} collective-permute-done((bf16[128,2048]{1,0:T(8,128)(2,1)S(1)}, bf16[128,2048]{1,0:T(8,128)(2,1)S(1)}, u32[]{:S(2)}, u32[]{:S(2)}) %collective-permute-start.63) | collective-permute-done | bytes 524320 | tf_op jit(solution)/shard_map/ppermute | solution.py:679
  699.6 12.1 %all-to-all-done.6.up_ref = bf16[16,464,128]{2,1,0:T(8,128)(2,1)S(1)} async-done(((bf16[16,464,128]{2,1,0:T(8,128)(2,1)}), bf16[16,464,128]{2,1,0:T(8,128)(2,1)S(1)}, u32[]{:S(2)}, u32[]{:S(2)}) %all-to-all-start.6) | async-done | bytes 1900576 | tf_op jit(solution)/shard_map/all_to_all | solution.py:729
  713.0 7.3 %spread_gradients.3 = (f32[2,3,128,1024]{3,2,1,0:T(8,128)}, f32[2,1024,128]{2,1,0:T(8,128)}, f32[2,128,4096]{2,1,0:T(8,128)}, f32[2,4096,128]{2,1,0:T(8,128)}, f32[8,128]{1,0:T(8,128)}) custom-call(bf16[16,464,128]{2,1,0:T(8,128)(2,1)} %copy-done.3, ...), custom_call_target="tpu_custom_call", output_to_operand_aliasing={{0}: (2, {}), {1}: (3, {}), {2}: (4, {}), {3}: (5, {})} | custom-call | tf_op jit(solution)/shard_map/spread_gradients/pallas_call | solution.py:545
  (315 shorter events, 130.8 us)
Async XLA Ops:
  8.8 49.7 %all-to-all-start = ((bf16[16,464,128]{2,1,0:T(8,128)(2,1)}), bf16[16,464,128]{2,1,0:T(8,128)(2,1)S(1)}, u32[]{:S(2)}, u32[]{:S(2)}) async-start(bf16[16,464,128]{2,1,0:T(8,128)(2,1)} %pack_first.1), calls=%async_computation | async-start | bytes 3801088 | tf_op jit(solution)/shard_map/all_to_all | solution.py:729
  58.5 35.7 %all-to-all-start.1 = ((bf16[16,320,128]{2,1,0:T(8,128)(2,1)}), bf16[16,320,128]{2,1,0:T(8,128)(2,1)S(1)}, u32[]{:S(2)}, u32[]{:S(2)}) async-start(bf16[16,320,128]{2,1,0:T(8,128)(2,1)} %pack_down.1), calls=%async_computation.1 | async-start | bytes 2621440 | tf_op jit(solution)/shard_map/all_to_all | solution.py:729
  65.6 8.2 %collective-permute-start = (bf16[2,128,2048]{2,1,0:T(8,128)(2,1)}, bf16[2,128,2048]{2,1,0:T(8,128)(2,1)}, u32[]{:S(2)}, u32[]{:S(2)}) collective-permute-start(bf16[2,128,2048]{2,1,0:T(8,128)(2,1)} %pad_maximum_fusion), channel_id=1, source_target_pairs={{0,2},{2,0},{4,6},{6,4},{8,10},{10,8},{12,14},{14,12},{16,18},{18,... | collective-permute-start | bytes 3145736 | tf_op jit(solution)/shard_map/ppermute | solution.py:676
  67.9 43.0 %collective-permute-start.2 = (bf16[16,464,128]{2,1,0:T(8,128)(2,1)S(1)}, bf16[16,464,128]{2,1,0:T(8,128)(2,1)}, u32[]{:S(2)}, u32[]{:S(2)}) collective-permute-start(bf16[16,464,128]{2,1,0:T(8,128)(2,1)S(1)} %all-to-all-done.own_ref), channel_id=1, source_target_pairs={{0,1},{1,0},{2,3},{3,2},{4,5},{5,4},{6,7},{7,6},{8,9},{9,8},{10,11... | collective-permute-start | bytes 5701640 | tf_op jit(solution)/shard_map/ppermute | solution.py:679
  94.3 16.6 %collective-permute-start.1 = (bf16[2,128,2048]{2,1,0:T(8,128)(2,1)}, bf16[2,128,2048]{2,1,0:T(8,128)(2,1)}, u32[]{:S(2)}, u32[]{:S(2)}) collective-permute-start(bf16[2,128,2048]{2,1,0:T(8,128)(2,1)} %select_multiply_fusion.refs_10_.refs_17_), channel_id=1, source_target_pairs={{0,8},{2,6},{8,16},{10,2},{16,24},{18,10},{24,28},{26,18},{28,20},... | collective-permute-start | bytes 3145736 | tf_op jit(solution)/shard_map/ppermute | solution.py:673
  110.9 14.3 %collective-permute-start.3 = (bf16[2,128,2048]{2,1,0:T(8,128)(2,1)}, bf16[2,128,2048]{2,1,0:T(8,128)(2,1)}, u32[]{:S(2)}, u32[]{:S(2)}) collective-permute-start(bf16[2,128,2048]{2,1,0:T(8,128)(2,1)} %collective-permute-done.1.refs_11_.refs_18_), channel_id=1, source_target_pairs={{0,8},{2,6},{8,16},{10,2},{16,24},{18,10},{24,28},{26,18},{28,20},... | collective-permute-start | bytes 3145736 | tf_op jit(solution)/shard_map/ppermute | solution.py:673
  112.0 30.2 %collective-permute-start.5 = (bf16[16,320,128]{2,1,0:T(8,128)(2,1)}, bf16[16,320,128]{2,1,0:T(8,128)(2,1)S(1)}, u32[]{:S(2)}, u32[]{:S(2)}) collective-permute-start(bf16[16,320,128]{2,1,0:T(8,128)(2,1)} %copy-done.11), channel_id=1, source_target_pairs={{0,1},{1,0},{2,3},{3,2},{4,5},{5,4},{6,7},{7,6},{8,9},{9,8},{10,11... | collective-permute-start | bytes 3932168 | tf_op jit(solution)/shard_map/ppermute | solution.py:679
  125.1 14.2 %collective-permute-start.4 = (bf16[2,128,2048]{2,1,0:T(8,128)(2,1)}, bf16[2,128,2048]{2,1,0:T(8,128)(2,1)S(1)}, u32[]{:S(2)}, u32[]{:S(2)}) collective-permute-start(bf16[2,128,2048]{2,1,0:T(8,128)(2,1)} %collective-permute-done.3.refs_12_.refs_19_), channel_id=1, source_target_pairs={{0,8},{2,6},{8,16},{10,2},{16,24},{18,10},{24,28},{26,18},{28,20},... | collective-permute-start | bytes 3145736 | tf_op jit(solution)/shard_map/ppermute | solution.py:673
  142.2 8.3 %collective-permute-start.6 = (bf16[2,64,2048]{2,1,0:T(8,128)(2,1)S(1)}, bf16[2,64,2048]{2,1,0:T(8,128)(2,1)S(1)}, u32[]{:S(2)}, u32[]{:S(2)}) collective-permute-start(bf16[2,64,2048]{2,1,0:T(8,128)(2,1)S(1)} %constant_dynamic-slice_fusion.4), channel_id=1, source_target_pairs={{0,8},{2,6},{8,16},{10,2},{16,24},{18,10},{24,28},{26,18},{28,20},... | collective-permute-start | bytes 1572872 | tf_op jit(solution)/shard_map/ppermute | solution.py:673
  151.4 76.7 %all-to-all-start.2 = ((bf16[16,768,128]{2,1,0:T(8,128)(2,1)}), bf16[16,768,128]{2,1,0:T(8,128)(2,1)S(1)}, u32[]{:S(2)}, u32[]{:S(2)}) async-start(bf16[16,768,128]{2,1,0:T(8,128)(2,1)} %pack_both.1), calls=%async_computation.2 | async-start | bytes 6291456 | tf_op jit(solution)/shard_map/all_to_all | solution.py:729
  158.3 10.5 %collective-permute-start.10 = (bf16[2,128,2048]{2,1,0:T(8,128)(2,1)}, bf16[2,128,2048]{2,1,0:T(8,128)(2,1)}, u32[]{:S(2)}, u32[]{:S(2)}) collective-permute-start(bf16[2,128,2048]{2,1,0:T(8,128)(2,1)} %collective-permute-done.1.refs_11_.refs_18_), channel_id=1, source_target_pairs={{0,2},{2,0},{4,6},{6,4},{8,10},{10,8},{12,14},{14,12},{16,18},{18,... | collective-permute-start | bytes 3145736 | tf_op jit(solution)/shard_map/ppermute | solution.py:676
  158.6 10.2 %collective-permute-start.11 = (bf16[2,128,2048]{2,1,0:T(8,128)(2,1)}, bf16[2,128,2048]{2,1,0:T(8,128)(2,1)}, u32[]{:S(2)}, u32[]{:S(2)}) collective-permute-start(bf16[2,128,2048]{2,1,0:T(8,128)(2,1)} %collective-permute-done.3.refs_12_.refs_19_), channel_id=1, source_target_pairs={{0,2},{2,0},{4,6},{6,4},{8,10},{10,8},{12,14},{14,12},{16,18},{18,... | collective-permute-start | bytes 3145736 | tf_op jit(solution)/shard_map/ppermute | solution.py:676
  158.8 10.0 %collective-permute-start.12 = (bf16[2,128,2048]{2,1,0:T(8,128)(2,1)}, bf16[2,128,2048]{2,1,0:T(8,128)(2,1)}, u32[]{:S(2)}, u32[]{:S(2)}) collective-permute-start(bf16[2,128,2048]{2,1,0:T(8,128)(2,1)} %copy-done.29), channel_id=1, source_target_pairs={{0,2},{2,0},{4,6},{6,4},{8,10},{10,8},{12,14},{14,12},{16,18},{18,... | collective-permute-start | bytes 3145736 | tf_op jit(solution)/shard_map/ppermute | solution.py:676
  162.9 6.0 collective-permute-start.13
  198.1 35.6 %collective-permute-start.14 = (bf16[448,2048]{1,0:T(8,128)(2,1)}, bf16[448,2048]{1,0:T(8,128)(2,1)}, u32[]{:S(2)}, u32[]{:S(2)}) collective-permute-start(bf16[448,2048]{1,0:T(8,128)(2,1)} %get-tuple-element.94), channel_id=1, source_target_pairs={{0,2},{2,0},{4,6},{6,4},{8,10},{10,8},{12,14},{14,12},{16,18},{18,... | collective-permute-start | bytes 5505032 | tf_op jit(solution)/shard_map/ppermute | solution.py:676
  230.8 5.7 collective-permute-start.16
  232.5 35.8 %collective-permute-start.7 = (bf16[8,768,128]{2,1,0:T(8,128)(2,1)S(1)}, bf16[8,768,128]{2,1,0:T(8,128)(2,1)S(1)}, u32[]{:S(2)}, u32[]{:S(2)}) collective-permute-start(bf16[8,768,128]{2,1,0:T(8,128)(2,1)S(1)} %get-tuple-element.225), channel_id=1, source_target_pairs={{0,1},{1,0},{2,3},{3,2},{4,5},{5,4},{6,7},{7,6},{8,9},{9,8},{10,11... | collective-permute-start | bytes 4718600 | tf_op jit(solution)/shard_map/ppermute | solution.py:679
  237.9 8.4 %collective-permute-start.17 = (bf16[1,128,2048]{2,1,0:T(8,128)(2,1)S(1)}, bf16[1,128,2048]{2,1,0:T(8,128)(2,1)S(1)}, u32[]{:S(2)}, u32[]{:S(2)}) collective-permute-start(bf16[1,128,2048]{2,1,0:T(8,128)(2,1)S(1)} %fusion.7), channel_id=1, source_target_pairs={{0,8},{2,6},{8,16},{10,2},{16,24},{18,10},{24,28},{26,18},{28,20},... | collective-permute-start | bytes 1572872 | tf_op jit(solution)/shard_map/ppermute | solution.py:673
  247.6 20.8 %collective-permute-start.18 = (bf16[1,128,2048]{2,1,0:T(8,128)(2,1)S(1)}, bf16[1,128,2048]{2,1,0:T(8,128)(2,1)S(1)}, u32[]{:S(2)}, u32[]{:S(2)}) collective-permute-start(bf16[1,128,2048]{2,1,0:T(8,128)(2,1)S(1)} %fusion.6), channel_id=1, source_target_pairs={{0,8},{2,6},{8,16},{10,2},{16,24},{18,10},{24,28},{26,18},{28,20},... | collective-permute-start | bytes 1572872 | tf_op jit(solution)/shard_map/ppermute | solution.py:673
  270.8 8.6 %collective-permute-start.19 = (bf16[1,128,2048]{2,1,0:T(8,128)(2,1)}, bf16[1,128,2048]{2,1,0:T(8,128)(2,1)S(1)}, u32[]{:S(2)}, u32[]{:S(2)}) collective-permute-start(bf16[1,128,2048]{2,1,0:T(8,128)(2,1)} %fusion.5), channel_id=1, source_target_pairs={{0,8},{2,6},{8,16},{10,2},{16,24},{18,10},{24,28},{26,18},{28,20},... | collective-permute-start | bytes 1572872 | tf_op jit(solution)/shard_map/ppermute | solution.py:673
  271.8 36.3 %collective-permute-start.8 = (bf16[8,768,128]{2,1,0:T(8,128)(2,1)}, bf16[8,768,128]{2,1,0:T(8,128)(2,1)}, u32[]{:S(2)}, u32[]{:S(2)}) collective-permute-start(bf16[8,768,128]{2,1,0:T(8,128)(2,1)} %get-tuple-element.224), channel_id=1, source_target_pairs={{0,1},{1,0},{2,3},{3,2},{4,5},{5,4},{6,7},{7,6},{8,9},{9,8},{10,11... | collective-permute-start | bytes 4718600 | tf_op jit(solution)/shard_map/ppermute | solution.py:679
  280.2 3.1 collective-permute-start.20
  289.4 18.8 %collective-permute-start.22 = (bf16[128,2048]{1,0:T(8,128)(2,1)S(1)}, bf16[128,2048]{1,0:T(8,128)(2,1)S(1)}, u32[]{:S(2)}, u32[]{:S(2)}) collective-permute-start(bf16[128,2048]{1,0:T(8,128)(2,1)S(1)} %maximum_select_fusion.refs_8_), channel_id=1, source_target_pairs={{0,8},{2,6},{8,16},{10,2},{16,24},{18,10},{24,28},{26,18},{28,20},... | collective-permute-start | bytes 1572872 | tf_op jit(solution)/shard_map/ppermute | solution.py:673
  308.2 8.3 %collective-permute-start.23 = (bf16[128,2048]{1,0:T(8,128)(2,1)S(1)}, bf16[128,2048]{1,0:T(8,128)(2,1)S(1)}, u32[]{:S(2)}, u32[]{:S(2)}) collective-permute-start(bf16[128,2048]{1,0:T(8,128)(2,1)S(1)} %collective-permute-done.22.refs_9_), channel_id=1, source_target_pairs={{0,8},{2,6},{8,16},{10,2},{16,24},{18,10},{24,28},{26,18},{28,20},... | collective-permute-start | bytes 1572872 | tf_op jit(solution)/shard_map/ppermute | solution.py:673
  316.5 8.3 %collective-permute-start.24 = (bf16[128,2048]{1,0:T(8,128)(2,1)S(1)}, bf16[128,2048]{1,0:T(8,128)(2,1)S(1)}, u32[]{:S(2)}, u32[]{:S(2)}) collective-permute-start(bf16[128,2048]{1,0:T(8,128)(2,1)S(1)} %collective-permute-done.23.refs_10_), channel_id=1, source_target_pairs={{0,8},{2,6},{8,16},{10,2},{16,24},{18,10},{24,28},{26,18},{28,20},... | collective-permute-start | bytes 1572872 | tf_op jit(solution)/shard_map/ppermute | solution.py:673
  316.5 23.7 %collective-permute-start.25 = (bf16[128,2048]{1,0:T(8,128)(2,1)S(1)}, bf16[128,2048]{1,0:T(8,128)(2,1)S(1)}, u32[]{:S(2)}, u32[]{:S(2)}) collective-permute-start(bf16[128,2048]{1,0:T(8,128)(2,1)S(1)} %collective-permute-done.22.refs_9_), channel_id=1, source_target_pairs={{0,2},{2,0},{4,6},{6,4},{8,10},{10,8},{12,14},{14,12},{16,18},{18,... | collective-permute-start | bytes 1572872 | tf_op jit(solution)/shard_map/ppermute | solution.py:676
  318.2 22.0 %collective-permute-start.26 = (bf16[128,2048]{1,0:T(8,128)(2,1)S(1)}, bf16[128,2048]{1,0:T(8,128)(2,1)S(1)}, u32[]{:S(2)}, u32[]{:S(2)}) collective-permute-start(bf16[128,2048]{1,0:T(8,128)(2,1)S(1)} %collective-permute-done.23.refs_10_), channel_id=1, source_target_pairs={{0,2},{2,0},{4,6},{6,4},{8,10},{10,8},{12,14},{14,12},{16,18},{18,... | collective-permute-start | bytes 1572872 | tf_op jit(solution)/shard_map/ppermute | solution.py:676
  324.9 5.3 collective-permute-start.28
  324.9 15.3 %collective-permute-start.27 = (bf16[128,2048]{1,0:T(8,128)(2,1)S(1)}, bf16[128,2048]{1,0:T(8,128)(2,1)}, u32[]{:S(2)}, u32[]{:S(2)}) collective-permute-start(bf16[128,2048]{1,0:T(8,128)(2,1)S(1)} %collective-permute-done.24.refs_11_), channel_id=1, source_target_pairs={{0,2},{2,0},{4,6},{6,4},{8,10},{10,8},{12,14},{14,12},{16,18},{18,... | collective-permute-start | bytes 1572872 | tf_op jit(solution)/shard_map/ppermute | solution.py:676
  330.1 10.1 %collective-permute-start.29 = (bf16[64,2048]{1,0:T(8,128)(2,1)S(1)}, bf16[64,2048]{1,0:T(8,128)(2,1)}, u32[]{:S(2)}, u32[]{:S(2)}) collective-permute-start(bf16[64,2048]{1,0:T(8,128)(2,1)S(1)} %collective-permute-done.28.refs_15_), channel_id=1, source_target_pairs={{0,2},{2,0},{4,6},{6,4},{8,10},{10,8},{12,14},{14,12},{16,18},{18,... | collective-permute-start | bytes 786440 | tf_op jit(solution)/shard_map/ppermute | solution.py:676
  377.2 8.9 %collective-permute-start.34 = (bf16[448,2048]{1,0:T(8,128)(2,1)}, bf16[448,2048]{1,0:T(8,128)(2,1)S(1)}, u32[]{:S(2)}, u32[]{:S(2)}) collective-permute-start(bf16[448,2048]{1,0:T(8,128)(2,1)} %get-tuple-element.105), channel_id=1, source_target_pairs={{0,2},{2,0},{4,6},{6,4},{8,10},{10,8},{12,14},{14,12},{16,18},{18,... | collective-permute-start | bytes 5505032 | tf_op jit(solution)/shard_map/ppermute | solution.py:676
  377.4 4.3 collective-permute-start.31
  377.8 9.9 %collective-permute-start.30 = (bf16[448,2048]{1,0:T(8,128)(2,1)}, bf16[448,2048]{1,0:T(8,128)(2,1)S(1)}, u32[]{:S(2)}, u32[]{:S(2)}) collective-permute-start(bf16[448,2048]{1,0:T(8,128)(2,1)} %get-tuple-element.101), channel_id=1, source_target_pairs={{0,2},{2,0},{4,6},{6,4},{8,10},{10,8},{12,14},{14,12},{16,18},{18,... | collective-permute-start | bytes 5505032 | tf_op jit(solution)/shard_map/ppermute | solution.py:676
  377.9 6.7 collective-permute-start.32
  385.8 8.4 %collective-permute-start.33 = (bf16[2,64,2048]{2,1,0:T(8,128)(2,1)S(1)}, bf16[2,64,2048]{2,1,0:T(8,128)(2,1)S(1)}, u32[]{:S(2)}, u32[]{:S(2)}) collective-permute-start(bf16[2,64,2048]{2,1,0:T(8,128)(2,1)S(1)} %pad_maximum_fusion.1), channel_id=1, source_target_pairs={{0,8},{2,6},{8,16},{10,2},{16,24},{18,10},{24,28},{26,18},{28,20},... | collective-permute-start | bytes 1572872 | tf_op jit(solution)/shard_map/ppermute | solution.py:673
  395.5 14.3 %collective-permute-start.35 = (bf16[2,128,2048]{2,1,0:T(8,128)(2,1)}, bf16[2,128,2048]{2,1,0:T(8,128)(2,1)}, u32[]{:S(2)}, u32[]{:S(2)}) collective-permute-start(bf16[2,128,2048]{2,1,0:T(8,128)(2,1)} %fusion), channel_id=1, source_target_pairs={{0,8},{2,6},{8,16},{10,2},{16,24},{18,10},{24,28},{26,18},{28,20},... | collective-permute-start | bytes 3145736 | tf_op jit(solution)/shard_map/ppermute | solution.py:673
  412.2 14.3 %collective-permute-start.36 = (bf16[2,128,2048]{2,1,0:T(8,128)(2,1)}, bf16[2,128,2048]{2,1,0:T(8,128)(2,1)S(1)}, u32[]{:S(2)}, u32[]{:S(2)}) collective-permute-start(bf16[2,128,2048]{2,1,0:T(8,128)(2,1)} %fusion.1), channel_id=1, source_target_pairs={{0,8},{2,6},{8,16},{10,2},{16,24},{18,10},{24,28},{26,18},{28,20},... | collective-permute-start | bytes 3145736 | tf_op jit(solution)/shard_map/ppermute | solution.py:673
  426.9 14.1 %collective-permute-start.37 = (bf16[2,128,2048]{2,1,0:T(8,128)(2,1)S(1)}, bf16[2,128,2048]{2,1,0:T(8,128)(2,1)S(1)}, u32[]{:S(2)}, u32[]{:S(2)}) collective-permute-start(bf16[2,128,2048]{2,1,0:T(8,128)(2,1)S(1)} %fusion.2), channel_id=1, source_target_pairs={{0,8},{2,6},{8,16},{10,2},{16,24},{18,10},{24,28},{26,18},{28,20},... | collective-permute-start | bytes 3145736 | tf_op jit(solution)/shard_map/ppermute | solution.py:673
  427.3 28.2 %collective-permute-start.42 = (bf16[16,320,128]{2,1,0:T(8,128)(2,1)}, bf16[16,320,128]{2,1,0:T(8,128)(2,1)}, u32[]{:S(2)}, u32[]{:S(2)}) collective-permute-start(bf16[16,320,128]{2,1,0:T(8,128)(2,1)} %get-tuple-element.120), channel_id=1, source_target_pairs={{0,1},{1,0},{2,3},{3,2},{4,5},{5,4},{6,7},{7,6},{8,9},{9,8},{10,11... | collective-permute-start | bytes 3932168 | tf_op jit(solution)/shard_map/ppermute | solution.py:679
  441.0 5.1 collective-permute-start.38
  444.5 64.8 %collective-permute-start.45 = (bf16[16,464,128]{2,1,0:T(8,128)(2,1)}, bf16[16,464,128]{2,1,0:T(8,128)(2,1)}, u32[]{:S(2)}, u32[]{:S(2)}) collective-permute-start(bf16[16,464,128]{2,1,0:T(8,128)(2,1)} %get-tuple-element.122), channel_id=1, source_target_pairs={{0,1},{1,0},{2,3},{3,2},{4,5},{5,4},{6,7},{7,6},{8,9},{9,8},{10,11... | collective-permute-start | bytes 5701640 | tf_op jit(solution)/shard_map/ppermute | solution.py:679
  449.9 20.5 %collective-permute-start.41 = (bf16[64,2048]{1,0:T(8,128)(2,1)}, bf16[64,2048]{1,0:T(8,128)(2,1)S(1)}, u32[]{:S(2)}, u32[]{:S(2)}) collective-permute-start(bf16[64,2048]{1,0:T(8,128)(2,1)} %get-tuple-element.119), channel_id=1, source_target_pairs={{0,2},{2,0},{4,6},{6,4},{8,10},{10,8},{12,14},{14,12},{16,18},{18,... | collective-permute-start | bytes 786440 | tf_op jit(solution)/shard_map/ppermute | solution.py:676
  458.2 65.4 %all-to-all-start.3 = ((bf16[16,320,128]{2,1,0:T(8,128)(2,1)}), bf16[16,320,128]{2,1,0:T(8,128)(2,1)S(1)}, u32[]{:S(2)}, u32[]{:S(2)}) async-start(bf16[16,320,128]{2,1,0:T(8,128)(2,1)} %add_convert_fusion.3), calls=%async_computation.3 | async-start | bytes 2621440 | tf_op jit(solution)/shard_map/all_to_all | solution.py:729
  471.3 33.7 %collective-permute-start.43 = (bf16[128,2048]{1,0:T(8,128)(2,1)}, bf16[128,2048]{1,0:T(8,128)(2,1)}, u32[]{:S(2)}, u32[]{:S(2)}) collective-permute-start(bf16[128,2048]{1,0:T(8,128)(2,1)} %maximum_select_fusion.2.rest_0_.refs_10_), channel_id=1, source_target_pairs={{0,8},{2,6},{8,16},{10,2},{16,24},{18,10},{24,28},{26,18},{28,20},... | collective-permute-start | bytes 1572872 | tf_op jit(solution)/shard_map/ppermute | solution.py:673
  474.8 32.2 %collective-permute-start.39 = (bf16[64,2048]{1,0:T(8,128)(2,1)}, bf16[64,2048]{1,0:T(8,128)(2,1)S(1)}, u32[]{:S(2)}, u32[]{:S(2)}) collective-permute-start(bf16[64,2048]{1,0:T(8,128)(2,1)} %forward_out.1), channel_id=1, source_target_pairs={{0,2},{2,0},{4,6},{6,4},{8,10},{10,8},{12,14},{14,12},{16,18},{18,... | collective-permute-start | bytes 786440 | tf_op jit(solution)/shard_map/ppermute | solution.py:676
  505.0 8.5 %collective-permute-start.44 = (bf16[128,2048]{1,0:T(8,128)(2,1)}, bf16[128,2048]{1,0:T(8,128)(2,1)S(1)}, u32[]{:S(2)}, u32[]{:S(2)}) collective-permute-start(bf16[128,2048]{1,0:T(8,128)(2,1)} %collective-permute-done.43.rest_1_.refs_11_), channel_id=1, source_target_pairs={{0,8},{2,6},{8,16},{10,2},{16,24},{18,10},{24,28},{26,18},{28,20},... | collective-permute-start | bytes 1572872 | tf_op jit(solution)/shard_map/ppermute | solution.py:673
  508.1 13.1 %collective-permute-start.40 = (bf16[128,2048]{1,0:T(8,128)(2,1)S(1)}, bf16[128,2048]{1,0:T(8,128)(2,1)S(1)}, u32[]{:S(2)}, u32[]{:S(2)}) collective-permute-start(bf16[128,2048]{1,0:T(8,128)(2,1)S(1)} %maximum_select_fusion.1), channel_id=1, source_target_pairs={{0,1},{1,0},{2,3},{3,2},{4,5},{5,4},{6,7},{7,6},{8,9},{9,8},{10,11... | collective-permute-start | bytes 1572872 | tf_op jit(solution)/shard_map/ppermute | solution.py:679
  513.5 8.5 %collective-permute-start.46 = (bf16[128,2048]{1,0:T(8,128)(2,1)S(1)}, bf16[128,2048]{1,0:T(8,128)(2,1)S(1)}, u32[]{:S(2)}, u32[]{:S(2)}) collective-permute-start(bf16[128,2048]{1,0:T(8,128)(2,1)S(1)} %collective-permute-done.44.rest_2_.refs_12_), channel_id=1, source_target_pairs={{0,8},{2,6},{8,16},{10,2},{16,24},{18,10},{24,28},{26,18},{28,20},... | collective-permute-start | bytes 1572872 | tf_op jit(solution)/shard_map/ppermute | solution.py:673
  523.6 5.5 collective-permute-start.50
  532.4 55.6 %all-to-all-start.4 = ((bf16[16,464,128]{2,1,0:T(8,128)(2,1)}), bf16[16,464,128]{2,1,0:T(8,128)(2,1)S(1)}, u32[]{:S(2)}, u32[]{:S(2)}) async-start(bf16[16,464,128]{2,1,0:T(8,128)(2,1)} %add_convert_fusion.1), calls=%async_computation.4 | async-start | bytes 3801088 | tf_op jit(solution)/shard_map/all_to_all | solution.py:729
  541.7 3.3 collective-permute-start.49
  542.1 3.1 collective-permute-start.51
  554.9 30.3 %collective-permute-start.56 = (bf16[16,320,128]{2,1,0:T(8,128)(2,1)}, bf16[16,320,128]{2,1,0:T(8,128)(2,1)}, u32[]{:S(2)}, u32[]{:S(2)}) collective-permute-start(bf16[16,320,128]{2,1,0:T(8,128)(2,1)} %get-tuple-element.139), channel_id=1, source_target_pairs={{0,1},{1,0},{2,3},{3,2},{4,5},{5,4},{6,7},{7,6},{8,9},{9,8},{10,11... | collective-permute-start | bytes 3932168 | tf_op jit(solution)/shard_map/ppermute | solution.py:679
  582.7 27.5 %collective-permute-start.52 = (bf16[448,2048]{1,0:T(8,128)(2,1)}, bf16[448,2048]{1,0:T(8,128)(2,1)}, u32[]{:S(2)}, u32[]{:S(2)}) collective-permute-start(bf16[448,2048]{1,0:T(8,128)(2,1)} %get-tuple-element.130), channel_id=1, source_target_pairs={{0,2},{2,0},{4,6},{6,4},{8,10},{10,8},{12,14},{14,12},{16,18},{18,... | collective-permute-start | bytes 5505032 | tf_op jit(solution)/shard_map/ppermute | solution.py:676
  588.0 48.7 %all-to-all-start.5 = ((bf16[16,320,128]{2,1,0:T(8,128)(2,1)}), bf16[16,320,128]{2,1,0:T(8,128)(2,1)S(1)}, u32[]{:S(2)}, u32[]{:S(2)}) async-start(bf16[16,320,128]{2,1,0:T(8,128)(2,1)} %add_convert_fusion.2), calls=%async_computation.5 | async-start | bytes 2621440 | tf_op jit(solution)/shard_map/all_to_all | solution.py:729
  607.8 18.7 %collective-permute-start.54 = (bf16[1,64,2048]{2,1,0:T(8,128)(2,1)S(1)}, bf16[1,64,2048]{2,1,0:T(8,128)(2,1)S(1)}, u32[]{:S(2)}, u32[]{:S(2)}) collective-permute-start(bf16[1,64,2048]{2,1,0:T(8,128)(2,1)S(1)} %fusion.16), channel_id=1, source_target_pairs={{0,8},{2,6},{8,16},{10,2},{16,24},{18,10},{24,28},{26,18},{28,20},... | collective-permute-start | bytes 786440 | tf_op jit(solution)/shard_map/ppermute | solution.py:673
  609.0 43.5 %collective-permute-start.58 = (bf16[16,464,128]{2,1,0:T(8,128)(2,1)}, bf16[16,464,128]{2,1,0:T(8,128)(2,1)}, u32[]{:S(2)}, u32[]{:S(2)}) collective-permute-start(bf16[16,464,128]{2,1,0:T(8,128)(2,1)} %get-tuple-element.143), channel_id=1, source_target_pairs={{0,1},{1,0},{2,3},{3,2},{4,5},{5,4},{6,7},{7,6},{8,9},{9,8},{10,11... | collective-permute-start | bytes 5701640 | tf_op jit(solution)/shard_map/ppermute | solution.py:679
  627.9 8.7 %collective-permute-start.55 = (bf16[1,128,2048]{2,1,0:T(8,128)(2,1)S(1)}, bf16[1,128,2048]{2,1,0:T(8,128)(2,1)}, u32[]{:S(2)}, u32[]{:S(2)}) collective-permute-start(bf16[1,128,2048]{2,1,0:T(8,128)(2,1)S(1)} %fusion.8), channel_id=1, source_target_pairs={{0,8},{2,6},{8,16},{10,2},{16,24},{18,10},{24,28},{26,18},{28,20},... | collective-permute-start | bytes 1572872 | tf_op jit(solution)/shard_map/ppermute | solution.py:673
  638.7 13.9 %collective-permute-start.57 = (bf16[1,128,2048]{2,1,0:T(8,128)(2,1)S(1)}, bf16[1,128,2048]{2,1,0:T(8,128)(2,1)S(1)}, u32[]{:S(2)}, u32[]{:S(2)}) collective-permute-start(bf16[1,128,2048]{2,1,0:T(8,128)(2,1)S(1)} %fusion.4), channel_id=1, source_target_pairs={{0,8},{2,6},{8,16},{10,2},{16,24},{18,10},{24,28},{26,18},{28,20},... | collective-permute-start | bytes 1572872 | tf_op jit(solution)/shard_map/ppermute | solution.py:673
  653.8 8.5 %collective-permute-start.59 = (bf16[1,128,2048]{2,1,0:T(8,128)(2,1)S(1)}, bf16[1,128,2048]{2,1,0:T(8,128)(2,1)}, u32[]{:S(2)}, u32[]{:S(2)}) collective-permute-start(bf16[1,128,2048]{2,1,0:T(8,128)(2,1)S(1)} %fusion.3), channel_id=1, source_target_pairs={{0,8},{2,6},{8,16},{10,2},{16,24},{18,10},{24,28},{26,18},{28,20},... | collective-permute-start | bytes 1572872 | tf_op jit(solution)/shard_map/ppermute | solution.py:673
  662.3 49.4 %all-to-all-start.6 = ((bf16[16,464,128]{2,1,0:T(8,128)(2,1)}), bf16[16,464,128]{2,1,0:T(8,128)(2,1)S(1)}, u32[]{:S(2)}, u32[]{:S(2)}) async-start(bf16[16,464,128]{2,1,0:T(8,128)(2,1)} %add_convert_fusion), calls=%async_computation.6 | async-start | bytes 3801088 | tf_op jit(solution)/shard_map/all_to_all | solution.py:729
  669.7 9.1 %collective-permute-start.60 = (bf16[1,64,2048]{2,1,0:T(8,128)(2,1)S(1)}, bf16[1,64,2048]{2,1,0:T(8,128)(2,1)S(1)}, u32[]{:S(2)}, u32[]{:S(2)}) collective-permute-start(bf16[1,64,2048]{2,1,0:T(8,128)(2,1)S(1)} %constant_dynamic-slice_fusion.5), channel_id=1, source_target_pairs={{0,2},{2,0},{4,6},{6,4},{8,10},{10,8},{12,14},{14,12},{16,18},{18,... | collective-permute-start | bytes 786440 | tf_op jit(solution)/shard_map/ppermute | solution.py:676
  670.3 8.5 %collective-permute-start.61 = (f32[2,448]{1,0:T(2,128)S(1)}, f32[2,448]{1,0:T(2,128)S(1)}, u32[]{:S(2)}, u32[]{:S(2)}) collective-permute-start(f32[2,448]{1,0:T(2,128)S(1)} %pad_maximum_fusion.3), channel_id=1, source_target_pairs={{0,1},{1,0},{2,3},{3,2},{4,5},{5,4},{6,7},{7,6},{8,9},{9,8},{10,11... | collective-permute-start | bytes 10760 | tf_op jit(solution)/shard_map/ppermute | solution.py:679
  685.4 13.2 %collective-permute-start.63 = (bf16[128,2048]{1,0:T(8,128)(2,1)S(1)}, bf16[128,2048]{1,0:T(8,128)(2,1)S(1)}, u32[]{:S(2)}, u32[]{:S(2)}) collective-permute-start(bf16[128,2048]{1,0:T(8,128)(2,1)S(1)} %maximum_select_fusion.3), channel_id=1, source_target_pairs={{0,1},{1,0},{2,3},{3,2},{4,5},{5,4},{6,7},{7,6},{8,9},{9,8},{10,11... | collective-permute-start | bytes 1572872 | tf_op jit(solution)/shard_map/ppermute | solution.py:679
  (62 other events, 869.1 us)

commit v12 on v11

--- a/solution.py
+++ b/solution.py
@@ -863,7 +863,7 @@
     next_state, normed_own = call_end(
         partial(forward_end, False),
         core_word,
-        ring_sum((after(parts[0], *slabs), parts[1], parts[2]), needed={0: others[:1]})[0],
+        ring_sum((after(parts[0], *slabs), parts[1], parts[2]), needed={1: others[:1]})[0],
         [state, added_bias[0], gains[1], shifts[1]],
         [jax.ShapeDtypeStruct(rows_shape, f32), jax.ShapeDtypeStruct(rows_shape, bf16)],
         "forward_end",

time: 732 us -> 739 us (level)
  transfers between devices with their start and end apart: 71 -> 71, of which waited for: 45 -> 45; matrix products, arithmetic and copies ran while one was open for 8% -> 7% of each run, Pallas kernels for 19% -> 19%
where the time goes in v12:
time: 739 us; the launch traced here: 728 us
  waiting for transfers between devices  349 us (47%)
  Pallas kernels  183 us (25%)
  starting transfers between devices  116 us (16%)
  other arithmetic  53.1 us (7%)
  local copies, waits for them, and re-layouts  25.1 us (3%)
    ppermute x24, waiting for transfers between devices, along(): return lax.ppermute(x, 'dp', ring_pairs)  153 us
    all_to_all x7, waiting for transfers between devices, spread(): return lax.all_to_all(x, 'dp', 0, 0, axis_index_groups=inner, tiled=True)  99.5 us
    pallas_call x3, Pallas kernels, call_pass(): pl.pallas_call(partial(layer_pass, mode), in_specs=[SMEM_SPEC] + [VMEM_SP...  91.9 us
    ppermute x12, waiting for transfers between devices, over(): return lax.ppermute(x, 'tensor', [(0, 1), (1, 0)])  83.1 us
    all_to_all x7, starting transfers between devices, spread(): return lax.all_to_all(x, 'dp', 0, 0, axis_index_groups=inner, tiled=True)  52.1 us
    pallas_call x4, Pallas kernels, call_gradients(): pl.pallas_call(partial(gradient_slabs, own_rows, other_rows, with_sums, l...  38.1 us
    ppermute x28, starting transfers between devices, across(): return lax.ppermute(x, 'dp', core_pairs)  25.3 us
    ppermute x24, starting transfers between devices, along(): return lax.ppermute(x, 'dp', ring_pairs)  25.2 us
  transfers between devices with their start and end apart: 71, of which 45 were waited for; matrix products, arithmetic and copies ran while one was open for 7% of the time, Pallas kernels for 19%

profile of v12, /device:TPU:13, one launch (start us, length us, event | category | flops | bytes accessed | tf_op | source)
XLA Modules:
  0.0 727.8 jit_solution(5562065417882083907)
XLA Ops:
  4.8 4.0 pack_first.1
  8.8 6.5 all-to-all-start
  15.3 3.5 pack_down.1
  18.9 39.7 %all-to-all-done.own_ref = bf16[16,464,128]{2,1,0:T(8,128)(2,1)S(1)} async-done(((bf16[16,464,128]{2,1,0:T(8,128)(2,1)}), bf16[16,464,128]{2,1,0:T(8,128)(2,1)S(1)}, u32[]{:S(2)}, u32[]{:S(2)}) %all-to-all-start) | async-done | bytes 1900576 | tf_op jit(solution)/shard_map/all_to_all | solution.py:729
  58.5 4.8 all-to-all-start.1
  69.3 4.4 pack_both.1
  76.4 17.9 %all-to-all-done.1.own_ref = bf16[16,320,128]{2,1,0:T(8,128)(2,1)S(1)} async-done(((bf16[16,320,128]{2,1,0:T(8,128)(2,1)}), bf16[16,320,128]{2,1,0:T(8,128)(2,1)S(1)}, u32[]{:S(2)}, u32[]{:S(2)}) %all-to-all-start.1) | async-done | bytes 1310752 | tf_op jit(solution)/shard_map/all_to_all | solution.py:729
  100.8 10.1 %collective-permute-done.2.other_ref = bf16[16,464,128]{2,1,0:T(8,128)(2,1)} collective-permute-done((bf16[16,464,128]{2,1,0:T(8,128)(2,1)S(1)}, bf16[16,464,128]{2,1,0:T(8,128)(2,1)}, u32[]{:S(2)}, u32[]{:S(2)}) %collective-permute-start.2) | collective-permute-done | bytes 1900576 | tf_op jit(solution)/shard_map/ppermute | solution.py:679
  118.0 7.1 collective-permute-done.3.refs_12_.refs_19_
  126.3 4.8 join_up.1.refs_1_
  131.1 8.1 %collective-permute-done.4.refs_13_.refs_20_ = bf16[2,128,2048]{2,1,0:T(8,128)(2,1)S(1)} collective-permute-done((bf16[2,128,2048]{2,1,0:T(8,128)(2,1)}, bf16[2,128,2048]{2,1,0:T(8,128)(2,1)S(1)}, u32[]{:S(2)}, u32[]{:S(2)}) %collective-permute-start.4) | collective-permute-done | bytes 1048608 | tf_op jit(solution)/shard_map/ppermute | solution.py:673
  139.3 2.9 collective-permute-done.5.other_ref
  143.4 7.1 collective-permute-done.6.refs_17_.refs_24_
  151.4 6.8 all-to-all-start.2
  164.6 4.2 join_down.1.refs_2_
  168.8 29.3 %pass_first.1 = (bf16[1024,2048]{1,0:T(8,128)(2,1)}, bf16[1024,384]{1,0:T(8,128)(2,1)}, f32[1024,512]{1,0:T(8,128)}, bf16[1024,640]{1,0:T(8,128)(2,1)}, bf16[64,...) custom-call(s32[1]{0:T(128)} %bitcast.refs_0_.core_ref, bf16[2048,896]{1,0:T(8,128)(2,1)} %join_up.1.refs_1_, ...), custom_call_target="tpu_custom_call" | custom-call | flops 19327352832 | bytes 20000000 | tf_op jit(solution)/shard_map/pass_first/pallas_call | solution.py:443
  198.2 29.8 %all-to-all-done.2.own_ref = bf16[16,768,128]{2,1,0:T(8,128)(2,1)S(1)} async-done(((bf16[16,768,128]{2,1,0:T(8,128)(2,1)}), bf16[16,768,128]{2,1,0:T(8,128)(2,1)S(1)}, u32[]{:S(2)}, u32[]{:S(2)}) %all-to-all-start.2) | async-done | bytes 3145760 | tf_op jit(solution)/shard_map/all_to_all | solution.py:729
  231.9 5.5 collective-permute-done.16
  238.8 8.3 %collective-permute-done.17 = bf16[1,128,2048]{2,1,0:T(8,128)(2,1)S(1)} collective-permute-done((bf16[1,128,2048]{2,1,0:T(8,128)(2,1)S(1)}, bf16[1,128,2048]{2,1,0:T(8,128)(2,1)S(1)}, u32[]{:S(2)}, u32[]{:S(2)}) %collective-permute-start.17) | collective-permute-done | bytes 524320 | tf_op jit(solution)/shard_map/ppermute | solution.py:673
  247.1 19.1 %collective-permute-done.7.lower_ref = bf16[8,768,128]{2,1,0:T(8,128)(2,1)S(1)} collective-permute-done((bf16[8,768,128]{2,1,0:T(8,128)(2,1)S(1)}, bf16[8,768,128]{2,1,0:T(8,128)(2,1)S(1)}, u32[]{:S(2)}, u32[]{:S(2)}) %collective-permute-start.7) | collective-permute-done | bytes 1572896 | tf_op jit(solution)/shard_map/ppermute | solution.py:679
  267.9 8.3 %collective-permute-done.18 = bf16[1,128,2048]{2,1,0:T(8,128)(2,1)S(1)} collective-permute-done((bf16[1,128,2048]{2,1,0:T(8,128)(2,1)S(1)}, bf16[1,128,2048]{2,1,0:T(8,128)(2,1)S(1)}, u32[]{:S(2)}, u32[]{:S(2)}) %collective-permute-start.18) | collective-permute-done | bytes 524320 | tf_op jit(solution)/shard_map/ppermute | solution.py:673
  279.5 7.3 %collective-permute-done.19.moving_ref = bf16[1,128,2048]{2,1,0:T(8,128)(2,1)S(1)} collective-permute-done((bf16[1,128,2048]{2,1,0:T(8,128)(2,1)}, bf16[1,128,2048]{2,1,0:T(8,128)(2,1)S(1)}, u32[]{:S(2)}, u32[]{:S(2)}) %collective-permute-start.19) | collective-permute-done | bytes 524320 | tf_op jit(solution)/shard_map/ppermute | solution.py:673
  287.6 2.7 collective-permute-start.20
  297.9 14.8 %collective-permute-done.8.upper_ref = bf16[8,768,128]{2,1,0:T(8,128)(2,1)S(1)} collective-permute-done((bf16[8,768,128]{2,1,0:T(8,128)(2,1)}, bf16[8,768,128]{2,1,0:T(8,128)(2,1)S(1)}, u32[]{:S(2)}, u32[]{:S(2)}) %collective-permute-start.8) | collective-permute-done | bytes 1572896 | tf_op jit(solution)/shard_map/ppermute | solution.py:679
  313.7 9.3 %collective-permute-done.23.refs_10_ = bf16[128,2048]{1,0:T(8,128)(2,1)} collective-permute-done((bf16[128,2048]{1,0:T(8,128)(2,1)}, bf16[128,2048]{1,0:T(8,128)(2,1)}, u32[]{:S(2)}, u32[]{:S(2)}) %collective-permute-start.23) | collective-permute-done | bytes 524320 | tf_op jit(solution)/shard_map/ppermute | solution.py:673
  323.0 3.5 collective-permute-start.25
  326.6 5.0 collective-permute-done.24.refs_11_
  331.7 4.4 collective-permute-start.27
  336.9 3.8 collective-permute-start.29
  340.7 6.3 join_halves.1
  347.8 36.0 %pass_middle.1 = (bf16[1024,2048]{1,0:T(8,128)(2,1)}, bf16[1024,2048]{1,0:T(8,128)(2,1)}, bf16[1024,640]{1,0:T(8,128)(2,1)}, bf16[1024,896]{1,0:T(8,128)(2,1)}, ...) custom-call(s32[1]{0:T(128)} %bitcast.refs_0_.core_ref, ...), custom_call_target="tpu_custom_call" | custom-call | flops 38654705664 | bytes 40000000 | tf_op jit(solution)/shard_map/pass_middle/pallas_call | solution.py:443
  384.9 3.3 collective-permute-done.31
  397.4 3.3 collective-permute-done.33
  403.5 8.9 %down_gradients.2 = (bf16[16,320,128]{2,1,0:T(8,128)(2,1)}, bf16[16,320,128]{2,1,0:T(8,128)(2,1)}) custom-call(s32[1]{0:T(128)} %bitcast.refs_0_.core_ref, bf16[1024,640]{1,0:T(8,128)(2,1)} %get-tuple-element.106.left_ref, bf16[1024,2048]{1,0:T(8,128)(2,1)} %get-tuple-element.107.rest_0_), custom_call_target="tpu_custom_call" | custom-call | flops 5368709120 | bytes 10747904 | tf_op jit(solution)/shard_map/down_gradients/pallas_call | solution.py:505
  412.4 3.9 collective-permute-done.35
  420.4 10.2 %up_gradients.2 = (bf16[16,464,128]{2,1,0:T(8,128)(2,1)}, bf16[16,464,128]{2,1,0:T(8,128)(2,1)}, f32[1,896]{1,0:T(1,128)}) custom-call(s32[1]{0:T(128)} %bitcast.refs_0_.core_ref, bf16[1024,896]{1,0:T(8,128)(2,1)} %get-tuple-element.110.left_ref, bf16[1024,2048]{1,0:T(8,128)(2,1)} %get-tuple-element.111.rest_0_, f32[16,2048]{1,0:T(8,128)} %get-tuple-element.112.rest_1_), custom_call_target="tpu_custom_call" | custom-call | flops 7516192768 | bytes 13369344 | tf_op jit(solution)/shard_map/up_gradients/pallas_call | solution.py:505
  436.1 11.4 %collective-permute-done.37.moving_ref = bf16[2,128,2048]{2,1,0:T(8,128)(2,1)S(1)} collective-permute-done((bf16[2,128,2048]{2,1,0:T(8,128)(2,1)S(1)}, bf16[2,128,2048]{2,1,0:T(8,128)(2,1)S(1)}, u32[]{:S(2)}, u32[]{:S(2)}) %collective-permute-start.37) | collective-permute-done | bytes 1048608 | tf_op jit(solution)/shard_map/ppermute | solution.py:673
  447.6 3.5 collective-permute-start.38
  453.5 3.0 backward_end.2
  456.8 5.7 collective-permute-done.42
  462.5 2.7 add_convert_fusion.3
  465.3 12.2 %all-to-all-start.3 = ((bf16[16,320,128]{2,1,0:T(8,128)(2,1)}), bf16[16,320,128]{2,1,0:T(8,128)(2,1)S(1)}, u32[]{:S(2)}, u32[]{:S(2)}) async-start(bf16[16,320,128]{2,1,0:T(8,128)(2,1)} %add_convert_fusion.3), calls=%async_computation.3 | async-start | bytes 2621440 | tf_op jit(solution)/shard_map/all_to_all | solution.py:729
  481.9 30.2 %collective-permute-done.43.rest_1_.refs_11_ = bf16[128,2048]{1,0:T(8,128)(2,1)} collective-permute-done((bf16[128,2048]{1,0:T(8,128)(2,1)}, bf16[128,2048]{1,0:T(8,128)(2,1)}, u32[]{:S(2)}, u32[]{:S(2)}) %collective-permute-start.43) | collective-permute-done | bytes 524320 | tf_op jit(solution)/shard_map/ppermute | solution.py:673
  516.4 4.2 collective-permute-done.44.rest_2_.refs_12_
  522.5 5.7 collective-permute-done.40
  532.4 3.8 collective-permute-done.50.rest_7_.refs_17_
  536.2 3.3 add_convert_fusion.1
  539.5 8.8 %all-to-all-start.4 = ((bf16[16,464,128]{2,1,0:T(8,128)(2,1)}), bf16[16,464,128]{2,1,0:T(8,128)(2,1)S(1)}, u32[]{:S(2)}, u32[]{:S(2)}) async-start(bf16[16,464,128]{2,1,0:T(8,128)(2,1)} %add_convert_fusion.1), calls=%async_computation.4 | async-start | bytes 3801088 | tf_op jit(solution)/shard_map/all_to_all | solution.py:729
  553.1 8.9 %down_gradients.3 = (bf16[16,320,128]{2,1,0:T(8,128)(2,1)}, bf16[16,320,128]{2,1,0:T(8,128)(2,1)}) custom-call(s32[1]{0:T(128)} %bitcast.refs_0_.core_ref, bf16[1024,640]{1,0:T(8,128)(2,1)} %get-tuple-element.118.left_ref, bf16[128,2048]{1,0:T(8,128)(2,1)} %maximum_select_fusion.2.rest_0_.refs_10_, ...), custom_call_target="tpu_custom_call" | custom-call | flops 5368709120 | bytes 10747904 | tf_op jit(solution)/shard_map/down_gradients/pallas_call | solution.py:505
  563.2 26.6 %pass_last.1 = (bf16[1024,2048]{1,0:T(8,128)(2,1)}, bf16[1024,896]{1,0:T(8,128)(2,1)}, f32[16,2048]{1,0:T(8,128)}, bf16[64,2048]{1,0:T(8,128)(2,1)}, bf16[448,20...) custom-call(s32[1]{0:T(128)} %bitcast.refs_0_.core_ref, bf16[2048,896]{1,0:T(8,128)(2,1)} %join_up.1.refs_1_, ...), custom_call_target="tpu_custom_call" | custom-call | flops 19327352832 | bytes 20000000 | tf_op jit(solution)/shard_map/pass_last/pallas_call | solution.py:443
  592.3 2.7 add_convert_fusion.2
  595.1 6.8 all-to-all-start.5
  601.9 10.1 %up_gradients.3 = (bf16[16,464,128]{2,1,0:T(8,128)(2,1)}, bf16[16,464,128]{2,1,0:T(8,128)(2,1)}, f32[1,896]{1,0:T(1,128)}) custom-call(s32[1]{0:T(128)} %bitcast.refs_0_.core_ref, bf16[1024,896]{1,0:T(8,128)(2,1)} %get-tuple-element.132.left_ref, bf16[1024,2048]{1,0:T(8,128)(2,1)} %get-tuple-element.135.refs_9_.rest_0_, f32[16,2048]{1,0:T(8,128)} %get-tuple-element.136.rest_1_), custom_call_target="tpu_custom_call" | custom-call | flops 7516192768 | bytes 13369344 | tf_op jit(solution)/shard_map/up_gradients/pallas_call | solution.py:505
  617.3 16.3 %collective-permute-done.54 = bf16[1,64,2048]{2,1,0:T(8,128)(2,1)S(1)} collective-permute-done((bf16[1,64,2048]{2,1,0:T(8,128)(2,1)S(1)}, bf16[1,64,2048]{2,1,0:T(8,128)(2,1)S(1)}, u32[]{:S(2)}, u32[]{:S(2)}) %collective-permute-start.54) | collective-permute-done | bytes 262176 | tf_op jit(solution)/shard_map/ppermute | solution.py:673
  637.6 6.1 collective-permute-done.55
  648.1 11.5 %collective-permute-done.58 = bf16[16,464,128]{2,1,0:T(8,128)(2,1)} collective-permute-done((bf16[16,464,128]{2,1,0:T(8,128)(2,1)}, bf16[16,464,128]{2,1,0:T(8,128)(2,1)}, u32[]{:S(2)}, u32[]{:S(2)}) %collective-permute-start.58) | collective-permute-done | bytes 1900576 | tf_op jit(solution)/shard_map/ppermute | solution.py:679
  662.2 3.3 add_convert_fusion
  665.5 4.0 collective-permute-done.59.moving_ref
  669.4 6.2 all-to-all-start.6
  678.6 7.3 %spread_gradients.2 = (f32[2,3,128,1024]{3,2,1,0:T(8,128)}, f32[2,1024,128]{2,1,0:T(8,128)}, f32[2,128,4096]{2,1,0:T(8,128)}, f32[2,4096,128]{2,1,0:T(8,128)}, f32[8,128]{1,0:T(8,128)}) custom-call(bf16[16,464,128]{2,1,0:T(8,128)(2,1)} %copy-done.2, bf16[16,320,128]{2,1,0:T(8,128)(2,1)} %copy-done.12), custom_call_target="tpu_custom_call" | custom-call | tf_op jit(solution)/shard_map/spread_gradients/pallas_call | solution.py:545
  686.6 2.9 backward_end.3
  695.8 9.9 %collective-permute-done.63 = bf16[128,2048]{1,0:T(8,128)(2,1)S(1)} collective-permute-done((bf16[128,2048]{1,0:T(8,128)(2,1)S(1)}, bf16[128,2048]{1,0:T(8,128)(2,1)S(1)}, u32[]{:S(2)}, u32[]{:S(2)}) %collective-permute-start.63) | collective-permute-done | bytes 524320 | tf_op jit(solution)/shard_map/ppermute | solution.py:679
  706.7 12.1 %all-to-all-done.6.up_ref = bf16[16,464,128]{2,1,0:T(8,128)(2,1)S(1)} async-done(((bf16[16,464,128]{2,1,0:T(8,128)(2,1)}), bf16[16,464,128]{2,1,0:T(8,128)(2,1)S(1)}, u32[]{:S(2)}, u32[]{:S(2)}) %all-to-all-start.6) | async-done | bytes 1900576 | tf_op jit(solution)/shard_map/all_to_all | solution.py:729
  720.1 7.3 %spread_gradients.3 = (f32[2,3,128,1024]{3,2,1,0:T(8,128)}, f32[2,1024,128]{2,1,0:T(8,128)}, f32[2,128,4096]{2,1,0:T(8,128)}, f32[2,4096,128]{2,1,0:T(8,128)}, f32[8,128]{1,0:T(8,128)}) custom-call(bf16[16,464,128]{2,1,0:T(8,128)(2,1)} %copy-done.3, ...), custom_call_target="tpu_custom_call", output_to_operand_aliasing={{0}: (2, {}), {1}: (3, {}), {2}: (4, {}), {3}: (5, {})} | custom-call | tf_op jit(solution)/shard_map/spread_gradients/pallas_call | solution.py:545
  (311 shorter events, 134.2 us)
Async XLA Ops:
  8.8 49.7 %all-to-all-start = ((bf16[16,464,128]{2,1,0:T(8,128)(2,1)}), bf16[16,464,128]{2,1,0:T(8,128)(2,1)S(1)}, u32[]{:S(2)}, u32[]{:S(2)}) async-start(bf16[16,464,128]{2,1,0:T(8,128)(2,1)} %pack_first.1), calls=%async_computation | async-start | bytes 3801088 | tf_op jit(solution)/shard_map/all_to_all | solution.py:729
  58.5 35.7 %all-to-all-start.1 = ((bf16[16,320,128]{2,1,0:T(8,128)(2,1)}), bf16[16,320,128]{2,1,0:T(8,128)(2,1)S(1)}, u32[]{:S(2)}, u32[]{:S(2)}) async-start(bf16[16,320,128]{2,1,0:T(8,128)(2,1)} %pack_down.1), calls=%async_computation.1 | async-start | bytes 2621440 | tf_op jit(solution)/shard_map/all_to_all | solution.py:729
  65.6 8.2 %collective-permute-start = (bf16[2,128,2048]{2,1,0:T(8,128)(2,1)}, bf16[2,128,2048]{2,1,0:T(8,128)(2,1)}, u32[]{:S(2)}, u32[]{:S(2)}) collective-permute-start(bf16[2,128,2048]{2,1,0:T(8,128)(2,1)} %pad_maximum_fusion), channel_id=1, source_target_pairs={{0,2},{2,0},{4,6},{6,4},{8,10},{10,8},{12,14},{14,12},{16,18},{18,... | collective-permute-start | bytes 3145736 | tf_op jit(solution)/shard_map/ppermute | solution.py:676
  67.9 43.0 %collective-permute-start.2 = (bf16[16,464,128]{2,1,0:T(8,128)(2,1)S(1)}, bf16[16,464,128]{2,1,0:T(8,128)(2,1)}, u32[]{:S(2)}, u32[]{:S(2)}) collective-permute-start(bf16[16,464,128]{2,1,0:T(8,128)(2,1)S(1)} %all-to-all-done.own_ref), channel_id=1, source_target_pairs={{0,1},{1,0},{2,3},{3,2},{4,5},{5,4},{6,7},{7,6},{8,9},{9,8},{10,11... | collective-permute-start | bytes 5701640 | tf_op jit(solution)/shard_map/ppermute | solution.py:679
  94.3 16.6 %collective-permute-start.1 = (bf16[2,128,2048]{2,1,0:T(8,128)(2,1)}, bf16[2,128,2048]{2,1,0:T(8,128)(2,1)}, u32[]{:S(2)}, u32[]{:S(2)}) collective-permute-start(bf16[2,128,2048]{2,1,0:T(8,128)(2,1)} %select_multiply_fusion.refs_10_.refs_17_), channel_id=1, source_target_pairs={{0,8},{2,6},{8,16},{10,2},{16,24},{18,10},{24,28},{26,18},{28,20},... | collective-permute-start | bytes 3145736 | tf_op jit(solution)/shard_map/ppermute | solution.py:673
  110.9 14.3 %collective-permute-start.3 = (bf16[2,128,2048]{2,1,0:T(8,128)(2,1)}, bf16[2,128,2048]{2,1,0:T(8,128)(2,1)}, u32[]{:S(2)}, u32[]{:S(2)}) collective-permute-start(bf16[2,128,2048]{2,1,0:T(8,128)(2,1)} %collective-permute-done.1.refs_11_.refs_18_), channel_id=1, source_target_pairs={{0,8},{2,6},{8,16},{10,2},{16,24},{18,10},{24,28},{26,18},{28,20},... | collective-permute-start | bytes 3145736 | tf_op jit(solution)/shard_map/ppermute | solution.py:673
  112.0 30.2 %collective-permute-start.5 = (bf16[16,320,128]{2,1,0:T(8,128)(2,1)}, bf16[16,320,128]{2,1,0:T(8,128)(2,1)S(1)}, u32[]{:S(2)}, u32[]{:S(2)}) collective-permute-start(bf16[16,320,128]{2,1,0:T(8,128)(2,1)} %copy-done.11), channel_id=1, source_target_pairs={{0,1},{1,0},{2,3},{3,2},{4,5},{5,4},{6,7},{7,6},{8,9},{9,8},{10,11... | collective-permute-start | bytes 3932168 | tf_op jit(solution)/shard_map/ppermute | solution.py:679
  125.1 14.2 %collective-permute-start.4 = (bf16[2,128,2048]{2,1,0:T(8,128)(2,1)}, bf16[2,128,2048]{2,1,0:T(8,128)(2,1)S(1)}, u32[]{:S(2)}, u32[]{:S(2)}) collective-permute-start(bf16[2,128,2048]{2,1,0:T(8,128)(2,1)} %collective-permute-done.3.refs_12_.refs_19_), channel_id=1, source_target_pairs={{0,8},{2,6},{8,16},{10,2},{16,24},{18,10},{24,28},{26,18},{28,20},... | collective-permute-start | bytes 3145736 | tf_op jit(solution)/shard_map/ppermute | solution.py:673
  142.2 8.3 %collective-permute-start.6 = (bf16[2,64,2048]{2,1,0:T(8,128)(2,1)S(1)}, bf16[2,64,2048]{2,1,0:T(8,128)(2,1)S(1)}, u32[]{:S(2)}, u32[]{:S(2)}) collective-permute-start(bf16[2,64,2048]{2,1,0:T(8,128)(2,1)S(1)} %constant_dynamic-slice_fusion.4), channel_id=1, source_target_pairs={{0,8},{2,6},{8,16},{10,2},{16,24},{18,10},{24,28},{26,18},{28,20},... | collective-permute-start | bytes 1572872 | tf_op jit(solution)/shard_map/ppermute | solution.py:673
  151.4 76.7 %all-to-all-start.2 = ((bf16[16,768,128]{2,1,0:T(8,128)(2,1)}), bf16[16,768,128]{2,1,0:T(8,128)(2,1)S(1)}, u32[]{:S(2)}, u32[]{:S(2)}) async-start(bf16[16,768,128]{2,1,0:T(8,128)(2,1)} %pack_both.1), calls=%async_computation.2 | async-start | bytes 6291456 | tf_op jit(solution)/shard_map/all_to_all | solution.py:729
  158.3 10.5 %collective-permute-start.10 = (bf16[2,128,2048]{2,1,0:T(8,128)(2,1)}, bf16[2,128,2048]{2,1,0:T(8,128)(2,1)}, u32[]{:S(2)}, u32[]{:S(2)}) collective-permute-start(bf16[2,128,2048]{2,1,0:T(8,128)(2,1)} %collective-permute-done.1.refs_11_.refs_18_), channel_id=1, source_target_pairs={{0,2},{2,0},{4,6},{6,4},{8,10},{10,8},{12,14},{14,12},{16,18},{18,... | collective-permute-start | bytes 3145736 | tf_op jit(solution)/shard_map/ppermute | solution.py:676
  158.6 10.1 %collective-permute-start.11 = (bf16[2,128,2048]{2,1,0:T(8,128)(2,1)}, bf16[2,128,2048]{2,1,0:T(8,128)(2,1)}, u32[]{:S(2)}, u32[]{:S(2)}) collective-permute-start(bf16[2,128,2048]{2,1,0:T(8,128)(2,1)} %collective-permute-done.3.refs_12_.refs_19_), channel_id=1, source_target_pairs={{0,2},{2,0},{4,6},{6,4},{8,10},{10,8},{12,14},{14,12},{16,18},{18,... | collective-permute-start | bytes 3145736 | tf_op jit(solution)/shard_map/ppermute | solution.py:676
  158.8 10.0 %collective-permute-start.12 = (bf16[2,128,2048]{2,1,0:T(8,128)(2,1)}, bf16[2,128,2048]{2,1,0:T(8,128)(2,1)}, u32[]{:S(2)}, u32[]{:S(2)}) collective-permute-start(bf16[2,128,2048]{2,1,0:T(8,128)(2,1)} %copy-done.30), channel_id=1, source_target_pairs={{0,2},{2,0},{4,6},{6,4},{8,10},{10,8},{12,14},{14,12},{16,18},{18,... | collective-permute-start | bytes 3145736 | tf_op jit(solution)/shard_map/ppermute | solution.py:676
  162.9 5.9 collective-permute-start.13
  198.1 33.8 %collective-permute-start.14 = (bf16[448,2048]{1,0:T(8,128)(2,1)}, bf16[448,2048]{1,0:T(8,128)(2,1)}, u32[]{:S(2)}, u32[]{:S(2)}) collective-permute-start(bf16[448,2048]{1,0:T(8,128)(2,1)} %get-tuple-element.94), channel_id=1, source_target_pairs={{0,2},{2,0},{4,6},{6,4},{8,10},{10,8},{12,14},{14,12},{16,18},{18,... | collective-permute-start | bytes 5505032 | tf_op jit(solution)/shard_map/ppermute | solution.py:676
  228.0 3.5 collective-permute-start.15
  230.4 35.8 %collective-permute-start.7 = (bf16[8,768,128]{2,1,0:T(8,128)(2,1)S(1)}, bf16[8,768,128]{2,1,0:T(8,128)(2,1)S(1)}, u32[]{:S(2)}, u32[]{:S(2)}) collective-permute-start(bf16[8,768,128]{2,1,0:T(8,128)(2,1)S(1)} %get-tuple-element.225), channel_id=1, source_target_pairs={{0,1},{1,0},{2,3},{3,2},{4,5},{5,4},{6,7},{7,6},{8,9},{9,8},{10,11... | collective-permute-start | bytes 4718600 | tf_op jit(solution)/shard_map/ppermute | solution.py:679
  231.7 5.7 collective-permute-start.16
  238.7 8.4 %collective-permute-start.17 = (bf16[1,128,2048]{2,1,0:T(8,128)(2,1)S(1)}, bf16[1,128,2048]{2,1,0:T(8,128)(2,1)S(1)}, u32[]{:S(2)}, u32[]{:S(2)}) collective-permute-start(bf16[1,128,2048]{2,1,0:T(8,128)(2,1)S(1)} %fusion.7), channel_id=1, source_target_pairs={{0,8},{2,6},{8,16},{10,2},{16,24},{18,10},{24,28},{26,18},{28,20},... | collective-permute-start | bytes 1572872 | tf_op jit(solution)/shard_map/ppermute | solution.py:673
  267.9 8.4 %collective-permute-start.18 = (bf16[1,128,2048]{2,1,0:T(8,128)(2,1)S(1)}, bf16[1,128,2048]{2,1,0:T(8,128)(2,1)S(1)}, u32[]{:S(2)}, u32[]{:S(2)}) collective-permute-start(bf16[1,128,2048]{2,1,0:T(8,128)(2,1)S(1)} %fusion.6), channel_id=1, source_target_pairs={{0,8},{2,6},{8,16},{10,2},{16,24},{18,10},{24,28},{26,18},{28,20},... | collective-permute-start | bytes 1572872 | tf_op jit(solution)/shard_map/ppermute | solution.py:673
  278.3 8.5 %collective-permute-start.19 = (bf16[1,128,2048]{2,1,0:T(8,128)(2,1)}, bf16[1,128,2048]{2,1,0:T(8,128)(2,1)S(1)}, u32[]{:S(2)}, u32[]{:S(2)}) collective-permute-start(bf16[1,128,2048]{2,1,0:T(8,128)(2,1)} %fusion.5), channel_id=1, source_target_pairs={{0,8},{2,6},{8,16},{10,2},{16,24},{18,10},{24,28},{26,18},{28,20},... | collective-permute-start | bytes 1572872 | tf_op jit(solution)/shard_map/ppermute | solution.py:673
  278.3 34.3 %collective-permute-start.8 = (bf16[8,768,128]{2,1,0:T(8,128)(2,1)}, bf16[8,768,128]{2,1,0:T(8,128)(2,1)S(1)}, u32[]{:S(2)}, u32[]{:S(2)}) collective-permute-start(bf16[8,768,128]{2,1,0:T(8,128)(2,1)} %get-tuple-element.224), channel_id=1, source_target_pairs={{0,1},{1,0},{2,3},{3,2},{4,5},{5,4},{6,7},{7,6},{8,9},{9,8},{10,11... | collective-permute-start | bytes 4718600 | tf_op jit(solution)/shard_map/ppermute | solution.py:679
  287.6 4.1 collective-permute-start.20
  297.8 14.9 %collective-permute-start.22 = (bf16[128,2048]{1,0:T(8,128)(2,1)S(1)}, bf16[128,2048]{1,0:T(8,128)(2,1)}, u32[]{:S(2)}, u32[]{:S(2)}) collective-permute-start(bf16[128,2048]{1,0:T(8,128)(2,1)S(1)} %maximum_select_fusion.refs_8_), channel_id=1, source_target_pairs={{0,8},{2,6},{8,16},{10,2},{16,24},{18,10},{24,28},{26,18},{28,20},... | collective-permute-start | bytes 1572872 | tf_op jit(solution)/shard_map/ppermute | solution.py:673
  312.7 10.4 %collective-permute-start.23 = (bf16[128,2048]{1,0:T(8,128)(2,1)}, bf16[128,2048]{1,0:T(8,128)(2,1)}, u32[]{:S(2)}, u32[]{:S(2)}) collective-permute-start(bf16[128,2048]{1,0:T(8,128)(2,1)} %collective-permute-done.22.refs_9_), channel_id=1, source_target_pairs={{0,8},{2,6},{8,16},{10,2},{16,24},{18,10},{24,28},{26,18},{28,20},... | collective-permute-start | bytes 1572872 | tf_op jit(solution)/shard_map/ppermute | solution.py:673
  323.0 8.5 %collective-permute-start.24 = (bf16[128,2048]{1,0:T(8,128)(2,1)}, bf16[128,2048]{1,0:T(8,128)(2,1)S(1)}, u32[]{:S(2)}, u32[]{:S(2)}) collective-permute-start(bf16[128,2048]{1,0:T(8,128)(2,1)} %collective-permute-done.23.refs_10_), channel_id=1, source_target_pairs={{0,8},{2,6},{8,16},{10,2},{16,24},{18,10},{24,28},{26,18},{28,20},... | collective-permute-start | bytes 1572872 | tf_op jit(solution)/shard_map/ppermute | solution.py:673
  323.0 24.0 %collective-permute-start.25 = (bf16[128,2048]{1,0:T(8,128)(2,1)}, bf16[128,2048]{1,0:T(8,128)(2,1)}, u32[]{:S(2)}, u32[]{:S(2)}) collective-permute-start(bf16[128,2048]{1,0:T(8,128)(2,1)} %collective-permute-done.22.refs_9_), channel_id=1, source_target_pairs={{0,2},{2,0},{4,6},{6,4},{8,10},{10,8},{12,14},{14,12},{16,18},{18,... | collective-permute-start | bytes 1572872 | tf_op jit(solution)/shard_map/ppermute | solution.py:676
  326.6 20.5 %collective-permute-start.26 = (bf16[128,2048]{1,0:T(8,128)(2,1)}, bf16[128,2048]{1,0:T(8,128)(2,1)}, u32[]{:S(2)}, u32[]{:S(2)}) collective-permute-start(bf16[128,2048]{1,0:T(8,128)(2,1)} %collective-permute-done.23.refs_10_), channel_id=1, source_target_pairs={{0,2},{2,0},{4,6},{6,4},{8,10},{10,8},{12,14},{14,12},{16,18},{18,... | collective-permute-start | bytes 1572872 | tf_op jit(solution)/shard_map/ppermute | solution.py:676
  331.6 5.3 collective-permute-start.28
  331.7 15.4 %collective-permute-start.27 = (bf16[128,2048]{1,0:T(8,128)(2,1)S(1)}, bf16[128,2048]{1,0:T(8,128)(2,1)}, u32[]{:S(2)}, u32[]{:S(2)}) collective-permute-start(bf16[128,2048]{1,0:T(8,128)(2,1)S(1)} %collective-permute-done.24.refs_11_), channel_id=1, source_target_pairs={{0,2},{2,0},{4,6},{6,4},{8,10},{10,8},{12,14},{14,12},{16,18},{18,... | collective-permute-start | bytes 1572872 | tf_op jit(solution)/shard_map/ppermute | solution.py:676
  336.9 10.2 %collective-permute-start.29 = (bf16[64,2048]{1,0:T(8,128)(2,1)S(1)}, bf16[64,2048]{1,0:T(8,128)(2,1)S(1)}, u32[]{:S(2)}, u32[]{:S(2)}) collective-permute-start(bf16[64,2048]{1,0:T(8,128)(2,1)S(1)} %collective-permute-done.28.refs_15_), channel_id=1, source_target_pairs={{0,2},{2,0},{4,6},{6,4},{8,10},{10,8},{12,14},{14,12},{16,18},{18,... | collective-permute-start | bytes 786440 | tf_op jit(solution)/shard_map/ppermute | solution.py:676
  383.8 10.0 %collective-permute-start.34 = (bf16[448,2048]{1,0:T(8,128)(2,1)}, bf16[448,2048]{1,0:T(8,128)(2,1)S(1)}, u32[]{:S(2)}, u32[]{:S(2)}) collective-permute-start(bf16[448,2048]{1,0:T(8,128)(2,1)} %get-tuple-element.105), channel_id=1, source_target_pairs={{0,2},{2,0},{4,6},{6,4},{8,10},{10,8},{12,14},{14,12},{16,18},{18,... | collective-permute-start | bytes 5505032 | tf_op jit(solution)/shard_map/ppermute | solution.py:676
  384.0 4.3 collective-permute-start.31
  384.4 11.1 %collective-permute-start.30 = (bf16[448,2048]{1,0:T(8,128)(2,1)}, bf16[448,2048]{1,0:T(8,128)(2,1)S(1)}, u32[]{:S(2)}, u32[]{:S(2)}) collective-permute-start(bf16[448,2048]{1,0:T(8,128)(2,1)} %get-tuple-element.101), channel_id=1, source_target_pairs={{0,2},{2,0},{4,6},{6,4},{8,10},{10,8},{12,14},{14,12},{16,18},{18,... | collective-permute-start | bytes 5505032 | tf_op jit(solution)/shard_map/ppermute | solution.py:676
  384.5 6.8 collective-permute-start.32
  392.3 8.4 %collective-permute-start.33 = (bf16[2,64,2048]{2,1,0:T(8,128)(2,1)S(1)}, bf16[2,64,2048]{2,1,0:T(8,128)(2,1)S(1)}, u32[]{:S(2)}, u32[]{:S(2)}) collective-permute-start(bf16[2,64,2048]{2,1,0:T(8,128)(2,1)S(1)} %pad_maximum_fusion.1), channel_id=1, source_target_pairs={{0,8},{2,6},{8,16},{10,2},{16,24},{18,10},{24,28},{26,18},{28,20},... | collective-permute-start | bytes 1572872 | tf_op jit(solution)/shard_map/ppermute | solution.py:673
  402.1 14.3 %collective-permute-start.35 = (bf16[2,128,2048]{2,1,0:T(8,128)(2,1)}, bf16[2,128,2048]{2,1,0:T(8,128)(2,1)}, u32[]{:S(2)}, u32[]{:S(2)}) collective-permute-start(bf16[2,128,2048]{2,1,0:T(8,128)(2,1)} %fusion), channel_id=1, source_target_pairs={{0,8},{2,6},{8,16},{10,2},{16,24},{18,10},{24,28},{26,18},{28,20},... | collective-permute-start | bytes 3145736 | tf_op jit(solution)/shard_map/ppermute | solution.py:673
  418.8 14.3 %collective-permute-start.36 = (bf16[2,128,2048]{2,1,0:T(8,128)(2,1)}, bf16[2,128,2048]{2,1,0:T(8,128)(2,1)S(1)}, u32[]{:S(2)}, u32[]{:S(2)}) collective-permute-start(bf16[2,128,2048]{2,1,0:T(8,128)(2,1)} %fusion.1), channel_id=1, source_target_pairs={{0,8},{2,6},{8,16},{10,2},{16,24},{18,10},{24,28},{26,18},{28,20},... | collective-permute-start | bytes 3145736 | tf_op jit(solution)/shard_map/ppermute | solution.py:673
  433.5 14.1 %collective-permute-start.37 = (bf16[2,128,2048]{2,1,0:T(8,128)(2,1)S(1)}, bf16[2,128,2048]{2,1,0:T(8,128)(2,1)S(1)}, u32[]{:S(2)}, u32[]{:S(2)}) collective-permute-start(bf16[2,128,2048]{2,1,0:T(8,128)(2,1)S(1)} %fusion.2), channel_id=1, source_target_pairs={{0,8},{2,6},{8,16},{10,2},{16,24},{18,10},{24,28},{26,18},{28,20},... | collective-permute-start | bytes 3145736 | tf_op jit(solution)/shard_map/ppermute | solution.py:673
  434.9 27.6 %collective-permute-start.42 = (bf16[16,320,128]{2,1,0:T(8,128)(2,1)}, bf16[16,320,128]{2,1,0:T(8,128)(2,1)}, u32[]{:S(2)}, u32[]{:S(2)}) collective-permute-start(bf16[16,320,128]{2,1,0:T(8,128)(2,1)} %get-tuple-element.120), channel_id=1, source_target_pairs={{0,1},{1,0},{2,3},{3,2},{4,5},{5,4},{6,7},{7,6},{8,9},{9,8},{10,11... | collective-permute-start | bytes 3932168 | tf_op jit(solution)/shard_map/ppermute | solution.py:679
  447.6 5.1 collective-permute-start.38
  451.1 65.3 %collective-permute-start.45 = (bf16[16,464,128]{2,1,0:T(8,128)(2,1)}, bf16[16,464,128]{2,1,0:T(8,128)(2,1)}, u32[]{:S(2)}, u32[]{:S(2)}) collective-permute-start(bf16[16,464,128]{2,1,0:T(8,128)(2,1)} %get-tuple-element.122), channel_id=1, source_target_pairs={{0,1},{1,0},{2,3},{3,2},{4,5},{5,4},{6,7},{7,6},{8,9},{9,8},{10,11... | collective-permute-start | bytes 5701640 | tf_op jit(solution)/shard_map/ppermute | solution.py:679
  456.5 21.0 %collective-permute-start.41 = (bf16[64,2048]{1,0:T(8,128)(2,1)}, bf16[64,2048]{1,0:T(8,128)(2,1)S(1)}, u32[]{:S(2)}, u32[]{:S(2)}) collective-permute-start(bf16[64,2048]{1,0:T(8,128)(2,1)} %get-tuple-element.119), channel_id=1, source_target_pairs={{0,2},{2,0},{4,6},{6,4},{8,10},{10,8},{12,14},{14,12},{16,18},{18,... | collective-permute-start | bytes 786440 | tf_op jit(solution)/shard_map/ppermute | solution.py:676
  465.3 65.4 %all-to-all-start.3 = ((bf16[16,320,128]{2,1,0:T(8,128)(2,1)}), bf16[16,320,128]{2,1,0:T(8,128)(2,1)S(1)}, u32[]{:S(2)}, u32[]{:S(2)}) async-start(bf16[16,320,128]{2,1,0:T(8,128)(2,1)} %add_convert_fusion.3), calls=%async_computation.3 | async-start | bytes 2621440 | tf_op jit(solution)/shard_map/all_to_all | solution.py:729
  478.4 33.7 %collective-permute-start.43 = (bf16[128,2048]{1,0:T(8,128)(2,1)}, bf16[128,2048]{1,0:T(8,128)(2,1)}, u32[]{:S(2)}, u32[]{:S(2)}) collective-permute-start(bf16[128,2048]{1,0:T(8,128)(2,1)} %maximum_select_fusion.2.rest_0_.refs_10_), channel_id=1, source_target_pairs={{0,8},{2,6},{8,16},{10,2},{16,24},{18,10},{24,28},{26,18},{28,20},... | collective-permute-start | bytes 1572872 | tf_op jit(solution)/shard_map/ppermute | solution.py:673
  481.8 32.1 %collective-permute-start.39 = (bf16[64,2048]{1,0:T(8,128)(2,1)}, bf16[64,2048]{1,0:T(8,128)(2,1)S(1)}, u32[]{:S(2)}, u32[]{:S(2)}) collective-permute-start(bf16[64,2048]{1,0:T(8,128)(2,1)} %forward_out.1), channel_id=1, source_target_pairs={{0,2},{2,0},{4,6},{6,4},{8,10},{10,8},{12,14},{14,12},{16,18},{18,... | collective-permute-start | bytes 786440 | tf_op jit(solution)/shard_map/ppermute | solution.py:676
  512.1 8.5 %collective-permute-start.44 = (bf16[128,2048]{1,0:T(8,128)(2,1)}, bf16[128,2048]{1,0:T(8,128)(2,1)S(1)}, u32[]{:S(2)}, u32[]{:S(2)}) collective-permute-start(bf16[128,2048]{1,0:T(8,128)(2,1)} %collective-permute-done.43.rest_1_.refs_11_), channel_id=1, source_target_pairs={{0,8},{2,6},{8,16},{10,2},{16,24},{18,10},{24,28},{26,18},{28,20},... | collective-permute-start | bytes 1572872 | tf_op jit(solution)/shard_map/ppermute | solution.py:673
  515.1 13.1 %collective-permute-start.40 = (bf16[128,2048]{1,0:T(8,128)(2,1)S(1)}, bf16[128,2048]{1,0:T(8,128)(2,1)S(1)}, u32[]{:S(2)}, u32[]{:S(2)}) collective-permute-start(bf16[128,2048]{1,0:T(8,128)(2,1)S(1)} %maximum_select_fusion.1), channel_id=1, source_target_pairs={{0,1},{1,0},{2,3},{3,2},{4,5},{5,4},{6,7},{7,6},{8,9},{9,8},{10,11... | collective-permute-start | bytes 1572872 | tf_op jit(solution)/shard_map/ppermute | solution.py:679
  520.6 8.5 %collective-permute-start.46 = (bf16[128,2048]{1,0:T(8,128)(2,1)S(1)}, bf16[128,2048]{1,0:T(8,128)(2,1)S(1)}, u32[]{:S(2)}, u32[]{:S(2)}) collective-permute-start(bf16[128,2048]{1,0:T(8,128)(2,1)S(1)} %collective-permute-done.44.rest_2_.refs_12_), channel_id=1, source_target_pairs={{0,8},{2,6},{8,16},{10,2},{16,24},{18,10},{24,28},{26,18},{28,20},... | collective-permute-start | bytes 1572872 | tf_op jit(solution)/shard_map/ppermute | solution.py:673
  530.7 5.5 collective-permute-start.50
  539.5 55.6 %all-to-all-start.4 = ((bf16[16,464,128]{2,1,0:T(8,128)(2,1)}), bf16[16,464,128]{2,1,0:T(8,128)(2,1)S(1)}, u32[]{:S(2)}, u32[]{:S(2)}) async-start(bf16[16,464,128]{2,1,0:T(8,128)(2,1)} %add_convert_fusion.1), calls=%async_computation.4 | async-start | bytes 3801088 | tf_op jit(solution)/shard_map/all_to_all | solution.py:729
  548.8 3.3 collective-permute-start.49
  562.0 30.4 %collective-permute-start.56 = (bf16[16,320,128]{2,1,0:T(8,128)(2,1)}, bf16[16,320,128]{2,1,0:T(8,128)(2,1)}, u32[]{:S(2)}, u32[]{:S(2)}) collective-permute-start(bf16[16,320,128]{2,1,0:T(8,128)(2,1)} %get-tuple-element.139), channel_id=1, source_target_pairs={{0,1},{1,0},{2,3},{3,2},{4,5},{5,4},{6,7},{7,6},{8,9},{9,8},{10,11... | collective-permute-start | bytes 3932168 | tf_op jit(solution)/shard_map/ppermute | solution.py:679
  589.8 27.5 %collective-permute-start.52 = (bf16[448,2048]{1,0:T(8,128)(2,1)}, bf16[448,2048]{1,0:T(8,128)(2,1)}, u32[]{:S(2)}, u32[]{:S(2)}) collective-permute-start(bf16[448,2048]{1,0:T(8,128)(2,1)} %get-tuple-element.130), channel_id=1, source_target_pairs={{0,2},{2,0},{4,6},{6,4},{8,10},{10,8},{12,14},{14,12},{16,18},{18,... | collective-permute-start | bytes 5505032 | tf_op jit(solution)/shard_map/ppermute | solution.py:676
  595.1 48.7 %all-to-all-start.5 = ((bf16[16,320,128]{2,1,0:T(8,128)(2,1)}), bf16[16,320,128]{2,1,0:T(8,128)(2,1)S(1)}, u32[]{:S(2)}, u32[]{:S(2)}) async-start(bf16[16,320,128]{2,1,0:T(8,128)(2,1)} %add_convert_fusion.2), calls=%async_computation.5 | async-start | bytes 2621440 | tf_op jit(solution)/shard_map/all_to_all | solution.py:729
  614.9 18.7 %collective-permute-start.54 = (bf16[1,64,2048]{2,1,0:T(8,128)(2,1)S(1)}, bf16[1,64,2048]{2,1,0:T(8,128)(2,1)S(1)}, u32[]{:S(2)}, u32[]{:S(2)}) collective-permute-start(bf16[1,64,2048]{2,1,0:T(8,128)(2,1)S(1)} %fusion.16), channel_id=1, source_target_pairs={{0,8},{2,6},{8,16},{10,2},{16,24},{18,10},{24,28},{26,18},{28,20},... | collective-permute-start | bytes 786440 | tf_op jit(solution)/shard_map/ppermute | solution.py:673
  616.1 43.5 %collective-permute-start.58 = (bf16[16,464,128]{2,1,0:T(8,128)(2,1)}, bf16[16,464,128]{2,1,0:T(8,128)(2,1)}, u32[]{:S(2)}, u32[]{:S(2)}) collective-permute-start(bf16[16,464,128]{2,1,0:T(8,128)(2,1)} %get-tuple-element.143), channel_id=1, source_target_pairs={{0,1},{1,0},{2,3},{3,2},{4,5},{5,4},{6,7},{7,6},{8,9},{9,8},{10,11... | collective-permute-start | bytes 5701640 | tf_op jit(solution)/shard_map/ppermute | solution.py:679
  635.0 8.7 %collective-permute-start.55 = (bf16[1,128,2048]{2,1,0:T(8,128)(2,1)S(1)}, bf16[1,128,2048]{2,1,0:T(8,128)(2,1)}, u32[]{:S(2)}, u32[]{:S(2)}) collective-permute-start(bf16[1,128,2048]{2,1,0:T(8,128)(2,1)S(1)} %fusion.8), channel_id=1, source_target_pairs={{0,8},{2,6},{8,16},{10,2},{16,24},{18,10},{24,28},{26,18},{28,20},... | collective-permute-start | bytes 1572872 | tf_op jit(solution)/shard_map/ppermute | solution.py:673
  645.8 13.9 %collective-permute-start.57 = (bf16[1,128,2048]{2,1,0:T(8,128)(2,1)S(1)}, bf16[1,128,2048]{2,1,0:T(8,128)(2,1)S(1)}, u32[]{:S(2)}, u32[]{:S(2)}) collective-permute-start(bf16[1,128,2048]{2,1,0:T(8,128)(2,1)S(1)} %fusion.4), channel_id=1, source_target_pairs={{0,8},{2,6},{8,16},{10,2},{16,24},{18,10},{24,28},{26,18},{28,20},... | collective-permute-start | bytes 1572872 | tf_op jit(solution)/shard_map/ppermute | solution.py:673
  660.9 8.5 %collective-permute-start.59 = (bf16[1,128,2048]{2,1,0:T(8,128)(2,1)S(1)}, bf16[1,128,2048]{2,1,0:T(8,128)(2,1)}, u32[]{:S(2)}, u32[]{:S(2)}) collective-permute-start(bf16[1,128,2048]{2,1,0:T(8,128)(2,1)S(1)} %fusion.3), channel_id=1, source_target_pairs={{0,8},{2,6},{8,16},{10,2},{16,24},{18,10},{24,28},{26,18},{28,20},... | collective-permute-start | bytes 1572872 | tf_op jit(solution)/shard_map/ppermute | solution.py:673
  669.4 49.4 %all-to-all-start.6 = ((bf16[16,464,128]{2,1,0:T(8,128)(2,1)}), bf16[16,464,128]{2,1,0:T(8,128)(2,1)S(1)}, u32[]{:S(2)}, u32[]{:S(2)}) async-start(bf16[16,464,128]{2,1,0:T(8,128)(2,1)} %add_convert_fusion), calls=%async_computation.6 | async-start | bytes 3801088 | tf_op jit(solution)/shard_map/all_to_all | solution.py:729
  676.8 9.1 %collective-permute-start.60 = (bf16[1,64,2048]{2,1,0:T(8,128)(2,1)S(1)}, bf16[1,64,2048]{2,1,0:T(8,128)(2,1)S(1)}, u32[]{:S(2)}, u32[]{:S(2)}) collective-permute-start(bf16[1,64,2048]{2,1,0:T(8,128)(2,1)S(1)} %constant_dynamic-slice_fusion.5), channel_id=1, source_target_pairs={{0,2},{2,0},{4,6},{6,4},{8,10},{10,8},{12,14},{14,12},{16,18},{18,... | collective-permute-start | bytes 786440 | tf_op jit(solution)/shard_map/ppermute | solution.py:676
  677.4 8.5 %collective-permute-start.61 = (f32[2,448]{1,0:T(2,128)S(1)}, f32[2,448]{1,0:T(2,128)S(1)}, u32[]{:S(2)}, u32[]{:S(2)}) collective-permute-start(f32[2,448]{1,0:T(2,128)S(1)} %pad_maximum_fusion.3), channel_id=1, source_target_pairs={{0,1},{1,0},{2,3},{3,2},{4,5},{5,4},{6,7},{7,6},{8,9},{9,8},{10,11... | collective-permute-start | bytes 10760 | tf_op jit(solution)/shard_map/ppermute | solution.py:679
  692.5 13.2 %collective-permute-start.63 = (bf16[128,2048]{1,0:T(8,128)(2,1)S(1)}, bf16[128,2048]{1,0:T(8,128)(2,1)S(1)}, u32[]{:S(2)}, u32[]{:S(2)}) collective-permute-start(bf16[128,2048]{1,0:T(8,128)(2,1)S(1)} %maximum_select_fusion.3), channel_id=1, source_target_pairs={{0,1},{1,0},{2,3},{3,2},{4,5},{5,4},{6,7},{7,6},{8,9},{9,8},{10,11... | collective-permute-start | bytes 1572872 | tf_op jit(solution)/shard_map/ppermute | solution.py:679
  (60 other events, 838.2 us)

commit v13 on v12

--- a/solution.py
+++ b/solution.py
@@ -116,11 +116,6 @@
     pack_up(qkv_ref, fc1_ref, out_ref)
     for d in range(MEMBERS):
         out_ref[d, UP_ROWS:] = small_ref[...]
-
-
-def pack_both(qkv_ref, fc1_ref, out_w_ref, fc2_ref, out_ref):
-    pack_up(qkv_ref, fc1_ref, out_ref)
-    pack_down(out_w_ref, fc2_ref, out_ref.at[:, UP_ROWS:])
 
 
 def pack_down(out_w_ref, fc2_ref, out_ref):
@@ -181,33 +176,9 @@
             out_ref[WIDE + n * 256 : WIDE + (n + 1) * 256, lanes] = ref[e, base + HEAD_DIM :]
 
 
-def join_both(own_ref, other_ref, up_ref, down_ref):
-    join_up(own_ref, other_ref, up_ref)
-    join_down(own_ref, other_ref, down_ref)
-
-
-def join_halves(own_ref, lower_ref, upper_ref, up_ref, down_ref):
-    lower = pl.program_id(0) < GROUP // MEMBERS // 2
-
-    @pl.when(lower)
-    def _():
-        join_both(own_ref, lower_ref, up_ref, down_ref)
-
-    @pl.when(jnp.logical_not(lower))
-    def _():
-        join_both(own_ref, upper_ref, up_ref, down_ref)
-
-
 def call_join(body, own, others, ups, downs):
     rows = own.shape[1]
-    steps = GROUP // MEMBERS
     spec = pl.BlockSpec((MEMBERS, rows, 128), lambda i: (i, 0, 0))
-    other_specs = [spec]
-    if len(others) == 2:
-        other_specs = [
-            pl.BlockSpec((MEMBERS, rows, 128), lambda i: (jnp.minimum(i, steps // 2 - 1), 0, 0)),
-            pl.BlockSpec((MEMBERS, rows, 128), lambda i: (jnp.maximum(i - steps // 2, 0), 0, 0)),
-        ]
     specs, shapes = [], []
     if ups:
         specs.append(pl.BlockSpec((MEMBERS * 128, 2 * UP_ROWS), lambda i: (i, 0)))
@@ -218,7 +189,7 @@
     return pl.pallas_call(
         body,
         grid=(GROUP // MEMBERS,),
-        in_specs=[spec] + other_specs,
+        in_specs=[spec] * (1 + len(others)),
         out_specs=specs,
         out_shape=shapes,
         cost_estimate=pl.CostEstimate(flops=0, bytes_accessed=GROUP * rows * 128 * 12, transcendentals=0),
@@ -749,7 +720,7 @@
         down = spread(after(packed_down, up))
         down_other = over(down)
         weights.append(call_join(join_up, up, [up_other], True, False) + call_join(join_down, down, [down_other], False, True))
-        packed_last = call_pack(pack_both, 1, ups, downs, ())
+        packed_last = (call_pack(pack_up, 1, ups, (), ()), call_pack(pack_down, 1, (), downs, ()))
         firsts = (up, up_other, down)
     else:
         small_all = lax.all_gather(small, "dp", axis=0, tiled=False)
@@ -843,27 +814,30 @@
     both = both * keeps[:, :, None]
     if groups == 1:
         inputs = gather_rows(
-            after(both, packed_down, packed_last, firsts[0], firsts[2]),
+            after(both, packed_down, *packed_last, firsts[0], firsts[2]),
             {1: (firsts[1], tables[0]), 2: (tables[1], tables[2], allowed), side: (down_other, weights[0][0])},
         )
-        slab = spread(after(packed_last, inputs[-2]))
-        others = tuple(over(slab[n * GROUP // 2 : (n + 1) * GROUP // 2]) for n in range(2))
-        weights.append(call_join(join_halves, slab, others, True, True))
-        slabs = (slab,)
+        up = spread(after(packed_last[0], inputs[-2]))
+        up_other = over(up)
     else:
         inputs = gather_rows(both)
-        slabs, others = (), ()
     mine_inputs = my_half(both, at, 1)
     state, grad_state = mine_inputs[0], mine_inputs[1]
 
     normed, heads, hidden_pre, wide, *parts = call_pass(
         "first", core_word, weights[0], tables, allowed, [bias_rows[0:1], gains[0], shifts[0]], inputs
     )
+    slabs, others = (), ()
+    if groups == 1:
+        down = spread(after(packed_last[1], up, parts[0]))
+        down_other = over(down)
+        weights.append(call_join(join_up, up, [up_other], True, False) + call_join(join_down, down, [down_other], False, True))
+        slabs, others = (down,), (up_other, down_other)
     rows_shape = (half, width)
     next_state, normed_own = call_end(
         partial(forward_end, False),
         core_word,
-        ring_sum((after(parts[0], *slabs), parts[1], parts[2]), needed={1: others[:1]})[0],
+        ring_sum((after(parts[0], *slabs), parts[1], parts[2]), needed={2: others[:1]})[0],
         [state, added_bias[0], gains[1], shifts[1]],
         [jax.ShapeDtypeStruct(rows_shape, f32), jax.ShapeDtypeStruct(rows_shape, bf16)],
         "forward_end",

time: 739 us -> 726 us (0.982)
  waiting for transfers between devices: 349 us -> 320 us
  starting transfers between devices: 116 us -> 128 us
    ppermute x12, waiting for transfers between devices: 83.1 us -> 65.3 us  [over(): return lax.ppermute(x, 'tensor', [(0, 1), (1, 0)])]
    ppermute x24, waiting for transfers between devices: 153 us -> 142 us  [along(): return lax.ppermute(x, 'dp', ring_pairs)]
    all_to_all x7 -> x8, starting transfers between devices: 52.1 us -> 55.9 us  [spread(): return lax.all_to_all(x, 'dp', 0, 0, axis_index_groups=inner, tiled=True)]
    pallas_call x3 -> x4, Pallas kernels: 11.9 us -> 14.9 us  [call_pack(): pl.pallas_call(body, grid=(GROUP // MEMBERS,), in_specs=specs, out_specs=...]
    pallas_call x3 -> x4, Pallas kernels: 15.4 us -> 17.9 us  [call_join(): pl.pallas_call(body, grid=(GROUP // MEMBERS,), in_specs=[spec] * (1 + len...]
    all_to_all x7 -> x8, waiting for transfers between devices: 99.5 us -> 97.6 us  [spread(): return lax.all_to_all(x, 'dp', 0, 0, axis_index_groups=inner, tiled=True)]
  transfers between devices with their start and end apart: 71 -> 72, of which waited for: 45 -> 46; matrix products, arithmetic and copies ran while one was open for 7% -> 7% of each run, Pallas kernels for 19% -> 20%
where the time goes in v13:
time: 726 us; the launch traced here: 714 us
  waiting for transfers between devices  320 us (44%)
  Pallas kernels  188 us (26%)
  starting transfers between devices  128 us (18%)
  other arithmetic  52.8 us (7%)
  local copies, waits for them, and re-layouts  23.2 us (3%)
    ppermute x24, waiting for transfers between devices, along(): return lax.ppermute(x, 'dp', ring_pairs)  142 us
    all_to_all x8, waiting for transfers between devices, spread(): return lax.all_to_all(x, 'dp', 0, 0, axis_index_groups=inner, tiled=True)  97.6 us
    pallas_call x3, Pallas kernels, call_pass(): pl.pallas_call(partial(layer_pass, mode), in_specs=[SMEM_SPEC] + [VMEM_SP...  92 us
    ppermute x12, waiting for transfers between devices, over(): return lax.ppermute(x, 'tensor', [(0, 1), (1, 0)])  65.3 us
    all_to_all x8, starting transfers between devices, spread(): return lax.all_to_all(x, 'dp', 0, 0, axis_index_groups=inner, tiled=True)  55.9 us
    pallas_call x4, Pallas kernels, call_gradients(): pl.pallas_call(partial(gradient_slabs, own_rows, other_rows, with_sums, l...  37.9 us
    ppermute x24, starting transfers between devices, along(): return lax.ppermute(x, 'dp', ring_pairs)  31.5 us
    ppermute x28, starting transfers between devices, across(): return lax.ppermute(x, 'dp', core_pairs)  27.2 us
  transfers between devices with their start and end apart: 72, of which 46 were waited for; matrix products, arithmetic and copies ran while one was open for 7% of the time, Pallas kernels for 20%

profile of v13, /device:TPU:13, one launch (start us, length us, event | category | flops | bytes accessed | tf_op | source)
XLA Modules:
  0.0 714.5 jit_solution(4846761594510222941)
XLA Ops:
  4.8 4.0 pack_first.1
  8.8 6.5 all-to-all-start
  15.3 3.5 pack_down.2
  18.9 39.7 %all-to-all-done.own_ref = bf16[16,464,128]{2,1,0:T(8,128)(2,1)S(1)} async-done(((bf16[16,464,128]{2,1,0:T(8,128)(2,1)}), bf16[16,464,128]{2,1,0:T(8,128)(2,1)S(1)}, u32[]{:S(2)}, u32[]{:S(2)}) %all-to-all-start) | async-done | bytes 1900576 | tf_op jit(solution)/shard_map/all_to_all | solution.py:700
  58.5 4.8 all-to-all-start.1
  69.3 3.5 pack_down.3
  72.9 3.9 pack_up.1
  79.5 14.8 %all-to-all-done.1.own_ref = bf16[16,320,128]{2,1,0:T(8,128)(2,1)S(1)} async-done(((bf16[16,320,128]{2,1,0:T(8,128)(2,1)}), bf16[16,320,128]{2,1,0:T(8,128)(2,1)S(1)}, u32[]{:S(2)}, u32[]{:S(2)}) %all-to-all-start.1) | async-done | bytes 1310752 | tf_op jit(solution)/shard_map/all_to_all | solution.py:700
  100.7 10.1 %collective-permute-done.2.other_ref = bf16[16,464,128]{2,1,0:T(8,128)(2,1)} collective-permute-done((bf16[16,464,128]{2,1,0:T(8,128)(2,1)S(1)}, bf16[16,464,128]{2,1,0:T(8,128)(2,1)}, u32[]{:S(2)}, u32[]{:S(2)}) %collective-permute-start.2) | collective-permute-done | bytes 1900576 | tf_op jit(solution)/shard_map/ppermute | solution.py:650
  118.0 7.1 collective-permute-done.3.refs_12_.refs_19_
  126.3 4.8 join_up.2.refs_1_
  131.1 8.2 %collective-permute-done.4.refs_13_.refs_20_ = bf16[2,128,2048]{2,1,0:T(8,128)(2,1)S(1)} collective-permute-done((bf16[2,128,2048]{2,1,0:T(8,128)(2,1)}, bf16[2,128,2048]{2,1,0:T(8,128)(2,1)S(1)}, u32[]{:S(2)}, u32[]{:S(2)}) %collective-permute-start.4) | collective-permute-done | bytes 1048608 | tf_op jit(solution)/shard_map/ppermute | solution.py:644
  139.3 2.9 collective-permute-done.5.other_ref
  143.4 7.1 collective-permute-done.6.refs_17_.refs_24_
  150.6 6.8 all-to-all-start.2
  163.8 4.2 join_down.2.refs_2_
  168.1 29.3 %pass_first.1 = (bf16[1024,2048]{1,0:T(8,128)(2,1)}, bf16[1024,384]{1,0:T(8,128)(2,1)}, f32[1024,512]{1,0:T(8,128)}, bf16[1024,640]{1,0:T(8,128)(2,1)}, bf16[64,...) custom-call(s32[1]{0:T(128)} %bitcast.refs_0_.core_ref, bf16[2048,896]{1,0:T(8,128)(2,1)} %join_up.2.refs_1_, ...), custom_call_target="tpu_custom_call" | custom-call | flops 19327352832 | bytes 20000000 | tf_op jit(solution)/shard_map/pass_first/pallas_call | solution.py:414
  199.3 4.8 all-to-all-start.3
  205.9 29.1 %all-to-all-done.3.own_ref = bf16[16,320,128]{2,1,0:T(8,128)(2,1)S(1)} async-done(((bf16[16,320,128]{2,1,0:T(8,128)(2,1)}), bf16[16,320,128]{2,1,0:T(8,128)(2,1)S(1)}, u32[]{:S(2)}, u32[]{:S(2)}) %all-to-all-start.3) | async-done | bytes 1310752 | tf_op jit(solution)/shard_map/all_to_all | solution.py:700
  237.1 8.4 %collective-permute-done.7.other_ref = bf16[16,448,128]{2,1,0:T(8,128)(2,1)} collective-permute-done((bf16[16,448,128]{2,1,0:T(8,128)(2,1)}, bf16[16,448,128]{2,1,0:T(8,128)(2,1)}, u32[]{:S(2)}, u32[]{:S(2)}) %collective-permute-start.7) | collective-permute-done | bytes 1835040 | tf_op jit(solution)/shard_map/ppermute | solution.py:650
  248.1 7.1 collective-permute-done.17
  257.7 7.1 collective-permute-done.18
  269.4 6.1 collective-permute-done.19.moving_ref
  276.3 3.8 collective-permute-start.20
  289.3 6.9 collective-permute-done.13.other_ref
  297.8 7.3 %collective-permute-done.23.refs_10_ = bf16[128,2048]{1,0:T(8,128)(2,1)S(1)} collective-permute-done((bf16[128,2048]{1,0:T(8,128)(2,1)}, bf16[128,2048]{1,0:T(8,128)(2,1)S(1)}, u32[]{:S(2)}, u32[]{:S(2)}) %collective-permute-start.23) | collective-permute-done | bytes 524320 | tf_op jit(solution)/shard_map/ppermute | solution.py:644
  306.3 3.0 collective-permute-start.25
  309.3 4.1 collective-permute-done.24.refs_11_
  314.7 3.9 collective-permute-start.27
  318.9 5.6 collective-permute-start.29
  324.5 4.8 join_up.3.refs_1_
  329.3 4.1 join_down.3.refs_2_
  334.2 36.1 %pass_middle.1 = (bf16[1024,2048]{1,0:T(8,128)(2,1)}, bf16[1024,2048]{1,0:T(8,128)(2,1)}, bf16[1024,640]{1,0:T(8,128)(2,1)}, bf16[1024,896]{1,0:T(8,128)(2,1)}, ...) custom-call(s32[1]{0:T(128)} %bitcast.refs_0_.core_ref, ...), custom_call_target="tpu_custom_call" | custom-call | flops 38654705664 | bytes 40000000 | tf_op jit(solution)/shard_map/pass_middle/pallas_call | solution.py:414
  371.5 3.3 collective-permute-done.31
  383.4 3.9 collective-permute-done.33
  389.8 8.8 %down_gradients.2 = (bf16[16,320,128]{2,1,0:T(8,128)(2,1)}, bf16[16,320,128]{2,1,0:T(8,128)(2,1)}) custom-call(s32[1]{0:T(128)} %bitcast.refs_0_.core_ref, bf16[1024,640]{1,0:T(8,128)(2,1)} %get-tuple-element.104.left_ref, bf16[1024,2048]{1,0:T(8,128)(2,1)} %get-tuple-element.105.rest_0_), custom_call_target="tpu_custom_call" | custom-call | flops 5368709120 | bytes 10747904 | tf_op jit(solution)/shard_map/down_gradients/pallas_call | solution.py:476
  398.7 4.2 collective-permute-done.35
  407.1 10.1 %up_gradients.2 = (bf16[16,464,128]{2,1,0:T(8,128)(2,1)}, bf16[16,464,128]{2,1,0:T(8,128)(2,1)}, f32[1,896]{1,0:T(1,128)}) custom-call(s32[1]{0:T(128)} %bitcast.refs_0_.core_ref, bf16[1024,896]{1,0:T(8,128)(2,1)} %get-tuple-element.108.left_ref, bf16[1024,2048]{1,0:T(8,128)(2,1)} %get-tuple-element.109.rest_0_, f32[16,2048]{1,0:T(8,128)} %get-tuple-element.110.rest_1_), custom_call_target="tpu_custom_call" | custom-call | flops 7516192768 | bytes 13369344 | tf_op jit(solution)/shard_map/up_gradients/pallas_call | solution.py:476
  422.8 11.7 %collective-permute-done.37.moving_ref = bf16[2,128,2048]{2,1,0:T(8,128)(2,1)S(1)} collective-permute-done((bf16[2,128,2048]{2,1,0:T(8,128)(2,1)S(1)}, bf16[2,128,2048]{2,1,0:T(8,128)(2,1)S(1)}, u32[]{:S(2)}, u32[]{:S(2)}) %collective-permute-start.37) | collective-permute-done | bytes 1048608 | tf_op jit(solution)/shard_map/ppermute | solution.py:644
  434.5 3.5 collective-permute-start.38
  440.3 3.0 backward_end.2
  443.7 6.4 collective-permute-done.42
  452.9 11.2 %all-to-all-start.4 = ((bf16[16,320,128]{2,1,0:T(8,128)(2,1)}), bf16[16,320,128]{2,1,0:T(8,128)(2,1)S(1)}, u32[]{:S(2)}, u32[]{:S(2)}) async-start(bf16[16,320,128]{2,1,0:T(8,128)(2,1)} %add_convert_fusion.3), calls=%async_computation.4 | async-start | bytes 2621440 | tf_op jit(solution)/shard_map/all_to_all | solution.py:700
  468.5 30.2 %collective-permute-done.43.rest_1_.refs_11_ = bf16[128,2048]{1,0:T(8,128)(2,1)} collective-permute-done((bf16[128,2048]{1,0:T(8,128)(2,1)}, bf16[128,2048]{1,0:T(8,128)(2,1)}, u32[]{:S(2)}, u32[]{:S(2)}) %collective-permute-start.43) | collective-permute-done | bytes 524320 | tf_op jit(solution)/shard_map/ppermute | solution.py:644
  503.1 4.2 collective-permute-done.44.rest_2_.refs_12_
  509.2 5.7 collective-permute-done.40
  519.1 3.8 collective-permute-done.50.rest_7_.refs_17_
  522.9 3.3 add_convert_fusion.1
  526.1 8.8 %all-to-all-start.5 = ((bf16[16,464,128]{2,1,0:T(8,128)(2,1)}), bf16[16,464,128]{2,1,0:T(8,128)(2,1)S(1)}, u32[]{:S(2)}, u32[]{:S(2)}) async-start(bf16[16,464,128]{2,1,0:T(8,128)(2,1)} %add_convert_fusion.1), calls=%async_computation.5 | async-start | bytes 3801088 | tf_op jit(solution)/shard_map/all_to_all | solution.py:700
  539.7 8.9 %down_gradients.3 = (bf16[16,320,128]{2,1,0:T(8,128)(2,1)}, bf16[16,320,128]{2,1,0:T(8,128)(2,1)}) custom-call(s32[1]{0:T(128)} %bitcast.refs_0_.core_ref, bf16[1024,640]{1,0:T(8,128)(2,1)} %get-tuple-element.116.left_ref, bf16[128,2048]{1,0:T(8,128)(2,1)} %maximum_select_fusion.2.rest_0_.refs_10_, ...), custom_call_target="tpu_custom_call" | custom-call | flops 5368709120 | bytes 10747904 | tf_op jit(solution)/shard_map/down_gradients/pallas_call | solution.py:476
  549.9 26.6 %pass_last.1 = (bf16[1024,2048]{1,0:T(8,128)(2,1)}, bf16[1024,896]{1,0:T(8,128)(2,1)}, f32[16,2048]{1,0:T(8,128)}, bf16[64,2048]{1,0:T(8,128)(2,1)}, bf16[448,20...) custom-call(s32[1]{0:T(128)} %bitcast.refs_0_.core_ref, bf16[2048,896]{1,0:T(8,128)(2,1)} %join_up.2.refs_1_, ...), custom_call_target="tpu_custom_call" | custom-call | flops 19327352832 | bytes 20000000 | tf_op jit(solution)/shard_map/pass_last/pallas_call | solution.py:414
  581.7 6.8 all-to-all-start.6
  588.5 10.1 %up_gradients.3 = (bf16[16,464,128]{2,1,0:T(8,128)(2,1)}, bf16[16,464,128]{2,1,0:T(8,128)(2,1)}, f32[1,896]{1,0:T(1,128)}) custom-call(s32[1]{0:T(128)} %bitcast.refs_0_.core_ref, bf16[1024,896]{1,0:T(8,128)(2,1)} %get-tuple-element.130.left_ref, bf16[1024,2048]{1,0:T(8,128)(2,1)} %get-tuple-element.133.refs_9_.rest_0_, f32[16,2048]{1,0:T(8,128)} %get-tuple-element.134.rest_1_), custom_call_target="tpu_custom_call" | custom-call | flops 7516192768 | bytes 13369344 | tf_op jit(solution)/shard_map/up_gradients/pallas_call | solution.py:476
  604.0 16.3 %collective-permute-done.54 = bf16[1,64,2048]{2,1,0:T(8,128)(2,1)S(1)} collective-permute-done((bf16[1,64,2048]{2,1,0:T(8,128)(2,1)S(1)}, bf16[1,64,2048]{2,1,0:T(8,128)(2,1)S(1)}, u32[]{:S(2)}, u32[]{:S(2)}) %collective-permute-start.54) | collective-permute-done | bytes 262176 | tf_op jit(solution)/shard_map/ppermute | solution.py:644
  624.3 6.1 collective-permute-done.55
  634.8 11.5 %collective-permute-done.58 = bf16[16,464,128]{2,1,0:T(8,128)(2,1)} collective-permute-done((bf16[16,464,128]{2,1,0:T(8,128)(2,1)}, bf16[16,464,128]{2,1,0:T(8,128)(2,1)}, u32[]{:S(2)}, u32[]{:S(2)}) %collective-permute-start.58) | collective-permute-done | bytes 1900576 | tf_op jit(solution)/shard_map/ppermute | solution.py:650
  648.8 3.3 add_convert_fusion
  652.1 4.0 collective-permute-done.59.moving_ref
  656.1 6.2 all-to-all-start.7
  665.2 7.3 %spread_gradients.2 = (f32[2,3,128,1024]{3,2,1,0:T(8,128)}, f32[2,1024,128]{2,1,0:T(8,128)}, f32[2,128,4096]{2,1,0:T(8,128)}, f32[2,4096,128]{2,1,0:T(8,128)}, f32[8,128]{1,0:T(8,128)}) custom-call(bf16[16,464,128]{2,1,0:T(8,128)(2,1)} %copy-done.1, bf16[16,320,128]{2,1,0:T(8,128)(2,1)} %copy-done.11), custom_call_target="tpu_custom_call" | custom-call | tf_op jit(solution)/shard_map/spread_gradients/pallas_call | solution.py:516
  673.3 2.9 backward_end.3
  682.4 9.9 %collective-permute-done.63 = bf16[128,2048]{1,0:T(8,128)(2,1)S(1)} collective-permute-done((bf16[128,2048]{1,0:T(8,128)(2,1)S(1)}, bf16[128,2048]{1,0:T(8,128)(2,1)S(1)}, u32[]{:S(2)}, u32[]{:S(2)}) %collective-permute-start.63) | collective-permute-done | bytes 524320 | tf_op jit(solution)/shard_map/ppermute | solution.py:650
  693.4 12.1 %all-to-all-done.7.up_ref = bf16[16,464,128]{2,1,0:T(8,128)(2,1)S(1)} async-done(((bf16[16,464,128]{2,1,0:T(8,128)(2,1)}), bf16[16,464,128]{2,1,0:T(8,128)(2,1)S(1)}, u32[]{:S(2)}, u32[]{:S(2)}) %all-to-all-start.7) | async-done | bytes 1900576 | tf_op jit(solution)/shard_map/all_to_all | solution.py:700
  706.7 7.3 %spread_gradients.3 = (f32[2,3,128,1024]{3,2,1,0:T(8,128)}, f32[2,1024,128]{2,1,0:T(8,128)}, f32[2,128,4096]{2,1,0:T(8,128)}, f32[2,4096,128]{2,1,0:T(8,128)}, f32[8,128]{1,0:T(8,128)}) custom-call(bf16[16,464,128]{2,1,0:T(8,128)(2,1)} %copy-done.2, ...), custom_call_target="tpu_custom_call", output_to_operand_aliasing={{0}: (2, {}), {1}: (3, {}), {2}: (4, {}), {3}: (5, {})} | custom-call | tf_op jit(solution)/shard_map/spread_gradients/pallas_call | solution.py:516
  (306 shorter events, 147.4 us)
Async XLA Ops:
  8.8 49.7 %all-to-all-start = ((bf16[16,464,128]{2,1,0:T(8,128)(2,1)}), bf16[16,464,128]{2,1,0:T(8,128)(2,1)S(1)}, u32[]{:S(2)}, u32[]{:S(2)}) async-start(bf16[16,464,128]{2,1,0:T(8,128)(2,1)} %pack_first.1), calls=%async_computation | async-start | bytes 3801088 | tf_op jit(solution)/shard_map/all_to_all | solution.py:700
  58.5 35.7 %all-to-all-start.1 = ((bf16[16,320,128]{2,1,0:T(8,128)(2,1)}), bf16[16,320,128]{2,1,0:T(8,128)(2,1)S(1)}, u32[]{:S(2)}, u32[]{:S(2)}) async-start(bf16[16,320,128]{2,1,0:T(8,128)(2,1)} %pack_down.2), calls=%async_computation.1 | async-start | bytes 2621440 | tf_op jit(solution)/shard_map/all_to_all | solution.py:700
  65.6 11.2 %collective-permute-start = (bf16[2,128,2048]{2,1,0:T(8,128)(2,1)}, bf16[2,128,2048]{2,1,0:T(8,128)(2,1)}, u32[]{:S(2)}, u32[]{:S(2)}) collective-permute-start(bf16[2,128,2048]{2,1,0:T(8,128)(2,1)} %pad_maximum_fusion), channel_id=1, source_target_pairs={{0,2},{2,0},{4,6},{6,4},{8,10},{10,8},{12,14},{14,12},{16,18},{18,... | collective-permute-start | bytes 3145736 | tf_op jit(solution)/shard_map/ppermute | solution.py:647
  67.9 43.0 %collective-permute-start.2 = (bf16[16,464,128]{2,1,0:T(8,128)(2,1)S(1)}, bf16[16,464,128]{2,1,0:T(8,128)(2,1)}, u32[]{:S(2)}, u32[]{:S(2)}) collective-permute-start(bf16[16,464,128]{2,1,0:T(8,128)(2,1)S(1)} %all-to-all-done.own_ref), channel_id=1, source_target_pairs={{0,1},{1,0},{2,3},{3,2},{4,5},{5,4},{6,7},{7,6},{8,9},{9,8},{10,11... | collective-permute-start | bytes 5701640 | tf_op jit(solution)/shard_map/ppermute | solution.py:650
  94.3 16.6 %collective-permute-start.1 = (bf16[2,128,2048]{2,1,0:T(8,128)(2,1)}, bf16[2,128,2048]{2,1,0:T(8,128)(2,1)}, u32[]{:S(2)}, u32[]{:S(2)}) collective-permute-start(bf16[2,128,2048]{2,1,0:T(8,128)(2,1)} %select_multiply_fusion.refs_10_.refs_17_), channel_id=1, source_target_pairs={{0,8},{2,6},{8,16},{10,2},{16,24},{18,10},{24,28},{26,18},{28,20},... | collective-permute-start | bytes 3145736 | tf_op jit(solution)/shard_map/ppermute | solution.py:644
  110.9 14.3 %collective-permute-start.3 = (bf16[2,128,2048]{2,1,0:T(8,128)(2,1)}, bf16[2,128,2048]{2,1,0:T(8,128)(2,1)}, u32[]{:S(2)}, u32[]{:S(2)}) collective-permute-start(bf16[2,128,2048]{2,1,0:T(8,128)(2,1)} %collective-permute-done.1.refs_11_.refs_18_), channel_id=1, source_target_pairs={{0,8},{2,6},{8,16},{10,2},{16,24},{18,10},{24,28},{26,18},{28,20},... | collective-permute-start | bytes 3145736 | tf_op jit(solution)/shard_map/ppermute | solution.py:644
  112.0 30.2 %collective-permute-start.5 = (bf16[16,320,128]{2,1,0:T(8,128)(2,1)}, bf16[16,320,128]{2,1,0:T(8,128)(2,1)S(1)}, u32[]{:S(2)}, u32[]{:S(2)}) collective-permute-start(bf16[16,320,128]{2,1,0:T(8,128)(2,1)} %copy-done.10), channel_id=1, source_target_pairs={{0,1},{1,0},{2,3},{3,2},{4,5},{5,4},{6,7},{7,6},{8,9},{9,8},{10,11... | collective-permute-start | bytes 3932168 | tf_op jit(solution)/shard_map/ppermute | solution.py:650
  125.1 14.2 %collective-permute-start.4 = (bf16[2,128,2048]{2,1,0:T(8,128)(2,1)}, bf16[2,128,2048]{2,1,0:T(8,128)(2,1)S(1)}, u32[]{:S(2)}, u32[]{:S(2)}) collective-permute-start(bf16[2,128,2048]{2,1,0:T(8,128)(2,1)} %collective-permute-done.3.refs_12_.refs_19_), channel_id=1, source_target_pairs={{0,8},{2,6},{8,16},{10,2},{16,24},{18,10},{24,28},{26,18},{28,20},... | collective-permute-start | bytes 3145736 | tf_op jit(solution)/shard_map/ppermute | solution.py:644
  142.2 8.3 %collective-permute-start.6 = (bf16[2,64,2048]{2,1,0:T(8,128)(2,1)S(1)}, bf16[2,64,2048]{2,1,0:T(8,128)(2,1)S(1)}, u32[]{:S(2)}, u32[]{:S(2)}) collective-permute-start(bf16[2,64,2048]{2,1,0:T(8,128)(2,1)S(1)} %constant_dynamic-slice_fusion.4), channel_id=1, source_target_pairs={{0,8},{2,6},{8,16},{10,2},{16,24},{18,10},{24,28},{26,18},{28,20},... | collective-permute-start | bytes 1572872 | tf_op jit(solution)/shard_map/ppermute | solution.py:644
  150.6 48.7 %all-to-all-start.2 = ((bf16[16,448,128]{2,1,0:T(8,128)(2,1)}), bf16[16,448,128]{2,1,0:T(8,128)(2,1)}, u32[]{:S(2)}, u32[]{:S(2)}) async-start(bf16[16,448,128]{2,1,0:T(8,128)(2,1)} %pack_up.1), calls=%async_computation.2 | async-start | bytes 3670016 | tf_op jit(solution)/shard_map/all_to_all | solution.py:700
  157.5 10.6 %collective-permute-start.9 = (bf16[2,128,2048]{2,1,0:T(8,128)(2,1)}, bf16[2,128,2048]{2,1,0:T(8,128)(2,1)}, u32[]{:S(2)}, u32[]{:S(2)}) collective-permute-start(bf16[2,128,2048]{2,1,0:T(8,128)(2,1)} %collective-permute-done.1.refs_11_.refs_18_), channel_id=1, source_target_pairs={{0,2},{2,0},{4,6},{6,4},{8,10},{10,8},{12,14},{14,12},{16,18},{18,... | collective-permute-start | bytes 3145736 | tf_op jit(solution)/shard_map/ppermute | solution.py:647
  157.9 10.2 %collective-permute-start.10 = (bf16[2,128,2048]{2,1,0:T(8,128)(2,1)}, bf16[2,128,2048]{2,1,0:T(8,128)(2,1)}, u32[]{:S(2)}, u32[]{:S(2)}) collective-permute-start(bf16[2,128,2048]{2,1,0:T(8,128)(2,1)} %collective-permute-done.3.refs_12_.refs_19_), channel_id=1, source_target_pairs={{0,2},{2,0},{4,6},{6,4},{8,10},{10,8},{12,14},{14,12},{16,18},{18,... | collective-permute-start | bytes 3145736 | tf_op jit(solution)/shard_map/ppermute | solution.py:647
  158.0 10.1 %collective-permute-start.11 = (bf16[2,128,2048]{2,1,0:T(8,128)(2,1)S(1)}, bf16[2,128,2048]{2,1,0:T(8,128)(2,1)}, u32[]{:S(2)}, u32[]{:S(2)}) collective-permute-start(bf16[2,128,2048]{2,1,0:T(8,128)(2,1)S(1)} %collective-permute-done.4.refs_13_.refs_20_), channel_id=1, source_target_pairs={{0,2},{2,0},{4,6},{6,4},{8,10},{10,8},{12,14},{14,12},{16,18},{18,... | collective-permute-start | bytes 3145736 | tf_op jit(solution)/shard_map/ppermute | solution.py:647
  162.2 5.9 collective-permute-start.12
  199.3 35.7 %all-to-all-start.3 = ((bf16[16,320,128]{2,1,0:T(8,128)(2,1)}), bf16[16,320,128]{2,1,0:T(8,128)(2,1)S(1)}, u32[]{:S(2)}, u32[]{:S(2)}) async-start(bf16[16,320,128]{2,1,0:T(8,128)(2,1)} %pack_down.3), calls=%async_computation.3 | async-start | bytes 2621440 | tf_op jit(solution)/shard_map/all_to_all | solution.py:700
  204.0 41.5 %collective-permute-start.7 = (bf16[16,448,128]{2,1,0:T(8,128)(2,1)}, bf16[16,448,128]{2,1,0:T(8,128)(2,1)}, u32[]{:S(2)}, u32[]{:S(2)}) collective-permute-start(bf16[16,448,128]{2,1,0:T(8,128)(2,1)} %all-to-all-done.2.own_ref), channel_id=1, source_target_pairs={{0,1},{1,0},{2,3},{3,2},{4,5},{5,4},{6,7},{7,6},{8,9},{9,8},{10,11... | collective-permute-start | bytes 5505032 | tf_op jit(solution)/shard_map/ppermute | solution.py:650
  205.3 40.3 %collective-permute-start.14 = (bf16[448,2048]{1,0:T(8,128)(2,1)}, bf16[448,2048]{1,0:T(8,128)(2,1)}, u32[]{:S(2)}, u32[]{:S(2)}) collective-permute-start(bf16[448,2048]{1,0:T(8,128)(2,1)} %get-tuple-element.93), channel_id=1, source_target_pairs={{0,2},{2,0},{4,6},{6,4},{8,10},{10,8},{12,14},{14,12},{16,18},{18,... | collective-permute-start | bytes 5505032 | tf_op jit(solution)/shard_map/ppermute | solution.py:647
  236.8 8.7 %collective-permute-start.16 = (bf16[1,64,2048]{2,1,0:T(8,128)(2,1)S(1)}, bf16[1,64,2048]{2,1,0:T(8,128)(2,1)S(1)}, u32[]{:S(2)}, u32[]{:S(2)}) collective-permute-start(bf16[1,64,2048]{2,1,0:T(8,128)(2,1)S(1)} %fusion.13), channel_id=1, source_target_pairs={{0,8},{2,6},{8,16},{10,2},{16,24},{18,10},{24,28},{26,18},{28,20},... | collective-permute-start | bytes 786440 | tf_op jit(solution)/shard_map/ppermute | solution.py:644
  246.8 8.4 %collective-permute-start.17 = (bf16[1,128,2048]{2,1,0:T(8,128)(2,1)S(1)}, bf16[1,128,2048]{2,1,0:T(8,128)(2,1)S(1)}, u32[]{:S(2)}, u32[]{:S(2)}) collective-permute-start(bf16[1,128,2048]{2,1,0:T(8,128)(2,1)S(1)} %fusion.7), channel_id=1, source_target_pairs={{0,8},{2,6},{8,16},{10,2},{16,24},{18,10},{24,28},{26,18},{28,20},... | collective-permute-start | bytes 1572872 | tf_op jit(solution)/shard_map/ppermute | solution.py:644
  256.5 8.4 %collective-permute-start.18 = (bf16[1,128,2048]{2,1,0:T(8,128)(2,1)S(1)}, bf16[1,128,2048]{2,1,0:T(8,128)(2,1)S(1)}, u32[]{:S(2)}, u32[]{:S(2)}) collective-permute-start(bf16[1,128,2048]{2,1,0:T(8,128)(2,1)S(1)} %fusion.6), channel_id=1, source_target_pairs={{0,8},{2,6},{8,16},{10,2},{16,24},{18,10},{24,28},{26,18},{28,20},... | collective-permute-start | bytes 1572872 | tf_op jit(solution)/shard_map/ppermute | solution.py:644
  267.0 8.5 %collective-permute-start.19 = (bf16[1,128,2048]{2,1,0:T(8,128)(2,1)}, bf16[1,128,2048]{2,1,0:T(8,128)(2,1)S(1)}, u32[]{:S(2)}, u32[]{:S(2)}) collective-permute-start(bf16[1,128,2048]{2,1,0:T(8,128)(2,1)} %fusion.5), channel_id=1, source_target_pairs={{0,8},{2,6},{8,16},{10,2},{16,24},{18,10},{24,28},{26,18},{28,20},... | collective-permute-start | bytes 1572872 | tf_op jit(solution)/shard_map/ppermute | solution.py:644
  268.2 28.1 %collective-permute-start.13 = (bf16[16,320,128]{2,1,0:T(8,128)(2,1)S(1)}, bf16[16,320,128]{2,1,0:T(8,128)(2,1)S(1)}, u32[]{:S(2)}, u32[]{:S(2)}) collective-permute-start(bf16[16,320,128]{2,1,0:T(8,128)(2,1)S(1)} %all-to-all-done.3.own_ref), channel_id=1, source_target_pairs={{0,1},{1,0},{2,3},{3,2},{4,5},{5,4},{6,7},{7,6},{8,9},{9,8},{10,11... | collective-permute-start | bytes 3932168 | tf_op jit(solution)/shard_map/ppermute | solution.py:650
  276.3 5.7 collective-permute-start.20
  288.1 8.5 %collective-permute-start.22 = (bf16[128,2048]{1,0:T(8,128)(2,1)S(1)}, bf16[128,2048]{1,0:T(8,128)(2,1)}, u32[]{:S(2)}, u32[]{:S(2)}) collective-permute-start(bf16[128,2048]{1,0:T(8,128)(2,1)S(1)} %maximum_select_fusion.refs_8_), channel_id=1, source_target_pairs={{0,8},{2,6},{8,16},{10,2},{16,24},{18,10},{24,28},{26,18},{28,20},... | collective-permute-start | bytes 1572872 | tf_op jit(solution)/shard_map/ppermute | solution.py:644
  296.6 8.5 %collective-permute-start.23 = (bf16[128,2048]{1,0:T(8,128)(2,1)}, bf16[128,2048]{1,0:T(8,128)(2,1)S(1)}, u32[]{:S(2)}, u32[]{:S(2)}) collective-permute-start(bf16[128,2048]{1,0:T(8,128)(2,1)} %collective-permute-done.22.refs_9_), channel_id=1, source_target_pairs={{0,8},{2,6},{8,16},{10,2},{16,24},{18,10},{24,28},{26,18},{28,20},... | collective-permute-start | bytes 1572872 | tf_op jit(solution)/shard_map/ppermute | solution.py:644
  305.1 8.3 %collective-permute-start.24 = (bf16[128,2048]{1,0:T(8,128)(2,1)S(1)}, bf16[128,2048]{1,0:T(8,128)(2,1)S(1)}, u32[]{:S(2)}, u32[]{:S(2)}) collective-permute-start(bf16[128,2048]{1,0:T(8,128)(2,1)S(1)} %collective-permute-done.23.refs_10_), channel_id=1, source_target_pairs={{0,8},{2,6},{8,16},{10,2},{16,24},{18,10},{24,28},{26,18},{28,20},... | collective-permute-start | bytes 1572872 | tf_op jit(solution)/shard_map/ppermute | solution.py:644
  306.3 27.1 %collective-permute-start.25 = (bf16[128,2048]{1,0:T(8,128)(2,1)}, bf16[128,2048]{1,0:T(8,128)(2,1)S(1)}, u32[]{:S(2)}, u32[]{:S(2)}) collective-permute-start(bf16[128,2048]{1,0:T(8,128)(2,1)} %collective-permute-done.22.refs_9_), channel_id=1, source_target_pairs={{0,2},{2,0},{4,6},{6,4},{8,10},{10,8},{12,14},{14,12},{16,18},{18,... | collective-permute-start | bytes 1572872 | tf_op jit(solution)/shard_map/ppermute | solution.py:647
  309.3 24.1 %collective-permute-start.26 = (bf16[128,2048]{1,0:T(8,128)(2,1)S(1)}, bf16[128,2048]{1,0:T(8,128)(2,1)}, u32[]{:S(2)}, u32[]{:S(2)}) collective-permute-start(bf16[128,2048]{1,0:T(8,128)(2,1)S(1)} %collective-permute-done.23.refs_10_), channel_id=1, source_target_pairs={{0,2},{2,0},{4,6},{6,4},{8,10},{10,8},{12,14},{14,12},{16,18},{18,... | collective-permute-start | bytes 1572872 | tf_op jit(solution)/shard_map/ppermute | solution.py:647
  313.5 5.4 collective-permute-start.28
  314.7 18.7 %collective-permute-start.27 = (bf16[128,2048]{1,0:T(8,128)(2,1)S(1)}, bf16[128,2048]{1,0:T(8,128)(2,1)}, u32[]{:S(2)}, u32[]{:S(2)}) collective-permute-start(bf16[128,2048]{1,0:T(8,128)(2,1)S(1)} %collective-permute-done.24.refs_11_), channel_id=1, source_target_pairs={{0,2},{2,0},{4,6},{6,4},{8,10},{10,8},{12,14},{14,12},{16,18},{18,... | collective-permute-start | bytes 1572872 | tf_op jit(solution)/shard_map/ppermute | solution.py:647
  318.9 14.6 %collective-permute-start.29 = (bf16[64,2048]{1,0:T(8,128)(2,1)}, bf16[64,2048]{1,0:T(8,128)(2,1)}, u32[]{:S(2)}, u32[]{:S(2)}) collective-permute-start(bf16[64,2048]{1,0:T(8,128)(2,1)} %collective-permute-done.28.refs_15_), channel_id=1, source_target_pairs={{0,2},{2,0},{4,6},{6,4},{8,10},{10,8},{12,14},{14,12},{16,18},{18,... | collective-permute-start | bytes 786440 | tf_op jit(solution)/shard_map/ppermute | solution.py:647
  370.4 9.8 %collective-permute-start.34 = (bf16[448,2048]{1,0:T(8,128)(2,1)}, bf16[448,2048]{1,0:T(8,128)(2,1)S(1)}, u32[]{:S(2)}, u32[]{:S(2)}) collective-permute-start(bf16[448,2048]{1,0:T(8,128)(2,1)} %get-tuple-element.103), channel_id=1, source_target_pairs={{0,2},{2,0},{4,6},{6,4},{8,10},{10,8},{12,14},{14,12},{16,18},{18,... | collective-permute-start | bytes 5505032 | tf_op jit(solution)/shard_map/ppermute | solution.py:647
  370.5 4.4 collective-permute-start.31
  371.0 10.8 %collective-permute-start.30 = (bf16[448,2048]{1,0:T(8,128)(2,1)}, bf16[448,2048]{1,0:T(8,128)(2,1)S(1)}, u32[]{:S(2)}, u32[]{:S(2)}) collective-permute-start(bf16[448,2048]{1,0:T(8,128)(2,1)} %get-tuple-element.99), channel_id=1, source_target_pairs={{0,2},{2,0},{4,6},{6,4},{8,10},{10,8},{12,14},{14,12},{16,18},{18,... | collective-permute-start | bytes 5505032 | tf_op jit(solution)/shard_map/ppermute | solution.py:647
  371.0 6.8 collective-permute-start.32
  378.9 8.4 %collective-permute-start.33 = (bf16[2,64,2048]{2,1,0:T(8,128)(2,1)S(1)}, bf16[2,64,2048]{2,1,0:T(8,128)(2,1)S(1)}, u32[]{:S(2)}, u32[]{:S(2)}) collective-permute-start(bf16[2,64,2048]{2,1,0:T(8,128)(2,1)S(1)} %pad_maximum_fusion.1), channel_id=1, source_target_pairs={{0,8},{2,6},{8,16},{10,2},{16,24},{18,10},{24,28},{26,18},{28,20},... | collective-permute-start | bytes 1572872 | tf_op jit(solution)/shard_map/ppermute | solution.py:644
  388.6 14.3 %collective-permute-start.35 = (bf16[2,128,2048]{2,1,0:T(8,128)(2,1)}, bf16[2,128,2048]{2,1,0:T(8,128)(2,1)}, u32[]{:S(2)}, u32[]{:S(2)}) collective-permute-start(bf16[2,128,2048]{2,1,0:T(8,128)(2,1)} %fusion), channel_id=1, source_target_pairs={{0,8},{2,6},{8,16},{10,2},{16,24},{18,10},{24,28},{26,18},{28,20},... | collective-permute-start | bytes 3145736 | tf_op jit(solution)/shard_map/ppermute | solution.py:644
  405.7 14.3 %collective-permute-start.36 = (bf16[2,128,2048]{2,1,0:T(8,128)(2,1)}, bf16[2,128,2048]{2,1,0:T(8,128)(2,1)S(1)}, u32[]{:S(2)}, u32[]{:S(2)}) collective-permute-start(bf16[2,128,2048]{2,1,0:T(8,128)(2,1)} %fusion.1), channel_id=1, source_target_pairs={{0,8},{2,6},{8,16},{10,2},{16,24},{18,10},{24,28},{26,18},{28,20},... | collective-permute-start | bytes 3145736 | tf_op jit(solution)/shard_map/ppermute | solution.py:644
  420.3 14.1 %collective-permute-start.37 = (bf16[2,128,2048]{2,1,0:T(8,128)(2,1)S(1)}, bf16[2,128,2048]{2,1,0:T(8,128)(2,1)S(1)}, u32[]{:S(2)}, u32[]{:S(2)}) collective-permute-start(bf16[2,128,2048]{2,1,0:T(8,128)(2,1)S(1)} %fusion.2), channel_id=1, source_target_pairs={{0,8},{2,6},{8,16},{10,2},{16,24},{18,10},{24,28},{26,18},{28,20},... | collective-permute-start | bytes 3145736 | tf_op jit(solution)/shard_map/ppermute | solution.py:644
  421.6 28.6 %collective-permute-start.42 = (bf16[16,320,128]{2,1,0:T(8,128)(2,1)}, bf16[16,320,128]{2,1,0:T(8,128)(2,1)}, u32[]{:S(2)}, u32[]{:S(2)}) collective-permute-start(bf16[16,320,128]{2,1,0:T(8,128)(2,1)} %get-tuple-element.118), channel_id=1, source_target_pairs={{0,1},{1,0},{2,3},{3,2},{4,5},{5,4},{6,7},{7,6},{8,9},{9,8},{10,11... | collective-permute-start | bytes 3932168 | tf_op jit(solution)/shard_map/ppermute | solution.py:650
  434.5 5.1 collective-permute-start.38
  438.0 65.1 %collective-permute-start.45 = (bf16[16,464,128]{2,1,0:T(8,128)(2,1)}, bf16[16,464,128]{2,1,0:T(8,128)(2,1)}, u32[]{:S(2)}, u32[]{:S(2)}) collective-permute-start(bf16[16,464,128]{2,1,0:T(8,128)(2,1)} %get-tuple-element.120), channel_id=1, source_target_pairs={{0,1},{1,0},{2,3},{3,2},{4,5},{5,4},{6,7},{7,6},{8,9},{9,8},{10,11... | collective-permute-start | bytes 5701640 | tf_op jit(solution)/shard_map/ppermute | solution.py:650
  443.3 20.8 %collective-permute-start.41 = (bf16[64,2048]{1,0:T(8,128)(2,1)}, bf16[64,2048]{1,0:T(8,128)(2,1)S(1)}, u32[]{:S(2)}, u32[]{:S(2)}) collective-permute-start(bf16[64,2048]{1,0:T(8,128)(2,1)} %get-tuple-element.117), channel_id=1, source_target_pairs={{0,2},{2,0},{4,6},{6,4},{8,10},{10,8},{12,14},{14,12},{16,18},{18,... | collective-permute-start | bytes 786440 | tf_op jit(solution)/shard_map/ppermute | solution.py:647
  452.9 64.5 %all-to-all-start.4 = ((bf16[16,320,128]{2,1,0:T(8,128)(2,1)}), bf16[16,320,128]{2,1,0:T(8,128)(2,1)S(1)}, u32[]{:S(2)}, u32[]{:S(2)}) async-start(bf16[16,320,128]{2,1,0:T(8,128)(2,1)} %add_convert_fusion.3), calls=%async_computation.4 | async-start | bytes 2621440 | tf_op jit(solution)/shard_map/all_to_all | solution.py:700
  465.0 33.7 %collective-permute-start.43 = (bf16[128,2048]{1,0:T(8,128)(2,1)}, bf16[128,2048]{1,0:T(8,128)(2,1)}, u32[]{:S(2)}, u32[]{:S(2)}) collective-permute-start(bf16[128,2048]{1,0:T(8,128)(2,1)} %maximum_select_fusion.2.rest_0_.refs_10_), channel_id=1, source_target_pairs={{0,8},{2,6},{8,16},{10,2},{16,24},{18,10},{24,28},{26,18},{28,20},... | collective-permute-start | bytes 1572872 | tf_op jit(solution)/shard_map/ppermute | solution.py:644
  468.5 32.1 %collective-permute-start.39 = (bf16[64,2048]{1,0:T(8,128)(2,1)}, bf16[64,2048]{1,0:T(8,128)(2,1)S(1)}, u32[]{:S(2)}, u32[]{:S(2)}) collective-permute-start(bf16[64,2048]{1,0:T(8,128)(2,1)} %forward_out.1), channel_id=1, source_target_pairs={{0,2},{2,0},{4,6},{6,4},{8,10},{10,8},{12,14},{14,12},{16,18},{18,... | collective-permute-start | bytes 786440 | tf_op jit(solution)/shard_map/ppermute | solution.py:647
  498.7 8.5 %collective-permute-start.44 = (bf16[128,2048]{1,0:T(8,128)(2,1)}, bf16[128,2048]{1,0:T(8,128)(2,1)S(1)}, u32[]{:S(2)}, u32[]{:S(2)}) collective-permute-start(bf16[128,2048]{1,0:T(8,128)(2,1)} %collective-permute-done.43.rest_1_.refs_11_), channel_id=1, source_target_pairs={{0,8},{2,6},{8,16},{10,2},{16,24},{18,10},{24,28},{26,18},{28,20},... | collective-permute-start | bytes 1572872 | tf_op jit(solution)/shard_map/ppermute | solution.py:644
  501.8 13.1 %collective-permute-start.40 = (bf16[128,2048]{1,0:T(8,128)(2,1)S(1)}, bf16[128,2048]{1,0:T(8,128)(2,1)S(1)}, u32[]{:S(2)}, u32[]{:S(2)}) collective-permute-start(bf16[128,2048]{1,0:T(8,128)(2,1)S(1)} %maximum_select_fusion.1), channel_id=1, source_target_pairs={{0,1},{1,0},{2,3},{3,2},{4,5},{5,4},{6,7},{7,6},{8,9},{9,8},{10,11... | collective-permute-start | bytes 1572872 | tf_op jit(solution)/shard_map/ppermute | solution.py:650
  507.3 8.5 %collective-permute-start.46 = (bf16[128,2048]{1,0:T(8,128)(2,1)S(1)}, bf16[128,2048]{1,0:T(8,128)(2,1)S(1)}, u32[]{:S(2)}, u32[]{:S(2)}) collective-permute-start(bf16[128,2048]{1,0:T(8,128)(2,1)S(1)} %collective-permute-done.44.rest_2_.refs_12_), channel_id=1, source_target_pairs={{0,8},{2,6},{8,16},{10,2},{16,24},{18,10},{24,28},{26,18},{28,20},... | collective-permute-start | bytes 1572872 | tf_op jit(solution)/shard_map/ppermute | solution.py:644
  517.3 5.5 collective-permute-start.50
  526.1 55.6 %all-to-all-start.5 = ((bf16[16,464,128]{2,1,0:T(8,128)(2,1)}), bf16[16,464,128]{2,1,0:T(8,128)(2,1)S(1)}, u32[]{:S(2)}, u32[]{:S(2)}) async-start(bf16[16,464,128]{2,1,0:T(8,128)(2,1)} %add_convert_fusion.1), calls=%async_computation.5 | async-start | bytes 3801088 | tf_op jit(solution)/shard_map/all_to_all | solution.py:700
  535.5 3.3 collective-permute-start.49
  548.6 30.3 %collective-permute-start.56 = (bf16[16,320,128]{2,1,0:T(8,128)(2,1)}, bf16[16,320,128]{2,1,0:T(8,128)(2,1)}, u32[]{:S(2)}, u32[]{:S(2)}) collective-permute-start(bf16[16,320,128]{2,1,0:T(8,128)(2,1)} %get-tuple-element.137), channel_id=1, source_target_pairs={{0,1},{1,0},{2,3},{3,2},{4,5},{5,4},{6,7},{7,6},{8,9},{9,8},{10,11... | collective-permute-start | bytes 3932168 | tf_op jit(solution)/shard_map/ppermute | solution.py:650
  576.5 27.5 %collective-permute-start.52 = (bf16[448,2048]{1,0:T(8,128)(2,1)}, bf16[448,2048]{1,0:T(8,128)(2,1)}, u32[]{:S(2)}, u32[]{:S(2)}) collective-permute-start(bf16[448,2048]{1,0:T(8,128)(2,1)} %get-tuple-element.128), channel_id=1, source_target_pairs={{0,2},{2,0},{4,6},{6,4},{8,10},{10,8},{12,14},{14,12},{16,18},{18,... | collective-permute-start | bytes 5505032 | tf_op jit(solution)/shard_map/ppermute | solution.py:647
  581.7 48.7 %all-to-all-start.6 = ((bf16[16,320,128]{2,1,0:T(8,128)(2,1)}), bf16[16,320,128]{2,1,0:T(8,128)(2,1)S(1)}, u32[]{:S(2)}, u32[]{:S(2)}) async-start(bf16[16,320,128]{2,1,0:T(8,128)(2,1)} %add_convert_fusion.2), calls=%async_computation.6 | async-start | bytes 2621440 | tf_op jit(solution)/shard_map/all_to_all | solution.py:700
  601.5 18.7 %collective-permute-start.54 = (bf16[1,64,2048]{2,1,0:T(8,128)(2,1)S(1)}, bf16[1,64,2048]{2,1,0:T(8,128)(2,1)S(1)}, u32[]{:S(2)}, u32[]{:S(2)}) collective-permute-start(bf16[1,64,2048]{2,1,0:T(8,128)(2,1)S(1)} %fusion.16), channel_id=1, source_target_pairs={{0,8},{2,6},{8,16},{10,2},{16,24},{18,10},{24,28},{26,18},{28,20},... | collective-permute-start | bytes 786440 | tf_op jit(solution)/shard_map/ppermute | solution.py:644
  602.7 43.5 %collective-permute-start.58 = (bf16[16,464,128]{2,1,0:T(8,128)(2,1)}, bf16[16,464,128]{2,1,0:T(8,128)(2,1)}, u32[]{:S(2)}, u32[]{:S(2)}) collective-permute-start(bf16[16,464,128]{2,1,0:T(8,128)(2,1)} %get-tuple-element.141), channel_id=1, source_target_pairs={{0,1},{1,0},{2,3},{3,2},{4,5},{5,4},{6,7},{7,6},{8,9},{9,8},{10,11... | collective-permute-start | bytes 5701640 | tf_op jit(solution)/shard_map/ppermute | solution.py:650
  621.7 8.7 %collective-permute-start.55 = (bf16[1,128,2048]{2,1,0:T(8,128)(2,1)S(1)}, bf16[1,128,2048]{2,1,0:T(8,128)(2,1)}, u32[]{:S(2)}, u32[]{:S(2)}) collective-permute-start(bf16[1,128,2048]{2,1,0:T(8,128)(2,1)S(1)} %fusion.8), channel_id=1, source_target_pairs={{0,8},{2,6},{8,16},{10,2},{16,24},{18,10},{24,28},{26,18},{28,20},... | collective-permute-start | bytes 1572872 | tf_op jit(solution)/shard_map/ppermute | solution.py:644
  632.4 13.9 %collective-permute-start.57 = (bf16[1,128,2048]{2,1,0:T(8,128)(2,1)S(1)}, bf16[1,128,2048]{2,1,0:T(8,128)(2,1)S(1)}, u32[]{:S(2)}, u32[]{:S(2)}) collective-permute-start(bf16[1,128,2048]{2,1,0:T(8,128)(2,1)S(1)} %fusion.4), channel_id=1, source_target_pairs={{0,8},{2,6},{8,16},{10,2},{16,24},{18,10},{24,28},{26,18},{28,20},... | collective-permute-start | bytes 1572872 | tf_op jit(solution)/shard_map/ppermute | solution.py:644
  647.6 8.5 %collective-permute-start.59 = (bf16[1,128,2048]{2,1,0:T(8,128)(2,1)S(1)}, bf16[1,128,2048]{2,1,0:T(8,128)(2,1)}, u32[]{:S(2)}, u32[]{:S(2)}) collective-permute-start(bf16[1,128,2048]{2,1,0:T(8,128)(2,1)S(1)} %fusion.3), channel_id=1, source_target_pairs={{0,8},{2,6},{8,16},{10,2},{16,24},{18,10},{24,28},{26,18},{28,20},... | collective-permute-start | bytes 1572872 | tf_op jit(solution)/shard_map/ppermute | solution.py:644
  656.1 49.4 %all-to-all-start.7 = ((bf16[16,464,128]{2,1,0:T(8,128)(2,1)}), bf16[16,464,128]{2,1,0:T(8,128)(2,1)S(1)}, u32[]{:S(2)}, u32[]{:S(2)}) async-start(bf16[16,464,128]{2,1,0:T(8,128)(2,1)} %add_convert_fusion), calls=%async_computation.7 | async-start | bytes 3801088 | tf_op jit(solution)/shard_map/all_to_all | solution.py:700
  663.5 9.1 %collective-permute-start.60 = (bf16[1,64,2048]{2,1,0:T(8,128)(2,1)S(1)}, bf16[1,64,2048]{2,1,0:T(8,128)(2,1)S(1)}, u32[]{:S(2)}, u32[]{:S(2)}) collective-permute-start(bf16[1,64,2048]{2,1,0:T(8,128)(2,1)S(1)} %constant_dynamic-slice_fusion.5), channel_id=1, source_target_pairs={{0,2},{2,0},{4,6},{6,4},{8,10},{10,8},{12,14},{14,12},{16,18},{18,... | collective-permute-start | bytes 786440 | tf_op jit(solution)/shard_map/ppermute | solution.py:647
  664.0 8.5 %collective-permute-start.61 = (f32[2,448]{1,0:T(2,128)S(1)}, f32[2,448]{1,0:T(2,128)S(1)}, u32[]{:S(2)}, u32[]{:S(2)}) collective-permute-start(f32[2,448]{1,0:T(2,128)S(1)} %pad_maximum_fusion.3), channel_id=1, source_target_pairs={{0,1},{1,0},{2,3},{3,2},{4,5},{5,4},{6,7},{7,6},{8,9},{9,8},{10,11... | collective-permute-start | bytes 10760 | tf_op jit(solution)/shard_map/ppermute | solution.py:650
  679.1 13.2 %collective-permute-start.63 = (bf16[128,2048]{1,0:T(8,128)(2,1)S(1)}, bf16[128,2048]{1,0:T(8,128)(2,1)S(1)}, u32[]{:S(2)}, u32[]{:S(2)}) collective-permute-start(bf16[128,2048]{1,0:T(8,128)(2,1)S(1)} %maximum_select_fusion.3), channel_id=1, source_target_pairs={{0,1},{1,0},{2,3},{3,2},{4,5},{5,4},{6,7},{7,6},{8,9},{9,8},{10,11... | collective-permute-start | bytes 1572872 | tf_op jit(solution)/shard_map/ppermute | solution.py:650
  (57 other events, 859.6 us)

commit v14 on v13

--- a/solution.py
+++ b/solution.py
@@ -842,7 +842,7 @@
         [jax.ShapeDtypeStruct(rows_shape, f32), jax.ShapeDtypeStruct(rows_shape, bf16)],
         "forward_end",
     )
-    normed_chunks = gather_rows(in_order(normed_own, across(normed_own)), {1: others[1:]})
+    normed_chunks = gather_rows(in_order(normed_own, across(normed_own)), {0: others[1:]})
 
     def handed_back(own_rows):
         filled = in_order(own_rows, across(own_rows))

time: 726 us -> 734 us (1.011)
  transfers between devices with their start and end apart: 72 -> 72, of which waited for: 46 -> 45; matrix products, arithmetic and copies ran while one was open for 7% -> 7% of each run, Pallas kernels for 20% -> 19%
where the time goes in v14:
time: 734 us; the launch traced here: 723 us
  waiting for transfers between devices  326 us (44%)
  Pallas kernels  188 us (26%)
  starting transfers between devices  131 us (18%)
  other arithmetic  52.8 us (7%)
  local copies, waits for them, and re-layouts  22.4 us (3%)
    ppermute x24, waiting for transfers between devices, along(): return lax.ppermute(x, 'dp', ring_pairs)  147 us
    all_to_all x8, waiting for transfers between devices, spread(): return lax.all_to_all(x, 'dp', 0, 0, axis_index_groups=inner, tiled=True)  97.6 us
    pallas_call x3, Pallas kernels, call_pass(): pl.pallas_call(partial(layer_pass, mode), in_specs=[SMEM_SPEC] + [VMEM_SP...  92.1 us
    ppermute x12, waiting for transfers between devices, over(): return lax.ppermute(x, 'tensor', [(0, 1), (1, 0)])  66.5 us
    all_to_all x8, starting transfers between devices, spread(): return lax.all_to_all(x, 'dp', 0, 0, axis_index_groups=inner, tiled=True)  55.9 us
    pallas_call x4, Pallas kernels, call_gradients(): pl.pallas_call(partial(gradient_slabs, own_rows, other_rows, with_sums, l...  37.9 us
    ppermute x24, starting transfers between devices, along(): return lax.ppermute(x, 'dp', ring_pairs)  31.4 us
    ppermute x28, starting transfers between devices, across(): return lax.ppermute(x, 'dp', core_pairs)  30 us
  transfers between devices with their start and end apart: 72, of which 45 were waited for; matrix products, arithmetic and copies ran while one was open for 7% of the time, Pallas kernels for 19%

profile of v14, /device:TPU:13, one launch (start us, length us, event | category | flops | bytes accessed | tf_op | source)
XLA Modules:
  0.0 722.7 jit_solution(6658784266072656229)
XLA Ops:
  4.8 4.0 pack_first.1
  8.8 6.5 all-to-all-start
  15.3 3.5 pack_down.2
  18.9 39.7 %all-to-all-done.own_ref = bf16[16,464,128]{2,1,0:T(8,128)(2,1)S(1)} async-done(((bf16[16,464,128]{2,1,0:T(8,128)(2,1)}), bf16[16,464,128]{2,1,0:T(8,128)(2,1)S(1)}, u32[]{:S(2)}, u32[]{:S(2)}) %all-to-all-start) | async-done | bytes 1900576 | tf_op jit(solution)/shard_map/all_to_all | solution.py:700
  58.5 4.8 all-to-all-start.1
  69.3 3.5 pack_down.3
  72.9 3.9 pack_up.1
  79.5 14.8 %all-to-all-done.1.own_ref = bf16[16,320,128]{2,1,0:T(8,128)(2,1)S(1)} async-done(((bf16[16,320,128]{2,1,0:T(8,128)(2,1)}), bf16[16,320,128]{2,1,0:T(8,128)(2,1)S(1)}, u32[]{:S(2)}, u32[]{:S(2)}) %all-to-all-start.1) | async-done | bytes 1310752 | tf_op jit(solution)/shard_map/all_to_all | solution.py:700
  100.7 10.1 %collective-permute-done.2.other_ref = bf16[16,464,128]{2,1,0:T(8,128)(2,1)} collective-permute-done((bf16[16,464,128]{2,1,0:T(8,128)(2,1)S(1)}, bf16[16,464,128]{2,1,0:T(8,128)(2,1)}, u32[]{:S(2)}, u32[]{:S(2)}) %collective-permute-start.2) | collective-permute-done | bytes 1900576 | tf_op jit(solution)/shard_map/ppermute | solution.py:650
  118.0 7.1 collective-permute-done.3.refs_12_.refs_19_
  126.3 4.8 join_up.2.refs_1_
  131.1 8.2 %collective-permute-done.4.refs_13_.refs_20_ = bf16[2,128,2048]{2,1,0:T(8,128)(2,1)S(1)} collective-permute-done((bf16[2,128,2048]{2,1,0:T(8,128)(2,1)}, bf16[2,128,2048]{2,1,0:T(8,128)(2,1)S(1)}, u32[]{:S(2)}, u32[]{:S(2)}) %collective-permute-start.4) | collective-permute-done | bytes 1048608 | tf_op jit(solution)/shard_map/ppermute | solution.py:644
  139.3 2.9 collective-permute-done.5.other_ref
  143.4 7.1 collective-permute-done.6.refs_17_.refs_24_
  150.6 6.8 all-to-all-start.2
  163.8 4.2 join_down.2.refs_2_
  168.1 29.3 %pass_first.1 = (bf16[1024,2048]{1,0:T(8,128)(2,1)}, bf16[1024,384]{1,0:T(8,128)(2,1)}, f32[1024,512]{1,0:T(8,128)}, bf16[1024,640]{1,0:T(8,128)(2,1)}, bf16[64,...) custom-call(s32[1]{0:T(128)} %bitcast.refs_0_.core_ref, bf16[2048,896]{1,0:T(8,128)(2,1)} %join_up.2.refs_1_, ...), custom_call_target="tpu_custom_call" | custom-call | flops 19327352832 | bytes 20000000 | tf_op jit(solution)/shard_map/pass_first/pallas_call | solution.py:414
  199.3 4.8 all-to-all-start.3
  205.9 29.1 %all-to-all-done.3.own_ref = bf16[16,320,128]{2,1,0:T(8,128)(2,1)S(1)} async-done(((bf16[16,320,128]{2,1,0:T(8,128)(2,1)}), bf16[16,320,128]{2,1,0:T(8,128)(2,1)S(1)}, u32[]{:S(2)}, u32[]{:S(2)}) %all-to-all-start.3) | async-done | bytes 1310752 | tf_op jit(solution)/shard_map/all_to_all | solution.py:700
  237.1 8.4 %collective-permute-done.7.other_ref = bf16[16,448,128]{2,1,0:T(8,128)(2,1)} collective-permute-done((bf16[16,448,128]{2,1,0:T(8,128)(2,1)}, bf16[16,448,128]{2,1,0:T(8,128)(2,1)}, u32[]{:S(2)}, u32[]{:S(2)}) %collective-permute-start.7) | collective-permute-done | bytes 1835040 | tf_op jit(solution)/shard_map/ppermute | solution.py:650
  248.1 7.1 collective-permute-done.17
  257.7 7.1 collective-permute-done.18
  269.4 6.1 collective-permute-done.19.moving_ref
  276.3 3.8 collective-permute-start.20
  288.1 8.1 %collective-permute-done.13.other_ref = bf16[16,320,128]{2,1,0:T(8,128)(2,1)S(1)} collective-permute-done((bf16[16,320,128]{2,1,0:T(8,128)(2,1)S(1)}, bf16[16,320,128]{2,1,0:T(8,128)(2,1)S(1)}, u32[]{:S(2)}, u32[]{:S(2)}) %collective-permute-start.13) | collective-permute-done | bytes 1310752 | tf_op jit(solution)/shard_map/ppermute | solution.py:650
  297.4 7.1 collective-permute-done.22.refs_9_
  305.7 7.1 collective-permute-done.23.refs_10_
  314.0 4.3 collective-permute-start.25
  322.4 5.1 collective-permute-start.27
  327.5 5.9 collective-permute-start.29
  333.5 4.8 join_up.3.refs_1_
  338.3 4.1 join_down.3.refs_2_
  342.4 36.2 %pass_middle.1 = (bf16[1024,2048]{1,0:T(8,128)(2,1)}, bf16[1024,2048]{1,0:T(8,128)(2,1)}, bf16[1024,640]{1,0:T(8,128)(2,1)}, bf16[1024,896]{1,0:T(8,128)(2,1)}, ...) custom-call(s32[1]{0:T(128)} %bitcast.refs_0_.core_ref, ...), custom_call_target="tpu_custom_call" | custom-call | flops 38654705664 | bytes 40000000 | tf_op jit(solution)/shard_map/pass_middle/pallas_call | solution.py:414
  379.7 3.3 collective-permute-done.31
  391.7 3.9 collective-permute-done.33
  398.1 8.8 %down_gradients.2 = (bf16[16,320,128]{2,1,0:T(8,128)(2,1)}, bf16[16,320,128]{2,1,0:T(8,128)(2,1)}) custom-call(s32[1]{0:T(128)} %bitcast.refs_0_.core_ref, bf16[1024,640]{1,0:T(8,128)(2,1)} %get-tuple-element.104.left_ref, bf16[1024,2048]{1,0:T(8,128)(2,1)} %get-tuple-element.105.rest_0_), custom_call_target="tpu_custom_call" | custom-call | flops 5368709120 | bytes 10747904 | tf_op jit(solution)/shard_map/down_gradients/pallas_call | solution.py:476
  406.9 4.2 collective-permute-done.35
  415.3 10.1 %up_gradients.2 = (bf16[16,464,128]{2,1,0:T(8,128)(2,1)}, bf16[16,464,128]{2,1,0:T(8,128)(2,1)}, f32[1,896]{1,0:T(1,128)}) custom-call(s32[1]{0:T(128)} %bitcast.refs_0_.core_ref, bf16[1024,896]{1,0:T(8,128)(2,1)} %get-tuple-element.108.left_ref, bf16[1024,2048]{1,0:T(8,128)(2,1)} %get-tuple-element.109.rest_0_, f32[16,2048]{1,0:T(8,128)} %get-tuple-element.110.rest_1_), custom_call_target="tpu_custom_call" | custom-call | flops 7516192768 | bytes 13369344 | tf_op jit(solution)/shard_map/up_gradients/pallas_call | solution.py:476
  431.0 11.7 %collective-permute-done.37.moving_ref = bf16[2,128,2048]{2,1,0:T(8,128)(2,1)S(1)} collective-permute-done((bf16[2,128,2048]{2,1,0:T(8,128)(2,1)S(1)}, bf16[2,128,2048]{2,1,0:T(8,128)(2,1)S(1)}, u32[]{:S(2)}, u32[]{:S(2)}) %collective-permute-start.37) | collective-permute-done | bytes 1048608 | tf_op jit(solution)/shard_map/ppermute | solution.py:644
  442.7 3.5 collective-permute-start.38
  448.6 3.0 backward_end.2
  452.0 6.4 collective-permute-done.42
  461.1 11.2 %all-to-all-start.4 = ((bf16[16,320,128]{2,1,0:T(8,128)(2,1)}), bf16[16,320,128]{2,1,0:T(8,128)(2,1)S(1)}, u32[]{:S(2)}, u32[]{:S(2)}) async-start(bf16[16,320,128]{2,1,0:T(8,128)(2,1)} %add_convert_fusion.3), calls=%async_computation.4 | async-start | bytes 2621440 | tf_op jit(solution)/shard_map/all_to_all | solution.py:700
  476.8 30.2 %collective-permute-done.43.rest_1_.refs_11_ = bf16[128,2048]{1,0:T(8,128)(2,1)} collective-permute-done((bf16[128,2048]{1,0:T(8,128)(2,1)}, bf16[128,2048]{1,0:T(8,128)(2,1)}, u32[]{:S(2)}, u32[]{:S(2)}) %collective-permute-start.43) | collective-permute-done | bytes 524320 | tf_op jit(solution)/shard_map/ppermute | solution.py:644
  511.3 4.2 collective-permute-done.44.rest_2_.refs_12_
  517.4 5.7 collective-permute-done.40
  527.3 3.8 collective-permute-done.50.rest_7_.refs_17_
  531.1 3.3 add_convert_fusion.1
  534.4 8.8 %all-to-all-start.5 = ((bf16[16,464,128]{2,1,0:T(8,128)(2,1)}), bf16[16,464,128]{2,1,0:T(8,128)(2,1)S(1)}, u32[]{:S(2)}, u32[]{:S(2)}) async-start(bf16[16,464,128]{2,1,0:T(8,128)(2,1)} %add_convert_fusion.1), calls=%async_computation.5 | async-start | bytes 3801088 | tf_op jit(solution)/shard_map/all_to_all | solution.py:700
  548.0 8.9 %down_gradients.3 = (bf16[16,320,128]{2,1,0:T(8,128)(2,1)}, bf16[16,320,128]{2,1,0:T(8,128)(2,1)}) custom-call(s32[1]{0:T(128)} %bitcast.refs_0_.core_ref, bf16[1024,640]{1,0:T(8,128)(2,1)} %get-tuple-element.116.left_ref, bf16[128,2048]{1,0:T(8,128)(2,1)} %maximum_select_fusion.2.rest_0_.refs_10_, ...), custom_call_target="tpu_custom_call" | custom-call | flops 5368709120 | bytes 10747904 | tf_op jit(solution)/shard_map/down_gradients/pallas_call | solution.py:476
  558.1 26.6 %pass_last.1 = (bf16[1024,2048]{1,0:T(8,128)(2,1)}, bf16[1024,896]{1,0:T(8,128)(2,1)}, f32[16,2048]{1,0:T(8,128)}, bf16[64,2048]{1,0:T(8,128)(2,1)}, bf16[448,20...) custom-call(s32[1]{0:T(128)} %bitcast.refs_0_.core_ref, bf16[2048,896]{1,0:T(8,128)(2,1)} %join_up.2.refs_1_, ...), custom_call_target="tpu_custom_call" | custom-call | flops 19327352832 | bytes 20000000 | tf_op jit(solution)/shard_map/pass_last/pallas_call | solution.py:414
  590.0 6.8 all-to-all-start.6
  596.8 10.1 %up_gradients.3 = (bf16[16,464,128]{2,1,0:T(8,128)(2,1)}, bf16[16,464,128]{2,1,0:T(8,128)(2,1)}, f32[1,896]{1,0:T(1,128)}) custom-call(s32[1]{0:T(128)} %bitcast.refs_0_.core_ref, bf16[1024,896]{1,0:T(8,128)(2,1)} %get-tuple-element.130.left_ref, bf16[1024,2048]{1,0:T(8,128)(2,1)} %get-tuple-element.133.refs_9_.rest_0_, f32[16,2048]{1,0:T(8,128)} %get-tuple-element.134.rest_1_), custom_call_target="tpu_custom_call" | custom-call | flops 7516192768 | bytes 13369344 | tf_op jit(solution)/shard_map/up_gradients/pallas_call | solution.py:476
  612.2 16.3 %collective-permute-done.54 = bf16[1,64,2048]{2,1,0:T(8,128)(2,1)S(1)} collective-permute-done((bf16[1,64,2048]{2,1,0:T(8,128)(2,1)S(1)}, bf16[1,64,2048]{2,1,0:T(8,128)(2,1)S(1)}, u32[]{:S(2)}, u32[]{:S(2)}) %collective-permute-start.54) | collective-permute-done | bytes 262176 | tf_op jit(solution)/shard_map/ppermute | solution.py:644
  632.6 6.1 collective-permute-done.55
  643.0 11.5 %collective-permute-done.58 = bf16[16,464,128]{2,1,0:T(8,128)(2,1)} collective-permute-done((bf16[16,464,128]{2,1,0:T(8,128)(2,1)}, bf16[16,464,128]{2,1,0:T(8,128)(2,1)}, u32[]{:S(2)}, u32[]{:S(2)}) %collective-permute-start.58) | collective-permute-done | bytes 1900576 | tf_op jit(solution)/shard_map/ppermute | solution.py:650
  657.1 3.3 add_convert_fusion
  660.4 4.0 collective-permute-done.59.moving_ref
  664.3 6.2 all-to-all-start.7
  673.5 7.3 %spread_gradients.2 = (f32[2,3,128,1024]{3,2,1,0:T(8,128)}, f32[2,1024,128]{2,1,0:T(8,128)}, f32[2,128,4096]{2,1,0:T(8,128)}, f32[2,4096,128]{2,1,0:T(8,128)}, f32[8,128]{1,0:T(8,128)}) custom-call(bf16[16,464,128]{2,1,0:T(8,128)(2,1)} %copy-done.1, bf16[16,320,128]{2,1,0:T(8,128)(2,1)} %copy-done.11), custom_call_target="tpu_custom_call" | custom-call | tf_op jit(solution)/shard_map/spread_gradients/pallas_call | solution.py:516
  681.5 2.9 backward_end.3
  690.7 9.9 %collective-permute-done.63 = bf16[128,2048]{1,0:T(8,128)(2,1)S(1)} collective-permute-done((bf16[128,2048]{1,0:T(8,128)(2,1)S(1)}, bf16[128,2048]{1,0:T(8,128)(2,1)S(1)}, u32[]{:S(2)}, u32[]{:S(2)}) %collective-permute-start.63) | collective-permute-done | bytes 524320 | tf_op jit(solution)/shard_map/ppermute | solution.py:650
  701.6 12.1 %all-to-all-done.7.up_ref = bf16[16,464,128]{2,1,0:T(8,128)(2,1)S(1)} async-done(((bf16[16,464,128]{2,1,0:T(8,128)(2,1)}), bf16[16,464,128]{2,1,0:T(8,128)(2,1)S(1)}, u32[]{:S(2)}, u32[]{:S(2)}) %all-to-all-start.7) | async-done | bytes 1900576 | tf_op jit(solution)/shard_map/all_to_all | solution.py:700
  715.0 7.3 %spread_gradients.3 = (f32[2,3,128,1024]{3,2,1,0:T(8,128)}, f32[2,1024,128]{2,1,0:T(8,128)}, f32[2,128,4096]{2,1,0:T(8,128)}, f32[2,4096,128]{2,1,0:T(8,128)}, f32[8,128]{1,0:T(8,128)}) custom-call(bf16[16,464,128]{2,1,0:T(8,128)(2,1)} %copy-done.2, ...), custom_call_target="tpu_custom_call", output_to_operand_aliasing={{0}: (2, {}), {1}: (3, {}), {2}: (4, {}), {3}: (5, {})} | custom-call | tf_op jit(solution)/shard_map/spread_gradients/pallas_call | solution.py:516
  (306 shorter events, 148.9 us)
Async XLA Ops:
  8.8 49.7 %all-to-all-start = ((bf16[16,464,128]{2,1,0:T(8,128)(2,1)}), bf16[16,464,128]{2,1,0:T(8,128)(2,1)S(1)}, u32[]{:S(2)}, u32[]{:S(2)}) async-start(bf16[16,464,128]{2,1,0:T(8,128)(2,1)} %pack_first.1), calls=%async_computation | async-start | bytes 3801088 | tf_op jit(solution)/shard_map/all_to_all | solution.py:700
  58.5 35.7 %all-to-all-start.1 = ((bf16[16,320,128]{2,1,0:T(8,128)(2,1)}), bf16[16,320,128]{2,1,0:T(8,128)(2,1)S(1)}, u32[]{:S(2)}, u32[]{:S(2)}) async-start(bf16[16,320,128]{2,1,0:T(8,128)(2,1)} %pack_down.2), calls=%async_computation.1 | async-start | bytes 2621440 | tf_op jit(solution)/shard_map/all_to_all | solution.py:700
  65.6 11.2 %collective-permute-start = (bf16[2,128,2048]{2,1,0:T(8,128)(2,1)}, bf16[2,128,2048]{2,1,0:T(8,128)(2,1)}, u32[]{:S(2)}, u32[]{:S(2)}) collective-permute-start(bf16[2,128,2048]{2,1,0:T(8,128)(2,1)} %pad_maximum_fusion), channel_id=1, source_target_pairs={{0,2},{2,0},{4,6},{6,4},{8,10},{10,8},{12,14},{14,12},{16,18},{18,... | collective-permute-start | bytes 3145736 | tf_op jit(solution)/shard_map/ppermute | solution.py:647
  67.9 43.0 %collective-permute-start.2 = (bf16[16,464,128]{2,1,0:T(8,128)(2,1)S(1)}, bf16[16,464,128]{2,1,0:T(8,128)(2,1)}, u32[]{:S(2)}, u32[]{:S(2)}) collective-permute-start(bf16[16,464,128]{2,1,0:T(8,128)(2,1)S(1)} %all-to-all-done.own_ref), channel_id=1, source_target_pairs={{0,1},{1,0},{2,3},{3,2},{4,5},{5,4},{6,7},{7,6},{8,9},{9,8},{10,11... | collective-permute-start | bytes 5701640 | tf_op jit(solution)/shard_map/ppermute | solution.py:650
  94.3 16.6 %collective-permute-start.1 = (bf16[2,128,2048]{2,1,0:T(8,128)(2,1)}, bf16[2,128,2048]{2,1,0:T(8,128)(2,1)}, u32[]{:S(2)}, u32[]{:S(2)}) collective-permute-start(bf16[2,128,2048]{2,1,0:T(8,128)(2,1)} %select_multiply_fusion.refs_10_.refs_17_), channel_id=1, source_target_pairs={{0,8},{2,6},{8,16},{10,2},{16,24},{18,10},{24,28},{26,18},{28,20},... | collective-permute-start | bytes 3145736 | tf_op jit(solution)/shard_map/ppermute | solution.py:644
  110.9 14.3 %collective-permute-start.3 = (bf16[2,128,2048]{2,1,0:T(8,128)(2,1)}, bf16[2,128,2048]{2,1,0:T(8,128)(2,1)}, u32[]{:S(2)}, u32[]{:S(2)}) collective-permute-start(bf16[2,128,2048]{2,1,0:T(8,128)(2,1)} %collective-permute-done.1.refs_11_.refs_18_), channel_id=1, source_target_pairs={{0,8},{2,6},{8,16},{10,2},{16,24},{18,10},{24,28},{26,18},{28,20},... | collective-permute-start | bytes 3145736 | tf_op jit(solution)/shard_map/ppermute | solution.py:644
  112.0 30.2 %collective-permute-start.5 = (bf16[16,320,128]{2,1,0:T(8,128)(2,1)}, bf16[16,320,128]{2,1,0:T(8,128)(2,1)S(1)}, u32[]{:S(2)}, u32[]{:S(2)}) collective-permute-start(bf16[16,320,128]{2,1,0:T(8,128)(2,1)} %copy-done.10), channel_id=1, source_target_pairs={{0,1},{1,0},{2,3},{3,2},{4,5},{5,4},{6,7},{7,6},{8,9},{9,8},{10,11... | collective-permute-start | bytes 3932168 | tf_op jit(solution)/shard_map/ppermute | solution.py:650
  125.1 14.2 %collective-permute-start.4 = (bf16[2,128,2048]{2,1,0:T(8,128)(2,1)}, bf16[2,128,2048]{2,1,0:T(8,128)(2,1)S(1)}, u32[]{:S(2)}, u32[]{:S(2)}) collective-permute-start(bf16[2,128,2048]{2,1,0:T(8,128)(2,1)} %collective-permute-done.3.refs_12_.refs_19_), channel_id=1, source_target_pairs={{0,8},{2,6},{8,16},{10,2},{16,24},{18,10},{24,28},{26,18},{28,20},... | collective-permute-start | bytes 3145736 | tf_op jit(solution)/shard_map/ppermute | solution.py:644
  142.2 8.3 %collective-permute-start.6 = (bf16[2,64,2048]{2,1,0:T(8,128)(2,1)S(1)}, bf16[2,64,2048]{2,1,0:T(8,128)(2,1)S(1)}, u32[]{:S(2)}, u32[]{:S(2)}) collective-permute-start(bf16[2,64,2048]{2,1,0:T(8,128)(2,1)S(1)} %constant_dynamic-slice_fusion.4), channel_id=1, source_target_pairs={{0,8},{2,6},{8,16},{10,2},{16,24},{18,10},{24,28},{26,18},{28,20},... | collective-permute-start | bytes 1572872 | tf_op jit(solution)/shard_map/ppermute | solution.py:644
  150.6 48.7 %all-to-all-start.2 = ((bf16[16,448,128]{2,1,0:T(8,128)(2,1)}), bf16[16,448,128]{2,1,0:T(8,128)(2,1)}, u32[]{:S(2)}, u32[]{:S(2)}) async-start(bf16[16,448,128]{2,1,0:T(8,128)(2,1)} %pack_up.1), calls=%async_computation.2 | async-start | bytes 3670016 | tf_op jit(solution)/shard_map/all_to_all | solution.py:700
  157.5 10.6 %collective-permute-start.9 = (bf16[2,128,2048]{2,1,0:T(8,128)(2,1)}, bf16[2,128,2048]{2,1,0:T(8,128)(2,1)}, u32[]{:S(2)}, u32[]{:S(2)}) collective-permute-start(bf16[2,128,2048]{2,1,0:T(8,128)(2,1)} %collective-permute-done.1.refs_11_.refs_18_), channel_id=1, source_target_pairs={{0,2},{2,0},{4,6},{6,4},{8,10},{10,8},{12,14},{14,12},{16,18},{18,... | collective-permute-start | bytes 3145736 | tf_op jit(solution)/shard_map/ppermute | solution.py:647
  157.9 10.2 %collective-permute-start.10 = (bf16[2,128,2048]{2,1,0:T(8,128)(2,1)}, bf16[2,128,2048]{2,1,0:T(8,128)(2,1)}, u32[]{:S(2)}, u32[]{:S(2)}) collective-permute-start(bf16[2,128,2048]{2,1,0:T(8,128)(2,1)} %collective-permute-done.3.refs_12_.refs_19_), channel_id=1, source_target_pairs={{0,2},{2,0},{4,6},{6,4},{8,10},{10,8},{12,14},{14,12},{16,18},{18,... | collective-permute-start | bytes 3145736 | tf_op jit(solution)/shard_map/ppermute | solution.py:647
  158.0 10.1 %collective-permute-start.11 = (bf16[2,128,2048]{2,1,0:T(8,128)(2,1)S(1)}, bf16[2,128,2048]{2,1,0:T(8,128)(2,1)}, u32[]{:S(2)}, u32[]{:S(2)}) collective-permute-start(bf16[2,128,2048]{2,1,0:T(8,128)(2,1)S(1)} %collective-permute-done.4.refs_13_.refs_20_), channel_id=1, source_target_pairs={{0,2},{2,0},{4,6},{6,4},{8,10},{10,8},{12,14},{14,12},{16,18},{18,... | collective-permute-start | bytes 3145736 | tf_op jit(solution)/shard_map/ppermute | solution.py:647
  162.2 5.9 collective-permute-start.12
  199.3 35.7 %all-to-all-start.3 = ((bf16[16,320,128]{2,1,0:T(8,128)(2,1)}), bf16[16,320,128]{2,1,0:T(8,128)(2,1)S(1)}, u32[]{:S(2)}, u32[]{:S(2)}) async-start(bf16[16,320,128]{2,1,0:T(8,128)(2,1)} %pack_down.3), calls=%async_computation.3 | async-start | bytes 2621440 | tf_op jit(solution)/shard_map/all_to_all | solution.py:700
  204.0 41.5 %collective-permute-start.7 = (bf16[16,448,128]{2,1,0:T(8,128)(2,1)}, bf16[16,448,128]{2,1,0:T(8,128)(2,1)}, u32[]{:S(2)}, u32[]{:S(2)}) collective-permute-start(bf16[16,448,128]{2,1,0:T(8,128)(2,1)} %all-to-all-done.2.own_ref), channel_id=1, source_target_pairs={{0,1},{1,0},{2,3},{3,2},{4,5},{5,4},{6,7},{7,6},{8,9},{9,8},{10,11... | collective-permute-start | bytes 5505032 | tf_op jit(solution)/shard_map/ppermute | solution.py:650
  205.3 40.3 %collective-permute-start.14 = (bf16[448,2048]{1,0:T(8,128)(2,1)}, bf16[448,2048]{1,0:T(8,128)(2,1)}, u32[]{:S(2)}, u32[]{:S(2)}) collective-permute-start(bf16[448,2048]{1,0:T(8,128)(2,1)} %get-tuple-element.93), channel_id=1, source_target_pairs={{0,2},{2,0},{4,6},{6,4},{8,10},{10,8},{12,14},{14,12},{16,18},{18,... | collective-permute-start | bytes 5505032 | tf_op jit(solution)/shard_map/ppermute | solution.py:647
  236.8 8.7 %collective-permute-start.16 = (bf16[1,64,2048]{2,1,0:T(8,128)(2,1)S(1)}, bf16[1,64,2048]{2,1,0:T(8,128)(2,1)S(1)}, u32[]{:S(2)}, u32[]{:S(2)}) collective-permute-start(bf16[1,64,2048]{2,1,0:T(8,128)(2,1)S(1)} %fusion.13), channel_id=1, source_target_pairs={{0,8},{2,6},{8,16},{10,2},{16,24},{18,10},{24,28},{26,18},{28,20},... | collective-permute-start | bytes 786440 | tf_op jit(solution)/shard_map/ppermute | solution.py:644
  246.8 8.4 %collective-permute-start.17 = (bf16[1,128,2048]{2,1,0:T(8,128)(2,1)S(1)}, bf16[1,128,2048]{2,1,0:T(8,128)(2,1)S(1)}, u32[]{:S(2)}, u32[]{:S(2)}) collective-permute-start(bf16[1,128,2048]{2,1,0:T(8,128)(2,1)S(1)} %fusion.7), channel_id=1, source_target_pairs={{0,8},{2,6},{8,16},{10,2},{16,24},{18,10},{24,28},{26,18},{28,20},... | collective-permute-start | bytes 1572872 | tf_op jit(solution)/shard_map/ppermute | solution.py:644
  256.5 8.4 %collective-permute-start.18 = (bf16[1,128,2048]{2,1,0:T(8,128)(2,1)S(1)}, bf16[1,128,2048]{2,1,0:T(8,128)(2,1)S(1)}, u32[]{:S(2)}, u32[]{:S(2)}) collective-permute-start(bf16[1,128,2048]{2,1,0:T(8,128)(2,1)S(1)} %fusion.6), channel_id=1, source_target_pairs={{0,8},{2,6},{8,16},{10,2},{16,24},{18,10},{24,28},{26,18},{28,20},... | collective-permute-start | bytes 1572872 | tf_op jit(solution)/shard_map/ppermute | solution.py:644
  267.0 8.5 %collective-permute-start.19 = (bf16[1,128,2048]{2,1,0:T(8,128)(2,1)}, bf16[1,128,2048]{2,1,0:T(8,128)(2,1)S(1)}, u32[]{:S(2)}, u32[]{:S(2)}) collective-permute-start(bf16[1,128,2048]{2,1,0:T(8,128)(2,1)} %fusion.5), channel_id=1, source_target_pairs={{0,8},{2,6},{8,16},{10,2},{16,24},{18,10},{24,28},{26,18},{28,20},... | collective-permute-start | bytes 1572872 | tf_op jit(solution)/shard_map/ppermute | solution.py:644
  268.2 28.0 %collective-permute-start.13 = (bf16[16,320,128]{2,1,0:T(8,128)(2,1)S(1)}, bf16[16,320,128]{2,1,0:T(8,128)(2,1)S(1)}, u32[]{:S(2)}, u32[]{:S(2)}) collective-permute-start(bf16[16,320,128]{2,1,0:T(8,128)(2,1)S(1)} %all-to-all-done.3.own_ref), channel_id=1, source_target_pairs={{0,1},{1,0},{2,3},{3,2},{4,5},{5,4},{6,7},{7,6},{8,9},{9,8},{10,11... | collective-permute-start | bytes 3932168 | tf_op jit(solution)/shard_map/ppermute | solution.py:650
  276.3 5.7 collective-permute-start.20
  296.2 8.3 %collective-permute-start.22 = (bf16[128,2048]{1,0:T(8,128)(2,1)S(1)}, bf16[128,2048]{1,0:T(8,128)(2,1)S(1)}, u32[]{:S(2)}, u32[]{:S(2)}) collective-permute-start(bf16[128,2048]{1,0:T(8,128)(2,1)S(1)} %maximum_select_fusion.refs_8_), channel_id=1, source_target_pairs={{0,8},{2,6},{8,16},{10,2},{16,24},{18,10},{24,28},{26,18},{28,20},... | collective-permute-start | bytes 1572872 | tf_op jit(solution)/shard_map/ppermute | solution.py:644
  304.5 8.3 %collective-permute-start.23 = (bf16[128,2048]{1,0:T(8,128)(2,1)S(1)}, bf16[128,2048]{1,0:T(8,128)(2,1)S(1)}, u32[]{:S(2)}, u32[]{:S(2)}) collective-permute-start(bf16[128,2048]{1,0:T(8,128)(2,1)S(1)} %collective-permute-done.22.refs_9_), channel_id=1, source_target_pairs={{0,8},{2,6},{8,16},{10,2},{16,24},{18,10},{24,28},{26,18},{28,20},... | collective-permute-start | bytes 1572872 | tf_op jit(solution)/shard_map/ppermute | solution.py:644
  312.8 8.3 %collective-permute-start.24 = (bf16[128,2048]{1,0:T(8,128)(2,1)S(1)}, bf16[128,2048]{1,0:T(8,128)(2,1)S(1)}, u32[]{:S(2)}, u32[]{:S(2)}) collective-permute-start(bf16[128,2048]{1,0:T(8,128)(2,1)S(1)} %collective-permute-done.23.refs_10_), channel_id=1, source_target_pairs={{0,8},{2,6},{8,16},{10,2},{16,24},{18,10},{24,28},{26,18},{28,20},... | collective-permute-start | bytes 1572872 | tf_op jit(solution)/shard_map/ppermute | solution.py:644
  314.0 28.4 %collective-permute-start.25 = (bf16[128,2048]{1,0:T(8,128)(2,1)S(1)}, bf16[128,2048]{1,0:T(8,128)(2,1)}, u32[]{:S(2)}, u32[]{:S(2)}) collective-permute-start(bf16[128,2048]{1,0:T(8,128)(2,1)S(1)} %collective-permute-done.22.refs_9_), channel_id=1, source_target_pairs={{0,2},{2,0},{4,6},{6,4},{8,10},{10,8},{12,14},{14,12},{16,18},{18,... | collective-permute-start | bytes 1572872 | tf_op jit(solution)/shard_map/ppermute | solution.py:647
  318.3 24.1 %collective-permute-start.26 = (bf16[128,2048]{1,0:T(8,128)(2,1)S(1)}, bf16[128,2048]{1,0:T(8,128)(2,1)}, u32[]{:S(2)}, u32[]{:S(2)}) collective-permute-start(bf16[128,2048]{1,0:T(8,128)(2,1)S(1)} %collective-permute-done.23.refs_10_), channel_id=1, source_target_pairs={{0,2},{2,0},{4,6},{6,4},{8,10},{10,8},{12,14},{14,12},{16,18},{18,... | collective-permute-start | bytes 1572872 | tf_op jit(solution)/shard_map/ppermute | solution.py:647
  321.2 6.4 collective-permute-start.28
  322.4 20.0 %collective-permute-start.27 = (bf16[128,2048]{1,0:T(8,128)(2,1)S(1)}, bf16[128,2048]{1,0:T(8,128)(2,1)}, u32[]{:S(2)}, u32[]{:S(2)}) collective-permute-start(bf16[128,2048]{1,0:T(8,128)(2,1)S(1)} %collective-permute-done.24.refs_11_), channel_id=1, source_target_pairs={{0,2},{2,0},{4,6},{6,4},{8,10},{10,8},{12,14},{14,12},{16,18},{18,... | collective-permute-start | bytes 1572872 | tf_op jit(solution)/shard_map/ppermute | solution.py:647
  327.5 14.9 %collective-permute-start.29 = (bf16[64,2048]{1,0:T(8,128)(2,1)}, bf16[64,2048]{1,0:T(8,128)(2,1)}, u32[]{:S(2)}, u32[]{:S(2)}) collective-permute-start(bf16[64,2048]{1,0:T(8,128)(2,1)} %collective-permute-done.28.refs_15_), channel_id=1, source_target_pairs={{0,2},{2,0},{4,6},{6,4},{8,10},{10,8},{12,14},{14,12},{16,18},{18,... | collective-permute-start | bytes 786440 | tf_op jit(solution)/shard_map/ppermute | solution.py:647
  378.6 9.8 %collective-permute-start.34 = (bf16[448,2048]{1,0:T(8,128)(2,1)}, bf16[448,2048]{1,0:T(8,128)(2,1)S(1)}, u32[]{:S(2)}, u32[]{:S(2)}) collective-permute-start(bf16[448,2048]{1,0:T(8,128)(2,1)} %get-tuple-element.103), channel_id=1, source_target_pairs={{0,2},{2,0},{4,6},{6,4},{8,10},{10,8},{12,14},{14,12},{16,18},{18,... | collective-permute-start | bytes 5505032 | tf_op jit(solution)/shard_map/ppermute | solution.py:647
  378.7 4.4 collective-permute-start.31
  379.2 10.8 %collective-permute-start.30 = (bf16[448,2048]{1,0:T(8,128)(2,1)}, bf16[448,2048]{1,0:T(8,128)(2,1)S(1)}, u32[]{:S(2)}, u32[]{:S(2)}) collective-permute-start(bf16[448,2048]{1,0:T(8,128)(2,1)} %get-tuple-element.99), channel_id=1, source_target_pairs={{0,2},{2,0},{4,6},{6,4},{8,10},{10,8},{12,14},{14,12},{16,18},{18,... | collective-permute-start | bytes 5505032 | tf_op jit(solution)/shard_map/ppermute | solution.py:647
  379.3 6.8 collective-permute-start.32
  387.2 8.4 %collective-permute-start.33 = (bf16[2,64,2048]{2,1,0:T(8,128)(2,1)S(1)}, bf16[2,64,2048]{2,1,0:T(8,128)(2,1)S(1)}, u32[]{:S(2)}, u32[]{:S(2)}) collective-permute-start(bf16[2,64,2048]{2,1,0:T(8,128)(2,1)S(1)} %pad_maximum_fusion.1), channel_id=1, source_target_pairs={{0,8},{2,6},{8,16},{10,2},{16,24},{18,10},{24,28},{26,18},{28,20},... | collective-permute-start | bytes 1572872 | tf_op jit(solution)/shard_map/ppermute | solution.py:644
  396.9 14.3 %collective-permute-start.35 = (bf16[2,128,2048]{2,1,0:T(8,128)(2,1)}, bf16[2,128,2048]{2,1,0:T(8,128)(2,1)}, u32[]{:S(2)}, u32[]{:S(2)}) collective-permute-start(bf16[2,128,2048]{2,1,0:T(8,128)(2,1)} %fusion), channel_id=1, source_target_pairs={{0,8},{2,6},{8,16},{10,2},{16,24},{18,10},{24,28},{26,18},{28,20},... | collective-permute-start | bytes 3145736 | tf_op jit(solution)/shard_map/ppermute | solution.py:644
  413.9 14.3 %collective-permute-start.36 = (bf16[2,128,2048]{2,1,0:T(8,128)(2,1)}, bf16[2,128,2048]{2,1,0:T(8,128)(2,1)S(1)}, u32[]{:S(2)}, u32[]{:S(2)}) collective-permute-start(bf16[2,128,2048]{2,1,0:T(8,128)(2,1)} %fusion.1), channel_id=1, source_target_pairs={{0,8},{2,6},{8,16},{10,2},{16,24},{18,10},{24,28},{26,18},{28,20},... | collective-permute-start | bytes 3145736 | tf_op jit(solution)/shard_map/ppermute | solution.py:644
  428.6 14.1 %collective-permute-start.37 = (bf16[2,128,2048]{2,1,0:T(8,128)(2,1)S(1)}, bf16[2,128,2048]{2,1,0:T(8,128)(2,1)S(1)}, u32[]{:S(2)}, u32[]{:S(2)}) collective-permute-start(bf16[2,128,2048]{2,1,0:T(8,128)(2,1)S(1)} %fusion.2), channel_id=1, source_target_pairs={{0,8},{2,6},{8,16},{10,2},{16,24},{18,10},{24,28},{26,18},{28,20},... | collective-permute-start | bytes 3145736 | tf_op jit(solution)/shard_map/ppermute | solution.py:644
  429.8 28.6 %collective-permute-start.42 = (bf16[16,320,128]{2,1,0:T(8,128)(2,1)}, bf16[16,320,128]{2,1,0:T(8,128)(2,1)}, u32[]{:S(2)}, u32[]{:S(2)}) collective-permute-start(bf16[16,320,128]{2,1,0:T(8,128)(2,1)} %get-tuple-element.118), channel_id=1, source_target_pairs={{0,1},{1,0},{2,3},{3,2},{4,5},{5,4},{6,7},{7,6},{8,9},{9,8},{10,11... | collective-permute-start | bytes 3932168 | tf_op jit(solution)/shard_map/ppermute | solution.py:650
  442.7 5.1 collective-permute-start.38
  446.2 65.1 %collective-permute-start.45 = (bf16[16,464,128]{2,1,0:T(8,128)(2,1)}, bf16[16,464,128]{2,1,0:T(8,128)(2,1)}, u32[]{:S(2)}, u32[]{:S(2)}) collective-permute-start(bf16[16,464,128]{2,1,0:T(8,128)(2,1)} %get-tuple-element.120), channel_id=1, source_target_pairs={{0,1},{1,0},{2,3},{3,2},{4,5},{5,4},{6,7},{7,6},{8,9},{9,8},{10,11... | collective-permute-start | bytes 5701640 | tf_op jit(solution)/shard_map/ppermute | solution.py:650
  451.6 20.8 %collective-permute-start.41 = (bf16[64,2048]{1,0:T(8,128)(2,1)}, bf16[64,2048]{1,0:T(8,128)(2,1)S(1)}, u32[]{:S(2)}, u32[]{:S(2)}) collective-permute-start(bf16[64,2048]{1,0:T(8,128)(2,1)} %get-tuple-element.117), channel_id=1, source_target_pairs={{0,2},{2,0},{4,6},{6,4},{8,10},{10,8},{12,14},{14,12},{16,18},{18,... | collective-permute-start | bytes 786440 | tf_op jit(solution)/shard_map/ppermute | solution.py:647
  461.1 64.5 %all-to-all-start.4 = ((bf16[16,320,128]{2,1,0:T(8,128)(2,1)}), bf16[16,320,128]{2,1,0:T(8,128)(2,1)S(1)}, u32[]{:S(2)}, u32[]{:S(2)}) async-start(bf16[16,320,128]{2,1,0:T(8,128)(2,1)} %add_convert_fusion.3), calls=%async_computation.4 | async-start | bytes 2621440 | tf_op jit(solution)/shard_map/all_to_all | solution.py:700
  473.3 33.7 %collective-permute-start.43 = (bf16[128,2048]{1,0:T(8,128)(2,1)}, bf16[128,2048]{1,0:T(8,128)(2,1)}, u32[]{:S(2)}, u32[]{:S(2)}) collective-permute-start(bf16[128,2048]{1,0:T(8,128)(2,1)} %maximum_select_fusion.2.rest_0_.refs_10_), channel_id=1, source_target_pairs={{0,8},{2,6},{8,16},{10,2},{16,24},{18,10},{24,28},{26,18},{28,20},... | collective-permute-start | bytes 1572872 | tf_op jit(solution)/shard_map/ppermute | solution.py:644
  476.8 32.1 %collective-permute-start.39 = (bf16[64,2048]{1,0:T(8,128)(2,1)}, bf16[64,2048]{1,0:T(8,128)(2,1)S(1)}, u32[]{:S(2)}, u32[]{:S(2)}) collective-permute-start(bf16[64,2048]{1,0:T(8,128)(2,1)} %forward_out.1), channel_id=1, source_target_pairs={{0,2},{2,0},{4,6},{6,4},{8,10},{10,8},{12,14},{14,12},{16,18},{18,... | collective-permute-start | bytes 786440 | tf_op jit(solution)/shard_map/ppermute | solution.py:647
  507.0 8.5 %collective-permute-start.44 = (bf16[128,2048]{1,0:T(8,128)(2,1)}, bf16[128,2048]{1,0:T(8,128)(2,1)S(1)}, u32[]{:S(2)}, u32[]{:S(2)}) collective-permute-start(bf16[128,2048]{1,0:T(8,128)(2,1)} %collective-permute-done.43.rest_1_.refs_11_), channel_id=1, source_target_pairs={{0,8},{2,6},{8,16},{10,2},{16,24},{18,10},{24,28},{26,18},{28,20},... | collective-permute-start | bytes 1572872 | tf_op jit(solution)/shard_map/ppermute | solution.py:644
  510.0 13.1 %collective-permute-start.40 = (bf16[128,2048]{1,0:T(8,128)(2,1)S(1)}, bf16[128,2048]{1,0:T(8,128)(2,1)S(1)}, u32[]{:S(2)}, u32[]{:S(2)}) collective-permute-start(bf16[128,2048]{1,0:T(8,128)(2,1)S(1)} %maximum_select_fusion.1), channel_id=1, source_target_pairs={{0,1},{1,0},{2,3},{3,2},{4,5},{5,4},{6,7},{7,6},{8,9},{9,8},{10,11... | collective-permute-start | bytes 1572872 | tf_op jit(solution)/shard_map/ppermute | solution.py:650
  515.5 8.5 %collective-permute-start.46 = (bf16[128,2048]{1,0:T(8,128)(2,1)S(1)}, bf16[128,2048]{1,0:T(8,128)(2,1)S(1)}, u32[]{:S(2)}, u32[]{:S(2)}) collective-permute-start(bf16[128,2048]{1,0:T(8,128)(2,1)S(1)} %collective-permute-done.44.rest_2_.refs_12_), channel_id=1, source_target_pairs={{0,8},{2,6},{8,16},{10,2},{16,24},{18,10},{24,28},{26,18},{28,20},... | collective-permute-start | bytes 1572872 | tf_op jit(solution)/shard_map/ppermute | solution.py:644
  525.6 5.5 collective-permute-start.50
  534.4 55.6 %all-to-all-start.5 = ((bf16[16,464,128]{2,1,0:T(8,128)(2,1)}), bf16[16,464,128]{2,1,0:T(8,128)(2,1)S(1)}, u32[]{:S(2)}, u32[]{:S(2)}) async-start(bf16[16,464,128]{2,1,0:T(8,128)(2,1)} %add_convert_fusion.1), calls=%async_computation.5 | async-start | bytes 3801088 | tf_op jit(solution)/shard_map/all_to_all | solution.py:700
  543.7 3.3 collective-permute-start.49
  556.9 30.3 %collective-permute-start.56 = (bf16[16,320,128]{2,1,0:T(8,128)(2,1)}, bf16[16,320,128]{2,1,0:T(8,128)(2,1)}, u32[]{:S(2)}, u32[]{:S(2)}) collective-permute-start(bf16[16,320,128]{2,1,0:T(8,128)(2,1)} %get-tuple-element.137), channel_id=1, source_target_pairs={{0,1},{1,0},{2,3},{3,2},{4,5},{5,4},{6,7},{7,6},{8,9},{9,8},{10,11... | collective-permute-start | bytes 3932168 | tf_op jit(solution)/shard_map/ppermute | solution.py:650
  584.8 27.5 %collective-permute-start.52 = (bf16[448,2048]{1,0:T(8,128)(2,1)}, bf16[448,2048]{1,0:T(8,128)(2,1)}, u32[]{:S(2)}, u32[]{:S(2)}) collective-permute-start(bf16[448,2048]{1,0:T(8,128)(2,1)} %get-tuple-element.128), channel_id=1, source_target_pairs={{0,2},{2,0},{4,6},{6,4},{8,10},{10,8},{12,14},{14,12},{16,18},{18,... | collective-permute-start | bytes 5505032 | tf_op jit(solution)/shard_map/ppermute | solution.py:647
  590.0 48.7 %all-to-all-start.6 = ((bf16[16,320,128]{2,1,0:T(8,128)(2,1)}), bf16[16,320,128]{2,1,0:T(8,128)(2,1)S(1)}, u32[]{:S(2)}, u32[]{:S(2)}) async-start(bf16[16,320,128]{2,1,0:T(8,128)(2,1)} %add_convert_fusion.2), calls=%async_computation.6 | async-start | bytes 2621440 | tf_op jit(solution)/shard_map/all_to_all | solution.py:700
  609.8 18.7 %collective-permute-start.54 = (bf16[1,64,2048]{2,1,0:T(8,128)(2,1)S(1)}, bf16[1,64,2048]{2,1,0:T(8,128)(2,1)S(1)}, u32[]{:S(2)}, u32[]{:S(2)}) collective-permute-start(bf16[1,64,2048]{2,1,0:T(8,128)(2,1)S(1)} %fusion.16), channel_id=1, source_target_pairs={{0,8},{2,6},{8,16},{10,2},{16,24},{18,10},{24,28},{26,18},{28,20},... | collective-permute-start | bytes 786440 | tf_op jit(solution)/shard_map/ppermute | solution.py:644
  611.0 43.5 %collective-permute-start.58 = (bf16[16,464,128]{2,1,0:T(8,128)(2,1)}, bf16[16,464,128]{2,1,0:T(8,128)(2,1)}, u32[]{:S(2)}, u32[]{:S(2)}) collective-permute-start(bf16[16,464,128]{2,1,0:T(8,128)(2,1)} %get-tuple-element.141), channel_id=1, source_target_pairs={{0,1},{1,0},{2,3},{3,2},{4,5},{5,4},{6,7},{7,6},{8,9},{9,8},{10,11... | collective-permute-start | bytes 5701640 | tf_op jit(solution)/shard_map/ppermute | solution.py:650
  629.9 8.7 %collective-permute-start.55 = (bf16[1,128,2048]{2,1,0:T(8,128)(2,1)S(1)}, bf16[1,128,2048]{2,1,0:T(8,128)(2,1)}, u32[]{:S(2)}, u32[]{:S(2)}) collective-permute-start(bf16[1,128,2048]{2,1,0:T(8,128)(2,1)S(1)} %fusion.8), channel_id=1, source_target_pairs={{0,8},{2,6},{8,16},{10,2},{16,24},{18,10},{24,28},{26,18},{28,20},... | collective-permute-start | bytes 1572872 | tf_op jit(solution)/shard_map/ppermute | solution.py:644
  640.7 13.9 %collective-permute-start.57 = (bf16[1,128,2048]{2,1,0:T(8,128)(2,1)S(1)}, bf16[1,128,2048]{2,1,0:T(8,128)(2,1)S(1)}, u32[]{:S(2)}, u32[]{:S(2)}) collective-permute-start(bf16[1,128,2048]{2,1,0:T(8,128)(2,1)S(1)} %fusion.4), channel_id=1, source_target_pairs={{0,8},{2,6},{8,16},{10,2},{16,24},{18,10},{24,28},{26,18},{28,20},... | collective-permute-start | bytes 1572872 | tf_op jit(solution)/shard_map/ppermute | solution.py:644
  655.8 8.5 %collective-permute-start.59 = (bf16[1,128,2048]{2,1,0:T(8,128)(2,1)S(1)}, bf16[1,128,2048]{2,1,0:T(8,128)(2,1)}, u32[]{:S(2)}, u32[]{:S(2)}) collective-permute-start(bf16[1,128,2048]{2,1,0:T(8,128)(2,1)S(1)} %fusion.3), channel_id=1, source_target_pairs={{0,8},{2,6},{8,16},{10,2},{16,24},{18,10},{24,28},{26,18},{28,20},... | collective-permute-start | bytes 1572872 | tf_op jit(solution)/shard_map/ppermute | solution.py:644
  664.3 49.4 %all-to-all-start.7 = ((bf16[16,464,128]{2,1,0:T(8,128)(2,1)}), bf16[16,464,128]{2,1,0:T(8,128)(2,1)S(1)}, u32[]{:S(2)}, u32[]{:S(2)}) async-start(bf16[16,464,128]{2,1,0:T(8,128)(2,1)} %add_convert_fusion), calls=%async_computation.7 | async-start | bytes 3801088 | tf_op jit(solution)/shard_map/all_to_all | solution.py:700
  671.7 9.1 %collective-permute-start.60 = (bf16[1,64,2048]{2,1,0:T(8,128)(2,1)S(1)}, bf16[1,64,2048]{2,1,0:T(8,128)(2,1)S(1)}, u32[]{:S(2)}, u32[]{:S(2)}) collective-permute-start(bf16[1,64,2048]{2,1,0:T(8,128)(2,1)S(1)} %constant_dynamic-slice_fusion.5), channel_id=1, source_target_pairs={{0,2},{2,0},{4,6},{6,4},{8,10},{10,8},{12,14},{14,12},{16,18},{18,... | collective-permute-start | bytes 786440 | tf_op jit(solution)/shard_map/ppermute | solution.py:647
  672.3 8.5 %collective-permute-start.61 = (f32[2,448]{1,0:T(2,128)S(1)}, f32[2,448]{1,0:T(2,128)S(1)}, u32[]{:S(2)}, u32[]{:S(2)}) collective-permute-start(f32[2,448]{1,0:T(2,128)S(1)} %pad_maximum_fusion.3), channel_id=1, source_target_pairs={{0,1},{1,0},{2,3},{3,2},{4,5},{5,4},{6,7},{7,6},{8,9},{9,8},{10,11... | collective-permute-start | bytes 10760 | tf_op jit(solution)/shard_map/ppermute | solution.py:650
  687.4 13.2 %collective-permute-start.63 = (bf16[128,2048]{1,0:T(8,128)(2,1)S(1)}, bf16[128,2048]{1,0:T(8,128)(2,1)S(1)}, u32[]{:S(2)}, u32[]{:S(2)}) collective-permute-start(bf16[128,2048]{1,0:T(8,128)(2,1)S(1)} %maximum_select_fusion.3), channel_id=1, source_target_pairs={{0,1},{1,0},{2,3},{3,2},{4,5},{5,4},{6,7},{7,6},{8,9},{9,8},{10,11... | collective-permute-start | bytes 1572872 | tf_op jit(solution)/shard_map/ppermute | solution.py:650
  (57 other events, 913.2 us)
